TPU v7x, 32 devices: a whole 2x2x4 slice. The times are simulated.
32 devices in a mesh: dp: 8 (over z, x), blk: 4 (over y, core).
Axes of the slice: x: 2, y: 2, z: 4, core: 2. Of those that a mesh axis runs over, the one named last changes fastest.
Arguments:
- inputs: bfloat16 [16, 1024, 512], P('dp', 'blk'), may hold values from -16 to 16
- w_query: bfloat16 [512, 512], replicated, may hold values from -0.03125 to 0.03125
- w_key: bfloat16 [512, 512], replicated, may hold values from -0.25 to 0.25
- w_value: bfloat16 [512, 512], replicated, may hold values from -0.25 to 0.25
- w_out: bfloat16 [512, 512], replicated, may hold values from -4 to 4
- w_in: bfloat16 [512, 2048], replicated, may hold values from -0.25 to 0.25
- w_back: bfloat16 [2048, 512], replicated, may hold values from -0.125 to 0.125
- norm1_gain: float32 [512], replicated, may hold values from 0.1 to 1.9
- norm2_gain: float32 [512], replicated, may hold values from 0.1 to 1.9
- final_gain: float32 [512], replicated, may hold values from 0.1 to 1.9
- bias_table: float32 [32, 8], replicated, may hold values from -4 to 4
- bucket_table: int32 [2047], replicated, may hold values from 0 to 31
- prefix_len: int32 [16], P('dp'), may hold values from 5 to 40
- pad_len: int32 [16], P('dp'), may hold values from 0 to 255
- pooled_grad: float32 [16, 512], P('dp'), may hold values from -8 to 8
Outputs:
- pooled: float32 [16, 512], P('dp')
- input_grad: bfloat16 [16, 1024, 512], P('dp', 'blk')
- query_grad: float32 [512, 512], replicated
- key_grad: float32 [512, 512], replicated
- value_grad: float32 [512, 512], replicated
- out_grad: float32 [512, 512], replicated
- in_grad: float32 [512, 2048], replicated
- back_grad: float32 [2048, 512], replicated
- norm1_grad: float32 [512], replicated
- norm2_grad: float32 [512], replicated
- final_grad: float32 [512], replicated
- bias_grad: float32 [32, 8], replicated
Inputs may be any that keep to these rules, and one draw needn't show every extreme that they name: `bucket_table`: entry r is the bucket of the offset r - 1023, key position minus query position.
All inputs are finite; a program needn't handle non-finite values.
Results may differ from a plain program's by a relative error of at most 0.03.
Values may be sent and summed in bfloat16 or wider, within the bound.
No kernel may reach another device: no remote copies, remote signals or barrier semaphores. Data moves between devices by JAX's collectives and lax.ppermute only.
A program may use at most 192 MiB of HBM per device.

v0:
```python
import functools
import jax, jax.numpy as jnp
from jax import lax
from jax.experimental import pallas as pl
from jax.experimental.pallas import tpu as pltpu
from jax.sharding import PartitionSpec as P

F32, BF16 = jnp.float32, jnp.bfloat16
NEG = -1000000000.0
NT = (((1,), (1,)), ((), ()))
TN = (((0,), (0,)), ((), ()))
NN = (((1,), (0,)), ((), ()))

def dot(a, b, dims=NN):
    return lax.dot_general(a, b, dims, preferred_element_type=F32)

def skew(row, width, dtype=F32):
    return pltpu.roll(jnp.broadcast_to(row, (128, width)), width - 127, 1, stride=1, stride_axis=0)


BUCKETS = 32
EPS = 1e-06
CORE, ROW, NEAR_X = 1, 2, 4

def rms_scale(values):
    return lax.rsqrt(jnp.mean(values * values, axis=-1, keepdims=True) + EPS)

def norm_back(grad_out, values, scale, gain):
    weighted = grad_out * gain
    inner = jnp.mean(weighted * values, axis=-1, keepdims=True)
    grad_in = scale * weighted - scale * scale * scale * values * inner
    return grad_in, jnp.sum(grad_out * values * scale, axis=0, keepdims=True)

def two_terms(value):
    high = value.astype(BF16)
    return jnp.concatenate([high, (value - high.astype(F32)).astype(BF16)])

def one_value(terms):
    return terms[:16].astype(F32) + terms[16:32].astype(F32)

def rows_of(*values):
    count = sum(v.shape[0] for v in values)
    return jnp.concatenate(list(values) + [jnp.zeros((16 - count, values[0].shape[1]), F32)])

def prepare_kernel(ids, pads, prefixes, mine, other, wq, wk, wv, gain, bias, buckets, hidden, query, keys, values, lines, info):
    rows = mine.shape[0]
    info[0] = 4 * rows - pads[ids[6]]
    info[5] = prefixes[ids[6]]
    for to, at in enumerate((0, 1, 2, 3)):
        info[1 + to] = ids[at]
    for to, at in enumerate((4, 5, 6)):
        info[6 + to] = ids[at]
    for part, raw in enumerate((mine, other)):
        tokens = raw[...].astype(F32)
        hidden[part * rows : (part + 1) * rows, :] = (tokens * rms_scale(tokens) * gain[...]).astype(BF16)
    h = hidden[...]
    query[...] = dot(h[:rows], wq[...]).astype(BF16)
    keys[...] = dot(h, wk[...]).astype(BF16)
    values[...] = dot(h, wv[...]).astype(BF16)
    picker = jnp.where(lax.broadcasted_iota(jnp.int32, (bias.shape[0], 1), 0) == buckets[...], 1.0, 0.0).astype(BF16)
    left, total = bias[...], None
    for _ in range(3):
        part = left.astype(BF16)
        left = left - part.astype(F32)
        made = dot(part, picker, TN)
        total = made if total is None else total + made
    lines[...] = jnp.zeros_like(lines)
    lines[:, : buckets.shape[1]] = total

def prepare(ids, pads, prefixes, mine, other, wq, wk, wv, gain, bias, buckets):
    rows, width = mine.shape
    span = buckets.shape[1] + 1
    heads = bias.shape[1]
    shape = lambda n: jax.ShapeDtypeStruct((n, width), BF16)
    smem, vmem = pl.BlockSpec(memory_space=pltpu.SMEM), pl.BlockSpec(memory_space=pltpu.VMEM)
    return pl.pallas_call(
        prepare_kernel,
        in_specs=[smem] * 3 + [vmem] * 8,
        out_specs=[vmem] * 5 + [smem],
        out_shape=[shape(2 * rows), shape(rows), shape(2 * rows), shape(2 * rows),
                   jax.ShapeDtypeStruct((heads, span), F32), jax.ShapeDtypeStruct((16,), jnp.int32)],
        name="prepare",
    )(ids, pads, prefixes, mine, other, wq, wk, wv, gain, bias, buckets)

def swap_in(to, hidden, index, mine, made, columns):
    for b in range(2):
        if columns:
            to[(2 * index + b) ^ mine] = made[:, b * 128 : (b + 1) * 128]
        else:
            to[(2 * index + b) ^ mine] = jnp.concatenate([made[b * 128 : (b + 1) * 128, q * 128 : (q + 1) * 128] for q in range(4)])

def back_pieces(to, active, low, mine):
    @pl.loop(0, active.shape[1] // 256)
    def _(pair):
        made = dot(active[:, pl.ds(pl.multiple_of(pair * 256, 256), 256)], low, TN).astype(BF16)
        swap_in(to, active.shape[1], pair, mine, made, False)

def in_pieces(to, slopes, turned, mine):
    @pl.loop(0, slopes.shape[1] // 256)
    def _(pair):
        made = dot(turned, slopes[:, pl.ds(pl.multiple_of(pair * 256, 256), 256)]).astype(BF16)
        swap_in(to, slopes.shape[1], pair, mine, made, True)

def front_kernel(info, far, far_other, near, q_l, k_l, v_l, lines, wq, wk, wv, gain1, gain2, gain3, cots, wo_h, win_h, wback_h,
                 hid_o, q_o, k_o, v_o, expo_o, inv_o, att_o, send_o, active_o, slopes_o, turned_o, mixed_o, steep_o, rows,
                 hid, qs, ks, vs, inv, att, send, active, slopes, turned, mixed, steep, wo, win, wback, expo, scores, skewed, edges, sems):
    count, width = near.shape
    hidden = win.shape[1]
    step = pl.program_id(0)
    late = [pltpu.make_async_copy(a, b, sems.at[i]) for i, (a, b) in enumerate(((wo_h, wo), (win_h, win), (wback_h, wback)))]
    early = [pltpu.make_async_copy(a, b, sems.at[3 + i]) for i, (a, b) in enumerate(((hid, hid_o), (qs, q_o), (ks, k_o), (vs, v_o)))]
    dense = [pltpu.make_async_copy(a, b, sems.at[7 + i]) for i, (a, b) in enumerate((
        (inv, inv_o), (att, att_o), (mixed, mixed_o), (turned, turned_o), (active, active_o), (steep, steep_o), (slopes, slopes_o), (send, send_o)))]
    kept = lambda g: pltpu.make_async_copy(expo, expo_o.at[pl.ds(2 * g, 2)], sems.at[15])

    @pl.when(step == 0)
    def _():
        for copy in late:
            copy.start()
        for part, raw in enumerate((far, far_other)):
            tokens = raw[...].astype(F32)
            hid[part * count : (part + 1) * count, :] = (tokens * rms_scale(tokens) * gain1[...]).astype(BF16)
        h = hid[...]
        qs[...] = dot(h[:count], wq[...]).astype(BF16)
        ks[...] = dot(h, wk[...]).astype(BF16)
        vs[...] = dot(h, wv[...]).astype(BF16)
        for copy in early:
            copy.start()
        column = lax.broadcasted_iota(jnp.int32, (1, 128), 1)
        for b in range(4):
            place = info[1 + b] + lax.broadcasted_iota(jnp.int32, (count, 1), 0)
            gate = jnp.where(place < info[0], 0.0, NEG)
            for head in range(2):
                edges[head, b * count : (b + 1) * count, :] = jnp.where(column == (64 if head == 0 else 0), gate, 0.0).astype(BF16)

    @pl.when(step > 0)
    def _():
        kept(step - 1).wait()

    cols = pl.ds(pl.multiple_of(step * 128, 128), 128)
    lane = lax.broadcasted_iota(jnp.int32, (1, 128), 1)
    first = lane < 64
    limit = info[0]
    starts = [info[1 + b] for b in range(4)]
    keys = [k_l[:count, :], k_l[count:, :], ks[:count, cols], ks[count:, cols]]
    values = jnp.concatenate([v_l[...], vs[:, cols]])
    query = jnp.concatenate([q_l[...], qs[:, cols]])
    made = []
    for head in range(2):
        mine = jnp.where(first if head == 0 else lane >= 64, 1.0, 0.0).astype(BF16)
        one = jnp.where(lane == (64 if head == 0 else 0), 1.0, 0.0).astype(BF16)
        q = query * mine + one
        v = values * mine + one
        skewed[head] = skew(lines[pl.ds(2 * step + head, 1), :], lines.shape[1])
        for b in range(4):
            s = dot(q, keys[b] * mine + edges[head, b * count : (b + 1) * count, :], NT)
            for r in range(4):
                at = starts[b] - starts[2 * (r // 2)] + 896 - 128 * (r % 2)
                part = s[r * 128 : (r + 1) * 128] + skewed[head, :, pl.ds(pl.multiple_of(at, 128), 256)]
                scores[head, r * 128 : (r + 1) * 128, b * 256 : (b + 1) * 256] = part
        for r in range(4):
            rs = slice(r * 128, (r + 1) * 128)
            value = scores[head, rs, :]
            top = jnp.max(value, axis=1, keepdims=True)
            expo[head, rs, :] = jnp.exp(value - top).astype(BF16)
        acc = dot(expo[head], v)
        made.append((acc, 1.0 / (acc[:, 64:65] if head == 0 else acc[:, 0:1])))
    (a0, i0), (a1, i1) = made
    scale = jnp.where(first, i0, i1)
    att[:, cols] = (jnp.where(first, a0, a1) * scale).astype(BF16)
    inv[:, cols] = scale
    kept(step).start()

    @pl.when(step == 3)
    def _():
        for copy in late:
            copy.wait()
        dense[0].start()
        dense[1].start()
        for part, raw in enumerate((near, far)):
            spot = slice(part * count, (part + 1) * count)
            mixed[spot, :] = raw[...].astype(F32) + dot(att[spot, :], wo[...])
        dense[2].start()
        values = mixed[...]
        inner = (values * rms_scale(values) * gain2[...]).astype(BF16)
        turned[...] = inner.T
        dense[3].start()
        total = values
        for at in range(0, hidden, 512):
            lifted = jnp.maximum(dot(inner, win[:, at : at + 512]), 0.0).astype(BF16)
            active[:, at : at + 512] = lifted
            total = total + dot(lifted, wback[at : at + 512, :])
        dense[4].start()
        scale = rms_scale(total)
        place = lax.broadcasted_iota(jnp.int32, (2 * count, 1), 0)
        place = jnp.where(place < count, place + info[1], place + (info[3] - count))
        live = jnp.where((place >= info[5]) & (place < limit), 1.0, 0.0)
        pool = jnp.sum(total * scale * gain3[...] * live, axis=0, keepdims=True)
        cot = jnp.where(info[8] == 0, cots[0:1, :], cots[1:2, :]) / (limit - info[5]).astype(F32)
        slope, grad_end = norm_back(live * cot, total, scale, gain3[...])
        steep[...] = slope
        dense[5].start()
        rows[...] = jnp.concatenate([pool, grad_end, jnp.zeros((6, width), F32)])
        low = slope.astype(BF16)
        for at in range(0, hidden, 512):
            through = dot(low, wback[at : at + 512, :], NT).astype(BF16)
            slopes[:, at : at + 512] = jnp.where(active[:, at : at + 512] > 0, through, jnp.zeros_like(through))
        dense[6].start()
        mine = info[6] & 15

        @pl.when(info[7] == 0)
        def _():
            in_pieces(send, slopes, turned[...], mine)

        @pl.when(info[7] == 1)
        def _():
            back_pieces(send, active, steep[...].astype(BF16), mine)

        dense[7].start()
        for copy in early + dense:
            copy.wait()
        kept(step).wait()

def front(info, far, far_other, near, q_l, k_l, v_l, lines, wq, wk, wv, gain1, gain2, gain3, cots, wo, win, wback):
    count, width = near.shape
    hidden = win.shape[1]
    heads, span = lines.shape
    shape = jax.ShapeDtypeStruct
    smem, free = pl.BlockSpec(memory_space=pltpu.SMEM), pl.BlockSpec(memory_space=pl.ANY)
    whole = lambda *dims: pl.BlockSpec(dims, lambda g: (0,) * len(dims))
    col = lambda n: pl.BlockSpec((n, 128), lambda g: (0, g))
    outs = [shape((2 * count, width), BF16), shape((count, width), BF16), shape((2 * count, width), BF16), shape((2 * count, width), BF16),
            shape((heads, 2 * count, 4 * count), BF16), shape((2 * count, width), F32), shape((2 * count, width), BF16),
            shape((16, width, 128), BF16), shape((2 * count, hidden), BF16), shape((2 * count, hidden), BF16),
            shape((width, 2 * count), BF16), shape((2 * count, width), F32), shape((2 * count, width), F32)]
    return pl.pallas_call(
        front_kernel,
        grid=(heads // 2,),
        in_specs=[smem, whole(count, width), whole(count, width), whole(count, width), col(count), col(2 * count), col(2 * count),
                  whole(heads, span)] + [whole(width, width)] * 3 + [whole(1, width)] * 3
                 + [whole(2, width)] + [free] * 3,
        out_specs=[free] * 13 + [whole(8, width)],
        out_shape=outs + [shape((8, width), F32)],
        scratch_shapes=[pltpu.VMEM(o.shape, o.dtype) for o in outs[:4] + outs[5:]]
                       + [pltpu.VMEM(wo.shape, BF16), pltpu.VMEM(win.shape, BF16), pltpu.VMEM(wback.shape, BF16),
                          pltpu.VMEM((2, 2 * count, 4 * count), BF16), pltpu.VMEM((2, 2 * count, 4 * count), F32),
                          pltpu.VMEM((2, 128, span), F32), pltpu.VMEM((2, 4 * count, 128), BF16), pltpu.SemaphoreType.DMA((16,))],
        name="front",
    )(info, far, far_other, near, q_l, k_l, v_l, lines, wq, wk, wv, gain1, gain2, gain3, cots, wo, win, wback)

def through_kernel(info, slopes_h, win_h, mixed_h, steep_h, wo_h, att_h, active_h, turned_h, gain2, keep, grad_mixed, grad_out, grad_attended, rows,
                   slopes, win, mixed, steep, wo, att, active, turned, sems):
    hidden, width = slopes.shape[1], mixed.shape[1]
    chunks = []
    for i, at in enumerate(range(0, hidden, 512)):
        for a, b, s in ((slopes_h, slopes, i), (win_h, win, 4 + i)):
            chunks.append(pltpu.make_async_copy(a.at[:, at : at + 512], b.at[:, at : at + 512], sems.at[s]))
    copies = [pltpu.make_async_copy(a, b, sems.at[8 + i]) for i, (a, b) in enumerate((
        (mixed_h, mixed), (steep_h, steep), (wo_h, wo), (att_h, att), (active_h, active), (turned_h, turned)))]
    for copy in chunks + copies:
        copy.start()
    grad_inner = None
    for i, at in enumerate(range(0, hidden, 512)):
        chunks[2 * i].wait()
        chunks[2 * i + 1].wait()
        part = dot(slopes[:, at : at + 512], win[:, at : at + 512], NT)
        grad_inner = part if grad_inner is None else grad_inner + part
    copies[0].wait()
    copies[1].wait()
    values = mixed[...]
    more, grad_two = norm_back(grad_inner, values, rms_scale(values), gain2[...])
    total = steep[...] + more
    grad_mixed[...] = total
    low = total.astype(BF16)
    copies[2].wait()
    grad_attended[...] = dot(low, wo[...], NT).astype(BF16)
    copies[3].wait()
    grad_out[...] = dot(att[...], low, TN).astype(BF16)
    rows[...] = jnp.concatenate([grad_two, jnp.zeros((7, width), F32)])
    copies[4].wait()
    copies[5].wait()
    mine = info[6] & 15

    @pl.when(info[7] == 0)
    def _():
        back_pieces(keep, active, steep[...].astype(BF16), mine)

    @pl.when(info[7] == 1)
    def _():
        in_pieces(keep, slopes, turned[...], mine)

def through(info, slopes, win, mixed, steep, wo, att, active, turned, gain2):
    n, width = mixed.shape
    smem, vmem, free = (pl.BlockSpec(memory_space=m) for m in (pltpu.SMEM, pltpu.VMEM, pl.ANY))
    shape = jax.ShapeDtypeStruct
    given = (slopes, win, mixed, steep, wo, att, active, turned)
    return pl.pallas_call(
        through_kernel,
        in_specs=[smem] + [free] * 8 + [vmem],
        out_specs=[vmem] * 5,
        out_shape=[shape((16, width, 128), BF16), shape((n, width), F32), shape((width, width), BF16), shape((n, width), BF16), shape((8, width), F32)],
        scratch_shapes=[pltpu.VMEM(g.shape, g.dtype) for g in given] + [pltpu.SemaphoreType.DMA((14,))],
        name="through",
    )(info, *given, gain2)

CLASS = {(0, 0): 0, (1, 2): 0, (0, 1): 1, (1, 3): 1, (0, 2): 2, (0, 3): 3, (1, 0): 4, (1, 1): 5}

def back_kernel(info, ql, qr, kl, kr, vl, vr, gout, out, inv, expo, buckets, dense_rows, through_rows,
                hid_l_h, hid_r_h, near_h, near_other_h, far_h, far_other_h, wq_h, wk_h, wv_h, grad_out_h,
                keep_o, send_o, stay_o, leave_o, small,
                hid_l, hid_r, near, near_other, far, far_other, wq, wk, wv, made,
                keep, send, stay, leave, dq, dk, dv, offsets, sums, acc, slopes, sems):
    count, width = near.shape
    step = pl.program_id(0)
    pairs = width // 128
    late = [pltpu.make_async_copy(a, b, sems.at[i]) for i, (a, b) in enumerate((
        (hid_l_h, hid_l), (hid_r_h, hid_r), (near_h, near), (near_other_h, near_other), (far_h, far), (far_other_h, far_other),
        (wq_h, wq), (wk_h, wk), (wv_h, wv), (grad_out_h, made.at[0:width])))]
    done = [pltpu.make_async_copy(a, b, sems.at[10 + i]) for i, (a, b) in enumerate(((send, send_o), (keep, keep_o), (leave, leave_o), (stay, stay_o)))]

    @pl.when(step == 0)
    def _():
        for copy in late:
            copy.start()

    cols = pl.ds(pl.multiple_of(step * 128, 128), 128)
    lane = lax.broadcasted_iota(jnp.int32, (1, 128), 1)
    starts = [info[1 + b] for b in range(4)]
    keys = jnp.concatenate([kl[...], kr[...]])
    values = jnp.concatenate([vl[...], vr[...]])
    query = jnp.concatenate([ql[...], qr[...]])
    scaled = gout[...].astype(F32) * inv[...]
    prod = scaled * out[...].astype(F32)
    low = scaled.astype(BF16)
    query_t, low_t = query.T, low.T
    grads_q, grads_k, grads_v = None, [], []
    for head in range(2):
        mine = (lane < 64) if head == 0 else (lane >= 64)
        base = 64 if head == 0 else 0
        pick = jnp.where(mine, 1.0, 0.0).astype(BF16)
        delta = jnp.sum(jnp.where(mine, prod, 0.0), axis=1, keepdims=True)
        high = delta.astype(BF16).astype(F32)
        extra = jnp.where(lane == base, high, jnp.where(lane == base + 1, delta - high, 0.0)).astype(BF16)
        grad = low * pick + extra
        minus = jnp.where((lane == base) | (lane == base + 1), -1.0, 0.0).astype(BF16)
        for b in range(4):
            spot = slice(b * count, (b + 1) * count)
            ds = dot(grad, values[spot] * pick + minus, NT) * expo[head, :, spot].astype(F32)
            slopes[head, :, spot] = ds.astype(BF16)
            for chunk in range(2):
                upper, lower = (ds[chunk * count + r * 128 : chunk * count + (r + 1) * 128] for r in range(2))
                group = CLASS[chunk, b]
                block = jnp.concatenate([lower[:, :128], lower[:, 128:] + upper[:, :128], upper[:, 128:]], axis=1)
                if (chunk, b) in ((1, 2), (1, 3)):
                    block = block + sums[head, group]
                sums[head, group] = block
        part = dot(slopes[head], keys * pick)
        grads_q = part if grads_q is None else grads_q + part
        half = slice(head * 64, (head + 1) * 64)
        grads_k.append(dot(query_t[half], slopes[head]))
        grads_v.append(dot(low_t[half], expo[head]))
    dq[:, cols] = grads_q.astype(BF16)
    dk[:, cols] = jnp.concatenate(grads_k).astype(BF16).T
    dv[:, cols] = jnp.concatenate(grads_v).astype(BF16).T
    for head in range(2):
        acc[head] = jnp.zeros(acc.shape[1:], F32)
        for (chunk, b), group in CLASS.items():
            if (chunk, b) not in ((1, 2), (1, 3)):
                at = starts[b] - starts[2 * chunk] + 768
                to = pl.ds(pl.multiple_of(at, 128), 384)
                acc[head, :, to] += sums[head, group]
        rest = acc[head]
        n = 64
        while n >= 8:
            rest = rest[:n] + pltpu.roll(rest[n:], 2048 - n, 1)
            n //= 2
        line = rest[7:8]
        for r in range(6, -1, -1):
            line = rest[r : r + 1] + pltpu.roll(line, 2047, 1)
        offsets[pl.ds(2 * step + head, 1), :] = pltpu.roll(line, 127, 1)

    @pl.when(step == pairs - 1)
    def _():
        for copy in late:
            copy.wait()
        made[width : 2 * width, :] = (dot(hid_l[:count, :], dq[:count, :], TN) + dot(hid_r[:count, :], dq[count:, :], TN)).astype(BF16)
        for at, grads in ((2 * width, dk), (3 * width, dv)):
            made[at : at + width, :] = (dot(hid_l[...], grads[: 2 * count, :], TN) + dot(hid_r[...], grads[2 * count :, :], TN)).astype(BF16)
        me = info[6]
        size = made.shape[0] // 32

        @pl.loop(0, 16)
        def _(r):
            keep[r] = made[pl.ds(pl.multiple_of((r ^ me) * size, size), size), :]
            send[pl.ds(pl.multiple_of(r * size, size), size), :] = made[pl.ds(pl.multiple_of(((r + 16) ^ me) * size, size), size), :]

        gain = jnp.zeros((1, width), F32)
        for b, raw in enumerate((near, near_other, far, far_other)):
            spot = slice(b * count, (b + 1) * count)
            grad = dot(dk[spot, :], wk[...], NT) + dot(dv[spot, :], wv[...], NT)
            half = slice((b // 2) * count, (b // 2 + 1) * count)
            if b % 2 == 0:
                grad = grad + dot(dq[half, :], wq[...], NT)
                stay[half, :] = grad
            else:
                leave[half, :] = grad.astype(BF16)
            tokens = raw[...].astype(F32)
            gain = gain + jnp.sum(grad * (tokens * rms_scale(tokens)), axis=0, keepdims=True)
        leave[2 * count :, :] = two_terms(rows_of(dense_rows[0:1, :]))
        picker = jnp.where(lax.broadcasted_iota(jnp.int32, (128, 1), 0) == buckets[...], 1.0, 0.0).astype(BF16)
        left = offsets[...][:, : buckets.shape[1]]
        bias = None
        for _ in range(3):
            part = left.astype(BF16)
            left = left - part.astype(F32)
            bias = dot(part, picker, NT) if bias is None else bias + dot(part, picker, NT)
        bias = jnp.concatenate([bias, jnp.zeros((bias.shape[0], width - 128), F32)], axis=1)
        total = jnp.concatenate([gain, through_rows[0:1, :], dense_rows[1:2, :], jnp.zeros((5, width), F32), bias])
        small[...] = total
        send[16 * size :, :] = two_terms(total)
        for copy in done:
            copy.start()
        for copy in done:
            copy.wait()

def back(info, ql, qr, kl, kr, vl, vr, gout, out, inv, expo, buckets, dense_rows, through_rows,
         hid_l, hid_r, near, near_other, far, far_other, wq, wk, wv, grad_out):
    count, width = near.shape
    smem, free = pl.BlockSpec(memory_space=pltpu.SMEM), pl.BlockSpec(memory_space=pl.ANY)
    whole = lambda *dims: pl.BlockSpec(dims, lambda g: (0,) * len(dims))
    col = lambda n: pl.BlockSpec((n, 128), lambda g: (0, g))
    shape = jax.ShapeDtypeStruct
    size = 4 * width // 32
    outs = [shape((16, size, width), BF16), shape((16 * size + 32, width), BF16), shape((2 * count, width), F32), shape((2 * count + 32, width), BF16)]
    given = (hid_l, hid_r, near, near_other, far, far_other, wq, wk, wv)
    return pl.pallas_call(
        back_kernel,
        grid=(width // 128,),
        in_specs=[smem, col(count), col(count)] + [col(2 * count)] * 7 + [pl.BlockSpec((2, 2 * count, 4 * count), lambda g: (g, 0, 0)),
                  whole(*buckets.shape), whole(8, width), whole(8, width)] + [free] * 10,
        out_specs=[free] * 4 + [whole(16, width)],
        out_shape=outs + [shape((16, width), F32)],
        scratch_shapes=[pltpu.VMEM(g.shape, BF16) for g in given] + [pltpu.VMEM((4 * width, width), BF16)]
                       + [pltpu.VMEM(o.shape, o.dtype) for o in outs]
                       + [pltpu.VMEM((2 * count, width), BF16), pltpu.VMEM((4 * count, width), BF16), pltpu.VMEM((4 * count, width), BF16),
                          pltpu.VMEM((8, 2048), F32), pltpu.VMEM((2, 6, 128, 384), F32), pltpu.VMEM((2, 128, 2048), F32),
                          pltpu.VMEM((2, 2 * count, 4 * count), BF16), pltpu.SemaphoreType.DMA((14,))],
        name="back",
    )(info, ql, qr, kl, kr, vl, vr, gout, out, inv, expo, buckets, dense_rows, through_rows, *given, grad_out)

def ending_kernel(info, stay, came, near, far, grad_mixed, gain, dense_rows, home, away):
    count, width = near.shape
    for part, raw in enumerate((near, far)):
        spot = slice(part * count, (part + 1) * count)
        tokens = raw[...].astype(F32)
        grad = stay[spot, :] + came[spot, :].astype(F32)
        more, _ = norm_back(grad, tokens, rms_scale(tokens), gain[...])
        value = (grad_mixed[spot, :] + more).astype(BF16)
        if part == 0:
            home[:count, :] = value
        else:
            away[:count, :] = value
    alive = (info[0] - info[5]).astype(F32)
    pool = two_terms((rows_of(dense_rows[0:1, :]) + one_value(came[2 * count :, :])) / alive)
    home[count:, :] = pool
    away[count:, :] = pool

def ending(info, stay, came, near, far, grad_mixed, gain, dense_rows):
    count, width = near.shape
    smem, vmem = pl.BlockSpec(memory_space=pltpu.SMEM), pl.BlockSpec(memory_space=pltpu.VMEM)
    shape = jax.ShapeDtypeStruct((count + 32, width), BF16)
    return pl.pallas_call(
        ending_kernel, in_specs=[smem] + [vmem] * 7, out_specs=[vmem] * 2, out_shape=[shape, shape], name="ending"
    )(info, stay, came, near, far, grad_mixed, gain, dense_rows)

def place_kernel(half, info, *refs):
    parts, (back, front), (tall, sems) = refs[:4], refs[-4:-2], refs[-2:]
    mine = info[6] & 15

    @pl.when(info[7] == half)
    def _():
        copies = []
        for r in range(16):
            to = pl.ds(pl.multiple_of((r ^ mine) * 128, 128), 128)
            for q in range(4):
                tall[r, :128, q * 128 : (q + 1) * 128] = parts[r // 4][r % 4, q * 128 : (q + 1) * 128, :].astype(F32)
            copies.append(pltpu.make_async_copy(tall.at[r, :128, :], back.at[to, :], sems.at[r]))
            copies[-1].start()
        for copy in copies:
            copy.wait()

    @pl.when(info[7] != half)
    def _():
        copies = []
        for r in range(16):
            to = pl.ds(pl.multiple_of((r ^ mine) * 128, 128), 128)
            tall[r, :, :128] = parts[r // 4][r % 4].astype(F32)
            copies.append(pltpu.make_async_copy(tall.at[r, :, :128], front.at[:, to], sems.at[r]))
            copies[-1].start()
        for copy in copies:
            copy.wait()

def place(info, half, parts, made, width):
    smem, vmem, free = (pl.BlockSpec(memory_space=m) for m in (pltpu.SMEM, pltpu.VMEM, pl.ANY))
    shape = jax.ShapeDtypeStruct
    return pl.pallas_call(
        functools.partial(place_kernel, half),
        in_specs=[smem] + [vmem] * 4 + [free] * len(made),
        out_specs=[free] * 2,
        out_shape=[shape((16 * 128, width), F32), shape((width, 16 * 128), F32)],
        scratch_shapes=[pltpu.VMEM((16, width, width), F32), pltpu.SemaphoreType.DMA((16,))],
        input_output_aliases={5 + i: i for i in range(len(made))},
        name="place",
    )(info, *parts, *made)

def sort_kernel(half, info, *refs):
    parts, made, (tall, sems) = refs[:4], refs[-6:-2], refs[-2:]
    size = parts[0].shape[1]
    per = tall.shape[1] // size
    mine = info[6] & 15
    for r in range(16):
        to = r ^ mine
        tall[to // per, pl.ds(pl.multiple_of((to % per) * size, size), size), :] = parts[r // 4][r % 4].astype(F32)
    for top in range(2):
        @pl.when((info[7] ^ half) == top)
        def _(top=top):
            copies = [pltpu.make_async_copy(tall.at[w], made[2 * top + w], sems.at[w]) for w in range(2)]
            for copy in copies:
                copy.start()
            for copy in copies:
                copy.wait()

def sort(info, half, parts, made, width):
    smem, vmem, free = (pl.BlockSpec(memory_space=m) for m in (pltpu.SMEM, pltpu.VMEM, pl.ANY))
    shape = jax.ShapeDtypeStruct((width, width), F32)
    return pl.pallas_call(
        functools.partial(sort_kernel, half),
        in_specs=[smem] + [vmem] * 4 + [free] * len(made),
        out_specs=[free] * 4,
        out_shape=[shape] * 4,
        scratch_shapes=[pltpu.VMEM((2, width, width), F32), pltpu.SemaphoreType.DMA((2,))],
        input_output_aliases={5 + i: i for i in range(len(made))},
        name="sort",
    )(info, *parts, *made)

def mix_kernel(*refs):
    ins, outs = refs[: -4], refs[-4:]
    for k in range(4):
        outs[k][...] = added(*[term[k] for term in ins])

def mix(terms):
    block = terms[0].shape[1:]
    spec = pl.BlockSpec((4,) + block, lambda i: (0,) * (1 + len(block)))
    out = pl.BlockSpec(block, lambda i: (0,) * len(block))
    return pl.pallas_call(
        mix_kernel, grid=(1,), in_specs=[spec] * len(terms), out_specs=[out] * 4,
        out_shape=[jax.ShapeDtypeStruct(block, BF16)] * 4, name="mix",
    )(*terms)

def exchange(value, bits):
    size = lax.axis_size("dp") * lax.axis_size("blk")
    return lax.ppermute(value, ("dp", "blk"), [(i, i ^ bits) for i in range(size)])

def wait(*values):
    return lax.optimization_barrier(values)

def added(*terms):
    total = terms[0].astype(F32)
    for term in terms[1:]:
        total = total + term.astype(F32)
    return total.astype(BF16)

def local(inputs, w_query, w_key, w_value, w_out, w_in, w_back, norm1_gain, norm2_gain, final_gain, bias_table, bucket_table, prefix_len, pad_len, pooled_grad):
    rows, width = inputs.shape[1:]
    spot, far_off = lax.axis_index("blk"), lax.axis_index("dp")
    doc, core = spot // 2, spot % 2
    block = [doc * 2 + core, doc * 2 + 1 - core, (1 - doc) * 2 + core, (1 - doc) * 2 + 1 - core]
    line = [8, 16]
    further = [32 << b for b in range((lax.axis_size("dp") // 8).bit_length() - 1)]
    piece = core * 16 + doc * 4 + (far_off % 2) * 8 + (far_off // 2) % 4
    near = jnp.where(doc == 0, inputs[0], inputs[1])
    far_send = jnp.where(doc == 0, inputs[1], inputs[0])
    near, far_send = wait(near, far_send)
    far = exchange(far_send, ROW)
    near_other = exchange(near, CORE)
    slot = jnp.arange(8, dtype=jnp.int32)
    ids = jnp.zeros_like(slot)
    for i, value in enumerate([b * rows for b in block] + [piece, core, doc]):
        ids = jnp.where(slot == i, value, ids)
    gain1, gain2, gain3 = norm1_gain[None, :], norm2_gain[None, :], final_gain[None, :]
    buckets = bucket_table[None, :]
    hid_l, q_l, k_l, v_l, lines, info = prepare(ids, pad_len, prefix_len, near, near_other, w_query, w_key, w_value, gain1, bias_table, buckets)
    far, info = wait(far, info)
    far_other = exchange(far, CORE)
    (hid_r, q_r, k_r, v_r, expo, inverse, attended, send, active, slopes, turned, mixed, steep, dense_rows) = front(
        info, far, far_other, near, q_l, k_l, v_l, lines, w_query, w_key, w_value, gain1, gain2, gain3, pooled_grad, w_out, w_in, w_back)

    xy = [ROW, NEAR_X, ROW ^ NEAR_X]
    zz = [line[0], line[1], line[0] ^ line[1]]

    token, send = wait(info, send)
    got = exchange(send, CORE)
    keep, grad_mixed, grad_out_w, grad_attended, through_rows = through(token, slopes, w_in, mixed, steep, w_out, attended, active, turned, gain2)
    token, through_rows, got = wait(token, through_rows, got)

    sends = [added(keep[4 * k : 4 * k + 4], got[4 * k : 4 * k + 4]) for k in (3, 1, 2)]
    came = [exchange(s, m) for s, m in zip(sends, (xy[2], xy[0], xy[1]))]
    token, sends = wait(token, sends)
    rest_keep, rest_send, stay, leave, small = back(
        token, q_l, q_r, k_l, k_r, v_l, v_r, grad_attended, attended, inverse, expo, buckets, dense_rows, through_rows,
        hid_l, hid_r, near, near_other, far, far_other, w_query, w_key, w_value, grad_out_w)
    token, small, rest_send, leave, came = wait(token, small, rest_send, leave, came)

    rest_got = exchange(rest_send, CORE)
    hidden_got = exchange(leave, CORE)
    lines = mix([keep, got] + list(came))
    token, lines = wait(token, lines)
    took = [exchange(lines[k + 1], m) for k, m in enumerate(zz)]
    token, rest_got, hidden_got = wait(token, rest_got, hidden_got)

    count = rest_keep.shape[0] * rest_keep.shape[1]
    small = small + one_value(rest_got[count:])
    rest_got = rest_got[:count].reshape(rest_keep.shape)
    terms = two_terms(small)
    sends = [jnp.concatenate([added(rest_keep[4 * k : 4 * k + 4], rest_got[4 * k : 4 * k + 4]).reshape(-1, width), terms]) for k in (1, 2, 3)]
    token, sends = wait(token, sends)
    rest_came = [exchange(s, m) for s, m in zip(sends, xy)]
    home, away = ending(token, stay, hidden_got, near, far, grad_mixed, gain1, dense_rows)
    token, took, away = wait(token, took, away)

    whole = added(lines[0], *took)
    for bit in further:
        whole = added(whole, exchange(whole, bit))
    token, whole = wait(token, whole)
    back_line = [exchange(whole, m) for m in zz]
    away_got = exchange(away, ROW)
    token, rest_came = wait(token, rest_came)

    count = count // 4
    for part in rest_came:
        small = small + one_value(part[count:])
    rest_came = [part[:count].reshape((4,) + rest_keep.shape[1:]) for part in rest_came]
    terms = two_terms(small)
    lines = [added(rest_keep[k], rest_got[k], *[c[k] for c in rest_came]) for k in range(4)]
    sends = [jnp.concatenate([lines[k], terms]) for k in (1, 2, 3)]
    token, sends = wait(token, sends)
    took = [exchange(s, m) for s, m in zip(sends, zz)]
    token, back_line = wait(token, back_line)

    quarter = jnp.stack([whole] + back_line)
    token, quarter = wait(token, quarter)
    quarters = [exchange(quarter, m) for m in xy]
    token, took = wait(token, took)

    count = count // 4
    for part in took:
        small = small + one_value(part[count:])
    rest = added(lines[0], *[part[:count] for part in took])
    for bit in further:
        rest = added(rest, exchange(rest, bit))
        small = small + exchange(small, bit)
    token, rest = wait(token, rest)
    back_line = [exchange(rest, m) for m in zz]
    token, back_line = wait(token, back_line)
    rest_quarter = jnp.stack([rest] + back_line)
    token, rest_quarter = wait(token, rest_quarter)
    rest_quarters = [exchange(rest_quarter, m) for m in xy]

    token, quarters = wait(token, quarters)
    mine = [quarter] + quarters
    others = [exchange(value, CORE) for value in mine]
    out_big = place(token, 0, mine, [], width)
    token, out_big, others = wait(token, out_big, others)
    out_back, out_in = place(token, 1, others, out_big, width)
    token, out_back, out_in, rest_quarters, away_got = wait(token, out_back, out_in, rest_quarters, away_got)
    mine = [rest_quarter] + rest_quarters
    others = [exchange(value, CORE) for value in mine]
    out_rest = sort(token, 0, mine, [], width)
    token, out_rest, others = wait(token, out_rest, others)
    out_out, out_query, out_key, out_value = sort(token, 1, others, out_rest, width)

    pool_mine, pool_other = one_value(home[rows:])[:1], one_value(away_got[rows:])[:1]
    pooled = jnp.where(doc == 0, jnp.concatenate([pool_mine, pool_other]), jnp.concatenate([pool_other, pool_mine]))
    home, away_got = home[:rows], away_got[:rows]
    input_grad = jnp.where(doc == 0, jnp.stack([home, away_got]), jnp.stack([away_got, home]))
    return (
        pooled,
        input_grad,
        out_query,
        out_key,
        out_value,
        out_out,
        out_in,
        out_back,
        small[0],
        small[1],
        small[2],
        small[8:, :BUCKETS].T,
    )

def solution(mesh):
    data = P("dp", "blk", None)
    placed = (data,) + (P(),) * 11 + (P("dp"), P("dp"), P("dp", None))
    return jax.shard_map(local, mesh=mesh, in_specs=placed, out_specs=(P("dp", None), data) + (P(),) * 10, check_vma=False)
```

profile of v0, /device:TPU:0, one launch (start us, length us, event | category | flops | bytes accessed | tf_op | source)
XLA Modules:
  0.0 166.7 jit_solution(11682151773130924564)
XLA Ops:
  2.3 2.6 %collective-permute-start = (bf16[256,512]{1,0:T(8,128)(2,1)S(1)}, bf16[256,512]{1,0:T(8,128)(2,1)S(1)}, u32[]{:S(2)}, u32[]{:S(2)}) collective-permute-start(bf16[256,512]{1,0:T(8,128)(2,1)S(1)} %get-tuple-element.149), channel_id=1, source_target_pairs={{0,2},{1,3},{2,0},{3,1},{4,6},{5,7},{6,4},{7,5},{8,10},{9,11},{10,... | collective-permute-start | bytes 786440 | tf_op jit(solution)/shard_map/ppermute | solution.py:562
  7.4 3.3 %prepare.1 = (bf16[512,512]{1,0:T(8,128)(2,1)}, bf16[256,512]{1,0:T(8,128)(2,1)}, bf16[512,512]{1,0:T(8,128)(2,1)}, bf16[512,512]{1,0:T(8,128)(2,1)}, f32[8,2048]{1,0:T(8,128)}, /*index=5*/s32[16]{0:T(128)}) custom-call(s32[8]{0:T(128)} %compare_select_fusion.6.ids, s32[2]{0:T(128)} %pads.1, s32[2]{0:T(128)} %prefixes.1, bf16[256,512]{1,0:T(8,128)(2,1)} %copy-done, ...), custom_call_target="tpu_custom_call" | custom-call | tf_op jit(solution)/shard_map/prepare/pallas_call | solution.py:76
  11.8 1.5 collective-permute-done.2.far_other.far_other_h
  14.0 24.4 %front.1 = (bf16[512,512]{1,0:T(8,128)(2,1)}, bf16[256,512]{1,0:T(8,128)(2,1)}, bf16[512,512]{1,0:T(8,128)(2,1)}, bf16[512,512]{1,0:T(8,128)(2,1)}, bf16[8,512,1...) custom-call(s32[16]{0:T(128)} %get-tuple-element.271.info, ...), custom_call_target="tpu_custom_call" | custom-call | tf_op jit(solution)/shard_map/front/pallas_call | solution.py:236
  38.8 10.2 %through.1 = (bf16[16,512,128]{2,1,0:T(8,128)(2,1)}, f32[512,512]{1,0:T(8,128)}, bf16[512,512]{1,0:T(8,128)(2,1)}, bf16[512,512]{1,0:T(8,128)(2,1)}, f32[8,512]{1,0:T(8,128)}) custom-call(s32[16]{0:T(128)} %get-tuple-element.271.info, bf16[512,2048]{1,0:T(8,128)(2,1)} %get-tuple-element.160.slopes_h, bf16[512,2048]{1,0:T(8,128)(2,1)} %win_h.3, ...), custom_call_target="tpu_custom_call" | custom-call | tf_op jit(solution)/shard_map/through/pallas_call | solution.py:297
  49.1 3.3 %add_convert_fusion = (bf16[4,512,128]{2,1,0:T(8,128)(2,1)}, bf16[4,512,128]{2,1,0:T(8,128)(2,1)S(1)}, bf16[4,512,128]{2,1,0:T(8,128)(2,1)S(1)}) fusion(bf16[16,512,128]{2,1,0:T(8,128)(2,1)S(1)} %collective-permute-done.3.refs_1_, bf16[16,512,128]{2,1,0:T(8,128)(2,1)} %get-tuple-element.169.refs_0_), kind=kLoop, calls=%fused_computation | loop fusion | flops 3145728 | bytes 4718592 | tf_op jit(solution)/shard_map/convert_element_type | solution.py:571
  52.4 1.7 %collective-permute-start.6 = (bf16[4,512,128]{2,1,0:T(8,128)(2,1)}, bf16[4,512,128]{2,1,0:T(8,128)(2,1)S(1)}, u32[]{:S(2)}, u32[]{:S(2)}) collective-permute-start(bf16[4,512,128]{2,1,0:T(8,128)(2,1)} %get-tuple-element.291), channel_id=1, source_target_pairs={{0,4},{1,5},{2,6},{3,7},{4,0},{5,1},{6,2},{7,3},{8,12},{9,13},{10,... | collective-permute-start | bytes 1572872 | tf_op jit(solution)/shard_map/ppermute | solution.py:562
  54.1 1.5 collective-permute-start.5
  55.9 20.7 %back.1 = (bf16[16,64,512]{2,1,0:T(8,128)(2,1)}, bf16[1056,512]{1,0:T(8,128)(2,1)}, f32[512,512]{1,0:T(8,128)}, bf16[544,512]{1,0:T(8,128)(2,1)}, f32[16,512]{1,0:T(8,128)}) custom-call(s32[16]{0:T(128)} %get-tuple-element.271.info, bf16[256,512]{1,0:T(8,128)(2,1)} %get-tuple-element.154.q_l.ql, bf16[256,512]{1,0:T(8,128)(2,1)} %get-tuple-element.172.qr, ...), custom_call_target="tpu_custom_call" | custom-call | tf_op jit(solution)/shard_map/back/pallas_call | solution.py:436
  80.2 2.6 %mix.1 = (bf16[512,128]{1,0:T(8,128)(2,1)}, bf16[512,128]{1,0:T(8,128)(2,1)}, bf16[512,128]{1,0:T(8,128)(2,1)}, bf16[512,128]{1,0:T(8,128)(2,1)}) custom-call(bf16[16,512,128]{2,1,0:T(8,128)(2,1)} %get-tuple-element.169.refs_0_, bf16[16,512,128]{2,1,0:T(8,128)(2,1)} %copy-done.1, bf16[4,512,128]{2,1,0:T(8,128)(2,1)} %copy-done.14, ...), custom_call_target="tpu_custom_call" | custom-call | tf_op jit(solution)/shard_map/mix/pallas_call | solution.py:555
  82.8 1.6 collective-permute-start.9
  84.4 2.6 %collective-permute-start.10 = (bf16[512,128]{1,0:T(8,128)(2,1)}, bf16[512,128]{1,0:T(8,128)(2,1)}, u32[]{:S(2)}, u32[]{:S(2)}) collective-permute-start(bf16[512,128]{1,0:T(8,128)(2,1)} %get-tuple-element.207), channel_id=1, source_target_pairs={{0,16},{1,17},{2,18},{3,19},{4,20},{5,21},{6,22},{7,23},{8,24},{9,... | collective-permute-start | bytes 393224 | tf_op jit(solution)/shard_map/ppermute | solution.py:562
  88.5 1.7 %collective-permute-start.12 = (bf16[288,512]{1,0:T(8,128)(2,1)}, bf16[288,512]{1,0:T(8,128)(2,1)S(1)}, u32[]{:S(2)}, u32[]{:S(2)}) collective-permute-start(bf16[288,512]{1,0:T(8,128)(2,1)} %get-tuple-element.216), channel_id=1, source_target_pairs={{0,2},{1,3},{2,0},{3,1},{4,6},{5,7},{6,4},{7,5},{8,10},{9,11},{10,... | collective-permute-start | bytes 884744 | tf_op jit(solution)/shard_map/ppermute | solution.py:562
  92.0 3.2 %ending.1 = (bf16[288,512]{1,0:T(8,128)(2,1)}, bf16[288,512]{1,0:T(8,128)(2,1)}) custom-call(s32[16]{0:T(128)} %get-tuple-element.271.info, f32[512,512]{1,0:T(8,128)} %get-tuple-element.202.stay, bf16[544,512]{1,0:T(8,128)(2,1)} %copy-done.8, bf16[256,512]{1,0:T(8,128)(2,1)} %copy-done, bf16[256,512]{1,0:T(8,128)(2,1)} %copy-done.2, ...), custom_call_target="tpu_custom_call" | custom-call | tf_op jit(solution)/shard_map/ending/pallas_call | solution.py:472
  95.2 2.4 %collective-permute-done.10 = bf16[512,128]{1,0:T(8,128)(2,1)} collective-permute-done((bf16[512,128]{1,0:T(8,128)(2,1)}, bf16[512,128]{1,0:T(8,128)(2,1)}, u32[]{:S(2)}, u32[]{:S(2)}) %collective-permute-start.10) | collective-permute-done | bytes 131104 | tf_op jit(solution)/shard_map/ppermute | solution.py:562
  98.8 2.5 %collective-permute-start.17 = (bf16[512,128]{1,0:T(8,128)(2,1)S(1)}, bf16[512,128]{1,0:T(8,128)(2,1)S(1)}, u32[]{:S(2)}, u32[]{:S(2)}) collective-permute-start(bf16[512,128]{1,0:T(8,128)(2,1)S(1)} %add_convert_fusion.3), channel_id=1, source_target_pairs={{0,24},{1,25},{2,26},{3,27},{4,28},{5,29},{6,30},{7,31},{8,16},{9,... | collective-permute-start | bytes 393224 | tf_op jit(solution)/shard_map/ppermute | solution.py:562
  104.6 2.5 %collective-permute-done.17 = bf16[512,128]{1,0:T(8,128)(2,1)S(1)} collective-permute-done((bf16[512,128]{1,0:T(8,128)(2,1)S(1)}, bf16[512,128]{1,0:T(8,128)(2,1)S(1)}, u32[]{:S(2)}, u32[]{:S(2)}) %collective-permute-start.17) | collective-permute-done | bytes 131104 | tf_op jit(solution)/shard_map/ppermute | solution.py:562
  107.1 5.1 %collective-permute-done.16 = bf16[512,128]{1,0:T(8,128)(2,1)S(1)} collective-permute-done((bf16[512,128]{1,0:T(8,128)(2,1)S(1)}, bf16[512,128]{1,0:T(8,128)(2,1)S(1)}, u32[]{:S(2)}, u32[]{:S(2)}) %collective-permute-start.16) | collective-permute-done | bytes 131104 | tf_op jit(solution)/shard_map/ppermute | solution.py:562
  112.2 3.0 %collective-permute-start.19 = (bf16[96,512]{1,0:T(8,128)(2,1)S(1)}, bf16[96,512]{1,0:T(8,128)(2,1)S(1)}, u32[]{:S(2)}, u32[]{:S(2)}) collective-permute-start(bf16[96,512]{1,0:T(8,128)(2,1)S(1)} %get-tuple-element.231), channel_id=1, source_target_pairs={{0,16},{1,17},{2,18},{3,19},{4,20},{5,21},{6,22},{7,23},{8,24},{9,... | collective-permute-start | bytes 294920 | tf_op jit(solution)/shard_map/ppermute | solution.py:562
  116.7 1.6 collective-permute-start.26
  118.3 1.7 collective-permute-start.25
  120.3 2.3 %collective-permute-done.19 = bf16[96,512]{1,0:T(8,128)(2,1)S(1)} collective-permute-done((bf16[96,512]{1,0:T(8,128)(2,1)S(1)}, bf16[96,512]{1,0:T(8,128)(2,1)S(1)}, u32[]{:S(2)}, u32[]{:S(2)}) %collective-permute-start.19) | collective-permute-done | bytes 98336 | tf_op jit(solution)/shard_map/ppermute | solution.py:562
  123.5 2.5 %collective-permute-start.23 = (bf16[64,512]{1,0:T(8,128)(2,1)S(1)}, bf16[64,512]{1,0:T(8,128)(2,1)S(1)}, u32[]{:S(2)}, u32[]{:S(2)}) collective-permute-start(bf16[64,512]{1,0:T(8,128)(2,1)S(1)} %add_convert_fusion.4), channel_id=1, source_target_pairs={{0,24},{1,25},{2,26},{3,27},{4,28},{5,29},{6,30},{7,31},{8,16},{9,... | collective-permute-start | bytes 196616 | tf_op jit(solution)/shard_map/ppermute | solution.py:562
  126.7 3.1 %collective-permute-done.23 = bf16[64,512]{1,0:T(8,128)(2,1)S(1)} collective-permute-done((bf16[64,512]{1,0:T(8,128)(2,1)S(1)}, bf16[64,512]{1,0:T(8,128)(2,1)S(1)}, u32[]{:S(2)}, u32[]{:S(2)}) %collective-permute-start.23) | collective-permute-done | bytes 65568 | tf_op jit(solution)/shard_map/ppermute | solution.py:562
  131.7 1.7 %collective-permute-start.34 = (bf16[288,512]{1,0:T(8,128)(2,1)}, bf16[288,512]{1,0:T(8,128)(2,1)S(1)}, u32[]{:S(2)}, u32[]{:S(2)}) collective-permute-start(bf16[288,512]{1,0:T(8,128)(2,1)} %get-tuple-element.261), channel_id=1, source_target_pairs={{0,2},{1,3},{2,0},{3,1},{4,6},{5,7},{6,4},{7,5},{8,10},{9,11},{10,... | collective-permute-start | bytes 884744 | tf_op jit(solution)/shard_map/ppermute | solution.py:562
  134.1 6.4 %collective-permute-done.25.refs_2_ = bf16[4,512,128]{2,1,0:T(8,128)(2,1)S(1)} collective-permute-done((bf16[4,512,128]{2,1,0:T(8,128)(2,1)S(1)}, bf16[4,512,128]{2,1,0:T(8,128)(2,1)S(1)}, u32[]{:S(2)}, u32[]{:S(2)}) %collective-permute-start.25) | collective-permute-done | bytes 524320 | tf_op jit(solution)/shard_map/ppermute | solution.py:562
  142.6 1.6 collective-permute-start.32
  146.6 3.7 %place.2 = (f32[2048,512]{1,0:T(8,128)}, f32[512,2048]{1,0:T(8,128)}) custom-call(s32[16]{0:T(128)} %get-tuple-element.271.info, bf16[4,512,128]{2,1,0:T(8,128)(2,1)} %copy-done.3, bf16[4,512,128]{2,1,0:T(8,128)(2,1)} %copy-done.11, bf16[4,512,128]{2,1,0:T(8,128)(2,1)} %copy-done.10, bf16[4,512,128]{2,1,0:T(8,128)(2,1)} %copy-done.9), custom_call_target="tpu_custom_call" | custom-call | tf_op jit(solution)/shard_map/place/pallas_call | solution.py:506
  150.4 3.7 %place.3 = (f32[2048,512]{1,0:T(8,128)}, f32[512,2048]{1,0:T(8,128)}) custom-call(s32[16]{0:T(128)} %get-tuple-element.271.info, bf16[4,512,128]{2,1,0:T(8,128)(2,1)} %copy-done.15, bf16[4,512,128]{2,1,0:T(8,128)(2,1)} %copy-done.16, bf16[4,512,128]{2,1,0:T(8,128)(2,1)} %copy-done.17, ...), custom_call_target="tpu_custom_call", output_to_operand_aliasing={{0}: (5, {}), {1}: (6, {})} | custom-call | tf_op jit(solution)/shard_map/place/pallas_call | solution.py:506
  154.2 2.5 %collective-permute-done.32.refs_2_ = bf16[4,64,512]{2,1,0:T(8,128)(2,1)} collective-permute-done((bf16[4,64,512]{2,1,0:T(8,128)(2,1)S(1)}, bf16[4,64,512]{2,1,0:T(8,128)(2,1)}, u32[]{:S(2)}, u32[]{:S(2)}) %collective-permute-start.32) | collective-permute-done | bytes 262176 | tf_op jit(solution)/shard_map/ppermute | solution.py:562
  158.6 2.8 %sort.2 = (f32[512,512]{1,0:T(8,128)}, f32[512,512]{1,0:T(8,128)}, f32[512,512]{1,0:T(8,128)}, f32[512,512]{1,0:T(8,128)}) custom-call(s32[16]{0:T(128)} %get-tuple-element.271.info, bf16[4,64,512]{2,1,0:T(8,128)(2,1)} %copy-done.7, bf16[4,64,512]{2,1,0:T(8,128)(2,1)} %collective-permute-done.31.refs_1_, ...), custom_call_target="tpu_custom_call" | custom-call | tf_op jit(solution)/shard_map/sort/pallas_call | solution.py:536
  163.8 2.8 %sort.3 = (f32[512,512]{1,0:T(8,128)}, f32[512,512]{1,0:T(8,128)}, f32[512,512]{1,0:T(8,128)}, f32[512,512]{1,0:T(8,128)}) custom-call(s32[16]{0:T(128)} %get-tuple-element.271.info, bf16[4,64,512]{2,1,0:T(8,128)(2,1)} %copy-done.21, bf16[4,64,512]{2,1,0:T(8,128)(2,1)} %copy-done.22, ...), custom_call_target="tpu_custom_call", output_to_operand_aliasing={{0}: (5, {}), {1}: (6, {}), {2}: (7, {}), {3}: (8, {})} | custom-call | tf_op jit(solution)/shard_map/sort/pallas_call | solution.py:536
  (136 shorter events, 32.7 us)
Async XLA Ops:
  1.7 5.0 %collective-permute-start.1 = (bf16[256,512]{1,0:T(8,128)(2,1)S(1)}, bf16[256,512]{1,0:T(8,128)(2,1)S(1)}, u32[]{:S(2)}, u32[]{:S(2)}) collective-permute-start(bf16[256,512]{1,0:T(8,128)(2,1)S(1)} %get-tuple-element.150.mine.near.near_h), channel_id=1, source_target_pairs={{0,1},{1,0},{2,3},{3,2},{4,5},{5,4},{6,7},{7,6},{8,9},{9,8},{10,11... | collective-permute-start | bytes 786440 | tf_op jit(solution)/shard_map/ppermute | solution.py:562
  2.3 9.5 %collective-permute-start = (bf16[256,512]{1,0:T(8,128)(2,1)S(1)}, bf16[256,512]{1,0:T(8,128)(2,1)S(1)}, u32[]{:S(2)}, u32[]{:S(2)}) collective-permute-start(bf16[256,512]{1,0:T(8,128)(2,1)S(1)} %get-tuple-element.149), channel_id=1, source_target_pairs={{0,2},{1,3},{2,0},{3,1},{4,6},{5,7},{6,4},{7,5},{8,10},{9,11},{10,... | collective-permute-start | bytes 786440 | tf_op jit(solution)/shard_map/ppermute | solution.py:562
  38.4 10.6 %collective-permute-start.3 = (bf16[16,512,128]{2,1,0:T(8,128)(2,1)}, bf16[16,512,128]{2,1,0:T(8,128)(2,1)S(1)}, u32[]{:S(2)}, u32[]{:S(2)}) collective-permute-start(bf16[16,512,128]{2,1,0:T(8,128)(2,1)} %get-tuple-element.167), channel_id=1, source_target_pairs={{0,1},{1,0},{2,3},{3,2},{4,5},{5,4},{6,7},{7,6},{8,9},{9,8},{10,11... | collective-permute-start | bytes 6291464 | tf_op jit(solution)/shard_map/ppermute | solution.py:562
  52.4 24.2 %collective-permute-start.6 = (bf16[4,512,128]{2,1,0:T(8,128)(2,1)}, bf16[4,512,128]{2,1,0:T(8,128)(2,1)S(1)}, u32[]{:S(2)}, u32[]{:S(2)}) collective-permute-start(bf16[4,512,128]{2,1,0:T(8,128)(2,1)} %get-tuple-element.291), channel_id=1, source_target_pairs={{0,4},{1,5},{2,6},{3,7},{4,0},{5,1},{6,2},{7,3},{8,12},{9,13},{10,... | collective-permute-start | bytes 1572872 | tf_op jit(solution)/shard_map/ppermute | solution.py:562
  54.1 23.8 %collective-permute-start.5 = (bf16[4,512,128]{2,1,0:T(8,128)(2,1)S(1)}, bf16[4,512,128]{2,1,0:T(8,128)(2,1)S(1)}, u32[]{:S(2)}, u32[]{:S(2)}) collective-permute-start(bf16[4,512,128]{2,1,0:T(8,128)(2,1)S(1)} %get-tuple-element.292), channel_id=1, source_target_pairs={{0,2},{1,3},{2,0},{3,1},{4,6},{5,7},{6,4},{7,5},{8,10},{9,11},{10,... | collective-permute-start | bytes 1572872 | tf_op jit(solution)/shard_map/ppermute | solution.py:562
  55.7 23.2 %collective-permute-start.4 = (bf16[4,512,128]{2,1,0:T(8,128)(2,1)S(1)}, bf16[4,512,128]{2,1,0:T(8,128)(2,1)S(1)}, u32[]{:S(2)}, u32[]{:S(2)}) collective-permute-start(bf16[4,512,128]{2,1,0:T(8,128)(2,1)S(1)} %get-tuple-element.293), channel_id=1, source_target_pairs={{0,6},{1,7},{2,4},{3,5},{4,2},{5,3},{6,0},{7,1},{8,14},{9,15},{10,... | collective-permute-start | bytes 1572872 | tf_op jit(solution)/shard_map/ppermute | solution.py:562
  79.7 7.6 %collective-permute-start.7 = (bf16[1056,512]{1,0:T(8,128)(2,1)}, bf16[1056,512]{1,0:T(8,128)(2,1)S(1)}, u32[]{:S(2)}, u32[]{:S(2)}) collective-permute-start(bf16[1056,512]{1,0:T(8,128)(2,1)} %get-tuple-element.195), channel_id=1, source_target_pairs={{0,1},{1,0},{2,3},{3,2},{4,5},{5,4},{6,7},{7,6},{8,9},{9,8},{10,11... | collective-permute-start | bytes 3244040 | tf_op jit(solution)/shard_map/ppermute | solution.py:562
  79.7 7.5 %collective-permute-start.8 = (bf16[544,512]{1,0:T(8,128)(2,1)}, bf16[544,512]{1,0:T(8,128)(2,1)S(1)}, u32[]{:S(2)}, u32[]{:S(2)}) collective-permute-start(bf16[544,512]{1,0:T(8,128)(2,1)} %get-tuple-element.196), channel_id=1, source_target_pairs={{0,1},{1,0},{2,3},{3,2},{4,5},{5,4},{6,7},{7,6},{8,9},{9,8},{10,11... | collective-permute-start | bytes 1671176 | tf_op jit(solution)/shard_map/ppermute | solution.py:562
  82.8 7.7 %collective-permute-start.9 = (bf16[512,128]{1,0:T(8,128)(2,1)}, bf16[512,128]{1,0:T(8,128)(2,1)}, u32[]{:S(2)}, u32[]{:S(2)}) collective-permute-start(bf16[512,128]{1,0:T(8,128)(2,1)} %get-tuple-element.206), channel_id=1, source_target_pairs={{0,8},{1,9},{2,10},{3,11},{4,12},{5,13},{6,14},{7,15},{8,0},{9,1},... | collective-permute-start | bytes 393224 | tf_op jit(solution)/shard_map/ppermute | solution.py:562
  84.4 13.2 %collective-permute-start.10 = (bf16[512,128]{1,0:T(8,128)(2,1)}, bf16[512,128]{1,0:T(8,128)(2,1)}, u32[]{:S(2)}, u32[]{:S(2)}) collective-permute-start(bf16[512,128]{1,0:T(8,128)(2,1)} %get-tuple-element.207), channel_id=1, source_target_pairs={{0,16},{1,17},{2,18},{3,19},{4,20},{5,21},{6,22},{7,23},{8,24},{9,... | collective-permute-start | bytes 393224 | tf_op jit(solution)/shard_map/ppermute | solution.py:562
  87.0 10.6 %collective-permute-start.11 = (bf16[512,128]{1,0:T(8,128)(2,1)}, bf16[512,128]{1,0:T(8,128)(2,1)}, u32[]{:S(2)}, u32[]{:S(2)}) collective-permute-start(bf16[512,128]{1,0:T(8,128)(2,1)} %get-tuple-element.208), channel_id=1, source_target_pairs={{0,24},{1,25},{2,26},{3,27},{4,28},{5,29},{6,30},{7,31},{8,16},{9,... | collective-permute-start | bytes 393224 | tf_op jit(solution)/shard_map/ppermute | solution.py:562
  88.5 14.0 %collective-permute-start.12 = (bf16[288,512]{1,0:T(8,128)(2,1)}, bf16[288,512]{1,0:T(8,128)(2,1)S(1)}, u32[]{:S(2)}, u32[]{:S(2)}) collective-permute-start(bf16[288,512]{1,0:T(8,128)(2,1)} %get-tuple-element.216), channel_id=1, source_target_pairs={{0,2},{1,3},{2,0},{3,1},{4,6},{5,7},{6,4},{7,5},{8,10},{9,11},{10,... | collective-permute-start | bytes 884744 | tf_op jit(solution)/shard_map/ppermute | solution.py:562
  90.2 13.1 %collective-permute-start.13 = (bf16[288,512]{1,0:T(8,128)(2,1)}, bf16[288,512]{1,0:T(8,128)(2,1)S(1)}, u32[]{:S(2)}, u32[]{:S(2)}) collective-permute-start(bf16[288,512]{1,0:T(8,128)(2,1)} %get-tuple-element.217), channel_id=1, source_target_pairs={{0,4},{1,5},{2,6},{3,7},{4,0},{5,1},{6,2},{7,3},{8,12},{9,13},{10,... | collective-permute-start | bytes 884744 | tf_op jit(solution)/shard_map/ppermute | solution.py:562
  90.6 13.8 %collective-permute-start.14 = (bf16[288,512]{1,0:T(8,128)(2,1)S(1)}, bf16[288,512]{1,0:T(8,128)(2,1)S(1)}, u32[]{:S(2)}, u32[]{:S(2)}) collective-permute-start(bf16[288,512]{1,0:T(8,128)(2,1)S(1)} %get-tuple-element.218), channel_id=1, source_target_pairs={{0,6},{1,7},{2,4},{3,5},{4,2},{5,3},{6,0},{7,1},{8,14},{9,15},{10,... | collective-permute-start | bytes 884744 | tf_op jit(solution)/shard_map/ppermute | solution.py:562
  98.8 8.3 %collective-permute-start.17 = (bf16[512,128]{1,0:T(8,128)(2,1)S(1)}, bf16[512,128]{1,0:T(8,128)(2,1)S(1)}, u32[]{:S(2)}, u32[]{:S(2)}) collective-permute-start(bf16[512,128]{1,0:T(8,128)(2,1)S(1)} %add_convert_fusion.3), channel_id=1, source_target_pairs={{0,24},{1,25},{2,26},{3,27},{4,28},{5,29},{6,30},{7,31},{8,16},{9,... | collective-permute-start | bytes 393224 | tf_op jit(solution)/shard_map/ppermute | solution.py:562
  101.2 11.0 %collective-permute-start.16 = (bf16[512,128]{1,0:T(8,128)(2,1)S(1)}, bf16[512,128]{1,0:T(8,128)(2,1)S(1)}, u32[]{:S(2)}, u32[]{:S(2)}) collective-permute-start(bf16[512,128]{1,0:T(8,128)(2,1)S(1)} %add_convert_fusion.3), channel_id=1, source_target_pairs={{0,16},{1,17},{2,18},{3,19},{4,20},{5,21},{6,22},{7,23},{8,24},{9,... | collective-permute-start | bytes 393224 | tf_op jit(solution)/shard_map/ppermute | solution.py:562
  102.5 9.8 %collective-permute-start.15 = (bf16[512,128]{1,0:T(8,128)(2,1)S(1)}, bf16[512,128]{1,0:T(8,128)(2,1)S(1)}, u32[]{:S(2)}, u32[]{:S(2)}) collective-permute-start(bf16[512,128]{1,0:T(8,128)(2,1)S(1)} %add_convert_fusion.3), channel_id=1, source_target_pairs={{0,8},{1,9},{2,10},{3,11},{4,12},{5,13},{6,14},{7,15},{8,0},{9,1},... | collective-permute-start | bytes 393224 | tf_op jit(solution)/shard_map/ppermute | solution.py:562
  112.2 7.7 %collective-permute-start.18 = (bf16[96,512]{1,0:T(8,128)(2,1)S(1)}, bf16[96,512]{1,0:T(8,128)(2,1)S(1)}, u32[]{:S(2)}, u32[]{:S(2)}) collective-permute-start(bf16[96,512]{1,0:T(8,128)(2,1)S(1)} %get-tuple-element.230), channel_id=1, source_target_pairs={{0,8},{1,9},{2,10},{3,11},{4,12},{5,13},{6,14},{7,15},{8,0},{9,1},... | collective-permute-start | bytes 294920 | tf_op jit(solution)/shard_map/ppermute | solution.py:562
  112.2 10.3 %collective-permute-start.19 = (bf16[96,512]{1,0:T(8,128)(2,1)S(1)}, bf16[96,512]{1,0:T(8,128)(2,1)S(1)}, u32[]{:S(2)}, u32[]{:S(2)}) collective-permute-start(bf16[96,512]{1,0:T(8,128)(2,1)S(1)} %get-tuple-element.231), channel_id=1, source_target_pairs={{0,16},{1,17},{2,18},{3,19},{4,20},{5,21},{6,22},{7,23},{8,24},{9,... | collective-permute-start | bytes 294920 | tf_op jit(solution)/shard_map/ppermute | solution.py:562
  115.3 7.3 %collective-permute-start.20 = (bf16[96,512]{1,0:T(8,128)(2,1)S(1)}, bf16[96,512]{1,0:T(8,128)(2,1)S(1)}, u32[]{:S(2)}, u32[]{:S(2)}) collective-permute-start(bf16[96,512]{1,0:T(8,128)(2,1)S(1)} %get-tuple-element.232), channel_id=1, source_target_pairs={{0,24},{1,25},{2,26},{3,27},{4,28},{5,29},{6,30},{7,31},{8,16},{9,... | collective-permute-start | bytes 294920 | tf_op jit(solution)/shard_map/ppermute | solution.py:562
  116.7 17.4 %collective-permute-start.26 = (bf16[4,512,128]{2,1,0:T(8,128)(2,1)S(1)}, bf16[4,512,128]{2,1,0:T(8,128)(2,1)S(1)}, u32[]{:S(2)}, u32[]{:S(2)}) collective-permute-start(bf16[4,512,128]{2,1,0:T(8,128)(2,1)S(1)} %pad_maximum_fusion.refs_0_), channel_id=1, source_target_pairs={{0,6},{1,7},{2,4},{3,5},{4,2},{5,3},{6,0},{7,1},{8,14},{9,15},{10,... | collective-permute-start | bytes 1572872 | tf_op jit(solution)/shard_map/ppermute | solution.py:562
  118.3 22.2 %collective-permute-start.25 = (bf16[4,512,128]{2,1,0:T(8,128)(2,1)S(1)}, bf16[4,512,128]{2,1,0:T(8,128)(2,1)S(1)}, u32[]{:S(2)}, u32[]{:S(2)}) collective-permute-start(bf16[4,512,128]{2,1,0:T(8,128)(2,1)S(1)} %pad_maximum_fusion.refs_0_), channel_id=1, source_target_pairs={{0,4},{1,5},{2,6},{3,7},{4,0},{5,1},{6,2},{7,3},{8,12},{9,13},{10,... | collective-permute-start | bytes 1572872 | tf_op jit(solution)/shard_map/ppermute | solution.py:562
  119.9 20.6 %collective-permute-start.24 = (bf16[4,512,128]{2,1,0:T(8,128)(2,1)S(1)}, bf16[4,512,128]{2,1,0:T(8,128)(2,1)S(1)}, u32[]{:S(2)}, u32[]{:S(2)}) collective-permute-start(bf16[4,512,128]{2,1,0:T(8,128)(2,1)S(1)} %pad_maximum_fusion.refs_0_), channel_id=1, source_target_pairs={{0,2},{1,3},{2,0},{3,1},{4,6},{5,7},{6,4},{7,5},{8,10},{9,11},{10,... | collective-permute-start | bytes 1572872 | tf_op jit(solution)/shard_map/ppermute | solution.py:562
  123.5 6.2 %collective-permute-start.23 = (bf16[64,512]{1,0:T(8,128)(2,1)S(1)}, bf16[64,512]{1,0:T(8,128)(2,1)S(1)}, u32[]{:S(2)}, u32[]{:S(2)}) collective-permute-start(bf16[64,512]{1,0:T(8,128)(2,1)S(1)} %add_convert_fusion.4), channel_id=1, source_target_pairs={{0,24},{1,25},{2,26},{3,27},{4,28},{5,29},{6,30},{7,31},{8,16},{9,... | collective-permute-start | bytes 196616 | tf_op jit(solution)/shard_map/ppermute | solution.py:562
  126.0 5.7 %collective-permute-start.22 = (bf16[64,512]{1,0:T(8,128)(2,1)S(1)}, bf16[64,512]{1,0:T(8,128)(2,1)S(1)}, u32[]{:S(2)}, u32[]{:S(2)}) collective-permute-start(bf16[64,512]{1,0:T(8,128)(2,1)S(1)} %add_convert_fusion.4), channel_id=1, source_target_pairs={{0,16},{1,17},{2,18},{3,19},{4,20},{5,21},{6,22},{7,23},{8,24},{9,... | collective-permute-start | bytes 196616 | tf_op jit(solution)/shard_map/ppermute | solution.py:562
  131.7 22.5 %collective-permute-start.34 = (bf16[288,512]{1,0:T(8,128)(2,1)}, bf16[288,512]{1,0:T(8,128)(2,1)S(1)}, u32[]{:S(2)}, u32[]{:S(2)}) collective-permute-start(bf16[288,512]{1,0:T(8,128)(2,1)} %get-tuple-element.261), channel_id=1, source_target_pairs={{0,2},{1,3},{2,0},{3,1},{4,6},{5,7},{6,4},{7,5},{8,10},{9,11},{10,... | collective-permute-start | bytes 884744 | tf_op jit(solution)/shard_map/ppermute | solution.py:562
  134.0 7.2 %collective-permute-start.27 = (bf16[4,512,128]{2,1,0:T(8,128)(2,1)S(1)}, bf16[4,512,128]{2,1,0:T(8,128)(2,1)S(1)}, u32[]{:S(2)}, u32[]{:S(2)}) collective-permute-start(bf16[4,512,128]{2,1,0:T(8,128)(2,1)S(1)} %pad_maximum_fusion.refs_0_), channel_id=1, source_target_pairs={{0,1},{1,0},{2,3},{3,2},{4,5},{5,4},{6,7},{7,6},{8,9},{9,8},{10,11... | collective-permute-start | bytes 1572872 | tf_op jit(solution)/shard_map/ppermute | solution.py:562
  141.1 9.2 %collective-permute-start.30 = (bf16[4,512,128]{2,1,0:T(8,128)(2,1)S(1)}, bf16[4,512,128]{2,1,0:T(8,128)(2,1)}, u32[]{:S(2)}, u32[]{:S(2)}) collective-permute-start(bf16[4,512,128]{2,1,0:T(8,128)(2,1)S(1)} %collective-permute-done.26.refs_3_), channel_id=1, source_target_pairs={{0,1},{1,0},{2,3},{3,2},{4,5},{5,4},{6,7},{7,6},{8,9},{9,8},{10,11... | collective-permute-start | bytes 1572872 | tf_op jit(solution)/shard_map/ppermute | solution.py:562
  141.3 12.9 %collective-permute-start.33 = (bf16[4,64,512]{2,1,0:T(8,128)(2,1)S(1)}, bf16[4,64,512]{2,1,0:T(8,128)(2,1)}, u32[]{:S(2)}, u32[]{:S(2)}) collective-permute-start(bf16[4,64,512]{2,1,0:T(8,128)(2,1)S(1)} %pad_maximum_fusion.7.refs_0_), channel_id=1, source_target_pairs={{0,6},{1,7},{2,4},{3,5},{4,2},{5,3},{6,0},{7,1},{8,14},{9,15},{10,... | collective-permute-start | bytes 786440 | tf_op jit(solution)/shard_map/ppermute | solution.py:562
  142.6 14.1 %collective-permute-start.32 = (bf16[4,64,512]{2,1,0:T(8,128)(2,1)S(1)}, bf16[4,64,512]{2,1,0:T(8,128)(2,1)}, u32[]{:S(2)}, u32[]{:S(2)}) collective-permute-start(bf16[4,64,512]{2,1,0:T(8,128)(2,1)S(1)} %pad_maximum_fusion.7.refs_0_), channel_id=1, source_target_pairs={{0,4},{1,5},{2,6},{3,7},{4,0},{5,1},{6,2},{7,3},{8,12},{9,13},{10,... | collective-permute-start | bytes 786440 | tf_op jit(solution)/shard_map/ppermute | solution.py:562
  144.2 13.7 %collective-permute-start.31 = (bf16[4,64,512]{2,1,0:T(8,128)(2,1)S(1)}, bf16[4,64,512]{2,1,0:T(8,128)(2,1)}, u32[]{:S(2)}, u32[]{:S(2)}) collective-permute-start(bf16[4,64,512]{2,1,0:T(8,128)(2,1)S(1)} %pad_maximum_fusion.7.refs_0_), channel_id=1, source_target_pairs={{0,2},{1,3},{2,0},{3,1},{4,6},{5,7},{6,4},{7,5},{8,10},{9,11},{10,... | collective-permute-start | bytes 786440 | tf_op jit(solution)/shard_map/ppermute | solution.py:562
  150.3 12.5 %collective-permute-start.35 = (bf16[4,64,512]{2,1,0:T(8,128)(2,1)S(1)}, bf16[4,64,512]{2,1,0:T(8,128)(2,1)S(1)}, u32[]{:S(2)}, u32[]{:S(2)}) collective-permute-start(bf16[4,64,512]{2,1,0:T(8,128)(2,1)S(1)} %pad_maximum_fusion.7.refs_0_), channel_id=1, source_target_pairs={{0,1},{1,0},{2,3},{3,2},{4,5},{5,4},{6,7},{7,6},{8,9},{9,8},{10,11... | collective-permute-start | bytes 786440 | tf_op jit(solution)/shard_map/ppermute | solution.py:562
  (34 other events, 221.0 us)
where the time goes:
time: 167 us
  Pallas kernels  77.4 us (46%)
  starting transfers between devices  39.3 us (24%)
  waiting for transfers between devices  33 us (20%)
  other arithmetic  9.97 us (6%)
  local copies, waits for them, and re-layouts  5.88 us (4%)
    ppermute x39, starting transfers between devices, exchange(): lax.ppermute(value, ('dp', 'blk'), [(i, i ^ bits) for i in range(size)])  39.3 us
    ppermute x39, waiting for transfers between devices, exchange(): lax.ppermute(value, ('dp', 'blk'), [(i, i ^ bits) for i in range(size)])  33 us
    pallas_call x1, Pallas kernels, front(): pl.pallas_call(front_kernel, grid=(heads // 2,), in_specs=[smem, whole(co...  24.4 us
    pallas_call x1, Pallas kernels, back(): pl.pallas_call(back_kernel, grid=(width // 128,), in_specs=[smem, col(cou...  20.7 us
    pallas_call x1, Pallas kernels, through(): pl.pallas_call(through_kernel, in_specs=[smem] + [free] * 8 + [vmem], out...  10.2 us
    pallas_call x2, Pallas kernels, place(): pl.pallas_call(functools.partial(place_kernel, half), in_specs=[smem] + [...  7.4 us
    convert_element_type x5, other arithmetic, added(): return total.astype(BF16)  5.78 us
    pallas_call x2, Pallas kernels, sort(): pl.pallas_call(functools.partial(sort_kernel, half), in_specs=[smem] + [v...  5.52 us
  transfers between devices with their start and end apart: 39, of which 15 were waited for; matrix products, arithmetic and copies ran while one was open for 5% of the time, Pallas kernels for 30%

commit v1 on v0

--- a/solution.py
+++ b/solution.py
@@ -82,24 +82,20 @@
         name="prepare",
     )(ids, pads, prefixes, mine, other, wq, wk, wv, gain, bias, buckets)
 
-def swap_in(to, hidden, index, mine, made, columns):
-    for b in range(2):
-        if columns:
-            to[(2 * index + b) ^ mine] = made[:, b * 128 : (b + 1) * 128]
-        else:
-            to[(2 * index + b) ^ mine] = jnp.concatenate([made[b * 128 : (b + 1) * 128, q * 128 : (q + 1) * 128] for q in range(4)])
-
 def back_pieces(to, active, low, mine):
-    @pl.loop(0, active.shape[1] // 256)
-    def _(pair):
-        made = dot(active[:, pl.ds(pl.multiple_of(pair * 256, 256), 256)], low, TN).astype(BF16)
-        swap_in(to, active.shape[1], pair, mine, made, False)
+    @pl.loop(0, active.shape[1] // 512)
+    def _(group):
+        made = dot(active[:, pl.ds(pl.multiple_of(group * 512, 512), 512)], low, TN).astype(BF16)
+        for b in range(4):
+            rows = made[b * 128 : (b + 1) * 128]
+            to[(4 * group + b) ^ mine] = jnp.concatenate([rows[:, q * 128 : (q + 1) * 128] for q in range(4)])
 
 def in_pieces(to, slopes, turned, mine):
-    @pl.loop(0, slopes.shape[1] // 256)
-    def _(pair):
-        made = dot(turned, slopes[:, pl.ds(pl.multiple_of(pair * 256, 256), 256)]).astype(BF16)
-        swap_in(to, slopes.shape[1], pair, mine, made, True)
+    @pl.loop(0, slopes.shape[1] // 512)
+    def _(group):
+        made = dot(turned, slopes[:, pl.ds(pl.multiple_of(group * 512, 512), 512)]).astype(BF16)
+        for b in range(4):
+            to[(4 * group + b) ^ mine] = made[:, b * 128 : (b + 1) * 128]
 
 def front_kernel(info, far, far_other, near, q_l, k_l, v_l, lines, wq, wk, wv, gain1, gain2, gain3, cots, wo_h, win_h, wback_h,
                  hid_o, q_o, k_o, v_o, expo_o, inv_o, att_o, send_o, active_o, slopes_o, turned_o, mixed_o, steep_o, rows,
@@ -248,8 +244,9 @@
         name="front",
     )(info, far, far_other, near, q_l, k_l, v_l, lines, wq, wk, wv, gain1, gain2, gain3, cots, wo, win, wback)
 
-def through_kernel(info, slopes_h, win_h, mixed_h, steep_h, wo_h, att_h, active_h, turned_h, gain2, keep, grad_mixed, grad_out, grad_attended, rows,
-                   slopes, win, mixed, steep, wo, att, active, turned, sems):
+def through_kernel(info, slopes_h, win_h, mixed_h, steep_h, wo_h, att_h, active_h, turned_h, gain2,
+                   keep, grad_mixed_o, grad_attended_o, grad_out_o, rows,
+                   slopes, win, mixed, steep, wo, att, active, turned, grad_mixed, grad_attended, grad_out, sems):
     hidden, width = slopes.shape[1], mixed.shape[1]
     chunks = []
     for i, at in enumerate(range(0, hidden, 512)):
@@ -257,8 +254,19 @@
             chunks.append(pltpu.make_async_copy(a.at[:, at : at + 512], b.at[:, at : at + 512], sems.at[s]))
     copies = [pltpu.make_async_copy(a, b, sems.at[8 + i]) for i, (a, b) in enumerate((
         (mixed_h, mixed), (steep_h, steep), (wo_h, wo), (att_h, att), (active_h, active), (turned_h, turned)))]
-    for copy in chunks + copies:
+    outs = [pltpu.make_async_copy(a, b, sems.at[14 + i]) for i, (a, b) in enumerate((
+        (grad_mixed, grad_mixed_o), (grad_attended, grad_attended_o), (grad_out, grad_out_o)))]
+    for copy in chunks + copies[:4]:
         copy.start()
+
+    @pl.when(info[7] == 0)
+    def _():
+        copies[4].start()
+
+    @pl.when(info[7] == 1)
+    def _():
+        copies[5].start()
+
     grad_inner = None
     for i, at in enumerate(range(0, hidden, 512)):
         chunks[2 * i].wait()
@@ -271,35 +279,42 @@
     more, grad_two = norm_back(grad_inner, values, rms_scale(values), gain2[...])
     total = steep[...] + more
     grad_mixed[...] = total
+    outs[0].start()
     low = total.astype(BF16)
     copies[2].wait()
     grad_attended[...] = dot(low, wo[...], NT).astype(BF16)
+    outs[1].start()
     copies[3].wait()
     grad_out[...] = dot(att[...], low, TN).astype(BF16)
+    outs[2].start()
     rows[...] = jnp.concatenate([grad_two, jnp.zeros((7, width), F32)])
-    copies[4].wait()
-    copies[5].wait()
     mine = info[6] & 15
 
     @pl.when(info[7] == 0)
     def _():
+        copies[4].wait()
         back_pieces(keep, active, steep[...].astype(BF16), mine)
 
     @pl.when(info[7] == 1)
     def _():
+        copies[5].wait()
         in_pieces(keep, slopes, turned[...], mine)
+
+    for copy in outs:
+        copy.wait()
 
 def through(info, slopes, win, mixed, steep, wo, att, active, turned, gain2):
     n, width = mixed.shape
     smem, vmem, free = (pl.BlockSpec(memory_space=m) for m in (pltpu.SMEM, pltpu.VMEM, pl.ANY))
     shape = jax.ShapeDtypeStruct
     given = (slopes, win, mixed, steep, wo, att, active, turned)
+    outs = [shape((n, width), F32), shape((n, width), BF16), shape((width, width), BF16)]
     return pl.pallas_call(
         through_kernel,
         in_specs=[smem] + [free] * 8 + [vmem],
-        out_specs=[vmem] * 5,
-        out_shape=[shape((16, width, 128), BF16), shape((n, width), F32), shape((width, width), BF16), shape((n, width), BF16), shape((8, width), F32)],
-        scratch_shapes=[pltpu.VMEM(g.shape, g.dtype) for g in given] + [pltpu.SemaphoreType.DMA((14,))],
+        out_specs=[vmem] + [free] * 3 + [vmem],
+        out_shape=[shape((16, width, 128), BF16)] + outs + [shape((8, width), F32)],
+        scratch_shapes=[pltpu.VMEM(g.shape, g.dtype) for g in given] + [pltpu.VMEM(o.shape, o.dtype) for o in outs] + [pltpu.SemaphoreType.DMA((17,))],
         name="through",
     )(info, *given, gain2)
 
@@ -473,75 +488,83 @@
         ending_kernel, in_specs=[smem] + [vmem] * 7, out_specs=[vmem] * 2, out_shape=[shape, shape], name="ending"
     )(info, stay, came, near, far, grad_mixed, gain, dense_rows)
 
-def place_kernel(half, info, *refs):
-    parts, (back, front), (tall, sems) = refs[:4], refs[-4:-2], refs[-2:]
+def place_kernel(firsts, info, *refs):
+    parts, (back, front, rows, columns, sems) = refs[: len(firsts)], refs[-5:]
+    pieces = [(part, i, first + i) for part, first in zip(parts, firsts) for i in range(part.shape[0])]
     mine = info[6] & 15
-
-    @pl.when(info[7] == half)
-    def _():
-        copies = []
-        for r in range(16):
-            to = pl.ds(pl.multiple_of((r ^ mine) * 128, 128), 128)
-            for q in range(4):
-                tall[r, :128, q * 128 : (q + 1) * 128] = parts[r // 4][r % 4, q * 128 : (q + 1) * 128, :].astype(F32)
-            copies.append(pltpu.make_async_copy(tall.at[r, :128, :], back.at[to, :], sems.at[r]))
-            copies[-1].start()
-        for copy in copies:
-            copy.wait()
-
-    @pl.when(info[7] != half)
-    def _():
-        copies = []
-        for r in range(16):
-            to = pl.ds(pl.multiple_of((r ^ mine) * 128, 128), 128)
-            tall[r, :, :128] = parts[r // 4][r % 4].astype(F32)
-            copies.append(pltpu.make_async_copy(tall.at[r, :, :128], front.at[:, to], sems.at[r]))
-            copies[-1].start()
-        for copy in copies:
-            copy.wait()
-
-def place(info, half, parts, made, width):
+    for side in range(2):
+        @pl.when(info[7] == side)
+        def _(side=side):
+            copies = []
+            for n, (part, i, r) in enumerate(pieces):
+                to = pl.ds(pl.multiple_of(((r & 15) ^ mine) * 128, 128), 128)
+                if (r >= 16) == (side == 1):
+                    for q in range(4):
+                        rows[n, :, q * 128 : (q + 1) * 128] = part[i, q * 128 : (q + 1) * 128, :].astype(F32)
+                    copies.append(pltpu.make_async_copy(rows.at[n], back.at[to, :], sems.at[n]))
+                else:
+                    columns[n] = part[i].astype(F32)
+                    copies.append(pltpu.make_async_copy(columns.at[n], front.at[:, to], sems.at[n]))
+                copies[-1].start()
+            for copy in copies:
+                copy.wait()
+
+def place(info, parts, made, width):
     smem, vmem, free = (pl.BlockSpec(memory_space=m) for m in (pltpu.SMEM, pltpu.VMEM, pl.ANY))
     shape = jax.ShapeDtypeStruct
-    return pl.pallas_call(
-        functools.partial(place_kernel, half),
-        in_specs=[smem] + [vmem] * 4 + [free] * len(made),
+    count = sum(p.shape[0] for _, p in parts)
+    return pl.pallas_call(
+        functools.partial(place_kernel, [first for first, _ in parts]),
+        in_specs=[smem] + [vmem] * len(parts) + [free] * len(made),
         out_specs=[free] * 2,
         out_shape=[shape((16 * 128, width), F32), shape((width, 16 * 128), F32)],
-        scratch_shapes=[pltpu.VMEM((16, width, width), F32), pltpu.SemaphoreType.DMA((16,))],
-        input_output_aliases={5 + i: i for i in range(len(made))},
+        scratch_shapes=[pltpu.VMEM((count, 128, width), F32), pltpu.VMEM((count, width, 128), F32), pltpu.SemaphoreType.DMA((count,))],
+        input_output_aliases={1 + len(parts) + i: i for i in range(len(made))},
         name="place",
-    )(info, *parts, *made)
-
-def sort_kernel(half, info, *refs):
-    parts, made, (tall, sems) = refs[:4], refs[-6:-2], refs[-2:]
+    )(info, *[p for _, p in parts], *made)
+
+def sort_kernel(firsts, info, *refs):
+    parts, made, (tall, sems) = refs[: len(firsts)], refs[-6:-2], refs[-2:]
+    pieces = [(part, i, first + i) for part, first in zip(parts, firsts) for i in range(part.shape[0])]
     size = parts[0].shape[1]
-    per = tall.shape[1] // size
-    mine = info[6] & 15
-    for r in range(16):
-        to = r ^ mine
-        tall[to // per, pl.ds(pl.multiple_of((to % per) * size, size), size), :] = parts[r // 4][r % 4].astype(F32)
-    for top in range(2):
-        @pl.when((info[7] ^ half) == top)
+    mine = info[6]
+    for n, (part, i, r) in enumerate(pieces):
+        tall[n] = part[i].astype(F32)
+    for top in range(4):
+        @pl.when((mine >> 3) == top)
         def _(top=top):
-            copies = [pltpu.make_async_copy(tall.at[w], made[2 * top + w], sems.at[w]) for w in range(2)]
-            for copy in copies:
-                copy.start()
+            copies = []
+            for n, (part, i, r) in enumerate(pieces):
+                to = pl.ds(pl.multiple_of(((r ^ mine) & 7) * size, size), size)
+                copies.append(pltpu.make_async_copy(tall.at[n], made[top ^ (r >> 3)].at[to, :], sems.at[n]))
+                copies[-1].start()
             for copy in copies:
                 copy.wait()
 
-def sort(info, half, parts, made, width):
+def sort(info, parts, made, width):
     smem, vmem, free = (pl.BlockSpec(memory_space=m) for m in (pltpu.SMEM, pltpu.VMEM, pl.ANY))
     shape = jax.ShapeDtypeStruct((width, width), F32)
-    return pl.pallas_call(
-        functools.partial(sort_kernel, half),
-        in_specs=[smem] + [vmem] * 4 + [free] * len(made),
+    count = sum(p.shape[0] for _, p in parts)
+    return pl.pallas_call(
+        functools.partial(sort_kernel, [first for first, _ in parts]),
+        in_specs=[smem] + [vmem] * len(parts) + [free] * len(made),
         out_specs=[free] * 4,
         out_shape=[shape] * 4,
-        scratch_shapes=[pltpu.VMEM((2, width, width), F32), pltpu.SemaphoreType.DMA((2,))],
-        input_output_aliases={5 + i: i for i in range(len(made))},
+        scratch_shapes=[pltpu.VMEM((count,) + parts[0][1].shape[1:], F32), pltpu.SemaphoreType.DMA((count,))],
+        input_output_aliases={1 + len(parts) + i: i for i in range(len(made))},
         name="sort",
-    )(info, *parts, *made)
+    )(info, *[p for _, p in parts], *made)
+
+def spread_kernel(keep, got, out):
+    out[...] = added(keep[...], got[...])
+
+def spread(keep, got, k):
+    block = (1,) + keep.shape[1:]
+    spec = pl.BlockSpec(block, lambda i: (4 * k + i, 0, 0))
+    return pl.pallas_call(
+        spread_kernel, grid=(4,), in_specs=[spec, spec], out_specs=pl.BlockSpec(block, lambda i: (i, 0, 0)),
+        out_shape=jax.ShapeDtypeStruct((4,) + keep.shape[1:], BF16), name="spread",
+    )(keep, got)
 
 def mix_kernel(*refs):
     ins, outs = refs[: -4], refs[-4:]
@@ -600,10 +623,10 @@
 
     token, send = wait(info, send)
     got = exchange(send, CORE)
-    keep, grad_mixed, grad_out_w, grad_attended, through_rows = through(token, slopes, w_in, mixed, steep, w_out, attended, active, turned, gain2)
+    keep, grad_mixed, grad_attended, grad_out_w, through_rows = through(token, slopes, w_in, mixed, steep, w_out, attended, active, turned, gain2)
     token, through_rows, got = wait(token, through_rows, got)
 
-    sends = [added(keep[4 * k : 4 * k + 4], got[4 * k : 4 * k + 4]) for k in (3, 1, 2)]
+    sends = [spread(keep, got, k) for k in (3, 1, 2)]
     came = [exchange(s, m) for s, m in zip(sends, (xy[2], xy[0], xy[1]))]
     token, sends = wait(token, sends)
     rest_keep, rest_send, stay, leave, small = back(
@@ -648,8 +671,8 @@
     token, back_line = wait(token, back_line)
 
     quarter = jnp.stack([whole] + back_line)
-    token, quarter = wait(token, quarter)
-    quarters = [exchange(quarter, m) for m in xy]
+    token, quarter, away_got = wait(token, quarter, away_got)
+    from_y, from_x = exchange(quarter, ROW), exchange(quarter, NEAR_X)
     token, took = wait(token, took)
 
     count = count // 4
@@ -661,23 +684,30 @@
         small = small + exchange(small, bit)
     token, rest = wait(token, rest)
     back_line = [exchange(rest, m) for m in zz]
-    token, back_line = wait(token, back_line)
-    rest_quarter = jnp.stack([rest] + back_line)
-    token, rest_quarter = wait(token, rest_quarter)
-    rest_quarters = [exchange(rest_quarter, m) for m in xy]
-
-    token, quarters = wait(token, quarters)
-    mine = [quarter] + quarters
-    others = [exchange(value, CORE) for value in mine]
-    out_big = place(token, 0, mine, [], width)
-    token, out_big, others = wait(token, out_big, others)
-    out_back, out_in = place(token, 1, others, out_big, width)
-    token, out_back, out_in, rest_quarters, away_got = wait(token, out_back, out_in, rest_quarters, away_got)
-    mine = [rest_quarter] + rest_quarters
-    others = [exchange(value, CORE) for value in mine]
-    out_rest = sort(token, 0, mine, [], width)
-    token, out_rest, others = wait(token, out_rest, others)
-    out_out, out_query, out_key, out_value = sort(token, 1, others, out_rest, width)
+    token, back_line, from_y, from_x = wait(token, back_line, from_y, from_x)
+    fourth = jnp.stack([rest] + back_line)
+
+    sends = [from_x[:2], from_y[2:], fourth, fourth]
+    token, sends = wait(token, sends)
+    far_a, far_b, fourth_y, fourth_x = (exchange(s, m) for s, m in zip(sends, (ROW, NEAR_X, ROW, NEAR_X)))
+    grads = place(token, [(0, quarter), (4, from_y), (8, from_x)], [], width)
+    token, grads, quarter, from_y, from_x = wait(token, grads, quarter, from_y, from_x)
+    others = [exchange(value, CORE) for value in (quarter, from_y, from_x)]
+    token, grads, others, far_a, far_b, fourth_y, fourth_x = wait(token, grads, others, far_a, far_b, fourth_y, fourth_x)
+
+    sends = [fourth_x[:2], fourth_y[2:], far_a, far_b]
+    token, sends = wait(token, sends)
+    last_a, last_b, other_a, other_b = (exchange(s, m) for s, m in zip(sends, (ROW, NEAR_X, CORE, CORE)))
+    grads = place(token, [(12, far_a), (14, far_b), (16, others[0]), (20, others[1]), (24, others[2])], grads, width)
+    token, grads, fourth, fourth_y, fourth_x = wait(token, grads, fourth, fourth_y, fourth_x)
+    pair = [exchange(value, CORE) for value in (fourth, fourth_y, fourth_x)]
+    token, grads, last_a, last_b, other_a, other_b, pair = wait(token, grads, last_a, last_b, other_a, other_b, pair)
+
+    ends = [exchange(last_a, CORE), exchange(last_b, CORE)]
+    made = sort(token, [(0, fourth), (4, fourth_y), (8, fourth_x), (12, last_a), (14, last_b), (16, pair[0]), (20, pair[1]), (24, pair[2])], [], width)
+    out_back, out_in = place(token, [(28, other_a), (30, other_b)], grads, width)
+    token, made, ends = wait(token, made, ends)
+    out_out, out_query, out_key, out_value = sort(token, [(28, ends[0]), (30, ends[1])], made, width)
 
     pool_mine, pool_other = one_value(home[rows:])[:1], one_value(away_got[rows:])[:1]
     pooled = jnp.where(doc == 0, jnp.concatenate([pool_mine, pool_other]), jnp.concatenate([pool_other, pool_mine]))

time: 167 us -> 175 us (1.048)
  Pallas kernels: 77.4 us -> 87 us
  waiting for transfers between devices: 33 us -> 31.1 us
  other arithmetic: 9.97 us -> 8.14 us
    pallas_call x4 -> x8, Pallas kernels: 12.9 us -> 24.6 us  [the longest x3 10.1 us: spread(): pl.pallas_call(spread_kernel, grid=(4,), in_specs=[spec, spec], out_specs...]
    convert_element_type x5 -> x4, other arithmetic: 5.78 us -> 2.52 us  [added(): return total.astype(BF16)]
    ppermute x39 -> x43, waiting for transfers between devices: 33 us -> 31.1 us  [exchange(): lax.ppermute(value, ('dp', 'blk'), [(i, i ^ bits) for i in range(size)])]
    unnamed x55 -> x79, local copies, waits for them, and re-layouts: 4.6 us -> 5.94 us
    ppermute x39 -> x43, starting transfers between devices: 39.3 us -> 39.3 us  [exchange(): lax.ppermute(value, ('dp', 'blk'), [(i, i ^ bits) for i in range(size)])]
  transfers between devices with their start and end apart: 39 -> 43, of which waited for: 15 -> 16; matrix products, arithmetic and copies ran while one was open for 5% -> 6% of each run, Pallas kernels for 30% -> 29%
where the time goes in v1:
time: 175 us; the launch traced here: 174 us
  Pallas kernels  87 us (50%)
  starting transfers between devices  39.3 us (22%)
  waiting for transfers between devices  31.1 us (18%)
  other arithmetic  8.14 us (5%)
  local copies, waits for them, and re-layouts  7.28 us (4%)
    ppermute x43, starting transfers between devices, exchange(): lax.ppermute(value, ('dp', 'blk'), [(i, i ^ bits) for i in range(size)])  39.3 us
    ppermute x43, waiting for transfers between devices, exchange(): lax.ppermute(value, ('dp', 'blk'), [(i, i ^ bits) for i in range(size)])  31.1 us
    pallas_call x1, Pallas kernels, front(): pl.pallas_call(front_kernel, grid=(heads // 2,), in_specs=[smem, whole(co...  23.7 us
    pallas_call x1, Pallas kernels, back(): pl.pallas_call(back_kernel, grid=(width // 128,), in_specs=[smem, col(cou...  20.7 us
    pallas_call x3, Pallas kernels, spread(): pl.pallas_call(spread_kernel, grid=(4,), in_specs=[spec, spec], out_specs...  10.1 us
    pallas_call x3, Pallas kernels, place(): pl.pallas_call(functools.partial(place_kernel, [first for first, _ in par...  8.91 us
    pallas_call x1, Pallas kernels, through(): pl.pallas_call(through_kernel, in_specs=[smem] + [free] * 8 + [vmem], out...  8.82 us
    unnamed x79, local copies, waits for them, and re-layouts  5.94 us
  transfers between devices with their start and end apart: 43, of which 16 were waited for; matrix products, arithmetic and copies ran while one was open for 6% of the time, Pallas kernels for 29%

profile of v1, /device:TPU:0, one launch (start us, length us, event | category | flops | bytes accessed | tf_op | source)
XLA Modules:
  0.0 174.2 jit_solution(4240183948972683476)
XLA Ops:
  2.3 2.6 %collective-permute-start = (bf16[256,512]{1,0:T(8,128)(2,1)S(1)}, bf16[256,512]{1,0:T(8,128)(2,1)S(1)}, u32[]{:S(2)}, u32[]{:S(2)}) collective-permute-start(bf16[256,512]{1,0:T(8,128)(2,1)S(1)} %get-tuple-element.174), channel_id=1, source_target_pairs={{0,2},{1,3},{2,0},{3,1},{4,6},{5,7},{6,4},{7,5},{8,10},{9,11},{10,... | collective-permute-start | bytes 786440 | tf_op jit(solution)/shard_map/ppermute | solution.py:585
  7.4 3.3 %prepare.1 = (bf16[512,512]{1,0:T(8,128)(2,1)}, bf16[256,512]{1,0:T(8,128)(2,1)}, bf16[512,512]{1,0:T(8,128)(2,1)}, bf16[512,512]{1,0:T(8,128)(2,1)}, f32[8,2048]{1,0:T(8,128)}, /*index=5*/s32[16]{0:T(128)}) custom-call(s32[8]{0:T(128)} %compare_select_fusion.6.ids, s32[2]{0:T(128)} %pads.1, s32[2]{0:T(128)} %prefixes.1, bf16[256,512]{1,0:T(8,128)(2,1)} %copy-done.1, ...), custom_call_target="tpu_custom_call" | custom-call | tf_op jit(solution)/shard_map/prepare/pallas_call | solution.py:76
  11.8 1.5 collective-permute-done.2.far_other.far_other_h
  14.0 23.7 %front.1 = (bf16[512,512]{1,0:T(8,128)(2,1)}, bf16[256,512]{1,0:T(8,128)(2,1)}, bf16[512,512]{1,0:T(8,128)(2,1)}, bf16[512,512]{1,0:T(8,128)(2,1)}, bf16[8,512,1...) custom-call(s32[16]{0:T(128)} %get-tuple-element.319.info, ...), custom_call_target="tpu_custom_call" | custom-call | tf_op jit(solution)/shard_map/front/pallas_call | solution.py:232
  38.0 8.8 %through.1 = (bf16[16,512,128]{2,1,0:T(8,128)(2,1)}, f32[512,512]{1,0:T(8,128)}, bf16[512,512]{1,0:T(8,128)(2,1)}, bf16[512,512]{1,0:T(8,128)(2,1)}, f32[8,512]{1,0:T(8,128)}) custom-call(s32[16]{0:T(128)} %get-tuple-element.319.info, bf16[512,2048]{1,0:T(8,128)(2,1)} %get-tuple-element.185.slopes_h, bf16[512,2048]{1,0:T(8,128)(2,1)} %win_h.3, ...), custom_call_target="tpu_custom_call" | custom-call | tf_op jit(solution)/shard_map/through/pallas_call | solution.py:312
  48.1 3.3 %spread.5 = bf16[4,512,128]{2,1,0:T(8,128)(2,1)} custom-call(bf16[16,512,128]{2,1,0:T(8,128)(2,1)} %get-tuple-element.194.keep.refs_0_, bf16[16,512,128]{2,1,0:T(8,128)(2,1)} %copy-done), custom_call_target="tpu_custom_call" | custom-call | tf_op jit(solution)/shard_map/spread/pallas_call | solution.py:564
  51.5 3.3 %spread.4 = bf16[4,512,128]{2,1,0:T(8,128)(2,1)} custom-call(bf16[16,512,128]{2,1,0:T(8,128)(2,1)} %get-tuple-element.194.keep.refs_0_, bf16[16,512,128]{2,1,0:T(8,128)(2,1)} %copy-done), custom_call_target="tpu_custom_call" | custom-call | tf_op jit(solution)/shard_map/spread/pallas_call | solution.py:564
  54.8 3.4 %spread.3 = bf16[4,512,128]{2,1,0:T(8,128)(2,1)} custom-call(bf16[16,512,128]{2,1,0:T(8,128)(2,1)} %get-tuple-element.194.keep.refs_0_, bf16[16,512,128]{2,1,0:T(8,128)(2,1)} %copy-done), custom_call_target="tpu_custom_call" | custom-call | tf_op jit(solution)/shard_map/spread/pallas_call | solution.py:564
  58.2 2.7 %collective-permute-start.4 = (bf16[4,512,128]{2,1,0:T(8,128)(2,1)}, bf16[4,512,128]{2,1,0:T(8,128)(2,1)S(1)}, u32[]{:S(2)}, u32[]{:S(2)}) collective-permute-start(bf16[4,512,128]{2,1,0:T(8,128)(2,1)} %spread.3), channel_id=1, source_target_pairs={{0,6},{1,7},{2,4},{3,5},{4,2},{5,3},{6,0},{7,1},{8,14},{9,15},{10,... | collective-permute-start | bytes 1572872 | tf_op jit(solution)/shard_map/ppermute | solution.py:585
  61.7 20.7 %back.1 = (bf16[16,64,512]{2,1,0:T(8,128)(2,1)}, bf16[1056,512]{1,0:T(8,128)(2,1)}, f32[512,512]{1,0:T(8,128)}, bf16[544,512]{1,0:T(8,128)(2,1)}, f32[16,512]{1,0:T(8,128)}) custom-call(s32[16]{0:T(128)} %get-tuple-element.319.info, bf16[256,512]{1,0:T(8,128)(2,1)} %get-tuple-element.179.q_l.ql, bf16[256,512]{1,0:T(8,128)(2,1)} %get-tuple-element.197.qr, ...), custom_call_target="tpu_custom_call" | custom-call | tf_op jit(solution)/shard_map/back/pallas_call | solution.py:451
  82.5 2.3 %collective-permute-done.5.refs_3_ = bf16[4,512,128]{2,1,0:T(8,128)(2,1)S(1)} collective-permute-done((bf16[4,512,128]{2,1,0:T(8,128)(2,1)S(1)}, bf16[4,512,128]{2,1,0:T(8,128)(2,1)S(1)}, u32[]{:S(2)}, u32[]{:S(2)}) %collective-permute-start.5) | collective-permute-done | bytes 524320 | tf_op jit(solution)/shard_map/ppermute | solution.py:585
  85.8 2.7 %mix.1 = (bf16[512,128]{1,0:T(8,128)(2,1)}, bf16[512,128]{1,0:T(8,128)(2,1)}, bf16[512,128]{1,0:T(8,128)(2,1)}, bf16[512,128]{1,0:T(8,128)(2,1)}) custom-call(bf16[16,512,128]{2,1,0:T(8,128)(2,1)} %get-tuple-element.194.keep.refs_0_, bf16[16,512,128]{2,1,0:T(8,128)(2,1)} %copy-done, bf16[4,512,128]{2,1,0:T(8,128)(2,1)} %copy-done.15, ...), custom_call_target="tpu_custom_call" | custom-call | tf_op jit(solution)/shard_map/mix/pallas_call | solution.py:578
  88.5 1.6 collective-permute-start.9
  90.1 2.6 %collective-permute-start.10 = (bf16[512,128]{1,0:T(8,128)(2,1)}, bf16[512,128]{1,0:T(8,128)(2,1)}, u32[]{:S(2)}, u32[]{:S(2)}) collective-permute-start(bf16[512,128]{1,0:T(8,128)(2,1)} %get-tuple-element.232), channel_id=1, source_target_pairs={{0,16},{1,17},{2,18},{3,19},{4,20},{5,21},{6,22},{7,23},{8,24},{9,... | collective-permute-start | bytes 393224 | tf_op jit(solution)/shard_map/ppermute | solution.py:585
  94.2 1.6 collective-permute-start.12
  97.7 3.2 %ending.1 = (bf16[288,512]{1,0:T(8,128)(2,1)}, bf16[288,512]{1,0:T(8,128)(2,1)}) custom-call(s32[16]{0:T(128)} %get-tuple-element.319.info, f32[512,512]{1,0:T(8,128)} %get-tuple-element.227.stay, bf16[544,512]{1,0:T(8,128)(2,1)} %copy-done.12, bf16[256,512]{1,0:T(8,128)(2,1)} %copy-done.1, bf16[256,512]{1,0:T(8,128)(2,1)} %copy-done.2, ...), custom_call_target="tpu_custom_call" | custom-call | tf_op jit(solution)/shard_map/ending/pallas_call | solution.py:487
  100.9 2.5 %collective-permute-done.10 = bf16[512,128]{1,0:T(8,128)(2,1)} collective-permute-done((bf16[512,128]{1,0:T(8,128)(2,1)}, bf16[512,128]{1,0:T(8,128)(2,1)}, u32[]{:S(2)}, u32[]{:S(2)}) %collective-permute-start.10) | collective-permute-done | bytes 131104 | tf_op jit(solution)/shard_map/ppermute | solution.py:585
  104.6 2.5 %collective-permute-start.17 = (bf16[512,128]{1,0:T(8,128)(2,1)S(1)}, bf16[512,128]{1,0:T(8,128)(2,1)S(1)}, u32[]{:S(2)}, u32[]{:S(2)}) collective-permute-start(bf16[512,128]{1,0:T(8,128)(2,1)S(1)} %add_convert_fusion), channel_id=1, source_target_pairs={{0,24},{1,25},{2,26},{3,27},{4,28},{5,29},{6,30},{7,31},{8,16},{9,... | collective-permute-start | bytes 393224 | tf_op jit(solution)/shard_map/ppermute | solution.py:585
  112.9 5.2 %collective-permute-done.16 = bf16[512,128]{1,0:T(8,128)(2,1)S(1)} collective-permute-done((bf16[512,128]{1,0:T(8,128)(2,1)S(1)}, bf16[512,128]{1,0:T(8,128)(2,1)S(1)}, u32[]{:S(2)}, u32[]{:S(2)}) %collective-permute-start.16) | collective-permute-done | bytes 131104 | tf_op jit(solution)/shard_map/ppermute | solution.py:585
  118.1 3.0 %collective-permute-start.20 = (bf16[96,512]{1,0:T(8,128)(2,1)S(1)}, bf16[96,512]{1,0:T(8,128)(2,1)S(1)}, u32[]{:S(2)}, u32[]{:S(2)}) collective-permute-start(bf16[96,512]{1,0:T(8,128)(2,1)S(1)} %get-tuple-element.258), channel_id=1, source_target_pairs={{0,16},{1,17},{2,18},{3,19},{4,20},{5,21},{6,22},{7,23},{8,24},{9,... | collective-permute-start | bytes 294920 | tf_op jit(solution)/shard_map/ppermute | solution.py:585
  124.9 3.5 %collective-permute-done.20 = bf16[96,512]{1,0:T(8,128)(2,1)S(1)} collective-permute-done((bf16[96,512]{1,0:T(8,128)(2,1)S(1)}, bf16[96,512]{1,0:T(8,128)(2,1)S(1)}, u32[]{:S(2)}, u32[]{:S(2)}) %collective-permute-start.20) | collective-permute-done | bytes 98336 | tf_op jit(solution)/shard_map/ppermute | solution.py:585
  129.4 2.5 %collective-permute-start.24 = (bf16[64,512]{1,0:T(8,128)(2,1)S(1)}, bf16[64,512]{1,0:T(8,128)(2,1)S(1)}, u32[]{:S(2)}, u32[]{:S(2)}) collective-permute-start(bf16[64,512]{1,0:T(8,128)(2,1)S(1)} %add_convert_fusion.1), channel_id=1, source_target_pairs={{0,24},{1,25},{2,26},{3,27},{4,28},{5,29},{6,30},{7,31},{8,16},{9,... | collective-permute-start | bytes 196616 | tf_op jit(solution)/shard_map/ppermute | solution.py:585
  133.9 2.3 %collective-permute-done.24 = bf16[64,512]{1,0:T(8,128)(2,1)S(1)} collective-permute-done((bf16[64,512]{1,0:T(8,128)(2,1)S(1)}, bf16[64,512]{1,0:T(8,128)(2,1)S(1)}, u32[]{:S(2)}, u32[]{:S(2)}) %collective-permute-start.24) | collective-permute-done | bytes 65568 | tf_op jit(solution)/shard_map/ppermute | solution.py:585
  136.1 1.6 collective-permute-done.23
  137.9 1.6 collective-permute-start.30
  139.5 3.2 %place.3 = (f32[2048,512]{1,0:T(8,128)}, f32[512,2048]{1,0:T(8,128)}) custom-call(s32[16]{0:T(128)} %get-tuple-element.319.info, bf16[4,512,128]{2,1,0:T(8,128)(2,1)} %copy-done.3, bf16[4,512,128]{2,1,0:T(8,128)(2,1)} %copy-done.5, bf16[4,512,128]{2,1,0:T(8,128)(2,1)} %copy-done.4), custom_call_target="tpu_custom_call" | custom-call | tf_op jit(solution)/shard_map/place/pallas_call | solution.py:516
  146.0 6.3 %collective-permute-done.32.refs_1_ = bf16[4,64,512]{2,1,0:T(8,128)(2,1)S(1)} collective-permute-done((bf16[4,64,512]{2,1,0:T(8,128)(2,1)S(1)}, bf16[4,64,512]{2,1,0:T(8,128)(2,1)S(1)}, u32[]{:S(2)}, u32[]{:S(2)}) %collective-permute-start.32) | collective-permute-done | bytes 262176 | tf_op jit(solution)/shard_map/ppermute | solution.py:585
  154.3 1.7 collective-permute-start.35
  157.5 3.7 %place.4 = (f32[2048,512]{1,0:T(8,128)}, f32[512,2048]{1,0:T(8,128)}) custom-call(s32[16]{0:T(128)} %get-tuple-element.319.info, bf16[2,512,128]{2,1,0:T(8,128)(2,1)} %copy-done.29, bf16[2,512,128]{2,1,0:T(8,128)(2,1)} %copy-done.30, bf16[4,512,128]{2,1,0:T(8,128)(2,1)} %copy-done.18, ...), custom_call_target="tpu_custom_call", output_to_operand_aliasing={{0}: (6, {}), {1}: (7, {})} | custom-call | tf_op jit(solution)/shard_map/place/pallas_call | solution.py:516
  165.6 3.8 %sort.2 = (f32[512,512]{1,0:T(8,128)}, f32[512,512]{1,0:T(8,128)}, f32[512,512]{1,0:T(8,128)}, f32[512,512]{1,0:T(8,128)}) custom-call(s32[16]{0:T(128)} %get-tuple-element.319.info, bf16[4,64,512]{2,1,0:T(8,128)(2,1)} %copy-done.9, bf16[4,64,512]{2,1,0:T(8,128)(2,1)} %copy-done.10, bf16[4,64,512]{2,1,0:T(8,128)(2,1)} %copy-done.11, ...), custom_call_target="tpu_custom_call" | custom-call | tf_op jit(solution)/shard_map/sort/pallas_call | solution.py:548
  169.4 2.1 %place.5 = (f32[2048,512]{1,0:T(8,128)}, f32[512,2048]{1,0:T(8,128)}) custom-call(s32[16]{0:T(128)} %get-tuple-element.319.info, bf16[2,512,128]{2,1,0:T(8,128)(2,1)} %copy-done.24, bf16[2,512,128]{2,1,0:T(8,128)(2,1)} %copy-done.25, f32[2048,512]{1,0:T(8,128)} %get-tuple-element.332.refs_2_, ...), custom_call_target="tpu_custom_call", output_to_operand_aliasing={{0}: (3, {}), {1}: (4, {})} | custom-call | tf_op jit(solution)/shard_map/place/pallas_call | solution.py:516
  172.2 1.8 %sort.3 = (f32[512,512]{1,0:T(8,128)}, f32[512,512]{1,0:T(8,128)}, f32[512,512]{1,0:T(8,128)}, f32[512,512]{1,0:T(8,128)}) custom-call(s32[16]{0:T(128)} %get-tuple-element.319.info, bf16[2,64,512]{2,1,0:T(8,128)(2,1)} %copy-done.31, bf16[2,64,512]{2,1,0:T(8,128)(2,1)} %copy-done.32, ...), custom_call_target="tpu_custom_call", output_to_operand_aliasing={{0}: (3, {}), {1}: (4, {}), {2}: (5, {}), {3}: (6, {})} | custom-call | tf_op jit(solution)/shard_map/sort/pallas_call | solution.py:548
  (174 shorter events, 38.3 us)
Async XLA Ops:
  2.3 9.5 %collective-permute-start = (bf16[256,512]{1,0:T(8,128)(2,1)S(1)}, bf16[256,512]{1,0:T(8,128)(2,1)S(1)}, u32[]{:S(2)}, u32[]{:S(2)}) collective-permute-start(bf16[256,512]{1,0:T(8,128)(2,1)S(1)} %get-tuple-element.174), channel_id=1, source_target_pairs={{0,2},{1,3},{2,0},{3,1},{4,6},{5,7},{6,4},{7,5},{8,10},{9,11},{10,... | collective-permute-start | bytes 786440 | tf_op jit(solution)/shard_map/ppermute | solution.py:585
  37.7 9.1 %collective-permute-start.3 = (bf16[16,512,128]{2,1,0:T(8,128)(2,1)}, bf16[16,512,128]{2,1,0:T(8,128)(2,1)S(1)}, u32[]{:S(2)}, u32[]{:S(2)}) collective-permute-start(bf16[16,512,128]{2,1,0:T(8,128)(2,1)} %get-tuple-element.192), channel_id=1, source_target_pairs={{0,1},{1,0},{2,3},{3,2},{4,5},{5,4},{6,7},{7,6},{8,9},{9,8},{10,11... | collective-permute-start | bytes 6291464 | tf_op jit(solution)/shard_map/ppermute | solution.py:585
  58.2 24.2 %collective-permute-start.4 = (bf16[4,512,128]{2,1,0:T(8,128)(2,1)}, bf16[4,512,128]{2,1,0:T(8,128)(2,1)S(1)}, u32[]{:S(2)}, u32[]{:S(2)}) collective-permute-start(bf16[4,512,128]{2,1,0:T(8,128)(2,1)} %spread.3), channel_id=1, source_target_pairs={{0,6},{1,7},{2,4},{3,5},{4,2},{5,3},{6,0},{7,1},{8,14},{9,15},{10,... | collective-permute-start | bytes 1572872 | tf_op jit(solution)/shard_map/ppermute | solution.py:585
  60.9 23.8 %collective-permute-start.5 = (bf16[4,512,128]{2,1,0:T(8,128)(2,1)S(1)}, bf16[4,512,128]{2,1,0:T(8,128)(2,1)S(1)}, u32[]{:S(2)}, u32[]{:S(2)}) collective-permute-start(bf16[4,512,128]{2,1,0:T(8,128)(2,1)S(1)} %copy-done.14), channel_id=1, source_target_pairs={{0,2},{1,3},{2,0},{3,1},{4,6},{5,7},{6,4},{7,5},{8,10},{9,11},{10,... | collective-permute-start | bytes 1572872 | tf_op jit(solution)/shard_map/ppermute | solution.py:585
  61.4 23.6 %collective-permute-start.6 = (bf16[4,512,128]{2,1,0:T(8,128)(2,1)S(1)}, bf16[4,512,128]{2,1,0:T(8,128)(2,1)S(1)}, u32[]{:S(2)}, u32[]{:S(2)}) collective-permute-start(bf16[4,512,128]{2,1,0:T(8,128)(2,1)S(1)} %copy-done.13), channel_id=1, source_target_pairs={{0,4},{1,5},{2,6},{3,7},{4,0},{5,1},{6,2},{7,3},{8,12},{9,13},{10,... | collective-permute-start | bytes 1572872 | tf_op jit(solution)/shard_map/ppermute | solution.py:585
  85.0 7.8 %collective-permute-start.7 = (bf16[1056,512]{1,0:T(8,128)(2,1)}, bf16[1056,512]{1,0:T(8,128)(2,1)S(1)}, u32[]{:S(2)}, u32[]{:S(2)}) collective-permute-start(bf16[1056,512]{1,0:T(8,128)(2,1)} %get-tuple-element.220), channel_id=1, source_target_pairs={{0,1},{1,0},{2,3},{3,2},{4,5},{5,4},{6,7},{7,6},{8,9},{9,8},{10,11... | collective-permute-start | bytes 3244040 | tf_op jit(solution)/shard_map/ppermute | solution.py:585
  85.0 7.8 %collective-permute-start.8 = (bf16[544,512]{1,0:T(8,128)(2,1)}, bf16[544,512]{1,0:T(8,128)(2,1)S(1)}, u32[]{:S(2)}, u32[]{:S(2)}) collective-permute-start(bf16[544,512]{1,0:T(8,128)(2,1)} %get-tuple-element.221), channel_id=1, source_target_pairs={{0,1},{1,0},{2,3},{3,2},{4,5},{5,4},{6,7},{7,6},{8,9},{9,8},{10,11... | collective-permute-start | bytes 1671176 | tf_op jit(solution)/shard_map/ppermute | solution.py:585
  88.5 7.7 %collective-permute-start.9 = (bf16[512,128]{1,0:T(8,128)(2,1)}, bf16[512,128]{1,0:T(8,128)(2,1)}, u32[]{:S(2)}, u32[]{:S(2)}) collective-permute-start(bf16[512,128]{1,0:T(8,128)(2,1)} %get-tuple-element.231), channel_id=1, source_target_pairs={{0,8},{1,9},{2,10},{3,11},{4,12},{5,13},{6,14},{7,15},{8,0},{9,1},... | collective-permute-start | bytes 393224 | tf_op jit(solution)/shard_map/ppermute | solution.py:585
  90.1 13.2 %collective-permute-start.10 = (bf16[512,128]{1,0:T(8,128)(2,1)}, bf16[512,128]{1,0:T(8,128)(2,1)}, u32[]{:S(2)}, u32[]{:S(2)}) collective-permute-start(bf16[512,128]{1,0:T(8,128)(2,1)} %get-tuple-element.232), channel_id=1, source_target_pairs={{0,16},{1,17},{2,18},{3,19},{4,20},{5,21},{6,22},{7,23},{8,24},{9,... | collective-permute-start | bytes 393224 | tf_op jit(solution)/shard_map/ppermute | solution.py:585
  92.7 10.6 %collective-permute-start.11 = (bf16[512,128]{1,0:T(8,128)(2,1)}, bf16[512,128]{1,0:T(8,128)(2,1)}, u32[]{:S(2)}, u32[]{:S(2)}) collective-permute-start(bf16[512,128]{1,0:T(8,128)(2,1)} %get-tuple-element.233), channel_id=1, source_target_pairs={{0,24},{1,25},{2,26},{3,27},{4,28},{5,29},{6,30},{7,31},{8,16},{9,... | collective-permute-start | bytes 393224 | tf_op jit(solution)/shard_map/ppermute | solution.py:585
  94.2 14.1 %collective-permute-start.12 = (bf16[288,512]{1,0:T(8,128)(2,1)}, bf16[288,512]{1,0:T(8,128)(2,1)S(1)}, u32[]{:S(2)}, u32[]{:S(2)}) collective-permute-start(bf16[288,512]{1,0:T(8,128)(2,1)} %get-tuple-element.241), channel_id=1, source_target_pairs={{0,2},{1,3},{2,0},{3,1},{4,6},{5,7},{6,4},{7,5},{8,10},{9,11},{10,... | collective-permute-start | bytes 884744 | tf_op jit(solution)/shard_map/ppermute | solution.py:585
  95.8 13.3 %collective-permute-start.13 = (bf16[288,512]{1,0:T(8,128)(2,1)}, bf16[288,512]{1,0:T(8,128)(2,1)S(1)}, u32[]{:S(2)}, u32[]{:S(2)}) collective-permute-start(bf16[288,512]{1,0:T(8,128)(2,1)} %get-tuple-element.242), channel_id=1, source_target_pairs={{0,4},{1,5},{2,6},{3,7},{4,0},{5,1},{6,2},{7,3},{8,12},{9,13},{10,... | collective-permute-start | bytes 884744 | tf_op jit(solution)/shard_map/ppermute | solution.py:585
  96.2 14.3 %collective-permute-start.14 = (bf16[288,512]{1,0:T(8,128)(2,1)}, bf16[288,512]{1,0:T(8,128)(2,1)S(1)}, u32[]{:S(2)}, u32[]{:S(2)}) collective-permute-start(bf16[288,512]{1,0:T(8,128)(2,1)} %get-tuple-element.243), channel_id=1, source_target_pairs={{0,6},{1,7},{2,4},{3,5},{4,2},{5,3},{6,0},{7,1},{8,14},{9,15},{10,... | collective-permute-start | bytes 884744 | tf_op jit(solution)/shard_map/ppermute | solution.py:585
  104.6 8.3 %collective-permute-start.17 = (bf16[512,128]{1,0:T(8,128)(2,1)S(1)}, bf16[512,128]{1,0:T(8,128)(2,1)S(1)}, u32[]{:S(2)}, u32[]{:S(2)}) collective-permute-start(bf16[512,128]{1,0:T(8,128)(2,1)S(1)} %add_convert_fusion), channel_id=1, source_target_pairs={{0,24},{1,25},{2,26},{3,27},{4,28},{5,29},{6,30},{7,31},{8,16},{9,... | collective-permute-start | bytes 393224 | tf_op jit(solution)/shard_map/ppermute | solution.py:585
  107.0 11.0 %collective-permute-start.16 = (bf16[512,128]{1,0:T(8,128)(2,1)S(1)}, bf16[512,128]{1,0:T(8,128)(2,1)S(1)}, u32[]{:S(2)}, u32[]{:S(2)}) collective-permute-start(bf16[512,128]{1,0:T(8,128)(2,1)S(1)} %add_convert_fusion), channel_id=1, source_target_pairs={{0,16},{1,17},{2,18},{3,19},{4,20},{5,21},{6,22},{7,23},{8,24},{9,... | collective-permute-start | bytes 393224 | tf_op jit(solution)/shard_map/ppermute | solution.py:585
  108.3 9.8 %collective-permute-start.15 = (bf16[512,128]{1,0:T(8,128)(2,1)S(1)}, bf16[512,128]{1,0:T(8,128)(2,1)S(1)}, u32[]{:S(2)}, u32[]{:S(2)}) collective-permute-start(bf16[512,128]{1,0:T(8,128)(2,1)S(1)} %add_convert_fusion), channel_id=1, source_target_pairs={{0,8},{1,9},{2,10},{3,11},{4,12},{5,13},{6,14},{7,15},{8,0},{9,1},... | collective-permute-start | bytes 393224 | tf_op jit(solution)/shard_map/ppermute | solution.py:585
  109.0 13.5 %collective-permute-start.18 = (bf16[288,512]{1,0:T(8,128)(2,1)}, bf16[288,512]{1,0:T(8,128)(2,1)S(1)}, u32[]{:S(2)}, u32[]{:S(2)}) collective-permute-start(bf16[288,512]{1,0:T(8,128)(2,1)} %get-tuple-element.254), channel_id=1, source_target_pairs={{0,2},{1,3},{2,0},{3,1},{4,6},{5,7},{6,4},{7,5},{8,10},{9,11},{10,... | collective-permute-start | bytes 884744 | tf_op jit(solution)/shard_map/ppermute | solution.py:585
  118.1 6.8 %collective-permute-start.19 = (bf16[96,512]{1,0:T(8,128)(2,1)S(1)}, bf16[96,512]{1,0:T(8,128)(2,1)S(1)}, u32[]{:S(2)}, u32[]{:S(2)}) collective-permute-start(bf16[96,512]{1,0:T(8,128)(2,1)S(1)} %get-tuple-element.257), channel_id=1, source_target_pairs={{0,8},{1,9},{2,10},{3,11},{4,12},{5,13},{6,14},{7,15},{8,0},{9,1},... | collective-permute-start | bytes 294920 | tf_op jit(solution)/shard_map/ppermute | solution.py:585
  118.1 10.3 %collective-permute-start.20 = (bf16[96,512]{1,0:T(8,128)(2,1)S(1)}, bf16[96,512]{1,0:T(8,128)(2,1)S(1)}, u32[]{:S(2)}, u32[]{:S(2)}) collective-permute-start(bf16[96,512]{1,0:T(8,128)(2,1)S(1)} %get-tuple-element.258), channel_id=1, source_target_pairs={{0,16},{1,17},{2,18},{3,19},{4,20},{5,21},{6,22},{7,23},{8,24},{9,... | collective-permute-start | bytes 294920 | tf_op jit(solution)/shard_map/ppermute | solution.py:585
  121.1 7.3 %collective-permute-start.21 = (bf16[96,512]{1,0:T(8,128)(2,1)S(1)}, bf16[96,512]{1,0:T(8,128)(2,1)S(1)}, u32[]{:S(2)}, u32[]{:S(2)}) collective-permute-start(bf16[96,512]{1,0:T(8,128)(2,1)S(1)} %get-tuple-element.259), channel_id=1, source_target_pairs={{0,24},{1,25},{2,26},{3,27},{4,28},{5,29},{6,30},{7,31},{8,16},{9,... | collective-permute-start | bytes 294920 | tf_op jit(solution)/shard_map/ppermute | solution.py:585
  123.3 14.4 %collective-permute-start.26 = (bf16[4,512,128]{2,1,0:T(8,128)(2,1)S(1)}, bf16[4,512,128]{2,1,0:T(8,128)(2,1)S(1)}, u32[]{:S(2)}, u32[]{:S(2)}) collective-permute-start(bf16[4,512,128]{2,1,0:T(8,128)(2,1)S(1)} %pad_maximum_fusion.refs_0_), channel_id=1, source_target_pairs={{0,4},{1,5},{2,6},{3,7},{4,0},{5,1},{6,2},{7,3},{8,12},{9,13},{10,... | collective-permute-start | bytes 1572872 | tf_op jit(solution)/shard_map/ppermute | solution.py:585
  124.8 12.9 %collective-permute-start.25 = (bf16[4,512,128]{2,1,0:T(8,128)(2,1)S(1)}, bf16[4,512,128]{2,1,0:T(8,128)(2,1)S(1)}, u32[]{:S(2)}, u32[]{:S(2)}) collective-permute-start(bf16[4,512,128]{2,1,0:T(8,128)(2,1)S(1)} %pad_maximum_fusion.refs_0_), channel_id=1, source_target_pairs={{0,2},{1,3},{2,0},{3,1},{4,6},{5,7},{6,4},{7,5},{8,10},{9,11},{10,... | collective-permute-start | bytes 1572872 | tf_op jit(solution)/shard_map/ppermute | solution.py:585
  129.4 6.7 %collective-permute-start.24 = (bf16[64,512]{1,0:T(8,128)(2,1)S(1)}, bf16[64,512]{1,0:T(8,128)(2,1)S(1)}, u32[]{:S(2)}, u32[]{:S(2)}) collective-permute-start(bf16[64,512]{1,0:T(8,128)(2,1)S(1)} %add_convert_fusion.1), channel_id=1, source_target_pairs={{0,24},{1,25},{2,26},{3,27},{4,28},{5,29},{6,30},{7,31},{8,16},{9,... | collective-permute-start | bytes 196616 | tf_op jit(solution)/shard_map/ppermute | solution.py:585
  142.7 11.1 %collective-permute-start.27 = (bf16[4,512,128]{2,1,0:T(8,128)(2,1)}, bf16[4,512,128]{2,1,0:T(8,128)(2,1)S(1)}, u32[]{:S(2)}, u32[]{:S(2)}) collective-permute-start(bf16[4,512,128]{2,1,0:T(8,128)(2,1)} %copy-done.3), channel_id=1, source_target_pairs={{0,1},{1,0},{2,3},{3,2},{4,5},{5,4},{6,7},{7,6},{8,9},{9,8},{10,11... | collective-permute-start | bytes 1572872 | tf_op jit(solution)/shard_map/ppermute | solution.py:585
  142.8 11.0 %collective-permute-start.28 = (bf16[4,512,128]{2,1,0:T(8,128)(2,1)}, bf16[4,512,128]{2,1,0:T(8,128)(2,1)S(1)}, u32[]{:S(2)}, u32[]{:S(2)}) collective-permute-start(bf16[4,512,128]{2,1,0:T(8,128)(2,1)} %copy-done.5), channel_id=1, source_target_pairs={{0,1},{1,0},{2,3},{3,2},{4,5},{5,4},{6,7},{7,6},{8,9},{9,8},{10,11... | collective-permute-start | bytes 1572872 | tf_op jit(solution)/shard_map/ppermute | solution.py:585
  143.3 10.5 %collective-permute-start.29 = (bf16[4,512,128]{2,1,0:T(8,128)(2,1)}, bf16[4,512,128]{2,1,0:T(8,128)(2,1)S(1)}, u32[]{:S(2)}, u32[]{:S(2)}) collective-permute-start(bf16[4,512,128]{2,1,0:T(8,128)(2,1)} %copy-done.4), channel_id=1, source_target_pairs={{0,1},{1,0},{2,3},{3,2},{4,5},{5,4},{6,7},{7,6},{8,9},{9,8},{10,11... | collective-permute-start | bytes 1572872 | tf_op jit(solution)/shard_map/ppermute | solution.py:585
  144.3 8.0 %collective-permute-start.32 = (bf16[4,64,512]{2,1,0:T(8,128)(2,1)S(1)}, bf16[4,64,512]{2,1,0:T(8,128)(2,1)S(1)}, u32[]{:S(2)}, u32[]{:S(2)}) collective-permute-start(bf16[4,64,512]{2,1,0:T(8,128)(2,1)S(1)} %pad_maximum_fusion.7.refs_0_), channel_id=1, source_target_pairs={{0,2},{1,3},{2,0},{3,1},{4,6},{5,7},{6,4},{7,5},{8,10},{9,11},{10,... | collective-permute-start | bytes 786440 | tf_op jit(solution)/shard_map/ppermute | solution.py:585
  145.8 7.9 %collective-permute-start.33 = (bf16[4,64,512]{2,1,0:T(8,128)(2,1)S(1)}, bf16[4,64,512]{2,1,0:T(8,128)(2,1)S(1)}, u32[]{:S(2)}, u32[]{:S(2)}) collective-permute-start(bf16[4,64,512]{2,1,0:T(8,128)(2,1)S(1)} %pad_maximum_fusion.7.refs_0_), channel_id=1, source_target_pairs={{0,4},{1,5},{2,6},{3,7},{4,0},{5,1},{6,2},{7,3},{8,12},{9,13},{10,... | collective-permute-start | bytes 786440 | tf_op jit(solution)/shard_map/ppermute | solution.py:585
  153.9 8.0 %collective-permute-start.34 = (bf16[2,64,512]{2,1,0:T(8,128)(2,1)S(1)}, bf16[2,64,512]{2,1,0:T(8,128)(2,1)}, u32[]{:S(2)}, u32[]{:S(2)}) collective-permute-start(bf16[2,64,512]{2,1,0:T(8,128)(2,1)S(1)} %slice.303), channel_id=1, source_target_pairs={{0,2},{1,3},{2,0},{3,1},{4,6},{5,7},{6,4},{7,5},{8,10},{9,11},{10,... | collective-permute-start | bytes 393224 | tf_op jit(solution)/shard_map/ppermute | solution.py:585
  154.3 8.0 %collective-permute-start.35 = (bf16[2,64,512]{2,1,0:T(8,128)(2,1)S(1)}, bf16[2,64,512]{2,1,0:T(8,128)(2,1)}, u32[]{:S(2)}, u32[]{:S(2)}) collective-permute-start(bf16[2,64,512]{2,1,0:T(8,128)(2,1)S(1)} %slice.304), channel_id=1, source_target_pairs={{0,4},{1,5},{2,6},{3,7},{4,0},{5,1},{6,2},{7,3},{8,12},{9,13},{10,... | collective-permute-start | bytes 393224 | tf_op jit(solution)/shard_map/ppermute | solution.py:585
  164.5 7.0 %collective-permute-start.41 = (bf16[2,64,512]{2,1,0:T(8,128)(2,1)}, bf16[2,64,512]{2,1,0:T(8,128)(2,1)S(1)}, u32[]{:S(2)}, u32[]{:S(2)}) collective-permute-start(bf16[2,64,512]{2,1,0:T(8,128)(2,1)} %collective-permute-done.34.refs_3_), channel_id=1, source_target_pairs={{0,1},{1,0},{2,3},{3,2},{4,5},{5,4},{6,7},{7,6},{8,9},{9,8},{10,11... | collective-permute-start | bytes 393224 | tf_op jit(solution)/shard_map/ppermute | solution.py:585
  164.6 6.8 %collective-permute-start.42 = (bf16[2,64,512]{2,1,0:T(8,128)(2,1)}, bf16[2,64,512]{2,1,0:T(8,128)(2,1)S(1)}, u32[]{:S(2)}, u32[]{:S(2)}) collective-permute-start(bf16[2,64,512]{2,1,0:T(8,128)(2,1)} %collective-permute-done.35.refs_4_), channel_id=1, source_target_pairs={{0,1},{1,0},{2,3},{3,2},{4,5},{5,4},{6,7},{7,6},{8,9},{9,8},{10,11... | collective-permute-start | bytes 393224 | tf_op jit(solution)/shard_map/ppermute | solution.py:585
  (50 other events, 296.1 us)

commit v2 on v1

--- a/solution.py
+++ b/solution.py
@@ -244,29 +244,19 @@
         name="front",
     )(info, far, far_other, near, q_l, k_l, v_l, lines, wq, wk, wv, gain1, gain2, gain3, cots, wo, win, wback)
 
-def through_kernel(info, slopes_h, win_h, mixed_h, steep_h, wo_h, att_h, active_h, turned_h, gain2,
-                   keep, grad_mixed_o, grad_attended_o, grad_out_o, rows,
-                   slopes, win, mixed, steep, wo, att, active, turned, grad_mixed, grad_attended, grad_out, sems):
+def through_kernel(info, slopes_h, win_h, mixed_h, steep_h, wo_h, att_h, gain2, grad_mixed_o, grad_attended_o, grad_out_o, rows,
+                   slopes, win, mixed, steep, wo, att, grad_mixed, grad_attended, grad_out, sems):
     hidden, width = slopes.shape[1], mixed.shape[1]
     chunks = []
     for i, at in enumerate(range(0, hidden, 512)):
         for a, b, s in ((slopes_h, slopes, i), (win_h, win, 4 + i)):
             chunks.append(pltpu.make_async_copy(a.at[:, at : at + 512], b.at[:, at : at + 512], sems.at[s]))
     copies = [pltpu.make_async_copy(a, b, sems.at[8 + i]) for i, (a, b) in enumerate((
-        (mixed_h, mixed), (steep_h, steep), (wo_h, wo), (att_h, att), (active_h, active), (turned_h, turned)))]
-    outs = [pltpu.make_async_copy(a, b, sems.at[14 + i]) for i, (a, b) in enumerate((
+        (mixed_h, mixed), (steep_h, steep), (wo_h, wo), (att_h, att)))]
+    outs = [pltpu.make_async_copy(a, b, sems.at[12 + i]) for i, (a, b) in enumerate((
         (grad_mixed, grad_mixed_o), (grad_attended, grad_attended_o), (grad_out, grad_out_o)))]
-    for copy in chunks + copies[:4]:
+    for copy in chunks + copies:
         copy.start()
-
-    @pl.when(info[7] == 0)
-    def _():
-        copies[4].start()
-
-    @pl.when(info[7] == 1)
-    def _():
-        copies[5].start()
-
     grad_inner = None
     for i, at in enumerate(range(0, hidden, 512)):
         chunks[2 * i].wait()
@@ -288,35 +278,74 @@
     grad_out[...] = dot(att[...], low, TN).astype(BF16)
     outs[2].start()
     rows[...] = jnp.concatenate([grad_two, jnp.zeros((7, width), F32)])
-    mine = info[6] & 15
-
-    @pl.when(info[7] == 0)
-    def _():
-        copies[4].wait()
-        back_pieces(keep, active, steep[...].astype(BF16), mine)
-
-    @pl.when(info[7] == 1)
-    def _():
-        copies[5].wait()
-        in_pieces(keep, slopes, turned[...], mine)
-
     for copy in outs:
         copy.wait()
 
-def through(info, slopes, win, mixed, steep, wo, att, active, turned, gain2):
+def through(info, slopes, win, mixed, steep, wo, att, gain2):
     n, width = mixed.shape
     smem, vmem, free = (pl.BlockSpec(memory_space=m) for m in (pltpu.SMEM, pltpu.VMEM, pl.ANY))
     shape = jax.ShapeDtypeStruct
-    given = (slopes, win, mixed, steep, wo, att, active, turned)
+    given = (slopes, win, mixed, steep, wo, att)
     outs = [shape((n, width), F32), shape((n, width), BF16), shape((width, width), BF16)]
     return pl.pallas_call(
         through_kernel,
-        in_specs=[smem] + [free] * 8 + [vmem],
-        out_specs=[vmem] + [free] * 3 + [vmem],
-        out_shape=[shape((16, width, 128), BF16)] + outs + [shape((8, width), F32)],
-        scratch_shapes=[pltpu.VMEM(g.shape, g.dtype) for g in given] + [pltpu.VMEM(o.shape, o.dtype) for o in outs] + [pltpu.SemaphoreType.DMA((17,))],
+        in_specs=[smem] + [free] * 6 + [vmem],
+        out_specs=[free] * 3 + [vmem],
+        out_shape=outs + [shape((8, width), F32)],
+        scratch_shapes=[pltpu.VMEM(g.shape, g.dtype) for g in given] + [pltpu.VMEM(o.shape, o.dtype) for o in outs] + [pltpu.SemaphoreType.DMA((15,))],
         name="through",
     )(info, *given, gain2)
+
+def meet_kernel(info, got_h, active_h, slopes_h, turned_h, steep_h, *refs):
+    outs, (got, chunk, turned, steep, blocks, sems) = refs[:4], refs[4:]
+    order = (3, 1, 2, 0)
+    high, lowest = (info[6] & 15) >> 2, info[6] & 3
+    load = [pltpu.make_async_copy(got_h.at[4 * k : 4 * k + 4], got.at[k], sems.at[k]) for k in range(4)]
+    save = [pltpu.make_async_copy(blocks.at[k], outs[k], sems.at[4 + k]) for k in range(4)]
+
+    def columns(source, k):
+        at = pl.ds(pl.multiple_of((k ^ high) * 512, 512), 512)
+        return pltpu.make_async_copy(source.at[:, at], chunk.at[k], sems.at[8 + k])
+
+    for side, source in ((0, active_h), (1, slopes_h)):
+        @pl.when(info[7] == side)
+        def _(side=side, source=source):
+            extra = pltpu.make_async_copy(*((steep_h, steep) if side == 0 else (turned_h, turned)), sems.at[12])
+            extra.start()
+            for k in order:
+                columns(source, k).start()
+                load[k].start()
+            extra.wait()
+            low = steep[...].astype(BF16) if side == 0 else turned[...]
+            for k in order:
+                columns(source, k).wait()
+                made = dot(chunk[k], low, TN) if side == 0 else dot(low, chunk[k])
+                load[k].wait()
+                for b in range(4):
+                    piece = made[:, b * 128 : (b + 1) * 128]
+                    if side == 0:
+                        piece = made[b * 128 : (b + 1) * 128]
+                        piece = jnp.concatenate([piece[:, q * 128 : (q + 1) * 128] for q in range(4)])
+                    to = b ^ lowest
+                    blocks[k, to] = (piece + got[k, to].astype(F32)).astype(BF16)
+                save[k].start()
+
+    for copy in save:
+        copy.wait()
+
+def meet(info, got, active, slopes, turned, steep):
+    smem, free = pl.BlockSpec(memory_space=pltpu.SMEM), pl.BlockSpec(memory_space=pl.ANY)
+    block = (4,) + got.shape[1:]
+    n, width = steep.shape
+    return pl.pallas_call(
+        meet_kernel,
+        in_specs=[smem] + [free] * 5,
+        out_specs=[free] * 4,
+        out_shape=[jax.ShapeDtypeStruct(block, BF16)] * 4,
+        scratch_shapes=[pltpu.VMEM((4,) + block, BF16), pltpu.VMEM((4, n, 512), BF16), pltpu.VMEM(turned.shape, BF16), pltpu.VMEM(steep.shape, F32),
+                        pltpu.VMEM((4,) + block, BF16), pltpu.SemaphoreType.DMA((13,))],
+        name="meet",
+    )(info, got, active, slopes, turned, steep)
 
 CLASS = {(0, 0): 0, (1, 2): 0, (0, 1): 1, (1, 3): 1, (0, 2): 2, (0, 3): 3, (1, 0): 4, (1, 1): 5}
 
@@ -489,95 +518,109 @@
     )(info, stay, came, near, far, grad_mixed, gain, dense_rows)
 
 def place_kernel(firsts, info, *refs):
-    parts, (back, front, rows, columns, sems) = refs[: len(firsts)], refs[-5:]
-    pieces = [(part, i, first + i) for part, first in zip(parts, firsts) for i in range(part.shape[0])]
+    count = len(firsts)
+    given, (back, front), parts, (rows, columns, sems) = refs[:count], refs[-5 - count : -3 - count], refs[-3 - count : -3], refs[-3:]
+    load = [pltpu.make_async_copy(a, b, sems.at[i]) for i, (a, b) in enumerate(zip(given, parts))]
+    for copy in load:
+        copy.start()
     mine = info[6] & 15
     for side in range(2):
         @pl.when(info[7] == side)
         def _(side=side):
-            copies = []
-            for n, (part, i, r) in enumerate(pieces):
-                to = pl.ds(pl.multiple_of(((r & 15) ^ mine) * 128, 128), 128)
-                if (r >= 16) == (side == 1):
-                    for q in range(4):
-                        rows[n, :, q * 128 : (q + 1) * 128] = part[i, q * 128 : (q + 1) * 128, :].astype(F32)
-                    copies.append(pltpu.make_async_copy(rows.at[n], back.at[to, :], sems.at[n]))
-                else:
-                    columns[n] = part[i].astype(F32)
-                    copies.append(pltpu.make_async_copy(columns.at[n], front.at[:, to], sems.at[n]))
-                copies[-1].start()
+            copies, n = [], 0
+            for part, first, ready in zip(parts, firsts, load):
+                ready.wait()
+                for i in range(part.shape[0]):
+                    r = first + i
+                    to = pl.ds(pl.multiple_of(((r & 15) ^ mine) * 128, 128), 128)
+                    if (r >= 16) == (side == 1):
+                        for q in range(4):
+                            rows[n, :, q * 128 : (q + 1) * 128] = part[i, q * 128 : (q + 1) * 128, :].astype(F32)
+                        copies.append(pltpu.make_async_copy(rows.at[n], back.at[to, :], sems.at[count + n]))
+                    else:
+                        columns[n] = part[i].astype(F32)
+                        copies.append(pltpu.make_async_copy(columns.at[n], front.at[:, to], sems.at[count + n]))
+                    copies[-1].start()
+                    n += 1
             for copy in copies:
                 copy.wait()
 
 def place(info, parts, made, width):
-    smem, vmem, free = (pl.BlockSpec(memory_space=m) for m in (pltpu.SMEM, pltpu.VMEM, pl.ANY))
+    smem, free = pl.BlockSpec(memory_space=pltpu.SMEM), pl.BlockSpec(memory_space=pl.ANY)
     shape = jax.ShapeDtypeStruct
     count = sum(p.shape[0] for _, p in parts)
     return pl.pallas_call(
         functools.partial(place_kernel, [first for first, _ in parts]),
-        in_specs=[smem] + [vmem] * len(parts) + [free] * len(made),
+        in_specs=[smem] + [free] * (len(parts) + len(made)),
         out_specs=[free] * 2,
         out_shape=[shape((16 * 128, width), F32), shape((width, 16 * 128), F32)],
-        scratch_shapes=[pltpu.VMEM((count, 128, width), F32), pltpu.VMEM((count, width, 128), F32), pltpu.SemaphoreType.DMA((count,))],
+        scratch_shapes=[pltpu.VMEM(p.shape, BF16) for _, p in parts]
+                       + [pltpu.VMEM((count, 128, width), F32), pltpu.VMEM((count, width, 128), F32), pltpu.SemaphoreType.DMA((len(parts) + count,))],
         input_output_aliases={1 + len(parts) + i: i for i in range(len(made))},
         name="place",
     )(info, *[p for _, p in parts], *made)
 
 def sort_kernel(firsts, info, *refs):
-    parts, made, (tall, sems) = refs[: len(firsts)], refs[-6:-2], refs[-2:]
-    pieces = [(part, i, first + i) for part, first in zip(parts, firsts) for i in range(part.shape[0])]
+    count = len(firsts)
+    given, made, parts, (tall, sems) = refs[:count], refs[-6 - count : -2 - count], refs[-2 - count : -2], refs[-2:]
+    load = [pltpu.make_async_copy(a, b, sems.at[i]) for i, (a, b) in enumerate(zip(given, parts))]
+    for copy in load:
+        copy.start()
     size = parts[0].shape[1]
     mine = info[6]
-    for n, (part, i, r) in enumerate(pieces):
-        tall[n] = part[i].astype(F32)
+    pieces = []
+    for part, first, ready in zip(parts, firsts, load):
+        ready.wait()
+        for i in range(part.shape[0]):
+            tall[len(pieces)] = part[i].astype(F32)
+            pieces.append(first + i)
     for top in range(4):
         @pl.when((mine >> 3) == top)
         def _(top=top):
             copies = []
-            for n, (part, i, r) in enumerate(pieces):
+            for n, r in enumerate(pieces):
                 to = pl.ds(pl.multiple_of(((r ^ mine) & 7) * size, size), size)
-                copies.append(pltpu.make_async_copy(tall.at[n], made[top ^ (r >> 3)].at[to, :], sems.at[n]))
+                copies.append(pltpu.make_async_copy(tall.at[n], made[top ^ (r >> 3)].at[to, :], sems.at[count + n]))
                 copies[-1].start()
             for copy in copies:
                 copy.wait()
 
 def sort(info, parts, made, width):
-    smem, vmem, free = (pl.BlockSpec(memory_space=m) for m in (pltpu.SMEM, pltpu.VMEM, pl.ANY))
+    smem, free = pl.BlockSpec(memory_space=pltpu.SMEM), pl.BlockSpec(memory_space=pl.ANY)
     shape = jax.ShapeDtypeStruct((width, width), F32)
     count = sum(p.shape[0] for _, p in parts)
     return pl.pallas_call(
         functools.partial(sort_kernel, [first for first, _ in parts]),
-        in_specs=[smem] + [vmem] * len(parts) + [free] * len(made),
+        in_specs=[smem] + [free] * (len(parts) + len(made)),
         out_specs=[free] * 4,
         out_shape=[shape] * 4,
-        scratch_shapes=[pltpu.VMEM((count,) + parts[0][1].shape[1:], F32), pltpu.SemaphoreType.DMA((count,))],
+        scratch_shapes=[pltpu.VMEM(p.shape, BF16) for _, p in parts]
+                       + [pltpu.VMEM((count,) + parts[0][1].shape[1:], F32), pltpu.SemaphoreType.DMA((len(parts) + count,))],
         input_output_aliases={1 + len(parts) + i: i for i in range(len(made))},
         name="sort",
     )(info, *[p for _, p in parts], *made)
 
-def spread_kernel(keep, got, out):
-    out[...] = added(keep[...], got[...])
-
-def spread(keep, got, k):
-    block = (1,) + keep.shape[1:]
-    spec = pl.BlockSpec(block, lambda i: (4 * k + i, 0, 0))
-    return pl.pallas_call(
-        spread_kernel, grid=(4,), in_specs=[spec, spec], out_specs=pl.BlockSpec(block, lambda i: (i, 0, 0)),
-        out_shape=jax.ShapeDtypeStruct((4,) + keep.shape[1:], BF16), name="spread",
-    )(keep, got)
-
 def mix_kernel(*refs):
-    ins, outs = refs[: -4], refs[-4:]
-    for k in range(4):
-        outs[k][...] = added(*[term[k] for term in ins])
+    given, outs, terms, (sums, sems) = refs[:4], refs[4:8], refs[8:12], refs[12:]
+    order = (3, 1, 2, 0)
+    load = {(t, k): pltpu.make_async_copy(given[t].at[k], terms[t].at[k], sems.at[4 * t + k]) for k in order for t in range(4)}
+    save = {k: pltpu.make_async_copy(sums.at[k], outs[k], sems.at[16 + k]) for k in order}
+    for copy in load.values():
+        copy.start()
+    for k in order:
+        for t in range(4):
+            load[t, k].wait()
+        sums[k] = added(*[term[k] for term in terms])
+        save[k].start()
+    for copy in save.values():
+        copy.wait()
 
 def mix(terms):
     block = terms[0].shape[1:]
-    spec = pl.BlockSpec((4,) + block, lambda i: (0,) * (1 + len(block)))
-    out = pl.BlockSpec(block, lambda i: (0,) * len(block))
-    return pl.pallas_call(
-        mix_kernel, grid=(1,), in_specs=[spec] * len(terms), out_specs=[out] * 4,
-        out_shape=[jax.ShapeDtypeStruct(block, BF16)] * 4, name="mix",
+    free = pl.BlockSpec(memory_space=pl.ANY)
+    return pl.pallas_call(
+        mix_kernel, in_specs=[free] * 4, out_specs=[free] * 4, out_shape=[jax.ShapeDtypeStruct(block, BF16)] * 4,
+        scratch_shapes=[pltpu.VMEM((4,) + block, BF16)] * 5 + [pltpu.SemaphoreType.DMA((20,))], name="mix",
     )(*terms)
 
 def exchange(value, bits):
@@ -623,12 +666,12 @@
 
     token, send = wait(info, send)
     got = exchange(send, CORE)
-    keep, grad_mixed, grad_attended, grad_out_w, through_rows = through(token, slopes, w_in, mixed, steep, w_out, attended, active, turned, gain2)
+    grad_mixed, grad_attended, grad_out_w, through_rows = through(token, slopes, w_in, mixed, steep, w_out, attended, gain2)
     token, through_rows, got = wait(token, through_rows, got)
-
-    sends = [spread(keep, got, k) for k in (3, 1, 2)]
-    came = [exchange(s, m) for s, m in zip(sends, (xy[2], xy[0], xy[1]))]
+    stays, *sends = meet(token, got, active, slopes, turned, steep)
+
     token, sends = wait(token, sends)
+    came = [exchange(s, m) for s, m in zip(sends, xy)]
     rest_keep, rest_send, stay, leave, small = back(
         token, q_l, q_r, k_l, k_r, v_l, v_r, grad_attended, attended, inverse, expo, buckets, dense_rows, through_rows,
         hid_l, hid_r, near, near_other, far, far_other, w_query, w_key, w_value, grad_out_w)
@@ -636,7 +679,7 @@
 
     rest_got = exchange(rest_send, CORE)
     hidden_got = exchange(leave, CORE)
-    lines = mix([keep, got] + list(came))
+    lines = mix([stays] + list(came))
     token, lines = wait(token, lines)
     took = [exchange(lines[k + 1], m) for k, m in enumerate(zz)]
     token, rest_got, hidden_got = wait(token, rest_got, hidden_got)
@@ -663,51 +706,52 @@
     for part in rest_came:
         small = small + one_value(part[count:])
     rest_came = [part[:count].reshape((4,) + rest_keep.shape[1:]) for part in rest_came]
-    terms = two_terms(small)
-    lines = [added(rest_keep[k], rest_got[k], *[c[k] for c in rest_came]) for k in range(4)]
-    sends = [jnp.concatenate([lines[k], terms]) for k in (1, 2, 3)]
-    token, sends = wait(token, sends)
-    took = [exchange(s, m) for s, m in zip(sends, zz)]
-    token, back_line = wait(token, back_line)
+    piece = count // 4
+    lines = added(rest_keep[:4], rest_got[:4], *rest_came).reshape(-1, width)
+    send = jnp.concatenate([lines[2 * piece :], two_terms(small)])
+    token, send = wait(token, send)
+    took = exchange(send, line[1])
+    token, took = wait(token, took)
+    small = small + one_value(took[2 * piece :])
+    lines = added(lines[: 2 * piece], took[: 2 * piece])
+    send = jnp.concatenate([lines[piece:], two_terms(small)])
+    token, send, back_line, away_got = wait(token, send, back_line, away_got)
+    took = exchange(send, line[0])
 
     quarter = jnp.stack([whole] + back_line)
-    token, quarter, away_got = wait(token, quarter, away_got)
+    token, quarter = wait(token, quarter)
     from_y, from_x = exchange(quarter, ROW), exchange(quarter, NEAR_X)
     token, took = wait(token, took)
 
-    count = count // 4
-    for part in took:
-        small = small + one_value(part[count:])
-    rest = added(lines[0], *[part[:count] for part in took])
+    small = small + one_value(took[piece:])
+    rest = added(lines[:piece], took[:piece])
     for bit in further:
         rest = added(rest, exchange(rest, bit))
         small = small + exchange(small, bit)
     token, rest = wait(token, rest)
-    back_line = [exchange(rest, m) for m in zz]
-    token, back_line, from_y, from_x = wait(token, back_line, from_y, from_x)
-    fourth = jnp.stack([rest] + back_line)
+    rest_back = [exchange(rest, m) for m in zz]
+    token, rest_back, from_y, from_x = wait(token, rest_back, from_y, from_x)
+    fourth = jnp.stack([rest] + rest_back)
 
     sends = [from_x[:2], from_y[2:], fourth, fourth]
+    token, sends, quarter = wait(token, sends, quarter)
+    far_a, far_b, fourth_y, fourth_x = (exchange(s, m) for s, m in zip(sends, (ROW, NEAR_X, ROW, NEAR_X)))
+    other = exchange(quarter, CORE)
+    near_pair = jnp.concatenate([from_y, from_x])
+    grads = place(token, [(0, quarter), (4, from_y), (8, from_x)], [], width)
+    token, grads, other, near_pair, far_a, far_b, fourth_y, fourth_x = wait(token, grads, other, near_pair, far_a, far_b, fourth_y, fourth_x)
+
+    sends = [fourth_x[:2], fourth_y[2:], near_pair, jnp.concatenate([far_a, far_b]), jnp.concatenate([fourth, fourth_y, fourth_x])]
     token, sends = wait(token, sends)
-    far_a, far_b, fourth_y, fourth_x = (exchange(s, m) for s, m in zip(sends, (ROW, NEAR_X, ROW, NEAR_X)))
-    grads = place(token, [(0, quarter), (4, from_y), (8, from_x)], [], width)
-    token, grads, quarter, from_y, from_x = wait(token, grads, quarter, from_y, from_x)
-    others = [exchange(value, CORE) for value in (quarter, from_y, from_x)]
-    token, grads, others, far_a, far_b, fourth_y, fourth_x = wait(token, grads, others, far_a, far_b, fourth_y, fourth_x)
-
-    sends = [fourth_x[:2], fourth_y[2:], far_a, far_b]
-    token, sends = wait(token, sends)
-    last_a, last_b, other_a, other_b = (exchange(s, m) for s, m in zip(sends, (ROW, NEAR_X, CORE, CORE)))
-    grads = place(token, [(12, far_a), (14, far_b), (16, others[0]), (20, others[1]), (24, others[2])], grads, width)
-    token, grads, fourth, fourth_y, fourth_x = wait(token, grads, fourth, fourth_y, fourth_x)
-    pair = [exchange(value, CORE) for value in (fourth, fourth_y, fourth_x)]
-    token, grads, last_a, last_b, other_a, other_b, pair = wait(token, grads, last_a, last_b, other_a, other_b, pair)
-
-    ends = [exchange(last_a, CORE), exchange(last_b, CORE)]
-    made = sort(token, [(0, fourth), (4, fourth_y), (8, fourth_x), (12, last_a), (14, last_b), (16, pair[0]), (20, pair[1]), (24, pair[2])], [], width)
-    out_back, out_in = place(token, [(28, other_a), (30, other_b)], grads, width)
+    last_a, last_b, other_near, other_far, pair = (exchange(s, m) for s, m in zip(sends, (ROW, NEAR_X, CORE, CORE, CORE)))
+    grads = place(token, [(12, far_a), (14, far_b), (16, other)], grads, width)
+    token, grads, last_a, last_b, other_near, other_far, pair = wait(token, grads, last_a, last_b, other_near, other_far, pair)
+
+    ends = exchange(jnp.concatenate([last_a, last_b]), CORE)
+    made = sort(token, [(0, fourth), (4, fourth_y), (8, fourth_x), (12, last_a), (14, last_b), (16, pair)], [], width)
+    out_back, out_in = place(token, [(20, other_near), (28, other_far)], grads, width)
     token, made, ends = wait(token, made, ends)
-    out_out, out_query, out_key, out_value = sort(token, [(28, ends[0]), (30, ends[1])], made, width)
+    out_out, out_query, out_key, out_value = sort(token, [(28, ends)], made, width)
 
     pool_mine, pool_other = one_value(home[rows:])[:1], one_value(away_got[rows:])[:1]
     pooled = jnp.where(doc == 0, jnp.concatenate([pool_mine, pool_other]), jnp.concatenate([pool_other, pool_mine]))

time: 175 us -> 174 us (level)
  local copies, waits for them, and re-layouts: 7.28 us -> 16.4 us
  waiting for transfers between devices: 31.1 us -> 24.9 us
  Pallas kernels: 87 us -> 82.7 us
    pallas_call x5 -> x3, Pallas kernels: 21.6 us -> 14.6 us  [the longest x1 6.69 us: through(): pl.pallas_call(through_kernel, in_specs=[smem] + [free] * 6 + [vmem], out...]
    ppermute x43 -> x37, waiting for transfers between devices: 31.1 us -> 24.9 us  [exchange(): lax.ppermute(value, ('dp', 'blk'), [(i, i ^ bits) for i in range(size)])]
    unnamed x79 -> x62, local copies, waits for them, and re-layouts: 5.94 us -> 10.1 us
    slice x3 -> x8, local copies, waits for them, and re-layouts: 0.07 us -> 2.07 us  [the longest x3 1.95 us: local(): part[:count].reshape((4,) + rest_keep.shape[1:])]
    concatenate x1 -> x5, other arithmetic: 0.02 us -> 1.93 us  [the longest x1 1.79 us: local(): jnp.concatenate([far_a, far_b])]
    ppermute x43 -> x37, starting transfers between devices: 39.3 us -> 38.4 us  [exchange(): lax.ppermute(value, ('dp', 'blk'), [(i, i ^ bits) for i in range(size)])]
  transfers between devices with their start and end apart: 43 -> 37, of which waited for: 16 -> 12; matrix products, arithmetic and copies ran while one was open for 6% -> 8% of each run, Pallas kernels for 29% -> 29%
where the time goes in v2:
time: 174 us
  Pallas kernels  82.7 us (48%)
  starting transfers between devices  38.4 us (22%)
  waiting for transfers between devices  24.9 us (14%)
  local copies, waits for them, and re-layouts  16.4 us (9%)
  other arithmetic  9.71 us (6%)
    ppermute x37, starting transfers between devices, exchange(): lax.ppermute(value, ('dp', 'blk'), [(i, i ^ bits) for i in range(size)])  38.4 us
    ppermute x37, waiting for transfers between devices, exchange(): lax.ppermute(value, ('dp', 'blk'), [(i, i ^ bits) for i in range(size)])  24.9 us
    pallas_call x1, Pallas kernels, front(): pl.pallas_call(front_kernel, grid=(heads // 2,), in_specs=[smem, whole(co...  23.8 us
    pallas_call x1, Pallas kernels, back(): pl.pallas_call(back_kernel, grid=(width // 128,), in_specs=[smem, col(cou...  20.7 us
    pallas_call x3, Pallas kernels, place(): pl.pallas_call(functools.partial(place_kernel, [first for first, _ in par...  10.2 us
    unnamed x62, local copies, waits for them, and re-layouts  10.1 us
    pallas_call x2, Pallas kernels, sort(): pl.pallas_call(functools.partial(sort_kernel, [first for first, _ in part...  6.8 us
    pallas_call x1, Pallas kernels, through(): pl.pallas_call(through_kernel, in_specs=[smem] + [free] * 6 + [vmem], out...  6.69 us
  transfers between devices with their start and end apart: 37, of which 12 were waited for; matrix products, arithmetic and copies ran while one was open for 8% of the time, Pallas kernels for 29%

profile of v2, /device:TPU:0, one launch (start us, length us, event | category | flops | bytes accessed | tf_op | source)
XLA Modules:
  0.0 173.5 jit_solution(3894028689546664411)
XLA Ops:
  2.3 2.6 %collective-permute-start = (bf16[256,512]{1,0:T(8,128)(2,1)S(1)}, bf16[256,512]{1,0:T(8,128)(2,1)S(1)}, u32[]{:S(2)}, u32[]{:S(2)}) collective-permute-start(bf16[256,512]{1,0:T(8,128)(2,1)S(1)} %get-tuple-element.165), channel_id=1, source_target_pairs={{0,2},{1,3},{2,0},{3,1},{4,6},{5,7},{6,4},{7,5},{8,10},{9,11},{10,... | collective-permute-start | bytes 786440 | tf_op jit(solution)/shard_map/ppermute | solution.py:628
  7.4 3.3 %prepare.1 = (bf16[512,512]{1,0:T(8,128)(2,1)}, bf16[256,512]{1,0:T(8,128)(2,1)}, bf16[512,512]{1,0:T(8,128)(2,1)}, bf16[512,512]{1,0:T(8,128)(2,1)}, f32[8,2048]{1,0:T(8,128)}, /*index=5*/s32[16]{0:T(128)}) custom-call(s32[8]{0:T(128)} %compare_select_fusion.6.ids, s32[2]{0:T(128)} %pads.1, s32[2]{0:T(128)} %prefixes.1, bf16[256,512]{1,0:T(8,128)(2,1)} %copy-done, ...), custom_call_target="tpu_custom_call" | custom-call | tf_op jit(solution)/shard_map/prepare/pallas_call | solution.py:76
  11.8 1.5 collective-permute-done.2.far_other.far_other_h
  14.0 23.8 %front.1 = (bf16[512,512]{1,0:T(8,128)(2,1)}, bf16[256,512]{1,0:T(8,128)(2,1)}, bf16[512,512]{1,0:T(8,128)(2,1)}, bf16[512,512]{1,0:T(8,128)(2,1)}, bf16[8,512,1...) custom-call(s32[16]{0:T(128)} %get-tuple-element.302.info, ...), custom_call_target="tpu_custom_call" | custom-call | tf_op jit(solution)/shard_map/front/pallas_call | solution.py:232
  38.1 6.7 %through.1 = (f32[512,512]{1,0:T(8,128)}, bf16[512,512]{1,0:T(8,128)(2,1)}, bf16[512,512]{1,0:T(8,128)(2,1)}, f32[8,512]{1,0:T(8,128)}) custom-call(s32[16]{0:T(128)} %get-tuple-element.302.info, bf16[512,2048]{1,0:T(8,128)(2,1)} %get-tuple-element.176.slopes_h, bf16[512,2048]{1,0:T(8,128)(2,1)} %win_h.3, f32[512,512]{1,0:T(8,128)} %get-tuple-element.177.mixed_h, ...), custom_call_target="tpu_custom_call" | custom-call | tf_op jit(solution)/shard_map/through/pallas_call | solution.py:290
  46.1 5.4 %meet.1 = (bf16[4,512,128]{2,1,0:T(8,128)(2,1)}, bf16[4,512,128]{2,1,0:T(8,128)(2,1)}, bf16[4,512,128]{2,1,0:T(8,128)(2,1)}, bf16[4,512,128]{2,1,0:T(8,128)(2,1)}) custom-call(s32[16]{0:T(128)} %get-tuple-element.302.info, bf16[16,512,128]{2,1,0:T(8,128)(2,1)} %copy-done.5, bf16[512,2048]{1,0:T(8,128)(2,1)} %get-tuple-element.184.active_h, ...), custom_call_target="tpu_custom_call" | custom-call | tf_op jit(solution)/shard_map/meet/pallas_call | solution.py:340
  51.5 1.8 %collective-permute-start.4 = (bf16[4,512,128]{2,1,0:T(8,128)(2,1)}, bf16[4,512,128]{2,1,0:T(8,128)(2,1)S(1)}, u32[]{:S(2)}, u32[]{:S(2)}) collective-permute-start(bf16[4,512,128]{2,1,0:T(8,128)(2,1)} %get-tuple-element.204), channel_id=1, source_target_pairs={{0,2},{1,3},{2,0},{3,1},{4,6},{5,7},{6,4},{7,5},{8,10},{9,11},{10,... | collective-permute-start | bytes 1572872 | tf_op jit(solution)/shard_map/ppermute | solution.py:628
  55.1 20.7 %back.1 = (bf16[16,64,512]{2,1,0:T(8,128)(2,1)}, bf16[1056,512]{1,0:T(8,128)(2,1)}, f32[512,512]{1,0:T(8,128)}, bf16[544,512]{1,0:T(8,128)(2,1)}, f32[16,512]{1,0:T(8,128)}) custom-call(s32[16]{0:T(128)} %get-tuple-element.302.info, bf16[256,512]{1,0:T(8,128)(2,1)} %get-tuple-element.170.q_l.ql, bf16[256,512]{1,0:T(8,128)(2,1)} %get-tuple-element.190.qr, ...), custom_call_target="tpu_custom_call" | custom-call | tf_op jit(solution)/shard_map/back/pallas_call | solution.py:480
  75.8 2.4 %collective-permute-done.6.refs_3_ = bf16[4,512,128]{2,1,0:T(8,128)(2,1)S(1)} collective-permute-done((bf16[4,512,128]{2,1,0:T(8,128)(2,1)}, bf16[4,512,128]{2,1,0:T(8,128)(2,1)S(1)}, u32[]{:S(2)}, u32[]{:S(2)}) %collective-permute-start.6) | collective-permute-done | bytes 524320 | tf_op jit(solution)/shard_map/ppermute | solution.py:628
  79.5 2.6 %mix.1 = (bf16[512,128]{1,0:T(8,128)(2,1)}, bf16[512,128]{1,0:T(8,128)(2,1)}, bf16[512,128]{1,0:T(8,128)(2,1)}, bf16[512,128]{1,0:T(8,128)(2,1)}) custom-call(bf16[4,512,128]{2,1,0:T(8,128)(2,1)} %get-tuple-element.208.refs_0_, bf16[4,512,128]{2,1,0:T(8,128)(2,1)} %copy-done.15, bf16[4,512,128]{2,1,0:T(8,128)(2,1)} %copy-done.16, bf16[4,512,128]{2,1,0:T(8,128)(2,1)} %copy-done.17), custom_call_target="tpu_custom_call" | custom-call | tf_op jit(solution)/shard_map/mix/pallas_call | solution.py:621
  82.1 1.8 %collective-permute-start.9 = (bf16[512,128]{1,0:T(8,128)(2,1)}, bf16[512,128]{1,0:T(8,128)(2,1)S(1)}, u32[]{:S(2)}, u32[]{:S(2)}) collective-permute-start(bf16[512,128]{1,0:T(8,128)(2,1)} %get-tuple-element.228), channel_id=1, source_target_pairs={{0,8},{1,9},{2,10},{3,11},{4,12},{5,13},{6,14},{7,15},{8,0},{9,1},... | collective-permute-start | bytes 393224 | tf_op jit(solution)/shard_map/ppermute | solution.py:628
  83.9 2.6 %collective-permute-start.10 = (bf16[512,128]{1,0:T(8,128)(2,1)}, bf16[512,128]{1,0:T(8,128)(2,1)S(1)}, u32[]{:S(2)}, u32[]{:S(2)}) collective-permute-start(bf16[512,128]{1,0:T(8,128)(2,1)} %get-tuple-element.229), channel_id=1, source_target_pairs={{0,16},{1,17},{2,18},{3,19},{4,20},{5,21},{6,22},{7,23},{8,24},{9,... | collective-permute-start | bytes 393224 | tf_op jit(solution)/shard_map/ppermute | solution.py:628
  88.3 1.7 collective-permute-start.12
  92.2 3.2 %ending.1 = (bf16[288,512]{1,0:T(8,128)(2,1)}, bf16[288,512]{1,0:T(8,128)(2,1)}) custom-call(s32[16]{0:T(128)} %get-tuple-element.302.info, f32[512,512]{1,0:T(8,128)} %get-tuple-element.224.stay, bf16[544,512]{1,0:T(8,128)(2,1)} %copy-done.14, bf16[256,512]{1,0:T(8,128)(2,1)} %copy-done, bf16[256,512]{1,0:T(8,128)(2,1)} %copy-done.3, ...), custom_call_target="tpu_custom_call" | custom-call | tf_op jit(solution)/shard_map/ending/pallas_call | solution.py:516
  95.4 1.6 collective-permute-done.10
  98.0 2.5 %collective-permute-start.18 = (bf16[512,128]{1,0:T(8,128)(2,1)S(1)}, bf16[512,128]{1,0:T(8,128)(2,1)S(1)}, u32[]{:S(2)}, u32[]{:S(2)}) collective-permute-start(bf16[512,128]{1,0:T(8,128)(2,1)S(1)} %add_convert_fusion), channel_id=1, source_target_pairs={{0,24},{1,25},{2,26},{3,27},{4,28},{5,29},{6,30},{7,31},{8,16},{9,... | collective-permute-start | bytes 393224 | tf_op jit(solution)/shard_map/ppermute | solution.py:628
  102.5 1.5 collective-permute-start.19
  107.2 2.2 %collective-permute-start.15 = (bf16[160,512]{1,0:T(8,128)(2,1)S(1)}, bf16[160,512]{1,0:T(8,128)(2,1)S(1)}, u32[]{:S(2)}, u32[]{:S(2)}) collective-permute-start(bf16[160,512]{1,0:T(8,128)(2,1)S(1)} %pad_maximum_fusion.11), channel_id=1, source_target_pairs={{0,16},{1,17},{2,18},{3,19},{4,20},{5,21},{6,22},{7,23},{8,24},{9,... | collective-permute-start | bytes 491528 | tf_op jit(solution)/shard_map/ppermute | solution.py:628
  110.1 8.4 %collective-permute-done.15 = bf16[160,512]{1,0:T(8,128)(2,1)S(1)} collective-permute-done((bf16[160,512]{1,0:T(8,128)(2,1)S(1)}, bf16[160,512]{1,0:T(8,128)(2,1)S(1)}, u32[]{:S(2)}, u32[]{:S(2)}) %collective-permute-start.15) | collective-permute-done | bytes 163872 | tf_op jit(solution)/shard_map/ppermute | solution.py:628
  119.4 1.6 collective-permute-start.25
  121.0 1.5 collective-permute-start.24
  122.6 4.6 %collective-permute-done.20 = bf16[96,512]{1,0:T(8,128)(2,1)S(1)} collective-permute-done((bf16[96,512]{1,0:T(8,128)(2,1)S(1)}, bf16[96,512]{1,0:T(8,128)(2,1)S(1)}, u32[]{:S(2)}, u32[]{:S(2)}) %collective-permute-start.20) | collective-permute-done | bytes 98336 | tf_op jit(solution)/shard_map/ppermute | solution.py:628
  127.2 2.4 %collective-permute-start.23 = (bf16[64,512]{1,0:T(8,128)(2,1)S(1)}, bf16[64,512]{1,0:T(8,128)(2,1)S(1)}, u32[]{:S(2)}, u32[]{:S(2)}) collective-permute-start(bf16[64,512]{1,0:T(8,128)(2,1)S(1)} %add_convert_fusion.1), channel_id=1, source_target_pairs={{0,24},{1,25},{2,26},{3,27},{4,28},{5,29},{6,30},{7,31},{8,16},{9,... | collective-permute-start | bytes 196616 | tf_op jit(solution)/shard_map/ppermute | solution.py:628
  129.6 2.0 %collective-permute-start.21 = (bf16[64,512]{1,0:T(8,128)(2,1)S(1)}, bf16[64,512]{1,0:T(8,128)(2,1)S(1)}, u32[]{:S(2)}, u32[]{:S(2)}) collective-permute-start(bf16[64,512]{1,0:T(8,128)(2,1)S(1)} %add_convert_fusion.1), channel_id=1, source_target_pairs={{0,8},{1,9},{2,10},{3,11},{4,12},{5,13},{6,14},{7,15},{8,0},{9,1},... | collective-permute-start | bytes 196616 | tf_op jit(solution)/shard_map/ppermute | solution.py:628
  139.6 1.5 collective-permute-start.30
  142.5 3.5 %place.3 = (f32[2048,512]{1,0:T(8,128)}, f32[512,2048]{1,0:T(8,128)}) custom-call(s32[16]{0:T(128)} %get-tuple-element.302.info, bf16[4,512,128]{2,1,0:T(8,128)(2,1)} %copy-done.4, bf16[4,512,128]{2,1,0:T(8,128)(2,1)} %copy-done.2, bf16[4,512,128]{2,1,0:T(8,128)(2,1)} %copy-done.1), custom_call_target="tpu_custom_call" | custom-call | tf_op jit(solution)/shard_map/place/pallas_call | solution.py:552
  149.5 1.8 %pad_maximum_fusion.2 = bf16[4,512,128]{2,1,0:T(8,128)(2,1)} fusion(bf16[2,512,128]{2,1,0:T(8,128)(2,1)} %collective-permute-done.28.refs_1_, bf16[2,512,128]{2,1,0:T(8,128)(2,1)S(1)} %collective-permute-done.27.refs_0_), kind=kLoop, calls=%fused_computation.3 | loop fusion | flops 262144 | bytes 1048576 | tf_op jit(solution)/shard_map/concatenate | solution.py:744
  153.5 1.6 collective-permute-start.31
  156.4 3.0 %place.4 = (f32[2048,512]{1,0:T(8,128)}, f32[512,2048]{1,0:T(8,128)}) custom-call(s32[16]{0:T(128)} %get-tuple-element.302.info, bf16[2,512,128]{2,1,0:T(8,128)(2,1)} %copy-done.11, bf16[2,512,128]{2,1,0:T(8,128)(2,1)} %collective-permute-done.28.refs_1_, ...), custom_call_target="tpu_custom_call", output_to_operand_aliasing={{0}: (4, {}), {1}: (5, {})} | custom-call | tf_op jit(solution)/shard_map/place/pallas_call | solution.py:552
  162.1 4.3 %sort.2 = (f32[512,512]{1,0:T(8,128)}, f32[512,512]{1,0:T(8,128)}, f32[512,512]{1,0:T(8,128)}, f32[512,512]{1,0:T(8,128)}) custom-call(s32[16]{0:T(128)} %get-tuple-element.302.info, bf16[4,64,512]{2,1,0:T(8,128)(2,1)} %pad_maximum_fusion.9.refs_0_, bf16[4,64,512]{2,1,0:T(8,128)(2,1)} %copy-done.6, bf16[4,64,512]{2,1,0:T(8,128)(2,1)} %copy-done.7, ...), custom_call_target="tpu_custom_call" | custom-call | tf_op jit(solution)/shard_map/sort/pallas_call | solution.py:592
  166.5 3.7 %place.5 = (f32[2048,512]{1,0:T(8,128)}, f32[512,2048]{1,0:T(8,128)}) custom-call(s32[16]{0:T(128)} %get-tuple-element.302.info, bf16[8,512,128]{2,1,0:T(8,128)(2,1)} %copy-done.10, bf16[4,512,128]{2,1,0:T(8,128)(2,1)} %collective-permute-done.34.refs_1_, f32[2048,512]{1,0:T(8,128)} %get-tuple-element.314.refs_2_, ...), custom_call_target="tpu_custom_call", output_to_operand_aliasing={{0}: (3, {}), {1}: (4, {})} | custom-call | tf_op jit(solution)/shard_map/place/pallas_call | solution.py:552
  170.9 2.5 %sort.3 = (f32[512,512]{1,0:T(8,128)}, f32[512,512]{1,0:T(8,128)}, f32[512,512]{1,0:T(8,128)}, f32[512,512]{1,0:T(8,128)}) custom-call(s32[16]{0:T(128)} %get-tuple-element.302.info, bf16[4,64,512]{2,1,0:T(8,128)(2,1)} %copy-done.23, f32[512,512]{1,0:T(8,128)} %get-tuple-element.304.refs_1_, ...), custom_call_target="tpu_custom_call", output_to_operand_aliasing={{0}: (2, {}), {1}: (3, {}), {2}: (4, {}), {3}: (5, {})} | custom-call | tf_op jit(solution)/shard_map/sort/pallas_call | solution.py:592
  (155 shorter events, 41.8 us)
Async XLA Ops:
  2.3 9.5 %collective-permute-start = (bf16[256,512]{1,0:T(8,128)(2,1)S(1)}, bf16[256,512]{1,0:T(8,128)(2,1)S(1)}, u32[]{:S(2)}, u32[]{:S(2)}) collective-permute-start(bf16[256,512]{1,0:T(8,128)(2,1)S(1)} %get-tuple-element.165), channel_id=1, source_target_pairs={{0,2},{1,3},{2,0},{3,1},{4,6},{5,7},{6,4},{7,5},{8,10},{9,11},{10,... | collective-permute-start | bytes 786440 | tf_op jit(solution)/shard_map/ppermute | solution.py:628
  37.8 6.9 %collective-permute-start.3 = (bf16[16,512,128]{2,1,0:T(8,128)(2,1)}, bf16[16,512,128]{2,1,0:T(8,128)(2,1)S(1)}, u32[]{:S(2)}, u32[]{:S(2)}) collective-permute-start(bf16[16,512,128]{2,1,0:T(8,128)(2,1)} %get-tuple-element.181), channel_id=1, source_target_pairs={{0,1},{1,0},{2,3},{3,2},{4,5},{5,4},{6,7},{7,6},{8,9},{9,8},{10,11... | collective-permute-start | bytes 6291464 | tf_op jit(solution)/shard_map/ppermute | solution.py:628
  51.5 24.3 %collective-permute-start.4 = (bf16[4,512,128]{2,1,0:T(8,128)(2,1)}, bf16[4,512,128]{2,1,0:T(8,128)(2,1)S(1)}, u32[]{:S(2)}, u32[]{:S(2)}) collective-permute-start(bf16[4,512,128]{2,1,0:T(8,128)(2,1)} %get-tuple-element.204), channel_id=1, source_target_pairs={{0,2},{1,3},{2,0},{3,1},{4,6},{5,7},{6,4},{7,5},{8,10},{9,11},{10,... | collective-permute-start | bytes 1572872 | tf_op jit(solution)/shard_map/ppermute | solution.py:628
  53.4 22.5 %collective-permute-start.5 = (bf16[4,512,128]{2,1,0:T(8,128)(2,1)}, bf16[4,512,128]{2,1,0:T(8,128)(2,1)S(1)}, u32[]{:S(2)}, u32[]{:S(2)}) collective-permute-start(bf16[4,512,128]{2,1,0:T(8,128)(2,1)} %get-tuple-element.205), channel_id=1, source_target_pairs={{0,4},{1,5},{2,6},{3,7},{4,0},{5,1},{6,2},{7,3},{8,12},{9,13},{10,... | collective-permute-start | bytes 1572872 | tf_op jit(solution)/shard_map/ppermute | solution.py:628
  54.8 23.4 %collective-permute-start.6 = (bf16[4,512,128]{2,1,0:T(8,128)(2,1)}, bf16[4,512,128]{2,1,0:T(8,128)(2,1)S(1)}, u32[]{:S(2)}, u32[]{:S(2)}) collective-permute-start(bf16[4,512,128]{2,1,0:T(8,128)(2,1)} %get-tuple-element.206), channel_id=1, source_target_pairs={{0,6},{1,7},{2,4},{3,5},{4,2},{5,3},{6,0},{7,1},{8,14},{9,15},{10,... | collective-permute-start | bytes 1572872 | tf_op jit(solution)/shard_map/ppermute | solution.py:628
  79.0 7.6 %collective-permute-start.7 = (bf16[1056,512]{1,0:T(8,128)(2,1)}, bf16[1056,512]{1,0:T(8,128)(2,1)S(1)}, u32[]{:S(2)}, u32[]{:S(2)}) collective-permute-start(bf16[1056,512]{1,0:T(8,128)(2,1)} %get-tuple-element.217), channel_id=1, source_target_pairs={{0,1},{1,0},{2,3},{3,2},{4,5},{5,4},{6,7},{7,6},{8,9},{9,8},{10,11... | collective-permute-start | bytes 3244040 | tf_op jit(solution)/shard_map/ppermute | solution.py:628
  79.0 7.5 %collective-permute-start.8 = (bf16[544,512]{1,0:T(8,128)(2,1)}, bf16[544,512]{1,0:T(8,128)(2,1)S(1)}, u32[]{:S(2)}, u32[]{:S(2)}) collective-permute-start(bf16[544,512]{1,0:T(8,128)(2,1)} %get-tuple-element.218), channel_id=1, source_target_pairs={{0,1},{1,0},{2,3},{3,2},{4,5},{5,4},{6,7},{7,6},{8,9},{9,8},{10,11... | collective-permute-start | bytes 1671176 | tf_op jit(solution)/shard_map/ppermute | solution.py:628
  82.1 9.3 %collective-permute-start.9 = (bf16[512,128]{1,0:T(8,128)(2,1)}, bf16[512,128]{1,0:T(8,128)(2,1)S(1)}, u32[]{:S(2)}, u32[]{:S(2)}) collective-permute-start(bf16[512,128]{1,0:T(8,128)(2,1)} %get-tuple-element.228), channel_id=1, source_target_pairs={{0,8},{1,9},{2,10},{3,11},{4,12},{5,13},{6,14},{7,15},{8,0},{9,1},... | collective-permute-start | bytes 393224 | tf_op jit(solution)/shard_map/ppermute | solution.py:628
  83.9 13.1 %collective-permute-start.10 = (bf16[512,128]{1,0:T(8,128)(2,1)}, bf16[512,128]{1,0:T(8,128)(2,1)S(1)}, u32[]{:S(2)}, u32[]{:S(2)}) collective-permute-start(bf16[512,128]{1,0:T(8,128)(2,1)} %get-tuple-element.229), channel_id=1, source_target_pairs={{0,16},{1,17},{2,18},{3,19},{4,20},{5,21},{6,22},{7,23},{8,24},{9,... | collective-permute-start | bytes 393224 | tf_op jit(solution)/shard_map/ppermute | solution.py:628
  86.5 10.5 %collective-permute-start.11 = (bf16[512,128]{1,0:T(8,128)(2,1)}, bf16[512,128]{1,0:T(8,128)(2,1)}, u32[]{:S(2)}, u32[]{:S(2)}) collective-permute-start(bf16[512,128]{1,0:T(8,128)(2,1)} %get-tuple-element.230), channel_id=1, source_target_pairs={{0,24},{1,25},{2,26},{3,27},{4,28},{5,29},{6,30},{7,31},{8,16},{9,... | collective-permute-start | bytes 393224 | tf_op jit(solution)/shard_map/ppermute | solution.py:628
  88.3 13.5 %collective-permute-start.12 = (bf16[288,512]{1,0:T(8,128)(2,1)}, bf16[288,512]{1,0:T(8,128)(2,1)S(1)}, u32[]{:S(2)}, u32[]{:S(2)}) collective-permute-start(bf16[288,512]{1,0:T(8,128)(2,1)} %get-tuple-element.238), channel_id=1, source_target_pairs={{0,2},{1,3},{2,0},{3,1},{4,6},{5,7},{6,4},{7,5},{8,10},{9,11},{10,... | collective-permute-start | bytes 884744 | tf_op jit(solution)/shard_map/ppermute | solution.py:628
  89.9 12.5 %collective-permute-start.13 = (bf16[288,512]{1,0:T(8,128)(2,1)S(1)}, bf16[288,512]{1,0:T(8,128)(2,1)}, u32[]{:S(2)}, u32[]{:S(2)}) collective-permute-start(bf16[288,512]{1,0:T(8,128)(2,1)S(1)} %get-tuple-element.239), channel_id=1, source_target_pairs={{0,4},{1,5},{2,6},{3,7},{4,0},{5,1},{6,2},{7,3},{8,12},{9,13},{10,... | collective-permute-start | bytes 884744 | tf_op jit(solution)/shard_map/ppermute | solution.py:628
  91.4 12.8 %collective-permute-start.14 = (bf16[288,512]{1,0:T(8,128)(2,1)}, bf16[288,512]{1,0:T(8,128)(2,1)}, u32[]{:S(2)}, u32[]{:S(2)}) collective-permute-start(bf16[288,512]{1,0:T(8,128)(2,1)} %get-tuple-element.240), channel_id=1, source_target_pairs={{0,6},{1,7},{2,4},{3,5},{4,2},{5,3},{6,0},{7,1},{8,14},{9,15},{10,... | collective-permute-start | bytes 884744 | tf_op jit(solution)/shard_map/ppermute | solution.py:628
  98.0 21.3 %collective-permute-start.18 = (bf16[512,128]{1,0:T(8,128)(2,1)S(1)}, bf16[512,128]{1,0:T(8,128)(2,1)S(1)}, u32[]{:S(2)}, u32[]{:S(2)}) collective-permute-start(bf16[512,128]{1,0:T(8,128)(2,1)S(1)} %add_convert_fusion), channel_id=1, source_target_pairs={{0,24},{1,25},{2,26},{3,27},{4,28},{5,29},{6,30},{7,31},{8,16},{9,... | collective-permute-start | bytes 393224 | tf_op jit(solution)/shard_map/ppermute | solution.py:628
  100.5 18.9 %collective-permute-start.17 = (bf16[512,128]{1,0:T(8,128)(2,1)S(1)}, bf16[512,128]{1,0:T(8,128)(2,1)S(1)}, u32[]{:S(2)}, u32[]{:S(2)}) collective-permute-start(bf16[512,128]{1,0:T(8,128)(2,1)S(1)} %add_convert_fusion), channel_id=1, source_target_pairs={{0,16},{1,17},{2,18},{3,19},{4,20},{5,21},{6,22},{7,23},{8,24},{9,... | collective-permute-start | bytes 393224 | tf_op jit(solution)/shard_map/ppermute | solution.py:628
  101.8 17.5 %collective-permute-start.16 = (bf16[512,128]{1,0:T(8,128)(2,1)S(1)}, bf16[512,128]{1,0:T(8,128)(2,1)S(1)}, u32[]{:S(2)}, u32[]{:S(2)}) collective-permute-start(bf16[512,128]{1,0:T(8,128)(2,1)S(1)} %add_convert_fusion), channel_id=1, source_target_pairs={{0,8},{1,9},{2,10},{3,11},{4,12},{5,13},{6,14},{7,15},{8,0},{9,1},... | collective-permute-start | bytes 393224 | tf_op jit(solution)/shard_map/ppermute | solution.py:628
  102.5 16.9 %collective-permute-start.19 = (bf16[288,512]{1,0:T(8,128)(2,1)}, bf16[288,512]{1,0:T(8,128)(2,1)S(1)}, u32[]{:S(2)}, u32[]{:S(2)}) collective-permute-start(bf16[288,512]{1,0:T(8,128)(2,1)} %get-tuple-element.250), channel_id=1, source_target_pairs={{0,2},{1,3},{2,0},{3,1},{4,6},{5,7},{6,4},{7,5},{8,10},{9,11},{10,... | collective-permute-start | bytes 884744 | tf_op jit(solution)/shard_map/ppermute | solution.py:628
  107.2 11.3 %collective-permute-start.15 = (bf16[160,512]{1,0:T(8,128)(2,1)S(1)}, bf16[160,512]{1,0:T(8,128)(2,1)S(1)}, u32[]{:S(2)}, u32[]{:S(2)}) collective-permute-start(bf16[160,512]{1,0:T(8,128)(2,1)S(1)} %pad_maximum_fusion.11), channel_id=1, source_target_pairs={{0,16},{1,17},{2,18},{3,19},{4,20},{5,21},{6,22},{7,23},{8,24},{9,... | collective-permute-start | bytes 491528 | tf_op jit(solution)/shard_map/ppermute | solution.py:628
  119.4 15.3 %collective-permute-start.25 = (bf16[4,512,128]{2,1,0:T(8,128)(2,1)S(1)}, bf16[4,512,128]{2,1,0:T(8,128)(2,1)S(1)}, u32[]{:S(2)}, u32[]{:S(2)}) collective-permute-start(bf16[4,512,128]{2,1,0:T(8,128)(2,1)S(1)} %pad_maximum_fusion.1.refs_0_), channel_id=1, source_target_pairs={{0,4},{1,5},{2,6},{3,7},{4,0},{5,1},{6,2},{7,3},{8,12},{9,13},{10,... | collective-permute-start | bytes 1572872 | tf_op jit(solution)/shard_map/ppermute | solution.py:628
  121.0 13.8 %collective-permute-start.24 = (bf16[4,512,128]{2,1,0:T(8,128)(2,1)S(1)}, bf16[4,512,128]{2,1,0:T(8,128)(2,1)S(1)}, u32[]{:S(2)}, u32[]{:S(2)}) collective-permute-start(bf16[4,512,128]{2,1,0:T(8,128)(2,1)S(1)} %pad_maximum_fusion.1.refs_0_), channel_id=1, source_target_pairs={{0,2},{1,3},{2,0},{3,1},{4,6},{5,7},{6,4},{7,5},{8,10},{9,11},{10,... | collective-permute-start | bytes 1572872 | tf_op jit(solution)/shard_map/ppermute | solution.py:628
  127.2 6.1 %collective-permute-start.23 = (bf16[64,512]{1,0:T(8,128)(2,1)S(1)}, bf16[64,512]{1,0:T(8,128)(2,1)S(1)}, u32[]{:S(2)}, u32[]{:S(2)}) collective-permute-start(bf16[64,512]{1,0:T(8,128)(2,1)S(1)} %add_convert_fusion.1), channel_id=1, source_target_pairs={{0,24},{1,25},{2,26},{3,27},{4,28},{5,29},{6,30},{7,31},{8,16},{9,... | collective-permute-start | bytes 196616 | tf_op jit(solution)/shard_map/ppermute | solution.py:628
  137.1 9.6 %collective-permute-start.27 = (bf16[2,512,128]{2,1,0:T(8,128)(2,1)}, bf16[2,512,128]{2,1,0:T(8,128)(2,1)S(1)}, u32[]{:S(2)}, u32[]{:S(2)}) collective-permute-start(bf16[2,512,128]{2,1,0:T(8,128)(2,1)} %slice.218), channel_id=1, source_target_pairs={{0,2},{1,3},{2,0},{3,1},{4,6},{5,7},{6,4},{7,5},{8,10},{9,11},{10,... | collective-permute-start | bytes 786440 | tf_op jit(solution)/shard_map/ppermute | solution.py:628
  137.5 9.2 %collective-permute-start.28 = (bf16[2,512,128]{2,1,0:T(8,128)(2,1)}, bf16[2,512,128]{2,1,0:T(8,128)(2,1)}, u32[]{:S(2)}, u32[]{:S(2)}) collective-permute-start(bf16[2,512,128]{2,1,0:T(8,128)(2,1)} %slice.219), channel_id=1, source_target_pairs={{0,4},{1,5},{2,6},{3,7},{4,0},{5,1},{6,2},{7,3},{8,12},{9,13},{10,... | collective-permute-start | bytes 786440 | tf_op jit(solution)/shard_map/ppermute | solution.py:628
  138.7 9.1 %collective-permute-start.29 = (bf16[4,64,512]{2,1,0:T(8,128)(2,1)}, bf16[4,64,512]{2,1,0:T(8,128)(2,1)S(1)}, u32[]{:S(2)}, u32[]{:S(2)}) collective-permute-start(bf16[4,64,512]{2,1,0:T(8,128)(2,1)} %pad_maximum_fusion.9.refs_0_), channel_id=1, source_target_pairs={{0,2},{1,3},{2,0},{3,1},{4,6},{5,7},{6,4},{7,5},{8,10},{9,11},{10,... | collective-permute-start | bytes 786440 | tf_op jit(solution)/shard_map/ppermute | solution.py:628
  139.6 8.4 %collective-permute-start.30 = (bf16[4,64,512]{2,1,0:T(8,128)(2,1)}, bf16[4,64,512]{2,1,0:T(8,128)(2,1)S(1)}, u32[]{:S(2)}, u32[]{:S(2)}) collective-permute-start(bf16[4,64,512]{2,1,0:T(8,128)(2,1)} %pad_maximum_fusion.9.refs_0_), channel_id=1, source_target_pairs={{0,4},{1,5},{2,6},{3,7},{4,0},{5,1},{6,2},{7,3},{8,12},{9,13},{10,... | collective-permute-start | bytes 786440 | tf_op jit(solution)/shard_map/ppermute | solution.py:628
  141.1 6.9 %collective-permute-start.26 = (bf16[4,512,128]{2,1,0:T(8,128)(2,1)S(1)}, bf16[4,512,128]{2,1,0:T(8,128)(2,1)}, u32[]{:S(2)}, u32[]{:S(2)}) collective-permute-start(bf16[4,512,128]{2,1,0:T(8,128)(2,1)S(1)} %pad_maximum_fusion.1.refs_0_), channel_id=1, source_target_pairs={{0,1},{1,0},{2,3},{3,2},{4,5},{5,4},{6,7},{7,6},{8,9},{9,8},{10,11... | collective-permute-start | bytes 1572872 | tf_op jit(solution)/shard_map/ppermute | solution.py:628
  151.3 9.4 %collective-permute-start.33 = (bf16[8,512,128]{2,1,0:T(8,128)(2,1)S(1)}, bf16[8,512,128]{2,1,0:T(8,128)(2,1)S(1)}, u32[]{:S(2)}, u32[]{:S(2)}) collective-permute-start(bf16[8,512,128]{2,1,0:T(8,128)(2,1)S(1)} %pad_maximum_fusion), channel_id=1, source_target_pairs={{0,1},{1,0},{2,3},{3,2},{4,5},{5,4},{6,7},{7,6},{8,9},{9,8},{10,11... | collective-permute-start | bytes 3145736 | tf_op jit(solution)/shard_map/ppermute | solution.py:628
  151.4 9.3 %collective-permute-start.35 = (bf16[12,64,512]{2,1,0:T(8,128)(2,1)}, bf16[12,64,512]{2,1,0:T(8,128)(2,1)}, u32[]{:S(2)}, u32[]{:S(2)}) collective-permute-start(bf16[12,64,512]{2,1,0:T(8,128)(2,1)} %constant_dynamic-update-slice_fusion), channel_id=1, source_target_pairs={{0,1},{1,0},{2,3},{3,2},{4,5},{5,4},{6,7},{7,6},{8,9},{9,8},{10,11... | collective-permute-start | bytes 2359304 | tf_op jit(solution)/shard_map/ppermute | solution.py:628
  151.9 8.7 %collective-permute-start.34 = (bf16[4,512,128]{2,1,0:T(8,128)(2,1)}, bf16[4,512,128]{2,1,0:T(8,128)(2,1)}, u32[]{:S(2)}, u32[]{:S(2)}) collective-permute-start(bf16[4,512,128]{2,1,0:T(8,128)(2,1)} %pad_maximum_fusion.2), channel_id=1, source_target_pairs={{0,1},{1,0},{2,3},{3,2},{4,5},{5,4},{6,7},{7,6},{8,9},{9,8},{10,11... | collective-permute-start | bytes 1572872 | tf_op jit(solution)/shard_map/ppermute | solution.py:628
  153.5 5.9 %collective-permute-start.31 = (bf16[2,64,512]{2,1,0:T(8,128)(2,1)S(1)}, bf16[2,64,512]{2,1,0:T(8,128)(2,1)S(1)}, u32[]{:S(2)}, u32[]{:S(2)}) collective-permute-start(bf16[2,64,512]{2,1,0:T(8,128)(2,1)S(1)} %slice.220), channel_id=1, source_target_pairs={{0,2},{1,3},{2,0},{3,1},{4,6},{5,7},{6,4},{7,5},{8,10},{9,11},{10,... | collective-permute-start | bytes 393224 | tf_op jit(solution)/shard_map/ppermute | solution.py:628
  155.1 5.6 %collective-permute-start.32 = (bf16[2,64,512]{2,1,0:T(8,128)(2,1)S(1)}, bf16[2,64,512]{2,1,0:T(8,128)(2,1)S(1)}, u32[]{:S(2)}, u32[]{:S(2)}) collective-permute-start(bf16[2,64,512]{2,1,0:T(8,128)(2,1)S(1)} %slice.221), channel_id=1, source_target_pairs={{0,4},{1,5},{2,6},{3,7},{4,0},{5,1},{6,2},{7,3},{8,12},{9,13},{10,... | collective-permute-start | bytes 393224 | tf_op jit(solution)/shard_map/ppermute | solution.py:628
  160.7 9.5 %collective-permute-start.36 = (bf16[4,64,512]{2,1,0:T(8,128)(2,1)S(1)}, bf16[4,64,512]{2,1,0:T(8,128)(2,1)S(1)}, u32[]{:S(2)}, u32[]{:S(2)}) collective-permute-start(bf16[4,64,512]{2,1,0:T(8,128)(2,1)S(1)} %pad_maximum_fusion.10), channel_id=1, source_target_pairs={{0,1},{1,0},{2,3},{3,2},{4,5},{5,4},{6,7},{7,6},{8,9},{9,8},{10,11... | collective-permute-start | bytes 786440 | tf_op jit(solution)/shard_map/ppermute | solution.py:628
  (33 other events, 185.1 us)

commit v3 on v2

--- a/solution.py
+++ b/solution.py
@@ -79,7 +79,7 @@
         out_specs=[vmem] * 5 + [smem],
         out_shape=[shape(2 * rows), shape(rows), shape(2 * rows), shape(2 * rows),
                    jax.ShapeDtypeStruct((heads, span), F32), jax.ShapeDtypeStruct((16,), jnp.int32)],
-        name="prepare",
+        name="prepare", compiler_params=pltpu.CompilerParams(vmem_limit_bytes=14 << 20),
     )(ids, pads, prefixes, mine, other, wq, wk, wv, gain, bias, buckets)
 
 def back_pieces(to, active, low, mine):
@@ -241,7 +241,7 @@
                        + [pltpu.VMEM(wo.shape, BF16), pltpu.VMEM(win.shape, BF16), pltpu.VMEM(wback.shape, BF16),
                           pltpu.VMEM((2, 2 * count, 4 * count), BF16), pltpu.VMEM((2, 2 * count, 4 * count), F32),
                           pltpu.VMEM((2, 128, span), F32), pltpu.VMEM((2, 4 * count, 128), BF16), pltpu.SemaphoreType.DMA((16,))],
-        name="front",
+        name="front", compiler_params=pltpu.CompilerParams(vmem_limit_bytes=50 << 20),
     )(info, far, far_other, near, q_l, k_l, v_l, lines, wq, wk, wv, gain1, gain2, gain3, cots, wo, win, wback)
 
 def through_kernel(info, slopes_h, win_h, mixed_h, steep_h, wo_h, att_h, gain2, grad_mixed_o, grad_attended_o, grad_out_o, rows,
@@ -293,7 +293,7 @@
         out_specs=[free] * 3 + [vmem],
         out_shape=outs + [shape((8, width), F32)],
         scratch_shapes=[pltpu.VMEM(g.shape, g.dtype) for g in given] + [pltpu.VMEM(o.shape, o.dtype) for o in outs] + [pltpu.SemaphoreType.DMA((15,))],
-        name="through",
+        name="through", compiler_params=pltpu.CompilerParams(vmem_limit_bytes=16 << 20),
     )(info, *given, gain2)
 
 def meet_kernel(info, got_h, active_h, slopes_h, turned_h, steep_h, *refs):
@@ -344,7 +344,7 @@
         out_shape=[jax.ShapeDtypeStruct(block, BF16)] * 4,
         scratch_shapes=[pltpu.VMEM((4,) + block, BF16), pltpu.VMEM((4, n, 512), BF16), pltpu.VMEM(turned.shape, BF16), pltpu.VMEM(steep.shape, F32),
                         pltpu.VMEM((4,) + block, BF16), pltpu.SemaphoreType.DMA((13,))],
-        name="meet",
+        name="meet", compiler_params=pltpu.CompilerParams(vmem_limit_bytes=20 << 20),
     )(info, got, active, slopes, turned, steep)
 
 CLASS = {(0, 0): 0, (1, 2): 0, (0, 1): 1, (1, 3): 1, (0, 2): 2, (0, 3): 3, (1, 0): 4, (1, 1): 5}
@@ -489,7 +489,7 @@
                        + [pltpu.VMEM((2 * count, width), BF16), pltpu.VMEM((4 * count, width), BF16), pltpu.VMEM((4 * count, width), BF16),
                           pltpu.VMEM((8, 2048), F32), pltpu.VMEM((2, 6, 128, 384), F32), pltpu.VMEM((2, 128, 2048), F32),
                           pltpu.VMEM((2, 2 * count, 4 * count), BF16), pltpu.SemaphoreType.DMA((14,))],
-        name="back",
+        name="back", compiler_params=pltpu.CompilerParams(vmem_limit_bytes=44 << 20),
     )(info, ql, qr, kl, kr, vl, vr, gout, out, inv, expo, buckets, dense_rows, through_rows, *given, grad_out)
 
 def ending_kernel(info, stay, came, near, far, grad_mixed, gain, dense_rows, home, away):
@@ -514,7 +514,7 @@
     smem, vmem = pl.BlockSpec(memory_space=pltpu.SMEM), pl.BlockSpec(memory_space=pltpu.VMEM)
     shape = jax.ShapeDtypeStruct((count + 32, width), BF16)
     return pl.pallas_call(
-        ending_kernel, in_specs=[smem] + [vmem] * 7, out_specs=[vmem] * 2, out_shape=[shape, shape], name="ending"
+        ending_kernel, in_specs=[smem] + [vmem] * 7, out_specs=[vmem] * 2, out_shape=[shape, shape], name="ending", compiler_params=pltpu.CompilerParams(vmem_limit_bytes=10 << 20)
     )(info, stay, came, near, far, grad_mixed, gain, dense_rows)
 
 def place_kernel(firsts, info, *refs):
@@ -557,7 +557,7 @@
         scratch_shapes=[pltpu.VMEM(p.shape, BF16) for _, p in parts]
                        + [pltpu.VMEM((count, 128, width), F32), pltpu.VMEM((count, width, 128), F32), pltpu.SemaphoreType.DMA((len(parts) + count,))],
         input_output_aliases={1 + len(parts) + i: i for i in range(len(made))},
-        name="place",
+        name="place", compiler_params=pltpu.CompilerParams(vmem_limit_bytes=24 << 20),
     )(info, *[p for _, p in parts], *made)
 
 def sort_kernel(firsts, info, *refs):
@@ -597,7 +597,7 @@
         scratch_shapes=[pltpu.VMEM(p.shape, BF16) for _, p in parts]
                        + [pltpu.VMEM((count,) + parts[0][1].shape[1:], F32), pltpu.SemaphoreType.DMA((len(parts) + count,))],
         input_output_aliases={1 + len(parts) + i: i for i in range(len(made))},
-        name="sort",
+        name="sort", compiler_params=pltpu.CompilerParams(vmem_limit_bytes=12 << 20),
     )(info, *[p for _, p in parts], *made)
 
 def mix_kernel(*refs):
@@ -620,7 +620,7 @@
     free = pl.BlockSpec(memory_space=pl.ANY)
     return pl.pallas_call(
         mix_kernel, in_specs=[free] * 4, out_specs=[free] * 4, out_shape=[jax.ShapeDtypeStruct(block, BF16)] * 4,
-        scratch_shapes=[pltpu.VMEM((4,) + block, BF16)] * 5 + [pltpu.SemaphoreType.DMA((20,))], name="mix",
+        scratch_shapes=[pltpu.VMEM((4,) + block, BF16)] * 5 + [pltpu.SemaphoreType.DMA((20,))], name="mix", compiler_params=pltpu.CompilerParams(vmem_limit_bytes=10 << 20),
     )(*terms)
 
 def exchange(value, bits):

time: 174 us -> 164 us (0.943)
  waiting for transfers between devices: 24.9 us -> 38.3 us
  Pallas kernels: 82.7 us -> 70.4 us
  other arithmetic: 9.71 us -> 3.52 us
  starting transfers between devices: 38.4 us -> 35.1 us
    ppermute x37, waiting for transfers between devices: 24.9 us -> 38.3 us  [exchange(): lax.ppermute(value, ('dp', 'blk'), [(i, i ^ bits) for i in range(size)])]
    pallas_call x3, Pallas kernels: 10.2 us -> 6.96 us  [place(): pl.pallas_call(functools.partial(place_kernel, [first for first, _ in par...]
    ppermute x37, starting transfers between devices: 38.4 us -> 35.1 us  [exchange(): lax.ppermute(value, ('dp', 'blk'), [(i, i ^ bits) for i in range(size)])]
    unnamed x62 -> x68, local copies, waits for them, and re-layouts: 10.1 us -> 13.3 us
    pallas_call x1, Pallas kernels: 3.22 us -> 1.07 us  [ending(): pl.pallas_call(ending_kernel, in_specs=[smem] + [vmem] * 7, out_specs=[vm...]
    pallas_call x1, Pallas kernels: 6.69 us -> 4.66 us  [through(): pl.pallas_call(through_kernel, in_specs=[smem] + [free] * 6 + [vmem], out...]
    pallas_call x2, Pallas kernels: 6.8 us -> 4.77 us  [sort(): pl.pallas_call(functools.partial(sort_kernel, [first for first, _ in part...]
    slice x3, local copies, waits for them, and re-layouts: 1.95 us -> 0.06 us  [local(): part[:count].reshape((4,) + rest_keep.shape[1:])]
  transfers between devices with their start and end apart: 37 -> 37, of which waited for: 12 -> 15; matrix products, arithmetic and copies ran while one was open for 8% -> 3% of each run, Pallas kernels for 29% -> 26%
where the time goes in v3:
time: 164 us
  Pallas kernels  70.4 us (43%)
  waiting for transfers between devices  38.3 us (23%)
  starting transfers between devices  35.1 us (21%)
  local copies, waits for them, and re-layouts  14.7 us (9%)
  other arithmetic  3.52 us (2%)
    ppermute x37, waiting for transfers between devices, exchange(): lax.ppermute(value, ('dp', 'blk'), [(i, i ^ bits) for i in range(size)])  38.3 us
    ppermute x37, starting transfers between devices, exchange(): lax.ppermute(value, ('dp', 'blk'), [(i, i ^ bits) for i in range(size)])  35.1 us
    pallas_call x1, Pallas kernels, front(): pl.pallas_call(front_kernel, grid=(heads // 2,), in_specs=[smem, whole(co...  23.4 us
    pallas_call x1, Pallas kernels, back(): pl.pallas_call(back_kernel, grid=(width // 128,), in_specs=[smem, col(cou...  20 us
    unnamed x68, local copies, waits for them, and re-layouts  13.3 us
    pallas_call x3, Pallas kernels, place(): pl.pallas_call(functools.partial(place_kernel, [first for first, _ in par...  6.96 us
    pallas_call x2, Pallas kernels, sort(): pl.pallas_call(functools.partial(sort_kernel, [first for first, _ in part...  4.77 us
    pallas_call x1, Pallas kernels, through(): pl.pallas_call(through_kernel, in_specs=[smem] + [free] * 6 + [vmem], out...  4.66 us
  transfers between devices with their start and end apart: 37, of which 15 were waited for; matrix products, arithmetic and copies ran while one was open for 3% of the time, Pallas kernels for 26%

profile of v3, /device:TPU:0, one launch (start us, length us, event | category | flops | bytes accessed | tf_op | source)
XLA Modules:
  0.0 163.6 jit_solution(2786307985229566626)
XLA Ops:
  2.3 2.6 %collective-permute-start = (bf16[256,512]{1,0:T(8,128)(2,1)S(1)}, bf16[256,512]{1,0:T(8,128)(2,1)S(1)}, u32[]{:S(2)}, u32[]{:S(2)}) collective-permute-start(bf16[256,512]{1,0:T(8,128)(2,1)S(1)} %get-tuple-element.165), channel_id=1, source_target_pairs={{0,2},{1,3},{2,0},{3,1},{4,6},{5,7},{6,4},{7,5},{8,10},{9,11},{10,... | collective-permute-start | bytes 786440 | tf_op jit(solution)/shard_map/ppermute | solution.py:628
  11.5 2.0 %prepare.1 = (bf16[512,512]{1,0:T(8,128)(2,1)S(1)}, bf16[256,512]{1,0:T(8,128)(2,1)S(1)}, bf16[512,512]{1,0:T(8,128)(2,1)S(1)}, bf16[512,512]{1,0:T(8,128)(2,1)S...) custom-call(s32[8]{0:T(128)S(1)} %compare_select_fusion.6.ids, s32[2]{0:T(128)S(1)} %copy-done.29, s32[2]{0:T(128)S(1)} %copy-done.30, ...), custom_call_target="tpu_custom_call" | custom-call | tf_op jit(solution)/shard_map/prepare/pallas_call | solution.py:76
  16.7 23.4 %front.1 = (bf16[512,512]{1,0:T(8,128)(2,1)S(1)}, bf16[256,512]{1,0:T(8,128)(2,1)S(1)}, bf16[512,512]{1,0:T(8,128)(2,1)S(1)}, bf16[512,512]{1,0:T(8,128)(2,1)S(1...) custom-call(s32[16]{0:T(128)S(1)} %get-tuple-element.302.info, ...), custom_call_target="tpu_custom_call" | custom-call | tf_op jit(solution)/shard_map/front/pallas_call | solution.py:232
  41.1 1.8 %copy-done.1 = bf16[512,2048]{1,0:T(8,128)(2,1)S(1)} copy-done((bf16[512,2048]{1,0:T(8,128)(2,1)S(1)}, bf16[512,2048]{1,0:T(8,128)(2,1)}, u32[]{:S(2)}) %copy-start.1) | copy-done | bytes 2097176
  45.3 4.7 %through.1 = (f32[512,512]{1,0:T(8,128)S(1)}, bf16[512,512]{1,0:T(8,128)(2,1)S(1)}, bf16[512,512]{1,0:T(8,128)(2,1)S(1)}, f32[8,512]{1,0:T(8,128)S(1)}) custom-call(s32[16]{0:T(128)S(1)} %get-tuple-element.302.info, bf16[512,2048]{1,0:T(8,128)(2,1)S(1)} %copy-done.1, bf16[512,2048]{1,0:T(8,128)(2,1)S(1)} %copy-done, f32[512,512]{1,0:T(8,128)S(1)} %copy-done.17, ...), custom_call_target="tpu_custom_call" | custom-call | tf_op jit(solution)/shard_map/through/pallas_call | solution.py:290
  50.1 3.8 %meet.1 = (bf16[4,512,128]{2,1,0:T(8,128)(2,1)S(1)}, bf16[4,512,128]{2,1,0:T(8,128)(2,1)S(1)}, bf16[4,512,128]{2,1,0:T(8,128)(2,1)S(1)}, bf16[4,512,128]{2,1,0:T(8,128)(2,1)S(1)}) custom-call(s32[16]{0:T(128)S(1)} %get-tuple-element.302.info, bf16[16,512,128]{2,1,0:T(8,128)(2,1)S(1)} %collective-permute-done.3.got_h, bf16[512,2048]{1,0:T(8,128)(2,1)S(1)} %copy-done.14, ...), custom_call_target="tpu_custom_call" | custom-call | tf_op jit(solution)/shard_map/meet/pallas_call | solution.py:340
  54.6 1.5 collective-permute-start.5
  57.5 20.0 %back.1 = (bf16[16,64,512]{2,1,0:T(8,128)(2,1)S(1)}, bf16[1056,512]{1,0:T(8,128)(2,1)}, f32[512,512]{1,0:T(8,128)}, bf16[544,512]{1,0:T(8,128)(2,1)S(1)}, f32[16,512]{1,0:T(8,128)S(1)}) custom-call(s32[16]{0:T(128)S(1)} %get-tuple-element.302.info, bf16[256,512]{1,0:T(8,128)(2,1)S(1)} %get-tuple-element.170.q_l.ql, ...), custom_call_target="tpu_custom_call" | custom-call | tf_op jit(solution)/shard_map/back/pallas_call | solution.py:480
  77.5 2.7 %collective-permute-done.6.refs_3_ = bf16[4,512,128]{2,1,0:T(8,128)(2,1)S(1)} collective-permute-done((bf16[4,512,128]{2,1,0:T(8,128)(2,1)S(1)}, bf16[4,512,128]{2,1,0:T(8,128)(2,1)S(1)}, u32[]{:S(2)}, u32[]{:S(2)}) %collective-permute-start.6) | collective-permute-done | bytes 524320 | tf_op jit(solution)/shard_map/ppermute | solution.py:628
  80.7 3.8 %mix.1 = (bf16[512,128]{1,0:T(8,128)(2,1)S(1)}, bf16[512,128]{1,0:T(8,128)(2,1)S(1)}, bf16[512,128]{1,0:T(8,128)(2,1)S(1)}, bf16[512,128]{1,0:T(8,128)(2,1)S(1)}) custom-call(bf16[4,512,128]{2,1,0:T(8,128)(2,1)S(1)} %get-tuple-element.208.refs_0_, bf16[4,512,128]{2,1,0:T(8,128)(2,1)S(1)} %collective-permute-done.4.refs_1_, ...), custom_call_target="tpu_custom_call" | custom-call | tf_op jit(solution)/shard_map/mix/pallas_call | solution.py:621
  84.5 1.6 %collective-permute-start.9 = (bf16[512,128]{1,0:T(8,128)(2,1)S(1)}, bf16[512,128]{1,0:T(8,128)(2,1)S(1)}, u32[]{:S(2)}, u32[]{:S(2)}) collective-permute-start(bf16[512,128]{1,0:T(8,128)(2,1)S(1)} %get-tuple-element.228), channel_id=1, source_target_pairs={{0,8},{1,9},{2,10},{3,11},{4,12},{5,13},{6,14},{7,15},{8,0},{9,1},... | collective-permute-start | bytes 393224 | tf_op jit(solution)/shard_map/ppermute | solution.py:628
  86.2 2.6 %collective-permute-start.10 = (bf16[512,128]{1,0:T(8,128)(2,1)S(1)}, bf16[512,128]{1,0:T(8,128)(2,1)S(1)}, u32[]{:S(2)}, u32[]{:S(2)}) collective-permute-start(bf16[512,128]{1,0:T(8,128)(2,1)S(1)} %get-tuple-element.229), channel_id=1, source_target_pairs={{0,16},{1,17},{2,18},{3,19},{4,20},{5,21},{6,22},{7,23},{8,24},{9,... | collective-permute-start | bytes 393224 | tf_op jit(solution)/shard_map/ppermute | solution.py:628
  90.1 1.5 collective-permute-start.13
  91.8 1.6 collective-permute-start.14
  94.4 4.7 %collective-permute-done.10 = bf16[512,128]{1,0:T(8,128)(2,1)S(1)} collective-permute-done((bf16[512,128]{1,0:T(8,128)(2,1)S(1)}, bf16[512,128]{1,0:T(8,128)(2,1)S(1)}, u32[]{:S(2)}, u32[]{:S(2)}) %collective-permute-start.10) | collective-permute-done | bytes 131104 | tf_op jit(solution)/shard_map/ppermute | solution.py:628
  99.2 2.4 %collective-permute-start.18 = (bf16[512,128]{1,0:T(8,128)(2,1)S(1)}, bf16[512,128]{1,0:T(8,128)(2,1)S(1)}, u32[]{:S(2)}, u32[]{:S(2)}) collective-permute-start(bf16[512,128]{1,0:T(8,128)(2,1)S(1)} %add_convert_fusion), channel_id=1, source_target_pairs={{0,24},{1,25},{2,26},{3,27},{4,28},{5,29},{6,30},{7,31},{8,16},{9,... | collective-permute-start | bytes 393224 | tf_op jit(solution)/shard_map/ppermute | solution.py:628
  105.6 1.6 collective-permute-start.15
  107.2 12.5 %collective-permute-done.15 = bf16[160,512]{1,0:T(8,128)(2,1)S(1)} collective-permute-done((bf16[160,512]{1,0:T(8,128)(2,1)S(1)}, bf16[160,512]{1,0:T(8,128)(2,1)S(1)}, u32[]{:S(2)}, u32[]{:S(2)}) %collective-permute-start.15) | collective-permute-done | bytes 163872 | tf_op jit(solution)/shard_map/ppermute | solution.py:628
  119.9 1.6 collective-permute-start.25
  122.1 4.6 %collective-permute-done.20 = bf16[96,512]{1,0:T(8,128)(2,1)S(1)} collective-permute-done((bf16[96,512]{1,0:T(8,128)(2,1)S(1)}, bf16[96,512]{1,0:T(8,128)(2,1)S(1)}, u32[]{:S(2)}, u32[]{:S(2)}) %collective-permute-start.20) | collective-permute-done | bytes 98336 | tf_op jit(solution)/shard_map/ppermute | solution.py:628
  126.7 2.5 %collective-permute-start.23 = (bf16[64,512]{1,0:T(8,128)(2,1)S(1)}, bf16[64,512]{1,0:T(8,128)(2,1)S(1)}, u32[]{:S(2)}, u32[]{:S(2)}) collective-permute-start(bf16[64,512]{1,0:T(8,128)(2,1)S(1)} %add_convert_fusion.1), channel_id=1, source_target_pairs={{0,24},{1,25},{2,26},{3,27},{4,28},{5,29},{6,30},{7,31},{8,16},{9,... | collective-permute-start | bytes 196616 | tf_op jit(solution)/shard_map/ppermute | solution.py:628
  129.2 1.9 %collective-permute-start.21 = (bf16[64,512]{1,0:T(8,128)(2,1)S(1)}, bf16[64,512]{1,0:T(8,128)(2,1)S(1)}, u32[]{:S(2)}, u32[]{:S(2)}) collective-permute-start(bf16[64,512]{1,0:T(8,128)(2,1)S(1)} %add_convert_fusion.1), channel_id=1, source_target_pairs={{0,8},{1,9},{2,10},{3,11},{4,12},{5,13},{6,14},{7,15},{8,0},{9,1},... | collective-permute-start | bytes 196616 | tf_op jit(solution)/shard_map/ppermute | solution.py:628
  131.2 1.8 %collective-permute-done.23 = bf16[64,512]{1,0:T(8,128)(2,1)S(1)} collective-permute-done((bf16[64,512]{1,0:T(8,128)(2,1)S(1)}, bf16[64,512]{1,0:T(8,128)(2,1)S(1)}, u32[]{:S(2)}, u32[]{:S(2)}) %collective-permute-start.23) | collective-permute-done | bytes 65568 | tf_op jit(solution)/shard_map/ppermute | solution.py:628
  134.5 1.5 collective-permute-start.27
  137.1 1.5 collective-permute-start.30
  138.8 2.5 %place.3 = (f32[2048,512]{1,0:T(8,128)}, f32[512,2048]{1,0:T(8,128)}) custom-call(s32[16]{0:T(128)S(1)} %get-tuple-element.302.info, bf16[4,512,128]{2,1,0:T(8,128)(2,1)S(1)} %pad_maximum_fusion.1.refs_0_, bf16[4,512,128]{2,1,0:T(8,128)(2,1)S(1)} %collective-permute-done.24.refs_1_, bf16[4,512,128]{2,1,0:T(8,128)(2,1)S(1)} %collective-permute-done.25.refs_2_), custom_call_target="tpu_custom_call" | custom-call | tf_op jit(solution)/shard_map/place/pallas_call | solution.py:552
  143.4 1.7 %collective-permute-done.29.refs_1_ = bf16[4,64,512]{2,1,0:T(8,128)(2,1)S(1)} collective-permute-done((bf16[4,64,512]{2,1,0:T(8,128)(2,1)S(1)}, bf16[4,64,512]{2,1,0:T(8,128)(2,1)S(1)}, u32[]{:S(2)}, u32[]{:S(2)}) %collective-permute-start.29) | collective-permute-done | bytes 262176 | tf_op jit(solution)/shard_map/ppermute | solution.py:628
  149.8 2.1 %place.4 = (f32[2048,512]{1,0:T(8,128)}, f32[512,2048]{1,0:T(8,128)}) custom-call(s32[16]{0:T(128)S(1)} %get-tuple-element.302.info, bf16[2,512,128]{2,1,0:T(8,128)(2,1)S(1)} %collective-permute-done.27.refs_0_, bf16[2,512,128]{2,1,0:T(8,128)(2,1)S(1)} %collective-permute-done.28.refs_1_, ...), custom_call_target="tpu_custom_call", output_to_operand_aliasing={{0}: (4, {}), {1}: (5, {})} | custom-call | tf_op jit(solution)/shard_map/place/pallas_call | solution.py:552
  151.9 2.6 %collective-permute-done.31.refs_3_ = bf16[2,64,512]{2,1,0:T(8,128)(2,1)S(1)} collective-permute-done((bf16[2,64,512]{2,1,0:T(8,128)(2,1)S(1)}, bf16[2,64,512]{2,1,0:T(8,128)(2,1)S(1)}, u32[]{:S(2)}, u32[]{:S(2)}) %collective-permute-start.31) | collective-permute-done | bytes 131104 | tf_op jit(solution)/shard_map/ppermute | solution.py:628
  156.2 3.3 %sort.2 = (f32[512,512]{1,0:T(8,128)}, f32[512,512]{1,0:T(8,128)}, f32[512,512]{1,0:T(8,128)}, f32[512,512]{1,0:T(8,128)}) custom-call(s32[16]{0:T(128)S(1)} %get-tuple-element.302.info, bf16[4,64,512]{2,1,0:T(8,128)(2,1)S(1)} %pad_maximum_fusion.9.refs_0_, bf16[4,64,512]{2,1,0:T(8,128)(2,1)S(1)} %collective-permute-done.29.refs_1_, ...), custom_call_target="tpu_custom_call" | custom-call | tf_op jit(solution)/shard_map/sort/pallas_call | solution.py:592
  159.5 2.4 %place.5 = (f32[2048,512]{1,0:T(8,128)}, f32[512,2048]{1,0:T(8,128)}) custom-call(s32[16]{0:T(128)S(1)} %get-tuple-element.302.info, bf16[8,512,128]{2,1,0:T(8,128)(2,1)S(1)} %collective-permute-done.33.refs_0_, bf16[4,512,128]{2,1,0:T(8,128)(2,1)S(1)} %collective-permute-done.34.refs_1_, ...), custom_call_target="tpu_custom_call", output_to_operand_aliasing={{0}: (3, {}), {1}: (4, {})} | custom-call | tf_op jit(solution)/shard_map/place/pallas_call | solution.py:552
  162.0 1.4 sort.3
  (161 shorter events, 36.0 us)
Async XLA Ops:
  2.3 12.8 %collective-permute-start = (bf16[256,512]{1,0:T(8,128)(2,1)S(1)}, bf16[256,512]{1,0:T(8,128)(2,1)S(1)}, u32[]{:S(2)}, u32[]{:S(2)}) collective-permute-start(bf16[256,512]{1,0:T(8,128)(2,1)S(1)} %get-tuple-element.165), channel_id=1, source_target_pairs={{0,2},{1,3},{2,0},{3,1},{4,6},{5,7},{6,4},{7,5},{8,10},{9,11},{10,... | collective-permute-start | bytes 786440 | tf_op jit(solution)/shard_map/ppermute | solution.py:628
  40.9 9.1 %collective-permute-start.3 = (bf16[16,512,128]{2,1,0:T(8,128)(2,1)}, bf16[16,512,128]{2,1,0:T(8,128)(2,1)S(1)}, u32[]{:S(2)}, u32[]{:S(2)}) collective-permute-start(bf16[16,512,128]{2,1,0:T(8,128)(2,1)} %get-tuple-element.181), channel_id=1, source_target_pairs={{0,1},{1,0},{2,3},{3,2},{4,5},{5,4},{6,7},{7,6},{8,9},{9,8},{10,11... | collective-permute-start | bytes 6291464 | tf_op jit(solution)/shard_map/ppermute | solution.py:628
  53.9 23.6 %collective-permute-start.4 = (bf16[4,512,128]{2,1,0:T(8,128)(2,1)S(1)}, bf16[4,512,128]{2,1,0:T(8,128)(2,1)S(1)}, u32[]{:S(2)}, u32[]{:S(2)}) collective-permute-start(bf16[4,512,128]{2,1,0:T(8,128)(2,1)S(1)} %get-tuple-element.204), channel_id=1, source_target_pairs={{0,2},{1,3},{2,0},{3,1},{4,6},{5,7},{6,4},{7,5},{8,10},{9,11},{10,... | collective-permute-start | bytes 1572872 | tf_op jit(solution)/shard_map/ppermute | solution.py:628
  54.6 22.9 %collective-permute-start.5 = (bf16[4,512,128]{2,1,0:T(8,128)(2,1)S(1)}, bf16[4,512,128]{2,1,0:T(8,128)(2,1)S(1)}, u32[]{:S(2)}, u32[]{:S(2)}) collective-permute-start(bf16[4,512,128]{2,1,0:T(8,128)(2,1)S(1)} %get-tuple-element.205), channel_id=1, source_target_pairs={{0,4},{1,5},{2,6},{3,7},{4,0},{5,1},{6,2},{7,3},{8,12},{9,13},{10,... | collective-permute-start | bytes 1572872 | tf_op jit(solution)/shard_map/ppermute | solution.py:628
  56.1 24.1 %collective-permute-start.6 = (bf16[4,512,128]{2,1,0:T(8,128)(2,1)S(1)}, bf16[4,512,128]{2,1,0:T(8,128)(2,1)S(1)}, u32[]{:S(2)}, u32[]{:S(2)}) collective-permute-start(bf16[4,512,128]{2,1,0:T(8,128)(2,1)S(1)} %get-tuple-element.206), channel_id=1, source_target_pairs={{0,6},{1,7},{2,4},{3,5},{4,2},{5,3},{6,0},{7,1},{8,14},{9,15},{10,... | collective-permute-start | bytes 1572872 | tf_op jit(solution)/shard_map/ppermute | solution.py:628
  80.2 8.8 %collective-permute-start.7 = (bf16[1056,512]{1,0:T(8,128)(2,1)}, bf16[1056,512]{1,0:T(8,128)(2,1)S(1)}, u32[]{:S(2)}, u32[]{:S(2)}) collective-permute-start(bf16[1056,512]{1,0:T(8,128)(2,1)} %get-tuple-element.217), channel_id=1, source_target_pairs={{0,1},{1,0},{2,3},{3,2},{4,5},{5,4},{6,7},{7,6},{8,9},{9,8},{10,11... | collective-permute-start | bytes 3244040 | tf_op jit(solution)/shard_map/ppermute | solution.py:628
  80.2 8.8 %collective-permute-start.8 = (bf16[544,512]{1,0:T(8,128)(2,1)S(1)}, bf16[544,512]{1,0:T(8,128)(2,1)S(1)}, u32[]{:S(2)}, u32[]{:S(2)}) collective-permute-start(bf16[544,512]{1,0:T(8,128)(2,1)S(1)} %get-tuple-element.218), channel_id=1, source_target_pairs={{0,1},{1,0},{2,3},{3,2},{4,5},{5,4},{6,7},{7,6},{8,9},{9,8},{10,11... | collective-permute-start | bytes 1671176 | tf_op jit(solution)/shard_map/ppermute | solution.py:628
  84.5 7.3 %collective-permute-start.9 = (bf16[512,128]{1,0:T(8,128)(2,1)S(1)}, bf16[512,128]{1,0:T(8,128)(2,1)S(1)}, u32[]{:S(2)}, u32[]{:S(2)}) collective-permute-start(bf16[512,128]{1,0:T(8,128)(2,1)S(1)} %get-tuple-element.228), channel_id=1, source_target_pairs={{0,8},{1,9},{2,10},{3,11},{4,12},{5,13},{6,14},{7,15},{8,0},{9,1},... | collective-permute-start | bytes 393224 | tf_op jit(solution)/shard_map/ppermute | solution.py:628
  86.2 12.9 %collective-permute-start.10 = (bf16[512,128]{1,0:T(8,128)(2,1)S(1)}, bf16[512,128]{1,0:T(8,128)(2,1)S(1)}, u32[]{:S(2)}, u32[]{:S(2)}) collective-permute-start(bf16[512,128]{1,0:T(8,128)(2,1)S(1)} %get-tuple-element.229), channel_id=1, source_target_pairs={{0,16},{1,17},{2,18},{3,19},{4,20},{5,21},{6,22},{7,23},{8,24},{9,... | collective-permute-start | bytes 393224 | tf_op jit(solution)/shard_map/ppermute | solution.py:628
  88.8 10.3 %collective-permute-start.11 = (bf16[512,128]{1,0:T(8,128)(2,1)S(1)}, bf16[512,128]{1,0:T(8,128)(2,1)S(1)}, u32[]{:S(2)}, u32[]{:S(2)}) collective-permute-start(bf16[512,128]{1,0:T(8,128)(2,1)S(1)} %get-tuple-element.230), channel_id=1, source_target_pairs={{0,24},{1,25},{2,26},{3,27},{4,28},{5,29},{6,30},{7,31},{8,16},{9,... | collective-permute-start | bytes 393224 | tf_op jit(solution)/shard_map/ppermute | solution.py:628
  89.4 13.5 %collective-permute-start.12 = (bf16[288,512]{1,0:T(8,128)(2,1)S(1)}, bf16[288,512]{1,0:T(8,128)(2,1)S(1)}, u32[]{:S(2)}, u32[]{:S(2)}) collective-permute-start(bf16[288,512]{1,0:T(8,128)(2,1)S(1)} %get-tuple-element.238), channel_id=1, source_target_pairs={{0,2},{1,3},{2,0},{3,1},{4,6},{5,7},{6,4},{7,5},{8,10},{9,11},{10,... | collective-permute-start | bytes 884744 | tf_op jit(solution)/shard_map/ppermute | solution.py:628
  90.1 13.5 %collective-permute-start.13 = (bf16[288,512]{1,0:T(8,128)(2,1)S(1)}, bf16[288,512]{1,0:T(8,128)(2,1)S(1)}, u32[]{:S(2)}, u32[]{:S(2)}) collective-permute-start(bf16[288,512]{1,0:T(8,128)(2,1)S(1)} %get-tuple-element.239), channel_id=1, source_target_pairs={{0,4},{1,5},{2,6},{3,7},{4,0},{5,1},{6,2},{7,3},{8,12},{9,13},{10,... | collective-permute-start | bytes 884744 | tf_op jit(solution)/shard_map/ppermute | solution.py:628
  91.8 13.4 %collective-permute-start.14 = (bf16[288,512]{1,0:T(8,128)(2,1)S(1)}, bf16[288,512]{1,0:T(8,128)(2,1)S(1)}, u32[]{:S(2)}, u32[]{:S(2)}) collective-permute-start(bf16[288,512]{1,0:T(8,128)(2,1)S(1)} %get-tuple-element.240), channel_id=1, source_target_pairs={{0,6},{1,7},{2,4},{3,5},{4,2},{5,3},{6,0},{7,1},{8,14},{9,15},{10,... | collective-permute-start | bytes 884744 | tf_op jit(solution)/shard_map/ppermute | solution.py:628
  99.2 20.6 %collective-permute-start.18 = (bf16[512,128]{1,0:T(8,128)(2,1)S(1)}, bf16[512,128]{1,0:T(8,128)(2,1)S(1)}, u32[]{:S(2)}, u32[]{:S(2)}) collective-permute-start(bf16[512,128]{1,0:T(8,128)(2,1)S(1)} %add_convert_fusion), channel_id=1, source_target_pairs={{0,24},{1,25},{2,26},{3,27},{4,28},{5,29},{6,30},{7,31},{8,16},{9,... | collective-permute-start | bytes 393224 | tf_op jit(solution)/shard_map/ppermute | solution.py:628
  101.6 18.1 %collective-permute-start.17 = (bf16[512,128]{1,0:T(8,128)(2,1)S(1)}, bf16[512,128]{1,0:T(8,128)(2,1)S(1)}, u32[]{:S(2)}, u32[]{:S(2)}) collective-permute-start(bf16[512,128]{1,0:T(8,128)(2,1)S(1)} %add_convert_fusion), channel_id=1, source_target_pairs={{0,16},{1,17},{2,18},{3,19},{4,20},{5,21},{6,22},{7,23},{8,24},{9,... | collective-permute-start | bytes 393224 | tf_op jit(solution)/shard_map/ppermute | solution.py:628
  102.9 16.9 %collective-permute-start.16 = (bf16[512,128]{1,0:T(8,128)(2,1)S(1)}, bf16[512,128]{1,0:T(8,128)(2,1)S(1)}, u32[]{:S(2)}, u32[]{:S(2)}) collective-permute-start(bf16[512,128]{1,0:T(8,128)(2,1)S(1)} %add_convert_fusion), channel_id=1, source_target_pairs={{0,8},{1,9},{2,10},{3,11},{4,12},{5,13},{6,14},{7,15},{8,0},{9,1},... | collective-permute-start | bytes 393224 | tf_op jit(solution)/shard_map/ppermute | solution.py:628
  103.6 16.2 %collective-permute-start.19 = (bf16[288,512]{1,0:T(8,128)(2,1)S(1)}, bf16[288,512]{1,0:T(8,128)(2,1)S(1)}, u32[]{:S(2)}, u32[]{:S(2)}) collective-permute-start(bf16[288,512]{1,0:T(8,128)(2,1)S(1)} %get-tuple-element.250), channel_id=1, source_target_pairs={{0,2},{1,3},{2,0},{3,1},{4,6},{5,7},{6,4},{7,5},{8,10},{9,11},{10,... | collective-permute-start | bytes 884744 | tf_op jit(solution)/shard_map/ppermute | solution.py:628
  105.6 14.1 %collective-permute-start.15 = (bf16[160,512]{1,0:T(8,128)(2,1)S(1)}, bf16[160,512]{1,0:T(8,128)(2,1)S(1)}, u32[]{:S(2)}, u32[]{:S(2)}) collective-permute-start(bf16[160,512]{1,0:T(8,128)(2,1)S(1)} %pad_maximum_fusion.11), channel_id=1, source_target_pairs={{0,16},{1,17},{2,18},{3,19},{4,20},{5,21},{6,22},{7,23},{8,24},{9,... | collective-permute-start | bytes 491528 | tf_op jit(solution)/shard_map/ppermute | solution.py:628
  119.9 14.5 %collective-permute-start.25 = (bf16[4,512,128]{2,1,0:T(8,128)(2,1)S(1)}, bf16[4,512,128]{2,1,0:T(8,128)(2,1)S(1)}, u32[]{:S(2)}, u32[]{:S(2)}) collective-permute-start(bf16[4,512,128]{2,1,0:T(8,128)(2,1)S(1)} %pad_maximum_fusion.1.refs_0_), channel_id=1, source_target_pairs={{0,4},{1,5},{2,6},{3,7},{4,0},{5,1},{6,2},{7,3},{8,12},{9,13},{10,... | collective-permute-start | bytes 1572872 | tf_op jit(solution)/shard_map/ppermute | solution.py:628
  121.4 13.0 %collective-permute-start.24 = (bf16[4,512,128]{2,1,0:T(8,128)(2,1)S(1)}, bf16[4,512,128]{2,1,0:T(8,128)(2,1)S(1)}, u32[]{:S(2)}, u32[]{:S(2)}) collective-permute-start(bf16[4,512,128]{2,1,0:T(8,128)(2,1)S(1)} %pad_maximum_fusion.1.refs_0_), channel_id=1, source_target_pairs={{0,2},{1,3},{2,0},{3,1},{4,6},{5,7},{6,4},{7,5},{8,10},{9,11},{10,... | collective-permute-start | bytes 1572872 | tf_op jit(solution)/shard_map/ppermute | solution.py:628
  126.7 6.3 %collective-permute-start.23 = (bf16[64,512]{1,0:T(8,128)(2,1)S(1)}, bf16[64,512]{1,0:T(8,128)(2,1)S(1)}, u32[]{:S(2)}, u32[]{:S(2)}) collective-permute-start(bf16[64,512]{1,0:T(8,128)(2,1)S(1)} %add_convert_fusion.1), channel_id=1, source_target_pairs={{0,24},{1,25},{2,26},{3,27},{4,28},{5,29},{6,30},{7,31},{8,16},{9,... | collective-permute-start | bytes 196616 | tf_op jit(solution)/shard_map/ppermute | solution.py:628
  134.5 7.8 %collective-permute-start.27 = (bf16[2,512,128]{2,1,0:T(8,128)(2,1)S(1)}, bf16[2,512,128]{2,1,0:T(8,128)(2,1)S(1)}, u32[]{:S(2)}, u32[]{:S(2)}) collective-permute-start(bf16[2,512,128]{2,1,0:T(8,128)(2,1)S(1)} %slice.218), channel_id=1, source_target_pairs={{0,2},{1,3},{2,0},{3,1},{4,6},{5,7},{6,4},{7,5},{8,10},{9,11},{10,... | collective-permute-start | bytes 786440 | tf_op jit(solution)/shard_map/ppermute | solution.py:628
  136.0 7.5 %collective-permute-start.28 = (bf16[2,512,128]{2,1,0:T(8,128)(2,1)S(1)}, bf16[2,512,128]{2,1,0:T(8,128)(2,1)S(1)}, u32[]{:S(2)}, u32[]{:S(2)}) collective-permute-start(bf16[2,512,128]{2,1,0:T(8,128)(2,1)S(1)} %slice.219), channel_id=1, source_target_pairs={{0,4},{1,5},{2,6},{3,7},{4,0},{5,1},{6,2},{7,3},{8,12},{9,13},{10,... | collective-permute-start | bytes 786440 | tf_op jit(solution)/shard_map/ppermute | solution.py:628
  136.5 8.6 %collective-permute-start.29 = (bf16[4,64,512]{2,1,0:T(8,128)(2,1)S(1)}, bf16[4,64,512]{2,1,0:T(8,128)(2,1)S(1)}, u32[]{:S(2)}, u32[]{:S(2)}) collective-permute-start(bf16[4,64,512]{2,1,0:T(8,128)(2,1)S(1)} %pad_maximum_fusion.9.refs_0_), channel_id=1, source_target_pairs={{0,2},{1,3},{2,0},{3,1},{4,6},{5,7},{6,4},{7,5},{8,10},{9,11},{10,... | collective-permute-start | bytes 786440 | tf_op jit(solution)/shard_map/ppermute | solution.py:628
  137.1 9.1 %collective-permute-start.30 = (bf16[4,64,512]{2,1,0:T(8,128)(2,1)S(1)}, bf16[4,64,512]{2,1,0:T(8,128)(2,1)S(1)}, u32[]{:S(2)}, u32[]{:S(2)}) collective-permute-start(bf16[4,64,512]{2,1,0:T(8,128)(2,1)S(1)} %pad_maximum_fusion.9.refs_0_), channel_id=1, source_target_pairs={{0,4},{1,5},{2,6},{3,7},{4,0},{5,1},{6,2},{7,3},{8,12},{9,13},{10,... | collective-permute-start | bytes 786440 | tf_op jit(solution)/shard_map/ppermute | solution.py:628
  138.6 7.6 %collective-permute-start.26 = (bf16[4,512,128]{2,1,0:T(8,128)(2,1)S(1)}, bf16[4,512,128]{2,1,0:T(8,128)(2,1)S(1)}, u32[]{:S(2)}, u32[]{:S(2)}) collective-permute-start(bf16[4,512,128]{2,1,0:T(8,128)(2,1)S(1)} %pad_maximum_fusion.1.refs_0_), channel_id=1, source_target_pairs={{0,1},{1,0},{2,3},{3,2},{4,5},{5,4},{6,7},{7,6},{8,9},{9,8},{10,11... | collective-permute-start | bytes 1572872 | tf_op jit(solution)/shard_map/ppermute | solution.py:628
  146.4 8.5 %collective-permute-start.33 = (bf16[8,512,128]{2,1,0:T(8,128)(2,1)S(1)}, bf16[8,512,128]{2,1,0:T(8,128)(2,1)S(1)}, u32[]{:S(2)}, u32[]{:S(2)}) collective-permute-start(bf16[8,512,128]{2,1,0:T(8,128)(2,1)S(1)} %pad_maximum_fusion), channel_id=1, source_target_pairs={{0,1},{1,0},{2,3},{3,2},{4,5},{5,4},{6,7},{7,6},{8,9},{9,8},{10,11... | collective-permute-start | bytes 3145736 | tf_op jit(solution)/shard_map/ppermute | solution.py:628
  146.5 8.3 %collective-permute-start.35 = (bf16[12,64,512]{2,1,0:T(8,128)(2,1)S(1)}, bf16[12,64,512]{2,1,0:T(8,128)(2,1)S(1)}, u32[]{:S(2)}, u32[]{:S(2)}) collective-permute-start(bf16[12,64,512]{2,1,0:T(8,128)(2,1)S(1)} %constant_dynamic-update-slice_fusion), channel_id=1, source_target_pairs={{0,1},{1,0},{2,3},{3,2},{4,5},{5,4},{6,7},{7,6},{8,9},{9,8},{10,11... | collective-permute-start | bytes 2359304 | tf_op jit(solution)/shard_map/ppermute | solution.py:628
  147.1 7.8 %collective-permute-start.34 = (bf16[4,512,128]{2,1,0:T(8,128)(2,1)S(1)}, bf16[4,512,128]{2,1,0:T(8,128)(2,1)S(1)}, u32[]{:S(2)}, u32[]{:S(2)}) collective-permute-start(bf16[4,512,128]{2,1,0:T(8,128)(2,1)S(1)} %pad_maximum_fusion.2), channel_id=1, source_target_pairs={{0,1},{1,0},{2,3},{3,2},{4,5},{5,4},{6,7},{7,6},{8,9},{9,8},{10,11... | collective-permute-start | bytes 1572872 | tf_op jit(solution)/shard_map/ppermute | solution.py:628
  148.6 5.8 %collective-permute-start.31 = (bf16[2,64,512]{2,1,0:T(8,128)(2,1)S(1)}, bf16[2,64,512]{2,1,0:T(8,128)(2,1)S(1)}, u32[]{:S(2)}, u32[]{:S(2)}) collective-permute-start(bf16[2,64,512]{2,1,0:T(8,128)(2,1)S(1)} %slice.220), channel_id=1, source_target_pairs={{0,2},{1,3},{2,0},{3,1},{4,6},{5,7},{6,4},{7,5},{8,10},{9,11},{10,... | collective-permute-start | bytes 393224 | tf_op jit(solution)/shard_map/ppermute | solution.py:628
  149.3 5.6 %collective-permute-start.32 = (bf16[2,64,512]{2,1,0:T(8,128)(2,1)S(1)}, bf16[2,64,512]{2,1,0:T(8,128)(2,1)S(1)}, u32[]{:S(2)}, u32[]{:S(2)}) collective-permute-start(bf16[2,64,512]{2,1,0:T(8,128)(2,1)S(1)} %slice.221), channel_id=1, source_target_pairs={{0,4},{1,5},{2,6},{3,7},{4,0},{5,1},{6,2},{7,3},{8,12},{9,13},{10,... | collective-permute-start | bytes 393224 | tf_op jit(solution)/shard_map/ppermute | solution.py:628
  154.9 7.1 %collective-permute-start.36 = (bf16[4,64,512]{2,1,0:T(8,128)(2,1)S(1)}, bf16[4,64,512]{2,1,0:T(8,128)(2,1)S(1)}, u32[]{:S(2)}, u32[]{:S(2)}) collective-permute-start(bf16[4,64,512]{2,1,0:T(8,128)(2,1)S(1)} %pad_maximum_fusion.10), channel_id=1, source_target_pairs={{0,1},{1,0},{2,3},{3,2},{4,5},{5,4},{6,7},{7,6},{8,9},{9,8},{10,11... | collective-permute-start | bytes 786440 | tf_op jit(solution)/shard_map/ppermute | solution.py:628
  (36 other events, 220.8 us)

commit v4 on v3

--- a/solution.py
+++ b/solution.py
@@ -36,51 +36,63 @@
     return jnp.concatenate([high, (value - high.astype(F32)).astype(BF16)])
 
 def one_value(terms):
-    return terms[:16].astype(F32) + terms[16:32].astype(F32)
+    return terms[:8].astype(F32) + terms[8:16].astype(F32)
 
 def rows_of(*values):
     count = sum(v.shape[0] for v in values)
-    return jnp.concatenate(list(values) + [jnp.zeros((16 - count, values[0].shape[1]), F32)])
-
-def prepare_kernel(ids, pads, prefixes, mine, other, wq, wk, wv, gain, bias, buckets, hidden, query, keys, values, lines, info):
+    return jnp.concatenate(list(values) + [jnp.zeros((8 - count, values[0].shape[1]), F32)])
+
+def prepare_kernel(ids, mine, other, gain, bias, buckets, pads_h, prefixes_h, wq_h, wk_h, wv_h, hidden, query, keys, values, lines, info,
+                   pads, prefixes, wq, wk, wv, sems):
     rows = mine.shape[0]
-    info[0] = 4 * rows - pads[ids[6]]
-    info[5] = prefixes[ids[6]]
+    load = [pltpu.make_async_copy(a, b, sems.at[i]) for i, (a, b) in enumerate(
+        ((pads_h, pads), (prefixes_h, prefixes), (wk_h, wk), (wv_h, wv), (wq_h, wq)))]
+    for copy in load:
+        copy.start()
+    picker = jnp.where(lax.broadcasted_iota(jnp.int32, (BUCKETS, 1), 0) == buckets[...], 1.0, 0.0).astype(BF16)
+    left, total = bias[...], None
+    for _ in range(3):
+        part = left.astype(BF16)
+        left = left - part.astype(F32)
+        made = dot(part, picker)
+        total = made if total is None else total + made
+    lines[...] = jnp.zeros_like(lines)
+    lines[:, : buckets.shape[1]] = total
+    for part, raw in enumerate((mine, other)):
+        tokens = raw[...].astype(F32)
+        hidden[part * rows : (part + 1) * rows, :] = (tokens * rms_scale(tokens) * gain[...]).astype(BF16)
+    h = hidden[...]
+    load[2].wait()
+    keys[...] = dot(h, wk[...]).astype(BF16)
+    load[3].wait()
+    values[...] = dot(h, wv[...]).astype(BF16)
+    load[4].wait()
+    query[...] = dot(h[:rows], wq[...]).astype(BF16)
+    load[0].wait()
+    load[1].wait()
+    doc = ids[6]
+    info[0] = 4 * rows - jnp.where(doc == 0, pads[0], pads[1])
+    info[5] = jnp.where(doc == 0, prefixes[0], prefixes[1])
     for to, at in enumerate((0, 1, 2, 3)):
         info[1 + to] = ids[at]
     for to, at in enumerate((4, 5, 6)):
         info[6 + to] = ids[at]
-    for part, raw in enumerate((mine, other)):
-        tokens = raw[...].astype(F32)
-        hidden[part * rows : (part + 1) * rows, :] = (tokens * rms_scale(tokens) * gain[...]).astype(BF16)
-    h = hidden[...]
-    query[...] = dot(h[:rows], wq[...]).astype(BF16)
-    keys[...] = dot(h, wk[...]).astype(BF16)
-    values[...] = dot(h, wv[...]).astype(BF16)
-    picker = jnp.where(lax.broadcasted_iota(jnp.int32, (bias.shape[0], 1), 0) == buckets[...], 1.0, 0.0).astype(BF16)
-    left, total = bias[...], None
-    for _ in range(3):
-        part = left.astype(BF16)
-        left = left - part.astype(F32)
-        made = dot(part, picker, TN)
-        total = made if total is None else total + made
-    lines[...] = jnp.zeros_like(lines)
-    lines[:, : buckets.shape[1]] = total
 
 def prepare(ids, pads, prefixes, mine, other, wq, wk, wv, gain, bias, buckets):
     rows, width = mine.shape
     span = buckets.shape[1] + 1
-    heads = bias.shape[1]
+    heads = bias.shape[0]
     shape = lambda n: jax.ShapeDtypeStruct((n, width), BF16)
-    smem, vmem = pl.BlockSpec(memory_space=pltpu.SMEM), pl.BlockSpec(memory_space=pltpu.VMEM)
+    smem, vmem, far = (pl.BlockSpec(memory_space=m) for m in (pltpu.SMEM, pltpu.VMEM, pltpu.HBM))
     return pl.pallas_call(
         prepare_kernel,
-        in_specs=[smem] * 3 + [vmem] * 8,
+        in_specs=[smem] + [vmem] * 5 + [far] * 5,
         out_specs=[vmem] * 5 + [smem],
         out_shape=[shape(2 * rows), shape(rows), shape(2 * rows), shape(2 * rows),
                    jax.ShapeDtypeStruct((heads, span), F32), jax.ShapeDtypeStruct((16,), jnp.int32)],
+        scratch_shapes=[pltpu.SMEM((2,), jnp.int32)] * 2 + [pltpu.VMEM((width, width), BF16)] * 3 + [pltpu.SemaphoreType.DMA((5,))],
         name="prepare", compiler_params=pltpu.CompilerParams(vmem_limit_bytes=14 << 20),
-    )(ids, pads, prefixes, mine, other, wq, wk, wv, gain, bias, buckets)
+    )(ids, mine, other, gain, bias, buckets, pads, prefixes, wq, wk, wv)
 
 def back_pieces(to, active, low, mine):
     @pl.loop(0, active.shape[1] // 512)
@@ -234,14 +246,14 @@
         grid=(heads // 2,),
         in_specs=[smem, whole(count, width), whole(count, width), whole(count, width), col(count), col(2 * count), col(2 * count),
                   whole(heads, span)] + [whole(width, width)] * 3 + [whole(1, width)] * 3
-                 + [whole(2, width)] + [free] * 3,
+                 + [whole(2, width)] + [pl.BlockSpec(memory_space=pltpu.HBM)] * 3,
         out_specs=[free] * 13 + [whole(8, width)],
         out_shape=outs + [shape((8, width), F32)],
         scratch_shapes=[pltpu.VMEM(o.shape, o.dtype) for o in outs[:4] + outs[5:]]
                        + [pltpu.VMEM(wo.shape, BF16), pltpu.VMEM(win.shape, BF16), pltpu.VMEM(wback.shape, BF16),
                           pltpu.VMEM((2, 2 * count, 4 * count), BF16), pltpu.VMEM((2, 2 * count, 4 * count), F32),
                           pltpu.VMEM((2, 128, span), F32), pltpu.VMEM((2, 4 * count, 128), BF16), pltpu.SemaphoreType.DMA((16,))],
-        name="front", compiler_params=pltpu.CompilerParams(vmem_limit_bytes=50 << 20),
+        name="front", compiler_params=pltpu.CompilerParams(vmem_limit_bytes=40 << 20),
     )(info, far, far_other, near, q_l, k_l, v_l, lines, wq, wk, wv, gain1, gain2, gain3, cots, wo, win, wback)
 
 def through_kernel(info, slopes_h, win_h, mixed_h, steep_h, wo_h, att_h, gain2, grad_mixed_o, grad_attended_o, grad_out_o, rows,
@@ -289,11 +301,11 @@
     outs = [shape((n, width), F32), shape((n, width), BF16), shape((width, width), BF16)]
     return pl.pallas_call(
         through_kernel,
-        in_specs=[smem] + [free] * 6 + [vmem],
+        in_specs=[smem, free, pl.BlockSpec(memory_space=pltpu.HBM)] + [free] * 4 + [vmem],
         out_specs=[free] * 3 + [vmem],
         out_shape=outs + [shape((8, width), F32)],
         scratch_shapes=[pltpu.VMEM(g.shape, g.dtype) for g in given] + [pltpu.VMEM(o.shape, o.dtype) for o in outs] + [pltpu.SemaphoreType.DMA((15,))],
-        name="through", compiler_params=pltpu.CompilerParams(vmem_limit_bytes=16 << 20),
+        name="through", compiler_params=pltpu.CompilerParams(vmem_limit_bytes=14 << 20),
     )(info, *given, gain2)
 
 def meet_kernel(info, got_h, active_h, slopes_h, turned_h, steep_h, *refs):
@@ -459,7 +471,10 @@
             left = left - part.astype(F32)
             bias = dot(part, picker, NT) if bias is None else bias + dot(part, picker, NT)
         bias = jnp.concatenate([bias, jnp.zeros((bias.shape[0], width - 128), F32)], axis=1)
-        total = jnp.concatenate([gain, through_rows[0:1, :], dense_rows[1:2, :], jnp.zeros((5, width), F32), bias])
+        line = bias[0:1]
+        for h in range(1, bias.shape[0]):
+            line = line + pltpu.roll(bias[h : h + 1], 32 * h, 1)
+        total = rows_of(gain, through_rows[0:1, :], dense_rows[1:2, :], line)
         small[...] = total
         send[16 * size :, :] = two_terms(total)
         for copy in done:
@@ -475,15 +490,15 @@
     col = lambda n: pl.BlockSpec((n, 128), lambda g: (0, g))
     shape = jax.ShapeDtypeStruct
     size = 4 * width // 32
-    outs = [shape((16, size, width), BF16), shape((16 * size + 32, width), BF16), shape((2 * count, width), F32), shape((2 * count + 32, width), BF16)]
+    outs = [shape((16, size, width), BF16), shape((16 * size + 16, width), BF16), shape((2 * count, width), F32), shape((2 * count + 16, width), BF16)]
     given = (hid_l, hid_r, near, near_other, far, far_other, wq, wk, wv)
     return pl.pallas_call(
         back_kernel,
         grid=(width // 128,),
         in_specs=[smem, col(count), col(count)] + [col(2 * count)] * 7 + [pl.BlockSpec((2, 2 * count, 4 * count), lambda g: (g, 0, 0)),
                   whole(*buckets.shape), whole(8, width), whole(8, width)] + [free] * 10,
-        out_specs=[free] * 4 + [whole(16, width)],
-        out_shape=outs + [shape((16, width), F32)],
+        out_specs=[free] * 4 + [whole(8, width)],
+        out_shape=outs + [shape((8, width), F32)],
         scratch_shapes=[pltpu.VMEM(g.shape, BF16) for g in given] + [pltpu.VMEM((4 * width, width), BF16)]
                        + [pltpu.VMEM(o.shape, o.dtype) for o in outs]
                        + [pltpu.VMEM((2 * count, width), BF16), pltpu.VMEM((4 * count, width), BF16), pltpu.VMEM((4 * count, width), BF16),
@@ -512,65 +527,54 @@
 def ending(info, stay, came, near, far, grad_mixed, gain, dense_rows):
     count, width = near.shape
     smem, vmem = pl.BlockSpec(memory_space=pltpu.SMEM), pl.BlockSpec(memory_space=pltpu.VMEM)
-    shape = jax.ShapeDtypeStruct((count + 32, width), BF16)
+    shape = jax.ShapeDtypeStruct((count + 16, width), BF16)
     return pl.pallas_call(
         ending_kernel, in_specs=[smem] + [vmem] * 7, out_specs=[vmem] * 2, out_shape=[shape, shape], name="ending", compiler_params=pltpu.CompilerParams(vmem_limit_bytes=10 << 20)
     )(info, stay, came, near, far, grad_mixed, gain, dense_rows)
 
 def place_kernel(firsts, info, *refs):
-    count = len(firsts)
-    given, (back, front), parts, (rows, columns, sems) = refs[:count], refs[-5 - count : -3 - count], refs[-3 - count : -3], refs[-3:]
-    load = [pltpu.make_async_copy(a, b, sems.at[i]) for i, (a, b) in enumerate(zip(given, parts))]
-    for copy in load:
-        copy.start()
+    parts, (back, front, rows, columns, sems) = refs[: len(firsts)], refs[-5:]
     mine = info[6] & 15
     for side in range(2):
         @pl.when(info[7] == side)
         def _(side=side):
             copies, n = [], 0
-            for part, first, ready in zip(parts, firsts, load):
-                ready.wait()
+            for part, first in zip(parts, firsts):
                 for i in range(part.shape[0]):
                     r = first + i
                     to = pl.ds(pl.multiple_of(((r & 15) ^ mine) * 128, 128), 128)
                     if (r >= 16) == (side == 1):
                         for q in range(4):
                             rows[n, :, q * 128 : (q + 1) * 128] = part[i, q * 128 : (q + 1) * 128, :].astype(F32)
-                        copies.append(pltpu.make_async_copy(rows.at[n], back.at[to, :], sems.at[count + n]))
+                        copies.append(pltpu.make_async_copy(rows.at[n], back.at[to, :], sems.at[n]))
                     else:
                         columns[n] = part[i].astype(F32)
-                        copies.append(pltpu.make_async_copy(columns.at[n], front.at[:, to], sems.at[count + n]))
+                        copies.append(pltpu.make_async_copy(columns.at[n], front.at[:, to], sems.at[n]))
                     copies[-1].start()
                     n += 1
             for copy in copies:
                 copy.wait()
 
 def place(info, parts, made, width):
-    smem, free = pl.BlockSpec(memory_space=pltpu.SMEM), pl.BlockSpec(memory_space=pl.ANY)
+    smem, vmem, far = (pl.BlockSpec(memory_space=m) for m in (pltpu.SMEM, pltpu.VMEM, pltpu.HBM))
     shape = jax.ShapeDtypeStruct
     count = sum(p.shape[0] for _, p in parts)
     return pl.pallas_call(
         functools.partial(place_kernel, [first for first, _ in parts]),
-        in_specs=[smem] + [free] * (len(parts) + len(made)),
-        out_specs=[free] * 2,
+        in_specs=[smem] + [vmem] * len(parts) + [far] * len(made),
+        out_specs=[far] * 2,
         out_shape=[shape((16 * 128, width), F32), shape((width, 16 * 128), F32)],
-        scratch_shapes=[pltpu.VMEM(p.shape, BF16) for _, p in parts]
-                       + [pltpu.VMEM((count, 128, width), F32), pltpu.VMEM((count, width, 128), F32), pltpu.SemaphoreType.DMA((len(parts) + count,))],
+        scratch_shapes=[pltpu.VMEM((count, 128, width), F32), pltpu.VMEM((count, width, 128), F32), pltpu.SemaphoreType.DMA((count,))],
         input_output_aliases={1 + len(parts) + i: i for i in range(len(made))},
-        name="place", compiler_params=pltpu.CompilerParams(vmem_limit_bytes=24 << 20),
+        name="place", compiler_params=pltpu.CompilerParams(vmem_limit_bytes=20 << 20),
     )(info, *[p for _, p in parts], *made)
 
 def sort_kernel(firsts, info, *refs):
-    count = len(firsts)
-    given, made, parts, (tall, sems) = refs[:count], refs[-6 - count : -2 - count], refs[-2 - count : -2], refs[-2:]
-    load = [pltpu.make_async_copy(a, b, sems.at[i]) for i, (a, b) in enumerate(zip(given, parts))]
-    for copy in load:
-        copy.start()
+    parts, made, (tall, sems) = refs[: len(firsts)], refs[-6:-2], refs[-2:]
     size = parts[0].shape[1]
     mine = info[6]
     pieces = []
-    for part, first, ready in zip(parts, firsts, load):
-        ready.wait()
+    for part, first in zip(parts, firsts):
         for i in range(part.shape[0]):
             tall[len(pieces)] = part[i].astype(F32)
             pieces.append(first + i)
@@ -580,47 +584,34 @@
             copies = []
             for n, r in enumerate(pieces):
                 to = pl.ds(pl.multiple_of(((r ^ mine) & 7) * size, size), size)
-                copies.append(pltpu.make_async_copy(tall.at[n], made[top ^ (r >> 3)].at[to, :], sems.at[count + n]))
+                copies.append(pltpu.make_async_copy(tall.at[n], made[top ^ (r >> 3)].at[to, :], sems.at[n]))
                 copies[-1].start()
             for copy in copies:
                 copy.wait()
 
 def sort(info, parts, made, width):
-    smem, free = pl.BlockSpec(memory_space=pltpu.SMEM), pl.BlockSpec(memory_space=pl.ANY)
+    smem, vmem, far = (pl.BlockSpec(memory_space=m) for m in (pltpu.SMEM, pltpu.VMEM, pltpu.HBM))
     shape = jax.ShapeDtypeStruct((width, width), F32)
     count = sum(p.shape[0] for _, p in parts)
     return pl.pallas_call(
         functools.partial(sort_kernel, [first for first, _ in parts]),
-        in_specs=[smem] + [free] * (len(parts) + len(made)),
-        out_specs=[free] * 4,
+        in_specs=[smem] + [vmem] * len(parts) + [far] * len(made),
+        out_specs=[far] * 4,
         out_shape=[shape] * 4,
-        scratch_shapes=[pltpu.VMEM(p.shape, BF16) for _, p in parts]
-                       + [pltpu.VMEM((count,) + parts[0][1].shape[1:], F32), pltpu.SemaphoreType.DMA((len(parts) + count,))],
+        scratch_shapes=[pltpu.VMEM((count,) + parts[0][1].shape[1:], F32), pltpu.SemaphoreType.DMA((count,))],
         input_output_aliases={1 + len(parts) + i: i for i in range(len(made))},
         name="sort", compiler_params=pltpu.CompilerParams(vmem_limit_bytes=12 << 20),
     )(info, *[p for _, p in parts], *made)
 
 def mix_kernel(*refs):
-    given, outs, terms, (sums, sems) = refs[:4], refs[4:8], refs[8:12], refs[12:]
-    order = (3, 1, 2, 0)
-    load = {(t, k): pltpu.make_async_copy(given[t].at[k], terms[t].at[k], sems.at[4 * t + k]) for k in order for t in range(4)}
-    save = {k: pltpu.make_async_copy(sums.at[k], outs[k], sems.at[16 + k]) for k in order}
-    for copy in load.values():
-        copy.start()
-    for k in order:
-        for t in range(4):
-            load[t, k].wait()
-        sums[k] = added(*[term[k] for term in terms])
-        save[k].start()
-    for copy in save.values():
-        copy.wait()
+    for k in range(4):
+        refs[4 + k][...] = added(*[term[k] for term in refs[:4]])
 
 def mix(terms):
     block = terms[0].shape[1:]
-    free = pl.BlockSpec(memory_space=pl.ANY)
-    return pl.pallas_call(
-        mix_kernel, in_specs=[free] * 4, out_specs=[free] * 4, out_shape=[jax.ShapeDtypeStruct(block, BF16)] * 4,
-        scratch_shapes=[pltpu.VMEM((4,) + block, BF16)] * 5 + [pltpu.SemaphoreType.DMA((20,))], name="mix", compiler_params=pltpu.CompilerParams(vmem_limit_bytes=10 << 20),
+    vmem = pl.BlockSpec(memory_space=pltpu.VMEM)
+    return pl.pallas_call(
+        mix_kernel, in_specs=[vmem] * 4, out_specs=[vmem] * 4, out_shape=[jax.ShapeDtypeStruct(block, BF16)] * 4, name="mix", compiler_params=pltpu.CompilerParams(vmem_limit_bytes=10 << 20),
     )(*terms)
 
 def exchange(value, bits):
@@ -655,7 +646,7 @@
         ids = jnp.where(slot == i, value, ids)
     gain1, gain2, gain3 = norm1_gain[None, :], norm2_gain[None, :], final_gain[None, :]
     buckets = bucket_table[None, :]
-    hid_l, q_l, k_l, v_l, lines, info = prepare(ids, pad_len, prefix_len, near, near_other, w_query, w_key, w_value, gain1, bias_table, buckets)
+    hid_l, q_l, k_l, v_l, lines, info = prepare(ids, pad_len, prefix_len, near, near_other, w_query, w_key, w_value, gain1, bias_table.T, buckets)
     far, info = wait(far, info)
     far_other = exchange(far, CORE)
     (hid_r, q_r, k_r, v_r, expo, inverse, attended, send, active, slopes, turned, mixed, steep, dense_rows) = front(
@@ -708,15 +699,15 @@
     rest_came = [part[:count].reshape((4,) + rest_keep.shape[1:]) for part in rest_came]
     piece = count // 4
     lines = added(rest_keep[:4], rest_got[:4], *rest_came).reshape(-1, width)
-    send = jnp.concatenate([lines[2 * piece :], two_terms(small)])
+    send = jnp.concatenate([lines[piece : 2 * piece], lines[3 * piece :], two_terms(small)])
     token, send = wait(token, send)
-    took = exchange(send, line[1])
+    took = exchange(send, line[0])
     token, took = wait(token, took)
     small = small + one_value(took[2 * piece :])
-    lines = added(lines[: 2 * piece], took[: 2 * piece])
-    send = jnp.concatenate([lines[piece:], two_terms(small)])
+    send = jnp.concatenate([added(lines[2 * piece : 3 * piece], took[piece : 2 * piece]), two_terms(small)])
+    lines = added(lines[:piece], took[:piece])
     token, send, back_line, away_got = wait(token, send, back_line, away_got)
-    took = exchange(send, line[0])
+    took = exchange(send, line[1])
 
     quarter = jnp.stack([whole] + back_line)
     token, quarter = wait(token, quarter)
@@ -724,7 +715,7 @@
     token, took = wait(token, took)
 
     small = small + one_value(took[piece:])
-    rest = added(lines[:piece], took[:piece])
+    rest = added(lines, took[:piece])
     for bit in further:
         rest = added(rest, exchange(rest, bit))
         small = small + exchange(small, bit)
@@ -769,7 +760,7 @@
         small[0],
         small[1],
         small[2],
-        small[8:, :BUCKETS].T,
+        small[3, : bias_table.size].reshape(bias_table.shape[::-1]).T,
     )
 
 def solution(mesh):

time: 164 us -> 153 us (0.933)
  waiting for transfers between devices: 38.3 us -> 31.4 us
  local copies, waits for them, and re-layouts: 14.7 us -> 9.83 us
  starting transfers between devices: 35.1 us -> 39.7 us
  Pallas kernels: 70.4 us -> 65.9 us
    ppermute x37, waiting for transfers between devices: 38.3 us -> 31.4 us  [exchange(): lax.ppermute(value, ('dp', 'blk'), [(i, i ^ bits) for i in range(size)])]
    unnamed x68 -> x47, local copies, waits for them, and re-layouts: 13.3 us -> 8.29 us
    ppermute x37, starting transfers between devices: 35.1 us -> 39.7 us  [exchange(): lax.ppermute(value, ('dp', 'blk'), [(i, i ^ bits) for i in range(size)])]
    pallas_call x3, Pallas kernels: 10.5 us -> 7.88 us  [the longest x1 4.85 us: through(): pl.pallas_call(through_kernel, in_specs=[smem, free, pl.BlockSpec(memory_...]
  transfers between devices with their start and end apart: 37 -> 37, of which waited for: 15 -> 12; matrix products, arithmetic and copies ran while one was open for 3% -> 2% of each run, Pallas kernels for 26% -> 25%
where the time goes in v4:
time: 153 us
  Pallas kernels  65.9 us (43%)
  starting transfers between devices  39.7 us (26%)
  waiting for transfers between devices  31.4 us (21%)
  local copies, waits for them, and re-layouts  9.83 us (6%)
  other arithmetic  4.28 us (3%)
    ppermute x37, starting transfers between devices, exchange(): lax.ppermute(value, ('dp', 'blk'), [(i, i ^ bits) for i in range(size)])  39.7 us
    ppermute x37, waiting for transfers between devices, exchange(): lax.ppermute(value, ('dp', 'blk'), [(i, i ^ bits) for i in range(size)])  31.4 us
    pallas_call x1, Pallas kernels, front(): pl.pallas_call(front_kernel, grid=(heads // 2,), in_specs=[smem, whole(co...  22 us
    pallas_call x1, Pallas kernels, back(): pl.pallas_call(back_kernel, grid=(width // 128,), in_specs=[smem, col(cou...  20 us
    unnamed x47, local copies, waits for them, and re-layouts  8.29 us
    pallas_call x3, Pallas kernels, place(): pl.pallas_call(functools.partial(place_kernel, [first for first, _ in par...  6.6 us
    pallas_call x1, Pallas kernels, through(): pl.pallas_call(through_kernel, in_specs=[smem, free, pl.BlockSpec(memory_...  4.85 us
    pallas_call x2, Pallas kernels, sort(): pl.pallas_call(functools.partial(sort_kernel, [first for first, _ in part...  4.65 us
  transfers between devices with their start and end apart: 37, of which 12 were waited for; matrix products, arithmetic and copies ran while one was open for 2% of the time, Pallas kernels for 25%

profile of v4, /device:TPU:0, one launch (start us, length us, event | category | flops | bytes accessed | tf_op | source)
XLA Modules:
  0.0 152.5 jit_solution(17159027503184869569)
XLA Ops:
  2.4 2.6 %collective-permute-start = (bf16[256,512]{1,0:T(8,128)(2,1)S(1)}, bf16[256,512]{1,0:T(8,128)(2,1)S(1)}, u32[]{:S(2)}, u32[]{:S(2)}) collective-permute-start(bf16[256,512]{1,0:T(8,128)(2,1)S(1)} %get-tuple-element.165), channel_id=1, source_target_pairs={{0,2},{1,3},{2,0},{3,1},{4,6},{5,7},{6,4},{7,5},{8,10},{9,11},{10,... | collective-permute-start | bytes 786440 | tf_op jit(solution)/shard_map/ppermute | solution.py:619
  11.5 2.8 %prepare.1 = (bf16[512,512]{1,0:T(8,128)(2,1)S(1)}, bf16[256,512]{1,0:T(8,128)(2,1)S(1)}, bf16[512,512]{1,0:T(8,128)(2,1)S(1)}, bf16[512,512]{1,0:T(8,128)(2,1)S...) custom-call(s32[8]{0:T(128)S(1)} %compare_select_fusion.6.ids, bf16[256,512]{1,0:T(8,128)(2,1)S(1)} %get-tuple-element.166.mine.near.near_h, ...), custom_call_target="tpu_custom_call" | custom-call | tf_op jit(solution)/shard_map/prepare/pallas_call | solution.py:87
  16.0 22.0 %front.1 = (bf16[512,512]{1,0:T(8,128)(2,1)S(1)}, bf16[256,512]{1,0:T(8,128)(2,1)S(1)}, bf16[512,512]{1,0:T(8,128)(2,1)S(1)}, bf16[512,512]{1,0:T(8,128)(2,1)S(1...) custom-call(s32[16]{0:T(128)S(1)} %get-tuple-element.302.info, ...), custom_call_target="tpu_custom_call" | custom-call | tf_op jit(solution)/shard_map/front/pallas_call | solution.py:244
  38.2 1.7 %copy-done.1 = bf16[512,2048]{1,0:T(8,128)(2,1)S(1)} copy-done((bf16[512,2048]{1,0:T(8,128)(2,1)S(1)}, bf16[512,2048]{1,0:T(8,128)(2,1)}, u32[]{:S(2)}) %copy-start.1) | copy-done | bytes 2097176
  39.9 4.8 %through.1 = (f32[512,512]{1,0:T(8,128)S(1)}, bf16[512,512]{1,0:T(8,128)(2,1)S(1)}, bf16[512,512]{1,0:T(8,128)(2,1)S(1)}, f32[8,512]{1,0:T(8,128)S(1)}) custom-call(s32[16]{0:T(128)S(1)} %get-tuple-element.302.info, bf16[512,2048]{1,0:T(8,128)(2,1)S(1)} %copy-done.1, bf16[512,2048]{1,0:T(8,128)(2,1)S(1)} %copy-done, ...), custom_call_target="tpu_custom_call" | custom-call | tf_op jit(solution)/shard_map/through/pallas_call | solution.py:302
  44.8 3.6 %meet.1 = (bf16[4,512,128]{2,1,0:T(8,128)(2,1)S(1)}, bf16[4,512,128]{2,1,0:T(8,128)(2,1)S(1)}, bf16[4,512,128]{2,1,0:T(8,128)(2,1)S(1)}, bf16[4,512,128]{2,1,0:T(8,128)(2,1)S(1)}) custom-call(s32[16]{0:T(128)S(1)} %get-tuple-element.302.info, bf16[16,512,128]{2,1,0:T(8,128)(2,1)S(1)} %collective-permute-done.3.got_h, ...), custom_call_target="tpu_custom_call" | custom-call | tf_op jit(solution)/shard_map/meet/pallas_call | solution.py:352
  48.4 1.5 collective-permute-start.4
  49.9 1.5 collective-permute-start.5
  52.0 20.0 %back.1 = (bf16[16,64,512]{2,1,0:T(8,128)(2,1)S(1)}, bf16[1040,512]{1,0:T(8,128)(2,1)}, f32[512,512]{1,0:T(8,128)}, bf16[528,512]{1,0:T(8,128)(2,1)S(1)}, f32[8,512]{1,0:T(8,128)S(1)}) custom-call(s32[16]{0:T(128)S(1)} %get-tuple-element.302.info, bf16[256,512]{1,0:T(8,128)(2,1)S(1)} %get-tuple-element.170.q_l.ql, ...), custom_call_target="tpu_custom_call" | custom-call | tf_op jit(solution)/shard_map/back/pallas_call | solution.py:495
  72.1 2.7 %collective-permute-done.6.refs_3_ = bf16[4,512,128]{2,1,0:T(8,128)(2,1)S(1)} collective-permute-done((bf16[4,512,128]{2,1,0:T(8,128)(2,1)S(1)}, bf16[4,512,128]{2,1,0:T(8,128)(2,1)S(1)}, u32[]{:S(2)}, u32[]{:S(2)}) %collective-permute-start.6) | collective-permute-done | bytes 524320 | tf_op jit(solution)/shard_map/ppermute | solution.py:619
  75.6 1.6 %collective-permute-start.9 = (bf16[512,128]{1,0:T(8,128)(2,1)S(1)}, bf16[512,128]{1,0:T(8,128)(2,1)S(1)}, u32[]{:S(2)}, u32[]{:S(2)}) collective-permute-start(bf16[512,128]{1,0:T(8,128)(2,1)S(1)} %get-tuple-element.228), channel_id=1, source_target_pairs={{0,8},{1,9},{2,10},{3,11},{4,12},{5,13},{6,14},{7,15},{8,0},{9,1},... | collective-permute-start | bytes 393224 | tf_op jit(solution)/shard_map/ppermute | solution.py:619
  77.2 2.6 %collective-permute-start.10 = (bf16[512,128]{1,0:T(8,128)(2,1)S(1)}, bf16[512,128]{1,0:T(8,128)(2,1)S(1)}, u32[]{:S(2)}, u32[]{:S(2)}) collective-permute-start(bf16[512,128]{1,0:T(8,128)(2,1)S(1)} %get-tuple-element.229), channel_id=1, source_target_pairs={{0,16},{1,17},{2,18},{3,19},{4,20},{5,21},{6,22},{7,23},{8,24},{9,... | collective-permute-start | bytes 393224 | tf_op jit(solution)/shard_map/ppermute | solution.py:619
  80.4 1.5 collective-permute-start.12
  81.9 1.5 collective-permute-start.13
  83.4 1.7 %collective-permute-start.14 = (bf16[272,512]{1,0:T(8,128)(2,1)S(1)}, bf16[272,512]{1,0:T(8,128)(2,1)S(1)}, u32[]{:S(2)}, u32[]{:S(2)}) collective-permute-start(bf16[272,512]{1,0:T(8,128)(2,1)S(1)} %get-tuple-element.240), channel_id=1, source_target_pairs={{0,6},{1,7},{2,4},{3,5},{4,2},{5,3},{6,0},{7,1},{8,14},{9,15},{10,... | collective-permute-start | bytes 835592 | tf_op jit(solution)/shard_map/ppermute | solution.py:619
  86.3 3.9 %collective-permute-done.10 = bf16[512,128]{1,0:T(8,128)(2,1)S(1)} collective-permute-done((bf16[512,128]{1,0:T(8,128)(2,1)S(1)}, bf16[512,128]{1,0:T(8,128)(2,1)S(1)}, u32[]{:S(2)}, u32[]{:S(2)}) %collective-permute-start.10) | collective-permute-done | bytes 131104 | tf_op jit(solution)/shard_map/ppermute | solution.py:619
  90.2 2.4 %collective-permute-start.18 = (bf16[512,128]{1,0:T(8,128)(2,1)S(1)}, bf16[512,128]{1,0:T(8,128)(2,1)S(1)}, u32[]{:S(2)}, u32[]{:S(2)}) collective-permute-start(bf16[512,128]{1,0:T(8,128)(2,1)S(1)} %add_convert_fusion), channel_id=1, source_target_pairs={{0,24},{1,25},{2,26},{3,27},{4,28},{5,29},{6,30},{7,31},{8,16},{9,... | collective-permute-start | bytes 393224 | tf_op jit(solution)/shard_map/ppermute | solution.py:619
  94.7 1.4 collective-permute-start.19
  97.7 7.2 %collective-permute-done.15 = bf16[144,512]{1,0:T(8,128)(2,1)S(1)} collective-permute-done((bf16[144,512]{1,0:T(8,128)(2,1)S(1)}, bf16[144,512]{1,0:T(8,128)(2,1)S(1)}, u32[]{:S(2)}, u32[]{:S(2)}) %collective-permute-start.15) | collective-permute-done | bytes 147488 | tf_op jit(solution)/shard_map/ppermute | solution.py:619
  105.1 1.6 %collective-permute-start.25 = (bf16[4,512,128]{2,1,0:T(8,128)(2,1)S(1)}, bf16[4,512,128]{2,1,0:T(8,128)(2,1)S(1)}, u32[]{:S(2)}, u32[]{:S(2)}) collective-permute-start(bf16[4,512,128]{2,1,0:T(8,128)(2,1)S(1)} %pad_maximum_fusion.1.refs_0_), channel_id=1, source_target_pairs={{0,4},{1,5},{2,6},{3,7},{4,0},{5,1},{6,2},{7,3},{8,12},{9,13},{10,... | collective-permute-start | bytes 1572872 | tf_op jit(solution)/shard_map/ppermute | solution.py:619
  109.6 6.8 %collective-permute-done.20 = bf16[80,512]{1,0:T(8,128)(2,1)S(1)} collective-permute-done((bf16[80,512]{1,0:T(8,128)(2,1)S(1)}, bf16[80,512]{1,0:T(8,128)(2,1)S(1)}, u32[]{:S(2)}, u32[]{:S(2)}) %collective-permute-start.20) | collective-permute-done | bytes 81952 | tf_op jit(solution)/shard_map/ppermute | solution.py:619
  117.5 3.4 %collective-permute-start.21 = (bf16[64,512]{1,0:T(8,128)(2,1)S(1)}, bf16[64,512]{1,0:T(8,128)(2,1)S(1)}, u32[]{:S(2)}, u32[]{:S(2)}) collective-permute-start(bf16[64,512]{1,0:T(8,128)(2,1)S(1)} %add_convert_fusion.1), channel_id=1, source_target_pairs={{0,8},{1,9},{2,10},{3,11},{4,12},{5,13},{6,14},{7,15},{8,0},{9,1},... | collective-permute-start | bytes 196616 | tf_op jit(solution)/shard_map/ppermute | solution.py:619
  120.9 1.8 %collective-permute-done.23 = bf16[64,512]{1,0:T(8,128)(2,1)S(1)} collective-permute-done((bf16[64,512]{1,0:T(8,128)(2,1)S(1)}, bf16[64,512]{1,0:T(8,128)(2,1)S(1)}, u32[]{:S(2)}, u32[]{:S(2)}) %collective-permute-start.23) | collective-permute-done | bytes 65568 | tf_op jit(solution)/shard_map/ppermute | solution.py:619
  125.3 1.5 collective-permute-start.29
  126.7 1.5 collective-permute-start.30
  128.3 2.3 %place.3 = (f32[2048,512]{1,0:T(8,128)}, f32[512,2048]{1,0:T(8,128)}) custom-call(s32[16]{0:T(128)S(1)} %get-tuple-element.302.info, bf16[4,512,128]{2,1,0:T(8,128)(2,1)S(1)} %pad_maximum_fusion.1.refs_0_, bf16[4,512,128]{2,1,0:T(8,128)(2,1)S(1)} %collective-permute-done.24.refs_1_, bf16[4,512,128]{2,1,0:T(8,128)(2,1)S(1)} %collective-permute-done.25.refs_2_), custom_call_target="tpu_custom_call" | custom-call | tf_op jit(solution)/shard_map/place/pallas_call | solution.py:562
  131.1 2.2 %collective-permute-done.29.refs_1_ = bf16[4,64,512]{2,1,0:T(8,128)(2,1)S(1)} collective-permute-done((bf16[4,64,512]{2,1,0:T(8,128)(2,1)S(1)}, bf16[4,64,512]{2,1,0:T(8,128)(2,1)S(1)}, u32[]{:S(2)}, u32[]{:S(2)}) %collective-permute-start.29) | collective-permute-done | bytes 262176 | tf_op jit(solution)/shard_map/ppermute | solution.py:619
  138.3 1.9 %place.4 = (f32[2048,512]{1,0:T(8,128)}, f32[512,2048]{1,0:T(8,128)}) custom-call(s32[16]{0:T(128)S(1)} %get-tuple-element.302.info, bf16[2,512,128]{2,1,0:T(8,128)(2,1)S(1)} %collective-permute-done.27.refs_0_, bf16[2,512,128]{2,1,0:T(8,128)(2,1)S(1)} %collective-permute-done.28.refs_1_, ...), custom_call_target="tpu_custom_call", output_to_operand_aliasing={{0}: (4, {}), {1}: (5, {})} | custom-call | tf_op jit(solution)/shard_map/place/pallas_call | solution.py:562
  140.3 1.9 %collective-permute-done.31.refs_3_ = bf16[2,64,512]{2,1,0:T(8,128)(2,1)S(1)} collective-permute-done((bf16[2,64,512]{2,1,0:T(8,128)(2,1)S(1)}, bf16[2,64,512]{2,1,0:T(8,128)(2,1)S(1)}, u32[]{:S(2)}, u32[]{:S(2)}) %collective-permute-start.31) | collective-permute-done | bytes 131104 | tf_op jit(solution)/shard_map/ppermute | solution.py:619
  145.4 2.8 %sort.2 = (f32[512,512]{1,0:T(8,128)}, f32[512,512]{1,0:T(8,128)}, f32[512,512]{1,0:T(8,128)}, f32[512,512]{1,0:T(8,128)}) custom-call(s32[16]{0:T(128)S(1)} %get-tuple-element.302.info, bf16[4,64,512]{2,1,0:T(8,128)(2,1)S(1)} %pad_maximum_fusion.9.refs_0_, bf16[4,64,512]{2,1,0:T(8,128)(2,1)S(1)} %collective-permute-done.29.refs_1_, ...), custom_call_target="tpu_custom_call" | custom-call | tf_op jit(solution)/shard_map/sort/pallas_call | solution.py:596
  148.2 2.3 %place.5 = (f32[2048,512]{1,0:T(8,128)}, f32[512,2048]{1,0:T(8,128)}) custom-call(s32[16]{0:T(128)S(1)} %get-tuple-element.302.info, bf16[8,512,128]{2,1,0:T(8,128)(2,1)S(1)} %collective-permute-done.33.refs_0_, bf16[4,512,128]{2,1,0:T(8,128)(2,1)S(1)} %collective-permute-done.34.refs_1_, ...), custom_call_target="tpu_custom_call", output_to_operand_aliasing={{0}: (3, {}), {1}: (4, {})} | custom-call | tf_op jit(solution)/shard_map/place/pallas_call | solution.py:562
  150.5 1.8 %sort.3 = (f32[512,512]{1,0:T(8,128)}, f32[512,512]{1,0:T(8,128)}, f32[512,512]{1,0:T(8,128)}, f32[512,512]{1,0:T(8,128)}) custom-call(s32[16]{0:T(128)S(1)} %get-tuple-element.302.info, bf16[4,64,512]{2,1,0:T(8,128)(2,1)} %collective-permute-done.36.refs_0_, ...), custom_call_target="tpu_custom_call", output_to_operand_aliasing={{0}: (2, {}), {1}: (3, {}), {2}: (4, {}), {3}: (5, {})} | custom-call | tf_op jit(solution)/shard_map/sort/pallas_call | solution.py:596
  (140 shorter events, 32.1 us)
Async XLA Ops:
  2.4 11.9 %collective-permute-start = (bf16[256,512]{1,0:T(8,128)(2,1)S(1)}, bf16[256,512]{1,0:T(8,128)(2,1)S(1)}, u32[]{:S(2)}, u32[]{:S(2)}) collective-permute-start(bf16[256,512]{1,0:T(8,128)(2,1)S(1)} %get-tuple-element.165), channel_id=1, source_target_pairs={{0,2},{1,3},{2,0},{3,1},{4,6},{5,7},{6,4},{7,5},{8,10},{9,11},{10,... | collective-permute-start | bytes 786440 | tf_op jit(solution)/shard_map/ppermute | solution.py:619
  38.0 6.8 %collective-permute-start.3 = (bf16[16,512,128]{2,1,0:T(8,128)(2,1)S(1)}, bf16[16,512,128]{2,1,0:T(8,128)(2,1)S(1)}, u32[]{:S(2)}, u32[]{:S(2)}) collective-permute-start(bf16[16,512,128]{2,1,0:T(8,128)(2,1)S(1)} %get-tuple-element.181), channel_id=1, source_target_pairs={{0,1},{1,0},{2,3},{3,2},{4,5},{5,4},{6,7},{7,6},{8,9},{9,8},{10,11... | collective-permute-start | bytes 6291464 | tf_op jit(solution)/shard_map/ppermute | solution.py:619
  48.4 23.6 %collective-permute-start.4 = (bf16[4,512,128]{2,1,0:T(8,128)(2,1)S(1)}, bf16[4,512,128]{2,1,0:T(8,128)(2,1)S(1)}, u32[]{:S(2)}, u32[]{:S(2)}) collective-permute-start(bf16[4,512,128]{2,1,0:T(8,128)(2,1)S(1)} %get-tuple-element.204), channel_id=1, source_target_pairs={{0,2},{1,3},{2,0},{3,1},{4,6},{5,7},{6,4},{7,5},{8,10},{9,11},{10,... | collective-permute-start | bytes 1572872 | tf_op jit(solution)/shard_map/ppermute | solution.py:619
  49.9 22.1 %collective-permute-start.5 = (bf16[4,512,128]{2,1,0:T(8,128)(2,1)S(1)}, bf16[4,512,128]{2,1,0:T(8,128)(2,1)S(1)}, u32[]{:S(2)}, u32[]{:S(2)}) collective-permute-start(bf16[4,512,128]{2,1,0:T(8,128)(2,1)S(1)} %get-tuple-element.205), channel_id=1, source_target_pairs={{0,4},{1,5},{2,6},{3,7},{4,0},{5,1},{6,2},{7,3},{8,12},{9,13},{10,... | collective-permute-start | bytes 1572872 | tf_op jit(solution)/shard_map/ppermute | solution.py:619
  51.4 23.4 %collective-permute-start.6 = (bf16[4,512,128]{2,1,0:T(8,128)(2,1)S(1)}, bf16[4,512,128]{2,1,0:T(8,128)(2,1)S(1)}, u32[]{:S(2)}, u32[]{:S(2)}) collective-permute-start(bf16[4,512,128]{2,1,0:T(8,128)(2,1)S(1)} %get-tuple-element.206), channel_id=1, source_target_pairs={{0,6},{1,7},{2,4},{3,5},{4,2},{5,3},{6,0},{7,1},{8,14},{9,15},{10,... | collective-permute-start | bytes 1572872 | tf_op jit(solution)/shard_map/ppermute | solution.py:619
  75.6 7.9 %collective-permute-start.9 = (bf16[512,128]{1,0:T(8,128)(2,1)S(1)}, bf16[512,128]{1,0:T(8,128)(2,1)S(1)}, u32[]{:S(2)}, u32[]{:S(2)}) collective-permute-start(bf16[512,128]{1,0:T(8,128)(2,1)S(1)} %get-tuple-element.228), channel_id=1, source_target_pairs={{0,8},{1,9},{2,10},{3,11},{4,12},{5,13},{6,14},{7,15},{8,0},{9,1},... | collective-permute-start | bytes 393224 | tf_op jit(solution)/shard_map/ppermute | solution.py:619
  77.2 12.9 %collective-permute-start.10 = (bf16[512,128]{1,0:T(8,128)(2,1)S(1)}, bf16[512,128]{1,0:T(8,128)(2,1)S(1)}, u32[]{:S(2)}, u32[]{:S(2)}) collective-permute-start(bf16[512,128]{1,0:T(8,128)(2,1)S(1)} %get-tuple-element.229), channel_id=1, source_target_pairs={{0,16},{1,17},{2,18},{3,19},{4,20},{5,21},{6,22},{7,23},{8,24},{9,... | collective-permute-start | bytes 393224 | tf_op jit(solution)/shard_map/ppermute | solution.py:619
  79.8 10.3 %collective-permute-start.11 = (bf16[512,128]{1,0:T(8,128)(2,1)S(1)}, bf16[512,128]{1,0:T(8,128)(2,1)S(1)}, u32[]{:S(2)}, u32[]{:S(2)}) collective-permute-start(bf16[512,128]{1,0:T(8,128)(2,1)S(1)} %get-tuple-element.230), channel_id=1, source_target_pairs={{0,24},{1,25},{2,26},{3,27},{4,28},{5,29},{6,30},{7,31},{8,16},{9,... | collective-permute-start | bytes 393224 | tf_op jit(solution)/shard_map/ppermute | solution.py:619
  80.4 13.4 %collective-permute-start.12 = (bf16[272,512]{1,0:T(8,128)(2,1)S(1)}, bf16[272,512]{1,0:T(8,128)(2,1)S(1)}, u32[]{:S(2)}, u32[]{:S(2)}) collective-permute-start(bf16[272,512]{1,0:T(8,128)(2,1)S(1)} %get-tuple-element.238), channel_id=1, source_target_pairs={{0,2},{1,3},{2,0},{3,1},{4,6},{5,7},{6,4},{7,5},{8,10},{9,11},{10,... | collective-permute-start | bytes 835592 | tf_op jit(solution)/shard_map/ppermute | solution.py:619
  81.9 12.7 %collective-permute-start.13 = (bf16[272,512]{1,0:T(8,128)(2,1)S(1)}, bf16[272,512]{1,0:T(8,128)(2,1)S(1)}, u32[]{:S(2)}, u32[]{:S(2)}) collective-permute-start(bf16[272,512]{1,0:T(8,128)(2,1)S(1)} %get-tuple-element.239), channel_id=1, source_target_pairs={{0,4},{1,5},{2,6},{3,7},{4,0},{5,1},{6,2},{7,3},{8,12},{9,13},{10,... | collective-permute-start | bytes 835592 | tf_op jit(solution)/shard_map/ppermute | solution.py:619
  83.4 12.7 %collective-permute-start.14 = (bf16[272,512]{1,0:T(8,128)(2,1)S(1)}, bf16[272,512]{1,0:T(8,128)(2,1)S(1)}, u32[]{:S(2)}, u32[]{:S(2)}) collective-permute-start(bf16[272,512]{1,0:T(8,128)(2,1)S(1)} %get-tuple-element.240), channel_id=1, source_target_pairs={{0,6},{1,7},{2,4},{3,5},{4,2},{5,3},{6,0},{7,1},{8,14},{9,15},{10,... | collective-permute-start | bytes 835592 | tf_op jit(solution)/shard_map/ppermute | solution.py:619
  90.2 14.8 %collective-permute-start.18 = (bf16[512,128]{1,0:T(8,128)(2,1)S(1)}, bf16[512,128]{1,0:T(8,128)(2,1)S(1)}, u32[]{:S(2)}, u32[]{:S(2)}) collective-permute-start(bf16[512,128]{1,0:T(8,128)(2,1)S(1)} %add_convert_fusion), channel_id=1, source_target_pairs={{0,24},{1,25},{2,26},{3,27},{4,28},{5,29},{6,30},{7,31},{8,16},{9,... | collective-permute-start | bytes 393224 | tf_op jit(solution)/shard_map/ppermute | solution.py:619
  92.6 12.4 %collective-permute-start.17 = (bf16[512,128]{1,0:T(8,128)(2,1)S(1)}, bf16[512,128]{1,0:T(8,128)(2,1)S(1)}, u32[]{:S(2)}, u32[]{:S(2)}) collective-permute-start(bf16[512,128]{1,0:T(8,128)(2,1)S(1)} %add_convert_fusion), channel_id=1, source_target_pairs={{0,16},{1,17},{2,18},{3,19},{4,20},{5,21},{6,22},{7,23},{8,24},{9,... | collective-permute-start | bytes 393224 | tf_op jit(solution)/shard_map/ppermute | solution.py:619
  93.9 11.2 %collective-permute-start.16 = (bf16[512,128]{1,0:T(8,128)(2,1)S(1)}, bf16[512,128]{1,0:T(8,128)(2,1)S(1)}, u32[]{:S(2)}, u32[]{:S(2)}) collective-permute-start(bf16[512,128]{1,0:T(8,128)(2,1)S(1)} %add_convert_fusion), channel_id=1, source_target_pairs={{0,8},{1,9},{2,10},{3,11},{4,12},{5,13},{6,14},{7,15},{8,0},{9,1},... | collective-permute-start | bytes 393224 | tf_op jit(solution)/shard_map/ppermute | solution.py:619
  94.7 10.4 %collective-permute-start.19 = (bf16[272,512]{1,0:T(8,128)(2,1)S(1)}, bf16[272,512]{1,0:T(8,128)(2,1)S(1)}, u32[]{:S(2)}, u32[]{:S(2)}) collective-permute-start(bf16[272,512]{1,0:T(8,128)(2,1)S(1)} %get-tuple-element.250), channel_id=1, source_target_pairs={{0,2},{1,3},{2,0},{3,1},{4,6},{5,7},{6,4},{7,5},{8,10},{9,11},{10,... | collective-permute-start | bytes 835592 | tf_op jit(solution)/shard_map/ppermute | solution.py:619
  96.4 8.5 %collective-permute-start.15 = (bf16[144,512]{1,0:T(8,128)(2,1)S(1)}, bf16[144,512]{1,0:T(8,128)(2,1)S(1)}, u32[]{:S(2)}, u32[]{:S(2)}) collective-permute-start(bf16[144,512]{1,0:T(8,128)(2,1)S(1)} %pad_maximum_fusion.11), channel_id=1, source_target_pairs={{0,8},{1,9},{2,10},{3,11},{4,12},{5,13},{6,14},{7,15},{8,0},{9,1},... | collective-permute-start | bytes 442376 | tf_op jit(solution)/shard_map/ppermute | solution.py:619
  105.1 18.9 %collective-permute-start.25 = (bf16[4,512,128]{2,1,0:T(8,128)(2,1)S(1)}, bf16[4,512,128]{2,1,0:T(8,128)(2,1)S(1)}, u32[]{:S(2)}, u32[]{:S(2)}) collective-permute-start(bf16[4,512,128]{2,1,0:T(8,128)(2,1)S(1)} %pad_maximum_fusion.1.refs_0_), channel_id=1, source_target_pairs={{0,4},{1,5},{2,6},{3,7},{4,0},{5,1},{6,2},{7,3},{8,12},{9,13},{10,... | collective-permute-start | bytes 1572872 | tf_op jit(solution)/shard_map/ppermute | solution.py:619
  106.7 17.3 %collective-permute-start.24 = (bf16[4,512,128]{2,1,0:T(8,128)(2,1)S(1)}, bf16[4,512,128]{2,1,0:T(8,128)(2,1)S(1)}, u32[]{:S(2)}, u32[]{:S(2)}) collective-permute-start(bf16[4,512,128]{2,1,0:T(8,128)(2,1)S(1)} %pad_maximum_fusion.1.refs_0_), channel_id=1, source_target_pairs={{0,2},{1,3},{2,0},{3,1},{4,6},{5,7},{6,4},{7,5},{8,10},{9,11},{10,... | collective-permute-start | bytes 1572872 | tf_op jit(solution)/shard_map/ppermute | solution.py:619
  108.1 8.3 %collective-permute-start.20 = (bf16[80,512]{1,0:T(8,128)(2,1)S(1)}, bf16[80,512]{1,0:T(8,128)(2,1)S(1)}, u32[]{:S(2)}, u32[]{:S(2)}) collective-permute-start(bf16[80,512]{1,0:T(8,128)(2,1)S(1)} %pad_maximum_fusion.12), channel_id=1, source_target_pairs={{0,16},{1,17},{2,18},{3,19},{4,20},{5,21},{6,22},{7,23},{8,24},{9,... | collective-permute-start | bytes 245768 | tf_op jit(solution)/shard_map/ppermute | solution.py:619
  116.5 6.2 %collective-permute-start.23 = (bf16[64,512]{1,0:T(8,128)(2,1)S(1)}, bf16[64,512]{1,0:T(8,128)(2,1)S(1)}, u32[]{:S(2)}, u32[]{:S(2)}) collective-permute-start(bf16[64,512]{1,0:T(8,128)(2,1)S(1)} %add_convert_fusion.1), channel_id=1, source_target_pairs={{0,24},{1,25},{2,26},{3,27},{4,28},{5,29},{6,30},{7,31},{8,16},{9,... | collective-permute-start | bytes 196616 | tf_op jit(solution)/shard_map/ppermute | solution.py:619
  117.5 6.5 %collective-permute-start.22 = (bf16[64,512]{1,0:T(8,128)(2,1)S(1)}, bf16[64,512]{1,0:T(8,128)(2,1)S(1)}, u32[]{:S(2)}, u32[]{:S(2)}) collective-permute-start(bf16[64,512]{1,0:T(8,128)(2,1)S(1)} %add_convert_fusion.1), channel_id=1, source_target_pairs={{0,16},{1,17},{2,18},{3,19},{4,20},{5,21},{6,22},{7,23},{8,24},{9,... | collective-permute-start | bytes 196616 | tf_op jit(solution)/shard_map/ppermute | solution.py:619
  117.5 6.5 %collective-permute-start.21 = (bf16[64,512]{1,0:T(8,128)(2,1)S(1)}, bf16[64,512]{1,0:T(8,128)(2,1)S(1)}, u32[]{:S(2)}, u32[]{:S(2)}) collective-permute-start(bf16[64,512]{1,0:T(8,128)(2,1)S(1)} %add_convert_fusion.1), channel_id=1, source_target_pairs={{0,8},{1,9},{2,10},{3,11},{4,12},{5,13},{6,14},{7,15},{8,0},{9,1},... | collective-permute-start | bytes 196616 | tf_op jit(solution)/shard_map/ppermute | solution.py:619
  124.1 6.6 %collective-permute-start.27 = (bf16[2,512,128]{2,1,0:T(8,128)(2,1)S(1)}, bf16[2,512,128]{2,1,0:T(8,128)(2,1)S(1)}, u32[]{:S(2)}, u32[]{:S(2)}) collective-permute-start(bf16[2,512,128]{2,1,0:T(8,128)(2,1)S(1)} %slice.227), channel_id=1, source_target_pairs={{0,2},{1,3},{2,0},{3,1},{4,6},{5,7},{6,4},{7,5},{8,10},{9,11},{10,... | collective-permute-start | bytes 786440 | tf_op jit(solution)/shard_map/ppermute | solution.py:619
  124.8 6.4 %collective-permute-start.28 = (bf16[2,512,128]{2,1,0:T(8,128)(2,1)S(1)}, bf16[2,512,128]{2,1,0:T(8,128)(2,1)S(1)}, u32[]{:S(2)}, u32[]{:S(2)}) collective-permute-start(bf16[2,512,128]{2,1,0:T(8,128)(2,1)S(1)} %slice.228), channel_id=1, source_target_pairs={{0,4},{1,5},{2,6},{3,7},{4,0},{5,1},{6,2},{7,3},{8,12},{9,13},{10,... | collective-permute-start | bytes 786440 | tf_op jit(solution)/shard_map/ppermute | solution.py:619
  125.3 8.1 %collective-permute-start.29 = (bf16[4,64,512]{2,1,0:T(8,128)(2,1)S(1)}, bf16[4,64,512]{2,1,0:T(8,128)(2,1)S(1)}, u32[]{:S(2)}, u32[]{:S(2)}) collective-permute-start(bf16[4,64,512]{2,1,0:T(8,128)(2,1)S(1)} %pad_maximum_fusion.9.refs_0_), channel_id=1, source_target_pairs={{0,2},{1,3},{2,0},{3,1},{4,6},{5,7},{6,4},{7,5},{8,10},{9,11},{10,... | collective-permute-start | bytes 786440 | tf_op jit(solution)/shard_map/ppermute | solution.py:619
  126.7 7.2 %collective-permute-start.30 = (bf16[4,64,512]{2,1,0:T(8,128)(2,1)S(1)}, bf16[4,64,512]{2,1,0:T(8,128)(2,1)S(1)}, u32[]{:S(2)}, u32[]{:S(2)}) collective-permute-start(bf16[4,64,512]{2,1,0:T(8,128)(2,1)S(1)} %pad_maximum_fusion.9.refs_0_), channel_id=1, source_target_pairs={{0,4},{1,5},{2,6},{3,7},{4,0},{5,1},{6,2},{7,3},{8,12},{9,13},{10,... | collective-permute-start | bytes 786440 | tf_op jit(solution)/shard_map/ppermute | solution.py:619
  128.2 5.7 %collective-permute-start.26 = (bf16[4,512,128]{2,1,0:T(8,128)(2,1)S(1)}, bf16[4,512,128]{2,1,0:T(8,128)(2,1)S(1)}, u32[]{:S(2)}, u32[]{:S(2)}) collective-permute-start(bf16[4,512,128]{2,1,0:T(8,128)(2,1)S(1)} %pad_maximum_fusion.1.refs_0_), channel_id=1, source_target_pairs={{0,1},{1,0},{2,3},{3,2},{4,5},{5,4},{6,7},{7,6},{8,9},{9,8},{10,11... | collective-permute-start | bytes 1572872 | tf_op jit(solution)/shard_map/ppermute | solution.py:619
  134.1 9.2 %collective-permute-start.33 = (bf16[8,512,128]{2,1,0:T(8,128)(2,1)S(1)}, bf16[8,512,128]{2,1,0:T(8,128)(2,1)S(1)}, u32[]{:S(2)}, u32[]{:S(2)}) collective-permute-start(bf16[8,512,128]{2,1,0:T(8,128)(2,1)S(1)} %pad_maximum_fusion), channel_id=1, source_target_pairs={{0,1},{1,0},{2,3},{3,2},{4,5},{5,4},{6,7},{7,6},{8,9},{9,8},{10,11... | collective-permute-start | bytes 3145736 | tf_op jit(solution)/shard_map/ppermute | solution.py:619
  134.2 9.1 %collective-permute-start.35 = (bf16[12,64,512]{2,1,0:T(8,128)(2,1)S(1)}, bf16[12,64,512]{2,1,0:T(8,128)(2,1)S(1)}, u32[]{:S(2)}, u32[]{:S(2)}) collective-permute-start(bf16[12,64,512]{2,1,0:T(8,128)(2,1)S(1)} %constant_dynamic-update-slice_fusion), channel_id=1, source_target_pairs={{0,1},{1,0},{2,3},{3,2},{4,5},{5,4},{6,7},{7,6},{8,9},{9,8},{10,11... | collective-permute-start | bytes 2359304 | tf_op jit(solution)/shard_map/ppermute | solution.py:619
  134.7 8.6 %collective-permute-start.34 = (bf16[4,512,128]{2,1,0:T(8,128)(2,1)S(1)}, bf16[4,512,128]{2,1,0:T(8,128)(2,1)S(1)}, u32[]{:S(2)}, u32[]{:S(2)}) collective-permute-start(bf16[4,512,128]{2,1,0:T(8,128)(2,1)S(1)} %pad_maximum_fusion.2), channel_id=1, source_target_pairs={{0,1},{1,0},{2,3},{3,2},{4,5},{5,4},{6,7},{7,6},{8,9},{9,8},{10,11... | collective-permute-start | bytes 1572872 | tf_op jit(solution)/shard_map/ppermute | solution.py:619
  136.3 5.8 %collective-permute-start.31 = (bf16[2,64,512]{2,1,0:T(8,128)(2,1)S(1)}, bf16[2,64,512]{2,1,0:T(8,128)(2,1)S(1)}, u32[]{:S(2)}, u32[]{:S(2)}) collective-permute-start(bf16[2,64,512]{2,1,0:T(8,128)(2,1)S(1)} %slice.229), channel_id=1, source_target_pairs={{0,2},{1,3},{2,0},{3,1},{4,6},{5,7},{6,4},{7,5},{8,10},{9,11},{10,... | collective-permute-start | bytes 393224 | tf_op jit(solution)/shard_map/ppermute | solution.py:619
  144.1 6.5 %collective-permute-start.36 = (bf16[4,64,512]{2,1,0:T(8,128)(2,1)}, bf16[4,64,512]{2,1,0:T(8,128)(2,1)}, u32[]{:S(2)}, u32[]{:S(2)}) collective-permute-start(bf16[4,64,512]{2,1,0:T(8,128)(2,1)} %pad_maximum_fusion.10), channel_id=1, source_target_pairs={{0,1},{1,0},{2,3},{3,2},{4,5},{5,4},{6,7},{7,6},{8,9},{9,8},{10,11... | collective-permute-start | bytes 786440 | tf_op jit(solution)/shard_map/ppermute | solution.py:619
  (26 other events, 160.2 us)

commit v5 on v4

--- a/solution.py
+++ b/solution.py
@@ -91,7 +91,7 @@
         out_shape=[shape(2 * rows), shape(rows), shape(2 * rows), shape(2 * rows),
                    jax.ShapeDtypeStruct((heads, span), F32), jax.ShapeDtypeStruct((16,), jnp.int32)],
         scratch_shapes=[pltpu.SMEM((2,), jnp.int32)] * 2 + [pltpu.VMEM((width, width), BF16)] * 3 + [pltpu.SemaphoreType.DMA((5,))],
-        name="prepare", compiler_params=pltpu.CompilerParams(vmem_limit_bytes=14 << 20),
+        name="prepare", compiler_params=pltpu.CompilerParams(vmem_limit_bytes=60 << 20),
     )(ids, mine, other, gain, bias, buckets, pads, prefixes, wq, wk, wv)
 
 def back_pieces(to, active, low, mine):
@@ -253,7 +253,7 @@
                        + [pltpu.VMEM(wo.shape, BF16), pltpu.VMEM(win.shape, BF16), pltpu.VMEM(wback.shape, BF16),
                           pltpu.VMEM((2, 2 * count, 4 * count), BF16), pltpu.VMEM((2, 2 * count, 4 * count), F32),
                           pltpu.VMEM((2, 128, span), F32), pltpu.VMEM((2, 4 * count, 128), BF16), pltpu.SemaphoreType.DMA((16,))],
-        name="front", compiler_params=pltpu.CompilerParams(vmem_limit_bytes=40 << 20),
+        name="front", compiler_params=pltpu.CompilerParams(vmem_limit_bytes=36 << 20),
     )(info, far, far_other, near, q_l, k_l, v_l, lines, wq, wk, wv, gain1, gain2, gain3, cots, wo, win, wback)
 
 def through_kernel(info, slopes_h, win_h, mixed_h, steep_h, wo_h, att_h, gain2, grad_mixed_o, grad_attended_o, grad_out_o, rows,
@@ -305,7 +305,7 @@
         out_specs=[free] * 3 + [vmem],
         out_shape=outs + [shape((8, width), F32)],
         scratch_shapes=[pltpu.VMEM(g.shape, g.dtype) for g in given] + [pltpu.VMEM(o.shape, o.dtype) for o in outs] + [pltpu.SemaphoreType.DMA((15,))],
-        name="through", compiler_params=pltpu.CompilerParams(vmem_limit_bytes=14 << 20),
+        name="through", compiler_params=pltpu.CompilerParams(vmem_limit_bytes=16 << 20),
     )(info, *given, gain2)
 
 def meet_kernel(info, got_h, active_h, slopes_h, turned_h, steep_h, *refs):
@@ -566,7 +566,7 @@
         out_shape=[shape((16 * 128, width), F32), shape((width, 16 * 128), F32)],
         scratch_shapes=[pltpu.VMEM((count, 128, width), F32), pltpu.VMEM((count, width, 128), F32), pltpu.SemaphoreType.DMA((count,))],
         input_output_aliases={1 + len(parts) + i: i for i in range(len(made))},
-        name="place", compiler_params=pltpu.CompilerParams(vmem_limit_bytes=20 << 20),
+        name="place", compiler_params=pltpu.CompilerParams(vmem_limit_bytes=24 << 20),
     )(info, *[p for _, p in parts], *made)
 
 def sort_kernel(firsts, info, *refs):
@@ -712,7 +712,11 @@
     quarter = jnp.stack([whole] + back_line)
     token, quarter = wait(token, quarter)
     from_y, from_x = exchange(quarter, ROW), exchange(quarter, NEAR_X)
-    token, took = wait(token, took)
+    pool_mine, pool_other = one_value(home[rows:])[:1], one_value(away_got[rows:])[:1]
+    pooled = jnp.where(doc == 0, jnp.concatenate([pool_mine, pool_other]), jnp.concatenate([pool_other, pool_mine]))
+    home, away_got = home[:rows], away_got[:rows]
+    input_grad = jnp.where(doc == 0, jnp.stack([home, away_got]), jnp.stack([away_got, home]))
+    token, took, pooled, input_grad = wait(token, took, pooled, input_grad)
 
     small = small + one_value(took[piece:])
     rest = added(lines, took[:piece])
@@ -721,12 +725,15 @@
         small = small + exchange(small, bit)
     token, rest = wait(token, rest)
     rest_back = [exchange(rest, m) for m in zz]
-    token, rest_back, from_y, from_x = wait(token, rest_back, from_y, from_x)
+    outs = [small[0], small[1], small[2], small[3, : bias_table.size].reshape(bias_table.shape[::-1]).T]
+    token, from_y, from_x, outs = wait(token, from_y, from_x, outs)
+
+    sends = [from_x[:2], from_y[2:]]
+    token, sends, rest_back = wait(token, sends, rest_back)
+    far_a, far_b = exchange(sends[0], ROW), exchange(sends[1], NEAR_X)
     fourth = jnp.stack([rest] + rest_back)
-
-    sends = [from_x[:2], from_y[2:], fourth, fourth]
-    token, sends, quarter = wait(token, sends, quarter)
-    far_a, far_b, fourth_y, fourth_x = (exchange(s, m) for s, m in zip(sends, (ROW, NEAR_X, ROW, NEAR_X)))
+    token, fourth, quarter = wait(token, fourth, quarter)
+    fourth_y, fourth_x = exchange(fourth, ROW), exchange(fourth, NEAR_X)
     other = exchange(quarter, CORE)
     near_pair = jnp.concatenate([from_y, from_x])
     grads = place(token, [(0, quarter), (4, from_y), (8, from_x)], [], width)
@@ -736,32 +743,15 @@
     token, sends = wait(token, sends)
     last_a, last_b, other_near, other_far, pair = (exchange(s, m) for s, m in zip(sends, (ROW, NEAR_X, CORE, CORE, CORE)))
     grads = place(token, [(12, far_a), (14, far_b), (16, other)], grads, width)
-    token, grads, last_a, last_b, other_near, other_far, pair = wait(token, grads, last_a, last_b, other_near, other_far, pair)
+    token, grads, other_near, other_far = wait(token, grads, other_near, other_far)
+    out_back, out_in = place(token, [(20, other_near), (28, other_far)], grads, width)
+    token, out_back, out_in, last_a, last_b, pair = wait(token, out_back, out_in, last_a, last_b, pair)
 
     ends = exchange(jnp.concatenate([last_a, last_b]), CORE)
     made = sort(token, [(0, fourth), (4, fourth_y), (8, fourth_x), (12, last_a), (14, last_b), (16, pair)], [], width)
-    out_back, out_in = place(token, [(20, other_near), (28, other_far)], grads, width)
     token, made, ends = wait(token, made, ends)
     out_out, out_query, out_key, out_value = sort(token, [(28, ends)], made, width)
-
-    pool_mine, pool_other = one_value(home[rows:])[:1], one_value(away_got[rows:])[:1]
-    pooled = jnp.where(doc == 0, jnp.concatenate([pool_mine, pool_other]), jnp.concatenate([pool_other, pool_mine]))
-    home, away_got = home[:rows], away_got[:rows]
-    input_grad = jnp.where(doc == 0, jnp.stack([home, away_got]), jnp.stack([away_got, home]))
-    return (
-        pooled,
-        input_grad,
-        out_query,
-        out_key,
-        out_value,
-        out_out,
-        out_in,
-        out_back,
-        small[0],
-        small[1],
-        small[2],
-        small[3, : bias_table.size].reshape(bias_table.shape[::-1]).T,
-    )
+    return (pooled, input_grad, out_query, out_key, out_value, out_out, out_in, out_back, *outs)
 
 def solution(mesh):
     data = P("dp", "blk", None)

time: 153 us -> 157 us (1.026)
  Pallas kernels: 65.9 us -> 68.6 us
    pallas_call x1, Pallas kernels: 2.77 us -> 4.59 us  [prepare(): pl.pallas_call(prepare_kernel, in_specs=[smem] + [vmem] * 5 + [far] * 5,...]
    unnamed x47 -> x54, local copies, waits for them, and re-layouts: 8.29 us -> 7.66 us
  transfers between devices with their start and end apart: 37 -> 37, of which waited for: 12 -> 11; matrix products, arithmetic and copies ran while one was open for 2% -> 3% of each run, Pallas kernels for 25% -> 26%
where the time goes in v5:
time: 157 us
  Pallas kernels  68.6 us (44%)
  starting transfers between devices  40 us (25%)
  waiting for transfers between devices  32.5 us (21%)
  local copies, waits for them, and re-layouts  9.17 us (6%)
  other arithmetic  4.93 us (3%)
    ppermute x37, starting transfers between devices, exchange(): lax.ppermute(value, ('dp', 'blk'), [(i, i ^ bits) for i in range(size)])  40 us
    ppermute x37, waiting for transfers between devices, exchange(): lax.ppermute(value, ('dp', 'blk'), [(i, i ^ bits) for i in range(size)])  32.5 us
    pallas_call x1, Pallas kernels, front(): pl.pallas_call(front_kernel, grid=(heads // 2,), in_specs=[smem, whole(co...  22.8 us
    pallas_call x1, Pallas kernels, back(): pl.pallas_call(back_kernel, grid=(width // 128,), in_specs=[smem, col(cou...  20.1 us
    unnamed x54, local copies, waits for them, and re-layouts  7.66 us
    pallas_call x3, Pallas kernels, place(): pl.pallas_call(functools.partial(place_kernel, [first for first, _ in par...  6.59 us
    pallas_call x1, Pallas kernels, through(): pl.pallas_call(through_kernel, in_specs=[smem, free, pl.BlockSpec(memory_...  4.66 us
    pallas_call x1, Pallas kernels, prepare(): pl.pallas_call(prepare_kernel, in_specs=[smem] + [vmem] * 5 + [far] * 5,...  4.59 us
  transfers between devices with their start and end apart: 37, of which 11 were waited for; matrix products, arithmetic and copies ran while one was open for 3% of the time, Pallas kernels for 26%

profile of v5, /device:TPU:0, one launch (start us, length us, event | category | flops | bytes accessed | tf_op | source)
XLA Modules:
  0.0 156.6 jit_solution(12800247734455040483)
XLA Ops:
  0.7 1.9 %select_bitcast_fusion = (bf16[256,512]{1,0:T(8,128)(2,1)}, bf16[256,512]{1,0:T(8,128)(2,1)S(1)}) fusion(pred[]{:T(512)S(6)} %eq.31, bf16[2,256,512]{2,1,0:T(8,128)(2,1)} %param.15), kind=kLoop, calls=%fused_computation.27 | loop fusion | flops 262144 | bytes 1048577 | tf_op jit(solution)/shard_map/jit(_where)/select_n | solution.py:639
  3.1 2.5 %collective-permute-start = (bf16[256,512]{1,0:T(8,128)(2,1)}, bf16[256,512]{1,0:T(8,128)(2,1)}, u32[]{:S(2)}, u32[]{:S(2)}) collective-permute-start(bf16[256,512]{1,0:T(8,128)(2,1)} %get-tuple-element.174), channel_id=1, source_target_pairs={{0,2},{1,3},{2,0},{3,1},{4,6},{5,7},{6,4},{7,5},{8,10},{9,11},{10,... | collective-permute-start | bytes 786440 | tf_op jit(solution)/shard_map/ppermute | solution.py:619
  6.2 4.6 %prepare.1 = (bf16[512,512]{1,0:T(8,128)(2,1)}, bf16[256,512]{1,0:T(8,128)(2,1)}, bf16[512,512]{1,0:T(8,128)(2,1)}, bf16[512,512]{1,0:T(8,128)(2,1)}, f32[8,2048]{1,0:T(8,128)}, /*index=5*/s32[16]{0:T(128)}) custom-call(s32[8]{0:T(128)} %compare_select_fusion.6.ids, bf16[256,512]{1,0:T(8,128)(2,1)} %copy-done.1, ...), custom_call_target="tpu_custom_call" | custom-call | tf_op jit(solution)/shard_map/prepare/pallas_call | solution.py:87
  10.8 2.2 %collective-permute-done.far.far_h = bf16[256,512]{1,0:T(8,128)(2,1)} collective-permute-done((bf16[256,512]{1,0:T(8,128)(2,1)}, bf16[256,512]{1,0:T(8,128)(2,1)}, u32[]{:S(2)}, u32[]{:S(2)}) %collective-permute-start) | collective-permute-done | bytes 262176 | tf_op jit(solution)/shard_map/ppermute | solution.py:619
  12.9 1.7 %collective-permute-done.2.far_other.far_other_h = bf16[256,512]{1,0:T(8,128)(2,1)S(1)} collective-permute-done((bf16[256,512]{1,0:T(8,128)(2,1)}, bf16[256,512]{1,0:T(8,128)(2,1)S(1)}, u32[]{:S(2)}, u32[]{:S(2)}) %collective-permute-start.2) | collective-permute-done | bytes 262176 | tf_op jit(solution)/shard_map/ppermute | solution.py:619
  22.3 22.8 %front.1 = (bf16[512,512]{1,0:T(8,128)(2,1)S(1)}, bf16[256,512]{1,0:T(8,128)(2,1)S(1)}, bf16[512,512]{1,0:T(8,128)(2,1)S(1)}, bf16[512,512]{1,0:T(8,128)(2,1)S(1...) custom-call(s32[16]{0:T(128)S(1)} %copy-done.20, ...), custom_call_target="tpu_custom_call" | custom-call | tf_op jit(solution)/shard_map/front/pallas_call | solution.py:244
  45.3 4.7 %through.1 = (f32[512,512]{1,0:T(8,128)S(1)}, bf16[512,512]{1,0:T(8,128)(2,1)S(1)}, bf16[512,512]{1,0:T(8,128)(2,1)S(1)}, f32[8,512]{1,0:T(8,128)S(1)}) custom-call(s32[16]{0:T(128)S(1)} %copy-done.21, bf16[512,2048]{1,0:T(8,128)(2,1)S(1)} %get-tuple-element.185.slopes_h, bf16[512,2048]{1,0:T(8,128)(2,1)S(1)} %copy-done, ...), custom_call_target="tpu_custom_call" | custom-call | tf_op jit(solution)/shard_map/through/pallas_call | solution.py:302
  50.1 3.9 %meet.1 = (bf16[4,512,128]{2,1,0:T(8,128)(2,1)S(1)}, bf16[4,512,128]{2,1,0:T(8,128)(2,1)S(1)}, bf16[4,512,128]{2,1,0:T(8,128)(2,1)S(1)}, bf16[4,512,128]{2,1,0:T(8,128)(2,1)S(1)}) custom-call(s32[16]{0:T(128)S(1)} %copy-done.21, bf16[16,512,128]{2,1,0:T(8,128)(2,1)S(1)} %collective-permute-done.3.got_h, bf16[512,2048]{1,0:T(8,128)(2,1)S(1)} %get-tuple-element.193.active_h, ...), custom_call_target="tpu_custom_call" | custom-call | tf_op jit(solution)/shard_map/meet/pallas_call | solution.py:352
  54.0 1.8 %collective-permute-start.4 = (bf16[4,512,128]{2,1,0:T(8,128)(2,1)S(1)}, bf16[4,512,128]{2,1,0:T(8,128)(2,1)S(1)}, u32[]{:S(2)}, u32[]{:S(2)}) collective-permute-start(bf16[4,512,128]{2,1,0:T(8,128)(2,1)S(1)} %get-tuple-element.213), channel_id=1, source_target_pairs={{0,2},{1,3},{2,0},{3,1},{4,6},{5,7},{6,4},{7,5},{8,10},{9,11},{10,... | collective-permute-start | bytes 1572872 | tf_op jit(solution)/shard_map/ppermute | solution.py:619
  57.6 20.1 %back.1 = (bf16[16,64,512]{2,1,0:T(8,128)(2,1)S(1)}, bf16[1040,512]{1,0:T(8,128)(2,1)}, f32[512,512]{1,0:T(8,128)}, bf16[528,512]{1,0:T(8,128)(2,1)S(1)}, f32[8,512]{1,0:T(8,128)S(1)}) custom-call(s32[16]{0:T(128)S(1)} %copy-done.21, bf16[256,512]{1,0:T(8,128)(2,1)S(1)} %copy-done.15, bf16[256,512]{1,0:T(8,128)(2,1)S(1)} %get-tuple-element.199.qr, ...), custom_call_target="tpu_custom_call" | custom-call | tf_op jit(solution)/shard_map/back/pallas_call | solution.py:495
  77.7 2.9 %collective-permute-done.6.refs_3_ = bf16[4,512,128]{2,1,0:T(8,128)(2,1)S(1)} collective-permute-done((bf16[4,512,128]{2,1,0:T(8,128)(2,1)S(1)}, bf16[4,512,128]{2,1,0:T(8,128)(2,1)S(1)}, u32[]{:S(2)}, u32[]{:S(2)}) %collective-permute-start.6) | collective-permute-done | bytes 524320 | tf_op jit(solution)/shard_map/ppermute | solution.py:619
  81.4 1.8 %collective-permute-start.9 = (bf16[512,128]{1,0:T(8,128)(2,1)S(1)}, bf16[512,128]{1,0:T(8,128)(2,1)S(1)}, u32[]{:S(2)}, u32[]{:S(2)}) collective-permute-start(bf16[512,128]{1,0:T(8,128)(2,1)S(1)} %get-tuple-element.233), channel_id=1, source_target_pairs={{0,8},{1,9},{2,10},{3,11},{4,12},{5,13},{6,14},{7,15},{8,0},{9,1},... | collective-permute-start | bytes 393224 | tf_op jit(solution)/shard_map/ppermute | solution.py:619
  83.1 2.6 %collective-permute-start.10 = (bf16[512,128]{1,0:T(8,128)(2,1)S(1)}, bf16[512,128]{1,0:T(8,128)(2,1)S(1)}, u32[]{:S(2)}, u32[]{:S(2)}) collective-permute-start(bf16[512,128]{1,0:T(8,128)(2,1)S(1)} %get-tuple-element.234), channel_id=1, source_target_pairs={{0,16},{1,17},{2,18},{3,19},{4,20},{5,21},{6,22},{7,23},{8,24},{9,... | collective-permute-start | bytes 393224 | tf_op jit(solution)/shard_map/ppermute | solution.py:619
  86.2 1.7 %collective-permute-start.12 = (bf16[272,512]{1,0:T(8,128)(2,1)S(1)}, bf16[272,512]{1,0:T(8,128)(2,1)S(1)}, u32[]{:S(2)}, u32[]{:S(2)}) collective-permute-start(bf16[272,512]{1,0:T(8,128)(2,1)S(1)} %get-tuple-element.246), channel_id=1, source_target_pairs={{0,2},{1,3},{2,0},{3,1},{4,6},{5,7},{6,4},{7,5},{8,10},{9,11},{10,... | collective-permute-start | bytes 835592 | tf_op jit(solution)/shard_map/ppermute | solution.py:619
  88.0 1.5 collective-permute-start.13
  89.5 1.7 %collective-permute-start.14 = (bf16[272,512]{1,0:T(8,128)(2,1)S(1)}, bf16[272,512]{1,0:T(8,128)(2,1)S(1)}, u32[]{:S(2)}, u32[]{:S(2)}) collective-permute-start(bf16[272,512]{1,0:T(8,128)(2,1)S(1)} %get-tuple-element.248), channel_id=1, source_target_pairs={{0,6},{1,7},{2,4},{3,5},{4,2},{5,3},{6,0},{7,1},{8,14},{9,15},{10,... | collective-permute-start | bytes 835592 | tf_op jit(solution)/shard_map/ppermute | solution.py:619
  91.2 1.5 ending.1
  92.7 3.3 %collective-permute-done.10 = bf16[512,128]{1,0:T(8,128)(2,1)S(1)} collective-permute-done((bf16[512,128]{1,0:T(8,128)(2,1)S(1)}, bf16[512,128]{1,0:T(8,128)(2,1)S(1)}, u32[]{:S(2)}, u32[]{:S(2)}) %collective-permute-start.10) | collective-permute-done | bytes 131104 | tf_op jit(solution)/shard_map/ppermute | solution.py:619
  96.1 2.4 %collective-permute-start.18 = (bf16[512,128]{1,0:T(8,128)(2,1)S(1)}, bf16[512,128]{1,0:T(8,128)(2,1)S(1)}, u32[]{:S(2)}, u32[]{:S(2)}) collective-permute-start(bf16[512,128]{1,0:T(8,128)(2,1)S(1)} %add_convert_fusion), channel_id=1, source_target_pairs={{0,24},{1,25},{2,26},{3,27},{4,28},{5,29},{6,30},{7,31},{8,16},{9,... | collective-permute-start | bytes 393224 | tf_op jit(solution)/shard_map/ppermute | solution.py:619
  100.6 1.5 collective-permute-start.19
  103.8 7.2 %collective-permute-done.15 = bf16[144,512]{1,0:T(8,128)(2,1)S(1)} collective-permute-done((bf16[144,512]{1,0:T(8,128)(2,1)S(1)}, bf16[144,512]{1,0:T(8,128)(2,1)S(1)}, u32[]{:S(2)}, u32[]{:S(2)}) %collective-permute-start.15) | collective-permute-done | bytes 147488 | tf_op jit(solution)/shard_map/ppermute | solution.py:619
  111.2 1.5 collective-permute-start.22
  112.7 1.5 collective-permute-start.21
  117.1 5.4 %collective-permute-done.20 = bf16[80,512]{1,0:T(8,128)(2,1)S(1)} collective-permute-done((bf16[80,512]{1,0:T(8,128)(2,1)S(1)}, bf16[80,512]{1,0:T(8,128)(2,1)S(1)}, u32[]{:S(2)}, u32[]{:S(2)}) %collective-permute-start.20) | collective-permute-done | bytes 81952 | tf_op jit(solution)/shard_map/ppermute | solution.py:619
  123.6 3.4 %collective-permute-start.23 = (bf16[64,512]{1,0:T(8,128)(2,1)S(1)}, bf16[64,512]{1,0:T(8,128)(2,1)S(1)}, u32[]{:S(2)}, u32[]{:S(2)}) collective-permute-start(bf16[64,512]{1,0:T(8,128)(2,1)S(1)} %add_convert_fusion.1), channel_id=1, source_target_pairs={{0,8},{1,9},{2,10},{3,11},{4,12},{5,13},{6,14},{7,15},{8,0},{9,1},... | collective-permute-start | bytes 196616 | tf_op jit(solution)/shard_map/ppermute | solution.py:619
  131.3 1.6 collective-permute-start.27
  134.3 2.3 %place.3 = (f32[2048,512]{1,0:T(8,128)}, f32[512,2048]{1,0:T(8,128)}) custom-call(s32[16]{0:T(128)S(1)} %copy-done.21, bf16[4,512,128]{2,1,0:T(8,128)(2,1)S(1)} %pad_maximum_fusion.2.refs_0_, bf16[4,512,128]{2,1,0:T(8,128)(2,1)S(1)} %collective-permute-done.21.refs_1_, bf16[4,512,128]{2,1,0:T(8,128)(2,1)S(1)} %collective-permute-done.22.refs_2_), custom_call_target="tpu_custom_call" | custom-call | tf_op jit(solution)/shard_map/place/pallas_call | solution.py:562
  136.8 2.6 %collective-permute-done.30.refs_2_ = bf16[4,64,512]{2,1,0:T(8,128)(2,1)S(1)} collective-permute-done((bf16[4,64,512]{2,1,0:T(8,128)(2,1)S(1)}, bf16[4,64,512]{2,1,0:T(8,128)(2,1)S(1)}, u32[]{:S(2)}, u32[]{:S(2)}) %collective-permute-start.30) | collective-permute-done | bytes 262176 | tf_op jit(solution)/shard_map/ppermute | solution.py:619
  140.0 4.8 %collective-permute-done.27.refs_0_ = bf16[2,512,128]{2,1,0:T(8,128)(2,1)S(1)} collective-permute-done((bf16[2,512,128]{2,1,0:T(8,128)(2,1)S(1)}, bf16[2,512,128]{2,1,0:T(8,128)(2,1)S(1)}, u32[]{:S(2)}, u32[]{:S(2)}) %collective-permute-start.27) | collective-permute-done | bytes 262176 | tf_op jit(solution)/shard_map/ppermute | solution.py:619
  147.6 1.9 %place.4 = (f32[2048,512]{1,0:T(8,128)}, f32[512,2048]{1,0:T(8,128)}) custom-call(s32[16]{0:T(128)S(1)} %copy-done.21, bf16[2,512,128]{2,1,0:T(8,128)(2,1)S(1)} %collective-permute-done.27.refs_0_, bf16[2,512,128]{2,1,0:T(8,128)(2,1)S(1)} %collective-permute-done.28.refs_1_, ...), custom_call_target="tpu_custom_call", output_to_operand_aliasing={{0}: (4, {}), {1}: (5, {})} | custom-call | tf_op jit(solution)/shard_map/place/pallas_call | solution.py:562
  149.6 2.3 %place.5 = (f32[2048,512]{1,0:T(8,128)}, f32[512,2048]{1,0:T(8,128)}) custom-call(s32[16]{0:T(128)S(1)} %copy-done.21, bf16[8,512,128]{2,1,0:T(8,128)(2,1)S(1)} %collective-permute-done.31.refs_0_, bf16[4,512,128]{2,1,0:T(8,128)(2,1)S(1)} %collective-permute-done.32.refs_1_, ...), custom_call_target="tpu_custom_call", output_to_operand_aliasing={{0}: (3, {}), {1}: (4, {})} | custom-call | tf_op jit(solution)/shard_map/place/pallas_call | solution.py:562
  152.2 2.8 %sort.2 = (f32[512,512]{1,0:T(8,128)}, f32[512,512]{1,0:T(8,128)}, f32[512,512]{1,0:T(8,128)}, f32[512,512]{1,0:T(8,128)}) custom-call(s32[16]{0:T(128)S(1)} %copy-done.21, bf16[4,64,512]{2,1,0:T(8,128)(2,1)S(1)} %pad_maximum_fusion.10.refs_0_, bf16[4,64,512]{2,1,0:T(8,128)(2,1)S(1)} %collective-permute-done.29.refs_1_, ...), custom_call_target="tpu_custom_call" | custom-call | tf_op jit(solution)/shard_map/sort/pallas_call | solution.py:596
  (146 shorter events, 30.5 us)
Async XLA Ops:
  3.1 9.8 %collective-permute-start = (bf16[256,512]{1,0:T(8,128)(2,1)}, bf16[256,512]{1,0:T(8,128)(2,1)}, u32[]{:S(2)}, u32[]{:S(2)}) collective-permute-start(bf16[256,512]{1,0:T(8,128)(2,1)} %get-tuple-element.174), channel_id=1, source_target_pairs={{0,2},{1,3},{2,0},{3,1},{4,6},{5,7},{6,4},{7,5},{8,10},{9,11},{10,... | collective-permute-start | bytes 786440 | tf_op jit(solution)/shard_map/ppermute | solution.py:619
  45.1 4.9 %collective-permute-start.3 = (bf16[16,512,128]{2,1,0:T(8,128)(2,1)S(1)}, bf16[16,512,128]{2,1,0:T(8,128)(2,1)S(1)}, u32[]{:S(2)}, u32[]{:S(2)}) collective-permute-start(bf16[16,512,128]{2,1,0:T(8,128)(2,1)S(1)} %get-tuple-element.190), channel_id=1, source_target_pairs={{0,1},{1,0},{2,3},{3,2},{4,5},{5,4},{6,7},{7,6},{8,9},{9,8},{10,11... | collective-permute-start | bytes 6291464 | tf_op jit(solution)/shard_map/ppermute | solution.py:619
  54.0 23.7 %collective-permute-start.4 = (bf16[4,512,128]{2,1,0:T(8,128)(2,1)S(1)}, bf16[4,512,128]{2,1,0:T(8,128)(2,1)S(1)}, u32[]{:S(2)}, u32[]{:S(2)}) collective-permute-start(bf16[4,512,128]{2,1,0:T(8,128)(2,1)S(1)} %get-tuple-element.213), channel_id=1, source_target_pairs={{0,2},{1,3},{2,0},{3,1},{4,6},{5,7},{6,4},{7,5},{8,10},{9,11},{10,... | collective-permute-start | bytes 1572872 | tf_op jit(solution)/shard_map/ppermute | solution.py:619
  55.8 21.9 %collective-permute-start.5 = (bf16[4,512,128]{2,1,0:T(8,128)(2,1)S(1)}, bf16[4,512,128]{2,1,0:T(8,128)(2,1)S(1)}, u32[]{:S(2)}, u32[]{:S(2)}) collective-permute-start(bf16[4,512,128]{2,1,0:T(8,128)(2,1)S(1)} %get-tuple-element.214), channel_id=1, source_target_pairs={{0,4},{1,5},{2,6},{3,7},{4,0},{5,1},{6,2},{7,3},{8,12},{9,13},{10,... | collective-permute-start | bytes 1572872 | tf_op jit(solution)/shard_map/ppermute | solution.py:619
  57.3 23.2 %collective-permute-start.6 = (bf16[4,512,128]{2,1,0:T(8,128)(2,1)S(1)}, bf16[4,512,128]{2,1,0:T(8,128)(2,1)S(1)}, u32[]{:S(2)}, u32[]{:S(2)}) collective-permute-start(bf16[4,512,128]{2,1,0:T(8,128)(2,1)S(1)} %get-tuple-element.215), channel_id=1, source_target_pairs={{0,6},{1,7},{2,4},{3,5},{4,2},{5,3},{6,0},{7,1},{8,14},{9,15},{10,... | collective-permute-start | bytes 1572872 | tf_op jit(solution)/shard_map/ppermute | solution.py:619
  80.6 5.2 %collective-permute-start.7 = (bf16[1040,512]{1,0:T(8,128)(2,1)}, bf16[1040,512]{1,0:T(8,128)(2,1)S(1)}, u32[]{:S(2)}, u32[]{:S(2)}) collective-permute-start(bf16[1040,512]{1,0:T(8,128)(2,1)} %get-tuple-element.226), channel_id=1, source_target_pairs={{0,1},{1,0},{2,3},{3,2},{4,5},{5,4},{6,7},{7,6},{8,9},{9,8},{10,11... | collective-permute-start | bytes 3194888 | tf_op jit(solution)/shard_map/ppermute | solution.py:619
  80.6 5.2 %collective-permute-start.8 = (bf16[528,512]{1,0:T(8,128)(2,1)S(1)}, bf16[528,512]{1,0:T(8,128)(2,1)S(1)}, u32[]{:S(2)}, u32[]{:S(2)}) collective-permute-start(bf16[528,512]{1,0:T(8,128)(2,1)S(1)} %get-tuple-element.227), channel_id=1, source_target_pairs={{0,1},{1,0},{2,3},{3,2},{4,5},{5,4},{6,7},{7,6},{8,9},{9,8},{10,11... | collective-permute-start | bytes 1622024 | tf_op jit(solution)/shard_map/ppermute | solution.py:619
  81.4 8.1 %collective-permute-start.9 = (bf16[512,128]{1,0:T(8,128)(2,1)S(1)}, bf16[512,128]{1,0:T(8,128)(2,1)S(1)}, u32[]{:S(2)}, u32[]{:S(2)}) collective-permute-start(bf16[512,128]{1,0:T(8,128)(2,1)S(1)} %get-tuple-element.233), channel_id=1, source_target_pairs={{0,8},{1,9},{2,10},{3,11},{4,12},{5,13},{6,14},{7,15},{8,0},{9,1},... | collective-permute-start | bytes 393224 | tf_op jit(solution)/shard_map/ppermute | solution.py:619
  83.1 12.9 %collective-permute-start.10 = (bf16[512,128]{1,0:T(8,128)(2,1)S(1)}, bf16[512,128]{1,0:T(8,128)(2,1)S(1)}, u32[]{:S(2)}, u32[]{:S(2)}) collective-permute-start(bf16[512,128]{1,0:T(8,128)(2,1)S(1)} %get-tuple-element.234), channel_id=1, source_target_pairs={{0,16},{1,17},{2,18},{3,19},{4,20},{5,21},{6,22},{7,23},{8,24},{9,... | collective-permute-start | bytes 393224 | tf_op jit(solution)/shard_map/ppermute | solution.py:619
  85.7 10.3 %collective-permute-start.11 = (bf16[512,128]{1,0:T(8,128)(2,1)S(1)}, bf16[512,128]{1,0:T(8,128)(2,1)S(1)}, u32[]{:S(2)}, u32[]{:S(2)}) collective-permute-start(bf16[512,128]{1,0:T(8,128)(2,1)S(1)} %get-tuple-element.235), channel_id=1, source_target_pairs={{0,24},{1,25},{2,26},{3,27},{4,28},{5,29},{6,30},{7,31},{8,16},{9,... | collective-permute-start | bytes 393224 | tf_op jit(solution)/shard_map/ppermute | solution.py:619
  86.2 13.6 %collective-permute-start.12 = (bf16[272,512]{1,0:T(8,128)(2,1)S(1)}, bf16[272,512]{1,0:T(8,128)(2,1)S(1)}, u32[]{:S(2)}, u32[]{:S(2)}) collective-permute-start(bf16[272,512]{1,0:T(8,128)(2,1)S(1)} %get-tuple-element.246), channel_id=1, source_target_pairs={{0,2},{1,3},{2,0},{3,1},{4,6},{5,7},{6,4},{7,5},{8,10},{9,11},{10,... | collective-permute-start | bytes 835592 | tf_op jit(solution)/shard_map/ppermute | solution.py:619
  88.0 12.6 %collective-permute-start.13 = (bf16[272,512]{1,0:T(8,128)(2,1)S(1)}, bf16[272,512]{1,0:T(8,128)(2,1)S(1)}, u32[]{:S(2)}, u32[]{:S(2)}) collective-permute-start(bf16[272,512]{1,0:T(8,128)(2,1)S(1)} %get-tuple-element.247), channel_id=1, source_target_pairs={{0,4},{1,5},{2,6},{3,7},{4,0},{5,1},{6,2},{7,3},{8,12},{9,13},{10,... | collective-permute-start | bytes 835592 | tf_op jit(solution)/shard_map/ppermute | solution.py:619
  89.5 12.7 %collective-permute-start.14 = (bf16[272,512]{1,0:T(8,128)(2,1)S(1)}, bf16[272,512]{1,0:T(8,128)(2,1)S(1)}, u32[]{:S(2)}, u32[]{:S(2)}) collective-permute-start(bf16[272,512]{1,0:T(8,128)(2,1)S(1)} %get-tuple-element.248), channel_id=1, source_target_pairs={{0,6},{1,7},{2,4},{3,5},{4,2},{5,3},{6,0},{7,1},{8,14},{9,15},{10,... | collective-permute-start | bytes 835592 | tf_op jit(solution)/shard_map/ppermute | solution.py:619
  96.1 14.8 %collective-permute-start.18 = (bf16[512,128]{1,0:T(8,128)(2,1)S(1)}, bf16[512,128]{1,0:T(8,128)(2,1)S(1)}, u32[]{:S(2)}, u32[]{:S(2)}) collective-permute-start(bf16[512,128]{1,0:T(8,128)(2,1)S(1)} %add_convert_fusion), channel_id=1, source_target_pairs={{0,24},{1,25},{2,26},{3,27},{4,28},{5,29},{6,30},{7,31},{8,16},{9,... | collective-permute-start | bytes 393224 | tf_op jit(solution)/shard_map/ppermute | solution.py:619
  98.6 12.4 %collective-permute-start.17 = (bf16[512,128]{1,0:T(8,128)(2,1)S(1)}, bf16[512,128]{1,0:T(8,128)(2,1)S(1)}, u32[]{:S(2)}, u32[]{:S(2)}) collective-permute-start(bf16[512,128]{1,0:T(8,128)(2,1)S(1)} %add_convert_fusion), channel_id=1, source_target_pairs={{0,16},{1,17},{2,18},{3,19},{4,20},{5,21},{6,22},{7,23},{8,24},{9,... | collective-permute-start | bytes 393224 | tf_op jit(solution)/shard_map/ppermute | solution.py:619
  99.8 11.2 %collective-permute-start.16 = (bf16[512,128]{1,0:T(8,128)(2,1)S(1)}, bf16[512,128]{1,0:T(8,128)(2,1)S(1)}, u32[]{:S(2)}, u32[]{:S(2)}) collective-permute-start(bf16[512,128]{1,0:T(8,128)(2,1)S(1)} %add_convert_fusion), channel_id=1, source_target_pairs={{0,8},{1,9},{2,10},{3,11},{4,12},{5,13},{6,14},{7,15},{8,0},{9,1},... | collective-permute-start | bytes 393224 | tf_op jit(solution)/shard_map/ppermute | solution.py:619
  100.6 10.4 %collective-permute-start.19 = (bf16[272,512]{1,0:T(8,128)(2,1)S(1)}, bf16[272,512]{1,0:T(8,128)(2,1)S(1)}, u32[]{:S(2)}, u32[]{:S(2)}) collective-permute-start(bf16[272,512]{1,0:T(8,128)(2,1)S(1)} %get-tuple-element.258), channel_id=1, source_target_pairs={{0,2},{1,3},{2,0},{3,1},{4,6},{5,7},{6,4},{7,5},{8,10},{9,11},{10,... | collective-permute-start | bytes 835592 | tf_op jit(solution)/shard_map/ppermute | solution.py:619
  102.5 8.5 %collective-permute-start.15 = (bf16[144,512]{1,0:T(8,128)(2,1)S(1)}, bf16[144,512]{1,0:T(8,128)(2,1)S(1)}, u32[]{:S(2)}, u32[]{:S(2)}) collective-permute-start(bf16[144,512]{1,0:T(8,128)(2,1)S(1)} %pad_maximum_fusion.12), channel_id=1, source_target_pairs={{0,8},{1,9},{2,10},{3,11},{4,12},{5,13},{6,14},{7,15},{8,0},{9,1},... | collective-permute-start | bytes 442376 | tf_op jit(solution)/shard_map/ppermute | solution.py:619
  111.2 17.1 %collective-permute-start.22 = (bf16[4,512,128]{2,1,0:T(8,128)(2,1)S(1)}, bf16[4,512,128]{2,1,0:T(8,128)(2,1)S(1)}, u32[]{:S(2)}, u32[]{:S(2)}) collective-permute-start(bf16[4,512,128]{2,1,0:T(8,128)(2,1)S(1)} %pad_maximum_fusion.2.refs_0_), channel_id=1, source_target_pairs={{0,4},{1,5},{2,6},{3,7},{4,0},{5,1},{6,2},{7,3},{8,12},{9,13},{10,... | collective-permute-start | bytes 1572872 | tf_op jit(solution)/shard_map/ppermute | solution.py:619
  112.7 15.6 %collective-permute-start.21 = (bf16[4,512,128]{2,1,0:T(8,128)(2,1)S(1)}, bf16[4,512,128]{2,1,0:T(8,128)(2,1)S(1)}, u32[]{:S(2)}, u32[]{:S(2)}) collective-permute-start(bf16[4,512,128]{2,1,0:T(8,128)(2,1)S(1)} %pad_maximum_fusion.2.refs_0_), channel_id=1, source_target_pairs={{0,2},{1,3},{2,0},{3,1},{4,6},{5,7},{6,4},{7,5},{8,10},{9,11},{10,... | collective-permute-start | bytes 1572872 | tf_op jit(solution)/shard_map/ppermute | solution.py:619
  114.2 8.3 %collective-permute-start.20 = (bf16[80,512]{1,0:T(8,128)(2,1)S(1)}, bf16[80,512]{1,0:T(8,128)(2,1)S(1)}, u32[]{:S(2)}, u32[]{:S(2)}) collective-permute-start(bf16[80,512]{1,0:T(8,128)(2,1)S(1)} %pad_maximum_fusion.13), channel_id=1, source_target_pairs={{0,16},{1,17},{2,18},{3,19},{4,20},{5,21},{6,22},{7,23},{8,24},{9,... | collective-permute-start | bytes 245768 | tf_op jit(solution)/shard_map/ppermute | solution.py:619
  122.5 6.2 %collective-permute-start.25 = (bf16[64,512]{1,0:T(8,128)(2,1)S(1)}, bf16[64,512]{1,0:T(8,128)(2,1)S(1)}, u32[]{:S(2)}, u32[]{:S(2)}) collective-permute-start(bf16[64,512]{1,0:T(8,128)(2,1)S(1)} %add_convert_fusion.1), channel_id=1, source_target_pairs={{0,24},{1,25},{2,26},{3,27},{4,28},{5,29},{6,30},{7,31},{8,16},{9,... | collective-permute-start | bytes 196616 | tf_op jit(solution)/shard_map/ppermute | solution.py:619
  123.6 6.5 %collective-permute-start.24 = (bf16[64,512]{1,0:T(8,128)(2,1)S(1)}, bf16[64,512]{1,0:T(8,128)(2,1)S(1)}, u32[]{:S(2)}, u32[]{:S(2)}) collective-permute-start(bf16[64,512]{1,0:T(8,128)(2,1)S(1)} %add_convert_fusion.1), channel_id=1, source_target_pairs={{0,16},{1,17},{2,18},{3,19},{4,20},{5,21},{6,22},{7,23},{8,24},{9,... | collective-permute-start | bytes 196616 | tf_op jit(solution)/shard_map/ppermute | solution.py:619
  123.6 6.5 %collective-permute-start.23 = (bf16[64,512]{1,0:T(8,128)(2,1)S(1)}, bf16[64,512]{1,0:T(8,128)(2,1)S(1)}, u32[]{:S(2)}, u32[]{:S(2)}) collective-permute-start(bf16[64,512]{1,0:T(8,128)(2,1)S(1)} %add_convert_fusion.1), channel_id=1, source_target_pairs={{0,8},{1,9},{2,10},{3,11},{4,12},{5,13},{6,14},{7,15},{8,0},{9,1},... | collective-permute-start | bytes 196616 | tf_op jit(solution)/shard_map/ppermute | solution.py:619
  130.1 14.7 %collective-permute-start.26 = (bf16[4,512,128]{2,1,0:T(8,128)(2,1)S(1)}, bf16[4,512,128]{2,1,0:T(8,128)(2,1)S(1)}, u32[]{:S(2)}, u32[]{:S(2)}) collective-permute-start(bf16[4,512,128]{2,1,0:T(8,128)(2,1)S(1)} %pad_maximum_fusion.2.refs_0_), channel_id=1, source_target_pairs={{0,1},{1,0},{2,3},{3,2},{4,5},{5,4},{6,7},{7,6},{8,9},{9,8},{10,11... | collective-permute-start | bytes 1572872 | tf_op jit(solution)/shard_map/ppermute | solution.py:619
  130.2 9.2 %collective-permute-start.30 = (bf16[4,64,512]{2,1,0:T(8,128)(2,1)S(1)}, bf16[4,64,512]{2,1,0:T(8,128)(2,1)S(1)}, u32[]{:S(2)}, u32[]{:S(2)}) collective-permute-start(bf16[4,64,512]{2,1,0:T(8,128)(2,1)S(1)} %pad_maximum_fusion.10.refs_0_), channel_id=1, source_target_pairs={{0,4},{1,5},{2,6},{3,7},{4,0},{5,1},{6,2},{7,3},{8,12},{9,13},{10,... | collective-permute-start | bytes 786440 | tf_op jit(solution)/shard_map/ppermute | solution.py:619
  130.8 9.2 %collective-permute-start.29 = (bf16[4,64,512]{2,1,0:T(8,128)(2,1)S(1)}, bf16[4,64,512]{2,1,0:T(8,128)(2,1)S(1)}, u32[]{:S(2)}, u32[]{:S(2)}) collective-permute-start(bf16[4,64,512]{2,1,0:T(8,128)(2,1)S(1)} %pad_maximum_fusion.10.refs_0_), channel_id=1, source_target_pairs={{0,2},{1,3},{2,0},{3,1},{4,6},{5,7},{6,4},{7,5},{8,10},{9,11},{10,... | collective-permute-start | bytes 786440 | tf_op jit(solution)/shard_map/ppermute | solution.py:619
  131.3 13.5 %collective-permute-start.27 = (bf16[2,512,128]{2,1,0:T(8,128)(2,1)S(1)}, bf16[2,512,128]{2,1,0:T(8,128)(2,1)S(1)}, u32[]{:S(2)}, u32[]{:S(2)}) collective-permute-start(bf16[2,512,128]{2,1,0:T(8,128)(2,1)S(1)} %slice.233), channel_id=1, source_target_pairs={{0,2},{1,3},{2,0},{3,1},{4,6},{5,7},{6,4},{7,5},{8,10},{9,11},{10,... | collective-permute-start | bytes 786440 | tf_op jit(solution)/shard_map/ppermute | solution.py:619
  132.8 11.9 %collective-permute-start.28 = (bf16[2,512,128]{2,1,0:T(8,128)(2,1)S(1)}, bf16[2,512,128]{2,1,0:T(8,128)(2,1)S(1)}, u32[]{:S(2)}, u32[]{:S(2)}) collective-permute-start(bf16[2,512,128]{2,1,0:T(8,128)(2,1)S(1)} %slice.234), channel_id=1, source_target_pairs={{0,4},{1,5},{2,6},{3,7},{4,0},{5,1},{6,2},{7,3},{8,12},{9,13},{10,... | collective-permute-start | bytes 786440 | tf_op jit(solution)/shard_map/ppermute | solution.py:619
  145.1 6.9 %collective-permute-start.35 = (bf16[12,64,512]{2,1,0:T(8,128)(2,1)S(1)}, bf16[12,64,512]{2,1,0:T(8,128)(2,1)S(1)}, u32[]{:S(2)}, u32[]{:S(2)}) collective-permute-start(bf16[12,64,512]{2,1,0:T(8,128)(2,1)S(1)} %pad_maximum_fusion.1), channel_id=1, source_target_pairs={{0,1},{1,0},{2,3},{3,2},{4,5},{5,4},{6,7},{7,6},{8,9},{9,8},{10,11... | collective-permute-start | bytes 2359304 | tf_op jit(solution)/shard_map/ppermute | solution.py:619
  145.6 6.3 %collective-permute-start.33 = (bf16[2,64,512]{2,1,0:T(8,128)(2,1)S(1)}, bf16[2,64,512]{2,1,0:T(8,128)(2,1)S(1)}, u32[]{:S(2)}, u32[]{:S(2)}) collective-permute-start(bf16[2,64,512]{2,1,0:T(8,128)(2,1)S(1)} %slice.235), channel_id=1, source_target_pairs={{0,2},{1,3},{2,0},{3,1},{4,6},{5,7},{6,4},{7,5},{8,10},{9,11},{10,... | collective-permute-start | bytes 393224 | tf_op jit(solution)/shard_map/ppermute | solution.py:619
  146.1 5.8 %collective-permute-start.34 = (bf16[2,64,512]{2,1,0:T(8,128)(2,1)S(1)}, bf16[2,64,512]{2,1,0:T(8,128)(2,1)S(1)}, u32[]{:S(2)}, u32[]{:S(2)}) collective-permute-start(bf16[2,64,512]{2,1,0:T(8,128)(2,1)S(1)} %slice.236), channel_id=1, source_target_pairs={{0,4},{1,5},{2,6},{3,7},{4,0},{5,1},{6,2},{7,3},{8,12},{9,13},{10,... | collective-permute-start | bytes 393224 | tf_op jit(solution)/shard_map/ppermute | solution.py:619
  (32 other events, 235.2 us)

commit v6 on v5

--- a/solution.py
+++ b/solution.py
@@ -42,57 +42,35 @@
     count = sum(v.shape[0] for v in values)
     return jnp.concatenate(list(values) + [jnp.zeros((8 - count, values[0].shape[1]), F32)])
 
-def prepare_kernel(ids, mine, other, gain, bias, buckets, pads_h, prefixes_h, wq_h, wk_h, wv_h, hidden, query, keys, values, lines, info,
-                   pads, prefixes, wq, wk, wv, sems):
+def prepare_kernel(mine, other, gain, wq_h, wk_h, wv_h, wo_h, hidden, query, keys, values, wq, wk, wv, wo, sems):
     rows = mine.shape[0]
-    load = [pltpu.make_async_copy(a, b, sems.at[i]) for i, (a, b) in enumerate(
-        ((pads_h, pads), (prefixes_h, prefixes), (wk_h, wk), (wv_h, wv), (wq_h, wq)))]
+    load = [pltpu.make_async_copy(a, b, sems.at[i]) for i, (a, b) in enumerate(((wk_h, wk), (wv_h, wv), (wq_h, wq), (wo_h, wo)))]
     for copy in load:
         copy.start()
-    picker = jnp.where(lax.broadcasted_iota(jnp.int32, (BUCKETS, 1), 0) == buckets[...], 1.0, 0.0).astype(BF16)
-    left, total = bias[...], None
-    for _ in range(3):
-        part = left.astype(BF16)
-        left = left - part.astype(F32)
-        made = dot(part, picker)
-        total = made if total is None else total + made
-    lines[...] = jnp.zeros_like(lines)
-    lines[:, : buckets.shape[1]] = total
     for part, raw in enumerate((mine, other)):
         tokens = raw[...].astype(F32)
         hidden[part * rows : (part + 1) * rows, :] = (tokens * rms_scale(tokens) * gain[...]).astype(BF16)
     h = hidden[...]
+    load[0].wait()
+    keys[...] = dot(h, wk[...]).astype(BF16)
+    load[1].wait()
+    values[...] = dot(h, wv[...]).astype(BF16)
     load[2].wait()
-    keys[...] = dot(h, wk[...]).astype(BF16)
+    query[...] = dot(h[:rows], wq[...]).astype(BF16)
     load[3].wait()
-    values[...] = dot(h, wv[...]).astype(BF16)
-    load[4].wait()
-    query[...] = dot(h[:rows], wq[...]).astype(BF16)
-    load[0].wait()
-    load[1].wait()
-    doc = ids[6]
-    info[0] = 4 * rows - jnp.where(doc == 0, pads[0], pads[1])
-    info[5] = jnp.where(doc == 0, prefixes[0], prefixes[1])
-    for to, at in enumerate((0, 1, 2, 3)):
-        info[1 + to] = ids[at]
-    for to, at in enumerate((4, 5, 6)):
-        info[6 + to] = ids[at]
-
-def prepare(ids, pads, prefixes, mine, other, wq, wk, wv, gain, bias, buckets):
+
+def prepare(mine, other, gain, wq, wk, wv, wo):
     rows, width = mine.shape
-    span = buckets.shape[1] + 1
-    heads = bias.shape[0]
     shape = lambda n: jax.ShapeDtypeStruct((n, width), BF16)
-    smem, vmem, far = (pl.BlockSpec(memory_space=m) for m in (pltpu.SMEM, pltpu.VMEM, pltpu.HBM))
+    vmem, free = (pl.BlockSpec(memory_space=m) for m in (pltpu.VMEM, pl.ANY))
     return pl.pallas_call(
         prepare_kernel,
-        in_specs=[smem] + [vmem] * 5 + [far] * 5,
-        out_specs=[vmem] * 5 + [smem],
-        out_shape=[shape(2 * rows), shape(rows), shape(2 * rows), shape(2 * rows),
-                   jax.ShapeDtypeStruct((heads, span), F32), jax.ShapeDtypeStruct((16,), jnp.int32)],
-        scratch_shapes=[pltpu.SMEM((2,), jnp.int32)] * 2 + [pltpu.VMEM((width, width), BF16)] * 3 + [pltpu.SemaphoreType.DMA((5,))],
-        name="prepare", compiler_params=pltpu.CompilerParams(vmem_limit_bytes=60 << 20),
-    )(ids, mine, other, gain, bias, buckets, pads, prefixes, wq, wk, wv)
+        in_specs=[vmem] * 3 + [free] * 4,
+        out_specs=[vmem] * 8,
+        out_shape=[shape(2 * rows), shape(rows), shape(2 * rows), shape(2 * rows)] + [shape(width)] * 4,
+        scratch_shapes=[pltpu.SemaphoreType.DMA((4,))],
+        name="prepare", compiler_params=pltpu.CompilerParams(vmem_limit_bytes=14 << 20),
+    )(mine, other, gain, wq, wk, wv, wo)
 
 def back_pieces(to, active, low, mine):
     @pl.loop(0, active.shape[1] // 512)
@@ -109,9 +87,9 @@
         for b in range(4):
             to[(4 * group + b) ^ mine] = made[:, b * 128 : (b + 1) * 128]
 
-def front_kernel(info, far, far_other, near, q_l, k_l, v_l, lines, wq, wk, wv, gain1, gain2, gain3, cots, wo_h, win_h, wback_h,
-                 hid_o, q_o, k_o, v_o, expo_o, inv_o, att_o, send_o, active_o, slopes_o, turned_o, mixed_o, steep_o, rows,
-                 hid, qs, ks, vs, inv, att, send, active, slopes, turned, mixed, steep, wo, win, wback, expo, scores, skewed, edges, sems):
+def front_kernel(ids, pads, prefixes, far, far_other, near, q_l, k_l, v_l, bias, buckets, wq, wk, wv, gain1, gain2, gain3, cots, wo_h, win_h, wback_h,
+                 hid_o, q_o, k_o, v_o, expo_o, inv_o, att_o, send_o, active_o, slopes_o, turned_o, mixed_o, steep_o, rows, info,
+                 hid, qs, ks, vs, inv, att, send, active, slopes, turned, mixed, steep, wo, win, wback, expo, scores, skewed, edges, lines, sems):
     count, width = near.shape
     hidden = win.shape[1]
     step = pl.program_id(0)
@@ -125,6 +103,22 @@
     def _():
         for copy in late:
             copy.start()
+        doc = ids[6]
+        info[0] = 4 * count - jnp.where(doc == 0, pads[0], pads[1])
+        info[5] = jnp.where(doc == 0, prefixes[0], prefixes[1])
+        for to, at in enumerate((0, 1, 2, 3)):
+            info[1 + to] = ids[at]
+        for to, at in enumerate((4, 5, 6)):
+            info[6 + to] = ids[at]
+        picker = jnp.where(lax.broadcasted_iota(jnp.int32, (BUCKETS, 1), 0) == buckets[...], 1.0, 0.0).astype(BF16)
+        left, total = bias[...], None
+        for _ in range(3):
+            part = left.astype(BF16)
+            left = left - part.astype(F32)
+            made = dot(part, picker)
+            total = made if total is None else total + made
+        lines[...] = jnp.zeros_like(lines)
+        lines[:, : buckets.shape[1]] = total
         for part, raw in enumerate((far, far_other)):
             tokens = raw[...].astype(F32)
             hid[part * count : (part + 1) * count, :] = (tokens * rms_scale(tokens) * gain1[...]).astype(BF16)
@@ -229,10 +223,10 @@
             copy.wait()
         kept(step).wait()
 
-def front(info, far, far_other, near, q_l, k_l, v_l, lines, wq, wk, wv, gain1, gain2, gain3, cots, wo, win, wback):
+def front(ids, pads, prefixes, far, far_other, near, q_l, k_l, v_l, bias, buckets, wq, wk, wv, gain1, gain2, gain3, cots, wo, win, wback):
     count, width = near.shape
     hidden = win.shape[1]
-    heads, span = lines.shape
+    heads, span = bias.shape[0], buckets.shape[1] + 1
     shape = jax.ShapeDtypeStruct
     smem, free = pl.BlockSpec(memory_space=pltpu.SMEM), pl.BlockSpec(memory_space=pl.ANY)
     whole = lambda *dims: pl.BlockSpec(dims, lambda g: (0,) * len(dims))
@@ -244,17 +238,18 @@
     return pl.pallas_call(
         front_kernel,
         grid=(heads // 2,),
-        in_specs=[smem, whole(count, width), whole(count, width), whole(count, width), col(count), col(2 * count), col(2 * count),
-                  whole(heads, span)] + [whole(width, width)] * 3 + [whole(1, width)] * 3
+        in_specs=[smem] * 3 + [whole(count, width)] * 3 + [col(count), col(2 * count), col(2 * count),
+                  whole(*bias.shape), whole(*buckets.shape)] + [whole(width, width)] * 3 + [whole(1, width)] * 3
                  + [whole(2, width)] + [pl.BlockSpec(memory_space=pltpu.HBM)] * 3,
-        out_specs=[free] * 13 + [whole(8, width)],
-        out_shape=outs + [shape((8, width), F32)],
+        out_specs=[free] * 13 + [whole(8, width), smem],
+        out_shape=outs + [shape((8, width), F32), shape((16,), jnp.int32)],
         scratch_shapes=[pltpu.VMEM(o.shape, o.dtype) for o in outs[:4] + outs[5:]]
                        + [pltpu.VMEM(wo.shape, BF16), pltpu.VMEM(win.shape, BF16), pltpu.VMEM(wback.shape, BF16),
                           pltpu.VMEM((2, 2 * count, 4 * count), BF16), pltpu.VMEM((2, 2 * count, 4 * count), F32),
-                          pltpu.VMEM((2, 128, span), F32), pltpu.VMEM((2, 4 * count, 128), BF16), pltpu.SemaphoreType.DMA((16,))],
-        name="front", compiler_params=pltpu.CompilerParams(vmem_limit_bytes=36 << 20),
-    )(info, far, far_other, near, q_l, k_l, v_l, lines, wq, wk, wv, gain1, gain2, gain3, cots, wo, win, wback)
+                          pltpu.VMEM((2, 128, span), F32), pltpu.VMEM((2, 4 * count, 128), BF16), pltpu.VMEM((heads, span), F32),
+                          pltpu.SemaphoreType.DMA((16,))],
+        name="front", compiler_params=pltpu.CompilerParams(vmem_limit_bytes=34 << 20),
+    )(ids, pads, prefixes, far, far_other, near, q_l, k_l, v_l, bias, buckets, wq, wk, wv, gain1, gain2, gain3, cots, wo, win, wback)
 
 def through_kernel(info, slopes_h, win_h, mixed_h, steep_h, wo_h, att_h, gain2, grad_mixed_o, grad_attended_o, grad_out_o, rows,
                    slopes, win, mixed, steep, wo, att, grad_mixed, grad_attended, grad_out, sems):
@@ -646,11 +641,12 @@
         ids = jnp.where(slot == i, value, ids)
     gain1, gain2, gain3 = norm1_gain[None, :], norm2_gain[None, :], final_gain[None, :]
     buckets = bucket_table[None, :]
-    hid_l, q_l, k_l, v_l, lines, info = prepare(ids, pad_len, prefix_len, near, near_other, w_query, w_key, w_value, gain1, bias_table.T, buckets)
-    far, info = wait(far, info)
+    hid_l, q_l, k_l, v_l, w_query, w_key, w_value, w_out = prepare(near, near_other, gain1, w_query, w_key, w_value, w_out)
+    far, q_l, ids = wait(far, q_l, ids)
     far_other = exchange(far, CORE)
-    (hid_r, q_r, k_r, v_r, expo, inverse, attended, send, active, slopes, turned, mixed, steep, dense_rows) = front(
-        info, far, far_other, near, q_l, k_l, v_l, lines, w_query, w_key, w_value, gain1, gain2, gain3, pooled_grad, w_out, w_in, w_back)
+    (hid_r, q_r, k_r, v_r, expo, inverse, attended, send, active, slopes, turned, mixed, steep, dense_rows, info) = front(
+        ids, pad_len, prefix_len, far, far_other, near, q_l, k_l, v_l, bias_table.T, buckets, w_query, w_key, w_value,
+        gain1, gain2, gain3, pooled_grad, w_out, w_in, w_back)
 
     xy = [ROW, NEAR_X, ROW ^ NEAR_X]
     zz = [line[0], line[1], line[0] ^ line[1]]

time: 157 us -> 151 us (0.962)
  Pallas kernels: 68.6 us -> 66.5 us
    pallas_call x2, Pallas kernels: 27.4 us -> 25.8 us  [the longest x1 24.2 us: front(): pl.pallas_call(front_kernel, grid=(heads // 2,), in_specs=[smem] * 3 + [w...]
    unnamed x54 -> x34, local copies, waits for them, and re-layouts: 7.66 us -> 6.48 us
  transfers between devices with their start and end apart: 37 -> 37, of which waited for: 11 -> 11; matrix products, arithmetic and copies ran while one was open for 3% -> 2% of each run, Pallas kernels for 26% -> 25%
where the time goes in v6:
time: 151 us
  Pallas kernels  66.5 us (44%)
  starting transfers between devices  40.1 us (27%)
  waiting for transfers between devices  31 us (21%)
  local copies, waits for them, and re-layouts  8 us (5%)
  other arithmetic  3.72 us (2%)
    ppermute x37, starting transfers between devices, exchange(): lax.ppermute(value, ('dp', 'blk'), [(i, i ^ bits) for i in range(size)])  40.1 us
    ppermute x37, waiting for transfers between devices, exchange(): lax.ppermute(value, ('dp', 'blk'), [(i, i ^ bits) for i in range(size)])  31 us
    pallas_call x1, Pallas kernels, front(): pl.pallas_call(front_kernel, grid=(heads // 2,), in_specs=[smem] * 3 + [w...  24.2 us
    pallas_call x1, Pallas kernels, back(): pl.pallas_call(back_kernel, grid=(width // 128,), in_specs=[smem, col(cou...  20 us
    pallas_call x3, Pallas kernels, place(): pl.pallas_call(functools.partial(place_kernel, [first for first, _ in par...  6.59 us
    unnamed x34, local copies, waits for them, and re-layouts  6.48 us
    pallas_call x1, Pallas kernels, through(): pl.pallas_call(through_kernel, in_specs=[smem, free, pl.BlockSpec(memory_...  4.85 us
    pallas_call x2, Pallas kernels, sort(): pl.pallas_call(functools.partial(sort_kernel, [first for first, _ in part...  4.23 us
  transfers between devices with their start and end apart: 37, of which 11 were waited for; matrix products, arithmetic and copies ran while one was open for 2% of the time, Pallas kernels for 25%

profile of v6, /device:TPU:0, one launch (start us, length us, event | category | flops | bytes accessed | tf_op | source)
XLA Modules:
  0.0 150.7 jit_solution(5834037879966001563)
XLA Ops:
  2.4 2.6 %collective-permute-start = (bf16[256,512]{1,0:T(8,128)(2,1)S(1)}, bf16[256,512]{1,0:T(8,128)(2,1)S(1)}, u32[]{:S(2)}, u32[]{:S(2)}) collective-permute-start(bf16[256,512]{1,0:T(8,128)(2,1)S(1)} %get-tuple-element.178), channel_id=1, source_target_pairs={{0,2},{1,3},{2,0},{3,1},{4,6},{5,7},{6,4},{7,5},{8,10},{9,11},{10,... | collective-permute-start | bytes 786440 | tf_op jit(solution)/shard_map/ppermute | solution.py:614
  9.9 1.6 %prepare.1 = (bf16[512,512]{1,0:T(8,128)(2,1)S(1)}, bf16[256,512]{1,0:T(8,128)(2,1)S(1)}, bf16[512,512]{1,0:T(8,128)(2,1)S(1)}, bf16[512,512]{1,0:T(8,128)(2,1)S...) custom-call(bf16[256,512]{1,0:T(8,128)(2,1)S(1)} %get-tuple-element., ...), custom_call_target="tpu_custom_call" | custom-call | tf_op jit(solution)/shard_map/prepare/pallas_call | solution.py:66
  11.9 1.5 %collective-permute-done.2.far_other.far_other_h = bf16[256,512]{1,0:T(8,128)(2,1)S(1)} collective-permute-done((bf16[256,512]{1,0:T(8,128)(2,1)S(1)}, bf16[256,512]{1,0:T(8,128)(2,1)S(1)}, u32[]{:S(2)}, u32[]{:S(2)}) %collective-permute-start.2) | collective-permute-done | bytes 262176 | tf_op jit(solution)/shard_map/ppermute | solution.py:614
  13.5 1.6 %copy-done.1 = bf16[2048,512]{1,0:T(8,128)(2,1)S(1)} copy-done((bf16[2048,512]{1,0:T(8,128)(2,1)S(1)}, bf16[2048,512]{1,0:T(8,128)(2,1)}, u32[]{:S(2)}) %copy-start.1) | copy-done | bytes 2097176
  15.1 24.2 %front.1 = (bf16[512,512]{1,0:T(8,128)(2,1)S(1)}, bf16[256,512]{1,0:T(8,128)(2,1)S(1)}, bf16[512,512]{1,0:T(8,128)(2,1)S(1)}, bf16[512,512]{1,0:T(8,128)(2,1)S(1...) custom-call(s32[8]{0:T(128)S(1)} %compare_select_fusion.6.ids, ...), custom_call_target="tpu_custom_call" | custom-call | tf_op jit(solution)/shard_map/front/pallas_call | solution.py:238
  39.6 4.9 %through.1 = (f32[512,512]{1,0:T(8,128)S(1)}, bf16[512,512]{1,0:T(8,128)(2,1)S(1)}, bf16[512,512]{1,0:T(8,128)(2,1)S(1)}, f32[8,512]{1,0:T(8,128)S(1)}) custom-call(s32[16]{0:T(128)S(1)} %get-tuple-element.328.info, bf16[512,2048]{1,0:T(8,128)(2,1)S(1)} %get-tuple-element.193.slopes_h, bf16[512,2048]{1,0:T(8,128)(2,1)S(1)} %copy-done, ...), custom_call_target="tpu_custom_call" | custom-call | tf_op jit(solution)/shard_map/through/pallas_call | solution.py:297
  44.4 3.6 %meet.1 = (bf16[4,512,128]{2,1,0:T(8,128)(2,1)S(1)}, bf16[4,512,128]{2,1,0:T(8,128)(2,1)S(1)}, bf16[4,512,128]{2,1,0:T(8,128)(2,1)S(1)}, bf16[4,512,128]{2,1,0:T(8,128)(2,1)S(1)}) custom-call(s32[16]{0:T(128)S(1)} %get-tuple-element.328.info, bf16[16,512,128]{2,1,0:T(8,128)(2,1)S(1)} %collective-permute-done.3.got_h, ...), custom_call_target="tpu_custom_call" | custom-call | tf_op jit(solution)/shard_map/meet/pallas_call | solution.py:347
  48.1 1.8 %collective-permute-start.4 = (bf16[4,512,128]{2,1,0:T(8,128)(2,1)S(1)}, bf16[4,512,128]{2,1,0:T(8,128)(2,1)S(1)}, u32[]{:S(2)}, u32[]{:S(2)}) collective-permute-start(bf16[4,512,128]{2,1,0:T(8,128)(2,1)S(1)} %get-tuple-element.221), channel_id=1, source_target_pairs={{0,2},{1,3},{2,0},{3,1},{4,6},{5,7},{6,4},{7,5},{8,10},{9,11},{10,... | collective-permute-start | bytes 1572872 | tf_op jit(solution)/shard_map/ppermute | solution.py:614
  51.6 20.0 %back.1 = (bf16[16,64,512]{2,1,0:T(8,128)(2,1)S(1)}, bf16[1040,512]{1,0:T(8,128)(2,1)}, f32[512,512]{1,0:T(8,128)}, bf16[528,512]{1,0:T(8,128)(2,1)S(1)}, f32[8,512]{1,0:T(8,128)S(1)}) custom-call(s32[16]{0:T(128)S(1)} %get-tuple-element.328.info, bf16[256,512]{1,0:T(8,128)(2,1)S(1)} %get-tuple-element.183.q_l.ql, ...), custom_call_target="tpu_custom_call" | custom-call | tf_op jit(solution)/shard_map/back/pallas_call | solution.py:490
  71.7 3.0 %collective-permute-done.6.refs_3_ = bf16[4,512,128]{2,1,0:T(8,128)(2,1)S(1)} collective-permute-done((bf16[4,512,128]{2,1,0:T(8,128)(2,1)S(1)}, bf16[4,512,128]{2,1,0:T(8,128)(2,1)S(1)}, u32[]{:S(2)}, u32[]{:S(2)}) %collective-permute-start.6) | collective-permute-done | bytes 524320 | tf_op jit(solution)/shard_map/ppermute | solution.py:614
  75.4 1.8 %collective-permute-start.9 = (bf16[512,128]{1,0:T(8,128)(2,1)S(1)}, bf16[512,128]{1,0:T(8,128)(2,1)S(1)}, u32[]{:S(2)}, u32[]{:S(2)}) collective-permute-start(bf16[512,128]{1,0:T(8,128)(2,1)S(1)} %get-tuple-element.241), channel_id=1, source_target_pairs={{0,8},{1,9},{2,10},{3,11},{4,12},{5,13},{6,14},{7,15},{8,0},{9,1},... | collective-permute-start | bytes 393224 | tf_op jit(solution)/shard_map/ppermute | solution.py:614
  77.2 2.6 %collective-permute-start.10 = (bf16[512,128]{1,0:T(8,128)(2,1)S(1)}, bf16[512,128]{1,0:T(8,128)(2,1)S(1)}, u32[]{:S(2)}, u32[]{:S(2)}) collective-permute-start(bf16[512,128]{1,0:T(8,128)(2,1)S(1)} %get-tuple-element.242), channel_id=1, source_target_pairs={{0,16},{1,17},{2,18},{3,19},{4,20},{5,21},{6,22},{7,23},{8,24},{9,... | collective-permute-start | bytes 393224 | tf_op jit(solution)/shard_map/ppermute | solution.py:614
  80.3 1.7 %collective-permute-start.12 = (bf16[272,512]{1,0:T(8,128)(2,1)S(1)}, bf16[272,512]{1,0:T(8,128)(2,1)S(1)}, u32[]{:S(2)}, u32[]{:S(2)}) collective-permute-start(bf16[272,512]{1,0:T(8,128)(2,1)S(1)} %get-tuple-element.254), channel_id=1, source_target_pairs={{0,2},{1,3},{2,0},{3,1},{4,6},{5,7},{6,4},{7,5},{8,10},{9,11},{10,... | collective-permute-start | bytes 835592 | tf_op jit(solution)/shard_map/ppermute | solution.py:614
  82.0 1.5 collective-permute-start.13
  83.5 1.7 %collective-permute-start.14 = (bf16[272,512]{1,0:T(8,128)(2,1)S(1)}, bf16[272,512]{1,0:T(8,128)(2,1)S(1)}, u32[]{:S(2)}, u32[]{:S(2)}) collective-permute-start(bf16[272,512]{1,0:T(8,128)(2,1)S(1)} %get-tuple-element.256), channel_id=1, source_target_pairs={{0,6},{1,7},{2,4},{3,5},{4,2},{5,3},{6,0},{7,1},{8,14},{9,15},{10,... | collective-permute-start | bytes 835592 | tf_op jit(solution)/shard_map/ppermute | solution.py:614
  86.4 3.7 %collective-permute-done.10 = bf16[512,128]{1,0:T(8,128)(2,1)S(1)} collective-permute-done((bf16[512,128]{1,0:T(8,128)(2,1)S(1)}, bf16[512,128]{1,0:T(8,128)(2,1)S(1)}, u32[]{:S(2)}, u32[]{:S(2)}) %collective-permute-start.10) | collective-permute-done | bytes 131104 | tf_op jit(solution)/shard_map/ppermute | solution.py:614
  90.2 2.4 %collective-permute-start.18 = (bf16[512,128]{1,0:T(8,128)(2,1)S(1)}, bf16[512,128]{1,0:T(8,128)(2,1)S(1)}, u32[]{:S(2)}, u32[]{:S(2)}) collective-permute-start(bf16[512,128]{1,0:T(8,128)(2,1)S(1)} %add_convert_fusion), channel_id=1, source_target_pairs={{0,24},{1,25},{2,26},{3,27},{4,28},{5,29},{6,30},{7,31},{8,16},{9,... | collective-permute-start | bytes 393224 | tf_op jit(solution)/shard_map/ppermute | solution.py:614
  94.7 1.5 %collective-permute-start.19 = (bf16[272,512]{1,0:T(8,128)(2,1)S(1)}, bf16[272,512]{1,0:T(8,128)(2,1)S(1)}, u32[]{:S(2)}, u32[]{:S(2)}) collective-permute-start(bf16[272,512]{1,0:T(8,128)(2,1)S(1)} %get-tuple-element.266), channel_id=1, source_target_pairs={{0,2},{1,3},{2,0},{3,1},{4,6},{5,7},{6,4},{7,5},{8,10},{9,11},{10,... | collective-permute-start | bytes 835592 | tf_op jit(solution)/shard_map/ppermute | solution.py:614
  97.8 7.2 %collective-permute-done.15 = bf16[144,512]{1,0:T(8,128)(2,1)S(1)} collective-permute-done((bf16[144,512]{1,0:T(8,128)(2,1)S(1)}, bf16[144,512]{1,0:T(8,128)(2,1)S(1)}, u32[]{:S(2)}, u32[]{:S(2)}) %collective-permute-start.15) | collective-permute-done | bytes 147488 | tf_op jit(solution)/shard_map/ppermute | solution.py:614
  105.2 1.6 %collective-permute-start.22 = (bf16[4,512,128]{2,1,0:T(8,128)(2,1)S(1)}, bf16[4,512,128]{2,1,0:T(8,128)(2,1)S(1)}, u32[]{:S(2)}, u32[]{:S(2)}) collective-permute-start(bf16[4,512,128]{2,1,0:T(8,128)(2,1)S(1)} %pad_maximum_fusion.2.refs_0_), channel_id=1, source_target_pairs={{0,4},{1,5},{2,6},{3,7},{4,0},{5,1},{6,2},{7,3},{8,12},{9,13},{10,... | collective-permute-start | bytes 1572872 | tf_op jit(solution)/shard_map/ppermute | solution.py:614
  106.8 1.5 %collective-permute-start.21 = (bf16[4,512,128]{2,1,0:T(8,128)(2,1)S(1)}, bf16[4,512,128]{2,1,0:T(8,128)(2,1)S(1)}, u32[]{:S(2)}, u32[]{:S(2)}) collective-permute-start(bf16[4,512,128]{2,1,0:T(8,128)(2,1)S(1)} %pad_maximum_fusion.2.refs_0_), channel_id=1, source_target_pairs={{0,2},{1,3},{2,0},{3,1},{4,6},{5,7},{6,4},{7,5},{8,10},{9,11},{10,... | collective-permute-start | bytes 1572872 | tf_op jit(solution)/shard_map/ppermute | solution.py:614
  111.2 5.4 %collective-permute-done.20 = bf16[80,512]{1,0:T(8,128)(2,1)S(1)} collective-permute-done((bf16[80,512]{1,0:T(8,128)(2,1)S(1)}, bf16[80,512]{1,0:T(8,128)(2,1)S(1)}, u32[]{:S(2)}, u32[]{:S(2)}) %collective-permute-start.20) | collective-permute-done | bytes 81952 | tf_op jit(solution)/shard_map/ppermute | solution.py:614
  117.6 3.4 %collective-permute-start.23 = (bf16[64,512]{1,0:T(8,128)(2,1)S(1)}, bf16[64,512]{1,0:T(8,128)(2,1)S(1)}, u32[]{:S(2)}, u32[]{:S(2)}) collective-permute-start(bf16[64,512]{1,0:T(8,128)(2,1)S(1)} %add_convert_fusion.1), channel_id=1, source_target_pairs={{0,8},{1,9},{2,10},{3,11},{4,12},{5,13},{6,14},{7,15},{8,0},{9,1},... | collective-permute-start | bytes 196616 | tf_op jit(solution)/shard_map/ppermute | solution.py:614
  125.4 1.5 %collective-permute-start.27 = (bf16[2,512,128]{2,1,0:T(8,128)(2,1)S(1)}, bf16[2,512,128]{2,1,0:T(8,128)(2,1)S(1)}, u32[]{:S(2)}, u32[]{:S(2)}) collective-permute-start(bf16[2,512,128]{2,1,0:T(8,128)(2,1)S(1)} %slice.233), channel_id=1, source_target_pairs={{0,2},{1,3},{2,0},{3,1},{4,6},{5,7},{6,4},{7,5},{8,10},{9,11},{10,... | collective-permute-start | bytes 786440 | tf_op jit(solution)/shard_map/ppermute | solution.py:614
  126.9 1.5 collective-permute-start.28
  128.4 2.3 %place.3 = (f32[2048,512]{1,0:T(8,128)}, f32[512,2048]{1,0:T(8,128)}) custom-call(s32[16]{0:T(128)S(1)} %get-tuple-element.328.info, bf16[4,512,128]{2,1,0:T(8,128)(2,1)S(1)} %pad_maximum_fusion.2.refs_0_, bf16[4,512,128]{2,1,0:T(8,128)(2,1)S(1)} %collective-permute-done.21.refs_1_, bf16[4,512,128]{2,1,0:T(8,128)(2,1)S(1)} %collective-permute-done.22.refs_2_), custom_call_target="tpu_custom_call" | custom-call | tf_op jit(solution)/shard_map/place/pallas_call | solution.py:557
  130.8 2.6 %collective-permute-done.30.refs_2_ = bf16[4,64,512]{2,1,0:T(8,128)(2,1)S(1)} collective-permute-done((bf16[4,64,512]{2,1,0:T(8,128)(2,1)S(1)}, bf16[4,64,512]{2,1,0:T(8,128)(2,1)S(1)}, u32[]{:S(2)}, u32[]{:S(2)}) %collective-permute-start.30) | collective-permute-done | bytes 262176 | tf_op jit(solution)/shard_map/ppermute | solution.py:614
  134.0 4.8 %collective-permute-done.27.refs_0_ = bf16[2,512,128]{2,1,0:T(8,128)(2,1)S(1)} collective-permute-done((bf16[2,512,128]{2,1,0:T(8,128)(2,1)S(1)}, bf16[2,512,128]{2,1,0:T(8,128)(2,1)S(1)}, u32[]{:S(2)}, u32[]{:S(2)}) %collective-permute-start.27) | collective-permute-done | bytes 262176 | tf_op jit(solution)/shard_map/ppermute | solution.py:614
  140.2 1.5 collective-permute-start.34
  141.7 1.9 %place.4 = (f32[2048,512]{1,0:T(8,128)}, f32[512,2048]{1,0:T(8,128)}) custom-call(s32[16]{0:T(128)S(1)} %get-tuple-element.328.info, bf16[2,512,128]{2,1,0:T(8,128)(2,1)S(1)} %collective-permute-done.27.refs_0_, bf16[2,512,128]{2,1,0:T(8,128)(2,1)S(1)} %collective-permute-done.28.refs_1_, ...), custom_call_target="tpu_custom_call", output_to_operand_aliasing={{0}: (4, {}), {1}: (5, {})} | custom-call | tf_op jit(solution)/shard_map/place/pallas_call | solution.py:557
  143.7 2.3 %place.5 = (f32[2048,512]{1,0:T(8,128)}, f32[512,2048]{1,0:T(8,128)}) custom-call(s32[16]{0:T(128)S(1)} %get-tuple-element.328.info, bf16[8,512,128]{2,1,0:T(8,128)(2,1)S(1)} %collective-permute-done.31.refs_0_, bf16[4,512,128]{2,1,0:T(8,128)(2,1)S(1)} %collective-permute-done.32.refs_1_, ...), custom_call_target="tpu_custom_call", output_to_operand_aliasing={{0}: (3, {}), {1}: (4, {})} | custom-call | tf_op jit(solution)/shard_map/place/pallas_call | solution.py:557
  146.3 2.8 %sort.2 = (f32[512,512]{1,0:T(8,128)}, f32[512,512]{1,0:T(8,128)}, f32[512,512]{1,0:T(8,128)}, f32[512,512]{1,0:T(8,128)}) custom-call(s32[16]{0:T(128)S(1)} %get-tuple-element.328.info, bf16[4,64,512]{2,1,0:T(8,128)(2,1)S(1)} %pad_maximum_fusion.10.refs_0_, bf16[4,64,512]{2,1,0:T(8,128)(2,1)S(1)} %collective-permute-done.29.refs_1_, ...), custom_call_target="tpu_custom_call" | custom-call | tf_op jit(solution)/shard_map/sort/pallas_call | solution.py:591
  (126 shorter events, 27.0 us)
Async XLA Ops:
  2.4 9.5 %collective-permute-start = (bf16[256,512]{1,0:T(8,128)(2,1)S(1)}, bf16[256,512]{1,0:T(8,128)(2,1)S(1)}, u32[]{:S(2)}, u32[]{:S(2)}) collective-permute-start(bf16[256,512]{1,0:T(8,128)(2,1)S(1)} %get-tuple-element.178), channel_id=1, source_target_pairs={{0,2},{1,3},{2,0},{3,1},{4,6},{5,7},{6,4},{7,5},{8,10},{9,11},{10,... | collective-permute-start | bytes 786440 | tf_op jit(solution)/shard_map/ppermute | solution.py:614
  39.3 5.1 %collective-permute-start.3 = (bf16[16,512,128]{2,1,0:T(8,128)(2,1)}, bf16[16,512,128]{2,1,0:T(8,128)(2,1)S(1)}, u32[]{:S(2)}, u32[]{:S(2)}) collective-permute-start(bf16[16,512,128]{2,1,0:T(8,128)(2,1)} %get-tuple-element.198), channel_id=1, source_target_pairs={{0,1},{1,0},{2,3},{3,2},{4,5},{5,4},{6,7},{7,6},{8,9},{9,8},{10,11... | collective-permute-start | bytes 6291464 | tf_op jit(solution)/shard_map/ppermute | solution.py:614
  48.1 23.6 %collective-permute-start.4 = (bf16[4,512,128]{2,1,0:T(8,128)(2,1)S(1)}, bf16[4,512,128]{2,1,0:T(8,128)(2,1)S(1)}, u32[]{:S(2)}, u32[]{:S(2)}) collective-permute-start(bf16[4,512,128]{2,1,0:T(8,128)(2,1)S(1)} %get-tuple-element.221), channel_id=1, source_target_pairs={{0,2},{1,3},{2,0},{3,1},{4,6},{5,7},{6,4},{7,5},{8,10},{9,11},{10,... | collective-permute-start | bytes 1572872 | tf_op jit(solution)/shard_map/ppermute | solution.py:614
  49.9 21.8 %collective-permute-start.5 = (bf16[4,512,128]{2,1,0:T(8,128)(2,1)S(1)}, bf16[4,512,128]{2,1,0:T(8,128)(2,1)S(1)}, u32[]{:S(2)}, u32[]{:S(2)}) collective-permute-start(bf16[4,512,128]{2,1,0:T(8,128)(2,1)S(1)} %get-tuple-element.222), channel_id=1, source_target_pairs={{0,4},{1,5},{2,6},{3,7},{4,0},{5,1},{6,2},{7,3},{8,12},{9,13},{10,... | collective-permute-start | bytes 1572872 | tf_op jit(solution)/shard_map/ppermute | solution.py:614
  51.4 23.3 %collective-permute-start.6 = (bf16[4,512,128]{2,1,0:T(8,128)(2,1)S(1)}, bf16[4,512,128]{2,1,0:T(8,128)(2,1)S(1)}, u32[]{:S(2)}, u32[]{:S(2)}) collective-permute-start(bf16[4,512,128]{2,1,0:T(8,128)(2,1)S(1)} %get-tuple-element.223), channel_id=1, source_target_pairs={{0,6},{1,7},{2,4},{3,5},{4,2},{5,3},{6,0},{7,1},{8,14},{9,15},{10,... | collective-permute-start | bytes 1572872 | tf_op jit(solution)/shard_map/ppermute | solution.py:614
  74.7 5.2 %collective-permute-start.7 = (bf16[1040,512]{1,0:T(8,128)(2,1)}, bf16[1040,512]{1,0:T(8,128)(2,1)S(1)}, u32[]{:S(2)}, u32[]{:S(2)}) collective-permute-start(bf16[1040,512]{1,0:T(8,128)(2,1)} %get-tuple-element.234), channel_id=1, source_target_pairs={{0,1},{1,0},{2,3},{3,2},{4,5},{5,4},{6,7},{7,6},{8,9},{9,8},{10,11... | collective-permute-start | bytes 3194888 | tf_op jit(solution)/shard_map/ppermute | solution.py:614
  74.7 5.2 %collective-permute-start.8 = (bf16[528,512]{1,0:T(8,128)(2,1)S(1)}, bf16[528,512]{1,0:T(8,128)(2,1)S(1)}, u32[]{:S(2)}, u32[]{:S(2)}) collective-permute-start(bf16[528,512]{1,0:T(8,128)(2,1)S(1)} %get-tuple-element.235), channel_id=1, source_target_pairs={{0,1},{1,0},{2,3},{3,2},{4,5},{5,4},{6,7},{7,6},{8,9},{9,8},{10,11... | collective-permute-start | bytes 1622024 | tf_op jit(solution)/shard_map/ppermute | solution.py:614
  75.4 8.1 %collective-permute-start.9 = (bf16[512,128]{1,0:T(8,128)(2,1)S(1)}, bf16[512,128]{1,0:T(8,128)(2,1)S(1)}, u32[]{:S(2)}, u32[]{:S(2)}) collective-permute-start(bf16[512,128]{1,0:T(8,128)(2,1)S(1)} %get-tuple-element.241), channel_id=1, source_target_pairs={{0,8},{1,9},{2,10},{3,11},{4,12},{5,13},{6,14},{7,15},{8,0},{9,1},... | collective-permute-start | bytes 393224 | tf_op jit(solution)/shard_map/ppermute | solution.py:614
  77.2 12.9 %collective-permute-start.10 = (bf16[512,128]{1,0:T(8,128)(2,1)S(1)}, bf16[512,128]{1,0:T(8,128)(2,1)S(1)}, u32[]{:S(2)}, u32[]{:S(2)}) collective-permute-start(bf16[512,128]{1,0:T(8,128)(2,1)S(1)} %get-tuple-element.242), channel_id=1, source_target_pairs={{0,16},{1,17},{2,18},{3,19},{4,20},{5,21},{6,22},{7,23},{8,24},{9,... | collective-permute-start | bytes 393224 | tf_op jit(solution)/shard_map/ppermute | solution.py:614
  79.8 10.3 %collective-permute-start.11 = (bf16[512,128]{1,0:T(8,128)(2,1)S(1)}, bf16[512,128]{1,0:T(8,128)(2,1)S(1)}, u32[]{:S(2)}, u32[]{:S(2)}) collective-permute-start(bf16[512,128]{1,0:T(8,128)(2,1)S(1)} %get-tuple-element.243), channel_id=1, source_target_pairs={{0,24},{1,25},{2,26},{3,27},{4,28},{5,29},{6,30},{7,31},{8,16},{9,... | collective-permute-start | bytes 393224 | tf_op jit(solution)/shard_map/ppermute | solution.py:614
  80.3 13.6 %collective-permute-start.12 = (bf16[272,512]{1,0:T(8,128)(2,1)S(1)}, bf16[272,512]{1,0:T(8,128)(2,1)S(1)}, u32[]{:S(2)}, u32[]{:S(2)}) collective-permute-start(bf16[272,512]{1,0:T(8,128)(2,1)S(1)} %get-tuple-element.254), channel_id=1, source_target_pairs={{0,2},{1,3},{2,0},{3,1},{4,6},{5,7},{6,4},{7,5},{8,10},{9,11},{10,... | collective-permute-start | bytes 835592 | tf_op jit(solution)/shard_map/ppermute | solution.py:614
  82.0 12.7 %collective-permute-start.13 = (bf16[272,512]{1,0:T(8,128)(2,1)S(1)}, bf16[272,512]{1,0:T(8,128)(2,1)S(1)}, u32[]{:S(2)}, u32[]{:S(2)}) collective-permute-start(bf16[272,512]{1,0:T(8,128)(2,1)S(1)} %get-tuple-element.255), channel_id=1, source_target_pairs={{0,4},{1,5},{2,6},{3,7},{4,0},{5,1},{6,2},{7,3},{8,12},{9,13},{10,... | collective-permute-start | bytes 835592 | tf_op jit(solution)/shard_map/ppermute | solution.py:614
  83.5 12.7 %collective-permute-start.14 = (bf16[272,512]{1,0:T(8,128)(2,1)S(1)}, bf16[272,512]{1,0:T(8,128)(2,1)S(1)}, u32[]{:S(2)}, u32[]{:S(2)}) collective-permute-start(bf16[272,512]{1,0:T(8,128)(2,1)S(1)} %get-tuple-element.256), channel_id=1, source_target_pairs={{0,6},{1,7},{2,4},{3,5},{4,2},{5,3},{6,0},{7,1},{8,14},{9,15},{10,... | collective-permute-start | bytes 835592 | tf_op jit(solution)/shard_map/ppermute | solution.py:614
  90.2 14.8 %collective-permute-start.18 = (bf16[512,128]{1,0:T(8,128)(2,1)S(1)}, bf16[512,128]{1,0:T(8,128)(2,1)S(1)}, u32[]{:S(2)}, u32[]{:S(2)}) collective-permute-start(bf16[512,128]{1,0:T(8,128)(2,1)S(1)} %add_convert_fusion), channel_id=1, source_target_pairs={{0,24},{1,25},{2,26},{3,27},{4,28},{5,29},{6,30},{7,31},{8,16},{9,... | collective-permute-start | bytes 393224 | tf_op jit(solution)/shard_map/ppermute | solution.py:614
  92.7 12.4 %collective-permute-start.17 = (bf16[512,128]{1,0:T(8,128)(2,1)S(1)}, bf16[512,128]{1,0:T(8,128)(2,1)S(1)}, u32[]{:S(2)}, u32[]{:S(2)}) collective-permute-start(bf16[512,128]{1,0:T(8,128)(2,1)S(1)} %add_convert_fusion), channel_id=1, source_target_pairs={{0,16},{1,17},{2,18},{3,19},{4,20},{5,21},{6,22},{7,23},{8,24},{9,... | collective-permute-start | bytes 393224 | tf_op jit(solution)/shard_map/ppermute | solution.py:614
  93.9 11.2 %collective-permute-start.16 = (bf16[512,128]{1,0:T(8,128)(2,1)S(1)}, bf16[512,128]{1,0:T(8,128)(2,1)S(1)}, u32[]{:S(2)}, u32[]{:S(2)}) collective-permute-start(bf16[512,128]{1,0:T(8,128)(2,1)S(1)} %add_convert_fusion), channel_id=1, source_target_pairs={{0,8},{1,9},{2,10},{3,11},{4,12},{5,13},{6,14},{7,15},{8,0},{9,1},... | collective-permute-start | bytes 393224 | tf_op jit(solution)/shard_map/ppermute | solution.py:614
  94.7 10.4 %collective-permute-start.19 = (bf16[272,512]{1,0:T(8,128)(2,1)S(1)}, bf16[272,512]{1,0:T(8,128)(2,1)S(1)}, u32[]{:S(2)}, u32[]{:S(2)}) collective-permute-start(bf16[272,512]{1,0:T(8,128)(2,1)S(1)} %get-tuple-element.266), channel_id=1, source_target_pairs={{0,2},{1,3},{2,0},{3,1},{4,6},{5,7},{6,4},{7,5},{8,10},{9,11},{10,... | collective-permute-start | bytes 835592 | tf_op jit(solution)/shard_map/ppermute | solution.py:614
  96.5 8.5 %collective-permute-start.15 = (bf16[144,512]{1,0:T(8,128)(2,1)S(1)}, bf16[144,512]{1,0:T(8,128)(2,1)S(1)}, u32[]{:S(2)}, u32[]{:S(2)}) collective-permute-start(bf16[144,512]{1,0:T(8,128)(2,1)S(1)} %pad_maximum_fusion.12), channel_id=1, source_target_pairs={{0,8},{1,9},{2,10},{3,11},{4,12},{5,13},{6,14},{7,15},{8,0},{9,1},... | collective-permute-start | bytes 442376 | tf_op jit(solution)/shard_map/ppermute | solution.py:614
  105.2 17.1 %collective-permute-start.22 = (bf16[4,512,128]{2,1,0:T(8,128)(2,1)S(1)}, bf16[4,512,128]{2,1,0:T(8,128)(2,1)S(1)}, u32[]{:S(2)}, u32[]{:S(2)}) collective-permute-start(bf16[4,512,128]{2,1,0:T(8,128)(2,1)S(1)} %pad_maximum_fusion.2.refs_0_), channel_id=1, source_target_pairs={{0,4},{1,5},{2,6},{3,7},{4,0},{5,1},{6,2},{7,3},{8,12},{9,13},{10,... | collective-permute-start | bytes 1572872 | tf_op jit(solution)/shard_map/ppermute | solution.py:614
  106.8 15.6 %collective-permute-start.21 = (bf16[4,512,128]{2,1,0:T(8,128)(2,1)S(1)}, bf16[4,512,128]{2,1,0:T(8,128)(2,1)S(1)}, u32[]{:S(2)}, u32[]{:S(2)}) collective-permute-start(bf16[4,512,128]{2,1,0:T(8,128)(2,1)S(1)} %pad_maximum_fusion.2.refs_0_), channel_id=1, source_target_pairs={{0,2},{1,3},{2,0},{3,1},{4,6},{5,7},{6,4},{7,5},{8,10},{9,11},{10,... | collective-permute-start | bytes 1572872 | tf_op jit(solution)/shard_map/ppermute | solution.py:614
  108.3 8.3 %collective-permute-start.20 = (bf16[80,512]{1,0:T(8,128)(2,1)S(1)}, bf16[80,512]{1,0:T(8,128)(2,1)S(1)}, u32[]{:S(2)}, u32[]{:S(2)}) collective-permute-start(bf16[80,512]{1,0:T(8,128)(2,1)S(1)} %pad_maximum_fusion.13), channel_id=1, source_target_pairs={{0,16},{1,17},{2,18},{3,19},{4,20},{5,21},{6,22},{7,23},{8,24},{9,... | collective-permute-start | bytes 245768 | tf_op jit(solution)/shard_map/ppermute | solution.py:614
  116.6 6.2 %collective-permute-start.25 = (bf16[64,512]{1,0:T(8,128)(2,1)S(1)}, bf16[64,512]{1,0:T(8,128)(2,1)S(1)}, u32[]{:S(2)}, u32[]{:S(2)}) collective-permute-start(bf16[64,512]{1,0:T(8,128)(2,1)S(1)} %add_convert_fusion.1), channel_id=1, source_target_pairs={{0,24},{1,25},{2,26},{3,27},{4,28},{5,29},{6,30},{7,31},{8,16},{9,... | collective-permute-start | bytes 196616 | tf_op jit(solution)/shard_map/ppermute | solution.py:614
  117.6 6.5 %collective-permute-start.24 = (bf16[64,512]{1,0:T(8,128)(2,1)S(1)}, bf16[64,512]{1,0:T(8,128)(2,1)S(1)}, u32[]{:S(2)}, u32[]{:S(2)}) collective-permute-start(bf16[64,512]{1,0:T(8,128)(2,1)S(1)} %add_convert_fusion.1), channel_id=1, source_target_pairs={{0,16},{1,17},{2,18},{3,19},{4,20},{5,21},{6,22},{7,23},{8,24},{9,... | collective-permute-start | bytes 196616 | tf_op jit(solution)/shard_map/ppermute | solution.py:614
  117.6 6.5 %collective-permute-start.23 = (bf16[64,512]{1,0:T(8,128)(2,1)S(1)}, bf16[64,512]{1,0:T(8,128)(2,1)S(1)}, u32[]{:S(2)}, u32[]{:S(2)}) collective-permute-start(bf16[64,512]{1,0:T(8,128)(2,1)S(1)} %add_convert_fusion.1), channel_id=1, source_target_pairs={{0,8},{1,9},{2,10},{3,11},{4,12},{5,13},{6,14},{7,15},{8,0},{9,1},... | collective-permute-start | bytes 196616 | tf_op jit(solution)/shard_map/ppermute | solution.py:614
  124.2 14.7 %collective-permute-start.26 = (bf16[4,512,128]{2,1,0:T(8,128)(2,1)S(1)}, bf16[4,512,128]{2,1,0:T(8,128)(2,1)S(1)}, u32[]{:S(2)}, u32[]{:S(2)}) collective-permute-start(bf16[4,512,128]{2,1,0:T(8,128)(2,1)S(1)} %pad_maximum_fusion.2.refs_0_), channel_id=1, source_target_pairs={{0,1},{1,0},{2,3},{3,2},{4,5},{5,4},{6,7},{7,6},{8,9},{9,8},{10,11... | collective-permute-start | bytes 1572872 | tf_op jit(solution)/shard_map/ppermute | solution.py:614
  124.3 9.2 %collective-permute-start.30 = (bf16[4,64,512]{2,1,0:T(8,128)(2,1)S(1)}, bf16[4,64,512]{2,1,0:T(8,128)(2,1)S(1)}, u32[]{:S(2)}, u32[]{:S(2)}) collective-permute-start(bf16[4,64,512]{2,1,0:T(8,128)(2,1)S(1)} %pad_maximum_fusion.10.refs_0_), channel_id=1, source_target_pairs={{0,4},{1,5},{2,6},{3,7},{4,0},{5,1},{6,2},{7,3},{8,12},{9,13},{10,... | collective-permute-start | bytes 786440 | tf_op jit(solution)/shard_map/ppermute | solution.py:614
  124.9 9.2 %collective-permute-start.29 = (bf16[4,64,512]{2,1,0:T(8,128)(2,1)S(1)}, bf16[4,64,512]{2,1,0:T(8,128)(2,1)S(1)}, u32[]{:S(2)}, u32[]{:S(2)}) collective-permute-start(bf16[4,64,512]{2,1,0:T(8,128)(2,1)S(1)} %pad_maximum_fusion.10.refs_0_), channel_id=1, source_target_pairs={{0,2},{1,3},{2,0},{3,1},{4,6},{5,7},{6,4},{7,5},{8,10},{9,11},{10,... | collective-permute-start | bytes 786440 | tf_op jit(solution)/shard_map/ppermute | solution.py:614
  125.4 13.5 %collective-permute-start.27 = (bf16[2,512,128]{2,1,0:T(8,128)(2,1)S(1)}, bf16[2,512,128]{2,1,0:T(8,128)(2,1)S(1)}, u32[]{:S(2)}, u32[]{:S(2)}) collective-permute-start(bf16[2,512,128]{2,1,0:T(8,128)(2,1)S(1)} %slice.233), channel_id=1, source_target_pairs={{0,2},{1,3},{2,0},{3,1},{4,6},{5,7},{6,4},{7,5},{8,10},{9,11},{10,... | collective-permute-start | bytes 786440 | tf_op jit(solution)/shard_map/ppermute | solution.py:614
  126.9 12.0 %collective-permute-start.28 = (bf16[2,512,128]{2,1,0:T(8,128)(2,1)S(1)}, bf16[2,512,128]{2,1,0:T(8,128)(2,1)S(1)}, u32[]{:S(2)}, u32[]{:S(2)}) collective-permute-start(bf16[2,512,128]{2,1,0:T(8,128)(2,1)S(1)} %slice.234), channel_id=1, source_target_pairs={{0,4},{1,5},{2,6},{3,7},{4,0},{5,1},{6,2},{7,3},{8,12},{9,13},{10,... | collective-permute-start | bytes 786440 | tf_op jit(solution)/shard_map/ppermute | solution.py:614
  139.1 6.9 %collective-permute-start.35 = (bf16[12,64,512]{2,1,0:T(8,128)(2,1)S(1)}, bf16[12,64,512]{2,1,0:T(8,128)(2,1)S(1)}, u32[]{:S(2)}, u32[]{:S(2)}) collective-permute-start(bf16[12,64,512]{2,1,0:T(8,128)(2,1)S(1)} %pad_maximum_fusion.1), channel_id=1, source_target_pairs={{0,1},{1,0},{2,3},{3,2},{4,5},{5,4},{6,7},{7,6},{8,9},{9,8},{10,11... | collective-permute-start | bytes 2359304 | tf_op jit(solution)/shard_map/ppermute | solution.py:614
  139.7 6.3 %collective-permute-start.33 = (bf16[2,64,512]{2,1,0:T(8,128)(2,1)S(1)}, bf16[2,64,512]{2,1,0:T(8,128)(2,1)S(1)}, u32[]{:S(2)}, u32[]{:S(2)}) collective-permute-start(bf16[2,64,512]{2,1,0:T(8,128)(2,1)S(1)} %slice.235), channel_id=1, source_target_pairs={{0,2},{1,3},{2,0},{3,1},{4,6},{5,7},{6,4},{7,5},{8,10},{9,11},{10,... | collective-permute-start | bytes 393224 | tf_op jit(solution)/shard_map/ppermute | solution.py:614
  140.2 5.8 %collective-permute-start.34 = (bf16[2,64,512]{2,1,0:T(8,128)(2,1)S(1)}, bf16[2,64,512]{2,1,0:T(8,128)(2,1)S(1)}, u32[]{:S(2)}, u32[]{:S(2)}) collective-permute-start(bf16[2,64,512]{2,1,0:T(8,128)(2,1)S(1)} %slice.236), channel_id=1, source_target_pairs={{0,4},{1,5},{2,6},{3,7},{4,0},{5,1},{6,2},{7,3},{8,12},{9,13},{10,... | collective-permute-start | bytes 393224 | tf_op jit(solution)/shard_map/ppermute | solution.py:614
  (22 other events, 74.7 us)

commit v7 on v5

--- a/solution.py
+++ b/solution.py
@@ -42,13 +42,43 @@
     count = sum(v.shape[0] for v in values)
     return jnp.concatenate(list(values) + [jnp.zeros((8 - count, values[0].shape[1]), F32)])
 
-def prepare_kernel(ids, mine, other, gain, bias, buckets, pads_h, prefixes_h, wq_h, wk_h, wv_h, hidden, query, keys, values, lines, info,
-                   pads, prefixes, wq, wk, wv, sems):
+def prepare_kernel(mine, other, gain, wq_h, wk_h, wv_h, hidden, query, keys, values, wq, wk, wv, sems):
     rows = mine.shape[0]
-    load = [pltpu.make_async_copy(a, b, sems.at[i]) for i, (a, b) in enumerate(
-        ((pads_h, pads), (prefixes_h, prefixes), (wk_h, wk), (wv_h, wv), (wq_h, wq)))]
+    load = [pltpu.make_async_copy(a, b, sems.at[i]) for i, (a, b) in enumerate(((wk_h, wk), (wv_h, wv), (wq_h, wq)))]
     for copy in load:
         copy.start()
+    for part, raw in enumerate((mine, other)):
+        tokens = raw[...].astype(F32)
+        hidden[part * rows : (part + 1) * rows, :] = (tokens * rms_scale(tokens) * gain[...]).astype(BF16)
+    h = hidden[...]
+    load[0].wait()
+    keys[...] = dot(h, wk[...]).astype(BF16)
+    load[1].wait()
+    values[...] = dot(h, wv[...]).astype(BF16)
+    load[2].wait()
+    query[...] = dot(h[:rows], wq[...]).astype(BF16)
+
+def prepare(mine, other, gain, wq, wk, wv):
+    rows, width = mine.shape
+    shape = lambda n: jax.ShapeDtypeStruct((n, width), BF16)
+    vmem, free = (pl.BlockSpec(memory_space=m) for m in (pltpu.VMEM, pl.ANY))
+    return pl.pallas_call(
+        prepare_kernel,
+        in_specs=[vmem] * 3 + [free] * 3,
+        out_specs=[vmem] * 7,
+        out_shape=[shape(2 * rows), shape(rows), shape(2 * rows), shape(2 * rows)] + [shape(width)] * 3,
+        scratch_shapes=[pltpu.SemaphoreType.DMA((3,))],
+        name="prepare", compiler_params=pltpu.CompilerParams(vmem_limit_bytes=14 << 20),
+    )(mine, other, gain, wq, wk, wv)
+
+def tables_kernel(ids, pads, prefixes, bias, buckets, lines, info, *, length):
+    doc = ids[6]
+    info[0] = length - jnp.where(doc == 0, pads[0], pads[1])
+    info[5] = jnp.where(doc == 0, prefixes[0], prefixes[1])
+    for to, at in enumerate((0, 1, 2, 3)):
+        info[1 + to] = ids[at]
+    for to, at in enumerate((4, 5, 6)):
+        info[6 + to] = ids[at]
     picker = jnp.where(lax.broadcasted_iota(jnp.int32, (BUCKETS, 1), 0) == buckets[...], 1.0, 0.0).astype(BF16)
     left, total = bias[...], None
     for _ in range(3):
@@ -58,41 +88,16 @@
         total = made if total is None else total + made
     lines[...] = jnp.zeros_like(lines)
     lines[:, : buckets.shape[1]] = total
-    for part, raw in enumerate((mine, other)):
-        tokens = raw[...].astype(F32)
-        hidden[part * rows : (part + 1) * rows, :] = (tokens * rms_scale(tokens) * gain[...]).astype(BF16)
-    h = hidden[...]
-    load[2].wait()
-    keys[...] = dot(h, wk[...]).astype(BF16)
-    load[3].wait()
-    values[...] = dot(h, wv[...]).astype(BF16)
-    load[4].wait()
-    query[...] = dot(h[:rows], wq[...]).astype(BF16)
-    load[0].wait()
-    load[1].wait()
-    doc = ids[6]
-    info[0] = 4 * rows - jnp.where(doc == 0, pads[0], pads[1])
-    info[5] = jnp.where(doc == 0, prefixes[0], prefixes[1])
-    for to, at in enumerate((0, 1, 2, 3)):
-        info[1 + to] = ids[at]
-    for to, at in enumerate((4, 5, 6)):
-        info[6 + to] = ids[at]
-
-def prepare(ids, pads, prefixes, mine, other, wq, wk, wv, gain, bias, buckets):
-    rows, width = mine.shape
-    span = buckets.shape[1] + 1
-    heads = bias.shape[0]
-    shape = lambda n: jax.ShapeDtypeStruct((n, width), BF16)
-    smem, vmem, far = (pl.BlockSpec(memory_space=m) for m in (pltpu.SMEM, pltpu.VMEM, pltpu.HBM))
-    return pl.pallas_call(
-        prepare_kernel,
-        in_specs=[smem] + [vmem] * 5 + [far] * 5,
-        out_specs=[vmem] * 5 + [smem],
-        out_shape=[shape(2 * rows), shape(rows), shape(2 * rows), shape(2 * rows),
-                   jax.ShapeDtypeStruct((heads, span), F32), jax.ShapeDtypeStruct((16,), jnp.int32)],
-        scratch_shapes=[pltpu.SMEM((2,), jnp.int32)] * 2 + [pltpu.VMEM((width, width), BF16)] * 3 + [pltpu.SemaphoreType.DMA((5,))],
-        name="prepare", compiler_params=pltpu.CompilerParams(vmem_limit_bytes=60 << 20),
-    )(ids, mine, other, gain, bias, buckets, pads, prefixes, wq, wk, wv)
+
+def tables(ids, pads, prefixes, bias, buckets, length):
+    smem, vmem = pl.BlockSpec(memory_space=pltpu.SMEM), pl.BlockSpec(memory_space=pltpu.VMEM)
+    return pl.pallas_call(
+        functools.partial(tables_kernel, length=length),
+        in_specs=[smem] * 3 + [vmem] * 2,
+        out_specs=[vmem, smem],
+        out_shape=[jax.ShapeDtypeStruct((bias.shape[0], buckets.shape[1] + 1), F32), jax.ShapeDtypeStruct((16,), jnp.int32)],
+        name="tables", compiler_params=pltpu.CompilerParams(vmem_limit_bytes=4 << 20),
+    )(ids, pads, prefixes, bias, buckets)
 
 def back_pieces(to, active, low, mine):
     @pl.loop(0, active.shape[1] // 512)
@@ -244,8 +249,7 @@
     return pl.pallas_call(
         front_kernel,
         grid=(heads // 2,),
-        in_specs=[smem, whole(count, width), whole(count, width), whole(count, width), col(count), col(2 * count), col(2 * count),
-                  whole(heads, span)] + [whole(width, width)] * 3 + [whole(1, width)] * 3
+        in_specs=[smem] + [whole(count, width)] * 3 + [col(count), col(2 * count), col(2 * count), whole(heads, span)] + [whole(width, width)] * 3 + [whole(1, width)] * 3
                  + [whole(2, width)] + [pl.BlockSpec(memory_space=pltpu.HBM)] * 3,
         out_specs=[free] * 13 + [whole(8, width)],
         out_shape=outs + [shape((8, width), F32)],
@@ -646,11 +650,13 @@
         ids = jnp.where(slot == i, value, ids)
     gain1, gain2, gain3 = norm1_gain[None, :], norm2_gain[None, :], final_gain[None, :]
     buckets = bucket_table[None, :]
-    hid_l, q_l, k_l, v_l, lines, info = prepare(ids, pad_len, prefix_len, near, near_other, w_query, w_key, w_value, gain1, bias_table.T, buckets)
-    far, info = wait(far, info)
+    hid_l, q_l, k_l, v_l, w_query, w_key, w_value = prepare(near, near_other, gain1, w_query, w_key, w_value)
+    far, q_l, ids = wait(far, q_l, ids)
     far_other = exchange(far, CORE)
+    lines, info = tables(ids, pad_len, prefix_len, bias_table.T, buckets, 4 * rows)
     (hid_r, q_r, k_r, v_r, expo, inverse, attended, send, active, slopes, turned, mixed, steep, dense_rows) = front(
-        info, far, far_other, near, q_l, k_l, v_l, lines, w_query, w_key, w_value, gain1, gain2, gain3, pooled_grad, w_out, w_in, w_back)
+        info, far, far_other, near, q_l, k_l, v_l, lines, w_query, w_key, w_value,
+        gain1, gain2, gain3, pooled_grad, w_out, w_in, w_back)
 
     xy = [ROW, NEAR_X, ROW ^ NEAR_X]
     zz = [line[0], line[1], line[0] ^ line[1]]

time: 157 us -> 148 us (0.943)
  local copies, waits for them, and re-layouts: 9.17 us -> 5.38 us
  Pallas kernels: 68.6 us -> 66 us
    unnamed x54 -> x32, local copies, waits for them, and re-layouts: 7.66 us -> 3.86 us
    pallas_call x2 -> x3, Pallas kernels: 27.4 us -> 25.1 us  [the longest x1 22.4 us: front(): pl.pallas_call(front_kernel, grid=(heads // 2,), in_specs=[smem] + [whole...]
  transfers between devices with their start and end apart: 37 -> 37, of which waited for: 11 -> 11; matrix products, arithmetic and copies ran while one was open for 3% -> 2% of each run, Pallas kernels for 26% -> 26%
where the time goes in v7:
time: 148 us
  Pallas kernels  66 us (45%)
  starting transfers between devices  40 us (27%)
  waiting for transfers between devices  31 us (21%)
  local copies, waits for them, and re-layouts  5.38 us (4%)
  other arithmetic  4.43 us (3%)
    ppermute x37, starting transfers between devices, exchange(): lax.ppermute(value, ('dp', 'blk'), [(i, i ^ bits) for i in range(size)])  40 us
    ppermute x37, waiting for transfers between devices, exchange(): lax.ppermute(value, ('dp', 'blk'), [(i, i ^ bits) for i in range(size)])  31 us
    pallas_call x1, Pallas kernels, front(): pl.pallas_call(front_kernel, grid=(heads // 2,), in_specs=[smem] + [whole...  22.4 us
    pallas_call x1, Pallas kernels, back(): pl.pallas_call(back_kernel, grid=(width // 128,), in_specs=[smem, col(cou...  20.1 us
    pallas_call x3, Pallas kernels, place(): pl.pallas_call(functools.partial(place_kernel, [first for first, _ in par...  6.59 us
    pallas_call x1, Pallas kernels, through(): pl.pallas_call(through_kernel, in_specs=[smem, free, pl.BlockSpec(memory_...  4.86 us
    pallas_call x2, Pallas kernels, sort(): pl.pallas_call(functools.partial(sort_kernel, [first for first, _ in part...  4.23 us
    unnamed x32, local copies, waits for them, and re-layouts  3.86 us
  transfers between devices with their start and end apart: 37, of which 11 were waited for; matrix products, arithmetic and copies ran while one was open for 2% of the time, Pallas kernels for 26%

profile of v7, /device:TPU:0, one launch (start us, length us, event | category | flops | bytes accessed | tf_op | source)
XLA Modules:
  0.0 148.2 jit_solution(3348862288873696764)
XLA Ops:
  0.7 1.9 %select_bitcast_fusion = (bf16[256,512]{1,0:T(8,128)(2,1)}, bf16[256,512]{1,0:T(8,128)(2,1)S(1)}) fusion(pred[]{:T(512)S(6)} %eq.31, bf16[2,256,512]{2,1,0:T(8,128)(2,1)} %param.15), kind=kLoop, calls=%fused_computation.27 | loop fusion | flops 262144 | bytes 1048577 | tf_op jit(solution)/shard_map/jit(_where)/select_n | solution.py:643
  3.1 2.5 %collective-permute-start = (bf16[256,512]{1,0:T(8,128)(2,1)}, bf16[256,512]{1,0:T(8,128)(2,1)S(1)}, u32[]{:S(2)}, u32[]{:S(2)}) collective-permute-start(bf16[256,512]{1,0:T(8,128)(2,1)} %get-tuple-element.178), channel_id=1, source_target_pairs={{0,2},{1,3},{2,0},{3,1},{4,6},{5,7},{6,4},{7,5},{8,10},{9,11},{10,... | collective-permute-start | bytes 786440 | tf_op jit(solution)/shard_map/ppermute | solution.py:623
  9.5 1.5 %prepare.1 = (bf16[512,512]{1,0:T(8,128)(2,1)S(1)}, bf16[256,512]{1,0:T(8,128)(2,1)S(1)}, bf16[512,512]{1,0:T(8,128)(2,1)S(1)}, bf16[512,512]{1,0:T(8,128)(2,1)S...) custom-call(bf16[256,512]{1,0:T(8,128)(2,1)S(1)} %get-tuple-element.179.mine.near.near, ...), custom_call_target="tpu_custom_call" | custom-call | tf_op jit(solution)/shard_map/prepare/pallas_call | solution.py:65
  11.0 1.8 %collective-permute-done.far.far_h = bf16[256,512]{1,0:T(8,128)(2,1)S(1)} collective-permute-done((bf16[256,512]{1,0:T(8,128)(2,1)}, bf16[256,512]{1,0:T(8,128)(2,1)S(1)}, u32[]{:S(2)}, u32[]{:S(2)}) %collective-permute-start) | collective-permute-done | bytes 262176 | tf_op jit(solution)/shard_map/ppermute | solution.py:623
  14.3 22.4 %front.1 = (bf16[512,512]{1,0:T(8,128)(2,1)S(1)}, bf16[256,512]{1,0:T(8,128)(2,1)S(1)}, bf16[512,512]{1,0:T(8,128)(2,1)S(1)}, bf16[512,512]{1,0:T(8,128)(2,1)S(1...) custom-call(s32[16]{0:T(128)S(1)} %get-tuple-element.328.info, ...), custom_call_target="tpu_custom_call" | custom-call | tf_op jit(solution)/shard_map/front/pallas_call | solution.py:249
  37.1 4.9 %through.1 = (f32[512,512]{1,0:T(8,128)S(1)}, bf16[512,512]{1,0:T(8,128)(2,1)S(1)}, bf16[512,512]{1,0:T(8,128)(2,1)S(1)}, f32[8,512]{1,0:T(8,128)S(1)}) custom-call(s32[16]{0:T(128)S(1)} %get-tuple-element.328.info, bf16[512,2048]{1,0:T(8,128)(2,1)S(1)} %get-tuple-element.193.slopes_h, bf16[512,2048]{1,0:T(8,128)(2,1)S(1)} %copy-done, ...), custom_call_target="tpu_custom_call" | custom-call | tf_op jit(solution)/shard_map/through/pallas_call | solution.py:306
  42.0 3.7 %meet.1 = (bf16[4,512,128]{2,1,0:T(8,128)(2,1)S(1)}, bf16[4,512,128]{2,1,0:T(8,128)(2,1)S(1)}, bf16[4,512,128]{2,1,0:T(8,128)(2,1)S(1)}, bf16[4,512,128]{2,1,0:T(8,128)(2,1)S(1)}) custom-call(s32[16]{0:T(128)S(1)} %get-tuple-element.328.info, bf16[16,512,128]{2,1,0:T(8,128)(2,1)S(1)} %collective-permute-done.3.got_h, ...), custom_call_target="tpu_custom_call" | custom-call | tf_op jit(solution)/shard_map/meet/pallas_call | solution.py:356
  45.7 1.8 %collective-permute-start.4 = (bf16[4,512,128]{2,1,0:T(8,128)(2,1)S(1)}, bf16[4,512,128]{2,1,0:T(8,128)(2,1)S(1)}, u32[]{:S(2)}, u32[]{:S(2)}) collective-permute-start(bf16[4,512,128]{2,1,0:T(8,128)(2,1)S(1)} %get-tuple-element.221), channel_id=1, source_target_pairs={{0,2},{1,3},{2,0},{3,1},{4,6},{5,7},{6,4},{7,5},{8,10},{9,11},{10,... | collective-permute-start | bytes 1572872 | tf_op jit(solution)/shard_map/ppermute | solution.py:623
  47.5 1.5 %collective-permute-start.5 = (bf16[4,512,128]{2,1,0:T(8,128)(2,1)S(1)}, bf16[4,512,128]{2,1,0:T(8,128)(2,1)S(1)}, u32[]{:S(2)}, u32[]{:S(2)}) collective-permute-start(bf16[4,512,128]{2,1,0:T(8,128)(2,1)S(1)} %get-tuple-element.222), channel_id=1, source_target_pairs={{0,4},{1,5},{2,6},{3,7},{4,0},{5,1},{6,2},{7,3},{8,12},{9,13},{10,... | collective-permute-start | bytes 1572872 | tf_op jit(solution)/shard_map/ppermute | solution.py:623
  49.2 20.1 %back.1 = (bf16[16,64,512]{2,1,0:T(8,128)(2,1)S(1)}, bf16[1040,512]{1,0:T(8,128)(2,1)}, f32[512,512]{1,0:T(8,128)}, bf16[528,512]{1,0:T(8,128)(2,1)S(1)}, f32[8,512]{1,0:T(8,128)S(1)}) custom-call(s32[16]{0:T(128)S(1)} %get-tuple-element.328.info, bf16[256,512]{1,0:T(8,128)(2,1)S(1)} %get-tuple-element.184.q_l.ql, ...), custom_call_target="tpu_custom_call" | custom-call | tf_op jit(solution)/shard_map/back/pallas_call | solution.py:499
  69.4 2.8 %collective-permute-done.6.refs_3_ = bf16[4,512,128]{2,1,0:T(8,128)(2,1)S(1)} collective-permute-done((bf16[4,512,128]{2,1,0:T(8,128)(2,1)S(1)}, bf16[4,512,128]{2,1,0:T(8,128)(2,1)S(1)}, u32[]{:S(2)}, u32[]{:S(2)}) %collective-permute-start.6) | collective-permute-done | bytes 524320 | tf_op jit(solution)/shard_map/ppermute | solution.py:623
  72.9 1.8 %collective-permute-start.9 = (bf16[512,128]{1,0:T(8,128)(2,1)S(1)}, bf16[512,128]{1,0:T(8,128)(2,1)S(1)}, u32[]{:S(2)}, u32[]{:S(2)}) collective-permute-start(bf16[512,128]{1,0:T(8,128)(2,1)S(1)} %get-tuple-element.241), channel_id=1, source_target_pairs={{0,8},{1,9},{2,10},{3,11},{4,12},{5,13},{6,14},{7,15},{8,0},{9,1},... | collective-permute-start | bytes 393224 | tf_op jit(solution)/shard_map/ppermute | solution.py:623
  74.7 2.6 %collective-permute-start.10 = (bf16[512,128]{1,0:T(8,128)(2,1)S(1)}, bf16[512,128]{1,0:T(8,128)(2,1)S(1)}, u32[]{:S(2)}, u32[]{:S(2)}) collective-permute-start(bf16[512,128]{1,0:T(8,128)(2,1)S(1)} %get-tuple-element.242), channel_id=1, source_target_pairs={{0,16},{1,17},{2,18},{3,19},{4,20},{5,21},{6,22},{7,23},{8,24},{9,... | collective-permute-start | bytes 393224 | tf_op jit(solution)/shard_map/ppermute | solution.py:623
  77.8 1.7 %collective-permute-start.12 = (bf16[272,512]{1,0:T(8,128)(2,1)S(1)}, bf16[272,512]{1,0:T(8,128)(2,1)S(1)}, u32[]{:S(2)}, u32[]{:S(2)}) collective-permute-start(bf16[272,512]{1,0:T(8,128)(2,1)S(1)} %get-tuple-element.254), channel_id=1, source_target_pairs={{0,2},{1,3},{2,0},{3,1},{4,6},{5,7},{6,4},{7,5},{8,10},{9,11},{10,... | collective-permute-start | bytes 835592 | tf_op jit(solution)/shard_map/ppermute | solution.py:623
  81.1 1.7 %collective-permute-start.14 = (bf16[272,512]{1,0:T(8,128)(2,1)S(1)}, bf16[272,512]{1,0:T(8,128)(2,1)S(1)}, u32[]{:S(2)}, u32[]{:S(2)}) collective-permute-start(bf16[272,512]{1,0:T(8,128)(2,1)S(1)} %get-tuple-element.256), channel_id=1, source_target_pairs={{0,6},{1,7},{2,4},{3,5},{4,2},{5,3},{6,0},{7,1},{8,14},{9,15},{10,... | collective-permute-start | bytes 835592 | tf_op jit(solution)/shard_map/ppermute | solution.py:623
  83.9 3.8 %collective-permute-done.10 = bf16[512,128]{1,0:T(8,128)(2,1)S(1)} collective-permute-done((bf16[512,128]{1,0:T(8,128)(2,1)S(1)}, bf16[512,128]{1,0:T(8,128)(2,1)S(1)}, u32[]{:S(2)}, u32[]{:S(2)}) %collective-permute-start.10) | collective-permute-done | bytes 131104 | tf_op jit(solution)/shard_map/ppermute | solution.py:623
  87.7 2.4 %collective-permute-start.18 = (bf16[512,128]{1,0:T(8,128)(2,1)S(1)}, bf16[512,128]{1,0:T(8,128)(2,1)S(1)}, u32[]{:S(2)}, u32[]{:S(2)}) collective-permute-start(bf16[512,128]{1,0:T(8,128)(2,1)S(1)} %add_convert_fusion), channel_id=1, source_target_pairs={{0,24},{1,25},{2,26},{3,27},{4,28},{5,29},{6,30},{7,31},{8,16},{9,... | collective-permute-start | bytes 393224 | tf_op jit(solution)/shard_map/ppermute | solution.py:623
  92.2 1.5 %collective-permute-start.19 = (bf16[272,512]{1,0:T(8,128)(2,1)S(1)}, bf16[272,512]{1,0:T(8,128)(2,1)S(1)}, u32[]{:S(2)}, u32[]{:S(2)}) collective-permute-start(bf16[272,512]{1,0:T(8,128)(2,1)S(1)} %get-tuple-element.266), channel_id=1, source_target_pairs={{0,2},{1,3},{2,0},{3,1},{4,6},{5,7},{6,4},{7,5},{8,10},{9,11},{10,... | collective-permute-start | bytes 835592 | tf_op jit(solution)/shard_map/ppermute | solution.py:623
  95.3 7.2 %collective-permute-done.15 = bf16[144,512]{1,0:T(8,128)(2,1)S(1)} collective-permute-done((bf16[144,512]{1,0:T(8,128)(2,1)S(1)}, bf16[144,512]{1,0:T(8,128)(2,1)S(1)}, u32[]{:S(2)}, u32[]{:S(2)}) %collective-permute-start.15) | collective-permute-done | bytes 147488 | tf_op jit(solution)/shard_map/ppermute | solution.py:623
  102.7 1.6 %collective-permute-start.22 = (bf16[4,512,128]{2,1,0:T(8,128)(2,1)S(1)}, bf16[4,512,128]{2,1,0:T(8,128)(2,1)S(1)}, u32[]{:S(2)}, u32[]{:S(2)}) collective-permute-start(bf16[4,512,128]{2,1,0:T(8,128)(2,1)S(1)} %pad_maximum_fusion.2.refs_0_), channel_id=1, source_target_pairs={{0,4},{1,5},{2,6},{3,7},{4,0},{5,1},{6,2},{7,3},{8,12},{9,13},{10,... | collective-permute-start | bytes 1572872 | tf_op jit(solution)/shard_map/ppermute | solution.py:623
  104.3 1.5 %collective-permute-start.21 = (bf16[4,512,128]{2,1,0:T(8,128)(2,1)S(1)}, bf16[4,512,128]{2,1,0:T(8,128)(2,1)S(1)}, u32[]{:S(2)}, u32[]{:S(2)}) collective-permute-start(bf16[4,512,128]{2,1,0:T(8,128)(2,1)S(1)} %pad_maximum_fusion.2.refs_0_), channel_id=1, source_target_pairs={{0,2},{1,3},{2,0},{3,1},{4,6},{5,7},{6,4},{7,5},{8,10},{9,11},{10,... | collective-permute-start | bytes 1572872 | tf_op jit(solution)/shard_map/ppermute | solution.py:623
  108.7 5.4 %collective-permute-done.20 = bf16[80,512]{1,0:T(8,128)(2,1)S(1)} collective-permute-done((bf16[80,512]{1,0:T(8,128)(2,1)S(1)}, bf16[80,512]{1,0:T(8,128)(2,1)S(1)}, u32[]{:S(2)}, u32[]{:S(2)}) %collective-permute-start.20) | collective-permute-done | bytes 81952 | tf_op jit(solution)/shard_map/ppermute | solution.py:623
  115.1 3.4 %collective-permute-start.23 = (bf16[64,512]{1,0:T(8,128)(2,1)S(1)}, bf16[64,512]{1,0:T(8,128)(2,1)S(1)}, u32[]{:S(2)}, u32[]{:S(2)}) collective-permute-start(bf16[64,512]{1,0:T(8,128)(2,1)S(1)} %add_convert_fusion.1), channel_id=1, source_target_pairs={{0,8},{1,9},{2,10},{3,11},{4,12},{5,13},{6,14},{7,15},{8,0},{9,1},... | collective-permute-start | bytes 196616 | tf_op jit(solution)/shard_map/ppermute | solution.py:623
  122.9 1.6 %collective-permute-start.27 = (bf16[2,512,128]{2,1,0:T(8,128)(2,1)S(1)}, bf16[2,512,128]{2,1,0:T(8,128)(2,1)S(1)}, u32[]{:S(2)}, u32[]{:S(2)}) collective-permute-start(bf16[2,512,128]{2,1,0:T(8,128)(2,1)S(1)} %slice.233), channel_id=1, source_target_pairs={{0,2},{1,3},{2,0},{3,1},{4,6},{5,7},{6,4},{7,5},{8,10},{9,11},{10,... | collective-permute-start | bytes 786440 | tf_op jit(solution)/shard_map/ppermute | solution.py:623
  124.4 1.5 %collective-permute-start.28 = (bf16[2,512,128]{2,1,0:T(8,128)(2,1)S(1)}, bf16[2,512,128]{2,1,0:T(8,128)(2,1)S(1)}, u32[]{:S(2)}, u32[]{:S(2)}) collective-permute-start(bf16[2,512,128]{2,1,0:T(8,128)(2,1)S(1)} %slice.234), channel_id=1, source_target_pairs={{0,4},{1,5},{2,6},{3,7},{4,0},{5,1},{6,2},{7,3},{8,12},{9,13},{10,... | collective-permute-start | bytes 786440 | tf_op jit(solution)/shard_map/ppermute | solution.py:623
  125.9 2.3 %place.3 = (f32[2048,512]{1,0:T(8,128)}, f32[512,2048]{1,0:T(8,128)}) custom-call(s32[16]{0:T(128)S(1)} %get-tuple-element.328.info, bf16[4,512,128]{2,1,0:T(8,128)(2,1)S(1)} %pad_maximum_fusion.2.refs_0_, bf16[4,512,128]{2,1,0:T(8,128)(2,1)S(1)} %collective-permute-done.21.refs_1_, bf16[4,512,128]{2,1,0:T(8,128)(2,1)S(1)} %collective-permute-done.22.refs_2_), custom_call_target="tpu_custom_call" | custom-call | tf_op jit(solution)/shard_map/place/pallas_call | solution.py:566
  128.4 2.6 %collective-permute-done.30.refs_2_ = bf16[4,64,512]{2,1,0:T(8,128)(2,1)S(1)} collective-permute-done((bf16[4,64,512]{2,1,0:T(8,128)(2,1)S(1)}, bf16[4,64,512]{2,1,0:T(8,128)(2,1)S(1)}, u32[]{:S(2)}, u32[]{:S(2)}) %collective-permute-start.30) | collective-permute-done | bytes 262176 | tf_op jit(solution)/shard_map/ppermute | solution.py:623
  131.5 4.8 %collective-permute-done.27.refs_0_ = bf16[2,512,128]{2,1,0:T(8,128)(2,1)S(1)} collective-permute-done((bf16[2,512,128]{2,1,0:T(8,128)(2,1)S(1)}, bf16[2,512,128]{2,1,0:T(8,128)(2,1)S(1)}, u32[]{:S(2)}, u32[]{:S(2)}) %collective-permute-start.27) | collective-permute-done | bytes 262176 | tf_op jit(solution)/shard_map/ppermute | solution.py:623
  137.7 1.5 %collective-permute-start.34 = (bf16[2,64,512]{2,1,0:T(8,128)(2,1)S(1)}, bf16[2,64,512]{2,1,0:T(8,128)(2,1)S(1)}, u32[]{:S(2)}, u32[]{:S(2)}) collective-permute-start(bf16[2,64,512]{2,1,0:T(8,128)(2,1)S(1)} %slice.236), channel_id=1, source_target_pairs={{0,4},{1,5},{2,6},{3,7},{4,0},{5,1},{6,2},{7,3},{8,12},{9,13},{10,... | collective-permute-start | bytes 393224 | tf_op jit(solution)/shard_map/ppermute | solution.py:623
  139.2 1.9 %place.4 = (f32[2048,512]{1,0:T(8,128)}, f32[512,2048]{1,0:T(8,128)}) custom-call(s32[16]{0:T(128)S(1)} %get-tuple-element.328.info, bf16[2,512,128]{2,1,0:T(8,128)(2,1)S(1)} %collective-permute-done.27.refs_0_, bf16[2,512,128]{2,1,0:T(8,128)(2,1)S(1)} %collective-permute-done.28.refs_1_, ...), custom_call_target="tpu_custom_call", output_to_operand_aliasing={{0}: (4, {}), {1}: (5, {})} | custom-call | tf_op jit(solution)/shard_map/place/pallas_call | solution.py:566
  141.2 2.3 %place.5 = (f32[2048,512]{1,0:T(8,128)}, f32[512,2048]{1,0:T(8,128)}) custom-call(s32[16]{0:T(128)S(1)} %get-tuple-element.328.info, bf16[8,512,128]{2,1,0:T(8,128)(2,1)S(1)} %collective-permute-done.31.refs_0_, bf16[4,512,128]{2,1,0:T(8,128)(2,1)S(1)} %collective-permute-done.32.refs_1_, ...), custom_call_target="tpu_custom_call", output_to_operand_aliasing={{0}: (3, {}), {1}: (4, {})} | custom-call | tf_op jit(solution)/shard_map/place/pallas_call | solution.py:566
  143.8 2.8 %sort.2 = (f32[512,512]{1,0:T(8,128)}, f32[512,512]{1,0:T(8,128)}, f32[512,512]{1,0:T(8,128)}, f32[512,512]{1,0:T(8,128)}) custom-call(s32[16]{0:T(128)S(1)} %get-tuple-element.328.info, bf16[4,64,512]{2,1,0:T(8,128)(2,1)S(1)} %pad_maximum_fusion.10.refs_0_, bf16[4,64,512]{2,1,0:T(8,128)(2,1)S(1)} %collective-permute-done.29.refs_1_, ...), custom_call_target="tpu_custom_call" | custom-call | tf_op jit(solution)/shard_map/sort/pallas_call | solution.py:600
  (125 shorter events, 25.8 us)
Async XLA Ops:
  3.1 9.7 %collective-permute-start = (bf16[256,512]{1,0:T(8,128)(2,1)}, bf16[256,512]{1,0:T(8,128)(2,1)S(1)}, u32[]{:S(2)}, u32[]{:S(2)}) collective-permute-start(bf16[256,512]{1,0:T(8,128)(2,1)} %get-tuple-element.178), channel_id=1, source_target_pairs={{0,2},{1,3},{2,0},{3,1},{4,6},{5,7},{6,4},{7,5},{8,10},{9,11},{10,... | collective-permute-start | bytes 786440 | tf_op jit(solution)/shard_map/ppermute | solution.py:623
  36.8 5.2 %collective-permute-start.3 = (bf16[16,512,128]{2,1,0:T(8,128)(2,1)S(1)}, bf16[16,512,128]{2,1,0:T(8,128)(2,1)S(1)}, u32[]{:S(2)}, u32[]{:S(2)}) collective-permute-start(bf16[16,512,128]{2,1,0:T(8,128)(2,1)S(1)} %get-tuple-element.198), channel_id=1, source_target_pairs={{0,1},{1,0},{2,3},{3,2},{4,5},{5,4},{6,7},{7,6},{8,9},{9,8},{10,11... | collective-permute-start | bytes 6291464 | tf_op jit(solution)/shard_map/ppermute | solution.py:623
  45.7 23.7 %collective-permute-start.4 = (bf16[4,512,128]{2,1,0:T(8,128)(2,1)S(1)}, bf16[4,512,128]{2,1,0:T(8,128)(2,1)S(1)}, u32[]{:S(2)}, u32[]{:S(2)}) collective-permute-start(bf16[4,512,128]{2,1,0:T(8,128)(2,1)S(1)} %get-tuple-element.221), channel_id=1, source_target_pairs={{0,2},{1,3},{2,0},{3,1},{4,6},{5,7},{6,4},{7,5},{8,10},{9,11},{10,... | collective-permute-start | bytes 1572872 | tf_op jit(solution)/shard_map/ppermute | solution.py:623
  47.5 21.9 %collective-permute-start.5 = (bf16[4,512,128]{2,1,0:T(8,128)(2,1)S(1)}, bf16[4,512,128]{2,1,0:T(8,128)(2,1)S(1)}, u32[]{:S(2)}, u32[]{:S(2)}) collective-permute-start(bf16[4,512,128]{2,1,0:T(8,128)(2,1)S(1)} %get-tuple-element.222), channel_id=1, source_target_pairs={{0,4},{1,5},{2,6},{3,7},{4,0},{5,1},{6,2},{7,3},{8,12},{9,13},{10,... | collective-permute-start | bytes 1572872 | tf_op jit(solution)/shard_map/ppermute | solution.py:623
  49.0 23.2 %collective-permute-start.6 = (bf16[4,512,128]{2,1,0:T(8,128)(2,1)S(1)}, bf16[4,512,128]{2,1,0:T(8,128)(2,1)S(1)}, u32[]{:S(2)}, u32[]{:S(2)}) collective-permute-start(bf16[4,512,128]{2,1,0:T(8,128)(2,1)S(1)} %get-tuple-element.223), channel_id=1, source_target_pairs={{0,6},{1,7},{2,4},{3,5},{4,2},{5,3},{6,0},{7,1},{8,14},{9,15},{10,... | collective-permute-start | bytes 1572872 | tf_op jit(solution)/shard_map/ppermute | solution.py:623
  72.2 5.2 %collective-permute-start.7 = (bf16[1040,512]{1,0:T(8,128)(2,1)}, bf16[1040,512]{1,0:T(8,128)(2,1)S(1)}, u32[]{:S(2)}, u32[]{:S(2)}) collective-permute-start(bf16[1040,512]{1,0:T(8,128)(2,1)} %get-tuple-element.234), channel_id=1, source_target_pairs={{0,1},{1,0},{2,3},{3,2},{4,5},{5,4},{6,7},{7,6},{8,9},{9,8},{10,11... | collective-permute-start | bytes 3194888 | tf_op jit(solution)/shard_map/ppermute | solution.py:623
  72.2 5.2 %collective-permute-start.8 = (bf16[528,512]{1,0:T(8,128)(2,1)S(1)}, bf16[528,512]{1,0:T(8,128)(2,1)S(1)}, u32[]{:S(2)}, u32[]{:S(2)}) collective-permute-start(bf16[528,512]{1,0:T(8,128)(2,1)S(1)} %get-tuple-element.235), channel_id=1, source_target_pairs={{0,1},{1,0},{2,3},{3,2},{4,5},{5,4},{6,7},{7,6},{8,9},{9,8},{10,11... | collective-permute-start | bytes 1622024 | tf_op jit(solution)/shard_map/ppermute | solution.py:623
  72.9 8.1 %collective-permute-start.9 = (bf16[512,128]{1,0:T(8,128)(2,1)S(1)}, bf16[512,128]{1,0:T(8,128)(2,1)S(1)}, u32[]{:S(2)}, u32[]{:S(2)}) collective-permute-start(bf16[512,128]{1,0:T(8,128)(2,1)S(1)} %get-tuple-element.241), channel_id=1, source_target_pairs={{0,8},{1,9},{2,10},{3,11},{4,12},{5,13},{6,14},{7,15},{8,0},{9,1},... | collective-permute-start | bytes 393224 | tf_op jit(solution)/shard_map/ppermute | solution.py:623
  74.7 12.9 %collective-permute-start.10 = (bf16[512,128]{1,0:T(8,128)(2,1)S(1)}, bf16[512,128]{1,0:T(8,128)(2,1)S(1)}, u32[]{:S(2)}, u32[]{:S(2)}) collective-permute-start(bf16[512,128]{1,0:T(8,128)(2,1)S(1)} %get-tuple-element.242), channel_id=1, source_target_pairs={{0,16},{1,17},{2,18},{3,19},{4,20},{5,21},{6,22},{7,23},{8,24},{9,... | collective-permute-start | bytes 393224 | tf_op jit(solution)/shard_map/ppermute | solution.py:623
  77.3 10.3 %collective-permute-start.11 = (bf16[512,128]{1,0:T(8,128)(2,1)S(1)}, bf16[512,128]{1,0:T(8,128)(2,1)S(1)}, u32[]{:S(2)}, u32[]{:S(2)}) collective-permute-start(bf16[512,128]{1,0:T(8,128)(2,1)S(1)} %get-tuple-element.243), channel_id=1, source_target_pairs={{0,24},{1,25},{2,26},{3,27},{4,28},{5,29},{6,30},{7,31},{8,16},{9,... | collective-permute-start | bytes 393224 | tf_op jit(solution)/shard_map/ppermute | solution.py:623
  77.8 13.6 %collective-permute-start.12 = (bf16[272,512]{1,0:T(8,128)(2,1)S(1)}, bf16[272,512]{1,0:T(8,128)(2,1)S(1)}, u32[]{:S(2)}, u32[]{:S(2)}) collective-permute-start(bf16[272,512]{1,0:T(8,128)(2,1)S(1)} %get-tuple-element.254), channel_id=1, source_target_pairs={{0,2},{1,3},{2,0},{3,1},{4,6},{5,7},{6,4},{7,5},{8,10},{9,11},{10,... | collective-permute-start | bytes 835592 | tf_op jit(solution)/shard_map/ppermute | solution.py:623
  79.5 12.6 %collective-permute-start.13 = (bf16[272,512]{1,0:T(8,128)(2,1)S(1)}, bf16[272,512]{1,0:T(8,128)(2,1)S(1)}, u32[]{:S(2)}, u32[]{:S(2)}) collective-permute-start(bf16[272,512]{1,0:T(8,128)(2,1)S(1)} %get-tuple-element.255), channel_id=1, source_target_pairs={{0,4},{1,5},{2,6},{3,7},{4,0},{5,1},{6,2},{7,3},{8,12},{9,13},{10,... | collective-permute-start | bytes 835592 | tf_op jit(solution)/shard_map/ppermute | solution.py:623
  81.1 12.7 %collective-permute-start.14 = (bf16[272,512]{1,0:T(8,128)(2,1)S(1)}, bf16[272,512]{1,0:T(8,128)(2,1)S(1)}, u32[]{:S(2)}, u32[]{:S(2)}) collective-permute-start(bf16[272,512]{1,0:T(8,128)(2,1)S(1)} %get-tuple-element.256), channel_id=1, source_target_pairs={{0,6},{1,7},{2,4},{3,5},{4,2},{5,3},{6,0},{7,1},{8,14},{9,15},{10,... | collective-permute-start | bytes 835592 | tf_op jit(solution)/shard_map/ppermute | solution.py:623
  87.7 14.8 %collective-permute-start.18 = (bf16[512,128]{1,0:T(8,128)(2,1)S(1)}, bf16[512,128]{1,0:T(8,128)(2,1)S(1)}, u32[]{:S(2)}, u32[]{:S(2)}) collective-permute-start(bf16[512,128]{1,0:T(8,128)(2,1)S(1)} %add_convert_fusion), channel_id=1, source_target_pairs={{0,24},{1,25},{2,26},{3,27},{4,28},{5,29},{6,30},{7,31},{8,16},{9,... | collective-permute-start | bytes 393224 | tf_op jit(solution)/shard_map/ppermute | solution.py:623
  90.2 12.4 %collective-permute-start.17 = (bf16[512,128]{1,0:T(8,128)(2,1)S(1)}, bf16[512,128]{1,0:T(8,128)(2,1)S(1)}, u32[]{:S(2)}, u32[]{:S(2)}) collective-permute-start(bf16[512,128]{1,0:T(8,128)(2,1)S(1)} %add_convert_fusion), channel_id=1, source_target_pairs={{0,16},{1,17},{2,18},{3,19},{4,20},{5,21},{6,22},{7,23},{8,24},{9,... | collective-permute-start | bytes 393224 | tf_op jit(solution)/shard_map/ppermute | solution.py:623
  91.4 11.2 %collective-permute-start.16 = (bf16[512,128]{1,0:T(8,128)(2,1)S(1)}, bf16[512,128]{1,0:T(8,128)(2,1)S(1)}, u32[]{:S(2)}, u32[]{:S(2)}) collective-permute-start(bf16[512,128]{1,0:T(8,128)(2,1)S(1)} %add_convert_fusion), channel_id=1, source_target_pairs={{0,8},{1,9},{2,10},{3,11},{4,12},{5,13},{6,14},{7,15},{8,0},{9,1},... | collective-permute-start | bytes 393224 | tf_op jit(solution)/shard_map/ppermute | solution.py:623
  92.2 10.4 %collective-permute-start.19 = (bf16[272,512]{1,0:T(8,128)(2,1)S(1)}, bf16[272,512]{1,0:T(8,128)(2,1)S(1)}, u32[]{:S(2)}, u32[]{:S(2)}) collective-permute-start(bf16[272,512]{1,0:T(8,128)(2,1)S(1)} %get-tuple-element.266), channel_id=1, source_target_pairs={{0,2},{1,3},{2,0},{3,1},{4,6},{5,7},{6,4},{7,5},{8,10},{9,11},{10,... | collective-permute-start | bytes 835592 | tf_op jit(solution)/shard_map/ppermute | solution.py:623
  94.0 8.4 %collective-permute-start.15 = (bf16[144,512]{1,0:T(8,128)(2,1)S(1)}, bf16[144,512]{1,0:T(8,128)(2,1)S(1)}, u32[]{:S(2)}, u32[]{:S(2)}) collective-permute-start(bf16[144,512]{1,0:T(8,128)(2,1)S(1)} %pad_maximum_fusion.12), channel_id=1, source_target_pairs={{0,8},{1,9},{2,10},{3,11},{4,12},{5,13},{6,14},{7,15},{8,0},{9,1},... | collective-permute-start | bytes 442376 | tf_op jit(solution)/shard_map/ppermute | solution.py:623
  102.7 17.2 %collective-permute-start.22 = (bf16[4,512,128]{2,1,0:T(8,128)(2,1)S(1)}, bf16[4,512,128]{2,1,0:T(8,128)(2,1)S(1)}, u32[]{:S(2)}, u32[]{:S(2)}) collective-permute-start(bf16[4,512,128]{2,1,0:T(8,128)(2,1)S(1)} %pad_maximum_fusion.2.refs_0_), channel_id=1, source_target_pairs={{0,4},{1,5},{2,6},{3,7},{4,0},{5,1},{6,2},{7,3},{8,12},{9,13},{10,... | collective-permute-start | bytes 1572872 | tf_op jit(solution)/shard_map/ppermute | solution.py:623
  104.3 15.6 %collective-permute-start.21 = (bf16[4,512,128]{2,1,0:T(8,128)(2,1)S(1)}, bf16[4,512,128]{2,1,0:T(8,128)(2,1)S(1)}, u32[]{:S(2)}, u32[]{:S(2)}) collective-permute-start(bf16[4,512,128]{2,1,0:T(8,128)(2,1)S(1)} %pad_maximum_fusion.2.refs_0_), channel_id=1, source_target_pairs={{0,2},{1,3},{2,0},{3,1},{4,6},{5,7},{6,4},{7,5},{8,10},{9,11},{10,... | collective-permute-start | bytes 1572872 | tf_op jit(solution)/shard_map/ppermute | solution.py:623
  105.8 8.3 %collective-permute-start.20 = (bf16[80,512]{1,0:T(8,128)(2,1)S(1)}, bf16[80,512]{1,0:T(8,128)(2,1)S(1)}, u32[]{:S(2)}, u32[]{:S(2)}) collective-permute-start(bf16[80,512]{1,0:T(8,128)(2,1)S(1)} %pad_maximum_fusion.13), channel_id=1, source_target_pairs={{0,16},{1,17},{2,18},{3,19},{4,20},{5,21},{6,22},{7,23},{8,24},{9,... | collective-permute-start | bytes 245768 | tf_op jit(solution)/shard_map/ppermute | solution.py:623
  114.1 6.2 %collective-permute-start.25 = (bf16[64,512]{1,0:T(8,128)(2,1)S(1)}, bf16[64,512]{1,0:T(8,128)(2,1)S(1)}, u32[]{:S(2)}, u32[]{:S(2)}) collective-permute-start(bf16[64,512]{1,0:T(8,128)(2,1)S(1)} %add_convert_fusion.1), channel_id=1, source_target_pairs={{0,24},{1,25},{2,26},{3,27},{4,28},{5,29},{6,30},{7,31},{8,16},{9,... | collective-permute-start | bytes 196616 | tf_op jit(solution)/shard_map/ppermute | solution.py:623
  115.1 6.5 %collective-permute-start.24 = (bf16[64,512]{1,0:T(8,128)(2,1)S(1)}, bf16[64,512]{1,0:T(8,128)(2,1)S(1)}, u32[]{:S(2)}, u32[]{:S(2)}) collective-permute-start(bf16[64,512]{1,0:T(8,128)(2,1)S(1)} %add_convert_fusion.1), channel_id=1, source_target_pairs={{0,16},{1,17},{2,18},{3,19},{4,20},{5,21},{6,22},{7,23},{8,24},{9,... | collective-permute-start | bytes 196616 | tf_op jit(solution)/shard_map/ppermute | solution.py:623
  115.1 6.5 %collective-permute-start.23 = (bf16[64,512]{1,0:T(8,128)(2,1)S(1)}, bf16[64,512]{1,0:T(8,128)(2,1)S(1)}, u32[]{:S(2)}, u32[]{:S(2)}) collective-permute-start(bf16[64,512]{1,0:T(8,128)(2,1)S(1)} %add_convert_fusion.1), channel_id=1, source_target_pairs={{0,8},{1,9},{2,10},{3,11},{4,12},{5,13},{6,14},{7,15},{8,0},{9,1},... | collective-permute-start | bytes 196616 | tf_op jit(solution)/shard_map/ppermute | solution.py:623
  121.7 14.7 %collective-permute-start.26 = (bf16[4,512,128]{2,1,0:T(8,128)(2,1)S(1)}, bf16[4,512,128]{2,1,0:T(8,128)(2,1)S(1)}, u32[]{:S(2)}, u32[]{:S(2)}) collective-permute-start(bf16[4,512,128]{2,1,0:T(8,128)(2,1)S(1)} %pad_maximum_fusion.2.refs_0_), channel_id=1, source_target_pairs={{0,1},{1,0},{2,3},{3,2},{4,5},{5,4},{6,7},{7,6},{8,9},{9,8},{10,11... | collective-permute-start | bytes 1572872 | tf_op jit(solution)/shard_map/ppermute | solution.py:623
  121.8 9.2 %collective-permute-start.30 = (bf16[4,64,512]{2,1,0:T(8,128)(2,1)S(1)}, bf16[4,64,512]{2,1,0:T(8,128)(2,1)S(1)}, u32[]{:S(2)}, u32[]{:S(2)}) collective-permute-start(bf16[4,64,512]{2,1,0:T(8,128)(2,1)S(1)} %pad_maximum_fusion.10.refs_0_), channel_id=1, source_target_pairs={{0,4},{1,5},{2,6},{3,7},{4,0},{5,1},{6,2},{7,3},{8,12},{9,13},{10,... | collective-permute-start | bytes 786440 | tf_op jit(solution)/shard_map/ppermute | solution.py:623
  122.4 9.2 %collective-permute-start.29 = (bf16[4,64,512]{2,1,0:T(8,128)(2,1)S(1)}, bf16[4,64,512]{2,1,0:T(8,128)(2,1)S(1)}, u32[]{:S(2)}, u32[]{:S(2)}) collective-permute-start(bf16[4,64,512]{2,1,0:T(8,128)(2,1)S(1)} %pad_maximum_fusion.10.refs_0_), channel_id=1, source_target_pairs={{0,2},{1,3},{2,0},{3,1},{4,6},{5,7},{6,4},{7,5},{8,10},{9,11},{10,... | collective-permute-start | bytes 786440 | tf_op jit(solution)/shard_map/ppermute | solution.py:623
  122.9 13.5 %collective-permute-start.27 = (bf16[2,512,128]{2,1,0:T(8,128)(2,1)S(1)}, bf16[2,512,128]{2,1,0:T(8,128)(2,1)S(1)}, u32[]{:S(2)}, u32[]{:S(2)}) collective-permute-start(bf16[2,512,128]{2,1,0:T(8,128)(2,1)S(1)} %slice.233), channel_id=1, source_target_pairs={{0,2},{1,3},{2,0},{3,1},{4,6},{5,7},{6,4},{7,5},{8,10},{9,11},{10,... | collective-permute-start | bytes 786440 | tf_op jit(solution)/shard_map/ppermute | solution.py:623
  124.4 11.9 %collective-permute-start.28 = (bf16[2,512,128]{2,1,0:T(8,128)(2,1)S(1)}, bf16[2,512,128]{2,1,0:T(8,128)(2,1)S(1)}, u32[]{:S(2)}, u32[]{:S(2)}) collective-permute-start(bf16[2,512,128]{2,1,0:T(8,128)(2,1)S(1)} %slice.234), channel_id=1, source_target_pairs={{0,4},{1,5},{2,6},{3,7},{4,0},{5,1},{6,2},{7,3},{8,12},{9,13},{10,... | collective-permute-start | bytes 786440 | tf_op jit(solution)/shard_map/ppermute | solution.py:623
  136.6 6.9 %collective-permute-start.35 = (bf16[12,64,512]{2,1,0:T(8,128)(2,1)S(1)}, bf16[12,64,512]{2,1,0:T(8,128)(2,1)S(1)}, u32[]{:S(2)}, u32[]{:S(2)}) collective-permute-start(bf16[12,64,512]{2,1,0:T(8,128)(2,1)S(1)} %pad_maximum_fusion.1), channel_id=1, source_target_pairs={{0,1},{1,0},{2,3},{3,2},{4,5},{5,4},{6,7},{7,6},{8,9},{9,8},{10,11... | collective-permute-start | bytes 2359304 | tf_op jit(solution)/shard_map/ppermute | solution.py:623
  137.2 6.3 %collective-permute-start.33 = (bf16[2,64,512]{2,1,0:T(8,128)(2,1)S(1)}, bf16[2,64,512]{2,1,0:T(8,128)(2,1)S(1)}, u32[]{:S(2)}, u32[]{:S(2)}) collective-permute-start(bf16[2,64,512]{2,1,0:T(8,128)(2,1)S(1)} %slice.235), channel_id=1, source_target_pairs={{0,2},{1,3},{2,0},{3,1},{4,6},{5,7},{6,4},{7,5},{8,10},{9,11},{10,... | collective-permute-start | bytes 393224 | tf_op jit(solution)/shard_map/ppermute | solution.py:623
  137.7 5.8 %collective-permute-start.34 = (bf16[2,64,512]{2,1,0:T(8,128)(2,1)S(1)}, bf16[2,64,512]{2,1,0:T(8,128)(2,1)S(1)}, u32[]{:S(2)}, u32[]{:S(2)}) collective-permute-start(bf16[2,64,512]{2,1,0:T(8,128)(2,1)S(1)} %slice.236), channel_id=1, source_target_pairs={{0,4},{1,5},{2,6},{3,7},{4,0},{5,1},{6,2},{7,3},{8,12},{9,13},{10,... | collective-permute-start | bytes 393224 | tf_op jit(solution)/shard_map/ppermute | solution.py:623
  (21 other events, 90.8 us)

commit v8 on v7

--- a/solution.py
+++ b/solution.py
@@ -165,18 +165,23 @@
         q = query * mine + one
         v = values * mine + one
         skewed[head] = skew(lines[pl.ds(2 * step + head, 1), :], lines.shape[1])
-        for b in range(4):
-            s = dot(q, keys[b] * mine + edges[head, b * count : (b + 1) * count, :], NT)
-            for r in range(4):
-                at = starts[b] - starts[2 * (r // 2)] + 896 - 128 * (r % 2)
-                part = s[r * 128 : (r + 1) * 128] + skewed[head, :, pl.ds(pl.multiple_of(at, 128), 256)]
-                scores[head, r * 128 : (r + 1) * 128, b * 256 : (b + 1) * 256] = part
+        k = jnp.concatenate(keys) * mine + edges[head]
+        for half in range(2):
+            s = dot(q[half * 256 : (half + 1) * 256], k, NT)
+            for r in range(2):
+                for b in range(4):
+                    at = starts[b] - starts[2 * half] + 896 - 128 * r
+                    part = s[r * 128 : (r + 1) * 128, b * 256 : (b + 1) * 256] + skewed[head, :, pl.ds(pl.multiple_of(at, 128), 256)]
+                    scores[head, half * 256 + r * 128 : half * 256 + (r + 1) * 128, b * 256 : (b + 1) * 256] = part
+        accs = []
         for r in range(4):
             rs = slice(r * 128, (r + 1) * 128)
             value = scores[head, rs, :]
             top = jnp.max(value, axis=1, keepdims=True)
-            expo[head, rs, :] = jnp.exp(value - top).astype(BF16)
-        acc = dot(expo[head], v)
+            e = jnp.exp(value - top).astype(BF16)
+            expo[head, rs, :] = e
+            accs.append(dot(e, v))
+        acc = jnp.concatenate(accs)
         made.append((acc, 1.0 / (acc[:, 64:65] if head == 0 else acc[:, 0:1])))
     (a0, i0), (a1, i1) = made
     scale = jnp.where(first, i0, i1)
@@ -639,10 +644,10 @@
     line = [8, 16]
     further = [32 << b for b in range((lax.axis_size("dp") // 8).bit_length() - 1)]
     piece = core * 16 + doc * 4 + (far_off % 2) * 8 + (far_off // 2) % 4
+    far_send = jnp.where(doc == 0, inputs[1], inputs[0])
+    far = exchange(far_send, ROW)
+    inputs, _ = wait(inputs, far_send)
     near = jnp.where(doc == 0, inputs[0], inputs[1])
-    far_send = jnp.where(doc == 0, inputs[1], inputs[0])
-    near, far_send = wait(near, far_send)
-    far = exchange(far_send, ROW)
     near_other = exchange(near, CORE)
     slot = jnp.arange(8, dtype=jnp.int32)
     ids = jnp.zeros_like(slot)
@@ -710,8 +715,8 @@
     took = exchange(send, line[0])
     token, took = wait(token, took)
     small = small + one_value(took[2 * piece :])
-    send = jnp.concatenate([added(lines[2 * piece : 3 * piece], took[piece : 2 * piece]), two_terms(small)])
-    lines = added(lines[:piece], took[:piece])
+    lines = added(jnp.concatenate([lines[:piece], lines[2 * piece : 3 * piece]]), took[: 2 * piece])
+    send = jnp.concatenate([lines, two_terms(small)])
     token, send, back_line, away_got = wait(token, send, back_line, away_got)
     took = exchange(send, line[1])
 
@@ -724,20 +729,20 @@
     input_grad = jnp.where(doc == 0, jnp.stack([home, away_got]), jnp.stack([away_got, home]))
     token, took, pooled, input_grad = wait(token, took, pooled, input_grad)
 
-    small = small + one_value(took[piece:])
-    rest = added(lines, took[:piece])
+    small = small + one_value(took[2 * piece :])
+    rest = added(lines, jnp.concatenate([took[piece : 2 * piece], took[:piece]]))
     for bit in further:
         rest = added(rest, exchange(rest, bit))
         small = small + exchange(small, bit)
     token, rest = wait(token, rest)
-    rest_back = [exchange(rest, m) for m in zz]
+    rest_back = exchange(rest, line[0])
     outs = [small[0], small[1], small[2], small[3, : bias_table.size].reshape(bias_table.shape[::-1]).T]
     token, from_y, from_x, outs = wait(token, from_y, from_x, outs)
 
     sends = [from_x[:2], from_y[2:]]
     token, sends, rest_back = wait(token, sends, rest_back)
     far_a, far_b = exchange(sends[0], ROW), exchange(sends[1], NEAR_X)
-    fourth = jnp.stack([rest] + rest_back)
+    fourth = jnp.stack([rest[:piece], rest_back[:piece], rest[piece:], rest_back[piece:]])
     token, fourth, quarter = wait(token, fourth, quarter)
     fourth_y, fourth_x = exchange(fourth, ROW), exchange(fourth, NEAR_X)
     other = exchange(quarter, CORE)

time: 148 us -> 147 us (level)
  starting transfers between devices: 40 us -> 35.7 us
  waiting for transfers between devices: 31 us -> 32.7 us
    ppermute x37 -> x35, starting transfers between devices: 40 us -> 35.7 us  [exchange(): lax.ppermute(value, ('dp', 'blk'), [(i, i ^ bits) for i in range(size)])]
    ppermute x37 -> x35, waiting for transfers between devices: 31 us -> 32.7 us  [exchange(): lax.ppermute(value, ('dp', 'blk'), [(i, i ^ bits) for i in range(size)])]
  transfers between devices with their start and end apart: 37 -> 35, of which waited for: 11 -> 11; matrix products, arithmetic and copies ran while one was open for 2% -> 3% of each run, Pallas kernels for 26% -> 26%
where the time goes in v8:
time: 147 us
  Pallas kernels  65.7 us (45%)
  starting transfers between devices  35.7 us (24%)
  waiting for transfers between devices  32.7 us (22%)
  other arithmetic  5.51 us (4%)
  local copies, waits for them, and re-layouts  5.42 us (4%)
    ppermute x35, starting transfers between devices, exchange(): lax.ppermute(value, ('dp', 'blk'), [(i, i ^ bits) for i in range(size)])  35.7 us
    ppermute x35, waiting for transfers between devices, exchange(): lax.ppermute(value, ('dp', 'blk'), [(i, i ^ bits) for i in range(size)])  32.7 us
    pallas_call x1, Pallas kernels, front(): pl.pallas_call(front_kernel, grid=(heads // 2,), in_specs=[smem] + [whole...  22.2 us
    pallas_call x1, Pallas kernels, back(): pl.pallas_call(back_kernel, grid=(width // 128,), in_specs=[smem, col(cou...  20.1 us
    pallas_call x3, Pallas kernels, place(): pl.pallas_call(functools.partial(place_kernel, [first for first, _ in par...  6.59 us
    pallas_call x1, Pallas kernels, through(): pl.pallas_call(through_kernel, in_specs=[smem, free, pl.BlockSpec(memory_...  4.87 us
    pallas_call x2, Pallas kernels, sort(): pl.pallas_call(functools.partial(sort_kernel, [first for first, _ in part...  4.23 us
    unnamed x32, local copies, waits for them, and re-layouts  3.86 us
  transfers between devices with their start and end apart: 35, of which 11 were waited for; matrix products, arithmetic and copies ran while one was open for 3% of the time, Pallas kernels for 26%

profile of v8, /device:TPU:0, one launch (start us, length us, event | category | flops | bytes accessed | tf_op | source)
XLA Modules:
  0.0 146.5 jit_solution(7247954941688370669)
XLA Ops:
  0.7 1.9 %select_bitcast_fusion.1 = bf16[256,512]{1,0:T(8,128)(2,1)} fusion(bf16[2,256,512]{2,1,0:T(8,128)(2,1)} %param.15, pred[]{:T(512)S(6)} %eq.31), kind=kLoop, calls=%fused_computation.30 | loop fusion | flops 131072 | bytes 786433 | tf_op jit(solution)/shard_map/jit(_where)/select_n | solution.py:647
  4.2 2.6 %collective-permute-start = (bf16[256,512]{1,0:T(8,128)(2,1)}, bf16[256,512]{1,0:T(8,128)(2,1)S(1)}, u32[]{:S(2)}, u32[]{:S(2)}) collective-permute-start(bf16[256,512]{1,0:T(8,128)(2,1)} %select_bitcast_fusion.1), channel_id=1, source_target_pairs={{0,2},{1,3},{2,0},{3,1},{4,6},{5,7},{6,4},{7,5},{8,10},{9,11},{10,... | collective-permute-start | bytes 786440 | tf_op jit(solution)/shard_map/ppermute | solution.py:628
  10.6 1.5 %prepare.1 = (bf16[512,512]{1,0:T(8,128)(2,1)S(1)}, bf16[256,512]{1,0:T(8,128)(2,1)S(1)}, bf16[512,512]{1,0:T(8,128)(2,1)S(1)}, bf16[512,512]{1,0:T(8,128)(2,1)S...) custom-call(bf16[256,512]{1,0:T(8,128)(2,1)S(1)} %select_bitcast_fusion.mine.near.near, ...), custom_call_target="tpu_custom_call" | custom-call | tf_op jit(solution)/shard_map/prepare/pallas_call | solution.py:65
  12.2 1.7 %collective-permute-done.far.far_h = bf16[256,512]{1,0:T(8,128)(2,1)S(1)} collective-permute-done((bf16[256,512]{1,0:T(8,128)(2,1)}, bf16[256,512]{1,0:T(8,128)(2,1)S(1)}, u32[]{:S(2)}, u32[]{:S(2)}) %collective-permute-start) | collective-permute-done | bytes 262176 | tf_op jit(solution)/shard_map/ppermute | solution.py:628
  15.5 22.2 %front.1 = (bf16[512,512]{1,0:T(8,128)(2,1)S(1)}, bf16[256,512]{1,0:T(8,128)(2,1)S(1)}, bf16[512,512]{1,0:T(8,128)(2,1)S(1)}, bf16[512,512]{1,0:T(8,128)(2,1)S(1...) custom-call(s32[16]{0:T(128)S(1)} %get-tuple-element.322.info, ...), custom_call_target="tpu_custom_call" | custom-call | tf_op jit(solution)/shard_map/front/pallas_call | solution.py:254
  37.9 4.9 %through.1 = (f32[512,512]{1,0:T(8,128)S(1)}, bf16[512,512]{1,0:T(8,128)(2,1)S(1)}, bf16[512,512]{1,0:T(8,128)(2,1)S(1)}, f32[8,512]{1,0:T(8,128)S(1)}) custom-call(s32[16]{0:T(128)S(1)} %get-tuple-element.322.info, bf16[512,2048]{1,0:T(8,128)(2,1)S(1)} %get-tuple-element.189.slopes_h, bf16[512,2048]{1,0:T(8,128)(2,1)S(1)} %copy-done, ...), custom_call_target="tpu_custom_call" | custom-call | tf_op jit(solution)/shard_map/through/pallas_call | solution.py:311
  42.8 3.7 %meet.1 = (bf16[4,512,128]{2,1,0:T(8,128)(2,1)S(1)}, bf16[4,512,128]{2,1,0:T(8,128)(2,1)S(1)}, bf16[4,512,128]{2,1,0:T(8,128)(2,1)S(1)}, bf16[4,512,128]{2,1,0:T(8,128)(2,1)S(1)}) custom-call(s32[16]{0:T(128)S(1)} %get-tuple-element.322.info, bf16[16,512,128]{2,1,0:T(8,128)(2,1)S(1)} %collective-permute-done.3.got_h, ...), custom_call_target="tpu_custom_call" | custom-call | tf_op jit(solution)/shard_map/meet/pallas_call | solution.py:361
  46.5 1.8 %collective-permute-start.4 = (bf16[4,512,128]{2,1,0:T(8,128)(2,1)S(1)}, bf16[4,512,128]{2,1,0:T(8,128)(2,1)S(1)}, u32[]{:S(2)}, u32[]{:S(2)}) collective-permute-start(bf16[4,512,128]{2,1,0:T(8,128)(2,1)S(1)} %get-tuple-element.217), channel_id=1, source_target_pairs={{0,2},{1,3},{2,0},{3,1},{4,6},{5,7},{6,4},{7,5},{8,10},{9,11},{10,... | collective-permute-start | bytes 1572872 | tf_op jit(solution)/shard_map/ppermute | solution.py:628
  48.4 1.5 %collective-permute-start.5 = (bf16[4,512,128]{2,1,0:T(8,128)(2,1)S(1)}, bf16[4,512,128]{2,1,0:T(8,128)(2,1)S(1)}, u32[]{:S(2)}, u32[]{:S(2)}) collective-permute-start(bf16[4,512,128]{2,1,0:T(8,128)(2,1)S(1)} %get-tuple-element.218), channel_id=1, source_target_pairs={{0,4},{1,5},{2,6},{3,7},{4,0},{5,1},{6,2},{7,3},{8,12},{9,13},{10,... | collective-permute-start | bytes 1572872 | tf_op jit(solution)/shard_map/ppermute | solution.py:628
  50.1 20.1 %back.1 = (bf16[16,64,512]{2,1,0:T(8,128)(2,1)S(1)}, bf16[1040,512]{1,0:T(8,128)(2,1)}, f32[512,512]{1,0:T(8,128)}, bf16[528,512]{1,0:T(8,128)(2,1)S(1)}, f32[8,512]{1,0:T(8,128)S(1)}) custom-call(s32[16]{0:T(128)S(1)} %get-tuple-element.322.info, bf16[256,512]{1,0:T(8,128)(2,1)S(1)} %get-tuple-element.180.q_l.ql, ...), custom_call_target="tpu_custom_call" | custom-call | tf_op jit(solution)/shard_map/back/pallas_call | solution.py:504
  70.3 2.8 %collective-permute-done.6.refs_3_ = bf16[4,512,128]{2,1,0:T(8,128)(2,1)S(1)} collective-permute-done((bf16[4,512,128]{2,1,0:T(8,128)(2,1)S(1)}, bf16[4,512,128]{2,1,0:T(8,128)(2,1)S(1)}, u32[]{:S(2)}, u32[]{:S(2)}) %collective-permute-start.6) | collective-permute-done | bytes 524320 | tf_op jit(solution)/shard_map/ppermute | solution.py:628
  73.8 1.8 %collective-permute-start.9 = (bf16[512,128]{1,0:T(8,128)(2,1)S(1)}, bf16[512,128]{1,0:T(8,128)(2,1)S(1)}, u32[]{:S(2)}, u32[]{:S(2)}) collective-permute-start(bf16[512,128]{1,0:T(8,128)(2,1)S(1)} %get-tuple-element.237), channel_id=1, source_target_pairs={{0,8},{1,9},{2,10},{3,11},{4,12},{5,13},{6,14},{7,15},{8,0},{9,1},... | collective-permute-start | bytes 393224 | tf_op jit(solution)/shard_map/ppermute | solution.py:628
  75.6 2.6 %collective-permute-start.10 = (bf16[512,128]{1,0:T(8,128)(2,1)S(1)}, bf16[512,128]{1,0:T(8,128)(2,1)S(1)}, u32[]{:S(2)}, u32[]{:S(2)}) collective-permute-start(bf16[512,128]{1,0:T(8,128)(2,1)S(1)} %get-tuple-element.238), channel_id=1, source_target_pairs={{0,16},{1,17},{2,18},{3,19},{4,20},{5,21},{6,22},{7,23},{8,24},{9,... | collective-permute-start | bytes 393224 | tf_op jit(solution)/shard_map/ppermute | solution.py:628
  78.7 1.7 %collective-permute-start.12 = (bf16[272,512]{1,0:T(8,128)(2,1)S(1)}, bf16[272,512]{1,0:T(8,128)(2,1)S(1)}, u32[]{:S(2)}, u32[]{:S(2)}) collective-permute-start(bf16[272,512]{1,0:T(8,128)(2,1)S(1)} %get-tuple-element.250), channel_id=1, source_target_pairs={{0,2},{1,3},{2,0},{3,1},{4,6},{5,7},{6,4},{7,5},{8,10},{9,11},{10,... | collective-permute-start | bytes 835592 | tf_op jit(solution)/shard_map/ppermute | solution.py:628
  80.4 1.5 %collective-permute-start.13 = (bf16[272,512]{1,0:T(8,128)(2,1)S(1)}, bf16[272,512]{1,0:T(8,128)(2,1)S(1)}, u32[]{:S(2)}, u32[]{:S(2)}) collective-permute-start(bf16[272,512]{1,0:T(8,128)(2,1)S(1)} %get-tuple-element.251), channel_id=1, source_target_pairs={{0,4},{1,5},{2,6},{3,7},{4,0},{5,1},{6,2},{7,3},{8,12},{9,13},{10,... | collective-permute-start | bytes 835592 | tf_op jit(solution)/shard_map/ppermute | solution.py:628
  81.9 1.7 %collective-permute-start.14 = (bf16[272,512]{1,0:T(8,128)(2,1)S(1)}, bf16[272,512]{1,0:T(8,128)(2,1)S(1)}, u32[]{:S(2)}, u32[]{:S(2)}) collective-permute-start(bf16[272,512]{1,0:T(8,128)(2,1)S(1)} %get-tuple-element.252), channel_id=1, source_target_pairs={{0,6},{1,7},{2,4},{3,5},{4,2},{5,3},{6,0},{7,1},{8,14},{9,15},{10,... | collective-permute-start | bytes 835592 | tf_op jit(solution)/shard_map/ppermute | solution.py:628
  84.7 3.8 %collective-permute-done.10 = bf16[512,128]{1,0:T(8,128)(2,1)S(1)} collective-permute-done((bf16[512,128]{1,0:T(8,128)(2,1)S(1)}, bf16[512,128]{1,0:T(8,128)(2,1)S(1)}, u32[]{:S(2)}, u32[]{:S(2)}) %collective-permute-start.10) | collective-permute-done | bytes 131104 | tf_op jit(solution)/shard_map/ppermute | solution.py:628
  88.6 2.5 %collective-permute-start.18 = (bf16[512,128]{1,0:T(8,128)(2,1)S(1)}, bf16[512,128]{1,0:T(8,128)(2,1)S(1)}, u32[]{:S(2)}, u32[]{:S(2)}) collective-permute-start(bf16[512,128]{1,0:T(8,128)(2,1)S(1)} %add_convert_fusion.2), channel_id=1, source_target_pairs={{0,24},{1,25},{2,26},{3,27},{4,28},{5,29},{6,30},{7,31},{8,16},{9,... | collective-permute-start | bytes 393224 | tf_op jit(solution)/shard_map/ppermute | solution.py:628
  93.0 1.5 %collective-permute-start.19 = (bf16[272,512]{1,0:T(8,128)(2,1)S(1)}, bf16[272,512]{1,0:T(8,128)(2,1)S(1)}, u32[]{:S(2)}, u32[]{:S(2)}) collective-permute-start(bf16[272,512]{1,0:T(8,128)(2,1)S(1)} %get-tuple-element.262), channel_id=1, source_target_pairs={{0,2},{1,3},{2,0},{3,1},{4,6},{5,7},{6,4},{7,5},{8,10},{9,11},{10,... | collective-permute-start | bytes 835592 | tf_op jit(solution)/shard_map/ppermute | solution.py:628
  96.2 7.2 %collective-permute-done.15 = bf16[144,512]{1,0:T(8,128)(2,1)S(1)} collective-permute-done((bf16[144,512]{1,0:T(8,128)(2,1)S(1)}, bf16[144,512]{1,0:T(8,128)(2,1)S(1)}, u32[]{:S(2)}, u32[]{:S(2)}) %collective-permute-start.15) | collective-permute-done | bytes 147488 | tf_op jit(solution)/shard_map/ppermute | solution.py:628
  103.6 1.6 %collective-permute-start.22 = (bf16[4,512,128]{2,1,0:T(8,128)(2,1)S(1)}, bf16[4,512,128]{2,1,0:T(8,128)(2,1)S(1)}, u32[]{:S(2)}, u32[]{:S(2)}) collective-permute-start(bf16[4,512,128]{2,1,0:T(8,128)(2,1)S(1)} %pad_maximum_fusion.2.refs_0_), channel_id=1, source_target_pairs={{0,4},{1,5},{2,6},{3,7},{4,0},{5,1},{6,2},{7,3},{8,12},{9,13},{10,... | collective-permute-start | bytes 1572872 | tf_op jit(solution)/shard_map/ppermute | solution.py:628
  105.2 1.5 %collective-permute-start.21 = (bf16[4,512,128]{2,1,0:T(8,128)(2,1)S(1)}, bf16[4,512,128]{2,1,0:T(8,128)(2,1)S(1)}, u32[]{:S(2)}, u32[]{:S(2)}) collective-permute-start(bf16[4,512,128]{2,1,0:T(8,128)(2,1)S(1)} %pad_maximum_fusion.2.refs_0_), channel_id=1, source_target_pairs={{0,2},{1,3},{2,0},{3,1},{4,6},{5,7},{6,4},{7,5},{8,10},{9,11},{10,... | collective-permute-start | bytes 1572872 | tf_op jit(solution)/shard_map/ppermute | solution.py:628
  109.6 4.6 %collective-permute-done.20 = bf16[144,512]{1,0:T(8,128)(2,1)S(1)} collective-permute-done((bf16[144,512]{1,0:T(8,128)(2,1)S(1)}, bf16[144,512]{1,0:T(8,128)(2,1)S(1)}, u32[]{:S(2)}, u32[]{:S(2)}) %collective-permute-start.20) | collective-permute-done | bytes 147488 | tf_op jit(solution)/shard_map/ppermute | solution.py:628
  116.0 3.9 %collective-permute-done.23 = bf16[128,512]{1,0:T(8,128)(2,1)S(1)} collective-permute-done((bf16[128,512]{1,0:T(8,128)(2,1)S(1)}, bf16[128,512]{1,0:T(8,128)(2,1)S(1)}, u32[]{:S(2)}, u32[]{:S(2)}) %collective-permute-start.23) | collective-permute-done | bytes 131104 | tf_op jit(solution)/shard_map/ppermute | solution.py:628
  121.2 1.6 %collective-permute-start.25 = (bf16[2,512,128]{2,1,0:T(8,128)(2,1)S(1)}, bf16[2,512,128]{2,1,0:T(8,128)(2,1)S(1)}, u32[]{:S(2)}, u32[]{:S(2)}) collective-permute-start(bf16[2,512,128]{2,1,0:T(8,128)(2,1)S(1)} %slice.257), channel_id=1, source_target_pairs={{0,2},{1,3},{2,0},{3,1},{4,6},{5,7},{6,4},{7,5},{8,10},{9,11},{10,... | collective-permute-start | bytes 786440 | tf_op jit(solution)/shard_map/ppermute | solution.py:628
  124.1 2.3 %place.3 = (f32[2048,512]{1,0:T(8,128)}, f32[512,2048]{1,0:T(8,128)}) custom-call(s32[16]{0:T(128)S(1)} %get-tuple-element.322.info, bf16[4,512,128]{2,1,0:T(8,128)(2,1)S(1)} %pad_maximum_fusion.2.refs_0_, bf16[4,512,128]{2,1,0:T(8,128)(2,1)S(1)} %collective-permute-done.21.refs_1_, bf16[4,512,128]{2,1,0:T(8,128)(2,1)S(1)} %collective-permute-done.22.refs_2_), custom_call_target="tpu_custom_call" | custom-call | tf_op jit(solution)/shard_map/place/pallas_call | solution.py:571
  126.6 2.6 %collective-permute-done.28.refs_2_ = bf16[4,64,512]{2,1,0:T(8,128)(2,1)S(1)} collective-permute-done((bf16[4,64,512]{2,1,0:T(8,128)(2,1)S(1)}, bf16[4,64,512]{2,1,0:T(8,128)(2,1)S(1)}, u32[]{:S(2)}, u32[]{:S(2)}) %collective-permute-start.28) | collective-permute-done | bytes 262176 | tf_op jit(solution)/shard_map/ppermute | solution.py:628
  129.9 4.8 %collective-permute-done.25.refs_0_ = bf16[2,512,128]{2,1,0:T(8,128)(2,1)S(1)} collective-permute-done((bf16[2,512,128]{2,1,0:T(8,128)(2,1)S(1)}, bf16[2,512,128]{2,1,0:T(8,128)(2,1)S(1)}, u32[]{:S(2)}, u32[]{:S(2)}) %collective-permute-start.25) | collective-permute-done | bytes 262176 | tf_op jit(solution)/shard_map/ppermute | solution.py:628
  136.0 1.5 %collective-permute-start.32 = (bf16[2,64,512]{2,1,0:T(8,128)(2,1)S(1)}, bf16[2,64,512]{2,1,0:T(8,128)(2,1)S(1)}, u32[]{:S(2)}, u32[]{:S(2)}) collective-permute-start(bf16[2,64,512]{2,1,0:T(8,128)(2,1)S(1)} %slice.264), channel_id=1, source_target_pairs={{0,4},{1,5},{2,6},{3,7},{4,0},{5,1},{6,2},{7,3},{8,12},{9,13},{10,... | collective-permute-start | bytes 393224 | tf_op jit(solution)/shard_map/ppermute | solution.py:628
  137.5 1.9 %place.4 = (f32[2048,512]{1,0:T(8,128)}, f32[512,2048]{1,0:T(8,128)}) custom-call(s32[16]{0:T(128)S(1)} %get-tuple-element.322.info, bf16[2,512,128]{2,1,0:T(8,128)(2,1)S(1)} %collective-permute-done.25.refs_0_, bf16[2,512,128]{2,1,0:T(8,128)(2,1)S(1)} %collective-permute-done.26.refs_1_, ...), custom_call_target="tpu_custom_call", output_to_operand_aliasing={{0}: (4, {}), {1}: (5, {})} | custom-call | tf_op jit(solution)/shard_map/place/pallas_call | solution.py:571
  139.5 2.3 %place.5 = (f32[2048,512]{1,0:T(8,128)}, f32[512,2048]{1,0:T(8,128)}) custom-call(s32[16]{0:T(128)S(1)} %get-tuple-element.322.info, bf16[8,512,128]{2,1,0:T(8,128)(2,1)S(1)} %collective-permute-done.29.refs_0_, bf16[4,512,128]{2,1,0:T(8,128)(2,1)S(1)} %collective-permute-done.30.refs_1_, ...), custom_call_target="tpu_custom_call", output_to_operand_aliasing={{0}: (3, {}), {1}: (4, {})} | custom-call | tf_op jit(solution)/shard_map/place/pallas_call | solution.py:571
  142.1 2.8 %sort.2 = (f32[512,512]{1,0:T(8,128)}, f32[512,512]{1,0:T(8,128)}, f32[512,512]{1,0:T(8,128)}, f32[512,512]{1,0:T(8,128)}) custom-call(s32[16]{0:T(128)S(1)} %get-tuple-element.322.info, bf16[4,64,512]{2,1,0:T(8,128)(2,1)S(1)} %pad_maximum_fusion.10.refs_0_, bf16[4,64,512]{2,1,0:T(8,128)(2,1)S(1)} %collective-permute-done.27.refs_1_, ...), custom_call_target="tpu_custom_call" | custom-call | tf_op jit(solution)/shard_map/sort/pallas_call | solution.py:605
  (125 shorter events, 24.7 us)
Async XLA Ops:
  4.2 9.7 %collective-permute-start = (bf16[256,512]{1,0:T(8,128)(2,1)}, bf16[256,512]{1,0:T(8,128)(2,1)S(1)}, u32[]{:S(2)}, u32[]{:S(2)}) collective-permute-start(bf16[256,512]{1,0:T(8,128)(2,1)} %select_bitcast_fusion.1), channel_id=1, source_target_pairs={{0,2},{1,3},{2,0},{3,1},{4,6},{5,7},{6,4},{7,5},{8,10},{9,11},{10,... | collective-permute-start | bytes 786440 | tf_op jit(solution)/shard_map/ppermute | solution.py:628
  37.6 5.2 %collective-permute-start.3 = (bf16[16,512,128]{2,1,0:T(8,128)(2,1)S(1)}, bf16[16,512,128]{2,1,0:T(8,128)(2,1)S(1)}, u32[]{:S(2)}, u32[]{:S(2)}) collective-permute-start(bf16[16,512,128]{2,1,0:T(8,128)(2,1)S(1)} %get-tuple-element.194), channel_id=1, source_target_pairs={{0,1},{1,0},{2,3},{3,2},{4,5},{5,4},{6,7},{7,6},{8,9},{9,8},{10,11... | collective-permute-start | bytes 6291464 | tf_op jit(solution)/shard_map/ppermute | solution.py:628
  46.5 23.7 %collective-permute-start.4 = (bf16[4,512,128]{2,1,0:T(8,128)(2,1)S(1)}, bf16[4,512,128]{2,1,0:T(8,128)(2,1)S(1)}, u32[]{:S(2)}, u32[]{:S(2)}) collective-permute-start(bf16[4,512,128]{2,1,0:T(8,128)(2,1)S(1)} %get-tuple-element.217), channel_id=1, source_target_pairs={{0,2},{1,3},{2,0},{3,1},{4,6},{5,7},{6,4},{7,5},{8,10},{9,11},{10,... | collective-permute-start | bytes 1572872 | tf_op jit(solution)/shard_map/ppermute | solution.py:628
  48.4 21.9 %collective-permute-start.5 = (bf16[4,512,128]{2,1,0:T(8,128)(2,1)S(1)}, bf16[4,512,128]{2,1,0:T(8,128)(2,1)S(1)}, u32[]{:S(2)}, u32[]{:S(2)}) collective-permute-start(bf16[4,512,128]{2,1,0:T(8,128)(2,1)S(1)} %get-tuple-element.218), channel_id=1, source_target_pairs={{0,4},{1,5},{2,6},{3,7},{4,0},{5,1},{6,2},{7,3},{8,12},{9,13},{10,... | collective-permute-start | bytes 1572872 | tf_op jit(solution)/shard_map/ppermute | solution.py:628
  49.9 23.2 %collective-permute-start.6 = (bf16[4,512,128]{2,1,0:T(8,128)(2,1)S(1)}, bf16[4,512,128]{2,1,0:T(8,128)(2,1)S(1)}, u32[]{:S(2)}, u32[]{:S(2)}) collective-permute-start(bf16[4,512,128]{2,1,0:T(8,128)(2,1)S(1)} %get-tuple-element.219), channel_id=1, source_target_pairs={{0,6},{1,7},{2,4},{3,5},{4,2},{5,3},{6,0},{7,1},{8,14},{9,15},{10,... | collective-permute-start | bytes 1572872 | tf_op jit(solution)/shard_map/ppermute | solution.py:628
  73.0 5.2 %collective-permute-start.7 = (bf16[1040,512]{1,0:T(8,128)(2,1)}, bf16[1040,512]{1,0:T(8,128)(2,1)S(1)}, u32[]{:S(2)}, u32[]{:S(2)}) collective-permute-start(bf16[1040,512]{1,0:T(8,128)(2,1)} %get-tuple-element.230), channel_id=1, source_target_pairs={{0,1},{1,0},{2,3},{3,2},{4,5},{5,4},{6,7},{7,6},{8,9},{9,8},{10,11... | collective-permute-start | bytes 3194888 | tf_op jit(solution)/shard_map/ppermute | solution.py:628
  73.0 5.2 %collective-permute-start.8 = (bf16[528,512]{1,0:T(8,128)(2,1)S(1)}, bf16[528,512]{1,0:T(8,128)(2,1)S(1)}, u32[]{:S(2)}, u32[]{:S(2)}) collective-permute-start(bf16[528,512]{1,0:T(8,128)(2,1)S(1)} %get-tuple-element.231), channel_id=1, source_target_pairs={{0,1},{1,0},{2,3},{3,2},{4,5},{5,4},{6,7},{7,6},{8,9},{9,8},{10,11... | collective-permute-start | bytes 1622024 | tf_op jit(solution)/shard_map/ppermute | solution.py:628
  73.8 8.1 %collective-permute-start.9 = (bf16[512,128]{1,0:T(8,128)(2,1)S(1)}, bf16[512,128]{1,0:T(8,128)(2,1)S(1)}, u32[]{:S(2)}, u32[]{:S(2)}) collective-permute-start(bf16[512,128]{1,0:T(8,128)(2,1)S(1)} %get-tuple-element.237), channel_id=1, source_target_pairs={{0,8},{1,9},{2,10},{3,11},{4,12},{5,13},{6,14},{7,15},{8,0},{9,1},... | collective-permute-start | bytes 393224 | tf_op jit(solution)/shard_map/ppermute | solution.py:628
  75.6 12.9 %collective-permute-start.10 = (bf16[512,128]{1,0:T(8,128)(2,1)S(1)}, bf16[512,128]{1,0:T(8,128)(2,1)S(1)}, u32[]{:S(2)}, u32[]{:S(2)}) collective-permute-start(bf16[512,128]{1,0:T(8,128)(2,1)S(1)} %get-tuple-element.238), channel_id=1, source_target_pairs={{0,16},{1,17},{2,18},{3,19},{4,20},{5,21},{6,22},{7,23},{8,24},{9,... | collective-permute-start | bytes 393224 | tf_op jit(solution)/shard_map/ppermute | solution.py:628
  78.2 10.3 %collective-permute-start.11 = (bf16[512,128]{1,0:T(8,128)(2,1)S(1)}, bf16[512,128]{1,0:T(8,128)(2,1)S(1)}, u32[]{:S(2)}, u32[]{:S(2)}) collective-permute-start(bf16[512,128]{1,0:T(8,128)(2,1)S(1)} %get-tuple-element.239), channel_id=1, source_target_pairs={{0,24},{1,25},{2,26},{3,27},{4,28},{5,29},{6,30},{7,31},{8,16},{9,... | collective-permute-start | bytes 393224 | tf_op jit(solution)/shard_map/ppermute | solution.py:628
  78.7 13.6 %collective-permute-start.12 = (bf16[272,512]{1,0:T(8,128)(2,1)S(1)}, bf16[272,512]{1,0:T(8,128)(2,1)S(1)}, u32[]{:S(2)}, u32[]{:S(2)}) collective-permute-start(bf16[272,512]{1,0:T(8,128)(2,1)S(1)} %get-tuple-element.250), channel_id=1, source_target_pairs={{0,2},{1,3},{2,0},{3,1},{4,6},{5,7},{6,4},{7,5},{8,10},{9,11},{10,... | collective-permute-start | bytes 835592 | tf_op jit(solution)/shard_map/ppermute | solution.py:628
  80.4 12.6 %collective-permute-start.13 = (bf16[272,512]{1,0:T(8,128)(2,1)S(1)}, bf16[272,512]{1,0:T(8,128)(2,1)S(1)}, u32[]{:S(2)}, u32[]{:S(2)}) collective-permute-start(bf16[272,512]{1,0:T(8,128)(2,1)S(1)} %get-tuple-element.251), channel_id=1, source_target_pairs={{0,4},{1,5},{2,6},{3,7},{4,0},{5,1},{6,2},{7,3},{8,12},{9,13},{10,... | collective-permute-start | bytes 835592 | tf_op jit(solution)/shard_map/ppermute | solution.py:628
  81.9 12.7 %collective-permute-start.14 = (bf16[272,512]{1,0:T(8,128)(2,1)S(1)}, bf16[272,512]{1,0:T(8,128)(2,1)S(1)}, u32[]{:S(2)}, u32[]{:S(2)}) collective-permute-start(bf16[272,512]{1,0:T(8,128)(2,1)S(1)} %get-tuple-element.252), channel_id=1, source_target_pairs={{0,6},{1,7},{2,4},{3,5},{4,2},{5,3},{6,0},{7,1},{8,14},{9,15},{10,... | collective-permute-start | bytes 835592 | tf_op jit(solution)/shard_map/ppermute | solution.py:628
  88.6 14.8 %collective-permute-start.18 = (bf16[512,128]{1,0:T(8,128)(2,1)S(1)}, bf16[512,128]{1,0:T(8,128)(2,1)S(1)}, u32[]{:S(2)}, u32[]{:S(2)}) collective-permute-start(bf16[512,128]{1,0:T(8,128)(2,1)S(1)} %add_convert_fusion.2), channel_id=1, source_target_pairs={{0,24},{1,25},{2,26},{3,27},{4,28},{5,29},{6,30},{7,31},{8,16},{9,... | collective-permute-start | bytes 393224 | tf_op jit(solution)/shard_map/ppermute | solution.py:628
  91.0 12.4 %collective-permute-start.17 = (bf16[512,128]{1,0:T(8,128)(2,1)S(1)}, bf16[512,128]{1,0:T(8,128)(2,1)S(1)}, u32[]{:S(2)}, u32[]{:S(2)}) collective-permute-start(bf16[512,128]{1,0:T(8,128)(2,1)S(1)} %add_convert_fusion.2), channel_id=1, source_target_pairs={{0,16},{1,17},{2,18},{3,19},{4,20},{5,21},{6,22},{7,23},{8,24},{9,... | collective-permute-start | bytes 393224 | tf_op jit(solution)/shard_map/ppermute | solution.py:628
  92.2 11.2 %collective-permute-start.16 = (bf16[512,128]{1,0:T(8,128)(2,1)S(1)}, bf16[512,128]{1,0:T(8,128)(2,1)S(1)}, u32[]{:S(2)}, u32[]{:S(2)}) collective-permute-start(bf16[512,128]{1,0:T(8,128)(2,1)S(1)} %add_convert_fusion.2), channel_id=1, source_target_pairs={{0,8},{1,9},{2,10},{3,11},{4,12},{5,13},{6,14},{7,15},{8,0},{9,1},... | collective-permute-start | bytes 393224 | tf_op jit(solution)/shard_map/ppermute | solution.py:628
  93.0 10.4 %collective-permute-start.19 = (bf16[272,512]{1,0:T(8,128)(2,1)S(1)}, bf16[272,512]{1,0:T(8,128)(2,1)S(1)}, u32[]{:S(2)}, u32[]{:S(2)}) collective-permute-start(bf16[272,512]{1,0:T(8,128)(2,1)S(1)} %get-tuple-element.262), channel_id=1, source_target_pairs={{0,2},{1,3},{2,0},{3,1},{4,6},{5,7},{6,4},{7,5},{8,10},{9,11},{10,... | collective-permute-start | bytes 835592 | tf_op jit(solution)/shard_map/ppermute | solution.py:628
  94.9 8.4 %collective-permute-start.15 = (bf16[144,512]{1,0:T(8,128)(2,1)S(1)}, bf16[144,512]{1,0:T(8,128)(2,1)S(1)}, u32[]{:S(2)}, u32[]{:S(2)}) collective-permute-start(bf16[144,512]{1,0:T(8,128)(2,1)S(1)} %pad_maximum_fusion.12), channel_id=1, source_target_pairs={{0,8},{1,9},{2,10},{3,11},{4,12},{5,13},{6,14},{7,15},{8,0},{9,1},... | collective-permute-start | bytes 442376 | tf_op jit(solution)/shard_map/ppermute | solution.py:628
  103.6 11.9 %collective-permute-start.22 = (bf16[4,512,128]{2,1,0:T(8,128)(2,1)S(1)}, bf16[4,512,128]{2,1,0:T(8,128)(2,1)S(1)}, u32[]{:S(2)}, u32[]{:S(2)}) collective-permute-start(bf16[4,512,128]{2,1,0:T(8,128)(2,1)S(1)} %pad_maximum_fusion.2.refs_0_), channel_id=1, source_target_pairs={{0,4},{1,5},{2,6},{3,7},{4,0},{5,1},{6,2},{7,3},{8,12},{9,13},{10,... | collective-permute-start | bytes 1572872 | tf_op jit(solution)/shard_map/ppermute | solution.py:628
  105.2 10.8 %collective-permute-start.21 = (bf16[4,512,128]{2,1,0:T(8,128)(2,1)S(1)}, bf16[4,512,128]{2,1,0:T(8,128)(2,1)S(1)}, u32[]{:S(2)}, u32[]{:S(2)}) collective-permute-start(bf16[4,512,128]{2,1,0:T(8,128)(2,1)S(1)} %pad_maximum_fusion.2.refs_0_), channel_id=1, source_target_pairs={{0,2},{1,3},{2,0},{3,1},{4,6},{5,7},{6,4},{7,5},{8,10},{9,11},{10,... | collective-permute-start | bytes 1572872 | tf_op jit(solution)/shard_map/ppermute | solution.py:628
  106.7 7.5 %collective-permute-start.20 = (bf16[144,512]{1,0:T(8,128)(2,1)S(1)}, bf16[144,512]{1,0:T(8,128)(2,1)S(1)}, u32[]{:S(2)}, u32[]{:S(2)}) collective-permute-start(bf16[144,512]{1,0:T(8,128)(2,1)S(1)} %pad_maximum_fusion.13), channel_id=1, source_target_pairs={{0,16},{1,17},{2,18},{3,19},{4,20},{5,21},{6,22},{7,23},{8,24},{9,... | collective-permute-start | bytes 442376 | tf_op jit(solution)/shard_map/ppermute | solution.py:628
  114.9 5.0 %collective-permute-start.23 = (bf16[128,512]{1,0:T(8,128)(2,1)S(1)}, bf16[128,512]{1,0:T(8,128)(2,1)S(1)}, u32[]{:S(2)}, u32[]{:S(2)}) collective-permute-start(bf16[128,512]{1,0:T(8,128)(2,1)S(1)} %add_convert_fusion), channel_id=1, source_target_pairs={{0,8},{1,9},{2,10},{3,11},{4,12},{5,13},{6,14},{7,15},{8,0},{9,1},... | collective-permute-start | bytes 393224 | tf_op jit(solution)/shard_map/ppermute | solution.py:628
  119.9 14.8 %collective-permute-start.24 = (bf16[4,512,128]{2,1,0:T(8,128)(2,1)S(1)}, bf16[4,512,128]{2,1,0:T(8,128)(2,1)S(1)}, u32[]{:S(2)}, u32[]{:S(2)}) collective-permute-start(bf16[4,512,128]{2,1,0:T(8,128)(2,1)S(1)} %pad_maximum_fusion.2.refs_0_), channel_id=1, source_target_pairs={{0,1},{1,0},{2,3},{3,2},{4,5},{5,4},{6,7},{7,6},{8,9},{9,8},{10,11... | collective-permute-start | bytes 1572872 | tf_op jit(solution)/shard_map/ppermute | solution.py:628
  120.0 9.2 %collective-permute-start.28 = (bf16[4,64,512]{2,1,0:T(8,128)(2,1)S(1)}, bf16[4,64,512]{2,1,0:T(8,128)(2,1)S(1)}, u32[]{:S(2)}, u32[]{:S(2)}) collective-permute-start(bf16[4,64,512]{2,1,0:T(8,128)(2,1)S(1)} %pad_maximum_fusion.10.refs_0_), channel_id=1, source_target_pairs={{0,4},{1,5},{2,6},{3,7},{4,0},{5,1},{6,2},{7,3},{8,12},{9,13},{10,... | collective-permute-start | bytes 786440 | tf_op jit(solution)/shard_map/ppermute | solution.py:628
  120.7 9.2 %collective-permute-start.27 = (bf16[4,64,512]{2,1,0:T(8,128)(2,1)S(1)}, bf16[4,64,512]{2,1,0:T(8,128)(2,1)S(1)}, u32[]{:S(2)}, u32[]{:S(2)}) collective-permute-start(bf16[4,64,512]{2,1,0:T(8,128)(2,1)S(1)} %pad_maximum_fusion.10.refs_0_), channel_id=1, source_target_pairs={{0,2},{1,3},{2,0},{3,1},{4,6},{5,7},{6,4},{7,5},{8,10},{9,11},{10,... | collective-permute-start | bytes 786440 | tf_op jit(solution)/shard_map/ppermute | solution.py:628
  121.2 13.5 %collective-permute-start.25 = (bf16[2,512,128]{2,1,0:T(8,128)(2,1)S(1)}, bf16[2,512,128]{2,1,0:T(8,128)(2,1)S(1)}, u32[]{:S(2)}, u32[]{:S(2)}) collective-permute-start(bf16[2,512,128]{2,1,0:T(8,128)(2,1)S(1)} %slice.257), channel_id=1, source_target_pairs={{0,2},{1,3},{2,0},{3,1},{4,6},{5,7},{6,4},{7,5},{8,10},{9,11},{10,... | collective-permute-start | bytes 786440 | tf_op jit(solution)/shard_map/ppermute | solution.py:628
  122.8 11.9 %collective-permute-start.26 = (bf16[2,512,128]{2,1,0:T(8,128)(2,1)S(1)}, bf16[2,512,128]{2,1,0:T(8,128)(2,1)S(1)}, u32[]{:S(2)}, u32[]{:S(2)}) collective-permute-start(bf16[2,512,128]{2,1,0:T(8,128)(2,1)S(1)} %slice.258), channel_id=1, source_target_pairs={{0,4},{1,5},{2,6},{3,7},{4,0},{5,1},{6,2},{7,3},{8,12},{9,13},{10,... | collective-permute-start | bytes 786440 | tf_op jit(solution)/shard_map/ppermute | solution.py:628
  134.9 4.6 %collective-permute-start.29 = (bf16[8,512,128]{2,1,0:T(8,128)(2,1)S(1)}, bf16[8,512,128]{2,1,0:T(8,128)(2,1)S(1)}, u32[]{:S(2)}, u32[]{:S(2)}) collective-permute-start(bf16[8,512,128]{2,1,0:T(8,128)(2,1)S(1)} %pad_maximum_fusion), channel_id=1, source_target_pairs={{0,1},{1,0},{2,3},{3,2},{4,5},{5,4},{6,7},{7,6},{8,9},{9,8},{10,11... | collective-permute-start | bytes 3145736 | tf_op jit(solution)/shard_map/ppermute | solution.py:628
  135.0 6.9 %collective-permute-start.33 = (bf16[12,64,512]{2,1,0:T(8,128)(2,1)S(1)}, bf16[12,64,512]{2,1,0:T(8,128)(2,1)S(1)}, u32[]{:S(2)}, u32[]{:S(2)}) collective-permute-start(bf16[12,64,512]{2,1,0:T(8,128)(2,1)S(1)} %pad_maximum_fusion.1), channel_id=1, source_target_pairs={{0,1},{1,0},{2,3},{3,2},{4,5},{5,4},{6,7},{7,6},{8,9},{9,8},{10,11... | collective-permute-start | bytes 2359304 | tf_op jit(solution)/shard_map/ppermute | solution.py:628
  135.5 4.0 %collective-permute-start.30 = (bf16[4,512,128]{2,1,0:T(8,128)(2,1)S(1)}, bf16[4,512,128]{2,1,0:T(8,128)(2,1)S(1)}, u32[]{:S(2)}, u32[]{:S(2)}) collective-permute-start(bf16[4,512,128]{2,1,0:T(8,128)(2,1)S(1)} %pad_maximum_fusion.3), channel_id=1, source_target_pairs={{0,1},{1,0},{2,3},{3,2},{4,5},{5,4},{6,7},{7,6},{8,9},{9,8},{10,11... | collective-permute-start | bytes 1572872 | tf_op jit(solution)/shard_map/ppermute | solution.py:628
  135.5 6.3 %collective-permute-start.31 = (bf16[2,64,512]{2,1,0:T(8,128)(2,1)S(1)}, bf16[2,64,512]{2,1,0:T(8,128)(2,1)S(1)}, u32[]{:S(2)}, u32[]{:S(2)}) collective-permute-start(bf16[2,64,512]{2,1,0:T(8,128)(2,1)S(1)} %slice.263), channel_id=1, source_target_pairs={{0,2},{1,3},{2,0},{3,1},{4,6},{5,7},{6,4},{7,5},{8,10},{9,11},{10,... | collective-permute-start | bytes 393224 | tf_op jit(solution)/shard_map/ppermute | solution.py:628
  136.0 5.8 %collective-permute-start.32 = (bf16[2,64,512]{2,1,0:T(8,128)(2,1)S(1)}, bf16[2,64,512]{2,1,0:T(8,128)(2,1)S(1)}, u32[]{:S(2)}, u32[]{:S(2)}) collective-permute-start(bf16[2,64,512]{2,1,0:T(8,128)(2,1)S(1)} %slice.264), channel_id=1, source_target_pairs={{0,4},{1,5},{2,6},{3,7},{4,0},{5,1},{6,2},{7,3},{8,12},{9,13},{10,... | collective-permute-start | bytes 393224 | tf_op jit(solution)/shard_map/ppermute | solution.py:628
  (19 other events, 84.0 us)

commit v9 on v8

--- a/solution.py
+++ b/solution.py
@@ -262,7 +262,7 @@
                        + [pltpu.VMEM(wo.shape, BF16), pltpu.VMEM(win.shape, BF16), pltpu.VMEM(wback.shape, BF16),
                           pltpu.VMEM((2, 2 * count, 4 * count), BF16), pltpu.VMEM((2, 2 * count, 4 * count), F32),
                           pltpu.VMEM((2, 128, span), F32), pltpu.VMEM((2, 4 * count, 128), BF16), pltpu.SemaphoreType.DMA((16,))],
-        name="front", compiler_params=pltpu.CompilerParams(vmem_limit_bytes=36 << 20),
+        name="front", compiler_params=pltpu.CompilerParams(vmem_limit_bytes=38 << 20),
     )(info, far, far_other, near, q_l, k_l, v_l, lines, wq, wk, wv, gain1, gain2, gain3, cots, wo, win, wback)
 
 def through_kernel(info, slopes_h, win_h, mixed_h, steep_h, wo_h, att_h, gain2, grad_mixed_o, grad_attended_o, grad_out_o, rows,
@@ -575,7 +575,7 @@
         out_shape=[shape((16 * 128, width), F32), shape((width, 16 * 128), F32)],
         scratch_shapes=[pltpu.VMEM((count, 128, width), F32), pltpu.VMEM((count, width, 128), F32), pltpu.SemaphoreType.DMA((count,))],
         input_output_aliases={1 + len(parts) + i: i for i in range(len(made))},
-        name="place", compiler_params=pltpu.CompilerParams(vmem_limit_bytes=24 << 20),
+        name="place", compiler_params=pltpu.CompilerParams(vmem_limit_bytes=28 << 20),
     )(info, *[p for _, p in parts], *made)
 
 def sort_kernel(firsts, info, *refs):
@@ -644,10 +644,10 @@
     line = [8, 16]
     further = [32 << b for b in range((lax.axis_size("dp") // 8).bit_length() - 1)]
     piece = core * 16 + doc * 4 + (far_off % 2) * 8 + (far_off // 2) % 4
+    near = jnp.where(doc == 0, inputs[0], inputs[1])
     far_send = jnp.where(doc == 0, inputs[1], inputs[0])
+    near, far_send = wait(near, far_send)
     far = exchange(far_send, ROW)
-    inputs, _ = wait(inputs, far_send)
-    near = jnp.where(doc == 0, inputs[0], inputs[1])
     near_other = exchange(near, CORE)
     slot = jnp.arange(8, dtype=jnp.int32)
     ids = jnp.zeros_like(slot)
@@ -753,9 +753,8 @@
     sends = [fourth_x[:2], fourth_y[2:], near_pair, jnp.concatenate([far_a, far_b]), jnp.concatenate([fourth, fourth_y, fourth_x])]
     token, sends = wait(token, sends)
     last_a, last_b, other_near, other_far, pair = (exchange(s, m) for s, m in zip(sends, (ROW, NEAR_X, CORE, CORE, CORE)))
-    grads = place(token, [(12, far_a), (14, far_b), (16, other)], grads, width)
-    token, grads, other_near, other_far = wait(token, grads, other_near, other_far)
-    out_back, out_in = place(token, [(20, other_near), (28, other_far)], grads, width)
+    token, other_near, other_far = wait(token, other_near, other_far)
+    out_back, out_in = place(token, [(12, far_a), (14, far_b), (16, other), (20, other_near), (28, other_far)], grads, width)
     token, out_back, out_in, last_a, last_b, pair = wait(token, out_back, out_in, last_a, last_b, pair)
 
     ends = exchange(jnp.concatenate([last_a, last_b]), CORE)

time: 147 us -> 145 us (0.986)
  waiting for transfers between devices: 32.7 us -> 34.7 us
  other arithmetic: 5.51 us -> 3.67 us
  Pallas kernels: 65.7 us -> 64.2 us
    ppermute x35, waiting for transfers between devices: 32.7 us -> 34.7 us  [exchange(): lax.ppermute(value, ('dp', 'blk'), [(i, i ^ bits) for i in range(size)])]
    pallas_call x3 -> x2, Pallas kernels: 6.59 us -> 5.38 us  [place(): pl.pallas_call(functools.partial(place_kernel, [first for first, _ in par...]
    unnamed x32 -> x40, local copies, waits for them, and re-layouts: 3.86 us -> 3.88 us
  transfers between devices with their start and end apart: 35 -> 35, of which waited for: 11 -> 12; matrix products, arithmetic and copies ran while one was open for 3% -> 3% of each run, Pallas kernels for 26% -> 26%
where the time goes in v9:
time: 145 us
  Pallas kernels  64.2 us (44%)
  starting transfers between devices  35.6 us (25%)
  waiting for transfers between devices  34.7 us (24%)
  local copies, waits for them, and re-layouts  5.46 us (4%)
  other arithmetic  3.67 us (3%)
  between operations  1.46 us (1%)
    ppermute x35, starting transfers between devices, exchange(): lax.ppermute(value, ('dp', 'blk'), [(i, i ^ bits) for i in range(size)])  35.6 us
    ppermute x35, waiting for transfers between devices, exchange(): lax.ppermute(value, ('dp', 'blk'), [(i, i ^ bits) for i in range(size)])  34.7 us
    pallas_call x1, Pallas kernels, front(): pl.pallas_call(front_kernel, grid=(heads // 2,), in_specs=[smem] + [whole...  22 us
    pallas_call x1, Pallas kernels, back(): pl.pallas_call(back_kernel, grid=(width // 128,), in_specs=[smem, col(cou...  20.1 us
    pallas_call x2, Pallas kernels, place(): pl.pallas_call(functools.partial(place_kernel, [first for first, _ in par...  5.38 us
    pallas_call x1, Pallas kernels, through(): pl.pallas_call(through_kernel, in_specs=[smem, free, pl.BlockSpec(memory_...  4.85 us
    pallas_call x2, Pallas kernels, sort(): pl.pallas_call(functools.partial(sort_kernel, [first for first, _ in part...  4.23 us
    unnamed x40, local copies, waits for them, and re-layouts  3.88 us
  transfers between devices with their start and end apart: 35, of which 12 were waited for; matrix products, arithmetic and copies ran while one was open for 3% of the time, Pallas kernels for 26%

profile of v9, /device:TPU:0, one launch (start us, length us, event | category | flops | bytes accessed | tf_op | source)
XLA Modules:
  0.0 145.0 jit_solution(5205771448316674904)
XLA Ops:
  2.4 2.6 %collective-permute-start = (bf16[256,512]{1,0:T(8,128)(2,1)S(1)}, bf16[256,512]{1,0:T(8,128)(2,1)S(1)}, u32[]{:S(2)}, u32[]{:S(2)}) collective-permute-start(bf16[256,512]{1,0:T(8,128)(2,1)S(1)} %get-tuple-element.172), channel_id=1, source_target_pairs={{0,2},{1,3},{2,0},{3,1},{4,6},{5,7},{6,4},{7,5},{8,10},{9,11},{10,... | collective-permute-start | bytes 786440 | tf_op jit(solution)/shard_map/ppermute | solution.py:628
  8.8 1.5 %prepare.1 = (bf16[512,512]{1,0:T(8,128)(2,1)S(1)}, bf16[256,512]{1,0:T(8,128)(2,1)S(1)}, bf16[512,512]{1,0:T(8,128)(2,1)S(1)}, bf16[512,512]{1,0:T(8,128)(2,1)S...) custom-call(bf16[256,512]{1,0:T(8,128)(2,1)S(1)} %get-tuple-element.173.mine.near.near, ...), custom_call_target="tpu_custom_call" | custom-call | tf_op jit(solution)/shard_map/prepare/pallas_call | solution.py:65
  10.4 1.5 %collective-permute-done.far.far_h = bf16[256,512]{1,0:T(8,128)(2,1)S(1)} collective-permute-done((bf16[256,512]{1,0:T(8,128)(2,1)S(1)}, bf16[256,512]{1,0:T(8,128)(2,1)S(1)}, u32[]{:S(2)}, u32[]{:S(2)}) %collective-permute-start) | collective-permute-done | bytes 262176 | tf_op jit(solution)/shard_map/ppermute | solution.py:628
  13.5 22.0 %front.1 = (bf16[512,512]{1,0:T(8,128)(2,1)S(1)}, bf16[256,512]{1,0:T(8,128)(2,1)S(1)}, bf16[512,512]{1,0:T(8,128)(2,1)S(1)}, bf16[512,512]{1,0:T(8,128)(2,1)S(1...) custom-call(s32[16]{0:T(128)S(1)} %get-tuple-element.316.info, ...), custom_call_target="tpu_custom_call" | custom-call | tf_op jit(solution)/shard_map/front/pallas_call | solution.py:254
  35.8 4.8 %through.1 = (f32[512,512]{1,0:T(8,128)S(1)}, bf16[512,512]{1,0:T(8,128)(2,1)S(1)}, bf16[512,512]{1,0:T(8,128)(2,1)S(1)}, f32[8,512]{1,0:T(8,128)S(1)}) custom-call(s32[16]{0:T(128)S(1)} %get-tuple-element.316.info, bf16[512,2048]{1,0:T(8,128)(2,1)S(1)} %get-tuple-element.187.slopes_h, bf16[512,2048]{1,0:T(8,128)(2,1)S(1)} %copy-done, ...), custom_call_target="tpu_custom_call" | custom-call | tf_op jit(solution)/shard_map/through/pallas_call | solution.py:311
  40.7 3.6 %meet.1 = (bf16[4,512,128]{2,1,0:T(8,128)(2,1)S(1)}, bf16[4,512,128]{2,1,0:T(8,128)(2,1)S(1)}, bf16[4,512,128]{2,1,0:T(8,128)(2,1)S(1)}, bf16[4,512,128]{2,1,0:T(8,128)(2,1)S(1)}) custom-call(s32[16]{0:T(128)S(1)} %get-tuple-element.316.info, bf16[16,512,128]{2,1,0:T(8,128)(2,1)S(1)} %collective-permute-done.3.got_h, ...), custom_call_target="tpu_custom_call" | custom-call | tf_op jit(solution)/shard_map/meet/pallas_call | solution.py:361
  44.3 1.8 %collective-permute-start.4 = (bf16[4,512,128]{2,1,0:T(8,128)(2,1)S(1)}, bf16[4,512,128]{2,1,0:T(8,128)(2,1)S(1)}, u32[]{:S(2)}, u32[]{:S(2)}) collective-permute-start(bf16[4,512,128]{2,1,0:T(8,128)(2,1)S(1)} %get-tuple-element.215), channel_id=1, source_target_pairs={{0,2},{1,3},{2,0},{3,1},{4,6},{5,7},{6,4},{7,5},{8,10},{9,11},{10,... | collective-permute-start | bytes 1572872 | tf_op jit(solution)/shard_map/ppermute | solution.py:628
  46.2 1.5 %collective-permute-start.5 = (bf16[4,512,128]{2,1,0:T(8,128)(2,1)S(1)}, bf16[4,512,128]{2,1,0:T(8,128)(2,1)S(1)}, u32[]{:S(2)}, u32[]{:S(2)}) collective-permute-start(bf16[4,512,128]{2,1,0:T(8,128)(2,1)S(1)} %get-tuple-element.216), channel_id=1, source_target_pairs={{0,4},{1,5},{2,6},{3,7},{4,0},{5,1},{6,2},{7,3},{8,12},{9,13},{10,... | collective-permute-start | bytes 1572872 | tf_op jit(solution)/shard_map/ppermute | solution.py:628
  47.9 20.1 %back.1 = (bf16[16,64,512]{2,1,0:T(8,128)(2,1)S(1)}, bf16[1040,512]{1,0:T(8,128)(2,1)}, f32[512,512]{1,0:T(8,128)}, bf16[528,512]{1,0:T(8,128)(2,1)S(1)}, f32[8,512]{1,0:T(8,128)S(1)}) custom-call(s32[16]{0:T(128)S(1)} %get-tuple-element.316.info, bf16[256,512]{1,0:T(8,128)(2,1)S(1)} %get-tuple-element.178.q_l.ql, ...), custom_call_target="tpu_custom_call" | custom-call | tf_op jit(solution)/shard_map/back/pallas_call | solution.py:504
  68.0 2.9 %collective-permute-done.6.refs_3_ = bf16[4,512,128]{2,1,0:T(8,128)(2,1)S(1)} collective-permute-done((bf16[4,512,128]{2,1,0:T(8,128)(2,1)S(1)}, bf16[4,512,128]{2,1,0:T(8,128)(2,1)S(1)}, u32[]{:S(2)}, u32[]{:S(2)}) %collective-permute-start.6) | collective-permute-done | bytes 524320 | tf_op jit(solution)/shard_map/ppermute | solution.py:628
  71.6 1.8 %collective-permute-start.9 = (bf16[512,128]{1,0:T(8,128)(2,1)S(1)}, bf16[512,128]{1,0:T(8,128)(2,1)S(1)}, u32[]{:S(2)}, u32[]{:S(2)}) collective-permute-start(bf16[512,128]{1,0:T(8,128)(2,1)S(1)} %get-tuple-element.235), channel_id=1, source_target_pairs={{0,8},{1,9},{2,10},{3,11},{4,12},{5,13},{6,14},{7,15},{8,0},{9,1},... | collective-permute-start | bytes 393224 | tf_op jit(solution)/shard_map/ppermute | solution.py:628
  73.4 2.6 %collective-permute-start.10 = (bf16[512,128]{1,0:T(8,128)(2,1)S(1)}, bf16[512,128]{1,0:T(8,128)(2,1)S(1)}, u32[]{:S(2)}, u32[]{:S(2)}) collective-permute-start(bf16[512,128]{1,0:T(8,128)(2,1)S(1)} %get-tuple-element.236), channel_id=1, source_target_pairs={{0,16},{1,17},{2,18},{3,19},{4,20},{5,21},{6,22},{7,23},{8,24},{9,... | collective-permute-start | bytes 393224 | tf_op jit(solution)/shard_map/ppermute | solution.py:628
  76.5 1.7 %collective-permute-start.12 = (bf16[272,512]{1,0:T(8,128)(2,1)S(1)}, bf16[272,512]{1,0:T(8,128)(2,1)S(1)}, u32[]{:S(2)}, u32[]{:S(2)}) collective-permute-start(bf16[272,512]{1,0:T(8,128)(2,1)S(1)} %get-tuple-element.248), channel_id=1, source_target_pairs={{0,2},{1,3},{2,0},{3,1},{4,6},{5,7},{6,4},{7,5},{8,10},{9,11},{10,... | collective-permute-start | bytes 835592 | tf_op jit(solution)/shard_map/ppermute | solution.py:628
  78.2 1.5 %collective-permute-start.13 = (bf16[272,512]{1,0:T(8,128)(2,1)S(1)}, bf16[272,512]{1,0:T(8,128)(2,1)S(1)}, u32[]{:S(2)}, u32[]{:S(2)}) collective-permute-start(bf16[272,512]{1,0:T(8,128)(2,1)S(1)} %get-tuple-element.249), channel_id=1, source_target_pairs={{0,4},{1,5},{2,6},{3,7},{4,0},{5,1},{6,2},{7,3},{8,12},{9,13},{10,... | collective-permute-start | bytes 835592 | tf_op jit(solution)/shard_map/ppermute | solution.py:628
  79.7 1.7 %collective-permute-start.14 = (bf16[272,512]{1,0:T(8,128)(2,1)S(1)}, bf16[272,512]{1,0:T(8,128)(2,1)S(1)}, u32[]{:S(2)}, u32[]{:S(2)}) collective-permute-start(bf16[272,512]{1,0:T(8,128)(2,1)S(1)} %get-tuple-element.250), channel_id=1, source_target_pairs={{0,6},{1,7},{2,4},{3,5},{4,2},{5,3},{6,0},{7,1},{8,14},{9,15},{10,... | collective-permute-start | bytes 835592 | tf_op jit(solution)/shard_map/ppermute | solution.py:628
  82.5 3.8 %collective-permute-done.10 = bf16[512,128]{1,0:T(8,128)(2,1)S(1)} collective-permute-done((bf16[512,128]{1,0:T(8,128)(2,1)S(1)}, bf16[512,128]{1,0:T(8,128)(2,1)S(1)}, u32[]{:S(2)}, u32[]{:S(2)}) %collective-permute-start.10) | collective-permute-done | bytes 131104 | tf_op jit(solution)/shard_map/ppermute | solution.py:628
  86.4 2.5 %collective-permute-start.18 = (bf16[512,128]{1,0:T(8,128)(2,1)S(1)}, bf16[512,128]{1,0:T(8,128)(2,1)S(1)}, u32[]{:S(2)}, u32[]{:S(2)}) collective-permute-start(bf16[512,128]{1,0:T(8,128)(2,1)S(1)} %add_convert_fusion.2), channel_id=1, source_target_pairs={{0,24},{1,25},{2,26},{3,27},{4,28},{5,29},{6,30},{7,31},{8,16},{9,... | collective-permute-start | bytes 393224 | tf_op jit(solution)/shard_map/ppermute | solution.py:628
  90.8 1.5 %collective-permute-start.19 = (bf16[272,512]{1,0:T(8,128)(2,1)S(1)}, bf16[272,512]{1,0:T(8,128)(2,1)S(1)}, u32[]{:S(2)}, u32[]{:S(2)}) collective-permute-start(bf16[272,512]{1,0:T(8,128)(2,1)S(1)} %get-tuple-element.260), channel_id=1, source_target_pairs={{0,2},{1,3},{2,0},{3,1},{4,6},{5,7},{6,4},{7,5},{8,10},{9,11},{10,... | collective-permute-start | bytes 835592 | tf_op jit(solution)/shard_map/ppermute | solution.py:628
  94.0 7.1 %collective-permute-done.15 = bf16[144,512]{1,0:T(8,128)(2,1)S(1)} collective-permute-done((bf16[144,512]{1,0:T(8,128)(2,1)S(1)}, bf16[144,512]{1,0:T(8,128)(2,1)S(1)}, u32[]{:S(2)}, u32[]{:S(2)}) %collective-permute-start.15) | collective-permute-done | bytes 147488 | tf_op jit(solution)/shard_map/ppermute | solution.py:628
  101.4 1.6 %collective-permute-start.22 = (bf16[4,512,128]{2,1,0:T(8,128)(2,1)S(1)}, bf16[4,512,128]{2,1,0:T(8,128)(2,1)S(1)}, u32[]{:S(2)}, u32[]{:S(2)}) collective-permute-start(bf16[4,512,128]{2,1,0:T(8,128)(2,1)S(1)} %pad_maximum_fusion.2.refs_0_), channel_id=1, source_target_pairs={{0,4},{1,5},{2,6},{3,7},{4,0},{5,1},{6,2},{7,3},{8,12},{9,13},{10,... | collective-permute-start | bytes 1572872 | tf_op jit(solution)/shard_map/ppermute | solution.py:628
  103.0 1.5 %collective-permute-start.21 = (bf16[4,512,128]{2,1,0:T(8,128)(2,1)S(1)}, bf16[4,512,128]{2,1,0:T(8,128)(2,1)S(1)}, u32[]{:S(2)}, u32[]{:S(2)}) collective-permute-start(bf16[4,512,128]{2,1,0:T(8,128)(2,1)S(1)} %pad_maximum_fusion.2.refs_0_), channel_id=1, source_target_pairs={{0,2},{1,3},{2,0},{3,1},{4,6},{5,7},{6,4},{7,5},{8,10},{9,11},{10,... | collective-permute-start | bytes 1572872 | tf_op jit(solution)/shard_map/ppermute | solution.py:628
  107.4 4.6 %collective-permute-done.20 = bf16[144,512]{1,0:T(8,128)(2,1)S(1)} collective-permute-done((bf16[144,512]{1,0:T(8,128)(2,1)S(1)}, bf16[144,512]{1,0:T(8,128)(2,1)S(1)}, u32[]{:S(2)}, u32[]{:S(2)}) %collective-permute-start.20) | collective-permute-done | bytes 147488 | tf_op jit(solution)/shard_map/ppermute | solution.py:628
  113.8 3.9 %collective-permute-done.23 = bf16[128,512]{1,0:T(8,128)(2,1)S(1)} collective-permute-done((bf16[128,512]{1,0:T(8,128)(2,1)S(1)}, bf16[128,512]{1,0:T(8,128)(2,1)S(1)}, u32[]{:S(2)}, u32[]{:S(2)}) %collective-permute-start.23) | collective-permute-done | bytes 131104 | tf_op jit(solution)/shard_map/ppermute | solution.py:628
  118.9 1.6 %collective-permute-start.25 = (bf16[2,512,128]{2,1,0:T(8,128)(2,1)S(1)}, bf16[2,512,128]{2,1,0:T(8,128)(2,1)S(1)}, u32[]{:S(2)}, u32[]{:S(2)}) collective-permute-start(bf16[2,512,128]{2,1,0:T(8,128)(2,1)S(1)} %slice.251), channel_id=1, source_target_pairs={{0,2},{1,3},{2,0},{3,1},{4,6},{5,7},{6,4},{7,5},{8,10},{9,11},{10,... | collective-permute-start | bytes 786440 | tf_op jit(solution)/shard_map/ppermute | solution.py:628
  120.5 1.5 %collective-permute-start.26 = (bf16[2,512,128]{2,1,0:T(8,128)(2,1)S(1)}, bf16[2,512,128]{2,1,0:T(8,128)(2,1)S(1)}, u32[]{:S(2)}, u32[]{:S(2)}) collective-permute-start(bf16[2,512,128]{2,1,0:T(8,128)(2,1)S(1)} %slice.252), channel_id=1, source_target_pairs={{0,4},{1,5},{2,6},{3,7},{4,0},{5,1},{6,2},{7,3},{8,12},{9,13},{10,... | collective-permute-start | bytes 786440 | tf_op jit(solution)/shard_map/ppermute | solution.py:628
  122.0 2.3 %place.2 = (f32[2048,512]{1,0:T(8,128)}, f32[512,2048]{1,0:T(8,128)}) custom-call(s32[16]{0:T(128)S(1)} %get-tuple-element.316.info, bf16[4,512,128]{2,1,0:T(8,128)(2,1)S(1)} %pad_maximum_fusion.2.refs_0_, bf16[4,512,128]{2,1,0:T(8,128)(2,1)S(1)} %collective-permute-done.21.refs_1_, bf16[4,512,128]{2,1,0:T(8,128)(2,1)S(1)} %collective-permute-done.22.refs_2_), custom_call_target="tpu_custom_call" | custom-call | tf_op jit(solution)/shard_map/place/pallas_call | solution.py:571
  124.4 2.6 %collective-permute-done.28.refs_2_ = bf16[4,64,512]{2,1,0:T(8,128)(2,1)S(1)} collective-permute-done((bf16[4,64,512]{2,1,0:T(8,128)(2,1)S(1)}, bf16[4,64,512]{2,1,0:T(8,128)(2,1)S(1)}, u32[]{:S(2)}, u32[]{:S(2)}) %collective-permute-start.28) | collective-permute-done | bytes 262176 | tf_op jit(solution)/shard_map/ppermute | solution.py:628
  127.6 4.8 %collective-permute-done.25.refs_0_ = bf16[2,512,128]{2,1,0:T(8,128)(2,1)S(1)} collective-permute-done((bf16[2,512,128]{2,1,0:T(8,128)(2,1)S(1)}, bf16[2,512,128]{2,1,0:T(8,128)(2,1)S(1)}, u32[]{:S(2)}, u32[]{:S(2)}) %collective-permute-start.25) | collective-permute-done | bytes 262176 | tf_op jit(solution)/shard_map/ppermute | solution.py:628
  133.8 1.5 %collective-permute-start.32 = (bf16[2,64,512]{2,1,0:T(8,128)(2,1)S(1)}, bf16[2,64,512]{2,1,0:T(8,128)(2,1)S(1)}, u32[]{:S(2)}, u32[]{:S(2)}) collective-permute-start(bf16[2,64,512]{2,1,0:T(8,128)(2,1)S(1)} %slice.258), channel_id=1, source_target_pairs={{0,4},{1,5},{2,6},{3,7},{4,0},{5,1},{6,2},{7,3},{8,12},{9,13},{10,... | collective-permute-start | bytes 393224 | tf_op jit(solution)/shard_map/ppermute | solution.py:628
  135.3 2.0 %collective-permute-done.30.refs_4_ = bf16[4,512,128]{2,1,0:T(8,128)(2,1)S(1)} collective-permute-done((bf16[4,512,128]{2,1,0:T(8,128)(2,1)S(1)}, bf16[4,512,128]{2,1,0:T(8,128)(2,1)S(1)}, u32[]{:S(2)}, u32[]{:S(2)}) %collective-permute-start.30) | collective-permute-done | bytes 524320 | tf_op jit(solution)/shard_map/ppermute | solution.py:628
  137.3 3.1 %place.3 = (f32[2048,512]{1,0:T(8,128)}, f32[512,2048]{1,0:T(8,128)}) custom-call(s32[16]{0:T(128)S(1)} %get-tuple-element.316.info, bf16[2,512,128]{2,1,0:T(8,128)(2,1)S(1)} %collective-permute-done.25.refs_0_, bf16[2,512,128]{2,1,0:T(8,128)(2,1)S(1)} %collective-permute-done.26.refs_1_, ...), custom_call_target="tpu_custom_call", output_to_operand_aliasing={{0}: (6, {}), {1}: (7, {})} | custom-call | tf_op jit(solution)/shard_map/place/pallas_call | solution.py:571
  140.6 2.8 %sort.2 = (f32[512,512]{1,0:T(8,128)}, f32[512,512]{1,0:T(8,128)}, f32[512,512]{1,0:T(8,128)}, f32[512,512]{1,0:T(8,128)}) custom-call(s32[16]{0:T(128)S(1)} %get-tuple-element.316.info, bf16[4,64,512]{2,1,0:T(8,128)(2,1)S(1)} %pad_maximum_fusion.10.refs_0_, bf16[4,64,512]{2,1,0:T(8,128)(2,1)S(1)} %collective-permute-done.27.refs_1_, ...), custom_call_target="tpu_custom_call" | custom-call | tf_op jit(solution)/shard_map/sort/pallas_call | solution.py:605
  (131 shorter events, 23.3 us)
Async XLA Ops:
  2.4 9.5 %collective-permute-start = (bf16[256,512]{1,0:T(8,128)(2,1)S(1)}, bf16[256,512]{1,0:T(8,128)(2,1)S(1)}, u32[]{:S(2)}, u32[]{:S(2)}) collective-permute-start(bf16[256,512]{1,0:T(8,128)(2,1)S(1)} %get-tuple-element.172), channel_id=1, source_target_pairs={{0,2},{1,3},{2,0},{3,1},{4,6},{5,7},{6,4},{7,5},{8,10},{9,11},{10,... | collective-permute-start | bytes 786440 | tf_op jit(solution)/shard_map/ppermute | solution.py:628
  35.5 5.2 %collective-permute-start.3 = (bf16[16,512,128]{2,1,0:T(8,128)(2,1)S(1)}, bf16[16,512,128]{2,1,0:T(8,128)(2,1)S(1)}, u32[]{:S(2)}, u32[]{:S(2)}) collective-permute-start(bf16[16,512,128]{2,1,0:T(8,128)(2,1)S(1)} %get-tuple-element.192), channel_id=1, source_target_pairs={{0,1},{1,0},{2,3},{3,2},{4,5},{5,4},{6,7},{7,6},{8,9},{9,8},{10,11... | collective-permute-start | bytes 6291464 | tf_op jit(solution)/shard_map/ppermute | solution.py:628
  44.3 23.6 %collective-permute-start.4 = (bf16[4,512,128]{2,1,0:T(8,128)(2,1)S(1)}, bf16[4,512,128]{2,1,0:T(8,128)(2,1)S(1)}, u32[]{:S(2)}, u32[]{:S(2)}) collective-permute-start(bf16[4,512,128]{2,1,0:T(8,128)(2,1)S(1)} %get-tuple-element.215), channel_id=1, source_target_pairs={{0,2},{1,3},{2,0},{3,1},{4,6},{5,7},{6,4},{7,5},{8,10},{9,11},{10,... | collective-permute-start | bytes 1572872 | tf_op jit(solution)/shard_map/ppermute | solution.py:628
  46.2 21.8 %collective-permute-start.5 = (bf16[4,512,128]{2,1,0:T(8,128)(2,1)S(1)}, bf16[4,512,128]{2,1,0:T(8,128)(2,1)S(1)}, u32[]{:S(2)}, u32[]{:S(2)}) collective-permute-start(bf16[4,512,128]{2,1,0:T(8,128)(2,1)S(1)} %get-tuple-element.216), channel_id=1, source_target_pairs={{0,4},{1,5},{2,6},{3,7},{4,0},{5,1},{6,2},{7,3},{8,12},{9,13},{10,... | collective-permute-start | bytes 1572872 | tf_op jit(solution)/shard_map/ppermute | solution.py:628
  47.6 23.2 %collective-permute-start.6 = (bf16[4,512,128]{2,1,0:T(8,128)(2,1)S(1)}, bf16[4,512,128]{2,1,0:T(8,128)(2,1)S(1)}, u32[]{:S(2)}, u32[]{:S(2)}) collective-permute-start(bf16[4,512,128]{2,1,0:T(8,128)(2,1)S(1)} %get-tuple-element.217), channel_id=1, source_target_pairs={{0,6},{1,7},{2,4},{3,5},{4,2},{5,3},{6,0},{7,1},{8,14},{9,15},{10,... | collective-permute-start | bytes 1572872 | tf_op jit(solution)/shard_map/ppermute | solution.py:628
  70.8 5.2 %collective-permute-start.7 = (bf16[1040,512]{1,0:T(8,128)(2,1)}, bf16[1040,512]{1,0:T(8,128)(2,1)S(1)}, u32[]{:S(2)}, u32[]{:S(2)}) collective-permute-start(bf16[1040,512]{1,0:T(8,128)(2,1)} %get-tuple-element.228), channel_id=1, source_target_pairs={{0,1},{1,0},{2,3},{3,2},{4,5},{5,4},{6,7},{7,6},{8,9},{9,8},{10,11... | collective-permute-start | bytes 3194888 | tf_op jit(solution)/shard_map/ppermute | solution.py:628
  70.8 5.2 %collective-permute-start.8 = (bf16[528,512]{1,0:T(8,128)(2,1)S(1)}, bf16[528,512]{1,0:T(8,128)(2,1)S(1)}, u32[]{:S(2)}, u32[]{:S(2)}) collective-permute-start(bf16[528,512]{1,0:T(8,128)(2,1)S(1)} %get-tuple-element.229), channel_id=1, source_target_pairs={{0,1},{1,0},{2,3},{3,2},{4,5},{5,4},{6,7},{7,6},{8,9},{9,8},{10,11... | collective-permute-start | bytes 1622024 | tf_op jit(solution)/shard_map/ppermute | solution.py:628
  71.6 8.1 %collective-permute-start.9 = (bf16[512,128]{1,0:T(8,128)(2,1)S(1)}, bf16[512,128]{1,0:T(8,128)(2,1)S(1)}, u32[]{:S(2)}, u32[]{:S(2)}) collective-permute-start(bf16[512,128]{1,0:T(8,128)(2,1)S(1)} %get-tuple-element.235), channel_id=1, source_target_pairs={{0,8},{1,9},{2,10},{3,11},{4,12},{5,13},{6,14},{7,15},{8,0},{9,1},... | collective-permute-start | bytes 393224 | tf_op jit(solution)/shard_map/ppermute | solution.py:628
  73.4 12.9 %collective-permute-start.10 = (bf16[512,128]{1,0:T(8,128)(2,1)S(1)}, bf16[512,128]{1,0:T(8,128)(2,1)S(1)}, u32[]{:S(2)}, u32[]{:S(2)}) collective-permute-start(bf16[512,128]{1,0:T(8,128)(2,1)S(1)} %get-tuple-element.236), channel_id=1, source_target_pairs={{0,16},{1,17},{2,18},{3,19},{4,20},{5,21},{6,22},{7,23},{8,24},{9,... | collective-permute-start | bytes 393224 | tf_op jit(solution)/shard_map/ppermute | solution.py:628
  76.0 10.3 %collective-permute-start.11 = (bf16[512,128]{1,0:T(8,128)(2,1)S(1)}, bf16[512,128]{1,0:T(8,128)(2,1)S(1)}, u32[]{:S(2)}, u32[]{:S(2)}) collective-permute-start(bf16[512,128]{1,0:T(8,128)(2,1)S(1)} %get-tuple-element.237), channel_id=1, source_target_pairs={{0,24},{1,25},{2,26},{3,27},{4,28},{5,29},{6,30},{7,31},{8,16},{9,... | collective-permute-start | bytes 393224 | tf_op jit(solution)/shard_map/ppermute | solution.py:628
  76.5 13.5 %collective-permute-start.12 = (bf16[272,512]{1,0:T(8,128)(2,1)S(1)}, bf16[272,512]{1,0:T(8,128)(2,1)S(1)}, u32[]{:S(2)}, u32[]{:S(2)}) collective-permute-start(bf16[272,512]{1,0:T(8,128)(2,1)S(1)} %get-tuple-element.248), channel_id=1, source_target_pairs={{0,2},{1,3},{2,0},{3,1},{4,6},{5,7},{6,4},{7,5},{8,10},{9,11},{10,... | collective-permute-start | bytes 835592 | tf_op jit(solution)/shard_map/ppermute | solution.py:628
  78.2 12.6 %collective-permute-start.13 = (bf16[272,512]{1,0:T(8,128)(2,1)S(1)}, bf16[272,512]{1,0:T(8,128)(2,1)S(1)}, u32[]{:S(2)}, u32[]{:S(2)}) collective-permute-start(bf16[272,512]{1,0:T(8,128)(2,1)S(1)} %get-tuple-element.249), channel_id=1, source_target_pairs={{0,4},{1,5},{2,6},{3,7},{4,0},{5,1},{6,2},{7,3},{8,12},{9,13},{10,... | collective-permute-start | bytes 835592 | tf_op jit(solution)/shard_map/ppermute | solution.py:628
  79.7 12.7 %collective-permute-start.14 = (bf16[272,512]{1,0:T(8,128)(2,1)S(1)}, bf16[272,512]{1,0:T(8,128)(2,1)S(1)}, u32[]{:S(2)}, u32[]{:S(2)}) collective-permute-start(bf16[272,512]{1,0:T(8,128)(2,1)S(1)} %get-tuple-element.250), channel_id=1, source_target_pairs={{0,6},{1,7},{2,4},{3,5},{4,2},{5,3},{6,0},{7,1},{8,14},{9,15},{10,... | collective-permute-start | bytes 835592 | tf_op jit(solution)/shard_map/ppermute | solution.py:628
  86.4 14.9 %collective-permute-start.18 = (bf16[512,128]{1,0:T(8,128)(2,1)S(1)}, bf16[512,128]{1,0:T(8,128)(2,1)S(1)}, u32[]{:S(2)}, u32[]{:S(2)}) collective-permute-start(bf16[512,128]{1,0:T(8,128)(2,1)S(1)} %add_convert_fusion.2), channel_id=1, source_target_pairs={{0,24},{1,25},{2,26},{3,27},{4,28},{5,29},{6,30},{7,31},{8,16},{9,... | collective-permute-start | bytes 393224 | tf_op jit(solution)/shard_map/ppermute | solution.py:628
  88.8 12.4 %collective-permute-start.17 = (bf16[512,128]{1,0:T(8,128)(2,1)S(1)}, bf16[512,128]{1,0:T(8,128)(2,1)S(1)}, u32[]{:S(2)}, u32[]{:S(2)}) collective-permute-start(bf16[512,128]{1,0:T(8,128)(2,1)S(1)} %add_convert_fusion.2), channel_id=1, source_target_pairs={{0,16},{1,17},{2,18},{3,19},{4,20},{5,21},{6,22},{7,23},{8,24},{9,... | collective-permute-start | bytes 393224 | tf_op jit(solution)/shard_map/ppermute | solution.py:628
  90.0 11.2 %collective-permute-start.16 = (bf16[512,128]{1,0:T(8,128)(2,1)S(1)}, bf16[512,128]{1,0:T(8,128)(2,1)S(1)}, u32[]{:S(2)}, u32[]{:S(2)}) collective-permute-start(bf16[512,128]{1,0:T(8,128)(2,1)S(1)} %add_convert_fusion.2), channel_id=1, source_target_pairs={{0,8},{1,9},{2,10},{3,11},{4,12},{5,13},{6,14},{7,15},{8,0},{9,1},... | collective-permute-start | bytes 393224 | tf_op jit(solution)/shard_map/ppermute | solution.py:628
  90.8 10.4 %collective-permute-start.19 = (bf16[272,512]{1,0:T(8,128)(2,1)S(1)}, bf16[272,512]{1,0:T(8,128)(2,1)S(1)}, u32[]{:S(2)}, u32[]{:S(2)}) collective-permute-start(bf16[272,512]{1,0:T(8,128)(2,1)S(1)} %get-tuple-element.260), channel_id=1, source_target_pairs={{0,2},{1,3},{2,0},{3,1},{4,6},{5,7},{6,4},{7,5},{8,10},{9,11},{10,... | collective-permute-start | bytes 835592 | tf_op jit(solution)/shard_map/ppermute | solution.py:628
  92.7 8.4 %collective-permute-start.15 = (bf16[144,512]{1,0:T(8,128)(2,1)S(1)}, bf16[144,512]{1,0:T(8,128)(2,1)S(1)}, u32[]{:S(2)}, u32[]{:S(2)}) collective-permute-start(bf16[144,512]{1,0:T(8,128)(2,1)S(1)} %pad_maximum_fusion.12), channel_id=1, source_target_pairs={{0,8},{1,9},{2,10},{3,11},{4,12},{5,13},{6,14},{7,15},{8,0},{9,1},... | collective-permute-start | bytes 442376 | tf_op jit(solution)/shard_map/ppermute | solution.py:628
  101.4 11.9 %collective-permute-start.22 = (bf16[4,512,128]{2,1,0:T(8,128)(2,1)S(1)}, bf16[4,512,128]{2,1,0:T(8,128)(2,1)S(1)}, u32[]{:S(2)}, u32[]{:S(2)}) collective-permute-start(bf16[4,512,128]{2,1,0:T(8,128)(2,1)S(1)} %pad_maximum_fusion.2.refs_0_), channel_id=1, source_target_pairs={{0,4},{1,5},{2,6},{3,7},{4,0},{5,1},{6,2},{7,3},{8,12},{9,13},{10,... | collective-permute-start | bytes 1572872 | tf_op jit(solution)/shard_map/ppermute | solution.py:628
  103.0 10.8 %collective-permute-start.21 = (bf16[4,512,128]{2,1,0:T(8,128)(2,1)S(1)}, bf16[4,512,128]{2,1,0:T(8,128)(2,1)S(1)}, u32[]{:S(2)}, u32[]{:S(2)}) collective-permute-start(bf16[4,512,128]{2,1,0:T(8,128)(2,1)S(1)} %pad_maximum_fusion.2.refs_0_), channel_id=1, source_target_pairs={{0,2},{1,3},{2,0},{3,1},{4,6},{5,7},{6,4},{7,5},{8,10},{9,11},{10,... | collective-permute-start | bytes 1572872 | tf_op jit(solution)/shard_map/ppermute | solution.py:628
  104.5 7.5 %collective-permute-start.20 = (bf16[144,512]{1,0:T(8,128)(2,1)S(1)}, bf16[144,512]{1,0:T(8,128)(2,1)S(1)}, u32[]{:S(2)}, u32[]{:S(2)}) collective-permute-start(bf16[144,512]{1,0:T(8,128)(2,1)S(1)} %pad_maximum_fusion.13), channel_id=1, source_target_pairs={{0,16},{1,17},{2,18},{3,19},{4,20},{5,21},{6,22},{7,23},{8,24},{9,... | collective-permute-start | bytes 442376 | tf_op jit(solution)/shard_map/ppermute | solution.py:628
  112.7 5.0 %collective-permute-start.23 = (bf16[128,512]{1,0:T(8,128)(2,1)S(1)}, bf16[128,512]{1,0:T(8,128)(2,1)S(1)}, u32[]{:S(2)}, u32[]{:S(2)}) collective-permute-start(bf16[128,512]{1,0:T(8,128)(2,1)S(1)} %add_convert_fusion), channel_id=1, source_target_pairs={{0,8},{1,9},{2,10},{3,11},{4,12},{5,13},{6,14},{7,15},{8,0},{9,1},... | collective-permute-start | bytes 393224 | tf_op jit(solution)/shard_map/ppermute | solution.py:628
  117.8 14.7 %collective-permute-start.24 = (bf16[4,512,128]{2,1,0:T(8,128)(2,1)S(1)}, bf16[4,512,128]{2,1,0:T(8,128)(2,1)S(1)}, u32[]{:S(2)}, u32[]{:S(2)}) collective-permute-start(bf16[4,512,128]{2,1,0:T(8,128)(2,1)S(1)} %pad_maximum_fusion.2.refs_0_), channel_id=1, source_target_pairs={{0,1},{1,0},{2,3},{3,2},{4,5},{5,4},{6,7},{7,6},{8,9},{9,8},{10,11... | collective-permute-start | bytes 1572872 | tf_op jit(solution)/shard_map/ppermute | solution.py:628
  117.8 9.2 %collective-permute-start.28 = (bf16[4,64,512]{2,1,0:T(8,128)(2,1)S(1)}, bf16[4,64,512]{2,1,0:T(8,128)(2,1)S(1)}, u32[]{:S(2)}, u32[]{:S(2)}) collective-permute-start(bf16[4,64,512]{2,1,0:T(8,128)(2,1)S(1)} %pad_maximum_fusion.10.refs_0_), channel_id=1, source_target_pairs={{0,4},{1,5},{2,6},{3,7},{4,0},{5,1},{6,2},{7,3},{8,12},{9,13},{10,... | collective-permute-start | bytes 786440 | tf_op jit(solution)/shard_map/ppermute | solution.py:628
  118.5 9.2 %collective-permute-start.27 = (bf16[4,64,512]{2,1,0:T(8,128)(2,1)S(1)}, bf16[4,64,512]{2,1,0:T(8,128)(2,1)S(1)}, u32[]{:S(2)}, u32[]{:S(2)}) collective-permute-start(bf16[4,64,512]{2,1,0:T(8,128)(2,1)S(1)} %pad_maximum_fusion.10.refs_0_), channel_id=1, source_target_pairs={{0,2},{1,3},{2,0},{3,1},{4,6},{5,7},{6,4},{7,5},{8,10},{9,11},{10,... | collective-permute-start | bytes 786440 | tf_op jit(solution)/shard_map/ppermute | solution.py:628
  118.9 13.5 %collective-permute-start.25 = (bf16[2,512,128]{2,1,0:T(8,128)(2,1)S(1)}, bf16[2,512,128]{2,1,0:T(8,128)(2,1)S(1)}, u32[]{:S(2)}, u32[]{:S(2)}) collective-permute-start(bf16[2,512,128]{2,1,0:T(8,128)(2,1)S(1)} %slice.251), channel_id=1, source_target_pairs={{0,2},{1,3},{2,0},{3,1},{4,6},{5,7},{6,4},{7,5},{8,10},{9,11},{10,... | collective-permute-start | bytes 786440 | tf_op jit(solution)/shard_map/ppermute | solution.py:628
  120.5 12.0 %collective-permute-start.26 = (bf16[2,512,128]{2,1,0:T(8,128)(2,1)S(1)}, bf16[2,512,128]{2,1,0:T(8,128)(2,1)S(1)}, u32[]{:S(2)}, u32[]{:S(2)}) collective-permute-start(bf16[2,512,128]{2,1,0:T(8,128)(2,1)S(1)} %slice.252), channel_id=1, source_target_pairs={{0,4},{1,5},{2,6},{3,7},{4,0},{5,1},{6,2},{7,3},{8,12},{9,13},{10,... | collective-permute-start | bytes 786440 | tf_op jit(solution)/shard_map/ppermute | solution.py:628
  132.7 4.6 %collective-permute-start.29 = (bf16[8,512,128]{2,1,0:T(8,128)(2,1)S(1)}, bf16[8,512,128]{2,1,0:T(8,128)(2,1)S(1)}, u32[]{:S(2)}, u32[]{:S(2)}) collective-permute-start(bf16[8,512,128]{2,1,0:T(8,128)(2,1)S(1)} %pad_maximum_fusion), channel_id=1, source_target_pairs={{0,1},{1,0},{2,3},{3,2},{4,5},{5,4},{6,7},{7,6},{8,9},{9,8},{10,11... | collective-permute-start | bytes 3145736 | tf_op jit(solution)/shard_map/ppermute | solution.py:628
  132.8 7.6 %collective-permute-start.33 = (bf16[12,64,512]{2,1,0:T(8,128)(2,1)S(1)}, bf16[12,64,512]{2,1,0:T(8,128)(2,1)S(1)}, u32[]{:S(2)}, u32[]{:S(2)}) collective-permute-start(bf16[12,64,512]{2,1,0:T(8,128)(2,1)S(1)} %pad_maximum_fusion.1), channel_id=1, source_target_pairs={{0,1},{1,0},{2,3},{3,2},{4,5},{5,4},{6,7},{7,6},{8,9},{9,8},{10,11... | collective-permute-start | bytes 2359304 | tf_op jit(solution)/shard_map/ppermute | solution.py:628
  133.3 4.0 %collective-permute-start.30 = (bf16[4,512,128]{2,1,0:T(8,128)(2,1)S(1)}, bf16[4,512,128]{2,1,0:T(8,128)(2,1)S(1)}, u32[]{:S(2)}, u32[]{:S(2)}) collective-permute-start(bf16[4,512,128]{2,1,0:T(8,128)(2,1)S(1)} %pad_maximum_fusion.3), channel_id=1, source_target_pairs={{0,1},{1,0},{2,3},{3,2},{4,5},{5,4},{6,7},{7,6},{8,9},{9,8},{10,11... | collective-permute-start | bytes 1572872 | tf_op jit(solution)/shard_map/ppermute | solution.py:628
  133.3 7.0 %collective-permute-start.31 = (bf16[2,64,512]{2,1,0:T(8,128)(2,1)S(1)}, bf16[2,64,512]{2,1,0:T(8,128)(2,1)S(1)}, u32[]{:S(2)}, u32[]{:S(2)}) collective-permute-start(bf16[2,64,512]{2,1,0:T(8,128)(2,1)S(1)} %slice.257), channel_id=1, source_target_pairs={{0,2},{1,3},{2,0},{3,1},{4,6},{5,7},{6,4},{7,5},{8,10},{9,11},{10,... | collective-permute-start | bytes 393224 | tf_op jit(solution)/shard_map/ppermute | solution.py:628
  133.8 6.6 %collective-permute-start.32 = (bf16[2,64,512]{2,1,0:T(8,128)(2,1)S(1)}, bf16[2,64,512]{2,1,0:T(8,128)(2,1)S(1)}, u32[]{:S(2)}, u32[]{:S(2)}) collective-permute-start(bf16[2,64,512]{2,1,0:T(8,128)(2,1)S(1)} %slice.258), channel_id=1, source_target_pairs={{0,4},{1,5},{2,6},{3,7},{4,0},{5,1},{6,2},{7,3},{8,12},{9,13},{10,... | collective-permute-start | bytes 393224 | tf_op jit(solution)/shard_map/ppermute | solution.py:628
  (23 other events, 177.7 us)

commit v10 on v9

--- a/solution.py
+++ b/solution.py
@@ -740,25 +740,29 @@
     token, from_y, from_x, outs = wait(token, from_y, from_x, outs)
 
     sends = [from_x[:2], from_y[2:]]
-    token, sends, rest_back = wait(token, sends, rest_back)
+    here = jnp.concatenate([quarter, from_y, from_x])
+    token, sends, here = wait(token, sends, here)
     far_a, far_b = exchange(sends[0], ROW), exchange(sends[1], NEAR_X)
+    other = exchange(here, CORE)
+    grads = place(token, [(0, here)], [], width)
+    token, grads, rest_back, far_a, far_b, other = wait(token, grads, rest_back, far_a, far_b, other)
+
     fourth = jnp.stack([rest[:piece], rest_back[:piece], rest[piece:], rest_back[piece:]])
-    token, fourth, quarter = wait(token, fourth, quarter)
+    far_pair = jnp.concatenate([far_a, far_b])
+    token, fourth, far_pair = wait(token, fourth, far_pair)
     fourth_y, fourth_x = exchange(fourth, ROW), exchange(fourth, NEAR_X)
-    other = exchange(quarter, CORE)
-    near_pair = jnp.concatenate([from_y, from_x])
-    grads = place(token, [(0, quarter), (4, from_y), (8, from_x)], [], width)
-    token, grads, other, near_pair, far_a, far_b, fourth_y, fourth_x = wait(token, grads, other, near_pair, far_a, far_b, fourth_y, fourth_x)
-
-    sends = [fourth_x[:2], fourth_y[2:], near_pair, jnp.concatenate([far_a, far_b]), jnp.concatenate([fourth, fourth_y, fourth_x])]
+    other_far = exchange(far_pair, CORE)
+    grads = place(token, [(12, far_pair), (16, other)], grads, width)
+    token, grads, other_far, fourth_y, fourth_x = wait(token, grads, other_far, fourth_y, fourth_x)
+
+    sends = [fourth_x[:2], fourth_y[2:], jnp.concatenate([fourth, fourth_y, fourth_x])]
     token, sends = wait(token, sends)
-    last_a, last_b, other_near, other_far, pair = (exchange(s, m) for s, m in zip(sends, (ROW, NEAR_X, CORE, CORE, CORE)))
-    token, other_near, other_far = wait(token, other_near, other_far)
-    out_back, out_in = place(token, [(12, far_a), (14, far_b), (16, other), (20, other_near), (28, other_far)], grads, width)
+    last_a, last_b, pair = (exchange(s, m) for s, m in zip(sends, (ROW, NEAR_X, CORE)))
+    out_back, out_in = place(token, [(28, other_far)], grads, width)
     token, out_back, out_in, last_a, last_b, pair = wait(token, out_back, out_in, last_a, last_b, pair)
 
     ends = exchange(jnp.concatenate([last_a, last_b]), CORE)
-    made = sort(token, [(0, fourth), (4, fourth_y), (8, fourth_x), (12, last_a), (14, last_b), (16, pair)], [], width)
+    made = sort(token, [(0, sends[2]), (12, last_a), (14, last_b), (16, pair)], [], width)
     token, made, ends = wait(token, made, ends)
     out_out, out_query, out_key, out_value = sort(token, [(28, ends)], made, width)
     return (pooled, input_grad, out_query, out_key, out_value, out_out, out_in, out_back, *outs)

time: 145 us -> 144 us (level)
  waiting for transfers between devices: 34.7 us -> 33.2 us
    ppermute x35 -> x34, waiting for transfers between devices: 34.7 us -> 33.2 us  [exchange(): lax.ppermute(value, ('dp', 'blk'), [(i, i ^ bits) for i in range(size)])]
    pallas_call x2 -> x3, Pallas kernels: 5.38 us -> 6.58 us  [place(): pl.pallas_call(functools.partial(place_kernel, [first for first, _ in par...]
    ppermute x35 -> x34, starting transfers between devices: 35.6 us -> 34.9 us  [exchange(): lax.ppermute(value, ('dp', 'blk'), [(i, i ^ bits) for i in range(size)])]
  transfers between devices with their start and end apart: 35 -> 34, of which waited for: 12 -> 14; matrix products, arithmetic and copies ran while one was open for 3% -> 3% of each run, Pallas kernels for 26% -> 27%
where the time goes in v10:
time: 144 us
  Pallas kernels  65.4 us (45%)
  starting transfers between devices  34.9 us (24%)
  waiting for transfers between devices  33.2 us (23%)
  local copies, waits for them, and re-layouts  5.46 us (4%)
  other arithmetic  3.75 us (3%)
  between operations  1.45 us (1%)
    ppermute x34, starting transfers between devices, exchange(): lax.ppermute(value, ('dp', 'blk'), [(i, i ^ bits) for i in range(size)])  34.9 us
    ppermute x34, waiting for transfers between devices, exchange(): lax.ppermute(value, ('dp', 'blk'), [(i, i ^ bits) for i in range(size)])  33.2 us
    pallas_call x1, Pallas kernels, front(): pl.pallas_call(front_kernel, grid=(heads // 2,), in_specs=[smem] + [whole...  22 us
    pallas_call x1, Pallas kernels, back(): pl.pallas_call(back_kernel, grid=(width // 128,), in_specs=[smem, col(cou...  20.1 us
    pallas_call x3, Pallas kernels, place(): pl.pallas_call(functools.partial(place_kernel, [first for first, _ in par...  6.58 us
    pallas_call x1, Pallas kernels, through(): pl.pallas_call(through_kernel, in_specs=[smem, free, pl.BlockSpec(memory_...  4.85 us
    pallas_call x2, Pallas kernels, sort(): pl.pallas_call(functools.partial(sort_kernel, [first for first, _ in part...  4.23 us
    unnamed x40, local copies, waits for them, and re-layouts  3.88 us
  transfers between devices with their start and end apart: 34, of which 14 were waited for; matrix products, arithmetic and copies ran while one was open for 3% of the time, Pallas kernels for 27%

profile of v10, /device:TPU:0, one launch (start us, length us, event | category | flops | bytes accessed | tf_op | source)
XLA Modules:
  0.0 144.1 jit_solution(1956559924165561575)
XLA Ops:
  2.4 2.6 %collective-permute-start = (bf16[256,512]{1,0:T(8,128)(2,1)S(1)}, bf16[256,512]{1,0:T(8,128)(2,1)S(1)}, u32[]{:S(2)}, u32[]{:S(2)}) collective-permute-start(bf16[256,512]{1,0:T(8,128)(2,1)S(1)} %get-tuple-element.173), channel_id=1, source_target_pairs={{0,2},{1,3},{2,0},{3,1},{4,6},{5,7},{6,4},{7,5},{8,10},{9,11},{10,... | collective-permute-start | bytes 786440 | tf_op jit(solution)/shard_map/ppermute | solution.py:628
  8.8 1.5 %prepare.1 = (bf16[512,512]{1,0:T(8,128)(2,1)S(1)}, bf16[256,512]{1,0:T(8,128)(2,1)S(1)}, bf16[512,512]{1,0:T(8,128)(2,1)S(1)}, bf16[512,512]{1,0:T(8,128)(2,1)S...) custom-call(bf16[256,512]{1,0:T(8,128)(2,1)S(1)} %get-tuple-element.174.mine.near.near, ...), custom_call_target="tpu_custom_call" | custom-call | tf_op jit(solution)/shard_map/prepare/pallas_call | solution.py:65
  10.4 1.5 %collective-permute-done.far.far_h = bf16[256,512]{1,0:T(8,128)(2,1)S(1)} collective-permute-done((bf16[256,512]{1,0:T(8,128)(2,1)S(1)}, bf16[256,512]{1,0:T(8,128)(2,1)S(1)}, u32[]{:S(2)}, u32[]{:S(2)}) %collective-permute-start) | collective-permute-done | bytes 262176 | tf_op jit(solution)/shard_map/ppermute | solution.py:628
  13.5 22.0 %front.1 = (bf16[512,512]{1,0:T(8,128)(2,1)S(1)}, bf16[256,512]{1,0:T(8,128)(2,1)S(1)}, bf16[512,512]{1,0:T(8,128)(2,1)S(1)}, bf16[512,512]{1,0:T(8,128)(2,1)S(1...) custom-call(s32[16]{0:T(128)S(1)} %get-tuple-element.318.info, ...), custom_call_target="tpu_custom_call" | custom-call | tf_op jit(solution)/shard_map/front/pallas_call | solution.py:254
  35.8 4.8 %through.1 = (f32[512,512]{1,0:T(8,128)S(1)}, bf16[512,512]{1,0:T(8,128)(2,1)S(1)}, bf16[512,512]{1,0:T(8,128)(2,1)S(1)}, f32[8,512]{1,0:T(8,128)S(1)}) custom-call(s32[16]{0:T(128)S(1)} %get-tuple-element.318.info, bf16[512,2048]{1,0:T(8,128)(2,1)S(1)} %get-tuple-element.188.slopes_h, bf16[512,2048]{1,0:T(8,128)(2,1)S(1)} %copy-done, ...), custom_call_target="tpu_custom_call" | custom-call | tf_op jit(solution)/shard_map/through/pallas_call | solution.py:311
  40.7 3.6 %meet.1 = (bf16[4,512,128]{2,1,0:T(8,128)(2,1)S(1)}, bf16[4,512,128]{2,1,0:T(8,128)(2,1)S(1)}, bf16[4,512,128]{2,1,0:T(8,128)(2,1)S(1)}, bf16[4,512,128]{2,1,0:T(8,128)(2,1)S(1)}) custom-call(s32[16]{0:T(128)S(1)} %get-tuple-element.318.info, bf16[16,512,128]{2,1,0:T(8,128)(2,1)S(1)} %collective-permute-done.3.got_h, ...), custom_call_target="tpu_custom_call" | custom-call | tf_op jit(solution)/shard_map/meet/pallas_call | solution.py:361
  44.3 1.8 %collective-permute-start.4 = (bf16[4,512,128]{2,1,0:T(8,128)(2,1)S(1)}, bf16[4,512,128]{2,1,0:T(8,128)(2,1)S(1)}, u32[]{:S(2)}, u32[]{:S(2)}) collective-permute-start(bf16[4,512,128]{2,1,0:T(8,128)(2,1)S(1)} %get-tuple-element.216), channel_id=1, source_target_pairs={{0,2},{1,3},{2,0},{3,1},{4,6},{5,7},{6,4},{7,5},{8,10},{9,11},{10,... | collective-permute-start | bytes 1572872 | tf_op jit(solution)/shard_map/ppermute | solution.py:628
  46.2 1.5 %collective-permute-start.5 = (bf16[4,512,128]{2,1,0:T(8,128)(2,1)S(1)}, bf16[4,512,128]{2,1,0:T(8,128)(2,1)S(1)}, u32[]{:S(2)}, u32[]{:S(2)}) collective-permute-start(bf16[4,512,128]{2,1,0:T(8,128)(2,1)S(1)} %get-tuple-element.217), channel_id=1, source_target_pairs={{0,4},{1,5},{2,6},{3,7},{4,0},{5,1},{6,2},{7,3},{8,12},{9,13},{10,... | collective-permute-start | bytes 1572872 | tf_op jit(solution)/shard_map/ppermute | solution.py:628
  47.9 20.1 %back.1 = (bf16[16,64,512]{2,1,0:T(8,128)(2,1)S(1)}, bf16[1040,512]{1,0:T(8,128)(2,1)}, f32[512,512]{1,0:T(8,128)}, bf16[528,512]{1,0:T(8,128)(2,1)S(1)}, f32[8,512]{1,0:T(8,128)S(1)}) custom-call(s32[16]{0:T(128)S(1)} %get-tuple-element.318.info, bf16[256,512]{1,0:T(8,128)(2,1)S(1)} %get-tuple-element.179.q_l.ql, ...), custom_call_target="tpu_custom_call" | custom-call | tf_op jit(solution)/shard_map/back/pallas_call | solution.py:504
  68.0 2.9 %collective-permute-done.6.refs_3_ = bf16[4,512,128]{2,1,0:T(8,128)(2,1)S(1)} collective-permute-done((bf16[4,512,128]{2,1,0:T(8,128)(2,1)S(1)}, bf16[4,512,128]{2,1,0:T(8,128)(2,1)S(1)}, u32[]{:S(2)}, u32[]{:S(2)}) %collective-permute-start.6) | collective-permute-done | bytes 524320 | tf_op jit(solution)/shard_map/ppermute | solution.py:628
  71.6 1.8 %collective-permute-start.9 = (bf16[512,128]{1,0:T(8,128)(2,1)S(1)}, bf16[512,128]{1,0:T(8,128)(2,1)S(1)}, u32[]{:S(2)}, u32[]{:S(2)}) collective-permute-start(bf16[512,128]{1,0:T(8,128)(2,1)S(1)} %get-tuple-element.236), channel_id=1, source_target_pairs={{0,8},{1,9},{2,10},{3,11},{4,12},{5,13},{6,14},{7,15},{8,0},{9,1},... | collective-permute-start | bytes 393224 | tf_op jit(solution)/shard_map/ppermute | solution.py:628
  73.4 2.6 %collective-permute-start.10 = (bf16[512,128]{1,0:T(8,128)(2,1)S(1)}, bf16[512,128]{1,0:T(8,128)(2,1)S(1)}, u32[]{:S(2)}, u32[]{:S(2)}) collective-permute-start(bf16[512,128]{1,0:T(8,128)(2,1)S(1)} %get-tuple-element.237), channel_id=1, source_target_pairs={{0,16},{1,17},{2,18},{3,19},{4,20},{5,21},{6,22},{7,23},{8,24},{9,... | collective-permute-start | bytes 393224 | tf_op jit(solution)/shard_map/ppermute | solution.py:628
  76.5 1.7 %collective-permute-start.12 = (bf16[272,512]{1,0:T(8,128)(2,1)S(1)}, bf16[272,512]{1,0:T(8,128)(2,1)S(1)}, u32[]{:S(2)}, u32[]{:S(2)}) collective-permute-start(bf16[272,512]{1,0:T(8,128)(2,1)S(1)} %get-tuple-element.249), channel_id=1, source_target_pairs={{0,2},{1,3},{2,0},{3,1},{4,6},{5,7},{6,4},{7,5},{8,10},{9,11},{10,... | collective-permute-start | bytes 835592 | tf_op jit(solution)/shard_map/ppermute | solution.py:628
  78.2 1.5 %collective-permute-start.13 = (bf16[272,512]{1,0:T(8,128)(2,1)S(1)}, bf16[272,512]{1,0:T(8,128)(2,1)S(1)}, u32[]{:S(2)}, u32[]{:S(2)}) collective-permute-start(bf16[272,512]{1,0:T(8,128)(2,1)S(1)} %get-tuple-element.250), channel_id=1, source_target_pairs={{0,4},{1,5},{2,6},{3,7},{4,0},{5,1},{6,2},{7,3},{8,12},{9,13},{10,... | collective-permute-start | bytes 835592 | tf_op jit(solution)/shard_map/ppermute | solution.py:628
  79.7 1.7 %collective-permute-start.14 = (bf16[272,512]{1,0:T(8,128)(2,1)S(1)}, bf16[272,512]{1,0:T(8,128)(2,1)S(1)}, u32[]{:S(2)}, u32[]{:S(2)}) collective-permute-start(bf16[272,512]{1,0:T(8,128)(2,1)S(1)} %get-tuple-element.251), channel_id=1, source_target_pairs={{0,6},{1,7},{2,4},{3,5},{4,2},{5,3},{6,0},{7,1},{8,14},{9,15},{10,... | collective-permute-start | bytes 835592 | tf_op jit(solution)/shard_map/ppermute | solution.py:628
  82.5 3.8 %collective-permute-done.10 = bf16[512,128]{1,0:T(8,128)(2,1)S(1)} collective-permute-done((bf16[512,128]{1,0:T(8,128)(2,1)S(1)}, bf16[512,128]{1,0:T(8,128)(2,1)S(1)}, u32[]{:S(2)}, u32[]{:S(2)}) %collective-permute-start.10) | collective-permute-done | bytes 131104 | tf_op jit(solution)/shard_map/ppermute | solution.py:628
  86.4 2.5 %collective-permute-start.18 = (bf16[512,128]{1,0:T(8,128)(2,1)S(1)}, bf16[512,128]{1,0:T(8,128)(2,1)S(1)}, u32[]{:S(2)}, u32[]{:S(2)}) collective-permute-start(bf16[512,128]{1,0:T(8,128)(2,1)S(1)} %add_convert_fusion.2), channel_id=1, source_target_pairs={{0,24},{1,25},{2,26},{3,27},{4,28},{5,29},{6,30},{7,31},{8,16},{9,... | collective-permute-start | bytes 393224 | tf_op jit(solution)/shard_map/ppermute | solution.py:628
  90.8 1.5 %collective-permute-start.19 = (bf16[272,512]{1,0:T(8,128)(2,1)S(1)}, bf16[272,512]{1,0:T(8,128)(2,1)S(1)}, u32[]{:S(2)}, u32[]{:S(2)}) collective-permute-start(bf16[272,512]{1,0:T(8,128)(2,1)S(1)} %get-tuple-element.261), channel_id=1, source_target_pairs={{0,2},{1,3},{2,0},{3,1},{4,6},{5,7},{6,4},{7,5},{8,10},{9,11},{10,... | collective-permute-start | bytes 835592 | tf_op jit(solution)/shard_map/ppermute | solution.py:628
  94.0 7.1 %collective-permute-done.15 = bf16[144,512]{1,0:T(8,128)(2,1)S(1)} collective-permute-done((bf16[144,512]{1,0:T(8,128)(2,1)S(1)}, bf16[144,512]{1,0:T(8,128)(2,1)S(1)}, u32[]{:S(2)}, u32[]{:S(2)}) %collective-permute-start.15) | collective-permute-done | bytes 147488 | tf_op jit(solution)/shard_map/ppermute | solution.py:628
  101.4 1.6 %collective-permute-start.22 = (bf16[4,512,128]{2,1,0:T(8,128)(2,1)S(1)}, bf16[4,512,128]{2,1,0:T(8,128)(2,1)S(1)}, u32[]{:S(2)}, u32[]{:S(2)}) collective-permute-start(bf16[4,512,128]{2,1,0:T(8,128)(2,1)S(1)} %pad_maximum_fusion.2), channel_id=1, source_target_pairs={{0,4},{1,5},{2,6},{3,7},{4,0},{5,1},{6,2},{7,3},{8,12},{9,13},{10,... | collective-permute-start | bytes 1572872 | tf_op jit(solution)/shard_map/ppermute | solution.py:628
  103.0 1.5 %collective-permute-start.21 = (bf16[4,512,128]{2,1,0:T(8,128)(2,1)S(1)}, bf16[4,512,128]{2,1,0:T(8,128)(2,1)S(1)}, u32[]{:S(2)}, u32[]{:S(2)}) collective-permute-start(bf16[4,512,128]{2,1,0:T(8,128)(2,1)S(1)} %pad_maximum_fusion.2), channel_id=1, source_target_pairs={{0,2},{1,3},{2,0},{3,1},{4,6},{5,7},{6,4},{7,5},{8,10},{9,11},{10,... | collective-permute-start | bytes 1572872 | tf_op jit(solution)/shard_map/ppermute | solution.py:628
  104.5 1.4 collective-permute-start.20
  107.4 4.6 %collective-permute-done.20 = bf16[144,512]{1,0:T(8,128)(2,1)S(1)} collective-permute-done((bf16[144,512]{1,0:T(8,128)(2,1)S(1)}, bf16[144,512]{1,0:T(8,128)(2,1)S(1)}, u32[]{:S(2)}, u32[]{:S(2)}) %collective-permute-start.20) | collective-permute-done | bytes 147488 | tf_op jit(solution)/shard_map/ppermute | solution.py:628
  114.1 1.6 %collective-permute-start.24 = (bf16[2,512,128]{2,1,0:T(8,128)(2,1)S(1)}, bf16[2,512,128]{2,1,0:T(8,128)(2,1)S(1)}, u32[]{:S(2)}, u32[]{:S(2)}) collective-permute-start(bf16[2,512,128]{2,1,0:T(8,128)(2,1)S(1)} %slice.251), channel_id=1, source_target_pairs={{0,2},{1,3},{2,0},{3,1},{4,6},{5,7},{6,4},{7,5},{8,10},{9,11},{10,... | collective-permute-start | bytes 786440 | tf_op jit(solution)/shard_map/ppermute | solution.py:628
  116.9 2.3 %place.3 = (f32[2048,512]{1,0:T(8,128)}, f32[512,2048]{1,0:T(8,128)}) custom-call(s32[16]{0:T(128)S(1)} %get-tuple-element.318.info, bf16[12,512,128]{2,1,0:T(8,128)(2,1)S(1)} %pad_maximum_fusion.refs_0_), custom_call_target="tpu_custom_call" | custom-call | tf_op jit(solution)/shard_map/place/pallas_call | solution.py:571
  119.2 2.3 %collective-permute-done.23 = bf16[128,512]{1,0:T(8,128)(2,1)S(1)} collective-permute-done((bf16[128,512]{1,0:T(8,128)(2,1)S(1)}, bf16[128,512]{1,0:T(8,128)(2,1)S(1)}, u32[]{:S(2)}, u32[]{:S(2)}) %collective-permute-start.23) | collective-permute-done | bytes 131104 | tf_op jit(solution)/shard_map/ppermute | solution.py:628
  125.3 2.7 %place.4 = (f32[2048,512]{1,0:T(8,128)}, f32[512,2048]{1,0:T(8,128)}) custom-call(s32[16]{0:T(128)S(1)} %get-tuple-element.318.info, bf16[4,512,128]{2,1,0:T(8,128)(2,1)S(1)} %pad_maximum_fusion.3.refs_0_, bf16[12,512,128]{2,1,0:T(8,128)(2,1)S(1)} %collective-permute-done.26.refs_1_, ...), custom_call_target="tpu_custom_call", output_to_operand_aliasing={{0}: (3, {}), {1}: (4, {})} | custom-call | tf_op jit(solution)/shard_map/place/pallas_call | solution.py:571
  128.0 4.9 %collective-permute-done.29 = bf16[4,64,512]{2,1,0:T(8,128)(2,1)S(1)} collective-permute-done((bf16[4,64,512]{2,1,0:T(8,128)(2,1)S(1)}, bf16[4,64,512]{2,1,0:T(8,128)(2,1)S(1)}, u32[]{:S(2)}, u32[]{:S(2)}) %collective-permute-start.29) | collective-permute-done | bytes 262176 | tf_op jit(solution)/shard_map/ppermute | solution.py:628
  134.0 1.5 %collective-permute-start.31 = (bf16[2,64,512]{2,1,0:T(8,128)(2,1)S(1)}, bf16[2,64,512]{2,1,0:T(8,128)(2,1)S(1)}, u32[]{:S(2)}, u32[]{:S(2)}) collective-permute-start(bf16[2,64,512]{2,1,0:T(8,128)(2,1)S(1)} %slice.258), channel_id=1, source_target_pairs={{0,4},{1,5},{2,6},{3,7},{4,0},{5,1},{6,2},{7,3},{8,12},{9,13},{10,... | collective-permute-start | bytes 393224 | tf_op jit(solution)/shard_map/ppermute | solution.py:628
  135.5 1.6 %place.5 = (f32[2048,512]{1,0:T(8,128)}, f32[512,2048]{1,0:T(8,128)}) custom-call(s32[16]{0:T(128)S(1)} %get-tuple-element.318.info, bf16[4,512,128]{2,1,0:T(8,128)(2,1)S(1)} %collective-permute-done.27.refs_0_, f32[2048,512]{1,0:T(8,128)} %get-tuple-element.303.refs_1_, ...), custom_call_target="tpu_custom_call", output_to_operand_aliasing={{0}: (2, {}), {1}: (3, {})} | custom-call | tf_op jit(solution)/shard_map/place/pallas_call | solution.py:571
  137.0 2.3 %collective-permute-done.30.refs_1_ = bf16[2,64,512]{2,1,0:T(8,128)(2,1)S(1)} collective-permute-done((bf16[2,64,512]{2,1,0:T(8,128)(2,1)S(1)}, bf16[2,64,512]{2,1,0:T(8,128)(2,1)S(1)}, u32[]{:S(2)}, u32[]{:S(2)}) %collective-permute-start.30) | collective-permute-done | bytes 131104 | tf_op jit(solution)/shard_map/ppermute | solution.py:628
  139.6 2.8 %sort.2 = (f32[512,512]{1,0:T(8,128)}, f32[512,512]{1,0:T(8,128)}, f32[512,512]{1,0:T(8,128)}, f32[512,512]{1,0:T(8,128)}) custom-call(s32[16]{0:T(128)S(1)} %get-tuple-element.318.info, bf16[12,64,512]{2,1,0:T(8,128)(2,1)S(1)} %pad_maximum_fusion.1.refs_0_, bf16[2,64,512]{2,1,0:T(8,128)(2,1)S(1)} %collective-permute-done.30.refs_1_, ...), custom_call_target="tpu_custom_call" | custom-call | tf_op jit(solution)/shard_map/sort/pallas_call | solution.py:605
  (130 shorter events, 25.0 us)
Async XLA Ops:
  1.9 3.1 %collective-permute-start.1 = (bf16[256,512]{1,0:T(8,128)(2,1)S(1)}, bf16[256,512]{1,0:T(8,128)(2,1)S(1)}, u32[]{:S(2)}, u32[]{:S(2)}) collective-permute-start(bf16[256,512]{1,0:T(8,128)(2,1)S(1)} %get-tuple-element.174.mine.near.near_h), channel_id=1, source_target_pairs={{0,1},{1,0},{2,3},{3,2},{4,5},{5,4},{6,7},{7,6},{8,9},{9,8},{10,11... | collective-permute-start | bytes 786440 | tf_op jit(solution)/shard_map/ppermute | solution.py:628
  2.4 9.5 %collective-permute-start = (bf16[256,512]{1,0:T(8,128)(2,1)S(1)}, bf16[256,512]{1,0:T(8,128)(2,1)S(1)}, u32[]{:S(2)}, u32[]{:S(2)}) collective-permute-start(bf16[256,512]{1,0:T(8,128)(2,1)S(1)} %get-tuple-element.173), channel_id=1, source_target_pairs={{0,2},{1,3},{2,0},{3,1},{4,6},{5,7},{6,4},{7,5},{8,10},{9,11},{10,... | collective-permute-start | bytes 786440 | tf_op jit(solution)/shard_map/ppermute | solution.py:628
  35.5 5.2 %collective-permute-start.3 = (bf16[16,512,128]{2,1,0:T(8,128)(2,1)S(1)}, bf16[16,512,128]{2,1,0:T(8,128)(2,1)S(1)}, u32[]{:S(2)}, u32[]{:S(2)}) collective-permute-start(bf16[16,512,128]{2,1,0:T(8,128)(2,1)S(1)} %get-tuple-element.193), channel_id=1, source_target_pairs={{0,1},{1,0},{2,3},{3,2},{4,5},{5,4},{6,7},{7,6},{8,9},{9,8},{10,11... | collective-permute-start | bytes 6291464 | tf_op jit(solution)/shard_map/ppermute | solution.py:628
  44.3 23.6 %collective-permute-start.4 = (bf16[4,512,128]{2,1,0:T(8,128)(2,1)S(1)}, bf16[4,512,128]{2,1,0:T(8,128)(2,1)S(1)}, u32[]{:S(2)}, u32[]{:S(2)}) collective-permute-start(bf16[4,512,128]{2,1,0:T(8,128)(2,1)S(1)} %get-tuple-element.216), channel_id=1, source_target_pairs={{0,2},{1,3},{2,0},{3,1},{4,6},{5,7},{6,4},{7,5},{8,10},{9,11},{10,... | collective-permute-start | bytes 1572872 | tf_op jit(solution)/shard_map/ppermute | solution.py:628
  46.2 21.8 %collective-permute-start.5 = (bf16[4,512,128]{2,1,0:T(8,128)(2,1)S(1)}, bf16[4,512,128]{2,1,0:T(8,128)(2,1)S(1)}, u32[]{:S(2)}, u32[]{:S(2)}) collective-permute-start(bf16[4,512,128]{2,1,0:T(8,128)(2,1)S(1)} %get-tuple-element.217), channel_id=1, source_target_pairs={{0,4},{1,5},{2,6},{3,7},{4,0},{5,1},{6,2},{7,3},{8,12},{9,13},{10,... | collective-permute-start | bytes 1572872 | tf_op jit(solution)/shard_map/ppermute | solution.py:628
  47.6 23.2 %collective-permute-start.6 = (bf16[4,512,128]{2,1,0:T(8,128)(2,1)S(1)}, bf16[4,512,128]{2,1,0:T(8,128)(2,1)S(1)}, u32[]{:S(2)}, u32[]{:S(2)}) collective-permute-start(bf16[4,512,128]{2,1,0:T(8,128)(2,1)S(1)} %get-tuple-element.218), channel_id=1, source_target_pairs={{0,6},{1,7},{2,4},{3,5},{4,2},{5,3},{6,0},{7,1},{8,14},{9,15},{10,... | collective-permute-start | bytes 1572872 | tf_op jit(solution)/shard_map/ppermute | solution.py:628
  70.8 5.2 %collective-permute-start.7 = (bf16[1040,512]{1,0:T(8,128)(2,1)}, bf16[1040,512]{1,0:T(8,128)(2,1)S(1)}, u32[]{:S(2)}, u32[]{:S(2)}) collective-permute-start(bf16[1040,512]{1,0:T(8,128)(2,1)} %get-tuple-element.229), channel_id=1, source_target_pairs={{0,1},{1,0},{2,3},{3,2},{4,5},{5,4},{6,7},{7,6},{8,9},{9,8},{10,11... | collective-permute-start | bytes 3194888 | tf_op jit(solution)/shard_map/ppermute | solution.py:628
  70.8 5.2 %collective-permute-start.8 = (bf16[528,512]{1,0:T(8,128)(2,1)S(1)}, bf16[528,512]{1,0:T(8,128)(2,1)S(1)}, u32[]{:S(2)}, u32[]{:S(2)}) collective-permute-start(bf16[528,512]{1,0:T(8,128)(2,1)S(1)} %get-tuple-element.230), channel_id=1, source_target_pairs={{0,1},{1,0},{2,3},{3,2},{4,5},{5,4},{6,7},{7,6},{8,9},{9,8},{10,11... | collective-permute-start | bytes 1622024 | tf_op jit(solution)/shard_map/ppermute | solution.py:628
  71.6 8.1 %collective-permute-start.9 = (bf16[512,128]{1,0:T(8,128)(2,1)S(1)}, bf16[512,128]{1,0:T(8,128)(2,1)S(1)}, u32[]{:S(2)}, u32[]{:S(2)}) collective-permute-start(bf16[512,128]{1,0:T(8,128)(2,1)S(1)} %get-tuple-element.236), channel_id=1, source_target_pairs={{0,8},{1,9},{2,10},{3,11},{4,12},{5,13},{6,14},{7,15},{8,0},{9,1},... | collective-permute-start | bytes 393224 | tf_op jit(solution)/shard_map/ppermute | solution.py:628
  73.4 12.9 %collective-permute-start.10 = (bf16[512,128]{1,0:T(8,128)(2,1)S(1)}, bf16[512,128]{1,0:T(8,128)(2,1)S(1)}, u32[]{:S(2)}, u32[]{:S(2)}) collective-permute-start(bf16[512,128]{1,0:T(8,128)(2,1)S(1)} %get-tuple-element.237), channel_id=1, source_target_pairs={{0,16},{1,17},{2,18},{3,19},{4,20},{5,21},{6,22},{7,23},{8,24},{9,... | collective-permute-start | bytes 393224 | tf_op jit(solution)/shard_map/ppermute | solution.py:628
  76.0 10.3 %collective-permute-start.11 = (bf16[512,128]{1,0:T(8,128)(2,1)S(1)}, bf16[512,128]{1,0:T(8,128)(2,1)S(1)}, u32[]{:S(2)}, u32[]{:S(2)}) collective-permute-start(bf16[512,128]{1,0:T(8,128)(2,1)S(1)} %get-tuple-element.238), channel_id=1, source_target_pairs={{0,24},{1,25},{2,26},{3,27},{4,28},{5,29},{6,30},{7,31},{8,16},{9,... | collective-permute-start | bytes 393224 | tf_op jit(solution)/shard_map/ppermute | solution.py:628
  76.5 13.5 %collective-permute-start.12 = (bf16[272,512]{1,0:T(8,128)(2,1)S(1)}, bf16[272,512]{1,0:T(8,128)(2,1)S(1)}, u32[]{:S(2)}, u32[]{:S(2)}) collective-permute-start(bf16[272,512]{1,0:T(8,128)(2,1)S(1)} %get-tuple-element.249), channel_id=1, source_target_pairs={{0,2},{1,3},{2,0},{3,1},{4,6},{5,7},{6,4},{7,5},{8,10},{9,11},{10,... | collective-permute-start | bytes 835592 | tf_op jit(solution)/shard_map/ppermute | solution.py:628
  78.2 12.6 %collective-permute-start.13 = (bf16[272,512]{1,0:T(8,128)(2,1)S(1)}, bf16[272,512]{1,0:T(8,128)(2,1)S(1)}, u32[]{:S(2)}, u32[]{:S(2)}) collective-permute-start(bf16[272,512]{1,0:T(8,128)(2,1)S(1)} %get-tuple-element.250), channel_id=1, source_target_pairs={{0,4},{1,5},{2,6},{3,7},{4,0},{5,1},{6,2},{7,3},{8,12},{9,13},{10,... | collective-permute-start | bytes 835592 | tf_op jit(solution)/shard_map/ppermute | solution.py:628
  79.7 12.7 %collective-permute-start.14 = (bf16[272,512]{1,0:T(8,128)(2,1)S(1)}, bf16[272,512]{1,0:T(8,128)(2,1)S(1)}, u32[]{:S(2)}, u32[]{:S(2)}) collective-permute-start(bf16[272,512]{1,0:T(8,128)(2,1)S(1)} %get-tuple-element.251), channel_id=1, source_target_pairs={{0,6},{1,7},{2,4},{3,5},{4,2},{5,3},{6,0},{7,1},{8,14},{9,15},{10,... | collective-permute-start | bytes 835592 | tf_op jit(solution)/shard_map/ppermute | solution.py:628
  86.4 14.9 %collective-permute-start.18 = (bf16[512,128]{1,0:T(8,128)(2,1)S(1)}, bf16[512,128]{1,0:T(8,128)(2,1)S(1)}, u32[]{:S(2)}, u32[]{:S(2)}) collective-permute-start(bf16[512,128]{1,0:T(8,128)(2,1)S(1)} %add_convert_fusion.2), channel_id=1, source_target_pairs={{0,24},{1,25},{2,26},{3,27},{4,28},{5,29},{6,30},{7,31},{8,16},{9,... | collective-permute-start | bytes 393224 | tf_op jit(solution)/shard_map/ppermute | solution.py:628
  88.8 12.4 %collective-permute-start.17 = (bf16[512,128]{1,0:T(8,128)(2,1)S(1)}, bf16[512,128]{1,0:T(8,128)(2,1)S(1)}, u32[]{:S(2)}, u32[]{:S(2)}) collective-permute-start(bf16[512,128]{1,0:T(8,128)(2,1)S(1)} %add_convert_fusion.2), channel_id=1, source_target_pairs={{0,16},{1,17},{2,18},{3,19},{4,20},{5,21},{6,22},{7,23},{8,24},{9,... | collective-permute-start | bytes 393224 | tf_op jit(solution)/shard_map/ppermute | solution.py:628
  90.0 11.2 %collective-permute-start.16 = (bf16[512,128]{1,0:T(8,128)(2,1)S(1)}, bf16[512,128]{1,0:T(8,128)(2,1)S(1)}, u32[]{:S(2)}, u32[]{:S(2)}) collective-permute-start(bf16[512,128]{1,0:T(8,128)(2,1)S(1)} %add_convert_fusion.2), channel_id=1, source_target_pairs={{0,8},{1,9},{2,10},{3,11},{4,12},{5,13},{6,14},{7,15},{8,0},{9,1},... | collective-permute-start | bytes 393224 | tf_op jit(solution)/shard_map/ppermute | solution.py:628
  90.8 10.4 %collective-permute-start.19 = (bf16[272,512]{1,0:T(8,128)(2,1)S(1)}, bf16[272,512]{1,0:T(8,128)(2,1)S(1)}, u32[]{:S(2)}, u32[]{:S(2)}) collective-permute-start(bf16[272,512]{1,0:T(8,128)(2,1)S(1)} %get-tuple-element.261), channel_id=1, source_target_pairs={{0,2},{1,3},{2,0},{3,1},{4,6},{5,7},{6,4},{7,5},{8,10},{9,11},{10,... | collective-permute-start | bytes 835592 | tf_op jit(solution)/shard_map/ppermute | solution.py:628
  92.7 8.4 %collective-permute-start.15 = (bf16[144,512]{1,0:T(8,128)(2,1)S(1)}, bf16[144,512]{1,0:T(8,128)(2,1)S(1)}, u32[]{:S(2)}, u32[]{:S(2)}) collective-permute-start(bf16[144,512]{1,0:T(8,128)(2,1)S(1)} %pad_maximum_fusion.12), channel_id=1, source_target_pairs={{0,8},{1,9},{2,10},{3,11},{4,12},{5,13},{6,14},{7,15},{8,0},{9,1},... | collective-permute-start | bytes 442376 | tf_op jit(solution)/shard_map/ppermute | solution.py:628
  101.4 11.9 %collective-permute-start.22 = (bf16[4,512,128]{2,1,0:T(8,128)(2,1)S(1)}, bf16[4,512,128]{2,1,0:T(8,128)(2,1)S(1)}, u32[]{:S(2)}, u32[]{:S(2)}) collective-permute-start(bf16[4,512,128]{2,1,0:T(8,128)(2,1)S(1)} %pad_maximum_fusion.2), channel_id=1, source_target_pairs={{0,4},{1,5},{2,6},{3,7},{4,0},{5,1},{6,2},{7,3},{8,12},{9,13},{10,... | collective-permute-start | bytes 1572872 | tf_op jit(solution)/shard_map/ppermute | solution.py:628
  103.0 10.8 %collective-permute-start.21 = (bf16[4,512,128]{2,1,0:T(8,128)(2,1)S(1)}, bf16[4,512,128]{2,1,0:T(8,128)(2,1)S(1)}, u32[]{:S(2)}, u32[]{:S(2)}) collective-permute-start(bf16[4,512,128]{2,1,0:T(8,128)(2,1)S(1)} %pad_maximum_fusion.2), channel_id=1, source_target_pairs={{0,2},{1,3},{2,0},{3,1},{4,6},{5,7},{6,4},{7,5},{8,10},{9,11},{10,... | collective-permute-start | bytes 1572872 | tf_op jit(solution)/shard_map/ppermute | solution.py:628
  104.5 7.5 %collective-permute-start.20 = (bf16[144,512]{1,0:T(8,128)(2,1)S(1)}, bf16[144,512]{1,0:T(8,128)(2,1)S(1)}, u32[]{:S(2)}, u32[]{:S(2)}) collective-permute-start(bf16[144,512]{1,0:T(8,128)(2,1)S(1)} %pad_maximum_fusion.13), channel_id=1, source_target_pairs={{0,16},{1,17},{2,18},{3,19},{4,20},{5,21},{6,22},{7,23},{8,24},{9,... | collective-permute-start | bytes 442376 | tf_op jit(solution)/shard_map/ppermute | solution.py:628
  114.0 10.0 %collective-permute-start.26 = (bf16[12,512,128]{2,1,0:T(8,128)(2,1)S(1)}, bf16[12,512,128]{2,1,0:T(8,128)(2,1)S(1)}, u32[]{:S(2)}, u32[]{:S(2)}) collective-permute-start(bf16[12,512,128]{2,1,0:T(8,128)(2,1)S(1)} %pad_maximum_fusion.refs_0_), channel_id=1, source_target_pairs={{0,1},{1,0},{2,3},{3,2},{4,5},{5,4},{6,7},{7,6},{8,9},{9,8},{10,11... | collective-permute-start | bytes 4718600 | tf_op jit(solution)/shard_map/ppermute | solution.py:628
  114.1 8.7 %collective-permute-start.24 = (bf16[2,512,128]{2,1,0:T(8,128)(2,1)S(1)}, bf16[2,512,128]{2,1,0:T(8,128)(2,1)S(1)}, u32[]{:S(2)}, u32[]{:S(2)}) collective-permute-start(bf16[2,512,128]{2,1,0:T(8,128)(2,1)S(1)} %slice.251), channel_id=1, source_target_pairs={{0,2},{1,3},{2,0},{3,1},{4,6},{5,7},{6,4},{7,5},{8,10},{9,11},{10,... | collective-permute-start | bytes 786440 | tf_op jit(solution)/shard_map/ppermute | solution.py:628
  115.6 8.4 %collective-permute-start.25 = (bf16[2,512,128]{2,1,0:T(8,128)(2,1)S(1)}, bf16[2,512,128]{2,1,0:T(8,128)(2,1)S(1)}, u32[]{:S(2)}, u32[]{:S(2)}) collective-permute-start(bf16[2,512,128]{2,1,0:T(8,128)(2,1)S(1)} %slice.252), channel_id=1, source_target_pairs={{0,4},{1,5},{2,6},{3,7},{4,0},{5,1},{6,2},{7,3},{8,12},{9,13},{10,... | collective-permute-start | bytes 786440 | tf_op jit(solution)/shard_map/ppermute | solution.py:628
  116.2 5.3 %collective-permute-start.23 = (bf16[128,512]{1,0:T(8,128)(2,1)S(1)}, bf16[128,512]{1,0:T(8,128)(2,1)S(1)}, u32[]{:S(2)}, u32[]{:S(2)}) collective-permute-start(bf16[128,512]{1,0:T(8,128)(2,1)S(1)} %add_convert_fusion), channel_id=1, source_target_pairs={{0,8},{1,9},{2,10},{3,11},{4,12},{5,13},{6,14},{7,15},{8,0},{9,1},... | collective-permute-start | bytes 393224 | tf_op jit(solution)/shard_map/ppermute | solution.py:628
  124.1 9.1 %collective-permute-start.27 = (bf16[4,512,128]{2,1,0:T(8,128)(2,1)S(1)}, bf16[4,512,128]{2,1,0:T(8,128)(2,1)S(1)}, u32[]{:S(2)}, u32[]{:S(2)}) collective-permute-start(bf16[4,512,128]{2,1,0:T(8,128)(2,1)S(1)} %pad_maximum_fusion.3.refs_0_), channel_id=1, source_target_pairs={{0,1},{1,0},{2,3},{3,2},{4,5},{5,4},{6,7},{7,6},{8,9},{9,8},{10,11... | collective-permute-start | bytes 1572872 | tf_op jit(solution)/shard_map/ppermute | solution.py:628
  124.2 8.7 %collective-permute-start.29 = (bf16[4,64,512]{2,1,0:T(8,128)(2,1)S(1)}, bf16[4,64,512]{2,1,0:T(8,128)(2,1)S(1)}, u32[]{:S(2)}, u32[]{:S(2)}) collective-permute-start(bf16[4,64,512]{2,1,0:T(8,128)(2,1)S(1)} %pad_maximum_fusion.10), channel_id=1, source_target_pairs={{0,4},{1,5},{2,6},{3,7},{4,0},{5,1},{6,2},{7,3},{8,12},{9,13},{10,... | collective-permute-start | bytes 786440 | tf_op jit(solution)/shard_map/ppermute | solution.py:628
  124.8 8.4 %collective-permute-start.28 = (bf16[4,64,512]{2,1,0:T(8,128)(2,1)S(1)}, bf16[4,64,512]{2,1,0:T(8,128)(2,1)S(1)}, u32[]{:S(2)}, u32[]{:S(2)}) collective-permute-start(bf16[4,64,512]{2,1,0:T(8,128)(2,1)S(1)} %pad_maximum_fusion.10), channel_id=1, source_target_pairs={{0,2},{1,3},{2,0},{3,1},{4,6},{5,7},{6,4},{7,5},{8,10},{9,11},{10,... | collective-permute-start | bytes 786440 | tf_op jit(solution)/shard_map/ppermute | solution.py:628
  133.3 6.2 %collective-permute-start.32 = (bf16[12,64,512]{2,1,0:T(8,128)(2,1)S(1)}, bf16[12,64,512]{2,1,0:T(8,128)(2,1)S(1)}, u32[]{:S(2)}, u32[]{:S(2)}) collective-permute-start(bf16[12,64,512]{2,1,0:T(8,128)(2,1)S(1)} %pad_maximum_fusion.1.refs_0_), channel_id=1, source_target_pairs={{0,1},{1,0},{2,3},{3,2},{4,5},{5,4},{6,7},{7,6},{8,9},{9,8},{10,11... | collective-permute-start | bytes 2359304 | tf_op jit(solution)/shard_map/ppermute | solution.py:628
  133.4 5.9 %collective-permute-start.30 = (bf16[2,64,512]{2,1,0:T(8,128)(2,1)S(1)}, bf16[2,64,512]{2,1,0:T(8,128)(2,1)S(1)}, u32[]{:S(2)}, u32[]{:S(2)}) collective-permute-start(bf16[2,64,512]{2,1,0:T(8,128)(2,1)S(1)} %slice.257), channel_id=1, source_target_pairs={{0,2},{1,3},{2,0},{3,1},{4,6},{5,7},{6,4},{7,5},{8,10},{9,11},{10,... | collective-permute-start | bytes 393224 | tf_op jit(solution)/shard_map/ppermute | solution.py:628
  134.0 5.6 %collective-permute-start.31 = (bf16[2,64,512]{2,1,0:T(8,128)(2,1)S(1)}, bf16[2,64,512]{2,1,0:T(8,128)(2,1)S(1)}, u32[]{:S(2)}, u32[]{:S(2)}) collective-permute-start(bf16[2,64,512]{2,1,0:T(8,128)(2,1)S(1)} %slice.258), channel_id=1, source_target_pairs={{0,4},{1,5},{2,6},{3,7},{4,0},{5,1},{6,2},{7,3},{8,12},{9,13},{10,... | collective-permute-start | bytes 393224 | tf_op jit(solution)/shard_map/ppermute | solution.py:628
  (22 other events, 174.5 us)

commit v11 on v10

--- a/solution.py
+++ b/solution.py
@@ -265,108 +265,75 @@
         name="front", compiler_params=pltpu.CompilerParams(vmem_limit_bytes=38 << 20),
     )(info, far, far_other, near, q_l, k_l, v_l, lines, wq, wk, wv, gain1, gain2, gain3, cots, wo, win, wback)
 
-def through_kernel(info, slopes_h, win_h, mixed_h, steep_h, wo_h, att_h, gain2, grad_mixed_o, grad_attended_o, grad_out_o, rows,
-                   slopes, win, mixed, steep, wo, att, grad_mixed, grad_attended, grad_out, sems):
-    hidden, width = slopes.shape[1], mixed.shape[1]
-    chunks = []
-    for i, at in enumerate(range(0, hidden, 512)):
-        for a, b, s in ((slopes_h, slopes, i), (win_h, win, 4 + i)):
-            chunks.append(pltpu.make_async_copy(a.at[:, at : at + 512], b.at[:, at : at + 512], sems.at[s]))
-    copies = [pltpu.make_async_copy(a, b, sems.at[8 + i]) for i, (a, b) in enumerate((
-        (mixed_h, mixed), (steep_h, steep), (wo_h, wo), (att_h, att)))]
-    outs = [pltpu.make_async_copy(a, b, sems.at[12 + i]) for i, (a, b) in enumerate((
-        (grad_mixed, grad_mixed_o), (grad_attended, grad_attended_o), (grad_out, grad_out_o)))]
-    for copy in chunks + copies:
-        copy.start()
-    grad_inner = None
-    for i, at in enumerate(range(0, hidden, 512)):
-        chunks[2 * i].wait()
-        chunks[2 * i + 1].wait()
+def inner_kernel(info, slopes, win, grad_inner):
+    total = None
+    for at in range(0, slopes.shape[1], 512):
         part = dot(slopes[:, at : at + 512], win[:, at : at + 512], NT)
-        grad_inner = part if grad_inner is None else grad_inner + part
-    copies[0].wait()
-    copies[1].wait()
+        total = part if total is None else total + part
+    grad_inner[...] = total
+
+def inner(info, slopes, win):
+    smem, vmem = pl.BlockSpec(memory_space=pltpu.SMEM), pl.BlockSpec(memory_space=pltpu.VMEM)
+    return pl.pallas_call(
+        inner_kernel, in_specs=[smem, vmem, vmem], out_specs=vmem,
+        out_shape=jax.ShapeDtypeStruct((slopes.shape[0], win.shape[0]), F32), name="inner", compiler_params=pltpu.CompilerParams(vmem_limit_bytes=10 << 20),
+    )(info, slopes, win)
+
+def through_kernel(info, grad_inner, mixed, steep, wo, att, gain2, grad_mixed, grad_attended, grad_out, rows):
     values = mixed[...]
-    more, grad_two = norm_back(grad_inner, values, rms_scale(values), gain2[...])
+    more, grad_two = norm_back(grad_inner[...], values, rms_scale(values), gain2[...])
     total = steep[...] + more
     grad_mixed[...] = total
-    outs[0].start()
     low = total.astype(BF16)
-    copies[2].wait()
     grad_attended[...] = dot(low, wo[...], NT).astype(BF16)
-    outs[1].start()
-    copies[3].wait()
     grad_out[...] = dot(att[...], low, TN).astype(BF16)
-    outs[2].start()
-    rows[...] = jnp.concatenate([grad_two, jnp.zeros((7, width), F32)])
-    for copy in outs:
-        copy.wait()
-
-def through(info, slopes, win, mixed, steep, wo, att, gain2):
+    rows[...] = jnp.concatenate([grad_two, jnp.zeros((7, low.shape[1]), F32)])
+
+def through(info, grad_inner, mixed, steep, wo, att, gain2):
     n, width = mixed.shape
-    smem, vmem, free = (pl.BlockSpec(memory_space=m) for m in (pltpu.SMEM, pltpu.VMEM, pl.ANY))
+    smem, vmem = pl.BlockSpec(memory_space=pltpu.SMEM), pl.BlockSpec(memory_space=pltpu.VMEM)
     shape = jax.ShapeDtypeStruct
-    given = (slopes, win, mixed, steep, wo, att)
-    outs = [shape((n, width), F32), shape((n, width), BF16), shape((width, width), BF16)]
     return pl.pallas_call(
         through_kernel,
-        in_specs=[smem, free, pl.BlockSpec(memory_space=pltpu.HBM)] + [free] * 4 + [vmem],
-        out_specs=[free] * 3 + [vmem],
-        out_shape=outs + [shape((8, width), F32)],
-        scratch_shapes=[pltpu.VMEM(g.shape, g.dtype) for g in given] + [pltpu.VMEM(o.shape, o.dtype) for o in outs] + [pltpu.SemaphoreType.DMA((15,))],
+        in_specs=[smem] + [vmem] * 6,
+        out_specs=[vmem] * 4,
+        out_shape=[shape((n, width), F32), shape((n, width), BF16), shape((width, width), BF16), shape((8, width), F32)],
         name="through", compiler_params=pltpu.CompilerParams(vmem_limit_bytes=16 << 20),
-    )(info, *given, gain2)
-
-def meet_kernel(info, got_h, active_h, slopes_h, turned_h, steep_h, *refs):
-    outs, (got, chunk, turned, steep, blocks, sems) = refs[:4], refs[4:]
-    order = (3, 1, 2, 0)
+    )(info, grad_inner, mixed, steep, wo, att, gain2)
+
+def stay_kernel(info, active, slopes, turned, steep, blocks):
     high, lowest = (info[6] & 15) >> 2, info[6] & 3
-    load = [pltpu.make_async_copy(got_h.at[4 * k : 4 * k + 4], got.at[k], sems.at[k]) for k in range(4)]
-    save = [pltpu.make_async_copy(blocks.at[k], outs[k], sems.at[4 + k]) for k in range(4)]
-
-    def columns(source, k):
-        at = pl.ds(pl.multiple_of((k ^ high) * 512, 512), 512)
-        return pltpu.make_async_copy(source.at[:, at], chunk.at[k], sems.at[8 + k])
-
-    for side, source in ((0, active_h), (1, slopes_h)):
+    for side in range(2):
         @pl.when(info[7] == side)
-        def _(side=side, source=source):
-            extra = pltpu.make_async_copy(*((steep_h, steep) if side == 0 else (turned_h, turned)), sems.at[12])
-            extra.start()
-            for k in order:
-                columns(source, k).start()
-                load[k].start()
-            extra.wait()
+        def _(side=side):
             low = steep[...].astype(BF16) if side == 0 else turned[...]
-            for k in order:
-                columns(source, k).wait()
-                made = dot(chunk[k], low, TN) if side == 0 else dot(low, chunk[k])
-                load[k].wait()
+            for k in range(4):
+                at = pl.ds(pl.multiple_of((k ^ high) * 512, 512), 512)
+                made = dot(active[:, at], low, TN) if side == 0 else dot(low, slopes[:, at])
                 for b in range(4):
                     piece = made[:, b * 128 : (b + 1) * 128]
                     if side == 0:
                         piece = made[b * 128 : (b + 1) * 128]
                         piece = jnp.concatenate([piece[:, q * 128 : (q + 1) * 128] for q in range(4)])
-                    to = b ^ lowest
-                    blocks[k, to] = (piece + got[k, to].astype(F32)).astype(BF16)
-                save[k].start()
-
-    for copy in save:
-        copy.wait()
-
-def meet(info, got, active, slopes, turned, steep):
-    smem, free = pl.BlockSpec(memory_space=pltpu.SMEM), pl.BlockSpec(memory_space=pl.ANY)
-    block = (4,) + got.shape[1:]
-    n, width = steep.shape
-    return pl.pallas_call(
-        meet_kernel,
-        in_specs=[smem] + [free] * 5,
-        out_specs=[free] * 4,
-        out_shape=[jax.ShapeDtypeStruct(block, BF16)] * 4,
-        scratch_shapes=[pltpu.VMEM((4,) + block, BF16), pltpu.VMEM((4, n, 512), BF16), pltpu.VMEM(turned.shape, BF16), pltpu.VMEM(steep.shape, F32),
-                        pltpu.VMEM((4,) + block, BF16), pltpu.SemaphoreType.DMA((13,))],
-        name="meet", compiler_params=pltpu.CompilerParams(vmem_limit_bytes=20 << 20),
-    )(info, got, active, slopes, turned, steep)
+                    blocks[k, b ^ lowest] = piece.astype(BF16)
+
+def stay_half(info, active, slopes, turned, steep):
+    smem, vmem = pl.BlockSpec(memory_space=pltpu.SMEM), pl.BlockSpec(memory_space=pltpu.VMEM)
+    width = steep.shape[1]
+    return pl.pallas_call(
+        stay_kernel, in_specs=[smem] + [vmem] * 4, out_specs=vmem,
+        out_shape=jax.ShapeDtypeStruct((4, 4, width, 128), BF16), name="stay", compiler_params=pltpu.CompilerParams(vmem_limit_bytes=12 << 20),
+    )(info, active, slopes, turned, steep)
+
+def meet_kernel(kept, got, *outs):
+    for k in (3, 1, 2, 0):
+        outs[k][...] = added(kept[k], got[4 * k : 4 * k + 4])
+
+def meet(kept, got):
+    vmem = pl.BlockSpec(memory_space=pltpu.VMEM)
+    return pl.pallas_call(
+        meet_kernel, in_specs=[vmem] * 2, out_specs=[vmem] * 4, out_shape=[jax.ShapeDtypeStruct(kept.shape[1:], BF16)] * 4, name="meet", compiler_params=pltpu.CompilerParams(vmem_limit_bytes=20 << 20),
+    )(kept, got)
 
 CLASS = {(0, 0): 0, (1, 2): 0, (0, 1): 1, (1, 3): 1, (0, 2): 2, (0, 3): 3, (1, 0): 4, (1, 1): 5}
 
@@ -668,12 +635,16 @@
 
     token, send = wait(info, send)
     got = exchange(send, CORE)
-    grad_mixed, grad_attended, grad_out_w, through_rows = through(token, slopes, w_in, mixed, steep, w_out, attended, gain2)
-    token, through_rows, got = wait(token, through_rows, got)
-    stays, *sends = meet(token, got, active, slopes, turned, steep)
-
-    token, sends = wait(token, sends)
+    kept = stay_half(token, active, slopes, turned, steep)
+    token, kept = wait(token, kept)
+    grad_inner = inner(token, slopes, w_in)
+    token, grad_inner, got = wait(token, grad_inner, got)
+    stays, *sends = meet(kept, got)
+
+    token, sends, grad_inner = wait(token, sends, grad_inner)
     came = [exchange(s, m) for s, m in zip(sends, xy)]
+    grad_mixed, grad_attended, grad_out_w, through_rows = through(token, grad_inner, mixed, steep, w_out, attended, gain2)
+    token, through_rows = wait(token, through_rows)
     rest_keep, rest_send, stay, leave, small = back(
         token, q_l, q_r, k_l, k_r, v_l, v_r, grad_attended, attended, inverse, expo, buckets, dense_rows, through_rows,
         hid_l, hid_r, near, near_other, far, far_other, w_query, w_key, w_value, grad_out_w)
@@ -752,17 +723,18 @@
     token, fourth, far_pair = wait(token, fourth, far_pair)
     fourth_y, fourth_x = exchange(fourth, ROW), exchange(fourth, NEAR_X)
     other_far = exchange(far_pair, CORE)
-    grads = place(token, [(12, far_pair), (16, other)], grads, width)
-    token, grads, other_far, fourth_y, fourth_x = wait(token, grads, other_far, fourth_y, fourth_x)
+    token, other_far = wait(token, other_far)
+    out_back, out_in = place(token, [(12, far_pair), (16, other), (28, other_far)], grads, width)
+    token, out_back, out_in, fourth_y, fourth_x = wait(token, out_back, out_in, fourth_y, fourth_x)
 
     sends = [fourth_x[:2], fourth_y[2:], jnp.concatenate([fourth, fourth_y, fourth_x])]
     token, sends = wait(token, sends)
     last_a, last_b, pair = (exchange(s, m) for s, m in zip(sends, (ROW, NEAR_X, CORE)))
-    out_back, out_in = place(token, [(28, other_far)], grads, width)
-    token, out_back, out_in, last_a, last_b, pair = wait(token, out_back, out_in, last_a, last_b, pair)
+    made = sort(token, [(0, sends[2])], [], width)
+    token, made, last_a, last_b, pair = wait(token, made, last_a, last_b, pair)
 
     ends = exchange(jnp.concatenate([last_a, last_b]), CORE)
-    made = sort(token, [(0, sends[2]), (12, last_a), (14, last_b), (16, pair)], [], width)
+    made = sort(token, [(12, last_a), (14, last_b), (16, pair)], made, width)
     token, made, ends = wait(token, made, ends)
     out_out, out_query, out_key, out_value = sort(token, [(28, ends)], made, width)
     return (pooled, input_grad, out_query, out_key, out_value, out_out, out_in, out_back, *outs)

time: 144 us -> 140 us (0.972)
  Pallas kernels: 65.4 us -> 63 us
  waiting for transfers between devices: 33.2 us -> 31 us
    pallas_call x2 -> x4, Pallas kernels: 8.46 us -> 6.09 us  [the longest x1 2.03 us: stay_half(): pl.pallas_call(stay_kernel, in_specs=[smem] + [vmem] * 4, out_specs=vmem,...]
    ppermute x34, waiting for transfers between devices: 33.2 us -> 31 us  [exchange(): lax.ppermute(value, ('dp', 'blk'), [(i, i ^ bits) for i in range(size)])]
    pallas_call x3 -> x2, Pallas kernels: 6.58 us -> 5.38 us  [place(): pl.pallas_call(functools.partial(place_kernel, [first for first, _ in par...]
    pallas_call x2 -> x3, Pallas kernels: 4.23 us -> 5.39 us  [sort(): pl.pallas_call(functools.partial(sort_kernel, [first for first, _ in part...]
    unnamed x40 -> x32, local copies, waits for them, and re-layouts: 3.88 us -> 3.86 us
  transfers between devices with their start and end apart: 34 -> 34, of which waited for: 14 -> 15; matrix products, arithmetic and copies ran while one was open for 3% -> 3% of each run, Pallas kernels for 27% -> 28%
where the time goes in v11:
time: 140 us
  Pallas kernels  63 us (45%)
  starting transfers between devices  35 us (25%)
  waiting for transfers between devices  31 us (22%)
  local copies, waits for them, and re-layouts  5.41 us (4%)
  other arithmetic  3.76 us (3%)
    ppermute x34, starting transfers between devices, exchange(): lax.ppermute(value, ('dp', 'blk'), [(i, i ^ bits) for i in range(size)])  35 us
    ppermute x34, waiting for transfers between devices, exchange(): lax.ppermute(value, ('dp', 'blk'), [(i, i ^ bits) for i in range(size)])  31 us
    pallas_call x1, Pallas kernels, front(): pl.pallas_call(front_kernel, grid=(heads // 2,), in_specs=[smem] + [whole...  22 us
    pallas_call x1, Pallas kernels, back(): pl.pallas_call(back_kernel, grid=(width // 128,), in_specs=[smem, col(cou...  20.1 us
    pallas_call x3, Pallas kernels, sort(): pl.pallas_call(functools.partial(sort_kernel, [first for first, _ in part...  5.39 us
    pallas_call x2, Pallas kernels, place(): pl.pallas_call(functools.partial(place_kernel, [first for first, _ in par...  5.38 us
    unnamed x32, local copies, waits for them, and re-layouts  3.86 us
  transfers between devices with their start and end apart: 34, of which 15 were waited for; matrix products, arithmetic and copies ran while one was open for 3% of the time, Pallas kernels for 28%

profile of v11, /device:TPU:0, one launch (start us, length us, event | category | flops | bytes accessed | tf_op | source)
XLA Modules:
  0.0 139.5 jit_solution(13608446166742235904)
XLA Ops:
  2.4 2.6 %collective-permute-start = (bf16[256,512]{1,0:T(8,128)(2,1)S(1)}, bf16[256,512]{1,0:T(8,128)(2,1)S(1)}, u32[]{:S(2)}, u32[]{:S(2)}) collective-permute-start(bf16[256,512]{1,0:T(8,128)(2,1)S(1)} %get-tuple-element.183), channel_id=1, source_target_pairs={{0,2},{1,3},{2,0},{3,1},{4,6},{5,7},{6,4},{7,5},{8,10},{9,11},{10,... | collective-permute-start | bytes 786440 | tf_op jit(solution)/shard_map/ppermute | solution.py:595
  8.8 1.5 %prepare.1 = (bf16[512,512]{1,0:T(8,128)(2,1)S(1)}, bf16[256,512]{1,0:T(8,128)(2,1)S(1)}, bf16[512,512]{1,0:T(8,128)(2,1)S(1)}, bf16[512,512]{1,0:T(8,128)(2,1)S...) custom-call(bf16[256,512]{1,0:T(8,128)(2,1)S(1)} %get-tuple-element.184.mine.near.near, ...), custom_call_target="tpu_custom_call" | custom-call | tf_op jit(solution)/shard_map/prepare/pallas_call | solution.py:65
  10.4 1.5 %collective-permute-done.far.far_h = bf16[256,512]{1,0:T(8,128)(2,1)S(1)} collective-permute-done((bf16[256,512]{1,0:T(8,128)(2,1)S(1)}, bf16[256,512]{1,0:T(8,128)(2,1)S(1)}, u32[]{:S(2)}, u32[]{:S(2)}) %collective-permute-start) | collective-permute-done | bytes 262176 | tf_op jit(solution)/shard_map/ppermute | solution.py:595
  13.5 22.0 %front.1 = (bf16[512,512]{1,0:T(8,128)(2,1)S(1)}, bf16[256,512]{1,0:T(8,128)(2,1)S(1)}, bf16[512,512]{1,0:T(8,128)(2,1)S(1)}, bf16[512,512]{1,0:T(8,128)(2,1)S(1...) custom-call(s32[16]{0:T(128)S(1)} %get-tuple-element.338.info, ...), custom_call_target="tpu_custom_call" | custom-call | tf_op jit(solution)/shard_map/front/pallas_call | solution.py:254
  35.8 2.0 %stay.1.kept = bf16[4,4,512,128]{3,2,1,0:T(8,128)(2,1)S(1)} custom-call(s32[16]{0:T(128)S(1)} %get-tuple-element.338.info, bf16[512,2048]{1,0:T(8,128)(2,1)S(1)} %get-tuple-element.198.active, bf16[512,2048]{1,0:T(8,128)(2,1)S(1)} %get-tuple-element.199.slopes, bf16[512,512]{1,0:T(8,128)(2,1)S(1)} %get-tuple-element.200.turned, ...), custom_call_target="tpu_custom_call" | custom-call | tf_op jit(solution)/shard_map/stay/pallas_call | solution.py:323
  37.8 1.8 %inner.1.grad_inner = f32[512,512]{1,0:T(8,128)S(1)} custom-call(s32[16]{0:T(128)S(1)} %get-tuple-element.338.info, bf16[512,2048]{1,0:T(8,128)(2,1)S(1)} %get-tuple-element.199.slopes, bf16[512,2048]{1,0:T(8,128)(2,1)S(1)} %copy-done), custom_call_target="tpu_custom_call" | custom-call | tf_op jit(solution)/shard_map/inner/pallas_call | solution.py:277
  40.2 1.8 %collective-permute-start.4 = (bf16[4,512,128]{2,1,0:T(8,128)(2,1)S(1)}, bf16[4,512,128]{2,1,0:T(8,128)(2,1)S(1)}, u32[]{:S(2)}, u32[]{:S(2)}) collective-permute-start(bf16[4,512,128]{2,1,0:T(8,128)(2,1)S(1)} %get-tuple-element.231), channel_id=1, source_target_pairs={{0,2},{1,3},{2,0},{3,1},{4,6},{5,7},{6,4},{7,5},{8,10},{9,11},{10,... | collective-permute-start | bytes 1572872 | tf_op jit(solution)/shard_map/ppermute | solution.py:595
  42.1 1.5 %collective-permute-start.5 = (bf16[4,512,128]{2,1,0:T(8,128)(2,1)S(1)}, bf16[4,512,128]{2,1,0:T(8,128)(2,1)S(1)}, u32[]{:S(2)}, u32[]{:S(2)}) collective-permute-start(bf16[4,512,128]{2,1,0:T(8,128)(2,1)S(1)} %get-tuple-element.232), channel_id=1, source_target_pairs={{0,4},{1,5},{2,6},{3,7},{4,0},{5,1},{6,2},{7,3},{8,12},{9,13},{10,... | collective-permute-start | bytes 1572872 | tf_op jit(solution)/shard_map/ppermute | solution.py:595
  43.8 1.7 %through.1 = (f32[512,512]{1,0:T(8,128)S(1)}, bf16[512,512]{1,0:T(8,128)(2,1)S(1)}, bf16[512,512]{1,0:T(8,128)(2,1)S(1)}, f32[8,512]{1,0:T(8,128)S(1)}) custom-call(s32[16]{0:T(128)S(1)} %get-tuple-element.338.info, f32[512,512]{1,0:T(8,128)S(1)} %inner.1.grad_inner, f32[512,512]{1,0:T(8,128)S(1)} %get-tuple-element.213.mixed, ...), custom_call_target="tpu_custom_call" | custom-call | tf_op jit(solution)/shard_map/through/pallas_call | solution.py:296
  45.5 20.1 %back.1 = (bf16[16,64,512]{2,1,0:T(8,128)(2,1)S(1)}, bf16[1040,512]{1,0:T(8,128)(2,1)}, f32[512,512]{1,0:T(8,128)}, bf16[528,512]{1,0:T(8,128)(2,1)S(1)}, f32[8,512]{1,0:T(8,128)S(1)}) custom-call(s32[16]{0:T(128)S(1)} %get-tuple-element.338.info, bf16[256,512]{1,0:T(8,128)(2,1)S(1)} %get-tuple-element.189.q_l.ql, ...), custom_call_target="tpu_custom_call" | custom-call | tf_op jit(solution)/shard_map/back/pallas_call | solution.py:471
  67.8 1.8 %collective-permute-start.9 = (bf16[512,128]{1,0:T(8,128)(2,1)S(1)}, bf16[512,128]{1,0:T(8,128)(2,1)S(1)}, u32[]{:S(2)}, u32[]{:S(2)}) collective-permute-start(bf16[512,128]{1,0:T(8,128)(2,1)S(1)} %get-tuple-element.251), channel_id=1, source_target_pairs={{0,8},{1,9},{2,10},{3,11},{4,12},{5,13},{6,14},{7,15},{8,0},{9,1},... | collective-permute-start | bytes 393224 | tf_op jit(solution)/shard_map/ppermute | solution.py:595
  69.6 2.6 %collective-permute-start.10 = (bf16[512,128]{1,0:T(8,128)(2,1)S(1)}, bf16[512,128]{1,0:T(8,128)(2,1)S(1)}, u32[]{:S(2)}, u32[]{:S(2)}) collective-permute-start(bf16[512,128]{1,0:T(8,128)(2,1)S(1)} %get-tuple-element.252), channel_id=1, source_target_pairs={{0,16},{1,17},{2,18},{3,19},{4,20},{5,21},{6,22},{7,23},{8,24},{9,... | collective-permute-start | bytes 393224 | tf_op jit(solution)/shard_map/ppermute | solution.py:595
  72.7 1.7 %collective-permute-start.12 = (bf16[272,512]{1,0:T(8,128)(2,1)S(1)}, bf16[272,512]{1,0:T(8,128)(2,1)S(1)}, u32[]{:S(2)}, u32[]{:S(2)}) collective-permute-start(bf16[272,512]{1,0:T(8,128)(2,1)S(1)} %get-tuple-element.264), channel_id=1, source_target_pairs={{0,2},{1,3},{2,0},{3,1},{4,6},{5,7},{6,4},{7,5},{8,10},{9,11},{10,... | collective-permute-start | bytes 835592 | tf_op jit(solution)/shard_map/ppermute | solution.py:595
  74.4 1.5 %collective-permute-start.13 = (bf16[272,512]{1,0:T(8,128)(2,1)S(1)}, bf16[272,512]{1,0:T(8,128)(2,1)S(1)}, u32[]{:S(2)}, u32[]{:S(2)}) collective-permute-start(bf16[272,512]{1,0:T(8,128)(2,1)S(1)} %get-tuple-element.265), channel_id=1, source_target_pairs={{0,4},{1,5},{2,6},{3,7},{4,0},{5,1},{6,2},{7,3},{8,12},{9,13},{10,... | collective-permute-start | bytes 835592 | tf_op jit(solution)/shard_map/ppermute | solution.py:595
  75.9 1.7 %collective-permute-start.14 = (bf16[272,512]{1,0:T(8,128)(2,1)S(1)}, bf16[272,512]{1,0:T(8,128)(2,1)S(1)}, u32[]{:S(2)}, u32[]{:S(2)}) collective-permute-start(bf16[272,512]{1,0:T(8,128)(2,1)S(1)} %get-tuple-element.266), channel_id=1, source_target_pairs={{0,6},{1,7},{2,4},{3,5},{4,2},{5,3},{6,0},{7,1},{8,14},{9,15},{10,... | collective-permute-start | bytes 835592 | tf_op jit(solution)/shard_map/ppermute | solution.py:595
  78.7 3.8 %collective-permute-done.10 = bf16[512,128]{1,0:T(8,128)(2,1)S(1)} collective-permute-done((bf16[512,128]{1,0:T(8,128)(2,1)S(1)}, bf16[512,128]{1,0:T(8,128)(2,1)S(1)}, u32[]{:S(2)}, u32[]{:S(2)}) %collective-permute-start.10) | collective-permute-done | bytes 131104 | tf_op jit(solution)/shard_map/ppermute | solution.py:595
  82.6 2.5 %collective-permute-start.18 = (bf16[512,128]{1,0:T(8,128)(2,1)S(1)}, bf16[512,128]{1,0:T(8,128)(2,1)S(1)}, u32[]{:S(2)}, u32[]{:S(2)}) collective-permute-start(bf16[512,128]{1,0:T(8,128)(2,1)S(1)} %add_convert_fusion.2), channel_id=1, source_target_pairs={{0,24},{1,25},{2,26},{3,27},{4,28},{5,29},{6,30},{7,31},{8,16},{9,... | collective-permute-start | bytes 393224 | tf_op jit(solution)/shard_map/ppermute | solution.py:595
  87.0 1.6 %collective-permute-start.19 = (bf16[272,512]{1,0:T(8,128)(2,1)S(1)}, bf16[272,512]{1,0:T(8,128)(2,1)S(1)}, u32[]{:S(2)}, u32[]{:S(2)}) collective-permute-start(bf16[272,512]{1,0:T(8,128)(2,1)S(1)} %get-tuple-element.276), channel_id=1, source_target_pairs={{0,2},{1,3},{2,0},{3,1},{4,6},{5,7},{6,4},{7,5},{8,10},{9,11},{10,... | collective-permute-start | bytes 835592 | tf_op jit(solution)/shard_map/ppermute | solution.py:595
  90.2 7.1 %collective-permute-done.15 = bf16[144,512]{1,0:T(8,128)(2,1)S(1)} collective-permute-done((bf16[144,512]{1,0:T(8,128)(2,1)S(1)}, bf16[144,512]{1,0:T(8,128)(2,1)S(1)}, u32[]{:S(2)}, u32[]{:S(2)}) %collective-permute-start.15) | collective-permute-done | bytes 147488 | tf_op jit(solution)/shard_map/ppermute | solution.py:595
  97.6 1.6 %collective-permute-start.22 = (bf16[4,512,128]{2,1,0:T(8,128)(2,1)S(1)}, bf16[4,512,128]{2,1,0:T(8,128)(2,1)S(1)}, u32[]{:S(2)}, u32[]{:S(2)}) collective-permute-start(bf16[4,512,128]{2,1,0:T(8,128)(2,1)S(1)} %pad_maximum_fusion.2), channel_id=1, source_target_pairs={{0,4},{1,5},{2,6},{3,7},{4,0},{5,1},{6,2},{7,3},{8,12},{9,13},{10,... | collective-permute-start | bytes 1572872 | tf_op jit(solution)/shard_map/ppermute | solution.py:595
  99.2 1.5 %collective-permute-start.21 = (bf16[4,512,128]{2,1,0:T(8,128)(2,1)S(1)}, bf16[4,512,128]{2,1,0:T(8,128)(2,1)S(1)}, u32[]{:S(2)}, u32[]{:S(2)}) collective-permute-start(bf16[4,512,128]{2,1,0:T(8,128)(2,1)S(1)} %pad_maximum_fusion.2), channel_id=1, source_target_pairs={{0,2},{1,3},{2,0},{3,1},{4,6},{5,7},{6,4},{7,5},{8,10},{9,11},{10,... | collective-permute-start | bytes 1572872 | tf_op jit(solution)/shard_map/ppermute | solution.py:595
  100.7 1.4 %collective-permute-start.20 = (bf16[144,512]{1,0:T(8,128)(2,1)S(1)}, bf16[144,512]{1,0:T(8,128)(2,1)S(1)}, u32[]{:S(2)}, u32[]{:S(2)}) collective-permute-start(bf16[144,512]{1,0:T(8,128)(2,1)S(1)} %pad_maximum_fusion.13), channel_id=1, source_target_pairs={{0,16},{1,17},{2,18},{3,19},{4,20},{5,21},{6,22},{7,23},{8,24},{9,... | collective-permute-start | bytes 442376 | tf_op jit(solution)/shard_map/ppermute | solution.py:595
  103.6 4.6 %collective-permute-done.20 = bf16[144,512]{1,0:T(8,128)(2,1)S(1)} collective-permute-done((bf16[144,512]{1,0:T(8,128)(2,1)S(1)}, bf16[144,512]{1,0:T(8,128)(2,1)S(1)}, u32[]{:S(2)}, u32[]{:S(2)}) %collective-permute-start.20) | collective-permute-done | bytes 147488 | tf_op jit(solution)/shard_map/ppermute | solution.py:595
  110.3 1.6 %collective-permute-start.24 = (bf16[2,512,128]{2,1,0:T(8,128)(2,1)S(1)}, bf16[2,512,128]{2,1,0:T(8,128)(2,1)S(1)}, u32[]{:S(2)}, u32[]{:S(2)}) collective-permute-start(bf16[2,512,128]{2,1,0:T(8,128)(2,1)S(1)} %slice.251), channel_id=1, source_target_pairs={{0,2},{1,3},{2,0},{3,1},{4,6},{5,7},{6,4},{7,5},{8,10},{9,11},{10,... | collective-permute-start | bytes 786440 | tf_op jit(solution)/shard_map/ppermute | solution.py:595
  113.1 2.3 %place.2 = (f32[2048,512]{1,0:T(8,128)}, f32[512,2048]{1,0:T(8,128)}) custom-call(s32[16]{0:T(128)S(1)} %get-tuple-element.338.info, bf16[12,512,128]{2,1,0:T(8,128)(2,1)S(1)} %pad_maximum_fusion.refs_0_), custom_call_target="tpu_custom_call" | custom-call | tf_op jit(solution)/shard_map/place/pallas_call | solution.py:538
  115.4 2.2 %collective-permute-done.23 = bf16[128,512]{1,0:T(8,128)(2,1)S(1)} collective-permute-done((bf16[128,512]{1,0:T(8,128)(2,1)S(1)}, bf16[128,512]{1,0:T(8,128)(2,1)S(1)}, u32[]{:S(2)}, u32[]{:S(2)}) %collective-permute-start.23) | collective-permute-done | bytes 131104 | tf_op jit(solution)/shard_map/ppermute | solution.py:595
  122.3 3.1 %place.3 = (f32[2048,512]{1,0:T(8,128)}, f32[512,2048]{1,0:T(8,128)}) custom-call(s32[16]{0:T(128)S(1)} %get-tuple-element.338.info, bf16[4,512,128]{2,1,0:T(8,128)(2,1)S(1)} %pad_maximum_fusion.3.refs_0_, bf16[12,512,128]{2,1,0:T(8,128)(2,1)S(1)} %collective-permute-done.26.refs_1_, ...), custom_call_target="tpu_custom_call", output_to_operand_aliasing={{0}: (4, {}), {1}: (5, {})} | custom-call | tf_op jit(solution)/shard_map/place/pallas_call | solution.py:538
  125.4 3.8 %collective-permute-done.29 = bf16[4,64,512]{2,1,0:T(8,128)(2,1)S(1)} collective-permute-done((bf16[4,64,512]{2,1,0:T(8,128)(2,1)S(1)}, bf16[4,64,512]{2,1,0:T(8,128)(2,1)S(1)}, u32[]{:S(2)}, u32[]{:S(2)}) %collective-permute-start.29) | collective-permute-done | bytes 262176 | tf_op jit(solution)/shard_map/ppermute | solution.py:595
  130.1 1.5 %collective-permute-start.31 = (bf16[2,64,512]{2,1,0:T(8,128)(2,1)S(1)}, bf16[2,64,512]{2,1,0:T(8,128)(2,1)S(1)}, u32[]{:S(2)}, u32[]{:S(2)}) collective-permute-start(bf16[2,64,512]{2,1,0:T(8,128)(2,1)S(1)} %slice.258), channel_id=1, source_target_pairs={{0,4},{1,5},{2,6},{3,7},{4,0},{5,1},{6,2},{7,3},{8,12},{9,13},{10,... | collective-permute-start | bytes 393224 | tf_op jit(solution)/shard_map/ppermute | solution.py:595
  131.7 1.9 %sort.3 = (f32[512,512]{1,0:T(8,128)}, f32[512,512]{1,0:T(8,128)}, f32[512,512]{1,0:T(8,128)}, f32[512,512]{1,0:T(8,128)}) custom-call(s32[16]{0:T(128)S(1)} %get-tuple-element.338.info, bf16[12,64,512]{2,1,0:T(8,128)(2,1)S(1)} %pad_maximum_fusion.1.refs_0_), custom_call_target="tpu_custom_call" | custom-call | tf_op jit(solution)/shard_map/sort/pallas_call | solution.py:572
  133.5 1.9 %collective-permute-done.30.refs_0_ = bf16[2,64,512]{2,1,0:T(8,128)(2,1)S(1)} collective-permute-done((bf16[2,64,512]{2,1,0:T(8,128)(2,1)S(1)}, bf16[2,64,512]{2,1,0:T(8,128)(2,1)S(1)}, u32[]{:S(2)}, u32[]{:S(2)}) %collective-permute-start.30) | collective-permute-done | bytes 131104 | tf_op jit(solution)/shard_map/ppermute | solution.py:595
  135.8 2.1 %sort.4 = (f32[512,512]{1,0:T(8,128)}, f32[512,512]{1,0:T(8,128)}, f32[512,512]{1,0:T(8,128)}, f32[512,512]{1,0:T(8,128)}) custom-call(s32[16]{0:T(128)S(1)} %get-tuple-element.338.info, bf16[2,64,512]{2,1,0:T(8,128)(2,1)S(1)} %collective-permute-done.30.refs_0_, ...), custom_call_target="tpu_custom_call", output_to_operand_aliasing={{0}: (4, {}), {1}: (5, {}), {2}: (6, {}), {3}: (7, {})} | custom-call | tf_op jit(solution)/shard_map/sort/pallas_call | solution.py:572
  (124 shorter events, 27.8 us)
Async XLA Ops:
  1.9 3.1 %collective-permute-start.1 = (bf16[256,512]{1,0:T(8,128)(2,1)S(1)}, bf16[256,512]{1,0:T(8,128)(2,1)S(1)}, u32[]{:S(2)}, u32[]{:S(2)}) collective-permute-start(bf16[256,512]{1,0:T(8,128)(2,1)S(1)} %get-tuple-element.184.mine.near.near_h), channel_id=1, source_target_pairs={{0,1},{1,0},{2,3},{3,2},{4,5},{5,4},{6,7},{7,6},{8,9},{9,8},{10,11... | collective-permute-start | bytes 786440 | tf_op jit(solution)/shard_map/ppermute | solution.py:595
  2.4 9.5 %collective-permute-start = (bf16[256,512]{1,0:T(8,128)(2,1)S(1)}, bf16[256,512]{1,0:T(8,128)(2,1)S(1)}, u32[]{:S(2)}, u32[]{:S(2)}) collective-permute-start(bf16[256,512]{1,0:T(8,128)(2,1)S(1)} %get-tuple-element.183), channel_id=1, source_target_pairs={{0,2},{1,3},{2,0},{3,1},{4,6},{5,7},{6,4},{7,5},{8,10},{9,11},{10,... | collective-permute-start | bytes 786440 | tf_op jit(solution)/shard_map/ppermute | solution.py:595
  35.5 4.2 %collective-permute-start.3 = (bf16[16,512,128]{2,1,0:T(8,128)(2,1)S(1)}, bf16[16,512,128]{2,1,0:T(8,128)(2,1)S(1)}, u32[]{:S(2)}, u32[]{:S(2)}) collective-permute-start(bf16[16,512,128]{2,1,0:T(8,128)(2,1)S(1)} %get-tuple-element.203), channel_id=1, source_target_pairs={{0,1},{1,0},{2,3},{3,2},{4,5},{5,4},{6,7},{7,6},{8,9},{9,8},{10,11... | collective-permute-start | bytes 6291464 | tf_op jit(solution)/shard_map/ppermute | solution.py:595
  40.2 25.4 %collective-permute-start.4 = (bf16[4,512,128]{2,1,0:T(8,128)(2,1)S(1)}, bf16[4,512,128]{2,1,0:T(8,128)(2,1)S(1)}, u32[]{:S(2)}, u32[]{:S(2)}) collective-permute-start(bf16[4,512,128]{2,1,0:T(8,128)(2,1)S(1)} %get-tuple-element.231), channel_id=1, source_target_pairs={{0,2},{1,3},{2,0},{3,1},{4,6},{5,7},{6,4},{7,5},{8,10},{9,11},{10,... | collective-permute-start | bytes 1572872 | tf_op jit(solution)/shard_map/ppermute | solution.py:595
  42.1 23.5 %collective-permute-start.5 = (bf16[4,512,128]{2,1,0:T(8,128)(2,1)S(1)}, bf16[4,512,128]{2,1,0:T(8,128)(2,1)S(1)}, u32[]{:S(2)}, u32[]{:S(2)}) collective-permute-start(bf16[4,512,128]{2,1,0:T(8,128)(2,1)S(1)} %get-tuple-element.232), channel_id=1, source_target_pairs={{0,4},{1,5},{2,6},{3,7},{4,0},{5,1},{6,2},{7,3},{8,12},{9,13},{10,... | collective-permute-start | bytes 1572872 | tf_op jit(solution)/shard_map/ppermute | solution.py:595
  43.6 23.5 %collective-permute-start.6 = (bf16[4,512,128]{2,1,0:T(8,128)(2,1)S(1)}, bf16[4,512,128]{2,1,0:T(8,128)(2,1)S(1)}, u32[]{:S(2)}, u32[]{:S(2)}) collective-permute-start(bf16[4,512,128]{2,1,0:T(8,128)(2,1)S(1)} %get-tuple-element.233), channel_id=1, source_target_pairs={{0,6},{1,7},{2,4},{3,5},{4,2},{5,3},{6,0},{7,1},{8,14},{9,15},{10,... | collective-permute-start | bytes 1572872 | tf_op jit(solution)/shard_map/ppermute | solution.py:595
  67.0 5.2 %collective-permute-start.7 = (bf16[1040,512]{1,0:T(8,128)(2,1)}, bf16[1040,512]{1,0:T(8,128)(2,1)S(1)}, u32[]{:S(2)}, u32[]{:S(2)}) collective-permute-start(bf16[1040,512]{1,0:T(8,128)(2,1)} %get-tuple-element.244), channel_id=1, source_target_pairs={{0,1},{1,0},{2,3},{3,2},{4,5},{5,4},{6,7},{7,6},{8,9},{9,8},{10,11... | collective-permute-start | bytes 3194888 | tf_op jit(solution)/shard_map/ppermute | solution.py:595
  67.0 5.2 %collective-permute-start.8 = (bf16[528,512]{1,0:T(8,128)(2,1)S(1)}, bf16[528,512]{1,0:T(8,128)(2,1)S(1)}, u32[]{:S(2)}, u32[]{:S(2)}) collective-permute-start(bf16[528,512]{1,0:T(8,128)(2,1)S(1)} %get-tuple-element.245), channel_id=1, source_target_pairs={{0,1},{1,0},{2,3},{3,2},{4,5},{5,4},{6,7},{7,6},{8,9},{9,8},{10,11... | collective-permute-start | bytes 1622024 | tf_op jit(solution)/shard_map/ppermute | solution.py:595
  67.8 8.1 %collective-permute-start.9 = (bf16[512,128]{1,0:T(8,128)(2,1)S(1)}, bf16[512,128]{1,0:T(8,128)(2,1)S(1)}, u32[]{:S(2)}, u32[]{:S(2)}) collective-permute-start(bf16[512,128]{1,0:T(8,128)(2,1)S(1)} %get-tuple-element.251), channel_id=1, source_target_pairs={{0,8},{1,9},{2,10},{3,11},{4,12},{5,13},{6,14},{7,15},{8,0},{9,1},... | collective-permute-start | bytes 393224 | tf_op jit(solution)/shard_map/ppermute | solution.py:595
  69.6 12.9 %collective-permute-start.10 = (bf16[512,128]{1,0:T(8,128)(2,1)S(1)}, bf16[512,128]{1,0:T(8,128)(2,1)S(1)}, u32[]{:S(2)}, u32[]{:S(2)}) collective-permute-start(bf16[512,128]{1,0:T(8,128)(2,1)S(1)} %get-tuple-element.252), channel_id=1, source_target_pairs={{0,16},{1,17},{2,18},{3,19},{4,20},{5,21},{6,22},{7,23},{8,24},{9,... | collective-permute-start | bytes 393224 | tf_op jit(solution)/shard_map/ppermute | solution.py:595
  72.2 10.3 %collective-permute-start.11 = (bf16[512,128]{1,0:T(8,128)(2,1)S(1)}, bf16[512,128]{1,0:T(8,128)(2,1)S(1)}, u32[]{:S(2)}, u32[]{:S(2)}) collective-permute-start(bf16[512,128]{1,0:T(8,128)(2,1)S(1)} %get-tuple-element.253), channel_id=1, source_target_pairs={{0,24},{1,25},{2,26},{3,27},{4,28},{5,29},{6,30},{7,31},{8,16},{9,... | collective-permute-start | bytes 393224 | tf_op jit(solution)/shard_map/ppermute | solution.py:595
  72.7 13.6 %collective-permute-start.12 = (bf16[272,512]{1,0:T(8,128)(2,1)S(1)}, bf16[272,512]{1,0:T(8,128)(2,1)S(1)}, u32[]{:S(2)}, u32[]{:S(2)}) collective-permute-start(bf16[272,512]{1,0:T(8,128)(2,1)S(1)} %get-tuple-element.264), channel_id=1, source_target_pairs={{0,2},{1,3},{2,0},{3,1},{4,6},{5,7},{6,4},{7,5},{8,10},{9,11},{10,... | collective-permute-start | bytes 835592 | tf_op jit(solution)/shard_map/ppermute | solution.py:595
  74.4 12.6 %collective-permute-start.13 = (bf16[272,512]{1,0:T(8,128)(2,1)S(1)}, bf16[272,512]{1,0:T(8,128)(2,1)S(1)}, u32[]{:S(2)}, u32[]{:S(2)}) collective-permute-start(bf16[272,512]{1,0:T(8,128)(2,1)S(1)} %get-tuple-element.265), channel_id=1, source_target_pairs={{0,4},{1,5},{2,6},{3,7},{4,0},{5,1},{6,2},{7,3},{8,12},{9,13},{10,... | collective-permute-start | bytes 835592 | tf_op jit(solution)/shard_map/ppermute | solution.py:595
  75.9 12.7 %collective-permute-start.14 = (bf16[272,512]{1,0:T(8,128)(2,1)S(1)}, bf16[272,512]{1,0:T(8,128)(2,1)S(1)}, u32[]{:S(2)}, u32[]{:S(2)}) collective-permute-start(bf16[272,512]{1,0:T(8,128)(2,1)S(1)} %get-tuple-element.266), channel_id=1, source_target_pairs={{0,6},{1,7},{2,4},{3,5},{4,2},{5,3},{6,0},{7,1},{8,14},{9,15},{10,... | collective-permute-start | bytes 835592 | tf_op jit(solution)/shard_map/ppermute | solution.py:595
  82.6 14.9 %collective-permute-start.18 = (bf16[512,128]{1,0:T(8,128)(2,1)S(1)}, bf16[512,128]{1,0:T(8,128)(2,1)S(1)}, u32[]{:S(2)}, u32[]{:S(2)}) collective-permute-start(bf16[512,128]{1,0:T(8,128)(2,1)S(1)} %add_convert_fusion.2), channel_id=1, source_target_pairs={{0,24},{1,25},{2,26},{3,27},{4,28},{5,29},{6,30},{7,31},{8,16},{9,... | collective-permute-start | bytes 393224 | tf_op jit(solution)/shard_map/ppermute | solution.py:595
  85.0 12.4 %collective-permute-start.17 = (bf16[512,128]{1,0:T(8,128)(2,1)S(1)}, bf16[512,128]{1,0:T(8,128)(2,1)S(1)}, u32[]{:S(2)}, u32[]{:S(2)}) collective-permute-start(bf16[512,128]{1,0:T(8,128)(2,1)S(1)} %add_convert_fusion.2), channel_id=1, source_target_pairs={{0,16},{1,17},{2,18},{3,19},{4,20},{5,21},{6,22},{7,23},{8,24},{9,... | collective-permute-start | bytes 393224 | tf_op jit(solution)/shard_map/ppermute | solution.py:595
  86.2 11.2 %collective-permute-start.16 = (bf16[512,128]{1,0:T(8,128)(2,1)S(1)}, bf16[512,128]{1,0:T(8,128)(2,1)S(1)}, u32[]{:S(2)}, u32[]{:S(2)}) collective-permute-start(bf16[512,128]{1,0:T(8,128)(2,1)S(1)} %add_convert_fusion.2), channel_id=1, source_target_pairs={{0,8},{1,9},{2,10},{3,11},{4,12},{5,13},{6,14},{7,15},{8,0},{9,1},... | collective-permute-start | bytes 393224 | tf_op jit(solution)/shard_map/ppermute | solution.py:595
  87.0 10.4 %collective-permute-start.19 = (bf16[272,512]{1,0:T(8,128)(2,1)S(1)}, bf16[272,512]{1,0:T(8,128)(2,1)S(1)}, u32[]{:S(2)}, u32[]{:S(2)}) collective-permute-start(bf16[272,512]{1,0:T(8,128)(2,1)S(1)} %get-tuple-element.276), channel_id=1, source_target_pairs={{0,2},{1,3},{2,0},{3,1},{4,6},{5,7},{6,4},{7,5},{8,10},{9,11},{10,... | collective-permute-start | bytes 835592 | tf_op jit(solution)/shard_map/ppermute | solution.py:595
  88.9 8.4 %collective-permute-start.15 = (bf16[144,512]{1,0:T(8,128)(2,1)S(1)}, bf16[144,512]{1,0:T(8,128)(2,1)S(1)}, u32[]{:S(2)}, u32[]{:S(2)}) collective-permute-start(bf16[144,512]{1,0:T(8,128)(2,1)S(1)} %pad_maximum_fusion.12), channel_id=1, source_target_pairs={{0,8},{1,9},{2,10},{3,11},{4,12},{5,13},{6,14},{7,15},{8,0},{9,1},... | collective-permute-start | bytes 442376 | tf_op jit(solution)/shard_map/ppermute | solution.py:595
  97.6 11.9 %collective-permute-start.22 = (bf16[4,512,128]{2,1,0:T(8,128)(2,1)S(1)}, bf16[4,512,128]{2,1,0:T(8,128)(2,1)S(1)}, u32[]{:S(2)}, u32[]{:S(2)}) collective-permute-start(bf16[4,512,128]{2,1,0:T(8,128)(2,1)S(1)} %pad_maximum_fusion.2), channel_id=1, source_target_pairs={{0,4},{1,5},{2,6},{3,7},{4,0},{5,1},{6,2},{7,3},{8,12},{9,13},{10,... | collective-permute-start | bytes 1572872 | tf_op jit(solution)/shard_map/ppermute | solution.py:595
  99.2 10.8 %collective-permute-start.21 = (bf16[4,512,128]{2,1,0:T(8,128)(2,1)S(1)}, bf16[4,512,128]{2,1,0:T(8,128)(2,1)S(1)}, u32[]{:S(2)}, u32[]{:S(2)}) collective-permute-start(bf16[4,512,128]{2,1,0:T(8,128)(2,1)S(1)} %pad_maximum_fusion.2), channel_id=1, source_target_pairs={{0,2},{1,3},{2,0},{3,1},{4,6},{5,7},{6,4},{7,5},{8,10},{9,11},{10,... | collective-permute-start | bytes 1572872 | tf_op jit(solution)/shard_map/ppermute | solution.py:595
  100.7 7.5 %collective-permute-start.20 = (bf16[144,512]{1,0:T(8,128)(2,1)S(1)}, bf16[144,512]{1,0:T(8,128)(2,1)S(1)}, u32[]{:S(2)}, u32[]{:S(2)}) collective-permute-start(bf16[144,512]{1,0:T(8,128)(2,1)S(1)} %pad_maximum_fusion.13), channel_id=1, source_target_pairs={{0,16},{1,17},{2,18},{3,19},{4,20},{5,21},{6,22},{7,23},{8,24},{9,... | collective-permute-start | bytes 442376 | tf_op jit(solution)/shard_map/ppermute | solution.py:595
  110.2 10.0 %collective-permute-start.26 = (bf16[12,512,128]{2,1,0:T(8,128)(2,1)S(1)}, bf16[12,512,128]{2,1,0:T(8,128)(2,1)S(1)}, u32[]{:S(2)}, u32[]{:S(2)}) collective-permute-start(bf16[12,512,128]{2,1,0:T(8,128)(2,1)S(1)} %pad_maximum_fusion.refs_0_), channel_id=1, source_target_pairs={{0,1},{1,0},{2,3},{3,2},{4,5},{5,4},{6,7},{7,6},{8,9},{9,8},{10,11... | collective-permute-start | bytes 4718600 | tf_op jit(solution)/shard_map/ppermute | solution.py:595
  110.3 8.7 %collective-permute-start.24 = (bf16[2,512,128]{2,1,0:T(8,128)(2,1)S(1)}, bf16[2,512,128]{2,1,0:T(8,128)(2,1)S(1)}, u32[]{:S(2)}, u32[]{:S(2)}) collective-permute-start(bf16[2,512,128]{2,1,0:T(8,128)(2,1)S(1)} %slice.251), channel_id=1, source_target_pairs={{0,2},{1,3},{2,0},{3,1},{4,6},{5,7},{6,4},{7,5},{8,10},{9,11},{10,... | collective-permute-start | bytes 786440 | tf_op jit(solution)/shard_map/ppermute | solution.py:595
  111.8 8.4 %collective-permute-start.25 = (bf16[2,512,128]{2,1,0:T(8,128)(2,1)S(1)}, bf16[2,512,128]{2,1,0:T(8,128)(2,1)S(1)}, u32[]{:S(2)}, u32[]{:S(2)}) collective-permute-start(bf16[2,512,128]{2,1,0:T(8,128)(2,1)S(1)} %slice.252), channel_id=1, source_target_pairs={{0,4},{1,5},{2,6},{3,7},{4,0},{5,1},{6,2},{7,3},{8,12},{9,13},{10,... | collective-permute-start | bytes 786440 | tf_op jit(solution)/shard_map/ppermute | solution.py:595
  112.4 5.3 %collective-permute-start.23 = (bf16[128,512]{1,0:T(8,128)(2,1)S(1)}, bf16[128,512]{1,0:T(8,128)(2,1)S(1)}, u32[]{:S(2)}, u32[]{:S(2)}) collective-permute-start(bf16[128,512]{1,0:T(8,128)(2,1)S(1)} %add_convert_fusion), channel_id=1, source_target_pairs={{0,8},{1,9},{2,10},{3,11},{4,12},{5,13},{6,14},{7,15},{8,0},{9,1},... | collective-permute-start | bytes 393224 | tf_op jit(solution)/shard_map/ppermute | solution.py:595
  120.4 8.7 %collective-permute-start.29 = (bf16[4,64,512]{2,1,0:T(8,128)(2,1)S(1)}, bf16[4,64,512]{2,1,0:T(8,128)(2,1)S(1)}, u32[]{:S(2)}, u32[]{:S(2)}) collective-permute-start(bf16[4,64,512]{2,1,0:T(8,128)(2,1)S(1)} %pad_maximum_fusion.10), channel_id=1, source_target_pairs={{0,4},{1,5},{2,6},{3,7},{4,0},{5,1},{6,2},{7,3},{8,12},{9,13},{10,... | collective-permute-start | bytes 786440 | tf_op jit(solution)/shard_map/ppermute | solution.py:595
  121.0 8.4 %collective-permute-start.28 = (bf16[4,64,512]{2,1,0:T(8,128)(2,1)S(1)}, bf16[4,64,512]{2,1,0:T(8,128)(2,1)S(1)}, u32[]{:S(2)}, u32[]{:S(2)}) collective-permute-start(bf16[4,64,512]{2,1,0:T(8,128)(2,1)S(1)} %pad_maximum_fusion.10), channel_id=1, source_target_pairs={{0,2},{1,3},{2,0},{3,1},{4,6},{5,7},{6,4},{7,5},{8,10},{9,11},{10,... | collective-permute-start | bytes 786440 | tf_op jit(solution)/shard_map/ppermute | solution.py:595
  129.5 6.2 %collective-permute-start.32 = (bf16[12,64,512]{2,1,0:T(8,128)(2,1)S(1)}, bf16[12,64,512]{2,1,0:T(8,128)(2,1)S(1)}, u32[]{:S(2)}, u32[]{:S(2)}) collective-permute-start(bf16[12,64,512]{2,1,0:T(8,128)(2,1)S(1)} %pad_maximum_fusion.1.refs_0_), channel_id=1, source_target_pairs={{0,1},{1,0},{2,3},{3,2},{4,5},{5,4},{6,7},{7,6},{8,9},{9,8},{10,11... | collective-permute-start | bytes 2359304 | tf_op jit(solution)/shard_map/ppermute | solution.py:595
  129.6 5.9 %collective-permute-start.30 = (bf16[2,64,512]{2,1,0:T(8,128)(2,1)S(1)}, bf16[2,64,512]{2,1,0:T(8,128)(2,1)S(1)}, u32[]{:S(2)}, u32[]{:S(2)}) collective-permute-start(bf16[2,64,512]{2,1,0:T(8,128)(2,1)S(1)} %slice.257), channel_id=1, source_target_pairs={{0,2},{1,3},{2,0},{3,1},{4,6},{5,7},{6,4},{7,5},{8,10},{9,11},{10,... | collective-permute-start | bytes 393224 | tf_op jit(solution)/shard_map/ppermute | solution.py:595
  130.1 5.6 %collective-permute-start.31 = (bf16[2,64,512]{2,1,0:T(8,128)(2,1)S(1)}, bf16[2,64,512]{2,1,0:T(8,128)(2,1)S(1)}, u32[]{:S(2)}, u32[]{:S(2)}) collective-permute-start(bf16[2,64,512]{2,1,0:T(8,128)(2,1)S(1)} %slice.258), channel_id=1, source_target_pairs={{0,4},{1,5},{2,6},{3,7},{4,0},{5,1},{6,2},{7,3},{8,12},{9,13},{10,... | collective-permute-start | bytes 393224 | tf_op jit(solution)/shard_map/ppermute | solution.py:595
  135.7 2.2 %collective-permute-start.33 = (bf16[4,64,512]{2,1,0:T(8,128)(2,1)S(1)}, bf16[4,64,512]{2,1,0:T(8,128)(2,1)S(1)}, u32[]{:S(2)}, u32[]{:S(2)}) collective-permute-start(bf16[4,64,512]{2,1,0:T(8,128)(2,1)S(1)} %pad_maximum_fusion.11), channel_id=1, source_target_pairs={{0,1},{1,0},{2,3},{3,2},{4,5},{5,4},{6,7},{7,6},{8,9},{9,8},{10,11... | collective-permute-start | bytes 786440 | tf_op jit(solution)/shard_map/ppermute | solution.py:595
  (18 other events, 125.7 us)

commit v12 on v11

--- a/solution.py
+++ b/solution.py
@@ -115,153 +115,131 @@
             to[(4 * group + b) ^ mine] = made[:, b * 128 : (b + 1) * 128]
 
 def front_kernel(info, far, far_other, near, q_l, k_l, v_l, lines, wq, wk, wv, gain1, gain2, gain3, cots, wo_h, win_h, wback_h,
-                 hid_o, q_o, k_o, v_o, expo_o, inv_o, att_o, send_o, active_o, slopes_o, turned_o, mixed_o, steep_o, rows,
-                 hid, qs, ks, vs, inv, att, send, active, slopes, turned, mixed, steep, wo, win, wback, expo, scores, skewed, edges, sems):
+                 hid, qs, ks, vs, expo_o, inv, att, send, active, slopes, turned, mixed, steep, rows,
+                 wo, win, wback, expo, scores, skewed, edges, sems):
     count, width = near.shape
     hidden = win.shape[1]
-    step = pl.program_id(0)
     late = [pltpu.make_async_copy(a, b, sems.at[i]) for i, (a, b) in enumerate(((wo_h, wo), (win_h, win), (wback_h, wback)))]
-    early = [pltpu.make_async_copy(a, b, sems.at[3 + i]) for i, (a, b) in enumerate(((hid, hid_o), (qs, q_o), (ks, k_o), (vs, v_o)))]
-    dense = [pltpu.make_async_copy(a, b, sems.at[7 + i]) for i, (a, b) in enumerate((
-        (inv, inv_o), (att, att_o), (mixed, mixed_o), (turned, turned_o), (active, active_o), (steep, steep_o), (slopes, slopes_o), (send, send_o)))]
-    kept = lambda g: pltpu.make_async_copy(expo, expo_o.at[pl.ds(2 * g, 2)], sems.at[15])
-
-    @pl.when(step == 0)
+    kept = lambda g: pltpu.make_async_copy(expo, expo_o.at[pl.ds(2 * g, 2)], sems.at[3])
+
+    for copy in late:
+        copy.start()
+    for part, raw in enumerate((far, far_other)):
+        tokens = raw[...].astype(F32)
+        hid[part * count : (part + 1) * count, :] = (tokens * rms_scale(tokens) * gain1[...]).astype(BF16)
+    h = hid[...]
+    qs[...] = dot(h[:count], wq[...]).astype(BF16)
+    ks[...] = dot(h, wk[...]).astype(BF16)
+    vs[...] = dot(h, wv[...]).astype(BF16)
+    column = lax.broadcasted_iota(jnp.int32, (1, 128), 1)
+    for b in range(4):
+        place = info[1 + b] + lax.broadcasted_iota(jnp.int32, (count, 1), 0)
+        gate = jnp.where(place < info[0], 0.0, NEG)
+        for head in range(2):
+            edges[head, b * count : (b + 1) * count, :] = jnp.where(column == (64 if head == 0 else 0), gate, 0.0).astype(BF16)
+    limit = info[0]
+
+    @pl.loop(0, width // 128)
+    def _(step):
+        @pl.when(step > 0)
+        def _():
+            kept(step - 1).wait()
+
+        cols = pl.ds(pl.multiple_of(step * 128, 128), 128)
+        lane = lax.broadcasted_iota(jnp.int32, (1, 128), 1)
+        first = lane < 64
+        starts = [info[1 + b] for b in range(4)]
+        keys = [k_l[:count, cols], k_l[count:, cols], ks[:count, cols], ks[count:, cols]]
+        values = jnp.concatenate([v_l[:, cols], vs[:, cols]])
+        query = jnp.concatenate([q_l[:, cols], qs[:, cols]])
+        made = []
+        for head in range(2):
+            mine = jnp.where(first if head == 0 else lane >= 64, 1.0, 0.0).astype(BF16)
+            one = jnp.where(lane == (64 if head == 0 else 0), 1.0, 0.0).astype(BF16)
+            q = query * mine + one
+            v = values * mine + one
+            skewed[head] = skew(lines[pl.ds(2 * step + head, 1), :], lines.shape[1])
+            k = jnp.concatenate(keys) * mine + edges[head]
+            for half in range(2):
+                s = dot(q[half * 256 : (half + 1) * 256], k, NT)
+                for r in range(2):
+                    for b in range(4):
+                        at = starts[b] - starts[2 * half] + 896 - 128 * r
+                        part = s[r * 128 : (r + 1) * 128, b * 256 : (b + 1) * 256] + skewed[head, :, pl.ds(pl.multiple_of(at, 128), 256)]
+                        scores[head, half * 256 + r * 128 : half * 256 + (r + 1) * 128, b * 256 : (b + 1) * 256] = part
+            accs = []
+            for r in range(4):
+                rs = slice(r * 128, (r + 1) * 128)
+                value = scores[head, rs, :]
+                top = jnp.max(value, axis=1, keepdims=True)
+                e = jnp.exp(value - top).astype(BF16)
+                expo[head, rs, :] = e
+                accs.append(dot(e, v))
+            acc = jnp.concatenate(accs)
+            made.append((acc, 1.0 / (acc[:, 64:65] if head == 0 else acc[:, 0:1])))
+        (a0, i0), (a1, i1) = made
+        scale = jnp.where(first, i0, i1)
+        att[:, cols] = (jnp.where(first, a0, a1) * scale).astype(BF16)
+        inv[:, cols] = scale
+        kept(step).start()
+
+    for copy in late:
+        copy.wait()
+    for part, raw in enumerate((near, far)):
+        spot = slice(part * count, (part + 1) * count)
+        mixed[spot, :] = raw[...].astype(F32) + dot(att[spot, :], wo[...])
+    values = mixed[...]
+    inner = (values * rms_scale(values) * gain2[...]).astype(BF16)
+    turned[...] = inner.T
+    total = values
+    for at in range(0, hidden, 512):
+        lifted = jnp.maximum(dot(inner, win[:, at : at + 512]), 0.0).astype(BF16)
+        active[:, at : at + 512] = lifted
+        total = total + dot(lifted, wback[at : at + 512, :])
+    scale = rms_scale(total)
+    place = lax.broadcasted_iota(jnp.int32, (2 * count, 1), 0)
+    place = jnp.where(place < count, place + info[1], place + (info[3] - count))
+    live = jnp.where((place >= info[5]) & (place < limit), 1.0, 0.0)
+    pool = jnp.sum(total * scale * gain3[...] * live, axis=0, keepdims=True)
+    cot = jnp.where(info[8] == 0, cots[0:1, :], cots[1:2, :]) / (limit - info[5]).astype(F32)
+    slope, grad_end = norm_back(live * cot, total, scale, gain3[...])
+    steep[...] = slope
+    rows[...] = jnp.concatenate([pool, grad_end, jnp.zeros((6, width), F32)])
+    low = slope.astype(BF16)
+    for at in range(0, hidden, 512):
+        through = dot(low, wback[at : at + 512, :], NT).astype(BF16)
+        slopes[:, at : at + 512] = jnp.where(active[:, at : at + 512] > 0, through, jnp.zeros_like(through))
+    mine = info[6] & 15
+
+    @pl.when(info[7] == 0)
     def _():
-        for copy in late:
-            copy.start()
-        for part, raw in enumerate((far, far_other)):
-            tokens = raw[...].astype(F32)
-            hid[part * count : (part + 1) * count, :] = (tokens * rms_scale(tokens) * gain1[...]).astype(BF16)
-        h = hid[...]
-        qs[...] = dot(h[:count], wq[...]).astype(BF16)
-        ks[...] = dot(h, wk[...]).astype(BF16)
-        vs[...] = dot(h, wv[...]).astype(BF16)
-        for copy in early:
-            copy.start()
-        column = lax.broadcasted_iota(jnp.int32, (1, 128), 1)
-        for b in range(4):
-            place = info[1 + b] + lax.broadcasted_iota(jnp.int32, (count, 1), 0)
-            gate = jnp.where(place < info[0], 0.0, NEG)
-            for head in range(2):
-                edges[head, b * count : (b + 1) * count, :] = jnp.where(column == (64 if head == 0 else 0), gate, 0.0).astype(BF16)
-
-    @pl.when(step > 0)
+        in_pieces(send, slopes, turned[...], mine)
+
+    @pl.when(info[7] == 1)
     def _():
-        kept(step - 1).wait()
-
-    cols = pl.ds(pl.multiple_of(step * 128, 128), 128)
-    lane = lax.broadcasted_iota(jnp.int32, (1, 128), 1)
-    first = lane < 64
-    limit = info[0]
-    starts = [info[1 + b] for b in range(4)]
-    keys = [k_l[:count, :], k_l[count:, :], ks[:count, cols], ks[count:, cols]]
-    values = jnp.concatenate([v_l[...], vs[:, cols]])
-    query = jnp.concatenate([q_l[...], qs[:, cols]])
-    made = []
-    for head in range(2):
-        mine = jnp.where(first if head == 0 else lane >= 64, 1.0, 0.0).astype(BF16)
-        one = jnp.where(lane == (64 if head == 0 else 0), 1.0, 0.0).astype(BF16)
-        q = query * mine + one
-        v = values * mine + one
-        skewed[head] = skew(lines[pl.ds(2 * step + head, 1), :], lines.shape[1])
-        k = jnp.concatenate(keys) * mine + edges[head]
-        for half in range(2):
-            s = dot(q[half * 256 : (half + 1) * 256], k, NT)
-            for r in range(2):
-                for b in range(4):
-                    at = starts[b] - starts[2 * half] + 896 - 128 * r
-                    part = s[r * 128 : (r + 1) * 128, b * 256 : (b + 1) * 256] + skewed[head, :, pl.ds(pl.multiple_of(at, 128), 256)]
-                    scores[head, half * 256 + r * 128 : half * 256 + (r + 1) * 128, b * 256 : (b + 1) * 256] = part
-        accs = []
-        for r in range(4):
-            rs = slice(r * 128, (r + 1) * 128)
-            value = scores[head, rs, :]
-            top = jnp.max(value, axis=1, keepdims=True)
-            e = jnp.exp(value - top).astype(BF16)
-            expo[head, rs, :] = e
-            accs.append(dot(e, v))
-        acc = jnp.concatenate(accs)
-        made.append((acc, 1.0 / (acc[:, 64:65] if head == 0 else acc[:, 0:1])))
-    (a0, i0), (a1, i1) = made
-    scale = jnp.where(first, i0, i1)
-    att[:, cols] = (jnp.where(first, a0, a1) * scale).astype(BF16)
-    inv[:, cols] = scale
-    kept(step).start()
-
-    @pl.when(step == 3)
-    def _():
-        for copy in late:
-            copy.wait()
-        dense[0].start()
-        dense[1].start()
-        for part, raw in enumerate((near, far)):
-            spot = slice(part * count, (part + 1) * count)
-            mixed[spot, :] = raw[...].astype(F32) + dot(att[spot, :], wo[...])
-        dense[2].start()
-        values = mixed[...]
-        inner = (values * rms_scale(values) * gain2[...]).astype(BF16)
-        turned[...] = inner.T
-        dense[3].start()
-        total = values
-        for at in range(0, hidden, 512):
-            lifted = jnp.maximum(dot(inner, win[:, at : at + 512]), 0.0).astype(BF16)
-            active[:, at : at + 512] = lifted
-            total = total + dot(lifted, wback[at : at + 512, :])
-        dense[4].start()
-        scale = rms_scale(total)
-        place = lax.broadcasted_iota(jnp.int32, (2 * count, 1), 0)
-        place = jnp.where(place < count, place + info[1], place + (info[3] - count))
-        live = jnp.where((place >= info[5]) & (place < limit), 1.0, 0.0)
-        pool = jnp.sum(total * scale * gain3[...] * live, axis=0, keepdims=True)
-        cot = jnp.where(info[8] == 0, cots[0:1, :], cots[1:2, :]) / (limit - info[5]).astype(F32)
-        slope, grad_end = norm_back(live * cot, total, scale, gain3[...])
-        steep[...] = slope
-        dense[5].start()
-        rows[...] = jnp.concatenate([pool, grad_end, jnp.zeros((6, width), F32)])
-        low = slope.astype(BF16)
-        for at in range(0, hidden, 512):
-            through = dot(low, wback[at : at + 512, :], NT).astype(BF16)
-            slopes[:, at : at + 512] = jnp.where(active[:, at : at + 512] > 0, through, jnp.zeros_like(through))
-        dense[6].start()
-        mine = info[6] & 15
-
-        @pl.when(info[7] == 0)
-        def _():
-            in_pieces(send, slopes, turned[...], mine)
-
-        @pl.when(info[7] == 1)
-        def _():
-            back_pieces(send, active, steep[...].astype(BF16), mine)
-
-        dense[7].start()
-        for copy in early + dense:
-            copy.wait()
-        kept(step).wait()
+        back_pieces(send, active, steep[...].astype(BF16), mine)
+
+    kept(3).wait()
+
 
 def front(info, far, far_other, near, q_l, k_l, v_l, lines, wq, wk, wv, gain1, gain2, gain3, cots, wo, win, wback):
     count, width = near.shape
     hidden = win.shape[1]
     heads, span = lines.shape
     shape = jax.ShapeDtypeStruct
-    smem, free = pl.BlockSpec(memory_space=pltpu.SMEM), pl.BlockSpec(memory_space=pl.ANY)
-    whole = lambda *dims: pl.BlockSpec(dims, lambda g: (0,) * len(dims))
-    col = lambda n: pl.BlockSpec((n, 128), lambda g: (0, g))
+    smem, vmem, free = (pl.BlockSpec(memory_space=m) for m in (pltpu.SMEM, pltpu.VMEM, pl.ANY))
     outs = [shape((2 * count, width), BF16), shape((count, width), BF16), shape((2 * count, width), BF16), shape((2 * count, width), BF16),
             shape((heads, 2 * count, 4 * count), BF16), shape((2 * count, width), F32), shape((2 * count, width), BF16),
             shape((16, width, 128), BF16), shape((2 * count, hidden), BF16), shape((2 * count, hidden), BF16),
             shape((width, 2 * count), BF16), shape((2 * count, width), F32), shape((2 * count, width), F32)]
     return pl.pallas_call(
         front_kernel,
-        grid=(heads // 2,),
-        in_specs=[smem] + [whole(count, width)] * 3 + [col(count), col(2 * count), col(2 * count), whole(heads, span)] + [whole(width, width)] * 3 + [whole(1, width)] * 3
-                 + [whole(2, width)] + [pl.BlockSpec(memory_space=pltpu.HBM)] * 3,
-        out_specs=[free] * 13 + [whole(8, width)],
+        in_specs=[smem] + [vmem] * 14 + [free] * 3,
+        out_specs=[vmem] * 4 + [free] + [vmem] * 9,
         out_shape=outs + [shape((8, width), F32)],
-        scratch_shapes=[pltpu.VMEM(o.shape, o.dtype) for o in outs[:4] + outs[5:]]
-                       + [pltpu.VMEM(wo.shape, BF16), pltpu.VMEM(win.shape, BF16), pltpu.VMEM(wback.shape, BF16),
-                          pltpu.VMEM((2, 2 * count, 4 * count), BF16), pltpu.VMEM((2, 2 * count, 4 * count), F32),
-                          pltpu.VMEM((2, 128, span), F32), pltpu.VMEM((2, 4 * count, 128), BF16), pltpu.SemaphoreType.DMA((16,))],
+        scratch_shapes=[pltpu.VMEM(wo.shape, BF16), pltpu.VMEM(win.shape, BF16), pltpu.VMEM(wback.shape, BF16),
+                        pltpu.VMEM((2, 2 * count, 4 * count), BF16), pltpu.VMEM((2, 2 * count, 4 * count), F32),
+                        pltpu.VMEM((2, 128, span), F32), pltpu.VMEM((2, 4 * count, 128), BF16), pltpu.SemaphoreType.DMA((4,))],
         name="front", compiler_params=pltpu.CompilerParams(vmem_limit_bytes=38 << 20),
     )(info, far, far_other, near, q_l, k_l, v_l, lines, wq, wk, wv, gain1, gain2, gain3, cots, wo, win, wback)
 

time: 140 us -> 138 us (0.986)
  Pallas kernels: 63 us -> 61.4 us
    pallas_call x1, Pallas kernels: 22 us -> 20.4 us  [front(): pl.pallas_call(front_kernel, in_specs=[smem] + [vmem] * 14 + [free] * 3,...]
where the time goes in v12:
time: 138 us
  Pallas kernels  61.4 us (44%)
  starting transfers between devices  35 us (25%)
  waiting for transfers between devices  31 us (22%)
  local copies, waits for them, and re-layouts  5.41 us (4%)
  other arithmetic  3.76 us (3%)
    ppermute x34, starting transfers between devices, exchange(): lax.ppermute(value, ('dp', 'blk'), [(i, i ^ bits) for i in range(size)])  35 us
    ppermute x34, waiting for transfers between devices, exchange(): lax.ppermute(value, ('dp', 'blk'), [(i, i ^ bits) for i in range(size)])  31 us
    pallas_call x1, Pallas kernels, front(): pl.pallas_call(front_kernel, in_specs=[smem] + [vmem] * 14 + [free] * 3,...  20.4 us
    pallas_call x1, Pallas kernels, back(): pl.pallas_call(back_kernel, grid=(width // 128,), in_specs=[smem, col(cou...  20.1 us
    pallas_call x3, Pallas kernels, sort(): pl.pallas_call(functools.partial(sort_kernel, [first for first, _ in part...  5.39 us
    pallas_call x2, Pallas kernels, place(): pl.pallas_call(functools.partial(place_kernel, [first for first, _ in par...  5.38 us
    unnamed x32, local copies, waits for them, and re-layouts  3.86 us
  transfers between devices with their start and end apart: 34, of which 15 were waited for; matrix products, arithmetic and copies ran while one was open for 3% of the time, Pallas kernels for 28%

profile of v12, /device:TPU:0, one launch (start us, length us, event | category | flops | bytes accessed | tf_op | source)
XLA Modules:
  0.0 137.9 jit_solution(15218884783049707687)
XLA Ops:
  2.4 2.6 %collective-permute-start = (bf16[256,512]{1,0:T(8,128)(2,1)S(1)}, bf16[256,512]{1,0:T(8,128)(2,1)S(1)}, u32[]{:S(2)}, u32[]{:S(2)}) collective-permute-start(bf16[256,512]{1,0:T(8,128)(2,1)S(1)} %get-tuple-element.183), channel_id=1, source_target_pairs={{0,2},{1,3},{2,0},{3,1},{4,6},{5,7},{6,4},{7,5},{8,10},{9,11},{10,... | collective-permute-start | bytes 786440 | tf_op jit(solution)/shard_map/ppermute | solution.py:573
  8.8 1.5 %prepare.1 = (bf16[512,512]{1,0:T(8,128)(2,1)S(1)}, bf16[256,512]{1,0:T(8,128)(2,1)S(1)}, bf16[512,512]{1,0:T(8,128)(2,1)S(1)}, bf16[512,512]{1,0:T(8,128)(2,1)S...) custom-call(bf16[256,512]{1,0:T(8,128)(2,1)S(1)} %get-tuple-element.184.mine.near.near, ...), custom_call_target="tpu_custom_call" | custom-call | tf_op jit(solution)/shard_map/prepare/pallas_call | solution.py:65
  10.4 1.5 %collective-permute-done.far.far_h = bf16[256,512]{1,0:T(8,128)(2,1)S(1)} collective-permute-done((bf16[256,512]{1,0:T(8,128)(2,1)S(1)}, bf16[256,512]{1,0:T(8,128)(2,1)S(1)}, u32[]{:S(2)}, u32[]{:S(2)}) %collective-permute-start) | collective-permute-done | bytes 262176 | tf_op jit(solution)/shard_map/ppermute | solution.py:573
  13.5 20.4 %front.1 = (bf16[512,512]{1,0:T(8,128)(2,1)S(1)}, bf16[256,512]{1,0:T(8,128)(2,1)S(1)}, bf16[512,512]{1,0:T(8,128)(2,1)S(1)}, bf16[512,512]{1,0:T(8,128)(2,1)S(1...) custom-call(s32[16]{0:T(128)S(1)} %get-tuple-element.338.info, ...), custom_call_target="tpu_custom_call" | custom-call | tf_op jit(solution)/shard_map/front/pallas_call | solution.py:235
  34.2 2.0 %stay.1.kept = bf16[4,4,512,128]{3,2,1,0:T(8,128)(2,1)S(1)} custom-call(s32[16]{0:T(128)S(1)} %get-tuple-element.338.info, bf16[512,2048]{1,0:T(8,128)(2,1)S(1)} %get-tuple-element.198.active, bf16[512,2048]{1,0:T(8,128)(2,1)S(1)} %get-tuple-element.199.slopes, bf16[512,512]{1,0:T(8,128)(2,1)S(1)} %get-tuple-element.200.turned, ...), custom_call_target="tpu_custom_call" | custom-call | tf_op jit(solution)/shard_map/stay/pallas_call | solution.py:301
  36.2 1.8 %inner.1.grad_inner = f32[512,512]{1,0:T(8,128)S(1)} custom-call(s32[16]{0:T(128)S(1)} %get-tuple-element.338.info, bf16[512,2048]{1,0:T(8,128)(2,1)S(1)} %get-tuple-element.199.slopes, bf16[512,2048]{1,0:T(8,128)(2,1)S(1)} %copy-done), custom_call_target="tpu_custom_call" | custom-call | tf_op jit(solution)/shard_map/inner/pallas_call | solution.py:255
  38.6 1.8 %collective-permute-start.4 = (bf16[4,512,128]{2,1,0:T(8,128)(2,1)S(1)}, bf16[4,512,128]{2,1,0:T(8,128)(2,1)S(1)}, u32[]{:S(2)}, u32[]{:S(2)}) collective-permute-start(bf16[4,512,128]{2,1,0:T(8,128)(2,1)S(1)} %get-tuple-element.231), channel_id=1, source_target_pairs={{0,2},{1,3},{2,0},{3,1},{4,6},{5,7},{6,4},{7,5},{8,10},{9,11},{10,... | collective-permute-start | bytes 1572872 | tf_op jit(solution)/shard_map/ppermute | solution.py:573
  40.5 1.5 %collective-permute-start.5 = (bf16[4,512,128]{2,1,0:T(8,128)(2,1)S(1)}, bf16[4,512,128]{2,1,0:T(8,128)(2,1)S(1)}, u32[]{:S(2)}, u32[]{:S(2)}) collective-permute-start(bf16[4,512,128]{2,1,0:T(8,128)(2,1)S(1)} %get-tuple-element.232), channel_id=1, source_target_pairs={{0,4},{1,5},{2,6},{3,7},{4,0},{5,1},{6,2},{7,3},{8,12},{9,13},{10,... | collective-permute-start | bytes 1572872 | tf_op jit(solution)/shard_map/ppermute | solution.py:573
  42.2 1.7 %through.1 = (f32[512,512]{1,0:T(8,128)S(1)}, bf16[512,512]{1,0:T(8,128)(2,1)S(1)}, bf16[512,512]{1,0:T(8,128)(2,1)S(1)}, f32[8,512]{1,0:T(8,128)S(1)}) custom-call(s32[16]{0:T(128)S(1)} %get-tuple-element.338.info, f32[512,512]{1,0:T(8,128)S(1)} %inner.1.grad_inner, f32[512,512]{1,0:T(8,128)S(1)} %get-tuple-element.213.mixed, ...), custom_call_target="tpu_custom_call" | custom-call | tf_op jit(solution)/shard_map/through/pallas_call | solution.py:274
  43.9 20.1 %back.1 = (bf16[16,64,512]{2,1,0:T(8,128)(2,1)S(1)}, bf16[1040,512]{1,0:T(8,128)(2,1)}, f32[512,512]{1,0:T(8,128)}, bf16[528,512]{1,0:T(8,128)(2,1)S(1)}, f32[8,512]{1,0:T(8,128)S(1)}) custom-call(s32[16]{0:T(128)S(1)} %get-tuple-element.338.info, bf16[256,512]{1,0:T(8,128)(2,1)S(1)} %get-tuple-element.189.q_l.ql, ...), custom_call_target="tpu_custom_call" | custom-call | tf_op jit(solution)/shard_map/back/pallas_call | solution.py:449
  66.2 1.8 %collective-permute-start.9 = (bf16[512,128]{1,0:T(8,128)(2,1)S(1)}, bf16[512,128]{1,0:T(8,128)(2,1)S(1)}, u32[]{:S(2)}, u32[]{:S(2)}) collective-permute-start(bf16[512,128]{1,0:T(8,128)(2,1)S(1)} %get-tuple-element.251), channel_id=1, source_target_pairs={{0,8},{1,9},{2,10},{3,11},{4,12},{5,13},{6,14},{7,15},{8,0},{9,1},... | collective-permute-start | bytes 393224 | tf_op jit(solution)/shard_map/ppermute | solution.py:573
  68.0 2.6 %collective-permute-start.10 = (bf16[512,128]{1,0:T(8,128)(2,1)S(1)}, bf16[512,128]{1,0:T(8,128)(2,1)S(1)}, u32[]{:S(2)}, u32[]{:S(2)}) collective-permute-start(bf16[512,128]{1,0:T(8,128)(2,1)S(1)} %get-tuple-element.252), channel_id=1, source_target_pairs={{0,16},{1,17},{2,18},{3,19},{4,20},{5,21},{6,22},{7,23},{8,24},{9,... | collective-permute-start | bytes 393224 | tf_op jit(solution)/shard_map/ppermute | solution.py:573
  71.1 1.7 %collective-permute-start.12 = (bf16[272,512]{1,0:T(8,128)(2,1)S(1)}, bf16[272,512]{1,0:T(8,128)(2,1)S(1)}, u32[]{:S(2)}, u32[]{:S(2)}) collective-permute-start(bf16[272,512]{1,0:T(8,128)(2,1)S(1)} %get-tuple-element.264), channel_id=1, source_target_pairs={{0,2},{1,3},{2,0},{3,1},{4,6},{5,7},{6,4},{7,5},{8,10},{9,11},{10,... | collective-permute-start | bytes 835592 | tf_op jit(solution)/shard_map/ppermute | solution.py:573
  72.8 1.5 %collective-permute-start.13 = (bf16[272,512]{1,0:T(8,128)(2,1)S(1)}, bf16[272,512]{1,0:T(8,128)(2,1)S(1)}, u32[]{:S(2)}, u32[]{:S(2)}) collective-permute-start(bf16[272,512]{1,0:T(8,128)(2,1)S(1)} %get-tuple-element.265), channel_id=1, source_target_pairs={{0,4},{1,5},{2,6},{3,7},{4,0},{5,1},{6,2},{7,3},{8,12},{9,13},{10,... | collective-permute-start | bytes 835592 | tf_op jit(solution)/shard_map/ppermute | solution.py:573
  74.3 1.7 %collective-permute-start.14 = (bf16[272,512]{1,0:T(8,128)(2,1)S(1)}, bf16[272,512]{1,0:T(8,128)(2,1)S(1)}, u32[]{:S(2)}, u32[]{:S(2)}) collective-permute-start(bf16[272,512]{1,0:T(8,128)(2,1)S(1)} %get-tuple-element.266), channel_id=1, source_target_pairs={{0,6},{1,7},{2,4},{3,5},{4,2},{5,3},{6,0},{7,1},{8,14},{9,15},{10,... | collective-permute-start | bytes 835592 | tf_op jit(solution)/shard_map/ppermute | solution.py:573
  77.1 3.8 %collective-permute-done.10 = bf16[512,128]{1,0:T(8,128)(2,1)S(1)} collective-permute-done((bf16[512,128]{1,0:T(8,128)(2,1)S(1)}, bf16[512,128]{1,0:T(8,128)(2,1)S(1)}, u32[]{:S(2)}, u32[]{:S(2)}) %collective-permute-start.10) | collective-permute-done | bytes 131104 | tf_op jit(solution)/shard_map/ppermute | solution.py:573
  81.0 2.5 %collective-permute-start.18 = (bf16[512,128]{1,0:T(8,128)(2,1)S(1)}, bf16[512,128]{1,0:T(8,128)(2,1)S(1)}, u32[]{:S(2)}, u32[]{:S(2)}) collective-permute-start(bf16[512,128]{1,0:T(8,128)(2,1)S(1)} %add_convert_fusion.2), channel_id=1, source_target_pairs={{0,24},{1,25},{2,26},{3,27},{4,28},{5,29},{6,30},{7,31},{8,16},{9,... | collective-permute-start | bytes 393224 | tf_op jit(solution)/shard_map/ppermute | solution.py:573
  85.4 1.5 %collective-permute-start.19 = (bf16[272,512]{1,0:T(8,128)(2,1)S(1)}, bf16[272,512]{1,0:T(8,128)(2,1)S(1)}, u32[]{:S(2)}, u32[]{:S(2)}) collective-permute-start(bf16[272,512]{1,0:T(8,128)(2,1)S(1)} %get-tuple-element.276), channel_id=1, source_target_pairs={{0,2},{1,3},{2,0},{3,1},{4,6},{5,7},{6,4},{7,5},{8,10},{9,11},{10,... | collective-permute-start | bytes 835592 | tf_op jit(solution)/shard_map/ppermute | solution.py:573
  88.6 7.2 %collective-permute-done.15 = bf16[144,512]{1,0:T(8,128)(2,1)S(1)} collective-permute-done((bf16[144,512]{1,0:T(8,128)(2,1)S(1)}, bf16[144,512]{1,0:T(8,128)(2,1)S(1)}, u32[]{:S(2)}, u32[]{:S(2)}) %collective-permute-start.15) | collective-permute-done | bytes 147488 | tf_op jit(solution)/shard_map/ppermute | solution.py:573
  96.0 1.5 %collective-permute-start.22 = (bf16[4,512,128]{2,1,0:T(8,128)(2,1)S(1)}, bf16[4,512,128]{2,1,0:T(8,128)(2,1)S(1)}, u32[]{:S(2)}, u32[]{:S(2)}) collective-permute-start(bf16[4,512,128]{2,1,0:T(8,128)(2,1)S(1)} %pad_maximum_fusion.2), channel_id=1, source_target_pairs={{0,4},{1,5},{2,6},{3,7},{4,0},{5,1},{6,2},{7,3},{8,12},{9,13},{10,... | collective-permute-start | bytes 1572872 | tf_op jit(solution)/shard_map/ppermute | solution.py:573
  97.5 1.5 %collective-permute-start.21 = (bf16[4,512,128]{2,1,0:T(8,128)(2,1)S(1)}, bf16[4,512,128]{2,1,0:T(8,128)(2,1)S(1)}, u32[]{:S(2)}, u32[]{:S(2)}) collective-permute-start(bf16[4,512,128]{2,1,0:T(8,128)(2,1)S(1)} %pad_maximum_fusion.2), channel_id=1, source_target_pairs={{0,2},{1,3},{2,0},{3,1},{4,6},{5,7},{6,4},{7,5},{8,10},{9,11},{10,... | collective-permute-start | bytes 1572872 | tf_op jit(solution)/shard_map/ppermute | solution.py:573
  99.1 1.4 %collective-permute-start.20 = (bf16[144,512]{1,0:T(8,128)(2,1)S(1)}, bf16[144,512]{1,0:T(8,128)(2,1)S(1)}, u32[]{:S(2)}, u32[]{:S(2)}) collective-permute-start(bf16[144,512]{1,0:T(8,128)(2,1)S(1)} %pad_maximum_fusion.13), channel_id=1, source_target_pairs={{0,16},{1,17},{2,18},{3,19},{4,20},{5,21},{6,22},{7,23},{8,24},{9,... | collective-permute-start | bytes 442376 | tf_op jit(solution)/shard_map/ppermute | solution.py:573
  102.0 4.6 %collective-permute-done.20 = bf16[144,512]{1,0:T(8,128)(2,1)S(1)} collective-permute-done((bf16[144,512]{1,0:T(8,128)(2,1)S(1)}, bf16[144,512]{1,0:T(8,128)(2,1)S(1)}, u32[]{:S(2)}, u32[]{:S(2)}) %collective-permute-start.20) | collective-permute-done | bytes 147488 | tf_op jit(solution)/shard_map/ppermute | solution.py:573
  108.6 1.6 %collective-permute-start.24 = (bf16[2,512,128]{2,1,0:T(8,128)(2,1)S(1)}, bf16[2,512,128]{2,1,0:T(8,128)(2,1)S(1)}, u32[]{:S(2)}, u32[]{:S(2)}) collective-permute-start(bf16[2,512,128]{2,1,0:T(8,128)(2,1)S(1)} %slice.251), channel_id=1, source_target_pairs={{0,2},{1,3},{2,0},{3,1},{4,6},{5,7},{6,4},{7,5},{8,10},{9,11},{10,... | collective-permute-start | bytes 786440 | tf_op jit(solution)/shard_map/ppermute | solution.py:573
  111.4 2.3 %place.2 = (f32[2048,512]{1,0:T(8,128)}, f32[512,2048]{1,0:T(8,128)}) custom-call(s32[16]{0:T(128)S(1)} %get-tuple-element.338.info, bf16[12,512,128]{2,1,0:T(8,128)(2,1)S(1)} %pad_maximum_fusion.refs_0_), custom_call_target="tpu_custom_call" | custom-call | tf_op jit(solution)/shard_map/place/pallas_call | solution.py:516
  113.8 2.3 %collective-permute-done.23 = bf16[128,512]{1,0:T(8,128)(2,1)S(1)} collective-permute-done((bf16[128,512]{1,0:T(8,128)(2,1)S(1)}, bf16[128,512]{1,0:T(8,128)(2,1)S(1)}, u32[]{:S(2)}, u32[]{:S(2)}) %collective-permute-start.23) | collective-permute-done | bytes 131104 | tf_op jit(solution)/shard_map/ppermute | solution.py:573
  120.7 3.1 %place.3 = (f32[2048,512]{1,0:T(8,128)}, f32[512,2048]{1,0:T(8,128)}) custom-call(s32[16]{0:T(128)S(1)} %get-tuple-element.338.info, bf16[4,512,128]{2,1,0:T(8,128)(2,1)S(1)} %pad_maximum_fusion.3.refs_0_, bf16[12,512,128]{2,1,0:T(8,128)(2,1)S(1)} %collective-permute-done.26.refs_1_, ...), custom_call_target="tpu_custom_call", output_to_operand_aliasing={{0}: (4, {}), {1}: (5, {})} | custom-call | tf_op jit(solution)/shard_map/place/pallas_call | solution.py:516
  123.7 3.8 %collective-permute-done.29 = bf16[4,64,512]{2,1,0:T(8,128)(2,1)S(1)} collective-permute-done((bf16[4,64,512]{2,1,0:T(8,128)(2,1)S(1)}, bf16[4,64,512]{2,1,0:T(8,128)(2,1)S(1)}, u32[]{:S(2)}, u32[]{:S(2)}) %collective-permute-start.29) | collective-permute-done | bytes 262176 | tf_op jit(solution)/shard_map/ppermute | solution.py:573
  128.6 1.4 %collective-permute-start.31 = (bf16[2,64,512]{2,1,0:T(8,128)(2,1)S(1)}, bf16[2,64,512]{2,1,0:T(8,128)(2,1)S(1)}, u32[]{:S(2)}, u32[]{:S(2)}) collective-permute-start(bf16[2,64,512]{2,1,0:T(8,128)(2,1)S(1)} %slice.258), channel_id=1, source_target_pairs={{0,4},{1,5},{2,6},{3,7},{4,0},{5,1},{6,2},{7,3},{8,12},{9,13},{10,... | collective-permute-start | bytes 393224 | tf_op jit(solution)/shard_map/ppermute | solution.py:573
  130.0 1.9 %sort.3 = (f32[512,512]{1,0:T(8,128)}, f32[512,512]{1,0:T(8,128)}, f32[512,512]{1,0:T(8,128)}, f32[512,512]{1,0:T(8,128)}) custom-call(s32[16]{0:T(128)S(1)} %get-tuple-element.338.info, bf16[12,64,512]{2,1,0:T(8,128)(2,1)S(1)} %pad_maximum_fusion.1.refs_0_), custom_call_target="tpu_custom_call" | custom-call | tf_op jit(solution)/shard_map/sort/pallas_call | solution.py:550
  131.9 2.0 %collective-permute-done.30.refs_0_ = bf16[2,64,512]{2,1,0:T(8,128)(2,1)S(1)} collective-permute-done((bf16[2,64,512]{2,1,0:T(8,128)(2,1)S(1)}, bf16[2,64,512]{2,1,0:T(8,128)(2,1)S(1)}, u32[]{:S(2)}, u32[]{:S(2)}) %collective-permute-start.30) | collective-permute-done | bytes 131104 | tf_op jit(solution)/shard_map/ppermute | solution.py:573
  134.2 2.1 %sort.4 = (f32[512,512]{1,0:T(8,128)}, f32[512,512]{1,0:T(8,128)}, f32[512,512]{1,0:T(8,128)}, f32[512,512]{1,0:T(8,128)}) custom-call(s32[16]{0:T(128)S(1)} %get-tuple-element.338.info, bf16[2,64,512]{2,1,0:T(8,128)(2,1)S(1)} %collective-permute-done.30.refs_0_, ...), custom_call_target="tpu_custom_call", output_to_operand_aliasing={{0}: (4, {}), {1}: (5, {}), {2}: (6, {}), {3}: (7, {})} | custom-call | tf_op jit(solution)/shard_map/sort/pallas_call | solution.py:550
  (124 shorter events, 27.8 us)
Async XLA Ops:
  1.9 3.1 %collective-permute-start.1 = (bf16[256,512]{1,0:T(8,128)(2,1)S(1)}, bf16[256,512]{1,0:T(8,128)(2,1)S(1)}, u32[]{:S(2)}, u32[]{:S(2)}) collective-permute-start(bf16[256,512]{1,0:T(8,128)(2,1)S(1)} %get-tuple-element.184.mine.near.near_h), channel_id=1, source_target_pairs={{0,1},{1,0},{2,3},{3,2},{4,5},{5,4},{6,7},{7,6},{8,9},{9,8},{10,11... | collective-permute-start | bytes 786440 | tf_op jit(solution)/shard_map/ppermute | solution.py:573
  2.4 9.5 %collective-permute-start = (bf16[256,512]{1,0:T(8,128)(2,1)S(1)}, bf16[256,512]{1,0:T(8,128)(2,1)S(1)}, u32[]{:S(2)}, u32[]{:S(2)}) collective-permute-start(bf16[256,512]{1,0:T(8,128)(2,1)S(1)} %get-tuple-element.183), channel_id=1, source_target_pairs={{0,2},{1,3},{2,0},{3,1},{4,6},{5,7},{6,4},{7,5},{8,10},{9,11},{10,... | collective-permute-start | bytes 786440 | tf_op jit(solution)/shard_map/ppermute | solution.py:573
  33.9 4.2 %collective-permute-start.3 = (bf16[16,512,128]{2,1,0:T(8,128)(2,1)S(1)}, bf16[16,512,128]{2,1,0:T(8,128)(2,1)S(1)}, u32[]{:S(2)}, u32[]{:S(2)}) collective-permute-start(bf16[16,512,128]{2,1,0:T(8,128)(2,1)S(1)} %get-tuple-element.203), channel_id=1, source_target_pairs={{0,1},{1,0},{2,3},{3,2},{4,5},{5,4},{6,7},{7,6},{8,9},{9,8},{10,11... | collective-permute-start | bytes 6291464 | tf_op jit(solution)/shard_map/ppermute | solution.py:573
  38.6 25.4 %collective-permute-start.4 = (bf16[4,512,128]{2,1,0:T(8,128)(2,1)S(1)}, bf16[4,512,128]{2,1,0:T(8,128)(2,1)S(1)}, u32[]{:S(2)}, u32[]{:S(2)}) collective-permute-start(bf16[4,512,128]{2,1,0:T(8,128)(2,1)S(1)} %get-tuple-element.231), channel_id=1, source_target_pairs={{0,2},{1,3},{2,0},{3,1},{4,6},{5,7},{6,4},{7,5},{8,10},{9,11},{10,... | collective-permute-start | bytes 1572872 | tf_op jit(solution)/shard_map/ppermute | solution.py:573
  40.5 23.6 %collective-permute-start.5 = (bf16[4,512,128]{2,1,0:T(8,128)(2,1)S(1)}, bf16[4,512,128]{2,1,0:T(8,128)(2,1)S(1)}, u32[]{:S(2)}, u32[]{:S(2)}) collective-permute-start(bf16[4,512,128]{2,1,0:T(8,128)(2,1)S(1)} %get-tuple-element.232), channel_id=1, source_target_pairs={{0,4},{1,5},{2,6},{3,7},{4,0},{5,1},{6,2},{7,3},{8,12},{9,13},{10,... | collective-permute-start | bytes 1572872 | tf_op jit(solution)/shard_map/ppermute | solution.py:573
  42.0 23.4 %collective-permute-start.6 = (bf16[4,512,128]{2,1,0:T(8,128)(2,1)S(1)}, bf16[4,512,128]{2,1,0:T(8,128)(2,1)S(1)}, u32[]{:S(2)}, u32[]{:S(2)}) collective-permute-start(bf16[4,512,128]{2,1,0:T(8,128)(2,1)S(1)} %get-tuple-element.233), channel_id=1, source_target_pairs={{0,6},{1,7},{2,4},{3,5},{4,2},{5,3},{6,0},{7,1},{8,14},{9,15},{10,... | collective-permute-start | bytes 1572872 | tf_op jit(solution)/shard_map/ppermute | solution.py:573
  65.4 5.2 %collective-permute-start.7 = (bf16[1040,512]{1,0:T(8,128)(2,1)}, bf16[1040,512]{1,0:T(8,128)(2,1)S(1)}, u32[]{:S(2)}, u32[]{:S(2)}) collective-permute-start(bf16[1040,512]{1,0:T(8,128)(2,1)} %get-tuple-element.244), channel_id=1, source_target_pairs={{0,1},{1,0},{2,3},{3,2},{4,5},{5,4},{6,7},{7,6},{8,9},{9,8},{10,11... | collective-permute-start | bytes 3194888 | tf_op jit(solution)/shard_map/ppermute | solution.py:573
  65.4 5.2 %collective-permute-start.8 = (bf16[528,512]{1,0:T(8,128)(2,1)S(1)}, bf16[528,512]{1,0:T(8,128)(2,1)S(1)}, u32[]{:S(2)}, u32[]{:S(2)}) collective-permute-start(bf16[528,512]{1,0:T(8,128)(2,1)S(1)} %get-tuple-element.245), channel_id=1, source_target_pairs={{0,1},{1,0},{2,3},{3,2},{4,5},{5,4},{6,7},{7,6},{8,9},{9,8},{10,11... | collective-permute-start | bytes 1622024 | tf_op jit(solution)/shard_map/ppermute | solution.py:573
  66.2 8.1 %collective-permute-start.9 = (bf16[512,128]{1,0:T(8,128)(2,1)S(1)}, bf16[512,128]{1,0:T(8,128)(2,1)S(1)}, u32[]{:S(2)}, u32[]{:S(2)}) collective-permute-start(bf16[512,128]{1,0:T(8,128)(2,1)S(1)} %get-tuple-element.251), channel_id=1, source_target_pairs={{0,8},{1,9},{2,10},{3,11},{4,12},{5,13},{6,14},{7,15},{8,0},{9,1},... | collective-permute-start | bytes 393224 | tf_op jit(solution)/shard_map/ppermute | solution.py:573
  68.0 12.9 %collective-permute-start.10 = (bf16[512,128]{1,0:T(8,128)(2,1)S(1)}, bf16[512,128]{1,0:T(8,128)(2,1)S(1)}, u32[]{:S(2)}, u32[]{:S(2)}) collective-permute-start(bf16[512,128]{1,0:T(8,128)(2,1)S(1)} %get-tuple-element.252), channel_id=1, source_target_pairs={{0,16},{1,17},{2,18},{3,19},{4,20},{5,21},{6,22},{7,23},{8,24},{9,... | collective-permute-start | bytes 393224 | tf_op jit(solution)/shard_map/ppermute | solution.py:573
  70.6 10.3 %collective-permute-start.11 = (bf16[512,128]{1,0:T(8,128)(2,1)S(1)}, bf16[512,128]{1,0:T(8,128)(2,1)S(1)}, u32[]{:S(2)}, u32[]{:S(2)}) collective-permute-start(bf16[512,128]{1,0:T(8,128)(2,1)S(1)} %get-tuple-element.253), channel_id=1, source_target_pairs={{0,24},{1,25},{2,26},{3,27},{4,28},{5,29},{6,30},{7,31},{8,16},{9,... | collective-permute-start | bytes 393224 | tf_op jit(solution)/shard_map/ppermute | solution.py:573
  71.1 13.6 %collective-permute-start.12 = (bf16[272,512]{1,0:T(8,128)(2,1)S(1)}, bf16[272,512]{1,0:T(8,128)(2,1)S(1)}, u32[]{:S(2)}, u32[]{:S(2)}) collective-permute-start(bf16[272,512]{1,0:T(8,128)(2,1)S(1)} %get-tuple-element.264), channel_id=1, source_target_pairs={{0,2},{1,3},{2,0},{3,1},{4,6},{5,7},{6,4},{7,5},{8,10},{9,11},{10,... | collective-permute-start | bytes 835592 | tf_op jit(solution)/shard_map/ppermute | solution.py:573
  72.8 12.6 %collective-permute-start.13 = (bf16[272,512]{1,0:T(8,128)(2,1)S(1)}, bf16[272,512]{1,0:T(8,128)(2,1)S(1)}, u32[]{:S(2)}, u32[]{:S(2)}) collective-permute-start(bf16[272,512]{1,0:T(8,128)(2,1)S(1)} %get-tuple-element.265), channel_id=1, source_target_pairs={{0,4},{1,5},{2,6},{3,7},{4,0},{5,1},{6,2},{7,3},{8,12},{9,13},{10,... | collective-permute-start | bytes 835592 | tf_op jit(solution)/shard_map/ppermute | solution.py:573
  74.3 12.7 %collective-permute-start.14 = (bf16[272,512]{1,0:T(8,128)(2,1)S(1)}, bf16[272,512]{1,0:T(8,128)(2,1)S(1)}, u32[]{:S(2)}, u32[]{:S(2)}) collective-permute-start(bf16[272,512]{1,0:T(8,128)(2,1)S(1)} %get-tuple-element.266), channel_id=1, source_target_pairs={{0,6},{1,7},{2,4},{3,5},{4,2},{5,3},{6,0},{7,1},{8,14},{9,15},{10,... | collective-permute-start | bytes 835592 | tf_op jit(solution)/shard_map/ppermute | solution.py:573
  81.0 14.9 %collective-permute-start.18 = (bf16[512,128]{1,0:T(8,128)(2,1)S(1)}, bf16[512,128]{1,0:T(8,128)(2,1)S(1)}, u32[]{:S(2)}, u32[]{:S(2)}) collective-permute-start(bf16[512,128]{1,0:T(8,128)(2,1)S(1)} %add_convert_fusion.2), channel_id=1, source_target_pairs={{0,24},{1,25},{2,26},{3,27},{4,28},{5,29},{6,30},{7,31},{8,16},{9,... | collective-permute-start | bytes 393224 | tf_op jit(solution)/shard_map/ppermute | solution.py:573
  83.4 12.4 %collective-permute-start.17 = (bf16[512,128]{1,0:T(8,128)(2,1)S(1)}, bf16[512,128]{1,0:T(8,128)(2,1)S(1)}, u32[]{:S(2)}, u32[]{:S(2)}) collective-permute-start(bf16[512,128]{1,0:T(8,128)(2,1)S(1)} %add_convert_fusion.2), channel_id=1, source_target_pairs={{0,16},{1,17},{2,18},{3,19},{4,20},{5,21},{6,22},{7,23},{8,24},{9,... | collective-permute-start | bytes 393224 | tf_op jit(solution)/shard_map/ppermute | solution.py:573
  84.6 11.2 %collective-permute-start.16 = (bf16[512,128]{1,0:T(8,128)(2,1)S(1)}, bf16[512,128]{1,0:T(8,128)(2,1)S(1)}, u32[]{:S(2)}, u32[]{:S(2)}) collective-permute-start(bf16[512,128]{1,0:T(8,128)(2,1)S(1)} %add_convert_fusion.2), channel_id=1, source_target_pairs={{0,8},{1,9},{2,10},{3,11},{4,12},{5,13},{6,14},{7,15},{8,0},{9,1},... | collective-permute-start | bytes 393224 | tf_op jit(solution)/shard_map/ppermute | solution.py:573
  85.4 10.4 %collective-permute-start.19 = (bf16[272,512]{1,0:T(8,128)(2,1)S(1)}, bf16[272,512]{1,0:T(8,128)(2,1)S(1)}, u32[]{:S(2)}, u32[]{:S(2)}) collective-permute-start(bf16[272,512]{1,0:T(8,128)(2,1)S(1)} %get-tuple-element.276), channel_id=1, source_target_pairs={{0,2},{1,3},{2,0},{3,1},{4,6},{5,7},{6,4},{7,5},{8,10},{9,11},{10,... | collective-permute-start | bytes 835592 | tf_op jit(solution)/shard_map/ppermute | solution.py:573
  87.3 8.5 %collective-permute-start.15 = (bf16[144,512]{1,0:T(8,128)(2,1)S(1)}, bf16[144,512]{1,0:T(8,128)(2,1)S(1)}, u32[]{:S(2)}, u32[]{:S(2)}) collective-permute-start(bf16[144,512]{1,0:T(8,128)(2,1)S(1)} %pad_maximum_fusion.12), channel_id=1, source_target_pairs={{0,8},{1,9},{2,10},{3,11},{4,12},{5,13},{6,14},{7,15},{8,0},{9,1},... | collective-permute-start | bytes 442376 | tf_op jit(solution)/shard_map/ppermute | solution.py:573
  96.0 11.9 %collective-permute-start.22 = (bf16[4,512,128]{2,1,0:T(8,128)(2,1)S(1)}, bf16[4,512,128]{2,1,0:T(8,128)(2,1)S(1)}, u32[]{:S(2)}, u32[]{:S(2)}) collective-permute-start(bf16[4,512,128]{2,1,0:T(8,128)(2,1)S(1)} %pad_maximum_fusion.2), channel_id=1, source_target_pairs={{0,4},{1,5},{2,6},{3,7},{4,0},{5,1},{6,2},{7,3},{8,12},{9,13},{10,... | collective-permute-start | bytes 1572872 | tf_op jit(solution)/shard_map/ppermute | solution.py:573
  97.5 10.8 %collective-permute-start.21 = (bf16[4,512,128]{2,1,0:T(8,128)(2,1)S(1)}, bf16[4,512,128]{2,1,0:T(8,128)(2,1)S(1)}, u32[]{:S(2)}, u32[]{:S(2)}) collective-permute-start(bf16[4,512,128]{2,1,0:T(8,128)(2,1)S(1)} %pad_maximum_fusion.2), channel_id=1, source_target_pairs={{0,2},{1,3},{2,0},{3,1},{4,6},{5,7},{6,4},{7,5},{8,10},{9,11},{10,... | collective-permute-start | bytes 1572872 | tf_op jit(solution)/shard_map/ppermute | solution.py:573
  99.1 7.5 %collective-permute-start.20 = (bf16[144,512]{1,0:T(8,128)(2,1)S(1)}, bf16[144,512]{1,0:T(8,128)(2,1)S(1)}, u32[]{:S(2)}, u32[]{:S(2)}) collective-permute-start(bf16[144,512]{1,0:T(8,128)(2,1)S(1)} %pad_maximum_fusion.13), channel_id=1, source_target_pairs={{0,16},{1,17},{2,18},{3,19},{4,20},{5,21},{6,22},{7,23},{8,24},{9,... | collective-permute-start | bytes 442376 | tf_op jit(solution)/shard_map/ppermute | solution.py:573
  108.5 10.0 %collective-permute-start.26 = (bf16[12,512,128]{2,1,0:T(8,128)(2,1)S(1)}, bf16[12,512,128]{2,1,0:T(8,128)(2,1)S(1)}, u32[]{:S(2)}, u32[]{:S(2)}) collective-permute-start(bf16[12,512,128]{2,1,0:T(8,128)(2,1)S(1)} %pad_maximum_fusion.refs_0_), channel_id=1, source_target_pairs={{0,1},{1,0},{2,3},{3,2},{4,5},{5,4},{6,7},{7,6},{8,9},{9,8},{10,11... | collective-permute-start | bytes 4718600 | tf_op jit(solution)/shard_map/ppermute | solution.py:573
  108.6 8.7 %collective-permute-start.24 = (bf16[2,512,128]{2,1,0:T(8,128)(2,1)S(1)}, bf16[2,512,128]{2,1,0:T(8,128)(2,1)S(1)}, u32[]{:S(2)}, u32[]{:S(2)}) collective-permute-start(bf16[2,512,128]{2,1,0:T(8,128)(2,1)S(1)} %slice.251), channel_id=1, source_target_pairs={{0,2},{1,3},{2,0},{3,1},{4,6},{5,7},{6,4},{7,5},{8,10},{9,11},{10,... | collective-permute-start | bytes 786440 | tf_op jit(solution)/shard_map/ppermute | solution.py:573
  110.2 8.4 %collective-permute-start.25 = (bf16[2,512,128]{2,1,0:T(8,128)(2,1)S(1)}, bf16[2,512,128]{2,1,0:T(8,128)(2,1)S(1)}, u32[]{:S(2)}, u32[]{:S(2)}) collective-permute-start(bf16[2,512,128]{2,1,0:T(8,128)(2,1)S(1)} %slice.252), channel_id=1, source_target_pairs={{0,4},{1,5},{2,6},{3,7},{4,0},{5,1},{6,2},{7,3},{8,12},{9,13},{10,... | collective-permute-start | bytes 786440 | tf_op jit(solution)/shard_map/ppermute | solution.py:573
  110.7 5.3 %collective-permute-start.23 = (bf16[128,512]{1,0:T(8,128)(2,1)S(1)}, bf16[128,512]{1,0:T(8,128)(2,1)S(1)}, u32[]{:S(2)}, u32[]{:S(2)}) collective-permute-start(bf16[128,512]{1,0:T(8,128)(2,1)S(1)} %add_convert_fusion), channel_id=1, source_target_pairs={{0,8},{1,9},{2,10},{3,11},{4,12},{5,13},{6,14},{7,15},{8,0},{9,1},... | collective-permute-start | bytes 393224 | tf_op jit(solution)/shard_map/ppermute | solution.py:573
  118.8 8.7 %collective-permute-start.29 = (bf16[4,64,512]{2,1,0:T(8,128)(2,1)S(1)}, bf16[4,64,512]{2,1,0:T(8,128)(2,1)S(1)}, u32[]{:S(2)}, u32[]{:S(2)}) collective-permute-start(bf16[4,64,512]{2,1,0:T(8,128)(2,1)S(1)} %pad_maximum_fusion.10), channel_id=1, source_target_pairs={{0,4},{1,5},{2,6},{3,7},{4,0},{5,1},{6,2},{7,3},{8,12},{9,13},{10,... | collective-permute-start | bytes 786440 | tf_op jit(solution)/shard_map/ppermute | solution.py:573
  119.4 8.4 %collective-permute-start.28 = (bf16[4,64,512]{2,1,0:T(8,128)(2,1)S(1)}, bf16[4,64,512]{2,1,0:T(8,128)(2,1)S(1)}, u32[]{:S(2)}, u32[]{:S(2)}) collective-permute-start(bf16[4,64,512]{2,1,0:T(8,128)(2,1)S(1)} %pad_maximum_fusion.10), channel_id=1, source_target_pairs={{0,2},{1,3},{2,0},{3,1},{4,6},{5,7},{6,4},{7,5},{8,10},{9,11},{10,... | collective-permute-start | bytes 786440 | tf_op jit(solution)/shard_map/ppermute | solution.py:573
  127.9 6.3 %collective-permute-start.32 = (bf16[12,64,512]{2,1,0:T(8,128)(2,1)S(1)}, bf16[12,64,512]{2,1,0:T(8,128)(2,1)S(1)}, u32[]{:S(2)}, u32[]{:S(2)}) collective-permute-start(bf16[12,64,512]{2,1,0:T(8,128)(2,1)S(1)} %pad_maximum_fusion.1.refs_0_), channel_id=1, source_target_pairs={{0,1},{1,0},{2,3},{3,2},{4,5},{5,4},{6,7},{7,6},{8,9},{9,8},{10,11... | collective-permute-start | bytes 2359304 | tf_op jit(solution)/shard_map/ppermute | solution.py:573
  128.0 5.9 %collective-permute-start.30 = (bf16[2,64,512]{2,1,0:T(8,128)(2,1)S(1)}, bf16[2,64,512]{2,1,0:T(8,128)(2,1)S(1)}, u32[]{:S(2)}, u32[]{:S(2)}) collective-permute-start(bf16[2,64,512]{2,1,0:T(8,128)(2,1)S(1)} %slice.257), channel_id=1, source_target_pairs={{0,2},{1,3},{2,0},{3,1},{4,6},{5,7},{6,4},{7,5},{8,10},{9,11},{10,... | collective-permute-start | bytes 393224 | tf_op jit(solution)/shard_map/ppermute | solution.py:573
  128.6 5.6 %collective-permute-start.31 = (bf16[2,64,512]{2,1,0:T(8,128)(2,1)S(1)}, bf16[2,64,512]{2,1,0:T(8,128)(2,1)S(1)}, u32[]{:S(2)}, u32[]{:S(2)}) collective-permute-start(bf16[2,64,512]{2,1,0:T(8,128)(2,1)S(1)} %slice.258), channel_id=1, source_target_pairs={{0,4},{1,5},{2,6},{3,7},{4,0},{5,1},{6,2},{7,3},{8,12},{9,13},{10,... | collective-permute-start | bytes 393224 | tf_op jit(solution)/shard_map/ppermute | solution.py:573
  134.2 2.2 %collective-permute-start.33 = (bf16[4,64,512]{2,1,0:T(8,128)(2,1)S(1)}, bf16[4,64,512]{2,1,0:T(8,128)(2,1)S(1)}, u32[]{:S(2)}, u32[]{:S(2)}) collective-permute-start(bf16[4,64,512]{2,1,0:T(8,128)(2,1)S(1)} %pad_maximum_fusion.11), channel_id=1, source_target_pairs={{0,1},{1,0},{2,3},{3,2},{4,5},{5,4},{6,7},{7,6},{8,9},{9,8},{10,11... | collective-permute-start | bytes 786440 | tf_op jit(solution)/shard_map/ppermute | solution.py:573
  (18 other events, 125.7 us)

commit v13 on v12

--- a/solution.py
+++ b/solution.py
@@ -620,7 +620,7 @@
     stays, *sends = meet(kept, got)
 
     token, sends, grad_inner = wait(token, sends, grad_inner)
-    came = [exchange(s, m) for s, m in zip(sends, xy)]
+    came = [exchange(sends[k], xy[k]) for k in (2, 0, 1)]
     grad_mixed, grad_attended, grad_out_w, through_rows = through(token, grad_inner, mixed, steep, w_out, attended, gain2)
     token, through_rows = wait(token, through_rows)
     rest_keep, rest_send, stay, leave, small = back(

time: 138 us -> 138 us (level)
  starting transfers between devices: 35 us -> 33.6 us
  transfers between devices with their start and end apart: 34 -> 34, of which waited for: 15 -> 16; matrix products, arithmetic and copies ran while one was open for 3% -> 3% of each run, Pallas kernels for 28% -> 28%
where the time goes in v13:
time: 138 us
  Pallas kernels  61.4 us (44%)
  starting transfers between devices  33.6 us (24%)
  waiting for transfers between devices  32.2 us (23%)
  local copies, waits for them, and re-layouts  5.41 us (4%)
  other arithmetic  3.76 us (3%)
    ppermute x34, starting transfers between devices, exchange(): lax.ppermute(value, ('dp', 'blk'), [(i, i ^ bits) for i in range(size)])  33.6 us
    ppermute x34, waiting for transfers between devices, exchange(): lax.ppermute(value, ('dp', 'blk'), [(i, i ^ bits) for i in range(size)])  32.2 us
    pallas_call x1, Pallas kernels, front(): pl.pallas_call(front_kernel, in_specs=[smem] + [vmem] * 14 + [free] * 3,...  20.4 us
    pallas_call x1, Pallas kernels, back(): pl.pallas_call(back_kernel, grid=(width // 128,), in_specs=[smem, col(cou...  20.1 us
    pallas_call x3, Pallas kernels, sort(): pl.pallas_call(functools.partial(sort_kernel, [first for first, _ in part...  5.39 us
    pallas_call x2, Pallas kernels, place(): pl.pallas_call(functools.partial(place_kernel, [first for first, _ in par...  5.38 us
    unnamed x32, local copies, waits for them, and re-layouts  3.86 us
  transfers between devices with their start and end apart: 34, of which 16 were waited for; matrix products, arithmetic and copies ran while one was open for 3% of the time, Pallas kernels for 28%

profile of v13, /device:TPU:0, one launch (start us, length us, event | category | flops | bytes accessed | tf_op | source)
XLA Modules:
  0.0 137.7 jit_solution(9350503727014298154)
XLA Ops:
  2.4 2.6 %collective-permute-start = (bf16[256,512]{1,0:T(8,128)(2,1)S(1)}, bf16[256,512]{1,0:T(8,128)(2,1)S(1)}, u32[]{:S(2)}, u32[]{:S(2)}) collective-permute-start(bf16[256,512]{1,0:T(8,128)(2,1)S(1)} %get-tuple-element.183), channel_id=1, source_target_pairs={{0,2},{1,3},{2,0},{3,1},{4,6},{5,7},{6,4},{7,5},{8,10},{9,11},{10,... | collective-permute-start | bytes 786440 | tf_op jit(solution)/shard_map/ppermute | solution.py:573
  8.8 1.5 %prepare.1 = (bf16[512,512]{1,0:T(8,128)(2,1)S(1)}, bf16[256,512]{1,0:T(8,128)(2,1)S(1)}, bf16[512,512]{1,0:T(8,128)(2,1)S(1)}, bf16[512,512]{1,0:T(8,128)(2,1)S...) custom-call(bf16[256,512]{1,0:T(8,128)(2,1)S(1)} %get-tuple-element.184.mine.near.near, ...), custom_call_target="tpu_custom_call" | custom-call | tf_op jit(solution)/shard_map/prepare/pallas_call | solution.py:65
  10.4 1.5 %collective-permute-done.far.far_h = bf16[256,512]{1,0:T(8,128)(2,1)S(1)} collective-permute-done((bf16[256,512]{1,0:T(8,128)(2,1)S(1)}, bf16[256,512]{1,0:T(8,128)(2,1)S(1)}, u32[]{:S(2)}, u32[]{:S(2)}) %collective-permute-start) | collective-permute-done | bytes 262176 | tf_op jit(solution)/shard_map/ppermute | solution.py:573
  13.5 20.4 %front.1 = (bf16[512,512]{1,0:T(8,128)(2,1)S(1)}, bf16[256,512]{1,0:T(8,128)(2,1)S(1)}, bf16[512,512]{1,0:T(8,128)(2,1)S(1)}, bf16[512,512]{1,0:T(8,128)(2,1)S(1...) custom-call(s32[16]{0:T(128)S(1)} %get-tuple-element.338.info, ...), custom_call_target="tpu_custom_call" | custom-call | tf_op jit(solution)/shard_map/front/pallas_call | solution.py:235
  34.2 2.0 %stay.1.kept = bf16[4,4,512,128]{3,2,1,0:T(8,128)(2,1)S(1)} custom-call(s32[16]{0:T(128)S(1)} %get-tuple-element.338.info, bf16[512,2048]{1,0:T(8,128)(2,1)S(1)} %get-tuple-element.198.active, bf16[512,2048]{1,0:T(8,128)(2,1)S(1)} %get-tuple-element.199.slopes, bf16[512,512]{1,0:T(8,128)(2,1)S(1)} %get-tuple-element.200.turned, ...), custom_call_target="tpu_custom_call" | custom-call | tf_op jit(solution)/shard_map/stay/pallas_call | solution.py:301
  36.2 1.8 %inner.1.grad_inner = f32[512,512]{1,0:T(8,128)S(1)} custom-call(s32[16]{0:T(128)S(1)} %get-tuple-element.338.info, bf16[512,2048]{1,0:T(8,128)(2,1)S(1)} %get-tuple-element.199.slopes, bf16[512,2048]{1,0:T(8,128)(2,1)S(1)} %copy-done), custom_call_target="tpu_custom_call" | custom-call | tf_op jit(solution)/shard_map/inner/pallas_call | solution.py:255
  38.6 2.8 %collective-permute-start.4 = (bf16[4,512,128]{2,1,0:T(8,128)(2,1)S(1)}, bf16[4,512,128]{2,1,0:T(8,128)(2,1)S(1)}, u32[]{:S(2)}, u32[]{:S(2)}) collective-permute-start(bf16[4,512,128]{2,1,0:T(8,128)(2,1)S(1)} %get-tuple-element.231), channel_id=1, source_target_pairs={{0,6},{1,7},{2,4},{3,5},{4,2},{5,3},{6,0},{7,1},{8,14},{9,15},{10,... | collective-permute-start | bytes 1572872 | tf_op jit(solution)/shard_map/ppermute | solution.py:573
  42.2 1.7 %through.1 = (f32[512,512]{1,0:T(8,128)S(1)}, bf16[512,512]{1,0:T(8,128)(2,1)S(1)}, bf16[512,512]{1,0:T(8,128)(2,1)S(1)}, f32[8,512]{1,0:T(8,128)S(1)}) custom-call(s32[16]{0:T(128)S(1)} %get-tuple-element.338.info, f32[512,512]{1,0:T(8,128)S(1)} %inner.1.grad_inner, f32[512,512]{1,0:T(8,128)S(1)} %get-tuple-element.213.mixed, ...), custom_call_target="tpu_custom_call" | custom-call | tf_op jit(solution)/shard_map/through/pallas_call | solution.py:274
  43.9 20.1 %back.1 = (bf16[16,64,512]{2,1,0:T(8,128)(2,1)S(1)}, bf16[1040,512]{1,0:T(8,128)(2,1)}, f32[512,512]{1,0:T(8,128)}, bf16[528,512]{1,0:T(8,128)(2,1)S(1)}, f32[8,512]{1,0:T(8,128)S(1)}) custom-call(s32[16]{0:T(128)S(1)} %get-tuple-element.338.info, bf16[256,512]{1,0:T(8,128)(2,1)S(1)} %get-tuple-element.189.q_l.ql, ...), custom_call_target="tpu_custom_call" | custom-call | tf_op jit(solution)/shard_map/back/pallas_call | solution.py:449
  66.1 1.6 %collective-permute-start.9 = (bf16[512,128]{1,0:T(8,128)(2,1)S(1)}, bf16[512,128]{1,0:T(8,128)(2,1)S(1)}, u32[]{:S(2)}, u32[]{:S(2)}) collective-permute-start(bf16[512,128]{1,0:T(8,128)(2,1)S(1)} %get-tuple-element.251), channel_id=1, source_target_pairs={{0,8},{1,9},{2,10},{3,11},{4,12},{5,13},{6,14},{7,15},{8,0},{9,1},... | collective-permute-start | bytes 393224 | tf_op jit(solution)/shard_map/ppermute | solution.py:573
  67.8 2.6 %collective-permute-start.10 = (bf16[512,128]{1,0:T(8,128)(2,1)S(1)}, bf16[512,128]{1,0:T(8,128)(2,1)S(1)}, u32[]{:S(2)}, u32[]{:S(2)}) collective-permute-start(bf16[512,128]{1,0:T(8,128)(2,1)S(1)} %get-tuple-element.252), channel_id=1, source_target_pairs={{0,16},{1,17},{2,18},{3,19},{4,20},{5,21},{6,22},{7,23},{8,24},{9,... | collective-permute-start | bytes 393224 | tf_op jit(solution)/shard_map/ppermute | solution.py:573
  71.0 1.5 %collective-permute-start.12 = (bf16[272,512]{1,0:T(8,128)(2,1)S(1)}, bf16[272,512]{1,0:T(8,128)(2,1)S(1)}, u32[]{:S(2)}, u32[]{:S(2)}) collective-permute-start(bf16[272,512]{1,0:T(8,128)(2,1)S(1)} %get-tuple-element.264), channel_id=1, source_target_pairs={{0,2},{1,3},{2,0},{3,1},{4,6},{5,7},{6,4},{7,5},{8,10},{9,11},{10,... | collective-permute-start | bytes 835592 | tf_op jit(solution)/shard_map/ppermute | solution.py:573
  73.4 1.5 %collective-permute-start.14 = (bf16[272,512]{1,0:T(8,128)(2,1)S(1)}, bf16[272,512]{1,0:T(8,128)(2,1)S(1)}, u32[]{:S(2)}, u32[]{:S(2)}) collective-permute-start(bf16[272,512]{1,0:T(8,128)(2,1)S(1)} %get-tuple-element.266), channel_id=1, source_target_pairs={{0,6},{1,7},{2,4},{3,5},{4,2},{5,3},{6,0},{7,1},{8,14},{9,15},{10,... | collective-permute-start | bytes 835592 | tf_op jit(solution)/shard_map/ppermute | solution.py:573
  76.0 4.7 %collective-permute-done.10 = bf16[512,128]{1,0:T(8,128)(2,1)S(1)} collective-permute-done((bf16[512,128]{1,0:T(8,128)(2,1)S(1)}, bf16[512,128]{1,0:T(8,128)(2,1)S(1)}, u32[]{:S(2)}, u32[]{:S(2)}) %collective-permute-start.10) | collective-permute-done | bytes 131104 | tf_op jit(solution)/shard_map/ppermute | solution.py:573
  80.8 2.5 %collective-permute-start.18 = (bf16[512,128]{1,0:T(8,128)(2,1)S(1)}, bf16[512,128]{1,0:T(8,128)(2,1)S(1)}, u32[]{:S(2)}, u32[]{:S(2)}) collective-permute-start(bf16[512,128]{1,0:T(8,128)(2,1)S(1)} %add_convert_fusion.2), channel_id=1, source_target_pairs={{0,24},{1,25},{2,26},{3,27},{4,28},{5,29},{6,30},{7,31},{8,16},{9,... | collective-permute-start | bytes 393224 | tf_op jit(solution)/shard_map/ppermute | solution.py:573
  85.2 1.4 %collective-permute-start.19 = (bf16[272,512]{1,0:T(8,128)(2,1)S(1)}, bf16[272,512]{1,0:T(8,128)(2,1)S(1)}, u32[]{:S(2)}, u32[]{:S(2)}) collective-permute-start(bf16[272,512]{1,0:T(8,128)(2,1)S(1)} %get-tuple-element.276), channel_id=1, source_target_pairs={{0,2},{1,3},{2,0},{3,1},{4,6},{5,7},{6,4},{7,5},{8,10},{9,11},{10,... | collective-permute-start | bytes 835592 | tf_op jit(solution)/shard_map/ppermute | solution.py:573
  87.0 1.3 collective-permute-start.15
  88.3 7.2 %collective-permute-done.15 = bf16[144,512]{1,0:T(8,128)(2,1)S(1)} collective-permute-done((bf16[144,512]{1,0:T(8,128)(2,1)S(1)}, bf16[144,512]{1,0:T(8,128)(2,1)S(1)}, u32[]{:S(2)}, u32[]{:S(2)}) %collective-permute-start.15) | collective-permute-done | bytes 147488 | tf_op jit(solution)/shard_map/ppermute | solution.py:573
  95.8 1.6 %collective-permute-start.22 = (bf16[4,512,128]{2,1,0:T(8,128)(2,1)S(1)}, bf16[4,512,128]{2,1,0:T(8,128)(2,1)S(1)}, u32[]{:S(2)}, u32[]{:S(2)}) collective-permute-start(bf16[4,512,128]{2,1,0:T(8,128)(2,1)S(1)} %pad_maximum_fusion.2), channel_id=1, source_target_pairs={{0,4},{1,5},{2,6},{3,7},{4,0},{5,1},{6,2},{7,3},{8,12},{9,13},{10,... | collective-permute-start | bytes 1572872 | tf_op jit(solution)/shard_map/ppermute | solution.py:573
  98.1 1.4 %collective-permute-start.20 = (bf16[144,512]{1,0:T(8,128)(2,1)S(1)}, bf16[144,512]{1,0:T(8,128)(2,1)S(1)}, u32[]{:S(2)}, u32[]{:S(2)}) collective-permute-start(bf16[144,512]{1,0:T(8,128)(2,1)S(1)} %pad_maximum_fusion.13), channel_id=1, source_target_pairs={{0,16},{1,17},{2,18},{3,19},{4,20},{5,21},{6,22},{7,23},{8,24},{9,... | collective-permute-start | bytes 442376 | tf_op jit(solution)/shard_map/ppermute | solution.py:573
  101.0 4.6 %collective-permute-done.20 = bf16[144,512]{1,0:T(8,128)(2,1)S(1)} collective-permute-done((bf16[144,512]{1,0:T(8,128)(2,1)S(1)}, bf16[144,512]{1,0:T(8,128)(2,1)S(1)}, u32[]{:S(2)}, u32[]{:S(2)}) %collective-permute-start.20) | collective-permute-done | bytes 147488 | tf_op jit(solution)/shard_map/ppermute | solution.py:573
  111.3 2.3 %place.2 = (f32[2048,512]{1,0:T(8,128)}, f32[512,2048]{1,0:T(8,128)}) custom-call(s32[16]{0:T(128)S(1)} %get-tuple-element.338.info, bf16[12,512,128]{2,1,0:T(8,128)(2,1)S(1)} %pad_maximum_fusion.refs_0_), custom_call_target="tpu_custom_call" | custom-call | tf_op jit(solution)/shard_map/place/pallas_call | solution.py:516
  113.6 2.2 %collective-permute-done.23 = bf16[128,512]{1,0:T(8,128)(2,1)S(1)} collective-permute-done((bf16[128,512]{1,0:T(8,128)(2,1)S(1)}, bf16[128,512]{1,0:T(8,128)(2,1)S(1)}, u32[]{:S(2)}, u32[]{:S(2)}) %collective-permute-start.23) | collective-permute-done | bytes 131104 | tf_op jit(solution)/shard_map/ppermute | solution.py:573
  115.8 1.4 collective-permute-done.24
  117.8 1.3 collective-permute-start.29
  119.7 3.1 %place.3 = (f32[2048,512]{1,0:T(8,128)}, f32[512,2048]{1,0:T(8,128)}) custom-call(s32[16]{0:T(128)S(1)} %get-tuple-element.338.info, bf16[4,512,128]{2,1,0:T(8,128)(2,1)S(1)} %pad_maximum_fusion.3.refs_0_, bf16[12,512,128]{2,1,0:T(8,128)(2,1)S(1)} %collective-permute-done.26.refs_1_, ...), custom_call_target="tpu_custom_call", output_to_operand_aliasing={{0}: (4, {}), {1}: (5, {})} | custom-call | tf_op jit(solution)/shard_map/place/pallas_call | solution.py:516
  122.8 3.8 %collective-permute-done.29 = bf16[4,64,512]{2,1,0:T(8,128)(2,1)S(1)} collective-permute-done((bf16[4,64,512]{2,1,0:T(8,128)(2,1)S(1)}, bf16[4,64,512]{2,1,0:T(8,128)(2,1)S(1)}, u32[]{:S(2)}, u32[]{:S(2)}) %collective-permute-start.29) | collective-permute-done | bytes 262176 | tf_op jit(solution)/shard_map/ppermute | solution.py:573
  128.4 1.5 %collective-permute-start.31 = (bf16[2,64,512]{2,1,0:T(8,128)(2,1)S(1)}, bf16[2,64,512]{2,1,0:T(8,128)(2,1)S(1)}, u32[]{:S(2)}, u32[]{:S(2)}) collective-permute-start(bf16[2,64,512]{2,1,0:T(8,128)(2,1)S(1)} %slice.258), channel_id=1, source_target_pairs={{0,4},{1,5},{2,6},{3,7},{4,0},{5,1},{6,2},{7,3},{8,12},{9,13},{10,... | collective-permute-start | bytes 393224 | tf_op jit(solution)/shard_map/ppermute | solution.py:573
  129.9 1.9 %sort.3 = (f32[512,512]{1,0:T(8,128)}, f32[512,512]{1,0:T(8,128)}, f32[512,512]{1,0:T(8,128)}, f32[512,512]{1,0:T(8,128)}) custom-call(s32[16]{0:T(128)S(1)} %get-tuple-element.338.info, bf16[12,64,512]{2,1,0:T(8,128)(2,1)S(1)} %pad_maximum_fusion.1.refs_0_), custom_call_target="tpu_custom_call" | custom-call | tf_op jit(solution)/shard_map/sort/pallas_call | solution.py:550
  131.7 1.9 %collective-permute-done.30.refs_0_ = bf16[2,64,512]{2,1,0:T(8,128)(2,1)S(1)} collective-permute-done((bf16[2,64,512]{2,1,0:T(8,128)(2,1)S(1)}, bf16[2,64,512]{2,1,0:T(8,128)(2,1)S(1)}, u32[]{:S(2)}, u32[]{:S(2)}) %collective-permute-start.30) | collective-permute-done | bytes 131104 | tf_op jit(solution)/shard_map/ppermute | solution.py:573
  134.0 2.1 %sort.4 = (f32[512,512]{1,0:T(8,128)}, f32[512,512]{1,0:T(8,128)}, f32[512,512]{1,0:T(8,128)}, f32[512,512]{1,0:T(8,128)}) custom-call(s32[16]{0:T(128)S(1)} %get-tuple-element.338.info, bf16[2,64,512]{2,1,0:T(8,128)(2,1)S(1)} %collective-permute-done.30.refs_0_, ...), custom_call_target="tpu_custom_call", output_to_operand_aliasing={{0}: (4, {}), {1}: (5, {}), {2}: (6, {}), {3}: (7, {})} | custom-call | tf_op jit(solution)/shard_map/sort/pallas_call | solution.py:550
  136.2 1.4 %sort.5 = (f32[512,512]{1,0:T(8,128)}, f32[512,512]{1,0:T(8,128)}, f32[512,512]{1,0:T(8,128)}, f32[512,512]{1,0:T(8,128)}) custom-call(s32[16]{0:T(128)S(1)} %get-tuple-element.338.info, bf16[4,64,512]{2,1,0:T(8,128)(2,1)S(1)} %collective-permute-done.33.refs_0_, ...), custom_call_target="tpu_custom_call", output_to_operand_aliasing={{0}: (2, {}), {1}: (3, {}), {2}: (4, {}), {3}: (5, {})} | custom-call | tf_op jit(solution)/shard_map/sort/pallas_call | solution.py:550
  (124 shorter events, 27.1 us)
Async XLA Ops:
  1.9 3.1 %collective-permute-start.1 = (bf16[256,512]{1,0:T(8,128)(2,1)S(1)}, bf16[256,512]{1,0:T(8,128)(2,1)S(1)}, u32[]{:S(2)}, u32[]{:S(2)}) collective-permute-start(bf16[256,512]{1,0:T(8,128)(2,1)S(1)} %get-tuple-element.184.mine.near.near_h), channel_id=1, source_target_pairs={{0,1},{1,0},{2,3},{3,2},{4,5},{5,4},{6,7},{7,6},{8,9},{9,8},{10,11... | collective-permute-start | bytes 786440 | tf_op jit(solution)/shard_map/ppermute | solution.py:573
  2.4 9.5 %collective-permute-start = (bf16[256,512]{1,0:T(8,128)(2,1)S(1)}, bf16[256,512]{1,0:T(8,128)(2,1)S(1)}, u32[]{:S(2)}, u32[]{:S(2)}) collective-permute-start(bf16[256,512]{1,0:T(8,128)(2,1)S(1)} %get-tuple-element.183), channel_id=1, source_target_pairs={{0,2},{1,3},{2,0},{3,1},{4,6},{5,7},{6,4},{7,5},{8,10},{9,11},{10,... | collective-permute-start | bytes 786440 | tf_op jit(solution)/shard_map/ppermute | solution.py:573
  33.9 4.2 %collective-permute-start.3 = (bf16[16,512,128]{2,1,0:T(8,128)(2,1)S(1)}, bf16[16,512,128]{2,1,0:T(8,128)(2,1)S(1)}, u32[]{:S(2)}, u32[]{:S(2)}) collective-permute-start(bf16[16,512,128]{2,1,0:T(8,128)(2,1)S(1)} %get-tuple-element.203), channel_id=1, source_target_pairs={{0,1},{1,0},{2,3},{3,2},{4,5},{5,4},{6,7},{7,6},{8,9},{9,8},{10,11... | collective-permute-start | bytes 6291464 | tf_op jit(solution)/shard_map/ppermute | solution.py:573
  38.6 25.4 %collective-permute-start.4 = (bf16[4,512,128]{2,1,0:T(8,128)(2,1)S(1)}, bf16[4,512,128]{2,1,0:T(8,128)(2,1)S(1)}, u32[]{:S(2)}, u32[]{:S(2)}) collective-permute-start(bf16[4,512,128]{2,1,0:T(8,128)(2,1)S(1)} %get-tuple-element.231), channel_id=1, source_target_pairs={{0,6},{1,7},{2,4},{3,5},{4,2},{5,3},{6,0},{7,1},{8,14},{9,15},{10,... | collective-permute-start | bytes 1572872 | tf_op jit(solution)/shard_map/ppermute | solution.py:573
  41.4 23.7 %collective-permute-start.5 = (bf16[4,512,128]{2,1,0:T(8,128)(2,1)S(1)}, bf16[4,512,128]{2,1,0:T(8,128)(2,1)S(1)}, u32[]{:S(2)}, u32[]{:S(2)}) collective-permute-start(bf16[4,512,128]{2,1,0:T(8,128)(2,1)S(1)} %get-tuple-element.232), channel_id=1, source_target_pairs={{0,2},{1,3},{2,0},{3,1},{4,6},{5,7},{6,4},{7,5},{8,10},{9,11},{10,... | collective-permute-start | bytes 1572872 | tf_op jit(solution)/shard_map/ppermute | solution.py:573
  41.9 23.5 %collective-permute-start.6 = (bf16[4,512,128]{2,1,0:T(8,128)(2,1)S(1)}, bf16[4,512,128]{2,1,0:T(8,128)(2,1)S(1)}, u32[]{:S(2)}, u32[]{:S(2)}) collective-permute-start(bf16[4,512,128]{2,1,0:T(8,128)(2,1)S(1)} %get-tuple-element.233), channel_id=1, source_target_pairs={{0,4},{1,5},{2,6},{3,7},{4,0},{5,1},{6,2},{7,3},{8,12},{9,13},{10,... | collective-permute-start | bytes 1572872 | tf_op jit(solution)/shard_map/ppermute | solution.py:573
  65.4 5.2 %collective-permute-start.7 = (bf16[1040,512]{1,0:T(8,128)(2,1)}, bf16[1040,512]{1,0:T(8,128)(2,1)S(1)}, u32[]{:S(2)}, u32[]{:S(2)}) collective-permute-start(bf16[1040,512]{1,0:T(8,128)(2,1)} %get-tuple-element.244), channel_id=1, source_target_pairs={{0,1},{1,0},{2,3},{3,2},{4,5},{5,4},{6,7},{7,6},{8,9},{9,8},{10,11... | collective-permute-start | bytes 3194888 | tf_op jit(solution)/shard_map/ppermute | solution.py:573
  65.4 5.2 %collective-permute-start.8 = (bf16[528,512]{1,0:T(8,128)(2,1)S(1)}, bf16[528,512]{1,0:T(8,128)(2,1)S(1)}, u32[]{:S(2)}, u32[]{:S(2)}) collective-permute-start(bf16[528,512]{1,0:T(8,128)(2,1)S(1)} %get-tuple-element.245), channel_id=1, source_target_pairs={{0,1},{1,0},{2,3},{3,2},{4,5},{5,4},{6,7},{7,6},{8,9},{9,8},{10,11... | collective-permute-start | bytes 1622024 | tf_op jit(solution)/shard_map/ppermute | solution.py:573
  66.1 7.3 %collective-permute-start.9 = (bf16[512,128]{1,0:T(8,128)(2,1)S(1)}, bf16[512,128]{1,0:T(8,128)(2,1)S(1)}, u32[]{:S(2)}, u32[]{:S(2)}) collective-permute-start(bf16[512,128]{1,0:T(8,128)(2,1)S(1)} %get-tuple-element.251), channel_id=1, source_target_pairs={{0,8},{1,9},{2,10},{3,11},{4,12},{5,13},{6,14},{7,15},{8,0},{9,1},... | collective-permute-start | bytes 393224 | tf_op jit(solution)/shard_map/ppermute | solution.py:573
  67.8 12.9 %collective-permute-start.10 = (bf16[512,128]{1,0:T(8,128)(2,1)S(1)}, bf16[512,128]{1,0:T(8,128)(2,1)S(1)}, u32[]{:S(2)}, u32[]{:S(2)}) collective-permute-start(bf16[512,128]{1,0:T(8,128)(2,1)S(1)} %get-tuple-element.252), channel_id=1, source_target_pairs={{0,16},{1,17},{2,18},{3,19},{4,20},{5,21},{6,22},{7,23},{8,24},{9,... | collective-permute-start | bytes 393224 | tf_op jit(solution)/shard_map/ppermute | solution.py:573
  70.4 10.3 %collective-permute-start.11 = (bf16[512,128]{1,0:T(8,128)(2,1)S(1)}, bf16[512,128]{1,0:T(8,128)(2,1)S(1)}, u32[]{:S(2)}, u32[]{:S(2)}) collective-permute-start(bf16[512,128]{1,0:T(8,128)(2,1)S(1)} %get-tuple-element.253), channel_id=1, source_target_pairs={{0,24},{1,25},{2,26},{3,27},{4,28},{5,29},{6,30},{7,31},{8,16},{9,... | collective-permute-start | bytes 393224 | tf_op jit(solution)/shard_map/ppermute | solution.py:573
  71.0 13.4 %collective-permute-start.12 = (bf16[272,512]{1,0:T(8,128)(2,1)S(1)}, bf16[272,512]{1,0:T(8,128)(2,1)S(1)}, u32[]{:S(2)}, u32[]{:S(2)}) collective-permute-start(bf16[272,512]{1,0:T(8,128)(2,1)S(1)} %get-tuple-element.264), channel_id=1, source_target_pairs={{0,2},{1,3},{2,0},{3,1},{4,6},{5,7},{6,4},{7,5},{8,10},{9,11},{10,... | collective-permute-start | bytes 835592 | tf_op jit(solution)/shard_map/ppermute | solution.py:573
  72.5 12.7 %collective-permute-start.13 = (bf16[272,512]{1,0:T(8,128)(2,1)S(1)}, bf16[272,512]{1,0:T(8,128)(2,1)S(1)}, u32[]{:S(2)}, u32[]{:S(2)}) collective-permute-start(bf16[272,512]{1,0:T(8,128)(2,1)S(1)} %get-tuple-element.265), channel_id=1, source_target_pairs={{0,4},{1,5},{2,6},{3,7},{4,0},{5,1},{6,2},{7,3},{8,12},{9,13},{10,... | collective-permute-start | bytes 835592 | tf_op jit(solution)/shard_map/ppermute | solution.py:573
  73.4 13.3 %collective-permute-start.14 = (bf16[272,512]{1,0:T(8,128)(2,1)S(1)}, bf16[272,512]{1,0:T(8,128)(2,1)S(1)}, u32[]{:S(2)}, u32[]{:S(2)}) collective-permute-start(bf16[272,512]{1,0:T(8,128)(2,1)S(1)} %get-tuple-element.266), channel_id=1, source_target_pairs={{0,6},{1,7},{2,4},{3,5},{4,2},{5,3},{6,0},{7,1},{8,14},{9,15},{10,... | collective-permute-start | bytes 835592 | tf_op jit(solution)/shard_map/ppermute | solution.py:573
  80.8 14.8 %collective-permute-start.18 = (bf16[512,128]{1,0:T(8,128)(2,1)S(1)}, bf16[512,128]{1,0:T(8,128)(2,1)S(1)}, u32[]{:S(2)}, u32[]{:S(2)}) collective-permute-start(bf16[512,128]{1,0:T(8,128)(2,1)S(1)} %add_convert_fusion.2), channel_id=1, source_target_pairs={{0,24},{1,25},{2,26},{3,27},{4,28},{5,29},{6,30},{7,31},{8,16},{9,... | collective-permute-start | bytes 393224 | tf_op jit(solution)/shard_map/ppermute | solution.py:573
  83.2 12.4 %collective-permute-start.17 = (bf16[512,128]{1,0:T(8,128)(2,1)S(1)}, bf16[512,128]{1,0:T(8,128)(2,1)S(1)}, u32[]{:S(2)}, u32[]{:S(2)}) collective-permute-start(bf16[512,128]{1,0:T(8,128)(2,1)S(1)} %add_convert_fusion.2), channel_id=1, source_target_pairs={{0,16},{1,17},{2,18},{3,19},{4,20},{5,21},{6,22},{7,23},{8,24},{9,... | collective-permute-start | bytes 393224 | tf_op jit(solution)/shard_map/ppermute | solution.py:573
  84.5 11.2 %collective-permute-start.16 = (bf16[512,128]{1,0:T(8,128)(2,1)S(1)}, bf16[512,128]{1,0:T(8,128)(2,1)S(1)}, u32[]{:S(2)}, u32[]{:S(2)}) collective-permute-start(bf16[512,128]{1,0:T(8,128)(2,1)S(1)} %add_convert_fusion.2), channel_id=1, source_target_pairs={{0,8},{1,9},{2,10},{3,11},{4,12},{5,13},{6,14},{7,15},{8,0},{9,1},... | collective-permute-start | bytes 393224 | tf_op jit(solution)/shard_map/ppermute | solution.py:573
  85.2 10.4 %collective-permute-start.19 = (bf16[272,512]{1,0:T(8,128)(2,1)S(1)}, bf16[272,512]{1,0:T(8,128)(2,1)S(1)}, u32[]{:S(2)}, u32[]{:S(2)}) collective-permute-start(bf16[272,512]{1,0:T(8,128)(2,1)S(1)} %get-tuple-element.276), channel_id=1, source_target_pairs={{0,2},{1,3},{2,0},{3,1},{4,6},{5,7},{6,4},{7,5},{8,10},{9,11},{10,... | collective-permute-start | bytes 835592 | tf_op jit(solution)/shard_map/ppermute | solution.py:573
  87.0 8.5 %collective-permute-start.15 = (bf16[144,512]{1,0:T(8,128)(2,1)S(1)}, bf16[144,512]{1,0:T(8,128)(2,1)S(1)}, u32[]{:S(2)}, u32[]{:S(2)}) collective-permute-start(bf16[144,512]{1,0:T(8,128)(2,1)S(1)} %pad_maximum_fusion.12), channel_id=1, source_target_pairs={{0,8},{1,9},{2,10},{3,11},{4,12},{5,13},{6,14},{7,15},{8,0},{9,1},... | collective-permute-start | bytes 442376 | tf_op jit(solution)/shard_map/ppermute | solution.py:573
  95.8 11.1 %collective-permute-start.22 = (bf16[4,512,128]{2,1,0:T(8,128)(2,1)S(1)}, bf16[4,512,128]{2,1,0:T(8,128)(2,1)S(1)}, u32[]{:S(2)}, u32[]{:S(2)}) collective-permute-start(bf16[4,512,128]{2,1,0:T(8,128)(2,1)S(1)} %pad_maximum_fusion.2), channel_id=1, source_target_pairs={{0,4},{1,5},{2,6},{3,7},{4,0},{5,1},{6,2},{7,3},{8,12},{9,13},{10,... | collective-permute-start | bytes 1572872 | tf_op jit(solution)/shard_map/ppermute | solution.py:573
  97.4 10.8 %collective-permute-start.21 = (bf16[4,512,128]{2,1,0:T(8,128)(2,1)S(1)}, bf16[4,512,128]{2,1,0:T(8,128)(2,1)S(1)}, u32[]{:S(2)}, u32[]{:S(2)}) collective-permute-start(bf16[4,512,128]{2,1,0:T(8,128)(2,1)S(1)} %pad_maximum_fusion.2), channel_id=1, source_target_pairs={{0,2},{1,3},{2,0},{3,1},{4,6},{5,7},{6,4},{7,5},{8,10},{9,11},{10,... | collective-permute-start | bytes 1572872 | tf_op jit(solution)/shard_map/ppermute | solution.py:573
  98.1 7.5 %collective-permute-start.20 = (bf16[144,512]{1,0:T(8,128)(2,1)S(1)}, bf16[144,512]{1,0:T(8,128)(2,1)S(1)}, u32[]{:S(2)}, u32[]{:S(2)}) collective-permute-start(bf16[144,512]{1,0:T(8,128)(2,1)S(1)} %pad_maximum_fusion.13), channel_id=1, source_target_pairs={{0,16},{1,17},{2,18},{3,19},{4,20},{5,21},{6,22},{7,23},{8,24},{9,... | collective-permute-start | bytes 442376 | tf_op jit(solution)/shard_map/ppermute | solution.py:573
  108.4 9.3 %collective-permute-start.26 = (bf16[12,512,128]{2,1,0:T(8,128)(2,1)S(1)}, bf16[12,512,128]{2,1,0:T(8,128)(2,1)S(1)}, u32[]{:S(2)}, u32[]{:S(2)}) collective-permute-start(bf16[12,512,128]{2,1,0:T(8,128)(2,1)S(1)} %pad_maximum_fusion.refs_0_), channel_id=1, source_target_pairs={{0,1},{1,0},{2,3},{3,2},{4,5},{5,4},{6,7},{7,6},{8,9},{9,8},{10,11... | collective-permute-start | bytes 4718600 | tf_op jit(solution)/shard_map/ppermute | solution.py:573
  108.4 8.7 %collective-permute-start.24 = (bf16[2,512,128]{2,1,0:T(8,128)(2,1)S(1)}, bf16[2,512,128]{2,1,0:T(8,128)(2,1)S(1)}, u32[]{:S(2)}, u32[]{:S(2)}) collective-permute-start(bf16[2,512,128]{2,1,0:T(8,128)(2,1)S(1)} %slice.251), channel_id=1, source_target_pairs={{0,2},{1,3},{2,0},{3,1},{4,6},{5,7},{6,4},{7,5},{8,10},{9,11},{10,... | collective-permute-start | bytes 786440 | tf_op jit(solution)/shard_map/ppermute | solution.py:573
  109.3 8.4 %collective-permute-start.25 = (bf16[2,512,128]{2,1,0:T(8,128)(2,1)S(1)}, bf16[2,512,128]{2,1,0:T(8,128)(2,1)S(1)}, u32[]{:S(2)}, u32[]{:S(2)}) collective-permute-start(bf16[2,512,128]{2,1,0:T(8,128)(2,1)S(1)} %slice.252), channel_id=1, source_target_pairs={{0,4},{1,5},{2,6},{3,7},{4,0},{5,1},{6,2},{7,3},{8,12},{9,13},{10,... | collective-permute-start | bytes 786440 | tf_op jit(solution)/shard_map/ppermute | solution.py:573
  110.5 5.3 %collective-permute-start.23 = (bf16[128,512]{1,0:T(8,128)(2,1)S(1)}, bf16[128,512]{1,0:T(8,128)(2,1)S(1)}, u32[]{:S(2)}, u32[]{:S(2)}) collective-permute-start(bf16[128,512]{1,0:T(8,128)(2,1)S(1)} %add_convert_fusion), channel_id=1, source_target_pairs={{0,8},{1,9},{2,10},{3,11},{4,12},{5,13},{6,14},{7,15},{8,0},{9,1},... | collective-permute-start | bytes 393224 | tf_op jit(solution)/shard_map/ppermute | solution.py:573
  117.8 8.7 %collective-permute-start.29 = (bf16[4,64,512]{2,1,0:T(8,128)(2,1)S(1)}, bf16[4,64,512]{2,1,0:T(8,128)(2,1)S(1)}, u32[]{:S(2)}, u32[]{:S(2)}) collective-permute-start(bf16[4,64,512]{2,1,0:T(8,128)(2,1)S(1)} %pad_maximum_fusion.10), channel_id=1, source_target_pairs={{0,4},{1,5},{2,6},{3,7},{4,0},{5,1},{6,2},{7,3},{8,12},{9,13},{10,... | collective-permute-start | bytes 786440 | tf_op jit(solution)/shard_map/ppermute | solution.py:573
  119.2 8.4 %collective-permute-start.28 = (bf16[4,64,512]{2,1,0:T(8,128)(2,1)S(1)}, bf16[4,64,512]{2,1,0:T(8,128)(2,1)S(1)}, u32[]{:S(2)}, u32[]{:S(2)}) collective-permute-start(bf16[4,64,512]{2,1,0:T(8,128)(2,1)S(1)} %pad_maximum_fusion.10), channel_id=1, source_target_pairs={{0,2},{1,3},{2,0},{3,1},{4,6},{5,7},{6,4},{7,5},{8,10},{9,11},{10,... | collective-permute-start | bytes 786440 | tf_op jit(solution)/shard_map/ppermute | solution.py:573
  127.7 6.2 %collective-permute-start.32 = (bf16[12,64,512]{2,1,0:T(8,128)(2,1)S(1)}, bf16[12,64,512]{2,1,0:T(8,128)(2,1)S(1)}, u32[]{:S(2)}, u32[]{:S(2)}) collective-permute-start(bf16[12,64,512]{2,1,0:T(8,128)(2,1)S(1)} %pad_maximum_fusion.1.refs_0_), channel_id=1, source_target_pairs={{0,1},{1,0},{2,3},{3,2},{4,5},{5,4},{6,7},{7,6},{8,9},{9,8},{10,11... | collective-permute-start | bytes 2359304 | tf_op jit(solution)/shard_map/ppermute | solution.py:573
  127.8 5.9 %collective-permute-start.30 = (bf16[2,64,512]{2,1,0:T(8,128)(2,1)S(1)}, bf16[2,64,512]{2,1,0:T(8,128)(2,1)S(1)}, u32[]{:S(2)}, u32[]{:S(2)}) collective-permute-start(bf16[2,64,512]{2,1,0:T(8,128)(2,1)S(1)} %slice.257), channel_id=1, source_target_pairs={{0,2},{1,3},{2,0},{3,1},{4,6},{5,7},{6,4},{7,5},{8,10},{9,11},{10,... | collective-permute-start | bytes 393224 | tf_op jit(solution)/shard_map/ppermute | solution.py:573
  128.4 5.6 %collective-permute-start.31 = (bf16[2,64,512]{2,1,0:T(8,128)(2,1)S(1)}, bf16[2,64,512]{2,1,0:T(8,128)(2,1)S(1)}, u32[]{:S(2)}, u32[]{:S(2)}) collective-permute-start(bf16[2,64,512]{2,1,0:T(8,128)(2,1)S(1)} %slice.258), channel_id=1, source_target_pairs={{0,4},{1,5},{2,6},{3,7},{4,0},{5,1},{6,2},{7,3},{8,12},{9,13},{10,... | collective-permute-start | bytes 393224 | tf_op jit(solution)/shard_map/ppermute | solution.py:573
  134.0 2.2 %collective-permute-start.33 = (bf16[4,64,512]{2,1,0:T(8,128)(2,1)S(1)}, bf16[4,64,512]{2,1,0:T(8,128)(2,1)S(1)}, u32[]{:S(2)}, u32[]{:S(2)}) collective-permute-start(bf16[4,64,512]{2,1,0:T(8,128)(2,1)S(1)} %pad_maximum_fusion.11), channel_id=1, source_target_pairs={{0,1},{1,0},{2,3},{3,2},{4,5},{5,4},{6,7},{7,6},{8,9},{9,8},{10,11... | collective-permute-start | bytes 786440 | tf_op jit(solution)/shard_map/ppermute | solution.py:573
  (18 other events, 124.6 us)

commit v14 on v13

--- a/solution.py
+++ b/solution.py
@@ -689,9 +689,10 @@
     token, from_y, from_x, outs = wait(token, from_y, from_x, outs)
 
     sends = [from_x[:2], from_y[2:]]
+    far_a, far_b = exchange(sends[0], ROW), exchange(sends[1], NEAR_X)
+    quarter, from_y, from_x, _ = wait(quarter, from_y, from_x, sends)
     here = jnp.concatenate([quarter, from_y, from_x])
-    token, sends, here = wait(token, sends, here)
-    far_a, far_b = exchange(sends[0], ROW), exchange(sends[1], NEAR_X)
+    token, here = wait(token, here)
     other = exchange(here, CORE)
     grads = place(token, [(0, here)], [], width)
     token, grads, rest_back, far_a, far_b, other = wait(token, grads, rest_back, far_a, far_b, other)
@@ -708,11 +709,12 @@
     sends = [fourth_x[:2], fourth_y[2:], jnp.concatenate([fourth, fourth_y, fourth_x])]
     token, sends = wait(token, sends)
     last_a, last_b, pair = (exchange(s, m) for s, m in zip(sends, (ROW, NEAR_X, CORE)))
-    made = sort(token, [(0, sends[2])], [], width)
-    token, made, last_a, last_b, pair = wait(token, made, last_a, last_b, pair)
+    token, pair = wait(token, pair)
+    made = sort(token, [(0, sends[2]), (16, pair)], [], width)
+    token, made, last_a, last_b = wait(token, made, last_a, last_b)
 
     ends = exchange(jnp.concatenate([last_a, last_b]), CORE)
-    made = sort(token, [(12, last_a), (14, last_b), (16, pair)], made, width)
+    made = sort(token, [(12, last_a), (14, last_b)], made, width)
     token, made, ends = wait(token, made, ends)
     out_out, out_query, out_key, out_value = sort(token, [(28, ends)], made, width)
     return (pooled, input_grad, out_query, out_key, out_value, out_out, out_in, out_back, *outs)

time: 138 us -> 137 us (level)
  transfers between devices with their start and end apart: 34 -> 34, of which waited for: 16 -> 18; matrix products, arithmetic and copies ran while one was open for 3% -> 3% of each run, Pallas kernels for 28% -> 28%
where the time goes in v14:
time: 137 us
  Pallas kernels  61.4 us (45%)
  starting transfers between devices  33.6 us (25%)
  waiting for transfers between devices  31.6 us (23%)
  local copies, waits for them, and re-layouts  5.41 us (4%)
  other arithmetic  3.76 us (3%)
  between operations  1.37 us (1%)
    ppermute x34, starting transfers between devices, exchange(): lax.ppermute(value, ('dp', 'blk'), [(i, i ^ bits) for i in range(size)])  33.6 us
    ppermute x34, waiting for transfers between devices, exchange(): lax.ppermute(value, ('dp', 'blk'), [(i, i ^ bits) for i in range(size)])  31.6 us
    pallas_call x1, Pallas kernels, front(): pl.pallas_call(front_kernel, in_specs=[smem] + [vmem] * 14 + [free] * 3,...  20.4 us
    pallas_call x1, Pallas kernels, back(): pl.pallas_call(back_kernel, grid=(width // 128,), in_specs=[smem, col(cou...  20.1 us
    pallas_call x2, Pallas kernels, place(): pl.pallas_call(functools.partial(place_kernel, [first for first, _ in par...  5.38 us
    pallas_call x3, Pallas kernels, sort(): pl.pallas_call(functools.partial(sort_kernel, [first for first, _ in part...  5.38 us
    unnamed x32, local copies, waits for them, and re-layouts  3.86 us
  transfers between devices with their start and end apart: 34, of which 18 were waited for; matrix products, arithmetic and copies ran while one was open for 3% of the time, Pallas kernels for 28%

profile of v14, /device:TPU:0, one launch (start us, length us, event | category | flops | bytes accessed | tf_op | source)
XLA Modules:
  0.0 137.1 jit_solution(12187335220397155160)
XLA Ops:
  2.4 2.6 %collective-permute-start = (bf16[256,512]{1,0:T(8,128)(2,1)S(1)}, bf16[256,512]{1,0:T(8,128)(2,1)S(1)}, u32[]{:S(2)}, u32[]{:S(2)}) collective-permute-start(bf16[256,512]{1,0:T(8,128)(2,1)S(1)} %get-tuple-element.185), channel_id=1, source_target_pairs={{0,2},{1,3},{2,0},{3,1},{4,6},{5,7},{6,4},{7,5},{8,10},{9,11},{10,... | collective-permute-start | bytes 786440 | tf_op jit(solution)/shard_map/ppermute | solution.py:573
  8.8 1.5 %prepare.1 = (bf16[512,512]{1,0:T(8,128)(2,1)S(1)}, bf16[256,512]{1,0:T(8,128)(2,1)S(1)}, bf16[512,512]{1,0:T(8,128)(2,1)S(1)}, bf16[512,512]{1,0:T(8,128)(2,1)S...) custom-call(bf16[256,512]{1,0:T(8,128)(2,1)S(1)} %get-tuple-element.186.mine.near.near, ...), custom_call_target="tpu_custom_call" | custom-call | tf_op jit(solution)/shard_map/prepare/pallas_call | solution.py:65
  10.4 1.5 %collective-permute-done.far.far_h = bf16[256,512]{1,0:T(8,128)(2,1)S(1)} collective-permute-done((bf16[256,512]{1,0:T(8,128)(2,1)S(1)}, bf16[256,512]{1,0:T(8,128)(2,1)S(1)}, u32[]{:S(2)}, u32[]{:S(2)}) %collective-permute-start) | collective-permute-done | bytes 262176 | tf_op jit(solution)/shard_map/ppermute | solution.py:573
  13.5 20.4 %front.1 = (bf16[512,512]{1,0:T(8,128)(2,1)S(1)}, bf16[256,512]{1,0:T(8,128)(2,1)S(1)}, bf16[512,512]{1,0:T(8,128)(2,1)S(1)}, bf16[512,512]{1,0:T(8,128)(2,1)S(1...) custom-call(s32[16]{0:T(128)S(1)} %get-tuple-element.342.info, ...), custom_call_target="tpu_custom_call" | custom-call | tf_op jit(solution)/shard_map/front/pallas_call | solution.py:235
  34.2 2.0 %stay.1.kept = bf16[4,4,512,128]{3,2,1,0:T(8,128)(2,1)S(1)} custom-call(s32[16]{0:T(128)S(1)} %get-tuple-element.342.info, bf16[512,2048]{1,0:T(8,128)(2,1)S(1)} %get-tuple-element.200.active, bf16[512,2048]{1,0:T(8,128)(2,1)S(1)} %get-tuple-element.201.slopes, bf16[512,512]{1,0:T(8,128)(2,1)S(1)} %get-tuple-element.202.turned, ...), custom_call_target="tpu_custom_call" | custom-call | tf_op jit(solution)/shard_map/stay/pallas_call | solution.py:301
  36.2 1.8 %inner.1.grad_inner = f32[512,512]{1,0:T(8,128)S(1)} custom-call(s32[16]{0:T(128)S(1)} %get-tuple-element.342.info, bf16[512,2048]{1,0:T(8,128)(2,1)S(1)} %get-tuple-element.201.slopes, bf16[512,2048]{1,0:T(8,128)(2,1)S(1)} %copy-done), custom_call_target="tpu_custom_call" | custom-call | tf_op jit(solution)/shard_map/inner/pallas_call | solution.py:255
  38.6 2.8 %collective-permute-start.4 = (bf16[4,512,128]{2,1,0:T(8,128)(2,1)S(1)}, bf16[4,512,128]{2,1,0:T(8,128)(2,1)S(1)}, u32[]{:S(2)}, u32[]{:S(2)}) collective-permute-start(bf16[4,512,128]{2,1,0:T(8,128)(2,1)S(1)} %get-tuple-element.233), channel_id=1, source_target_pairs={{0,6},{1,7},{2,4},{3,5},{4,2},{5,3},{6,0},{7,1},{8,14},{9,15},{10,... | collective-permute-start | bytes 1572872 | tf_op jit(solution)/shard_map/ppermute | solution.py:573
  42.2 1.7 %through.1 = (f32[512,512]{1,0:T(8,128)S(1)}, bf16[512,512]{1,0:T(8,128)(2,1)S(1)}, bf16[512,512]{1,0:T(8,128)(2,1)S(1)}, f32[8,512]{1,0:T(8,128)S(1)}) custom-call(s32[16]{0:T(128)S(1)} %get-tuple-element.342.info, f32[512,512]{1,0:T(8,128)S(1)} %inner.1.grad_inner, f32[512,512]{1,0:T(8,128)S(1)} %get-tuple-element.215.mixed, ...), custom_call_target="tpu_custom_call" | custom-call | tf_op jit(solution)/shard_map/through/pallas_call | solution.py:274
  43.9 20.1 %back.1 = (bf16[16,64,512]{2,1,0:T(8,128)(2,1)S(1)}, bf16[1040,512]{1,0:T(8,128)(2,1)}, f32[512,512]{1,0:T(8,128)}, bf16[528,512]{1,0:T(8,128)(2,1)S(1)}, f32[8,512]{1,0:T(8,128)S(1)}) custom-call(s32[16]{0:T(128)S(1)} %get-tuple-element.342.info, bf16[256,512]{1,0:T(8,128)(2,1)S(1)} %get-tuple-element.191.q_l.ql, ...), custom_call_target="tpu_custom_call" | custom-call | tf_op jit(solution)/shard_map/back/pallas_call | solution.py:449
  66.1 1.6 %collective-permute-start.9 = (bf16[512,128]{1,0:T(8,128)(2,1)S(1)}, bf16[512,128]{1,0:T(8,128)(2,1)S(1)}, u32[]{:S(2)}, u32[]{:S(2)}) collective-permute-start(bf16[512,128]{1,0:T(8,128)(2,1)S(1)} %get-tuple-element.253), channel_id=1, source_target_pairs={{0,8},{1,9},{2,10},{3,11},{4,12},{5,13},{6,14},{7,15},{8,0},{9,1},... | collective-permute-start | bytes 393224 | tf_op jit(solution)/shard_map/ppermute | solution.py:573
  67.8 2.6 %collective-permute-start.10 = (bf16[512,128]{1,0:T(8,128)(2,1)S(1)}, bf16[512,128]{1,0:T(8,128)(2,1)S(1)}, u32[]{:S(2)}, u32[]{:S(2)}) collective-permute-start(bf16[512,128]{1,0:T(8,128)(2,1)S(1)} %get-tuple-element.254), channel_id=1, source_target_pairs={{0,16},{1,17},{2,18},{3,19},{4,20},{5,21},{6,22},{7,23},{8,24},{9,... | collective-permute-start | bytes 393224 | tf_op jit(solution)/shard_map/ppermute | solution.py:573
  71.0 1.5 %collective-permute-start.12 = (bf16[272,512]{1,0:T(8,128)(2,1)S(1)}, bf16[272,512]{1,0:T(8,128)(2,1)S(1)}, u32[]{:S(2)}, u32[]{:S(2)}) collective-permute-start(bf16[272,512]{1,0:T(8,128)(2,1)S(1)} %get-tuple-element.266), channel_id=1, source_target_pairs={{0,2},{1,3},{2,0},{3,1},{4,6},{5,7},{6,4},{7,5},{8,10},{9,11},{10,... | collective-permute-start | bytes 835592 | tf_op jit(solution)/shard_map/ppermute | solution.py:573
  73.4 1.5 %collective-permute-start.14 = (bf16[272,512]{1,0:T(8,128)(2,1)S(1)}, bf16[272,512]{1,0:T(8,128)(2,1)S(1)}, u32[]{:S(2)}, u32[]{:S(2)}) collective-permute-start(bf16[272,512]{1,0:T(8,128)(2,1)S(1)} %get-tuple-element.268), channel_id=1, source_target_pairs={{0,6},{1,7},{2,4},{3,5},{4,2},{5,3},{6,0},{7,1},{8,14},{9,15},{10,... | collective-permute-start | bytes 835592 | tf_op jit(solution)/shard_map/ppermute | solution.py:573
  76.0 4.7 %collective-permute-done.10 = bf16[512,128]{1,0:T(8,128)(2,1)S(1)} collective-permute-done((bf16[512,128]{1,0:T(8,128)(2,1)S(1)}, bf16[512,128]{1,0:T(8,128)(2,1)S(1)}, u32[]{:S(2)}, u32[]{:S(2)}) %collective-permute-start.10) | collective-permute-done | bytes 131104 | tf_op jit(solution)/shard_map/ppermute | solution.py:573
  80.8 2.5 %collective-permute-start.18 = (bf16[512,128]{1,0:T(8,128)(2,1)S(1)}, bf16[512,128]{1,0:T(8,128)(2,1)S(1)}, u32[]{:S(2)}, u32[]{:S(2)}) collective-permute-start(bf16[512,128]{1,0:T(8,128)(2,1)S(1)} %add_convert_fusion.2), channel_id=1, source_target_pairs={{0,24},{1,25},{2,26},{3,27},{4,28},{5,29},{6,30},{7,31},{8,16},{9,... | collective-permute-start | bytes 393224 | tf_op jit(solution)/shard_map/ppermute | solution.py:573
  85.2 1.4 %collective-permute-start.19 = (bf16[272,512]{1,0:T(8,128)(2,1)S(1)}, bf16[272,512]{1,0:T(8,128)(2,1)S(1)}, u32[]{:S(2)}, u32[]{:S(2)}) collective-permute-start(bf16[272,512]{1,0:T(8,128)(2,1)S(1)} %get-tuple-element.278), channel_id=1, source_target_pairs={{0,2},{1,3},{2,0},{3,1},{4,6},{5,7},{6,4},{7,5},{8,10},{9,11},{10,... | collective-permute-start | bytes 835592 | tf_op jit(solution)/shard_map/ppermute | solution.py:573
  87.0 1.3 collective-permute-start.15
  88.3 7.2 %collective-permute-done.15 = bf16[144,512]{1,0:T(8,128)(2,1)S(1)} collective-permute-done((bf16[144,512]{1,0:T(8,128)(2,1)S(1)}, bf16[144,512]{1,0:T(8,128)(2,1)S(1)}, u32[]{:S(2)}, u32[]{:S(2)}) %collective-permute-start.15) | collective-permute-done | bytes 147488 | tf_op jit(solution)/shard_map/ppermute | solution.py:573
  95.8 1.6 %collective-permute-start.22 = (bf16[4,512,128]{2,1,0:T(8,128)(2,1)S(1)}, bf16[4,512,128]{2,1,0:T(8,128)(2,1)S(1)}, u32[]{:S(2)}, u32[]{:S(2)}) collective-permute-start(bf16[4,512,128]{2,1,0:T(8,128)(2,1)S(1)} %pad_maximum_fusion.2), channel_id=1, source_target_pairs={{0,4},{1,5},{2,6},{3,7},{4,0},{5,1},{6,2},{7,3},{8,12},{9,13},{10,... | collective-permute-start | bytes 1572872 | tf_op jit(solution)/shard_map/ppermute | solution.py:573
  98.1 1.4 %collective-permute-start.20 = (bf16[144,512]{1,0:T(8,128)(2,1)S(1)}, bf16[144,512]{1,0:T(8,128)(2,1)S(1)}, u32[]{:S(2)}, u32[]{:S(2)}) collective-permute-start(bf16[144,512]{1,0:T(8,128)(2,1)S(1)} %pad_maximum_fusion.13), channel_id=1, source_target_pairs={{0,16},{1,17},{2,18},{3,19},{4,20},{5,21},{6,22},{7,23},{8,24},{9,... | collective-permute-start | bytes 442376 | tf_op jit(solution)/shard_map/ppermute | solution.py:573
  101.0 4.6 %collective-permute-done.20 = bf16[144,512]{1,0:T(8,128)(2,1)S(1)} collective-permute-done((bf16[144,512]{1,0:T(8,128)(2,1)S(1)}, bf16[144,512]{1,0:T(8,128)(2,1)S(1)}, u32[]{:S(2)}, u32[]{:S(2)}) %collective-permute-start.20) | collective-permute-done | bytes 147488 | tf_op jit(solution)/shard_map/ppermute | solution.py:573
  109.3 1.3 collective-permute-start.25
  111.3 2.3 %place.2 = (f32[2048,512]{1,0:T(8,128)}, f32[512,2048]{1,0:T(8,128)}) custom-call(s32[16]{0:T(128)S(1)} %get-tuple-element.342.info, bf16[12,512,128]{2,1,0:T(8,128)(2,1)S(1)} %pad_maximum_fusion.refs_0_), custom_call_target="tpu_custom_call" | custom-call | tf_op jit(solution)/shard_map/place/pallas_call | solution.py:516
  113.6 2.2 %collective-permute-done.23 = bf16[128,512]{1,0:T(8,128)(2,1)S(1)} collective-permute-done((bf16[128,512]{1,0:T(8,128)(2,1)S(1)}, bf16[128,512]{1,0:T(8,128)(2,1)S(1)}, u32[]{:S(2)}, u32[]{:S(2)}) %collective-permute-start.23) | collective-permute-done | bytes 131104 | tf_op jit(solution)/shard_map/ppermute | solution.py:573
  115.8 1.4 collective-permute-done.24
  117.8 1.3 collective-permute-start.29
  119.7 3.1 %place.3 = (f32[2048,512]{1,0:T(8,128)}, f32[512,2048]{1,0:T(8,128)}) custom-call(s32[16]{0:T(128)S(1)} %get-tuple-element.342.info, bf16[4,512,128]{2,1,0:T(8,128)(2,1)S(1)} %pad_maximum_fusion.3.refs_0_, bf16[12,512,128]{2,1,0:T(8,128)(2,1)S(1)} %collective-permute-done.26.refs_1_, ...), custom_call_target="tpu_custom_call", output_to_operand_aliasing={{0}: (4, {}), {1}: (5, {})} | custom-call | tf_op jit(solution)/shard_map/place/pallas_call | solution.py:516
  122.8 3.8 %collective-permute-done.29 = bf16[4,64,512]{2,1,0:T(8,128)(2,1)S(1)} collective-permute-done((bf16[4,64,512]{2,1,0:T(8,128)(2,1)S(1)}, bf16[4,64,512]{2,1,0:T(8,128)(2,1)S(1)}, u32[]{:S(2)}, u32[]{:S(2)}) %collective-permute-start.29) | collective-permute-done | bytes 262176 | tf_op jit(solution)/shard_map/ppermute | solution.py:573
  128.4 1.5 %collective-permute-start.32 = (bf16[2,64,512]{2,1,0:T(8,128)(2,1)S(1)}, bf16[2,64,512]{2,1,0:T(8,128)(2,1)S(1)}, u32[]{:S(2)}, u32[]{:S(2)}) collective-permute-start(bf16[2,64,512]{2,1,0:T(8,128)(2,1)S(1)} %slice.258), channel_id=1, source_target_pairs={{0,4},{1,5},{2,6},{3,7},{4,0},{5,1},{6,2},{7,3},{8,12},{9,13},{10,... | collective-permute-start | bytes 393224 | tf_op jit(solution)/shard_map/ppermute | solution.py:573
  130.0 2.6 %sort.3 = (f32[512,512]{1,0:T(8,128)}, f32[512,512]{1,0:T(8,128)}, f32[512,512]{1,0:T(8,128)}, f32[512,512]{1,0:T(8,128)}) custom-call(s32[16]{0:T(128)S(1)} %get-tuple-element.342.info, bf16[12,64,512]{2,1,0:T(8,128)(2,1)S(1)} %pad_maximum_fusion.1.refs_0_, bf16[12,64,512]{2,1,0:T(8,128)(2,1)S(1)} %collective-permute-done.30.refs_1_), custom_call_target="tpu_custom_call" | custom-call | tf_op jit(solution)/shard_map/sort/pallas_call | solution.py:550
  134.0 1.4 %sort.4 = (f32[512,512]{1,0:T(8,128)}, f32[512,512]{1,0:T(8,128)}, f32[512,512]{1,0:T(8,128)}, f32[512,512]{1,0:T(8,128)}) custom-call(s32[16]{0:T(128)S(1)} %get-tuple-element.342.info, bf16[2,64,512]{2,1,0:T(8,128)(2,1)S(1)} %collective-permute-done.31.refs_0_, ...), custom_call_target="tpu_custom_call", output_to_operand_aliasing={{0}: (3, {}), {1}: (4, {}), {2}: (5, {}), {3}: (6, {})} | custom-call | tf_op jit(solution)/shard_map/sort/pallas_call | solution.py:550
  135.6 1.4 %sort.5 = (f32[512,512]{1,0:T(8,128)}, f32[512,512]{1,0:T(8,128)}, f32[512,512]{1,0:T(8,128)}, f32[512,512]{1,0:T(8,128)}) custom-call(s32[16]{0:T(128)S(1)} %get-tuple-element.342.info, bf16[4,64,512]{2,1,0:T(8,128)(2,1)S(1)} %collective-permute-done.33.refs_0_, ...), custom_call_target="tpu_custom_call", output_to_operand_aliasing={{0}: (2, {}), {1}: (3, {}), {2}: (4, {}), {3}: (5, {})} | custom-call | tf_op jit(solution)/shard_map/sort/pallas_call | solution.py:550
  (124 shorter events, 27.2 us)
Async XLA Ops:
  1.9 3.1 %collective-permute-start.1 = (bf16[256,512]{1,0:T(8,128)(2,1)S(1)}, bf16[256,512]{1,0:T(8,128)(2,1)S(1)}, u32[]{:S(2)}, u32[]{:S(2)}) collective-permute-start(bf16[256,512]{1,0:T(8,128)(2,1)S(1)} %get-tuple-element.186.mine.near.near_h), channel_id=1, source_target_pairs={{0,1},{1,0},{2,3},{3,2},{4,5},{5,4},{6,7},{7,6},{8,9},{9,8},{10,11... | collective-permute-start | bytes 786440 | tf_op jit(solution)/shard_map/ppermute | solution.py:573
  2.4 9.5 %collective-permute-start = (bf16[256,512]{1,0:T(8,128)(2,1)S(1)}, bf16[256,512]{1,0:T(8,128)(2,1)S(1)}, u32[]{:S(2)}, u32[]{:S(2)}) collective-permute-start(bf16[256,512]{1,0:T(8,128)(2,1)S(1)} %get-tuple-element.185), channel_id=1, source_target_pairs={{0,2},{1,3},{2,0},{3,1},{4,6},{5,7},{6,4},{7,5},{8,10},{9,11},{10,... | collective-permute-start | bytes 786440 | tf_op jit(solution)/shard_map/ppermute | solution.py:573
  33.9 4.2 %collective-permute-start.3 = (bf16[16,512,128]{2,1,0:T(8,128)(2,1)S(1)}, bf16[16,512,128]{2,1,0:T(8,128)(2,1)S(1)}, u32[]{:S(2)}, u32[]{:S(2)}) collective-permute-start(bf16[16,512,128]{2,1,0:T(8,128)(2,1)S(1)} %get-tuple-element.205), channel_id=1, source_target_pairs={{0,1},{1,0},{2,3},{3,2},{4,5},{5,4},{6,7},{7,6},{8,9},{9,8},{10,11... | collective-permute-start | bytes 6291464 | tf_op jit(solution)/shard_map/ppermute | solution.py:573
  38.6 25.4 %collective-permute-start.4 = (bf16[4,512,128]{2,1,0:T(8,128)(2,1)S(1)}, bf16[4,512,128]{2,1,0:T(8,128)(2,1)S(1)}, u32[]{:S(2)}, u32[]{:S(2)}) collective-permute-start(bf16[4,512,128]{2,1,0:T(8,128)(2,1)S(1)} %get-tuple-element.233), channel_id=1, source_target_pairs={{0,6},{1,7},{2,4},{3,5},{4,2},{5,3},{6,0},{7,1},{8,14},{9,15},{10,... | collective-permute-start | bytes 1572872 | tf_op jit(solution)/shard_map/ppermute | solution.py:573
  41.4 23.7 %collective-permute-start.5 = (bf16[4,512,128]{2,1,0:T(8,128)(2,1)S(1)}, bf16[4,512,128]{2,1,0:T(8,128)(2,1)S(1)}, u32[]{:S(2)}, u32[]{:S(2)}) collective-permute-start(bf16[4,512,128]{2,1,0:T(8,128)(2,1)S(1)} %get-tuple-element.234), channel_id=1, source_target_pairs={{0,2},{1,3},{2,0},{3,1},{4,6},{5,7},{6,4},{7,5},{8,10},{9,11},{10,... | collective-permute-start | bytes 1572872 | tf_op jit(solution)/shard_map/ppermute | solution.py:573
  41.9 23.5 %collective-permute-start.6 = (bf16[4,512,128]{2,1,0:T(8,128)(2,1)S(1)}, bf16[4,512,128]{2,1,0:T(8,128)(2,1)S(1)}, u32[]{:S(2)}, u32[]{:S(2)}) collective-permute-start(bf16[4,512,128]{2,1,0:T(8,128)(2,1)S(1)} %get-tuple-element.235), channel_id=1, source_target_pairs={{0,4},{1,5},{2,6},{3,7},{4,0},{5,1},{6,2},{7,3},{8,12},{9,13},{10,... | collective-permute-start | bytes 1572872 | tf_op jit(solution)/shard_map/ppermute | solution.py:573
  65.4 5.2 %collective-permute-start.7 = (bf16[1040,512]{1,0:T(8,128)(2,1)}, bf16[1040,512]{1,0:T(8,128)(2,1)S(1)}, u32[]{:S(2)}, u32[]{:S(2)}) collective-permute-start(bf16[1040,512]{1,0:T(8,128)(2,1)} %get-tuple-element.246), channel_id=1, source_target_pairs={{0,1},{1,0},{2,3},{3,2},{4,5},{5,4},{6,7},{7,6},{8,9},{9,8},{10,11... | collective-permute-start | bytes 3194888 | tf_op jit(solution)/shard_map/ppermute | solution.py:573
  65.4 5.2 %collective-permute-start.8 = (bf16[528,512]{1,0:T(8,128)(2,1)S(1)}, bf16[528,512]{1,0:T(8,128)(2,1)S(1)}, u32[]{:S(2)}, u32[]{:S(2)}) collective-permute-start(bf16[528,512]{1,0:T(8,128)(2,1)S(1)} %get-tuple-element.247), channel_id=1, source_target_pairs={{0,1},{1,0},{2,3},{3,2},{4,5},{5,4},{6,7},{7,6},{8,9},{9,8},{10,11... | collective-permute-start | bytes 1622024 | tf_op jit(solution)/shard_map/ppermute | solution.py:573
  66.1 7.3 %collective-permute-start.9 = (bf16[512,128]{1,0:T(8,128)(2,1)S(1)}, bf16[512,128]{1,0:T(8,128)(2,1)S(1)}, u32[]{:S(2)}, u32[]{:S(2)}) collective-permute-start(bf16[512,128]{1,0:T(8,128)(2,1)S(1)} %get-tuple-element.253), channel_id=1, source_target_pairs={{0,8},{1,9},{2,10},{3,11},{4,12},{5,13},{6,14},{7,15},{8,0},{9,1},... | collective-permute-start | bytes 393224 | tf_op jit(solution)/shard_map/ppermute | solution.py:573
  67.8 12.9 %collective-permute-start.10 = (bf16[512,128]{1,0:T(8,128)(2,1)S(1)}, bf16[512,128]{1,0:T(8,128)(2,1)S(1)}, u32[]{:S(2)}, u32[]{:S(2)}) collective-permute-start(bf16[512,128]{1,0:T(8,128)(2,1)S(1)} %get-tuple-element.254), channel_id=1, source_target_pairs={{0,16},{1,17},{2,18},{3,19},{4,20},{5,21},{6,22},{7,23},{8,24},{9,... | collective-permute-start | bytes 393224 | tf_op jit(solution)/shard_map/ppermute | solution.py:573
  70.4 10.3 %collective-permute-start.11 = (bf16[512,128]{1,0:T(8,128)(2,1)S(1)}, bf16[512,128]{1,0:T(8,128)(2,1)S(1)}, u32[]{:S(2)}, u32[]{:S(2)}) collective-permute-start(bf16[512,128]{1,0:T(8,128)(2,1)S(1)} %get-tuple-element.255), channel_id=1, source_target_pairs={{0,24},{1,25},{2,26},{3,27},{4,28},{5,29},{6,30},{7,31},{8,16},{9,... | collective-permute-start | bytes 393224 | tf_op jit(solution)/shard_map/ppermute | solution.py:573
  71.0 13.4 %collective-permute-start.12 = (bf16[272,512]{1,0:T(8,128)(2,1)S(1)}, bf16[272,512]{1,0:T(8,128)(2,1)S(1)}, u32[]{:S(2)}, u32[]{:S(2)}) collective-permute-start(bf16[272,512]{1,0:T(8,128)(2,1)S(1)} %get-tuple-element.266), channel_id=1, source_target_pairs={{0,2},{1,3},{2,0},{3,1},{4,6},{5,7},{6,4},{7,5},{8,10},{9,11},{10,... | collective-permute-start | bytes 835592 | tf_op jit(solution)/shard_map/ppermute | solution.py:573
  72.5 12.7 %collective-permute-start.13 = (bf16[272,512]{1,0:T(8,128)(2,1)S(1)}, bf16[272,512]{1,0:T(8,128)(2,1)S(1)}, u32[]{:S(2)}, u32[]{:S(2)}) collective-permute-start(bf16[272,512]{1,0:T(8,128)(2,1)S(1)} %get-tuple-element.267), channel_id=1, source_target_pairs={{0,4},{1,5},{2,6},{3,7},{4,0},{5,1},{6,2},{7,3},{8,12},{9,13},{10,... | collective-permute-start | bytes 835592 | tf_op jit(solution)/shard_map/ppermute | solution.py:573
  73.4 13.3 %collective-permute-start.14 = (bf16[272,512]{1,0:T(8,128)(2,1)S(1)}, bf16[272,512]{1,0:T(8,128)(2,1)S(1)}, u32[]{:S(2)}, u32[]{:S(2)}) collective-permute-start(bf16[272,512]{1,0:T(8,128)(2,1)S(1)} %get-tuple-element.268), channel_id=1, source_target_pairs={{0,6},{1,7},{2,4},{3,5},{4,2},{5,3},{6,0},{7,1},{8,14},{9,15},{10,... | collective-permute-start | bytes 835592 | tf_op jit(solution)/shard_map/ppermute | solution.py:573
  80.8 14.8 %collective-permute-start.18 = (bf16[512,128]{1,0:T(8,128)(2,1)S(1)}, bf16[512,128]{1,0:T(8,128)(2,1)S(1)}, u32[]{:S(2)}, u32[]{:S(2)}) collective-permute-start(bf16[512,128]{1,0:T(8,128)(2,1)S(1)} %add_convert_fusion.2), channel_id=1, source_target_pairs={{0,24},{1,25},{2,26},{3,27},{4,28},{5,29},{6,30},{7,31},{8,16},{9,... | collective-permute-start | bytes 393224 | tf_op jit(solution)/shard_map/ppermute | solution.py:573
  83.2 12.4 %collective-permute-start.17 = (bf16[512,128]{1,0:T(8,128)(2,1)S(1)}, bf16[512,128]{1,0:T(8,128)(2,1)S(1)}, u32[]{:S(2)}, u32[]{:S(2)}) collective-permute-start(bf16[512,128]{1,0:T(8,128)(2,1)S(1)} %add_convert_fusion.2), channel_id=1, source_target_pairs={{0,16},{1,17},{2,18},{3,19},{4,20},{5,21},{6,22},{7,23},{8,24},{9,... | collective-permute-start | bytes 393224 | tf_op jit(solution)/shard_map/ppermute | solution.py:573
  84.5 11.2 %collective-permute-start.16 = (bf16[512,128]{1,0:T(8,128)(2,1)S(1)}, bf16[512,128]{1,0:T(8,128)(2,1)S(1)}, u32[]{:S(2)}, u32[]{:S(2)}) collective-permute-start(bf16[512,128]{1,0:T(8,128)(2,1)S(1)} %add_convert_fusion.2), channel_id=1, source_target_pairs={{0,8},{1,9},{2,10},{3,11},{4,12},{5,13},{6,14},{7,15},{8,0},{9,1},... | collective-permute-start | bytes 393224 | tf_op jit(solution)/shard_map/ppermute | solution.py:573
  85.2 10.4 %collective-permute-start.19 = (bf16[272,512]{1,0:T(8,128)(2,1)S(1)}, bf16[272,512]{1,0:T(8,128)(2,1)S(1)}, u32[]{:S(2)}, u32[]{:S(2)}) collective-permute-start(bf16[272,512]{1,0:T(8,128)(2,1)S(1)} %get-tuple-element.278), channel_id=1, source_target_pairs={{0,2},{1,3},{2,0},{3,1},{4,6},{5,7},{6,4},{7,5},{8,10},{9,11},{10,... | collective-permute-start | bytes 835592 | tf_op jit(solution)/shard_map/ppermute | solution.py:573
  87.0 8.5 %collective-permute-start.15 = (bf16[144,512]{1,0:T(8,128)(2,1)S(1)}, bf16[144,512]{1,0:T(8,128)(2,1)S(1)}, u32[]{:S(2)}, u32[]{:S(2)}) collective-permute-start(bf16[144,512]{1,0:T(8,128)(2,1)S(1)} %pad_maximum_fusion.12), channel_id=1, source_target_pairs={{0,8},{1,9},{2,10},{3,11},{4,12},{5,13},{6,14},{7,15},{8,0},{9,1},... | collective-permute-start | bytes 442376 | tf_op jit(solution)/shard_map/ppermute | solution.py:573
  95.8 11.1 %collective-permute-start.22 = (bf16[4,512,128]{2,1,0:T(8,128)(2,1)S(1)}, bf16[4,512,128]{2,1,0:T(8,128)(2,1)S(1)}, u32[]{:S(2)}, u32[]{:S(2)}) collective-permute-start(bf16[4,512,128]{2,1,0:T(8,128)(2,1)S(1)} %pad_maximum_fusion.2), channel_id=1, source_target_pairs={{0,4},{1,5},{2,6},{3,7},{4,0},{5,1},{6,2},{7,3},{8,12},{9,13},{10,... | collective-permute-start | bytes 1572872 | tf_op jit(solution)/shard_map/ppermute | solution.py:573
  97.4 10.8 %collective-permute-start.21 = (bf16[4,512,128]{2,1,0:T(8,128)(2,1)S(1)}, bf16[4,512,128]{2,1,0:T(8,128)(2,1)S(1)}, u32[]{:S(2)}, u32[]{:S(2)}) collective-permute-start(bf16[4,512,128]{2,1,0:T(8,128)(2,1)S(1)} %pad_maximum_fusion.2), channel_id=1, source_target_pairs={{0,2},{1,3},{2,0},{3,1},{4,6},{5,7},{6,4},{7,5},{8,10},{9,11},{10,... | collective-permute-start | bytes 1572872 | tf_op jit(solution)/shard_map/ppermute | solution.py:573
  98.1 7.5 %collective-permute-start.20 = (bf16[144,512]{1,0:T(8,128)(2,1)S(1)}, bf16[144,512]{1,0:T(8,128)(2,1)S(1)}, u32[]{:S(2)}, u32[]{:S(2)}) collective-permute-start(bf16[144,512]{1,0:T(8,128)(2,1)S(1)} %pad_maximum_fusion.13), channel_id=1, source_target_pairs={{0,16},{1,17},{2,18},{3,19},{4,20},{5,21},{6,22},{7,23},{8,24},{9,... | collective-permute-start | bytes 442376 | tf_op jit(solution)/shard_map/ppermute | solution.py:573
  108.4 9.3 %collective-permute-start.26 = (bf16[12,512,128]{2,1,0:T(8,128)(2,1)S(1)}, bf16[12,512,128]{2,1,0:T(8,128)(2,1)S(1)}, u32[]{:S(2)}, u32[]{:S(2)}) collective-permute-start(bf16[12,512,128]{2,1,0:T(8,128)(2,1)S(1)} %pad_maximum_fusion.refs_0_), channel_id=1, source_target_pairs={{0,1},{1,0},{2,3},{3,2},{4,5},{5,4},{6,7},{7,6},{8,9},{9,8},{10,11... | collective-permute-start | bytes 4718600 | tf_op jit(solution)/shard_map/ppermute | solution.py:573
  108.4 8.7 %collective-permute-start.24 = (bf16[2,512,128]{2,1,0:T(8,128)(2,1)S(1)}, bf16[2,512,128]{2,1,0:T(8,128)(2,1)S(1)}, u32[]{:S(2)}, u32[]{:S(2)}) collective-permute-start(bf16[2,512,128]{2,1,0:T(8,128)(2,1)S(1)} %slice.251), channel_id=1, source_target_pairs={{0,2},{1,3},{2,0},{3,1},{4,6},{5,7},{6,4},{7,5},{8,10},{9,11},{10,... | collective-permute-start | bytes 786440 | tf_op jit(solution)/shard_map/ppermute | solution.py:573
  109.3 8.4 %collective-permute-start.25 = (bf16[2,512,128]{2,1,0:T(8,128)(2,1)S(1)}, bf16[2,512,128]{2,1,0:T(8,128)(2,1)S(1)}, u32[]{:S(2)}, u32[]{:S(2)}) collective-permute-start(bf16[2,512,128]{2,1,0:T(8,128)(2,1)S(1)} %slice.252), channel_id=1, source_target_pairs={{0,4},{1,5},{2,6},{3,7},{4,0},{5,1},{6,2},{7,3},{8,12},{9,13},{10,... | collective-permute-start | bytes 786440 | tf_op jit(solution)/shard_map/ppermute | solution.py:573
  110.5 5.3 %collective-permute-start.23 = (bf16[128,512]{1,0:T(8,128)(2,1)S(1)}, bf16[128,512]{1,0:T(8,128)(2,1)S(1)}, u32[]{:S(2)}, u32[]{:S(2)}) collective-permute-start(bf16[128,512]{1,0:T(8,128)(2,1)S(1)} %add_convert_fusion), channel_id=1, source_target_pairs={{0,8},{1,9},{2,10},{3,11},{4,12},{5,13},{6,14},{7,15},{8,0},{9,1},... | collective-permute-start | bytes 393224 | tf_op jit(solution)/shard_map/ppermute | solution.py:573
  117.7 2.0 %collective-permute-start.27 = (bf16[4,512,128]{2,1,0:T(8,128)(2,1)S(1)}, bf16[4,512,128]{2,1,0:T(8,128)(2,1)S(1)}, u32[]{:S(2)}, u32[]{:S(2)}) collective-permute-start(bf16[4,512,128]{2,1,0:T(8,128)(2,1)S(1)} %pad_maximum_fusion.3.refs_0_), channel_id=1, source_target_pairs={{0,1},{1,0},{2,3},{3,2},{4,5},{5,4},{6,7},{7,6},{8,9},{9,8},{10,11... | collective-permute-start | bytes 1572872 | tf_op jit(solution)/shard_map/ppermute | solution.py:573
  117.8 8.7 %collective-permute-start.29 = (bf16[4,64,512]{2,1,0:T(8,128)(2,1)S(1)}, bf16[4,64,512]{2,1,0:T(8,128)(2,1)S(1)}, u32[]{:S(2)}, u32[]{:S(2)}) collective-permute-start(bf16[4,64,512]{2,1,0:T(8,128)(2,1)S(1)} %pad_maximum_fusion.10), channel_id=1, source_target_pairs={{0,4},{1,5},{2,6},{3,7},{4,0},{5,1},{6,2},{7,3},{8,12},{9,13},{10,... | collective-permute-start | bytes 786440 | tf_op jit(solution)/shard_map/ppermute | solution.py:573
  119.2 8.4 %collective-permute-start.28 = (bf16[4,64,512]{2,1,0:T(8,128)(2,1)S(1)}, bf16[4,64,512]{2,1,0:T(8,128)(2,1)S(1)}, u32[]{:S(2)}, u32[]{:S(2)}) collective-permute-start(bf16[4,64,512]{2,1,0:T(8,128)(2,1)S(1)} %pad_maximum_fusion.10), channel_id=1, source_target_pairs={{0,2},{1,3},{2,0},{3,1},{4,6},{5,7},{6,4},{7,5},{8,10},{9,11},{10,... | collective-permute-start | bytes 786440 | tf_op jit(solution)/shard_map/ppermute | solution.py:573
  127.7 2.4 %collective-permute-start.30 = (bf16[12,64,512]{2,1,0:T(8,128)(2,1)S(1)}, bf16[12,64,512]{2,1,0:T(8,128)(2,1)S(1)}, u32[]{:S(2)}, u32[]{:S(2)}) collective-permute-start(bf16[12,64,512]{2,1,0:T(8,128)(2,1)S(1)} %pad_maximum_fusion.1.refs_0_), channel_id=1, source_target_pairs={{0,1},{1,0},{2,3},{3,2},{4,5},{5,4},{6,7},{7,6},{8,9},{9,8},{10,11... | collective-permute-start | bytes 2359304 | tf_op jit(solution)/shard_map/ppermute | solution.py:573
  127.8 5.9 %collective-permute-start.31 = (bf16[2,64,512]{2,1,0:T(8,128)(2,1)S(1)}, bf16[2,64,512]{2,1,0:T(8,128)(2,1)S(1)}, u32[]{:S(2)}, u32[]{:S(2)}) collective-permute-start(bf16[2,64,512]{2,1,0:T(8,128)(2,1)S(1)} %slice.257), channel_id=1, source_target_pairs={{0,2},{1,3},{2,0},{3,1},{4,6},{5,7},{6,4},{7,5},{8,10},{9,11},{10,... | collective-permute-start | bytes 393224 | tf_op jit(solution)/shard_map/ppermute | solution.py:573
  128.4 5.6 %collective-permute-start.32 = (bf16[2,64,512]{2,1,0:T(8,128)(2,1)S(1)}, bf16[2,64,512]{2,1,0:T(8,128)(2,1)S(1)}, u32[]{:S(2)}, u32[]{:S(2)}) collective-permute-start(bf16[2,64,512]{2,1,0:T(8,128)(2,1)S(1)} %slice.258), channel_id=1, source_target_pairs={{0,4},{1,5},{2,6},{3,7},{4,0},{5,1},{6,2},{7,3},{8,12},{9,13},{10,... | collective-permute-start | bytes 393224 | tf_op jit(solution)/shard_map/ppermute | solution.py:573
  (18 other events, 124.3 us)

commit v15 on v14

--- a/solution.py
+++ b/solution.py
@@ -700,23 +700,19 @@
     fourth = jnp.stack([rest[:piece], rest_back[:piece], rest[piece:], rest_back[piece:]])
     far_pair = jnp.concatenate([far_a, far_b])
     token, fourth, far_pair = wait(token, fourth, far_pair)
-    fourth_y, fourth_x = exchange(fourth, ROW), exchange(fourth, NEAR_X)
+    fourths = [exchange(fourth, xy[k]) for k in (2, 0, 1)]
     other_far = exchange(far_pair, CORE)
     token, other_far = wait(token, other_far)
+    other_fourth = exchange(fourth, CORE)
     out_back, out_in = place(token, [(12, far_pair), (16, other), (28, other_far)], grads, width)
-    token, out_back, out_in, fourth_y, fourth_x = wait(token, out_back, out_in, fourth_y, fourth_x)
-
-    sends = [fourth_x[:2], fourth_y[2:], jnp.concatenate([fourth, fourth_y, fourth_x])]
-    token, sends = wait(token, sends)
-    last_a, last_b, pair = (exchange(s, m) for s, m in zip(sends, (ROW, NEAR_X, CORE)))
-    token, pair = wait(token, pair)
-    made = sort(token, [(0, sends[2]), (16, pair)], [], width)
-    token, made, last_a, last_b = wait(token, made, last_a, last_b)
-
-    ends = exchange(jnp.concatenate([last_a, last_b]), CORE)
-    made = sort(token, [(12, last_a), (14, last_b)], made, width)
-    token, made, ends = wait(token, made, ends)
-    out_out, out_query, out_key, out_value = sort(token, [(28, ends)], made, width)
+    token, out_back, out_in, other_fourth, fourths = wait(token, out_back, out_in, other_fourth, fourths)
+
+    three = jnp.concatenate([fourths[1], fourths[2], fourths[0]])
+    token, three = wait(token, three)
+    others = exchange(three, CORE)
+    made = sort(token, [(0, fourth), (4, three), (16, other_fourth)], [], width)
+    token, made, others = wait(token, made, others)
+    out_out, out_query, out_key, out_value = sort(token, [(20, others)], made, width)
     return (pooled, input_grad, out_query, out_key, out_value, out_out, out_in, out_back, *outs)
 
 def solution(mesh):

time: 137 us -> 138 us (level)
  waiting for transfers between devices: 31.6 us -> 33.9 us
    ppermute x34 -> x33, waiting for transfers between devices: 31.6 us -> 33.9 us  [exchange(): lax.ppermute(value, ('dp', 'blk'), [(i, i ^ bits) for i in range(size)])]
    pallas_call x3 -> x2, Pallas kernels: 5.38 us -> 4.23 us  [sort(): pl.pallas_call(functools.partial(sort_kernel, [first for first, _ in part...]
    ppermute x34 -> x33, starting transfers between devices: 33.6 us -> 33.1 us  [exchange(): lax.ppermute(value, ('dp', 'blk'), [(i, i ^ bits) for i in range(size)])]
  transfers between devices with their start and end apart: 34 -> 33, of which waited for: 18 -> 14; matrix products, arithmetic and copies ran while one was open for 3% -> 3% of each run, Pallas kernels for 28% -> 27%
where the time goes in v15:
time: 138 us
  Pallas kernels  60.2 us (44%)
  waiting for transfers between devices  33.9 us (25%)
  starting transfers between devices  33.1 us (24%)
  local copies, waits for them, and re-layouts  5.39 us (4%)
  other arithmetic  3.73 us (3%)
    ppermute x33, waiting for transfers between devices, exchange(): lax.ppermute(value, ('dp', 'blk'), [(i, i ^ bits) for i in range(size)])  33.9 us
    ppermute x33, starting transfers between devices, exchange(): lax.ppermute(value, ('dp', 'blk'), [(i, i ^ bits) for i in range(size)])  33.1 us
    pallas_call x1, Pallas kernels, front(): pl.pallas_call(front_kernel, in_specs=[smem] + [vmem] * 14 + [free] * 3,...  20.3 us
    pallas_call x1, Pallas kernels, back(): pl.pallas_call(back_kernel, grid=(width // 128,), in_specs=[smem, col(cou...  20.1 us
    pallas_call x2, Pallas kernels, place(): pl.pallas_call(functools.partial(place_kernel, [first for first, _ in par...  5.39 us
    pallas_call x2, Pallas kernels, sort(): pl.pallas_call(functools.partial(sort_kernel, [first for first, _ in part...  4.23 us
    unnamed x32, local copies, waits for them, and re-layouts  3.86 us
  transfers between devices with their start and end apart: 33, of which 14 were waited for; matrix products, arithmetic and copies ran while one was open for 3% of the time, Pallas kernels for 27%

profile of v15, /device:TPU:0, one launch (start us, length us, event | category | flops | bytes accessed | tf_op | source)
XLA Modules:
  0.0 137.7 jit_solution(2988295550296428789)
XLA Ops:
  2.4 2.6 %collective-permute-start = (bf16[256,512]{1,0:T(8,128)(2,1)S(1)}, bf16[256,512]{1,0:T(8,128)(2,1)S(1)}, u32[]{:S(2)}, u32[]{:S(2)}) collective-permute-start(bf16[256,512]{1,0:T(8,128)(2,1)S(1)} %get-tuple-element.172), channel_id=1, source_target_pairs={{0,2},{1,3},{2,0},{3,1},{4,6},{5,7},{6,4},{7,5},{8,10},{9,11},{10,... | collective-permute-start | bytes 786440 | tf_op jit(solution)/shard_map/ppermute | solution.py:573
  8.8 1.5 %prepare.1 = (bf16[512,512]{1,0:T(8,128)(2,1)S(1)}, bf16[256,512]{1,0:T(8,128)(2,1)S(1)}, bf16[512,512]{1,0:T(8,128)(2,1)S(1)}, bf16[512,512]{1,0:T(8,128)(2,1)S...) custom-call(bf16[256,512]{1,0:T(8,128)(2,1)S(1)} %get-tuple-element.173.mine.near.near, ...), custom_call_target="tpu_custom_call" | custom-call | tf_op jit(solution)/shard_map/prepare/pallas_call | solution.py:65
  10.4 1.5 %collective-permute-done.far.far_h = bf16[256,512]{1,0:T(8,128)(2,1)S(1)} collective-permute-done((bf16[256,512]{1,0:T(8,128)(2,1)S(1)}, bf16[256,512]{1,0:T(8,128)(2,1)S(1)}, u32[]{:S(2)}, u32[]{:S(2)}) %collective-permute-start) | collective-permute-done | bytes 262176 | tf_op jit(solution)/shard_map/ppermute | solution.py:573
  13.5 20.3 %front.1 = (bf16[512,512]{1,0:T(8,128)(2,1)S(1)}, bf16[256,512]{1,0:T(8,128)(2,1)S(1)}, bf16[512,512]{1,0:T(8,128)(2,1)S(1)}, bf16[512,512]{1,0:T(8,128)(2,1)S(1...) custom-call(s32[16]{0:T(128)S(1)} %get-tuple-element.316.info, ...), custom_call_target="tpu_custom_call" | custom-call | tf_op jit(solution)/shard_map/front/pallas_call | solution.py:235
  34.1 2.0 %stay.1.kept = bf16[4,4,512,128]{3,2,1,0:T(8,128)(2,1)S(1)} custom-call(s32[16]{0:T(128)S(1)} %get-tuple-element.316.info, bf16[512,2048]{1,0:T(8,128)(2,1)S(1)} %get-tuple-element.187.active, bf16[512,2048]{1,0:T(8,128)(2,1)S(1)} %get-tuple-element.188.slopes, bf16[512,512]{1,0:T(8,128)(2,1)S(1)} %get-tuple-element.189.turned, ...), custom_call_target="tpu_custom_call" | custom-call | tf_op jit(solution)/shard_map/stay/pallas_call | solution.py:301
  36.2 1.8 %inner.1.grad_inner = f32[512,512]{1,0:T(8,128)S(1)} custom-call(s32[16]{0:T(128)S(1)} %get-tuple-element.316.info, bf16[512,2048]{1,0:T(8,128)(2,1)S(1)} %get-tuple-element.188.slopes, bf16[512,2048]{1,0:T(8,128)(2,1)S(1)} %copy-done), custom_call_target="tpu_custom_call" | custom-call | tf_op jit(solution)/shard_map/inner/pallas_call | solution.py:255
  38.6 2.8 %collective-permute-start.4 = (bf16[4,512,128]{2,1,0:T(8,128)(2,1)S(1)}, bf16[4,512,128]{2,1,0:T(8,128)(2,1)S(1)}, u32[]{:S(2)}, u32[]{:S(2)}) collective-permute-start(bf16[4,512,128]{2,1,0:T(8,128)(2,1)S(1)} %get-tuple-element.220), channel_id=1, source_target_pairs={{0,6},{1,7},{2,4},{3,5},{4,2},{5,3},{6,0},{7,1},{8,14},{9,15},{10,... | collective-permute-start | bytes 1572872 | tf_op jit(solution)/shard_map/ppermute | solution.py:573
  42.2 1.7 %through.1 = (f32[512,512]{1,0:T(8,128)S(1)}, bf16[512,512]{1,0:T(8,128)(2,1)S(1)}, bf16[512,512]{1,0:T(8,128)(2,1)S(1)}, f32[8,512]{1,0:T(8,128)S(1)}) custom-call(s32[16]{0:T(128)S(1)} %get-tuple-element.316.info, f32[512,512]{1,0:T(8,128)S(1)} %inner.1.grad_inner, f32[512,512]{1,0:T(8,128)S(1)} %get-tuple-element.202.mixed, ...), custom_call_target="tpu_custom_call" | custom-call | tf_op jit(solution)/shard_map/through/pallas_call | solution.py:274
  43.9 20.1 %back.1 = (bf16[16,64,512]{2,1,0:T(8,128)(2,1)S(1)}, bf16[1040,512]{1,0:T(8,128)(2,1)}, f32[512,512]{1,0:T(8,128)}, bf16[528,512]{1,0:T(8,128)(2,1)S(1)}, f32[8,512]{1,0:T(8,128)S(1)}) custom-call(s32[16]{0:T(128)S(1)} %get-tuple-element.316.info, bf16[256,512]{1,0:T(8,128)(2,1)S(1)} %get-tuple-element.178.q_l.ql, ...), custom_call_target="tpu_custom_call" | custom-call | tf_op jit(solution)/shard_map/back/pallas_call | solution.py:449
  66.1 1.6 %collective-permute-start.9 = (bf16[512,128]{1,0:T(8,128)(2,1)S(1)}, bf16[512,128]{1,0:T(8,128)(2,1)S(1)}, u32[]{:S(2)}, u32[]{:S(2)}) collective-permute-start(bf16[512,128]{1,0:T(8,128)(2,1)S(1)} %get-tuple-element.240), channel_id=1, source_target_pairs={{0,8},{1,9},{2,10},{3,11},{4,12},{5,13},{6,14},{7,15},{8,0},{9,1},... | collective-permute-start | bytes 393224 | tf_op jit(solution)/shard_map/ppermute | solution.py:573
  67.7 2.6 %collective-permute-start.10 = (bf16[512,128]{1,0:T(8,128)(2,1)S(1)}, bf16[512,128]{1,0:T(8,128)(2,1)S(1)}, u32[]{:S(2)}, u32[]{:S(2)}) collective-permute-start(bf16[512,128]{1,0:T(8,128)(2,1)S(1)} %get-tuple-element.241), channel_id=1, source_target_pairs={{0,16},{1,17},{2,18},{3,19},{4,20},{5,21},{6,22},{7,23},{8,24},{9,... | collective-permute-start | bytes 393224 | tf_op jit(solution)/shard_map/ppermute | solution.py:573
  71.0 1.5 %collective-permute-start.12 = (bf16[272,512]{1,0:T(8,128)(2,1)S(1)}, bf16[272,512]{1,0:T(8,128)(2,1)S(1)}, u32[]{:S(2)}, u32[]{:S(2)}) collective-permute-start(bf16[272,512]{1,0:T(8,128)(2,1)S(1)} %get-tuple-element.253), channel_id=1, source_target_pairs={{0,2},{1,3},{2,0},{3,1},{4,6},{5,7},{6,4},{7,5},{8,10},{9,11},{10,... | collective-permute-start | bytes 835592 | tf_op jit(solution)/shard_map/ppermute | solution.py:573
  73.4 1.5 %collective-permute-start.14 = (bf16[272,512]{1,0:T(8,128)(2,1)S(1)}, bf16[272,512]{1,0:T(8,128)(2,1)S(1)}, u32[]{:S(2)}, u32[]{:S(2)}) collective-permute-start(bf16[272,512]{1,0:T(8,128)(2,1)S(1)} %get-tuple-element.255), channel_id=1, source_target_pairs={{0,6},{1,7},{2,4},{3,5},{4,2},{5,3},{6,0},{7,1},{8,14},{9,15},{10,... | collective-permute-start | bytes 835592 | tf_op jit(solution)/shard_map/ppermute | solution.py:573
  76.0 4.7 %collective-permute-done.10 = bf16[512,128]{1,0:T(8,128)(2,1)S(1)} collective-permute-done((bf16[512,128]{1,0:T(8,128)(2,1)S(1)}, bf16[512,128]{1,0:T(8,128)(2,1)S(1)}, u32[]{:S(2)}, u32[]{:S(2)}) %collective-permute-start.10) | collective-permute-done | bytes 131104 | tf_op jit(solution)/shard_map/ppermute | solution.py:573
  80.7 2.5 %collective-permute-start.18 = (bf16[512,128]{1,0:T(8,128)(2,1)S(1)}, bf16[512,128]{1,0:T(8,128)(2,1)S(1)}, u32[]{:S(2)}, u32[]{:S(2)}) collective-permute-start(bf16[512,128]{1,0:T(8,128)(2,1)S(1)} %add_convert_fusion.2), channel_id=1, source_target_pairs={{0,24},{1,25},{2,26},{3,27},{4,28},{5,29},{6,30},{7,31},{8,16},{9,... | collective-permute-start | bytes 393224 | tf_op jit(solution)/shard_map/ppermute | solution.py:573
  85.2 1.4 %collective-permute-start.19 = (bf16[272,512]{1,0:T(8,128)(2,1)S(1)}, bf16[272,512]{1,0:T(8,128)(2,1)S(1)}, u32[]{:S(2)}, u32[]{:S(2)}) collective-permute-start(bf16[272,512]{1,0:T(8,128)(2,1)S(1)} %get-tuple-element.265), channel_id=1, source_target_pairs={{0,2},{1,3},{2,0},{3,1},{4,6},{5,7},{6,4},{7,5},{8,10},{9,11},{10,... | collective-permute-start | bytes 835592 | tf_op jit(solution)/shard_map/ppermute | solution.py:573
  87.0 1.3 collective-permute-start.15
  88.3 7.2 %collective-permute-done.15 = bf16[144,512]{1,0:T(8,128)(2,1)S(1)} collective-permute-done((bf16[144,512]{1,0:T(8,128)(2,1)S(1)}, bf16[144,512]{1,0:T(8,128)(2,1)S(1)}, u32[]{:S(2)}, u32[]{:S(2)}) %collective-permute-start.15) | collective-permute-done | bytes 147488 | tf_op jit(solution)/shard_map/ppermute | solution.py:573
  95.8 1.6 %collective-permute-start.22 = (bf16[4,512,128]{2,1,0:T(8,128)(2,1)S(1)}, bf16[4,512,128]{2,1,0:T(8,128)(2,1)S(1)}, u32[]{:S(2)}, u32[]{:S(2)}) collective-permute-start(bf16[4,512,128]{2,1,0:T(8,128)(2,1)S(1)} %pad_maximum_fusion.2), channel_id=1, source_target_pairs={{0,4},{1,5},{2,6},{3,7},{4,0},{5,1},{6,2},{7,3},{8,12},{9,13},{10,... | collective-permute-start | bytes 1572872 | tf_op jit(solution)/shard_map/ppermute | solution.py:573
  98.0 1.4 %collective-permute-start.20 = (bf16[144,512]{1,0:T(8,128)(2,1)S(1)}, bf16[144,512]{1,0:T(8,128)(2,1)S(1)}, u32[]{:S(2)}, u32[]{:S(2)}) collective-permute-start(bf16[144,512]{1,0:T(8,128)(2,1)S(1)} %pad_maximum_fusion.12), channel_id=1, source_target_pairs={{0,16},{1,17},{2,18},{3,19},{4,20},{5,21},{6,22},{7,23},{8,24},{9,... | collective-permute-start | bytes 442376 | tf_op jit(solution)/shard_map/ppermute | solution.py:573
  100.9 4.6 %collective-permute-done.20 = bf16[144,512]{1,0:T(8,128)(2,1)S(1)} collective-permute-done((bf16[144,512]{1,0:T(8,128)(2,1)S(1)}, bf16[144,512]{1,0:T(8,128)(2,1)S(1)}, u32[]{:S(2)}, u32[]{:S(2)}) %collective-permute-start.20) | collective-permute-done | bytes 147488 | tf_op jit(solution)/shard_map/ppermute | solution.py:573
  109.2 1.3 collective-permute-start.25
  111.2 2.3 %place.2 = (f32[2048,512]{1,0:T(8,128)}, f32[512,2048]{1,0:T(8,128)}) custom-call(s32[16]{0:T(128)S(1)} %get-tuple-element.316.info, bf16[12,512,128]{2,1,0:T(8,128)(2,1)S(1)} %pad_maximum_fusion.refs_0_), custom_call_target="tpu_custom_call" | custom-call | tf_op jit(solution)/shard_map/place/pallas_call | solution.py:516
  113.5 2.2 %collective-permute-done.23 = bf16[128,512]{1,0:T(8,128)(2,1)S(1)} collective-permute-done((bf16[128,512]{1,0:T(8,128)(2,1)S(1)}, bf16[128,512]{1,0:T(8,128)(2,1)S(1)}, u32[]{:S(2)}, u32[]{:S(2)}) %collective-permute-start.23) | collective-permute-done | bytes 131104 | tf_op jit(solution)/shard_map/ppermute | solution.py:573
  115.8 1.3 collective-permute-done.24
  117.7 1.4 collective-permute-start.31
  119.7 1.6 %collective-permute-start.29 = (bf16[4,64,512]{2,1,0:T(8,128)(2,1)S(1)}, bf16[4,64,512]{2,1,0:T(8,128)(2,1)S(1)}, u32[]{:S(2)}, u32[]{:S(2)}) collective-permute-start(bf16[4,64,512]{2,1,0:T(8,128)(2,1)S(1)} %pad_maximum_fusion.10.refs_0_), channel_id=1, source_target_pairs={{0,6},{1,7},{2,4},{3,5},{4,2},{5,3},{6,0},{7,1},{8,14},{9,15},{10,... | collective-permute-start | bytes 786440 | tf_op jit(solution)/shard_map/ppermute | solution.py:573
  121.3 3.1 %place.3 = (f32[2048,512]{1,0:T(8,128)}, f32[512,2048]{1,0:T(8,128)}) custom-call(s32[16]{0:T(128)S(1)} %get-tuple-element.316.info, bf16[4,512,128]{2,1,0:T(8,128)(2,1)S(1)} %pad_maximum_fusion.3.refs_0_, bf16[12,512,128]{2,1,0:T(8,128)(2,1)S(1)} %collective-permute-done.26.refs_1_, ...), custom_call_target="tpu_custom_call", output_to_operand_aliasing={{0}: (4, {}), {1}: (5, {})} | custom-call | tf_op jit(solution)/shard_map/place/pallas_call | solution.py:516
  124.4 2.5 %collective-permute-done.31 = bf16[4,64,512]{2,1,0:T(8,128)(2,1)S(1)} collective-permute-done((bf16[4,64,512]{2,1,0:T(8,128)(2,1)S(1)}, bf16[4,64,512]{2,1,0:T(8,128)(2,1)S(1)}, u32[]{:S(2)}, u32[]{:S(2)}) %collective-permute-start.31) | collective-permute-done | bytes 262176 | tf_op jit(solution)/shard_map/ppermute | solution.py:573
  126.9 6.2 %collective-permute-done.30 = bf16[4,64,512]{2,1,0:T(8,128)(2,1)S(1)} collective-permute-done((bf16[4,64,512]{2,1,0:T(8,128)(2,1)S(1)}, bf16[4,64,512]{2,1,0:T(8,128)(2,1)S(1)}, u32[]{:S(2)}, u32[]{:S(2)}) %collective-permute-start.30) | collective-permute-done | bytes 262176 | tf_op jit(solution)/shard_map/ppermute | solution.py:573
  133.3 2.4 %sort.2 = (f32[512,512]{1,0:T(8,128)}, f32[512,512]{1,0:T(8,128)}, f32[512,512]{1,0:T(8,128)}, f32[512,512]{1,0:T(8,128)}) custom-call(s32[16]{0:T(128)S(1)} %get-tuple-element.316.info, bf16[4,64,512]{2,1,0:T(8,128)(2,1)S(1)} %pad_maximum_fusion.10.refs_0_, bf16[12,64,512]{2,1,0:T(8,128)(2,1)S(1)} %pad_maximum_fusion.1.refs_1_, ...), custom_call_target="tpu_custom_call" | custom-call | tf_op jit(solution)/shard_map/sort/pallas_call | solution.py:550
  135.7 1.9 %sort.3 = (f32[512,512]{1,0:T(8,128)}, f32[512,512]{1,0:T(8,128)}, f32[512,512]{1,0:T(8,128)}, f32[512,512]{1,0:T(8,128)}) custom-call(s32[16]{0:T(128)S(1)} %get-tuple-element.316.info, bf16[12,64,512]{2,1,0:T(8,128)(2,1)S(1)} %collective-permute-done.32.refs_0_, ...), custom_call_target="tpu_custom_call", output_to_operand_aliasing={{0}: (2, {}), {1}: (3, {}), {2}: (4, {}), {3}: (5, {})} | custom-call | tf_op jit(solution)/shard_map/sort/pallas_call | solution.py:550
  (118 shorter events, 23.8 us)
Async XLA Ops:
  1.9 3.1 %collective-permute-start.1 = (bf16[256,512]{1,0:T(8,128)(2,1)S(1)}, bf16[256,512]{1,0:T(8,128)(2,1)S(1)}, u32[]{:S(2)}, u32[]{:S(2)}) collective-permute-start(bf16[256,512]{1,0:T(8,128)(2,1)S(1)} %get-tuple-element.173.mine.near.near_h), channel_id=1, source_target_pairs={{0,1},{1,0},{2,3},{3,2},{4,5},{5,4},{6,7},{7,6},{8,9},{9,8},{10,11... | collective-permute-start | bytes 786440 | tf_op jit(solution)/shard_map/ppermute | solution.py:573
  2.4 9.5 %collective-permute-start = (bf16[256,512]{1,0:T(8,128)(2,1)S(1)}, bf16[256,512]{1,0:T(8,128)(2,1)S(1)}, u32[]{:S(2)}, u32[]{:S(2)}) collective-permute-start(bf16[256,512]{1,0:T(8,128)(2,1)S(1)} %get-tuple-element.172), channel_id=1, source_target_pairs={{0,2},{1,3},{2,0},{3,1},{4,6},{5,7},{6,4},{7,5},{8,10},{9,11},{10,... | collective-permute-start | bytes 786440 | tf_op jit(solution)/shard_map/ppermute | solution.py:573
  33.8 4.2 %collective-permute-start.3 = (bf16[16,512,128]{2,1,0:T(8,128)(2,1)S(1)}, bf16[16,512,128]{2,1,0:T(8,128)(2,1)S(1)}, u32[]{:S(2)}, u32[]{:S(2)}) collective-permute-start(bf16[16,512,128]{2,1,0:T(8,128)(2,1)S(1)} %get-tuple-element.192), channel_id=1, source_target_pairs={{0,1},{1,0},{2,3},{3,2},{4,5},{5,4},{6,7},{7,6},{8,9},{9,8},{10,11... | collective-permute-start | bytes 6291464 | tf_op jit(solution)/shard_map/ppermute | solution.py:573
  38.6 25.4 %collective-permute-start.4 = (bf16[4,512,128]{2,1,0:T(8,128)(2,1)S(1)}, bf16[4,512,128]{2,1,0:T(8,128)(2,1)S(1)}, u32[]{:S(2)}, u32[]{:S(2)}) collective-permute-start(bf16[4,512,128]{2,1,0:T(8,128)(2,1)S(1)} %get-tuple-element.220), channel_id=1, source_target_pairs={{0,6},{1,7},{2,4},{3,5},{4,2},{5,3},{6,0},{7,1},{8,14},{9,15},{10,... | collective-permute-start | bytes 1572872 | tf_op jit(solution)/shard_map/ppermute | solution.py:573
  41.4 23.7 %collective-permute-start.5 = (bf16[4,512,128]{2,1,0:T(8,128)(2,1)S(1)}, bf16[4,512,128]{2,1,0:T(8,128)(2,1)S(1)}, u32[]{:S(2)}, u32[]{:S(2)}) collective-permute-start(bf16[4,512,128]{2,1,0:T(8,128)(2,1)S(1)} %get-tuple-element.221), channel_id=1, source_target_pairs={{0,2},{1,3},{2,0},{3,1},{4,6},{5,7},{6,4},{7,5},{8,10},{9,11},{10,... | collective-permute-start | bytes 1572872 | tf_op jit(solution)/shard_map/ppermute | solution.py:573
  41.9 23.5 %collective-permute-start.6 = (bf16[4,512,128]{2,1,0:T(8,128)(2,1)S(1)}, bf16[4,512,128]{2,1,0:T(8,128)(2,1)S(1)}, u32[]{:S(2)}, u32[]{:S(2)}) collective-permute-start(bf16[4,512,128]{2,1,0:T(8,128)(2,1)S(1)} %get-tuple-element.222), channel_id=1, source_target_pairs={{0,4},{1,5},{2,6},{3,7},{4,0},{5,1},{6,2},{7,3},{8,12},{9,13},{10,... | collective-permute-start | bytes 1572872 | tf_op jit(solution)/shard_map/ppermute | solution.py:573
  65.3 5.2 %collective-permute-start.7 = (bf16[1040,512]{1,0:T(8,128)(2,1)}, bf16[1040,512]{1,0:T(8,128)(2,1)S(1)}, u32[]{:S(2)}, u32[]{:S(2)}) collective-permute-start(bf16[1040,512]{1,0:T(8,128)(2,1)} %get-tuple-element.233), channel_id=1, source_target_pairs={{0,1},{1,0},{2,3},{3,2},{4,5},{5,4},{6,7},{7,6},{8,9},{9,8},{10,11... | collective-permute-start | bytes 3194888 | tf_op jit(solution)/shard_map/ppermute | solution.py:573
  65.3 5.2 %collective-permute-start.8 = (bf16[528,512]{1,0:T(8,128)(2,1)S(1)}, bf16[528,512]{1,0:T(8,128)(2,1)S(1)}, u32[]{:S(2)}, u32[]{:S(2)}) collective-permute-start(bf16[528,512]{1,0:T(8,128)(2,1)S(1)} %get-tuple-element.234), channel_id=1, source_target_pairs={{0,1},{1,0},{2,3},{3,2},{4,5},{5,4},{6,7},{7,6},{8,9},{9,8},{10,11... | collective-permute-start | bytes 1622024 | tf_op jit(solution)/shard_map/ppermute | solution.py:573
  66.1 7.3 %collective-permute-start.9 = (bf16[512,128]{1,0:T(8,128)(2,1)S(1)}, bf16[512,128]{1,0:T(8,128)(2,1)S(1)}, u32[]{:S(2)}, u32[]{:S(2)}) collective-permute-start(bf16[512,128]{1,0:T(8,128)(2,1)S(1)} %get-tuple-element.240), channel_id=1, source_target_pairs={{0,8},{1,9},{2,10},{3,11},{4,12},{5,13},{6,14},{7,15},{8,0},{9,1},... | collective-permute-start | bytes 393224 | tf_op jit(solution)/shard_map/ppermute | solution.py:573
  67.7 12.9 %collective-permute-start.10 = (bf16[512,128]{1,0:T(8,128)(2,1)S(1)}, bf16[512,128]{1,0:T(8,128)(2,1)S(1)}, u32[]{:S(2)}, u32[]{:S(2)}) collective-permute-start(bf16[512,128]{1,0:T(8,128)(2,1)S(1)} %get-tuple-element.241), channel_id=1, source_target_pairs={{0,16},{1,17},{2,18},{3,19},{4,20},{5,21},{6,22},{7,23},{8,24},{9,... | collective-permute-start | bytes 393224 | tf_op jit(solution)/shard_map/ppermute | solution.py:573
  70.3 10.3 %collective-permute-start.11 = (bf16[512,128]{1,0:T(8,128)(2,1)S(1)}, bf16[512,128]{1,0:T(8,128)(2,1)S(1)}, u32[]{:S(2)}, u32[]{:S(2)}) collective-permute-start(bf16[512,128]{1,0:T(8,128)(2,1)S(1)} %get-tuple-element.242), channel_id=1, source_target_pairs={{0,24},{1,25},{2,26},{3,27},{4,28},{5,29},{6,30},{7,31},{8,16},{9,... | collective-permute-start | bytes 393224 | tf_op jit(solution)/shard_map/ppermute | solution.py:573
  71.0 13.4 %collective-permute-start.12 = (bf16[272,512]{1,0:T(8,128)(2,1)S(1)}, bf16[272,512]{1,0:T(8,128)(2,1)S(1)}, u32[]{:S(2)}, u32[]{:S(2)}) collective-permute-start(bf16[272,512]{1,0:T(8,128)(2,1)S(1)} %get-tuple-element.253), channel_id=1, source_target_pairs={{0,2},{1,3},{2,0},{3,1},{4,6},{5,7},{6,4},{7,5},{8,10},{9,11},{10,... | collective-permute-start | bytes 835592 | tf_op jit(solution)/shard_map/ppermute | solution.py:573
  72.5 12.7 %collective-permute-start.13 = (bf16[272,512]{1,0:T(8,128)(2,1)S(1)}, bf16[272,512]{1,0:T(8,128)(2,1)S(1)}, u32[]{:S(2)}, u32[]{:S(2)}) collective-permute-start(bf16[272,512]{1,0:T(8,128)(2,1)S(1)} %get-tuple-element.254), channel_id=1, source_target_pairs={{0,4},{1,5},{2,6},{3,7},{4,0},{5,1},{6,2},{7,3},{8,12},{9,13},{10,... | collective-permute-start | bytes 835592 | tf_op jit(solution)/shard_map/ppermute | solution.py:573
  73.4 13.3 %collective-permute-start.14 = (bf16[272,512]{1,0:T(8,128)(2,1)S(1)}, bf16[272,512]{1,0:T(8,128)(2,1)S(1)}, u32[]{:S(2)}, u32[]{:S(2)}) collective-permute-start(bf16[272,512]{1,0:T(8,128)(2,1)S(1)} %get-tuple-element.255), channel_id=1, source_target_pairs={{0,6},{1,7},{2,4},{3,5},{4,2},{5,3},{6,0},{7,1},{8,14},{9,15},{10,... | collective-permute-start | bytes 835592 | tf_op jit(solution)/shard_map/ppermute | solution.py:573
  80.7 14.8 %collective-permute-start.18 = (bf16[512,128]{1,0:T(8,128)(2,1)S(1)}, bf16[512,128]{1,0:T(8,128)(2,1)S(1)}, u32[]{:S(2)}, u32[]{:S(2)}) collective-permute-start(bf16[512,128]{1,0:T(8,128)(2,1)S(1)} %add_convert_fusion.2), channel_id=1, source_target_pairs={{0,24},{1,25},{2,26},{3,27},{4,28},{5,29},{6,30},{7,31},{8,16},{9,... | collective-permute-start | bytes 393224 | tf_op jit(solution)/shard_map/ppermute | solution.py:573
  83.2 12.4 %collective-permute-start.17 = (bf16[512,128]{1,0:T(8,128)(2,1)S(1)}, bf16[512,128]{1,0:T(8,128)(2,1)S(1)}, u32[]{:S(2)}, u32[]{:S(2)}) collective-permute-start(bf16[512,128]{1,0:T(8,128)(2,1)S(1)} %add_convert_fusion.2), channel_id=1, source_target_pairs={{0,16},{1,17},{2,18},{3,19},{4,20},{5,21},{6,22},{7,23},{8,24},{9,... | collective-permute-start | bytes 393224 | tf_op jit(solution)/shard_map/ppermute | solution.py:573
  84.4 11.2 %collective-permute-start.16 = (bf16[512,128]{1,0:T(8,128)(2,1)S(1)}, bf16[512,128]{1,0:T(8,128)(2,1)S(1)}, u32[]{:S(2)}, u32[]{:S(2)}) collective-permute-start(bf16[512,128]{1,0:T(8,128)(2,1)S(1)} %add_convert_fusion.2), channel_id=1, source_target_pairs={{0,8},{1,9},{2,10},{3,11},{4,12},{5,13},{6,14},{7,15},{8,0},{9,1},... | collective-permute-start | bytes 393224 | tf_op jit(solution)/shard_map/ppermute | solution.py:573
  85.2 10.4 %collective-permute-start.19 = (bf16[272,512]{1,0:T(8,128)(2,1)S(1)}, bf16[272,512]{1,0:T(8,128)(2,1)S(1)}, u32[]{:S(2)}, u32[]{:S(2)}) collective-permute-start(bf16[272,512]{1,0:T(8,128)(2,1)S(1)} %get-tuple-element.265), channel_id=1, source_target_pairs={{0,2},{1,3},{2,0},{3,1},{4,6},{5,7},{6,4},{7,5},{8,10},{9,11},{10,... | collective-permute-start | bytes 835592 | tf_op jit(solution)/shard_map/ppermute | solution.py:573
  87.0 8.5 %collective-permute-start.15 = (bf16[144,512]{1,0:T(8,128)(2,1)S(1)}, bf16[144,512]{1,0:T(8,128)(2,1)S(1)}, u32[]{:S(2)}, u32[]{:S(2)}) collective-permute-start(bf16[144,512]{1,0:T(8,128)(2,1)S(1)} %pad_maximum_fusion.11), channel_id=1, source_target_pairs={{0,8},{1,9},{2,10},{3,11},{4,12},{5,13},{6,14},{7,15},{8,0},{9,1},... | collective-permute-start | bytes 442376 | tf_op jit(solution)/shard_map/ppermute | solution.py:573
  95.8 11.1 %collective-permute-start.22 = (bf16[4,512,128]{2,1,0:T(8,128)(2,1)S(1)}, bf16[4,512,128]{2,1,0:T(8,128)(2,1)S(1)}, u32[]{:S(2)}, u32[]{:S(2)}) collective-permute-start(bf16[4,512,128]{2,1,0:T(8,128)(2,1)S(1)} %pad_maximum_fusion.2), channel_id=1, source_target_pairs={{0,4},{1,5},{2,6},{3,7},{4,0},{5,1},{6,2},{7,3},{8,12},{9,13},{10,... | collective-permute-start | bytes 1572872 | tf_op jit(solution)/shard_map/ppermute | solution.py:573
  97.3 10.8 %collective-permute-start.21 = (bf16[4,512,128]{2,1,0:T(8,128)(2,1)S(1)}, bf16[4,512,128]{2,1,0:T(8,128)(2,1)S(1)}, u32[]{:S(2)}, u32[]{:S(2)}) collective-permute-start(bf16[4,512,128]{2,1,0:T(8,128)(2,1)S(1)} %pad_maximum_fusion.2), channel_id=1, source_target_pairs={{0,2},{1,3},{2,0},{3,1},{4,6},{5,7},{6,4},{7,5},{8,10},{9,11},{10,... | collective-permute-start | bytes 1572872 | tf_op jit(solution)/shard_map/ppermute | solution.py:573
  98.0 7.5 %collective-permute-start.20 = (bf16[144,512]{1,0:T(8,128)(2,1)S(1)}, bf16[144,512]{1,0:T(8,128)(2,1)S(1)}, u32[]{:S(2)}, u32[]{:S(2)}) collective-permute-start(bf16[144,512]{1,0:T(8,128)(2,1)S(1)} %pad_maximum_fusion.12), channel_id=1, source_target_pairs={{0,16},{1,17},{2,18},{3,19},{4,20},{5,21},{6,22},{7,23},{8,24},{9,... | collective-permute-start | bytes 442376 | tf_op jit(solution)/shard_map/ppermute | solution.py:573
  108.3 9.3 %collective-permute-start.26 = (bf16[12,512,128]{2,1,0:T(8,128)(2,1)S(1)}, bf16[12,512,128]{2,1,0:T(8,128)(2,1)S(1)}, u32[]{:S(2)}, u32[]{:S(2)}) collective-permute-start(bf16[12,512,128]{2,1,0:T(8,128)(2,1)S(1)} %pad_maximum_fusion.refs_0_), channel_id=1, source_target_pairs={{0,1},{1,0},{2,3},{3,2},{4,5},{5,4},{6,7},{7,6},{8,9},{9,8},{10,11... | collective-permute-start | bytes 4718600 | tf_op jit(solution)/shard_map/ppermute | solution.py:573
  108.4 8.7 %collective-permute-start.24 = (bf16[2,512,128]{2,1,0:T(8,128)(2,1)S(1)}, bf16[2,512,128]{2,1,0:T(8,128)(2,1)S(1)}, u32[]{:S(2)}, u32[]{:S(2)}) collective-permute-start(bf16[2,512,128]{2,1,0:T(8,128)(2,1)S(1)} %slice.245), channel_id=1, source_target_pairs={{0,2},{1,3},{2,0},{3,1},{4,6},{5,7},{6,4},{7,5},{8,10},{9,11},{10,... | collective-permute-start | bytes 786440 | tf_op jit(solution)/shard_map/ppermute | solution.py:573
  109.2 8.4 %collective-permute-start.25 = (bf16[2,512,128]{2,1,0:T(8,128)(2,1)S(1)}, bf16[2,512,128]{2,1,0:T(8,128)(2,1)S(1)}, u32[]{:S(2)}, u32[]{:S(2)}) collective-permute-start(bf16[2,512,128]{2,1,0:T(8,128)(2,1)S(1)} %slice.246), channel_id=1, source_target_pairs={{0,4},{1,5},{2,6},{3,7},{4,0},{5,1},{6,2},{7,3},{8,12},{9,13},{10,... | collective-permute-start | bytes 786440 | tf_op jit(solution)/shard_map/ppermute | solution.py:573
  110.5 5.3 %collective-permute-start.23 = (bf16[128,512]{1,0:T(8,128)(2,1)S(1)}, bf16[128,512]{1,0:T(8,128)(2,1)S(1)}, u32[]{:S(2)}, u32[]{:S(2)}) collective-permute-start(bf16[128,512]{1,0:T(8,128)(2,1)S(1)} %add_convert_fusion), channel_id=1, source_target_pairs={{0,8},{1,9},{2,10},{3,11},{4,12},{5,13},{6,14},{7,15},{8,0},{9,1},... | collective-permute-start | bytes 393224 | tf_op jit(solution)/shard_map/ppermute | solution.py:573
  117.7 3.6 %collective-permute-start.27 = (bf16[4,512,128]{2,1,0:T(8,128)(2,1)S(1)}, bf16[4,512,128]{2,1,0:T(8,128)(2,1)S(1)}, u32[]{:S(2)}, u32[]{:S(2)}) collective-permute-start(bf16[4,512,128]{2,1,0:T(8,128)(2,1)S(1)} %pad_maximum_fusion.3.refs_0_), channel_id=1, source_target_pairs={{0,1},{1,0},{2,3},{3,2},{4,5},{5,4},{6,7},{7,6},{8,9},{9,8},{10,11... | collective-permute-start | bytes 1572872 | tf_op jit(solution)/shard_map/ppermute | solution.py:573
  117.7 9.2 %collective-permute-start.31 = (bf16[4,64,512]{2,1,0:T(8,128)(2,1)S(1)}, bf16[4,64,512]{2,1,0:T(8,128)(2,1)S(1)}, u32[]{:S(2)}, u32[]{:S(2)}) collective-permute-start(bf16[4,64,512]{2,1,0:T(8,128)(2,1)S(1)} %pad_maximum_fusion.10.refs_0_), channel_id=1, source_target_pairs={{0,4},{1,5},{2,6},{3,7},{4,0},{5,1},{6,2},{7,3},{8,12},{9,13},{10,... | collective-permute-start | bytes 786440 | tf_op jit(solution)/shard_map/ppermute | solution.py:573
  119.1 14.0 %collective-permute-start.30 = (bf16[4,64,512]{2,1,0:T(8,128)(2,1)S(1)}, bf16[4,64,512]{2,1,0:T(8,128)(2,1)S(1)}, u32[]{:S(2)}, u32[]{:S(2)}) collective-permute-start(bf16[4,64,512]{2,1,0:T(8,128)(2,1)S(1)} %pad_maximum_fusion.10.refs_0_), channel_id=1, source_target_pairs={{0,2},{1,3},{2,0},{3,1},{4,6},{5,7},{6,4},{7,5},{8,10},{9,11},{10,... | collective-permute-start | bytes 786440 | tf_op jit(solution)/shard_map/ppermute | solution.py:573
  119.7 13.5 %collective-permute-start.29 = (bf16[4,64,512]{2,1,0:T(8,128)(2,1)S(1)}, bf16[4,64,512]{2,1,0:T(8,128)(2,1)S(1)}, u32[]{:S(2)}, u32[]{:S(2)}) collective-permute-start(bf16[4,64,512]{2,1,0:T(8,128)(2,1)S(1)} %pad_maximum_fusion.10.refs_0_), channel_id=1, source_target_pairs={{0,6},{1,7},{2,4},{3,5},{4,2},{5,3},{6,0},{7,1},{8,14},{9,15},{10,... | collective-permute-start | bytes 786440 | tf_op jit(solution)/shard_map/ppermute | solution.py:573
  121.3 11.8 %collective-permute-start.28 = (bf16[4,64,512]{2,1,0:T(8,128)(2,1)S(1)}, bf16[4,64,512]{2,1,0:T(8,128)(2,1)S(1)}, u32[]{:S(2)}, u32[]{:S(2)}) collective-permute-start(bf16[4,64,512]{2,1,0:T(8,128)(2,1)S(1)} %pad_maximum_fusion.10.refs_0_), channel_id=1, source_target_pairs={{0,1},{1,0},{2,3},{3,2},{4,5},{5,4},{6,7},{7,6},{8,9},{9,8},{10,11... | collective-permute-start | bytes 786440 | tf_op jit(solution)/shard_map/ppermute | solution.py:573
  133.2 2.4 %collective-permute-start.32 = (bf16[12,64,512]{2,1,0:T(8,128)(2,1)S(1)}, bf16[12,64,512]{2,1,0:T(8,128)(2,1)S(1)}, u32[]{:S(2)}, u32[]{:S(2)}) collective-permute-start(bf16[12,64,512]{2,1,0:T(8,128)(2,1)S(1)} %pad_maximum_fusion.1.refs_1_), channel_id=1, source_target_pairs={{0,1},{1,0},{2,3},{3,2},{4,5},{5,4},{6,7},{7,6},{8,9},{9,8},{10,11... | collective-permute-start | bytes 2359304 | tf_op jit(solution)/shard_map/ppermute | solution.py:573
  (17 other events, 122.7 us)

commit v16 on v14

--- a/solution.py
+++ b/solution.py
@@ -458,7 +458,7 @@
                        + [pltpu.VMEM((2 * count, width), BF16), pltpu.VMEM((4 * count, width), BF16), pltpu.VMEM((4 * count, width), BF16),
                           pltpu.VMEM((8, 2048), F32), pltpu.VMEM((2, 6, 128, 384), F32), pltpu.VMEM((2, 128, 2048), F32),
                           pltpu.VMEM((2, 2 * count, 4 * count), BF16), pltpu.SemaphoreType.DMA((14,))],
-        name="back", compiler_params=pltpu.CompilerParams(vmem_limit_bytes=44 << 20),
+        name="back", compiler_params=pltpu.CompilerParams(vmem_limit_bytes=40 << 20),
     )(info, ql, qr, kl, kr, vl, vr, gout, out, inv, expo, buckets, dense_rows, through_rows, *given, grad_out)
 
 def ending_kernel(info, stay, came, near, far, grad_mixed, gain, dense_rows, home, away):

time: 137 us -> 137 us (level)
    unnamed x32 -> x28, local copies, waits for them, and re-layouts: 3.86 us -> 3.84 us
where the time goes in v16:
time: 137 us
  Pallas kernels  60.4 us (44%)
  starting transfers between devices  33.6 us (25%)
  waiting for transfers between devices  32.5 us (24%)
  local copies, waits for them, and re-layouts  5.43 us (4%)
  other arithmetic  3.74 us (3%)
    ppermute x34, starting transfers between devices, exchange(): lax.ppermute(value, ('dp', 'blk'), [(i, i ^ bits) for i in range(size)])  33.6 us
    ppermute x34, waiting for transfers between devices, exchange(): lax.ppermute(value, ('dp', 'blk'), [(i, i ^ bits) for i in range(size)])  32.5 us
    pallas_call x1, Pallas kernels, front(): pl.pallas_call(front_kernel, in_specs=[smem] + [vmem] * 14 + [free] * 3,...  20.3 us
    pallas_call x1, Pallas kernels, back(): pl.pallas_call(back_kernel, grid=(width // 128,), in_specs=[smem, col(cou...  19.1 us
    pallas_call x2, Pallas kernels, place(): pl.pallas_call(functools.partial(place_kernel, [first for first, _ in par...  5.39 us
    pallas_call x3, Pallas kernels, sort(): pl.pallas_call(functools.partial(sort_kernel, [first for first, _ in part...  5.38 us
    unnamed x28, local copies, waits for them, and re-layouts  3.84 us
  transfers between devices with their start and end apart: 34, of which 18 were waited for; matrix products, arithmetic and copies ran while one was open for 3% of the time, Pallas kernels for 28%

profile of v16, /device:TPU:0, one launch (start us, length us, event | category | flops | bytes accessed | tf_op | source)
XLA Modules:
  0.0 137.0 jit_solution(6662684031970014860)
XLA Ops:
  2.4 2.6 %collective-permute-start = (bf16[256,512]{1,0:T(8,128)(2,1)S(1)}, bf16[256,512]{1,0:T(8,128)(2,1)S(1)}, u32[]{:S(2)}, u32[]{:S(2)}) collective-permute-start(bf16[256,512]{1,0:T(8,128)(2,1)S(1)} %get-tuple-element.185), channel_id=1, source_target_pairs={{0,2},{1,3},{2,0},{3,1},{4,6},{5,7},{6,4},{7,5},{8,10},{9,11},{10,... | collective-permute-start | bytes 786440 | tf_op jit(solution)/shard_map/ppermute | solution.py:573
  8.8 1.5 %prepare.1 = (bf16[512,512]{1,0:T(8,128)(2,1)S(1)}, bf16[256,512]{1,0:T(8,128)(2,1)S(1)}, bf16[512,512]{1,0:T(8,128)(2,1)S(1)}, bf16[512,512]{1,0:T(8,128)(2,1)S...) custom-call(bf16[256,512]{1,0:T(8,128)(2,1)S(1)} %get-tuple-element.186.mine.near.near, ...), custom_call_target="tpu_custom_call" | custom-call | tf_op jit(solution)/shard_map/prepare/pallas_call | solution.py:65
  10.4 1.5 %collective-permute-done.far.far_h = bf16[256,512]{1,0:T(8,128)(2,1)S(1)} collective-permute-done((bf16[256,512]{1,0:T(8,128)(2,1)S(1)}, bf16[256,512]{1,0:T(8,128)(2,1)S(1)}, u32[]{:S(2)}, u32[]{:S(2)}) %collective-permute-start) | collective-permute-done | bytes 262176 | tf_op jit(solution)/shard_map/ppermute | solution.py:573
  13.5 20.3 %front.1 = (bf16[512,512]{1,0:T(8,128)(2,1)S(1)}, bf16[256,512]{1,0:T(8,128)(2,1)S(1)}, bf16[512,512]{1,0:T(8,128)(2,1)S(1)}, bf16[512,512]{1,0:T(8,128)(2,1)S(1...) custom-call(s32[16]{0:T(128)S(1)} %get-tuple-element.342.info, ...), custom_call_target="tpu_custom_call" | custom-call | tf_op jit(solution)/shard_map/front/pallas_call | solution.py:235
  34.1 2.0 %stay.1.kept = bf16[4,4,512,128]{3,2,1,0:T(8,128)(2,1)S(1)} custom-call(s32[16]{0:T(128)S(1)} %get-tuple-element.342.info, bf16[512,2048]{1,0:T(8,128)(2,1)S(1)} %get-tuple-element.200.active, bf16[512,2048]{1,0:T(8,128)(2,1)S(1)} %get-tuple-element.201.slopes, bf16[512,512]{1,0:T(8,128)(2,1)S(1)} %get-tuple-element.202.turned, ...), custom_call_target="tpu_custom_call" | custom-call | tf_op jit(solution)/shard_map/stay/pallas_call | solution.py:301
  36.2 1.8 %inner.1.grad_inner = f32[512,512]{1,0:T(8,128)S(1)} custom-call(s32[16]{0:T(128)S(1)} %get-tuple-element.342.info, bf16[512,2048]{1,0:T(8,128)(2,1)S(1)} %get-tuple-element.201.slopes, bf16[512,2048]{1,0:T(8,128)(2,1)S(1)} %copy-done), custom_call_target="tpu_custom_call" | custom-call | tf_op jit(solution)/shard_map/inner/pallas_call | solution.py:255
  38.6 2.8 %collective-permute-start.4 = (bf16[4,512,128]{2,1,0:T(8,128)(2,1)S(1)}, bf16[4,512,128]{2,1,0:T(8,128)(2,1)S(1)}, u32[]{:S(2)}, u32[]{:S(2)}) collective-permute-start(bf16[4,512,128]{2,1,0:T(8,128)(2,1)S(1)} %get-tuple-element.233), channel_id=1, source_target_pairs={{0,6},{1,7},{2,4},{3,5},{4,2},{5,3},{6,0},{7,1},{8,14},{9,15},{10,... | collective-permute-start | bytes 1572872 | tf_op jit(solution)/shard_map/ppermute | solution.py:573
  42.1 1.7 %through.1 = (f32[512,512]{1,0:T(8,128)S(1)}, bf16[512,512]{1,0:T(8,128)(2,1)S(1)}, bf16[512,512]{1,0:T(8,128)(2,1)S(1)}, f32[8,512]{1,0:T(8,128)S(1)}) custom-call(s32[16]{0:T(128)S(1)} %get-tuple-element.342.info, f32[512,512]{1,0:T(8,128)S(1)} %inner.1.grad_inner, f32[512,512]{1,0:T(8,128)S(1)} %get-tuple-element.215.mixed, ...), custom_call_target="tpu_custom_call" | custom-call | tf_op jit(solution)/shard_map/through/pallas_call | solution.py:274
  43.9 19.1 %back.1 = (bf16[16,64,512]{2,1,0:T(8,128)(2,1)S(1)}, bf16[1040,512]{1,0:T(8,128)(2,1)S(1)}, f32[512,512]{1,0:T(8,128)S(1)}, bf16[528,512]{1,0:T(8,128)(2,1)S(1)}, f32[8,512]{1,0:T(8,128)S(1)}) custom-call(s32[16]{0:T(128)S(1)} %get-tuple-element.342.info, bf16[256,512]{1,0:T(8,128)(2,1)S(1)} %get-tuple-element.191.q_l.ql, ...), custom_call_target="tpu_custom_call" | custom-call | tf_op jit(solution)/shard_map/back/pallas_call | solution.py:449
  63.0 2.0 %collective-permute-done.5.refs_2_ = bf16[4,512,128]{2,1,0:T(8,128)(2,1)S(1)} collective-permute-done((bf16[4,512,128]{2,1,0:T(8,128)(2,1)S(1)}, bf16[4,512,128]{2,1,0:T(8,128)(2,1)S(1)}, u32[]{:S(2)}, u32[]{:S(2)}) %collective-permute-start.5) | collective-permute-done | bytes 524320 | tf_op jit(solution)/shard_map/ppermute | solution.py:573
  66.1 1.7 %collective-permute-start.9 = (bf16[512,128]{1,0:T(8,128)(2,1)S(1)}, bf16[512,128]{1,0:T(8,128)(2,1)S(1)}, u32[]{:S(2)}, u32[]{:S(2)}) collective-permute-start(bf16[512,128]{1,0:T(8,128)(2,1)S(1)} %get-tuple-element.253), channel_id=1, source_target_pairs={{0,8},{1,9},{2,10},{3,11},{4,12},{5,13},{6,14},{7,15},{8,0},{9,1},... | collective-permute-start | bytes 393224 | tf_op jit(solution)/shard_map/ppermute | solution.py:573
  67.7 2.6 %collective-permute-start.10 = (bf16[512,128]{1,0:T(8,128)(2,1)S(1)}, bf16[512,128]{1,0:T(8,128)(2,1)S(1)}, u32[]{:S(2)}, u32[]{:S(2)}) collective-permute-start(bf16[512,128]{1,0:T(8,128)(2,1)S(1)} %get-tuple-element.254), channel_id=1, source_target_pairs={{0,16},{1,17},{2,18},{3,19},{4,20},{5,21},{6,22},{7,23},{8,24},{9,... | collective-permute-start | bytes 393224 | tf_op jit(solution)/shard_map/ppermute | solution.py:573
  71.0 1.5 %collective-permute-start.12 = (bf16[272,512]{1,0:T(8,128)(2,1)S(1)}, bf16[272,512]{1,0:T(8,128)(2,1)S(1)}, u32[]{:S(2)}, u32[]{:S(2)}) collective-permute-start(bf16[272,512]{1,0:T(8,128)(2,1)S(1)} %get-tuple-element.266), channel_id=1, source_target_pairs={{0,2},{1,3},{2,0},{3,1},{4,6},{5,7},{6,4},{7,5},{8,10},{9,11},{10,... | collective-permute-start | bytes 835592 | tf_op jit(solution)/shard_map/ppermute | solution.py:573
  73.3 1.5 %collective-permute-start.14 = (bf16[272,512]{1,0:T(8,128)(2,1)S(1)}, bf16[272,512]{1,0:T(8,128)(2,1)S(1)}, u32[]{:S(2)}, u32[]{:S(2)}) collective-permute-start(bf16[272,512]{1,0:T(8,128)(2,1)S(1)} %get-tuple-element.268), channel_id=1, source_target_pairs={{0,6},{1,7},{2,4},{3,5},{4,2},{5,3},{6,0},{7,1},{8,14},{9,15},{10,... | collective-permute-start | bytes 835592 | tf_op jit(solution)/shard_map/ppermute | solution.py:573
  75.9 4.7 %collective-permute-done.10 = bf16[512,128]{1,0:T(8,128)(2,1)S(1)} collective-permute-done((bf16[512,128]{1,0:T(8,128)(2,1)S(1)}, bf16[512,128]{1,0:T(8,128)(2,1)S(1)}, u32[]{:S(2)}, u32[]{:S(2)}) %collective-permute-start.10) | collective-permute-done | bytes 131104 | tf_op jit(solution)/shard_map/ppermute | solution.py:573
  80.7 2.4 %collective-permute-start.18 = (bf16[512,128]{1,0:T(8,128)(2,1)S(1)}, bf16[512,128]{1,0:T(8,128)(2,1)S(1)}, u32[]{:S(2)}, u32[]{:S(2)}) collective-permute-start(bf16[512,128]{1,0:T(8,128)(2,1)S(1)} %add_convert_fusion.2), channel_id=1, source_target_pairs={{0,24},{1,25},{2,26},{3,27},{4,28},{5,29},{6,30},{7,31},{8,16},{9,... | collective-permute-start | bytes 393224 | tf_op jit(solution)/shard_map/ppermute | solution.py:573
  85.2 1.4 %collective-permute-start.19 = (bf16[272,512]{1,0:T(8,128)(2,1)S(1)}, bf16[272,512]{1,0:T(8,128)(2,1)S(1)}, u32[]{:S(2)}, u32[]{:S(2)}) collective-permute-start(bf16[272,512]{1,0:T(8,128)(2,1)S(1)} %get-tuple-element.278), channel_id=1, source_target_pairs={{0,2},{1,3},{2,0},{3,1},{4,6},{5,7},{6,4},{7,5},{8,10},{9,11},{10,... | collective-permute-start | bytes 835592 | tf_op jit(solution)/shard_map/ppermute | solution.py:573
  86.9 1.3 collective-permute-start.15
  88.3 7.2 %collective-permute-done.15 = bf16[144,512]{1,0:T(8,128)(2,1)S(1)} collective-permute-done((bf16[144,512]{1,0:T(8,128)(2,1)S(1)}, bf16[144,512]{1,0:T(8,128)(2,1)S(1)}, u32[]{:S(2)}, u32[]{:S(2)}) %collective-permute-start.15) | collective-permute-done | bytes 147488 | tf_op jit(solution)/shard_map/ppermute | solution.py:573
  95.7 1.6 %collective-permute-start.22 = (bf16[4,512,128]{2,1,0:T(8,128)(2,1)S(1)}, bf16[4,512,128]{2,1,0:T(8,128)(2,1)S(1)}, u32[]{:S(2)}, u32[]{:S(2)}) collective-permute-start(bf16[4,512,128]{2,1,0:T(8,128)(2,1)S(1)} %pad_maximum_fusion.2), channel_id=1, source_target_pairs={{0,4},{1,5},{2,6},{3,7},{4,0},{5,1},{6,2},{7,3},{8,12},{9,13},{10,... | collective-permute-start | bytes 1572872 | tf_op jit(solution)/shard_map/ppermute | solution.py:573
  98.0 1.4 %collective-permute-start.20 = (bf16[144,512]{1,0:T(8,128)(2,1)S(1)}, bf16[144,512]{1,0:T(8,128)(2,1)S(1)}, u32[]{:S(2)}, u32[]{:S(2)}) collective-permute-start(bf16[144,512]{1,0:T(8,128)(2,1)S(1)} %pad_maximum_fusion.13), channel_id=1, source_target_pairs={{0,16},{1,17},{2,18},{3,19},{4,20},{5,21},{6,22},{7,23},{8,24},{9,... | collective-permute-start | bytes 442376 | tf_op jit(solution)/shard_map/ppermute | solution.py:573
  100.9 4.6 %collective-permute-done.20 = bf16[144,512]{1,0:T(8,128)(2,1)S(1)} collective-permute-done((bf16[144,512]{1,0:T(8,128)(2,1)S(1)}, bf16[144,512]{1,0:T(8,128)(2,1)S(1)}, u32[]{:S(2)}, u32[]{:S(2)}) %collective-permute-start.20) | collective-permute-done | bytes 147488 | tf_op jit(solution)/shard_map/ppermute | solution.py:573
  111.2 2.3 %place.2 = (f32[2048,512]{1,0:T(8,128)}, f32[512,2048]{1,0:T(8,128)}) custom-call(s32[16]{0:T(128)S(1)} %get-tuple-element.342.info, bf16[12,512,128]{2,1,0:T(8,128)(2,1)S(1)} %pad_maximum_fusion.refs_0_), custom_call_target="tpu_custom_call" | custom-call | tf_op jit(solution)/shard_map/place/pallas_call | solution.py:516
  113.5 2.2 %collective-permute-done.23 = bf16[128,512]{1,0:T(8,128)(2,1)S(1)} collective-permute-done((bf16[128,512]{1,0:T(8,128)(2,1)S(1)}, bf16[128,512]{1,0:T(8,128)(2,1)S(1)}, u32[]{:S(2)}, u32[]{:S(2)}) %collective-permute-start.23) | collective-permute-done | bytes 131104 | tf_op jit(solution)/shard_map/ppermute | solution.py:573
  115.7 1.3 collective-permute-done.24
  117.7 1.4 %collective-permute-start.29 = (bf16[4,64,512]{2,1,0:T(8,128)(2,1)S(1)}, bf16[4,64,512]{2,1,0:T(8,128)(2,1)S(1)}, u32[]{:S(2)}, u32[]{:S(2)}) collective-permute-start(bf16[4,64,512]{2,1,0:T(8,128)(2,1)S(1)} %pad_maximum_fusion.10), channel_id=1, source_target_pairs={{0,4},{1,5},{2,6},{3,7},{4,0},{5,1},{6,2},{7,3},{8,12},{9,13},{10,... | collective-permute-start | bytes 786440 | tf_op jit(solution)/shard_map/ppermute | solution.py:573
  119.6 3.1 %place.3 = (f32[2048,512]{1,0:T(8,128)}, f32[512,2048]{1,0:T(8,128)}) custom-call(s32[16]{0:T(128)S(1)} %get-tuple-element.342.info, bf16[4,512,128]{2,1,0:T(8,128)(2,1)S(1)} %pad_maximum_fusion.3.refs_0_, bf16[12,512,128]{2,1,0:T(8,128)(2,1)S(1)} %collective-permute-done.26.refs_1_, ...), custom_call_target="tpu_custom_call", output_to_operand_aliasing={{0}: (4, {}), {1}: (5, {})} | custom-call | tf_op jit(solution)/shard_map/place/pallas_call | solution.py:516
  122.7 3.8 %collective-permute-done.29 = bf16[4,64,512]{2,1,0:T(8,128)(2,1)S(1)} collective-permute-done((bf16[4,64,512]{2,1,0:T(8,128)(2,1)S(1)}, bf16[4,64,512]{2,1,0:T(8,128)(2,1)S(1)}, u32[]{:S(2)}, u32[]{:S(2)}) %collective-permute-start.29) | collective-permute-done | bytes 262176 | tf_op jit(solution)/shard_map/ppermute | solution.py:573
  128.3 1.5 %collective-permute-start.32 = (bf16[2,64,512]{2,1,0:T(8,128)(2,1)S(1)}, bf16[2,64,512]{2,1,0:T(8,128)(2,1)S(1)}, u32[]{:S(2)}, u32[]{:S(2)}) collective-permute-start(bf16[2,64,512]{2,1,0:T(8,128)(2,1)S(1)} %slice.258), channel_id=1, source_target_pairs={{0,4},{1,5},{2,6},{3,7},{4,0},{5,1},{6,2},{7,3},{8,12},{9,13},{10,... | collective-permute-start | bytes 393224 | tf_op jit(solution)/shard_map/ppermute | solution.py:573
  130.0 2.6 %sort.3 = (f32[512,512]{1,0:T(8,128)}, f32[512,512]{1,0:T(8,128)}, f32[512,512]{1,0:T(8,128)}, f32[512,512]{1,0:T(8,128)}) custom-call(s32[16]{0:T(128)S(1)} %get-tuple-element.342.info, bf16[12,64,512]{2,1,0:T(8,128)(2,1)S(1)} %pad_maximum_fusion.1.refs_0_, bf16[12,64,512]{2,1,0:T(8,128)(2,1)S(1)} %collective-permute-done.30.refs_1_), custom_call_target="tpu_custom_call" | custom-call | tf_op jit(solution)/shard_map/sort/pallas_call | solution.py:550
  134.0 1.4 %sort.4 = (f32[512,512]{1,0:T(8,128)}, f32[512,512]{1,0:T(8,128)}, f32[512,512]{1,0:T(8,128)}, f32[512,512]{1,0:T(8,128)}) custom-call(s32[16]{0:T(128)S(1)} %get-tuple-element.342.info, bf16[2,64,512]{2,1,0:T(8,128)(2,1)S(1)} %collective-permute-done.31.refs_0_, ...), custom_call_target="tpu_custom_call", output_to_operand_aliasing={{0}: (3, {}), {1}: (4, {}), {2}: (5, {}), {3}: (6, {})} | custom-call | tf_op jit(solution)/shard_map/sort/pallas_call | solution.py:550
  135.5 1.4 %sort.5 = (f32[512,512]{1,0:T(8,128)}, f32[512,512]{1,0:T(8,128)}, f32[512,512]{1,0:T(8,128)}, f32[512,512]{1,0:T(8,128)}) custom-call(s32[16]{0:T(128)S(1)} %get-tuple-element.342.info, bf16[4,64,512]{2,1,0:T(8,128)(2,1)S(1)} %collective-permute-done.33.refs_0_, ...), custom_call_target="tpu_custom_call", output_to_operand_aliasing={{0}: (2, {}), {1}: (3, {}), {2}: (4, {}), {3}: (5, {})} | custom-call | tf_op jit(solution)/shard_map/sort/pallas_call | solution.py:550
  (120 shorter events, 27.3 us)
Async XLA Ops:
  1.9 3.1 %collective-permute-start.1 = (bf16[256,512]{1,0:T(8,128)(2,1)S(1)}, bf16[256,512]{1,0:T(8,128)(2,1)S(1)}, u32[]{:S(2)}, u32[]{:S(2)}) collective-permute-start(bf16[256,512]{1,0:T(8,128)(2,1)S(1)} %get-tuple-element.186.mine.near.near_h), channel_id=1, source_target_pairs={{0,1},{1,0},{2,3},{3,2},{4,5},{5,4},{6,7},{7,6},{8,9},{9,8},{10,11... | collective-permute-start | bytes 786440 | tf_op jit(solution)/shard_map/ppermute | solution.py:573
  2.4 9.5 %collective-permute-start = (bf16[256,512]{1,0:T(8,128)(2,1)S(1)}, bf16[256,512]{1,0:T(8,128)(2,1)S(1)}, u32[]{:S(2)}, u32[]{:S(2)}) collective-permute-start(bf16[256,512]{1,0:T(8,128)(2,1)S(1)} %get-tuple-element.185), channel_id=1, source_target_pairs={{0,2},{1,3},{2,0},{3,1},{4,6},{5,7},{6,4},{7,5},{8,10},{9,11},{10,... | collective-permute-start | bytes 786440 | tf_op jit(solution)/shard_map/ppermute | solution.py:573
  33.8 4.2 %collective-permute-start.3 = (bf16[16,512,128]{2,1,0:T(8,128)(2,1)S(1)}, bf16[16,512,128]{2,1,0:T(8,128)(2,1)S(1)}, u32[]{:S(2)}, u32[]{:S(2)}) collective-permute-start(bf16[16,512,128]{2,1,0:T(8,128)(2,1)S(1)} %get-tuple-element.205), channel_id=1, source_target_pairs={{0,1},{1,0},{2,3},{3,2},{4,5},{5,4},{6,7},{7,6},{8,9},{9,8},{10,11... | collective-permute-start | bytes 6291464 | tf_op jit(solution)/shard_map/ppermute | solution.py:573
  38.6 24.4 %collective-permute-start.4 = (bf16[4,512,128]{2,1,0:T(8,128)(2,1)S(1)}, bf16[4,512,128]{2,1,0:T(8,128)(2,1)S(1)}, u32[]{:S(2)}, u32[]{:S(2)}) collective-permute-start(bf16[4,512,128]{2,1,0:T(8,128)(2,1)S(1)} %get-tuple-element.233), channel_id=1, source_target_pairs={{0,6},{1,7},{2,4},{3,5},{4,2},{5,3},{6,0},{7,1},{8,14},{9,15},{10,... | collective-permute-start | bytes 1572872 | tf_op jit(solution)/shard_map/ppermute | solution.py:573
  41.3 23.7 %collective-permute-start.5 = (bf16[4,512,128]{2,1,0:T(8,128)(2,1)S(1)}, bf16[4,512,128]{2,1,0:T(8,128)(2,1)S(1)}, u32[]{:S(2)}, u32[]{:S(2)}) collective-permute-start(bf16[4,512,128]{2,1,0:T(8,128)(2,1)S(1)} %get-tuple-element.234), channel_id=1, source_target_pairs={{0,2},{1,3},{2,0},{3,1},{4,6},{5,7},{6,4},{7,5},{8,10},{9,11},{10,... | collective-permute-start | bytes 1572872 | tf_op jit(solution)/shard_map/ppermute | solution.py:573
  41.8 23.5 %collective-permute-start.6 = (bf16[4,512,128]{2,1,0:T(8,128)(2,1)S(1)}, bf16[4,512,128]{2,1,0:T(8,128)(2,1)S(1)}, u32[]{:S(2)}, u32[]{:S(2)}) collective-permute-start(bf16[4,512,128]{2,1,0:T(8,128)(2,1)S(1)} %get-tuple-element.235), channel_id=1, source_target_pairs={{0,4},{1,5},{2,6},{3,7},{4,0},{5,1},{6,2},{7,3},{8,12},{9,13},{10,... | collective-permute-start | bytes 1572872 | tf_op jit(solution)/shard_map/ppermute | solution.py:573
  65.3 5.2 %collective-permute-start.7 = (bf16[1040,512]{1,0:T(8,128)(2,1)S(1)}, bf16[1040,512]{1,0:T(8,128)(2,1)S(1)}, u32[]{:S(2)}, u32[]{:S(2)}) collective-permute-start(bf16[1040,512]{1,0:T(8,128)(2,1)S(1)} %get-tuple-element.246), channel_id=1, source_target_pairs={{0,1},{1,0},{2,3},{3,2},{4,5},{5,4},{6,7},{7,6},{8,9},{9,8},{10,11... | collective-permute-start | bytes 3194888 | tf_op jit(solution)/shard_map/ppermute | solution.py:573
  65.3 5.2 %collective-permute-start.8 = (bf16[528,512]{1,0:T(8,128)(2,1)S(1)}, bf16[528,512]{1,0:T(8,128)(2,1)S(1)}, u32[]{:S(2)}, u32[]{:S(2)}) collective-permute-start(bf16[528,512]{1,0:T(8,128)(2,1)S(1)} %get-tuple-element.247), channel_id=1, source_target_pairs={{0,1},{1,0},{2,3},{3,2},{4,5},{5,4},{6,7},{7,6},{8,9},{9,8},{10,11... | collective-permute-start | bytes 1622024 | tf_op jit(solution)/shard_map/ppermute | solution.py:573
  66.1 7.2 %collective-permute-start.9 = (bf16[512,128]{1,0:T(8,128)(2,1)S(1)}, bf16[512,128]{1,0:T(8,128)(2,1)S(1)}, u32[]{:S(2)}, u32[]{:S(2)}) collective-permute-start(bf16[512,128]{1,0:T(8,128)(2,1)S(1)} %get-tuple-element.253), channel_id=1, source_target_pairs={{0,8},{1,9},{2,10},{3,11},{4,12},{5,13},{6,14},{7,15},{8,0},{9,1},... | collective-permute-start | bytes 393224 | tf_op jit(solution)/shard_map/ppermute | solution.py:573
  67.7 12.9 %collective-permute-start.10 = (bf16[512,128]{1,0:T(8,128)(2,1)S(1)}, bf16[512,128]{1,0:T(8,128)(2,1)S(1)}, u32[]{:S(2)}, u32[]{:S(2)}) collective-permute-start(bf16[512,128]{1,0:T(8,128)(2,1)S(1)} %get-tuple-element.254), channel_id=1, source_target_pairs={{0,16},{1,17},{2,18},{3,19},{4,20},{5,21},{6,22},{7,23},{8,24},{9,... | collective-permute-start | bytes 393224 | tf_op jit(solution)/shard_map/ppermute | solution.py:573
  70.3 10.3 %collective-permute-start.11 = (bf16[512,128]{1,0:T(8,128)(2,1)S(1)}, bf16[512,128]{1,0:T(8,128)(2,1)S(1)}, u32[]{:S(2)}, u32[]{:S(2)}) collective-permute-start(bf16[512,128]{1,0:T(8,128)(2,1)S(1)} %get-tuple-element.255), channel_id=1, source_target_pairs={{0,24},{1,25},{2,26},{3,27},{4,28},{5,29},{6,30},{7,31},{8,16},{9,... | collective-permute-start | bytes 393224 | tf_op jit(solution)/shard_map/ppermute | solution.py:573
  71.0 13.4 %collective-permute-start.12 = (bf16[272,512]{1,0:T(8,128)(2,1)S(1)}, bf16[272,512]{1,0:T(8,128)(2,1)S(1)}, u32[]{:S(2)}, u32[]{:S(2)}) collective-permute-start(bf16[272,512]{1,0:T(8,128)(2,1)S(1)} %get-tuple-element.266), channel_id=1, source_target_pairs={{0,2},{1,3},{2,0},{3,1},{4,6},{5,7},{6,4},{7,5},{8,10},{9,11},{10,... | collective-permute-start | bytes 835592 | tf_op jit(solution)/shard_map/ppermute | solution.py:573
  72.4 12.7 %collective-permute-start.13 = (bf16[272,512]{1,0:T(8,128)(2,1)S(1)}, bf16[272,512]{1,0:T(8,128)(2,1)S(1)}, u32[]{:S(2)}, u32[]{:S(2)}) collective-permute-start(bf16[272,512]{1,0:T(8,128)(2,1)S(1)} %get-tuple-element.267), channel_id=1, source_target_pairs={{0,4},{1,5},{2,6},{3,7},{4,0},{5,1},{6,2},{7,3},{8,12},{9,13},{10,... | collective-permute-start | bytes 835592 | tf_op jit(solution)/shard_map/ppermute | solution.py:573
  73.3 13.3 %collective-permute-start.14 = (bf16[272,512]{1,0:T(8,128)(2,1)S(1)}, bf16[272,512]{1,0:T(8,128)(2,1)S(1)}, u32[]{:S(2)}, u32[]{:S(2)}) collective-permute-start(bf16[272,512]{1,0:T(8,128)(2,1)S(1)} %get-tuple-element.268), channel_id=1, source_target_pairs={{0,6},{1,7},{2,4},{3,5},{4,2},{5,3},{6,0},{7,1},{8,14},{9,15},{10,... | collective-permute-start | bytes 835592 | tf_op jit(solution)/shard_map/ppermute | solution.py:573
  80.7 14.8 %collective-permute-start.18 = (bf16[512,128]{1,0:T(8,128)(2,1)S(1)}, bf16[512,128]{1,0:T(8,128)(2,1)S(1)}, u32[]{:S(2)}, u32[]{:S(2)}) collective-permute-start(bf16[512,128]{1,0:T(8,128)(2,1)S(1)} %add_convert_fusion.2), channel_id=1, source_target_pairs={{0,24},{1,25},{2,26},{3,27},{4,28},{5,29},{6,30},{7,31},{8,16},{9,... | collective-permute-start | bytes 393224 | tf_op jit(solution)/shard_map/ppermute | solution.py:573
  83.2 12.4 %collective-permute-start.17 = (bf16[512,128]{1,0:T(8,128)(2,1)S(1)}, bf16[512,128]{1,0:T(8,128)(2,1)S(1)}, u32[]{:S(2)}, u32[]{:S(2)}) collective-permute-start(bf16[512,128]{1,0:T(8,128)(2,1)S(1)} %add_convert_fusion.2), channel_id=1, source_target_pairs={{0,16},{1,17},{2,18},{3,19},{4,20},{5,21},{6,22},{7,23},{8,24},{9,... | collective-permute-start | bytes 393224 | tf_op jit(solution)/shard_map/ppermute | solution.py:573
  84.4 11.2 %collective-permute-start.16 = (bf16[512,128]{1,0:T(8,128)(2,1)S(1)}, bf16[512,128]{1,0:T(8,128)(2,1)S(1)}, u32[]{:S(2)}, u32[]{:S(2)}) collective-permute-start(bf16[512,128]{1,0:T(8,128)(2,1)S(1)} %add_convert_fusion.2), channel_id=1, source_target_pairs={{0,8},{1,9},{2,10},{3,11},{4,12},{5,13},{6,14},{7,15},{8,0},{9,1},... | collective-permute-start | bytes 393224 | tf_op jit(solution)/shard_map/ppermute | solution.py:573
  85.2 10.4 %collective-permute-start.19 = (bf16[272,512]{1,0:T(8,128)(2,1)S(1)}, bf16[272,512]{1,0:T(8,128)(2,1)S(1)}, u32[]{:S(2)}, u32[]{:S(2)}) collective-permute-start(bf16[272,512]{1,0:T(8,128)(2,1)S(1)} %get-tuple-element.278), channel_id=1, source_target_pairs={{0,2},{1,3},{2,0},{3,1},{4,6},{5,7},{6,4},{7,5},{8,10},{9,11},{10,... | collective-permute-start | bytes 835592 | tf_op jit(solution)/shard_map/ppermute | solution.py:573
  86.9 8.5 %collective-permute-start.15 = (bf16[144,512]{1,0:T(8,128)(2,1)S(1)}, bf16[144,512]{1,0:T(8,128)(2,1)S(1)}, u32[]{:S(2)}, u32[]{:S(2)}) collective-permute-start(bf16[144,512]{1,0:T(8,128)(2,1)S(1)} %pad_maximum_fusion.12), channel_id=1, source_target_pairs={{0,8},{1,9},{2,10},{3,11},{4,12},{5,13},{6,14},{7,15},{8,0},{9,1},... | collective-permute-start | bytes 442376 | tf_op jit(solution)/shard_map/ppermute | solution.py:573
  95.7 11.1 %collective-permute-start.22 = (bf16[4,512,128]{2,1,0:T(8,128)(2,1)S(1)}, bf16[4,512,128]{2,1,0:T(8,128)(2,1)S(1)}, u32[]{:S(2)}, u32[]{:S(2)}) collective-permute-start(bf16[4,512,128]{2,1,0:T(8,128)(2,1)S(1)} %pad_maximum_fusion.2), channel_id=1, source_target_pairs={{0,4},{1,5},{2,6},{3,7},{4,0},{5,1},{6,2},{7,3},{8,12},{9,13},{10,... | collective-permute-start | bytes 1572872 | tf_op jit(solution)/shard_map/ppermute | solution.py:573
  97.3 10.8 %collective-permute-start.21 = (bf16[4,512,128]{2,1,0:T(8,128)(2,1)S(1)}, bf16[4,512,128]{2,1,0:T(8,128)(2,1)S(1)}, u32[]{:S(2)}, u32[]{:S(2)}) collective-permute-start(bf16[4,512,128]{2,1,0:T(8,128)(2,1)S(1)} %pad_maximum_fusion.2), channel_id=1, source_target_pairs={{0,2},{1,3},{2,0},{3,1},{4,6},{5,7},{6,4},{7,5},{8,10},{9,11},{10,... | collective-permute-start | bytes 1572872 | tf_op jit(solution)/shard_map/ppermute | solution.py:573
  98.0 7.5 %collective-permute-start.20 = (bf16[144,512]{1,0:T(8,128)(2,1)S(1)}, bf16[144,512]{1,0:T(8,128)(2,1)S(1)}, u32[]{:S(2)}, u32[]{:S(2)}) collective-permute-start(bf16[144,512]{1,0:T(8,128)(2,1)S(1)} %pad_maximum_fusion.13), channel_id=1, source_target_pairs={{0,16},{1,17},{2,18},{3,19},{4,20},{5,21},{6,22},{7,23},{8,24},{9,... | collective-permute-start | bytes 442376 | tf_op jit(solution)/shard_map/ppermute | solution.py:573
  108.3 9.2 %collective-permute-start.26 = (bf16[12,512,128]{2,1,0:T(8,128)(2,1)S(1)}, bf16[12,512,128]{2,1,0:T(8,128)(2,1)S(1)}, u32[]{:S(2)}, u32[]{:S(2)}) collective-permute-start(bf16[12,512,128]{2,1,0:T(8,128)(2,1)S(1)} %pad_maximum_fusion.refs_0_), channel_id=1, source_target_pairs={{0,1},{1,0},{2,3},{3,2},{4,5},{5,4},{6,7},{7,6},{8,9},{9,8},{10,11... | collective-permute-start | bytes 4718600 | tf_op jit(solution)/shard_map/ppermute | solution.py:573
  108.4 8.7 %collective-permute-start.24 = (bf16[2,512,128]{2,1,0:T(8,128)(2,1)S(1)}, bf16[2,512,128]{2,1,0:T(8,128)(2,1)S(1)}, u32[]{:S(2)}, u32[]{:S(2)}) collective-permute-start(bf16[2,512,128]{2,1,0:T(8,128)(2,1)S(1)} %slice.251), channel_id=1, source_target_pairs={{0,2},{1,3},{2,0},{3,1},{4,6},{5,7},{6,4},{7,5},{8,10},{9,11},{10,... | collective-permute-start | bytes 786440 | tf_op jit(solution)/shard_map/ppermute | solution.py:573
  109.2 8.4 %collective-permute-start.25 = (bf16[2,512,128]{2,1,0:T(8,128)(2,1)S(1)}, bf16[2,512,128]{2,1,0:T(8,128)(2,1)S(1)}, u32[]{:S(2)}, u32[]{:S(2)}) collective-permute-start(bf16[2,512,128]{2,1,0:T(8,128)(2,1)S(1)} %slice.252), channel_id=1, source_target_pairs={{0,4},{1,5},{2,6},{3,7},{4,0},{5,1},{6,2},{7,3},{8,12},{9,13},{10,... | collective-permute-start | bytes 786440 | tf_op jit(solution)/shard_map/ppermute | solution.py:573
  110.5 5.3 %collective-permute-start.23 = (bf16[128,512]{1,0:T(8,128)(2,1)S(1)}, bf16[128,512]{1,0:T(8,128)(2,1)S(1)}, u32[]{:S(2)}, u32[]{:S(2)}) collective-permute-start(bf16[128,512]{1,0:T(8,128)(2,1)S(1)} %add_convert_fusion), channel_id=1, source_target_pairs={{0,8},{1,9},{2,10},{3,11},{4,12},{5,13},{6,14},{7,15},{8,0},{9,1},... | collective-permute-start | bytes 393224 | tf_op jit(solution)/shard_map/ppermute | solution.py:573
  117.7 2.0 %collective-permute-start.27 = (bf16[4,512,128]{2,1,0:T(8,128)(2,1)S(1)}, bf16[4,512,128]{2,1,0:T(8,128)(2,1)S(1)}, u32[]{:S(2)}, u32[]{:S(2)}) collective-permute-start(bf16[4,512,128]{2,1,0:T(8,128)(2,1)S(1)} %pad_maximum_fusion.3.refs_0_), channel_id=1, source_target_pairs={{0,1},{1,0},{2,3},{3,2},{4,5},{5,4},{6,7},{7,6},{8,9},{9,8},{10,11... | collective-permute-start | bytes 1572872 | tf_op jit(solution)/shard_map/ppermute | solution.py:573
  117.7 8.7 %collective-permute-start.29 = (bf16[4,64,512]{2,1,0:T(8,128)(2,1)S(1)}, bf16[4,64,512]{2,1,0:T(8,128)(2,1)S(1)}, u32[]{:S(2)}, u32[]{:S(2)}) collective-permute-start(bf16[4,64,512]{2,1,0:T(8,128)(2,1)S(1)} %pad_maximum_fusion.10), channel_id=1, source_target_pairs={{0,4},{1,5},{2,6},{3,7},{4,0},{5,1},{6,2},{7,3},{8,12},{9,13},{10,... | collective-permute-start | bytes 786440 | tf_op jit(solution)/shard_map/ppermute | solution.py:573
  119.1 8.4 %collective-permute-start.28 = (bf16[4,64,512]{2,1,0:T(8,128)(2,1)S(1)}, bf16[4,64,512]{2,1,0:T(8,128)(2,1)S(1)}, u32[]{:S(2)}, u32[]{:S(2)}) collective-permute-start(bf16[4,64,512]{2,1,0:T(8,128)(2,1)S(1)} %pad_maximum_fusion.10), channel_id=1, source_target_pairs={{0,2},{1,3},{2,0},{3,1},{4,6},{5,7},{6,4},{7,5},{8,10},{9,11},{10,... | collective-permute-start | bytes 786440 | tf_op jit(solution)/shard_map/ppermute | solution.py:573
  127.6 2.4 %collective-permute-start.30 = (bf16[12,64,512]{2,1,0:T(8,128)(2,1)S(1)}, bf16[12,64,512]{2,1,0:T(8,128)(2,1)S(1)}, u32[]{:S(2)}, u32[]{:S(2)}) collective-permute-start(bf16[12,64,512]{2,1,0:T(8,128)(2,1)S(1)} %pad_maximum_fusion.1.refs_0_), channel_id=1, source_target_pairs={{0,1},{1,0},{2,3},{3,2},{4,5},{5,4},{6,7},{7,6},{8,9},{9,8},{10,11... | collective-permute-start | bytes 2359304 | tf_op jit(solution)/shard_map/ppermute | solution.py:573
  127.7 5.9 %collective-permute-start.31 = (bf16[2,64,512]{2,1,0:T(8,128)(2,1)S(1)}, bf16[2,64,512]{2,1,0:T(8,128)(2,1)S(1)}, u32[]{:S(2)}, u32[]{:S(2)}) collective-permute-start(bf16[2,64,512]{2,1,0:T(8,128)(2,1)S(1)} %slice.257), channel_id=1, source_target_pairs={{0,2},{1,3},{2,0},{3,1},{4,6},{5,7},{6,4},{7,5},{8,10},{9,11},{10,... | collective-permute-start | bytes 393224 | tf_op jit(solution)/shard_map/ppermute | solution.py:573
  128.3 5.6 %collective-permute-start.32 = (bf16[2,64,512]{2,1,0:T(8,128)(2,1)S(1)}, bf16[2,64,512]{2,1,0:T(8,128)(2,1)S(1)}, u32[]{:S(2)}, u32[]{:S(2)}) collective-permute-start(bf16[2,64,512]{2,1,0:T(8,128)(2,1)S(1)} %slice.258), channel_id=1, source_target_pairs={{0,4},{1,5},{2,6},{3,7},{4,0},{5,1},{6,2},{7,3},{8,12},{9,13},{10,... | collective-permute-start | bytes 393224 | tf_op jit(solution)/shard_map/ppermute | solution.py:573
  (16 other events, 117.7 us)

commit v17 on v16

--- a/solution.py
+++ b/solution.py
@@ -192,10 +192,10 @@
     inner = (values * rms_scale(values) * gain2[...]).astype(BF16)
     turned[...] = inner.T
     total = values
-    for at in range(0, hidden, 512):
-        lifted = jnp.maximum(dot(inner, win[:, at : at + 512]), 0.0).astype(BF16)
-        active[:, at : at + 512] = lifted
-        total = total + dot(lifted, wback[at : at + 512, :])
+    for at in range(0, hidden, 1024):
+        lifted = jnp.maximum(dot(inner, win[:, at : at + 1024]), 0.0).astype(BF16)
+        active[:, at : at + 1024] = lifted
+        total = total + dot(lifted, wback[at : at + 1024, :])
     scale = rms_scale(total)
     place = lax.broadcasted_iota(jnp.int32, (2 * count, 1), 0)
     place = jnp.where(place < count, place + info[1], place + (info[3] - count))
@@ -206,9 +206,9 @@
     steep[...] = slope
     rows[...] = jnp.concatenate([pool, grad_end, jnp.zeros((6, width), F32)])
     low = slope.astype(BF16)
-    for at in range(0, hidden, 512):
-        through = dot(low, wback[at : at + 512, :], NT).astype(BF16)
-        slopes[:, at : at + 512] = jnp.where(active[:, at : at + 512] > 0, through, jnp.zeros_like(through))
+    for at in range(0, hidden, 1024):
+        through = dot(low, wback[at : at + 1024, :], NT).astype(BF16)
+        slopes[:, at : at + 1024] = jnp.where(active[:, at : at + 1024] > 0, through, jnp.zeros_like(through))
     mine = info[6] & 15
 
     @pl.when(info[7] == 0)

time: 137 us -> 137 us (level)
  no operation moved by 1% of the time
where the time goes in v17:
time: 137 us
  Pallas kernels  60.3 us (44%)
  starting transfers between devices  33.6 us (25%)
  waiting for transfers between devices  32.5 us (24%)
  local copies, waits for them, and re-layouts  5.43 us (4%)
  other arithmetic  3.74 us (3%)
    ppermute x34, starting transfers between devices, exchange(): lax.ppermute(value, ('dp', 'blk'), [(i, i ^ bits) for i in range(size)])  33.6 us
    ppermute x34, waiting for transfers between devices, exchange(): lax.ppermute(value, ('dp', 'blk'), [(i, i ^ bits) for i in range(size)])  32.5 us
    pallas_call x1, Pallas kernels, front(): pl.pallas_call(front_kernel, in_specs=[smem] + [vmem] * 14 + [free] * 3,...  20.3 us
    pallas_call x1, Pallas kernels, back(): pl.pallas_call(back_kernel, grid=(width // 128,), in_specs=[smem, col(cou...  19.1 us
    pallas_call x2, Pallas kernels, place(): pl.pallas_call(functools.partial(place_kernel, [first for first, _ in par...  5.39 us
    pallas_call x3, Pallas kernels, sort(): pl.pallas_call(functools.partial(sort_kernel, [first for first, _ in part...  5.38 us
    unnamed x28, local copies, waits for them, and re-layouts  3.84 us
  transfers between devices with their start and end apart: 34, of which 18 were waited for; matrix products, arithmetic and copies ran while one was open for 3% of the time, Pallas kernels for 28%

profile of v17, /device:TPU:0, one launch (start us, length us, event | category | flops | bytes accessed | tf_op | source)
XLA Modules:
  0.0 137.0 jit_solution(18400647887174676431)
XLA Ops:
  2.4 2.6 %collective-permute-start = (bf16[256,512]{1,0:T(8,128)(2,1)S(1)}, bf16[256,512]{1,0:T(8,128)(2,1)S(1)}, u32[]{:S(2)}, u32[]{:S(2)}) collective-permute-start(bf16[256,512]{1,0:T(8,128)(2,1)S(1)} %get-tuple-element.185), channel_id=1, source_target_pairs={{0,2},{1,3},{2,0},{3,1},{4,6},{5,7},{6,4},{7,5},{8,10},{9,11},{10,... | collective-permute-start | bytes 786440 | tf_op jit(solution)/shard_map/ppermute | solution.py:573
  8.8 1.5 %prepare.1 = (bf16[512,512]{1,0:T(8,128)(2,1)S(1)}, bf16[256,512]{1,0:T(8,128)(2,1)S(1)}, bf16[512,512]{1,0:T(8,128)(2,1)S(1)}, bf16[512,512]{1,0:T(8,128)(2,1)S...) custom-call(bf16[256,512]{1,0:T(8,128)(2,1)S(1)} %get-tuple-element.186.mine.near.near, ...), custom_call_target="tpu_custom_call" | custom-call | tf_op jit(solution)/shard_map/prepare/pallas_call | solution.py:65
  10.4 1.5 %collective-permute-done.far.far_h = bf16[256,512]{1,0:T(8,128)(2,1)S(1)} collective-permute-done((bf16[256,512]{1,0:T(8,128)(2,1)S(1)}, bf16[256,512]{1,0:T(8,128)(2,1)S(1)}, u32[]{:S(2)}, u32[]{:S(2)}) %collective-permute-start) | collective-permute-done | bytes 262176 | tf_op jit(solution)/shard_map/ppermute | solution.py:573
  13.5 20.3 %front.1 = (bf16[512,512]{1,0:T(8,128)(2,1)S(1)}, bf16[256,512]{1,0:T(8,128)(2,1)S(1)}, bf16[512,512]{1,0:T(8,128)(2,1)S(1)}, bf16[512,512]{1,0:T(8,128)(2,1)S(1...) custom-call(s32[16]{0:T(128)S(1)} %get-tuple-element.342.info, ...), custom_call_target="tpu_custom_call" | custom-call | tf_op jit(solution)/shard_map/front/pallas_call | solution.py:235
  34.1 2.0 %stay.1.kept = bf16[4,4,512,128]{3,2,1,0:T(8,128)(2,1)S(1)} custom-call(s32[16]{0:T(128)S(1)} %get-tuple-element.342.info, bf16[512,2048]{1,0:T(8,128)(2,1)S(1)} %get-tuple-element.200.active, bf16[512,2048]{1,0:T(8,128)(2,1)S(1)} %get-tuple-element.201.slopes, bf16[512,512]{1,0:T(8,128)(2,1)S(1)} %get-tuple-element.202.turned, ...), custom_call_target="tpu_custom_call" | custom-call | tf_op jit(solution)/shard_map/stay/pallas_call | solution.py:301
  36.2 1.8 %inner.1.grad_inner = f32[512,512]{1,0:T(8,128)S(1)} custom-call(s32[16]{0:T(128)S(1)} %get-tuple-element.342.info, bf16[512,2048]{1,0:T(8,128)(2,1)S(1)} %get-tuple-element.201.slopes, bf16[512,2048]{1,0:T(8,128)(2,1)S(1)} %copy-done), custom_call_target="tpu_custom_call" | custom-call | tf_op jit(solution)/shard_map/inner/pallas_call | solution.py:255
  38.6 2.8 %collective-permute-start.4 = (bf16[4,512,128]{2,1,0:T(8,128)(2,1)S(1)}, bf16[4,512,128]{2,1,0:T(8,128)(2,1)S(1)}, u32[]{:S(2)}, u32[]{:S(2)}) collective-permute-start(bf16[4,512,128]{2,1,0:T(8,128)(2,1)S(1)} %get-tuple-element.233), channel_id=1, source_target_pairs={{0,6},{1,7},{2,4},{3,5},{4,2},{5,3},{6,0},{7,1},{8,14},{9,15},{10,... | collective-permute-start | bytes 1572872 | tf_op jit(solution)/shard_map/ppermute | solution.py:573
  42.1 1.7 %through.1 = (f32[512,512]{1,0:T(8,128)S(1)}, bf16[512,512]{1,0:T(8,128)(2,1)S(1)}, bf16[512,512]{1,0:T(8,128)(2,1)S(1)}, f32[8,512]{1,0:T(8,128)S(1)}) custom-call(s32[16]{0:T(128)S(1)} %get-tuple-element.342.info, f32[512,512]{1,0:T(8,128)S(1)} %inner.1.grad_inner, f32[512,512]{1,0:T(8,128)S(1)} %get-tuple-element.215.mixed, ...), custom_call_target="tpu_custom_call" | custom-call | tf_op jit(solution)/shard_map/through/pallas_call | solution.py:274
  43.9 19.1 %back.1 = (bf16[16,64,512]{2,1,0:T(8,128)(2,1)S(1)}, bf16[1040,512]{1,0:T(8,128)(2,1)S(1)}, f32[512,512]{1,0:T(8,128)S(1)}, bf16[528,512]{1,0:T(8,128)(2,1)S(1)}, f32[8,512]{1,0:T(8,128)S(1)}) custom-call(s32[16]{0:T(128)S(1)} %get-tuple-element.342.info, bf16[256,512]{1,0:T(8,128)(2,1)S(1)} %get-tuple-element.191.q_l.ql, ...), custom_call_target="tpu_custom_call" | custom-call | tf_op jit(solution)/shard_map/back/pallas_call | solution.py:449
  63.0 2.0 %collective-permute-done.5.refs_2_ = bf16[4,512,128]{2,1,0:T(8,128)(2,1)S(1)} collective-permute-done((bf16[4,512,128]{2,1,0:T(8,128)(2,1)S(1)}, bf16[4,512,128]{2,1,0:T(8,128)(2,1)S(1)}, u32[]{:S(2)}, u32[]{:S(2)}) %collective-permute-start.5) | collective-permute-done | bytes 524320 | tf_op jit(solution)/shard_map/ppermute | solution.py:573
  66.1 1.7 %collective-permute-start.9 = (bf16[512,128]{1,0:T(8,128)(2,1)S(1)}, bf16[512,128]{1,0:T(8,128)(2,1)S(1)}, u32[]{:S(2)}, u32[]{:S(2)}) collective-permute-start(bf16[512,128]{1,0:T(8,128)(2,1)S(1)} %get-tuple-element.253), channel_id=1, source_target_pairs={{0,8},{1,9},{2,10},{3,11},{4,12},{5,13},{6,14},{7,15},{8,0},{9,1},... | collective-permute-start | bytes 393224 | tf_op jit(solution)/shard_map/ppermute | solution.py:573
  67.7 2.6 %collective-permute-start.10 = (bf16[512,128]{1,0:T(8,128)(2,1)S(1)}, bf16[512,128]{1,0:T(8,128)(2,1)S(1)}, u32[]{:S(2)}, u32[]{:S(2)}) collective-permute-start(bf16[512,128]{1,0:T(8,128)(2,1)S(1)} %get-tuple-element.254), channel_id=1, source_target_pairs={{0,16},{1,17},{2,18},{3,19},{4,20},{5,21},{6,22},{7,23},{8,24},{9,... | collective-permute-start | bytes 393224 | tf_op jit(solution)/shard_map/ppermute | solution.py:573
  71.0 1.5 %collective-permute-start.12 = (bf16[272,512]{1,0:T(8,128)(2,1)S(1)}, bf16[272,512]{1,0:T(8,128)(2,1)S(1)}, u32[]{:S(2)}, u32[]{:S(2)}) collective-permute-start(bf16[272,512]{1,0:T(8,128)(2,1)S(1)} %get-tuple-element.266), channel_id=1, source_target_pairs={{0,2},{1,3},{2,0},{3,1},{4,6},{5,7},{6,4},{7,5},{8,10},{9,11},{10,... | collective-permute-start | bytes 835592 | tf_op jit(solution)/shard_map/ppermute | solution.py:573
  73.3 1.5 %collective-permute-start.14 = (bf16[272,512]{1,0:T(8,128)(2,1)S(1)}, bf16[272,512]{1,0:T(8,128)(2,1)S(1)}, u32[]{:S(2)}, u32[]{:S(2)}) collective-permute-start(bf16[272,512]{1,0:T(8,128)(2,1)S(1)} %get-tuple-element.268), channel_id=1, source_target_pairs={{0,6},{1,7},{2,4},{3,5},{4,2},{5,3},{6,0},{7,1},{8,14},{9,15},{10,... | collective-permute-start | bytes 835592 | tf_op jit(solution)/shard_map/ppermute | solution.py:573
  75.9 4.7 %collective-permute-done.10 = bf16[512,128]{1,0:T(8,128)(2,1)S(1)} collective-permute-done((bf16[512,128]{1,0:T(8,128)(2,1)S(1)}, bf16[512,128]{1,0:T(8,128)(2,1)S(1)}, u32[]{:S(2)}, u32[]{:S(2)}) %collective-permute-start.10) | collective-permute-done | bytes 131104 | tf_op jit(solution)/shard_map/ppermute | solution.py:573
  80.7 2.4 %collective-permute-start.18 = (bf16[512,128]{1,0:T(8,128)(2,1)S(1)}, bf16[512,128]{1,0:T(8,128)(2,1)S(1)}, u32[]{:S(2)}, u32[]{:S(2)}) collective-permute-start(bf16[512,128]{1,0:T(8,128)(2,1)S(1)} %add_convert_fusion.2), channel_id=1, source_target_pairs={{0,24},{1,25},{2,26},{3,27},{4,28},{5,29},{6,30},{7,31},{8,16},{9,... | collective-permute-start | bytes 393224 | tf_op jit(solution)/shard_map/ppermute | solution.py:573
  85.2 1.4 %collective-permute-start.19 = (bf16[272,512]{1,0:T(8,128)(2,1)S(1)}, bf16[272,512]{1,0:T(8,128)(2,1)S(1)}, u32[]{:S(2)}, u32[]{:S(2)}) collective-permute-start(bf16[272,512]{1,0:T(8,128)(2,1)S(1)} %get-tuple-element.278), channel_id=1, source_target_pairs={{0,2},{1,3},{2,0},{3,1},{4,6},{5,7},{6,4},{7,5},{8,10},{9,11},{10,... | collective-permute-start | bytes 835592 | tf_op jit(solution)/shard_map/ppermute | solution.py:573
  86.9 1.3 collective-permute-start.15
  88.3 7.2 %collective-permute-done.15 = bf16[144,512]{1,0:T(8,128)(2,1)S(1)} collective-permute-done((bf16[144,512]{1,0:T(8,128)(2,1)S(1)}, bf16[144,512]{1,0:T(8,128)(2,1)S(1)}, u32[]{:S(2)}, u32[]{:S(2)}) %collective-permute-start.15) | collective-permute-done | bytes 147488 | tf_op jit(solution)/shard_map/ppermute | solution.py:573
  95.7 1.6 %collective-permute-start.22 = (bf16[4,512,128]{2,1,0:T(8,128)(2,1)S(1)}, bf16[4,512,128]{2,1,0:T(8,128)(2,1)S(1)}, u32[]{:S(2)}, u32[]{:S(2)}) collective-permute-start(bf16[4,512,128]{2,1,0:T(8,128)(2,1)S(1)} %pad_maximum_fusion.2), channel_id=1, source_target_pairs={{0,4},{1,5},{2,6},{3,7},{4,0},{5,1},{6,2},{7,3},{8,12},{9,13},{10,... | collective-permute-start | bytes 1572872 | tf_op jit(solution)/shard_map/ppermute | solution.py:573
  98.0 1.4 %collective-permute-start.20 = (bf16[144,512]{1,0:T(8,128)(2,1)S(1)}, bf16[144,512]{1,0:T(8,128)(2,1)S(1)}, u32[]{:S(2)}, u32[]{:S(2)}) collective-permute-start(bf16[144,512]{1,0:T(8,128)(2,1)S(1)} %pad_maximum_fusion.13), channel_id=1, source_target_pairs={{0,16},{1,17},{2,18},{3,19},{4,20},{5,21},{6,22},{7,23},{8,24},{9,... | collective-permute-start | bytes 442376 | tf_op jit(solution)/shard_map/ppermute | solution.py:573
  100.9 4.6 %collective-permute-done.20 = bf16[144,512]{1,0:T(8,128)(2,1)S(1)} collective-permute-done((bf16[144,512]{1,0:T(8,128)(2,1)S(1)}, bf16[144,512]{1,0:T(8,128)(2,1)S(1)}, u32[]{:S(2)}, u32[]{:S(2)}) %collective-permute-start.20) | collective-permute-done | bytes 147488 | tf_op jit(solution)/shard_map/ppermute | solution.py:573
  111.2 2.3 %place.2 = (f32[2048,512]{1,0:T(8,128)}, f32[512,2048]{1,0:T(8,128)}) custom-call(s32[16]{0:T(128)S(1)} %get-tuple-element.342.info, bf16[12,512,128]{2,1,0:T(8,128)(2,1)S(1)} %pad_maximum_fusion.refs_0_), custom_call_target="tpu_custom_call" | custom-call | tf_op jit(solution)/shard_map/place/pallas_call | solution.py:516
  113.5 2.2 %collective-permute-done.23 = bf16[128,512]{1,0:T(8,128)(2,1)S(1)} collective-permute-done((bf16[128,512]{1,0:T(8,128)(2,1)S(1)}, bf16[128,512]{1,0:T(8,128)(2,1)S(1)}, u32[]{:S(2)}, u32[]{:S(2)}) %collective-permute-start.23) | collective-permute-done | bytes 131104 | tf_op jit(solution)/shard_map/ppermute | solution.py:573
  115.8 1.3 collective-permute-done.24
  117.7 1.4 %collective-permute-start.29 = (bf16[4,64,512]{2,1,0:T(8,128)(2,1)S(1)}, bf16[4,64,512]{2,1,0:T(8,128)(2,1)S(1)}, u32[]{:S(2)}, u32[]{:S(2)}) collective-permute-start(bf16[4,64,512]{2,1,0:T(8,128)(2,1)S(1)} %pad_maximum_fusion.10), channel_id=1, source_target_pairs={{0,4},{1,5},{2,6},{3,7},{4,0},{5,1},{6,2},{7,3},{8,12},{9,13},{10,... | collective-permute-start | bytes 786440 | tf_op jit(solution)/shard_map/ppermute | solution.py:573
  119.6 3.1 %place.3 = (f32[2048,512]{1,0:T(8,128)}, f32[512,2048]{1,0:T(8,128)}) custom-call(s32[16]{0:T(128)S(1)} %get-tuple-element.342.info, bf16[4,512,128]{2,1,0:T(8,128)(2,1)S(1)} %pad_maximum_fusion.3.refs_0_, bf16[12,512,128]{2,1,0:T(8,128)(2,1)S(1)} %collective-permute-done.26.refs_1_, ...), custom_call_target="tpu_custom_call", output_to_operand_aliasing={{0}: (4, {}), {1}: (5, {})} | custom-call | tf_op jit(solution)/shard_map/place/pallas_call | solution.py:516
  122.7 3.8 %collective-permute-done.29 = bf16[4,64,512]{2,1,0:T(8,128)(2,1)S(1)} collective-permute-done((bf16[4,64,512]{2,1,0:T(8,128)(2,1)S(1)}, bf16[4,64,512]{2,1,0:T(8,128)(2,1)S(1)}, u32[]{:S(2)}, u32[]{:S(2)}) %collective-permute-start.29) | collective-permute-done | bytes 262176 | tf_op jit(solution)/shard_map/ppermute | solution.py:573
  128.3 1.5 %collective-permute-start.32 = (bf16[2,64,512]{2,1,0:T(8,128)(2,1)S(1)}, bf16[2,64,512]{2,1,0:T(8,128)(2,1)S(1)}, u32[]{:S(2)}, u32[]{:S(2)}) collective-permute-start(bf16[2,64,512]{2,1,0:T(8,128)(2,1)S(1)} %slice.258), channel_id=1, source_target_pairs={{0,4},{1,5},{2,6},{3,7},{4,0},{5,1},{6,2},{7,3},{8,12},{9,13},{10,... | collective-permute-start | bytes 393224 | tf_op jit(solution)/shard_map/ppermute | solution.py:573
  130.0 2.6 %sort.3 = (f32[512,512]{1,0:T(8,128)}, f32[512,512]{1,0:T(8,128)}, f32[512,512]{1,0:T(8,128)}, f32[512,512]{1,0:T(8,128)}) custom-call(s32[16]{0:T(128)S(1)} %get-tuple-element.342.info, bf16[12,64,512]{2,1,0:T(8,128)(2,1)S(1)} %pad_maximum_fusion.1.refs_0_, bf16[12,64,512]{2,1,0:T(8,128)(2,1)S(1)} %collective-permute-done.30.refs_1_), custom_call_target="tpu_custom_call" | custom-call | tf_op jit(solution)/shard_map/sort/pallas_call | solution.py:550
  134.0 1.4 %sort.4 = (f32[512,512]{1,0:T(8,128)}, f32[512,512]{1,0:T(8,128)}, f32[512,512]{1,0:T(8,128)}, f32[512,512]{1,0:T(8,128)}) custom-call(s32[16]{0:T(128)S(1)} %get-tuple-element.342.info, bf16[2,64,512]{2,1,0:T(8,128)(2,1)S(1)} %collective-permute-done.31.refs_0_, ...), custom_call_target="tpu_custom_call", output_to_operand_aliasing={{0}: (3, {}), {1}: (4, {}), {2}: (5, {}), {3}: (6, {})} | custom-call | tf_op jit(solution)/shard_map/sort/pallas_call | solution.py:550
  135.5 1.4 %sort.5 = (f32[512,512]{1,0:T(8,128)}, f32[512,512]{1,0:T(8,128)}, f32[512,512]{1,0:T(8,128)}, f32[512,512]{1,0:T(8,128)}) custom-call(s32[16]{0:T(128)S(1)} %get-tuple-element.342.info, bf16[4,64,512]{2,1,0:T(8,128)(2,1)S(1)} %collective-permute-done.33.refs_0_, ...), custom_call_target="tpu_custom_call", output_to_operand_aliasing={{0}: (2, {}), {1}: (3, {}), {2}: (4, {}), {3}: (5, {})} | custom-call | tf_op jit(solution)/shard_map/sort/pallas_call | solution.py:550
  (120 shorter events, 27.3 us)
Async XLA Ops:
  1.9 3.1 %collective-permute-start.1 = (bf16[256,512]{1,0:T(8,128)(2,1)S(1)}, bf16[256,512]{1,0:T(8,128)(2,1)S(1)}, u32[]{:S(2)}, u32[]{:S(2)}) collective-permute-start(bf16[256,512]{1,0:T(8,128)(2,1)S(1)} %get-tuple-element.186.mine.near.near_h), channel_id=1, source_target_pairs={{0,1},{1,0},{2,3},{3,2},{4,5},{5,4},{6,7},{7,6},{8,9},{9,8},{10,11... | collective-permute-start | bytes 786440 | tf_op jit(solution)/shard_map/ppermute | solution.py:573
  2.4 9.5 %collective-permute-start = (bf16[256,512]{1,0:T(8,128)(2,1)S(1)}, bf16[256,512]{1,0:T(8,128)(2,1)S(1)}, u32[]{:S(2)}, u32[]{:S(2)}) collective-permute-start(bf16[256,512]{1,0:T(8,128)(2,1)S(1)} %get-tuple-element.185), channel_id=1, source_target_pairs={{0,2},{1,3},{2,0},{3,1},{4,6},{5,7},{6,4},{7,5},{8,10},{9,11},{10,... | collective-permute-start | bytes 786440 | tf_op jit(solution)/shard_map/ppermute | solution.py:573
  33.8 4.2 %collective-permute-start.3 = (bf16[16,512,128]{2,1,0:T(8,128)(2,1)S(1)}, bf16[16,512,128]{2,1,0:T(8,128)(2,1)S(1)}, u32[]{:S(2)}, u32[]{:S(2)}) collective-permute-start(bf16[16,512,128]{2,1,0:T(8,128)(2,1)S(1)} %get-tuple-element.205), channel_id=1, source_target_pairs={{0,1},{1,0},{2,3},{3,2},{4,5},{5,4},{6,7},{7,6},{8,9},{9,8},{10,11... | collective-permute-start | bytes 6291464 | tf_op jit(solution)/shard_map/ppermute | solution.py:573
  38.6 24.4 %collective-permute-start.4 = (bf16[4,512,128]{2,1,0:T(8,128)(2,1)S(1)}, bf16[4,512,128]{2,1,0:T(8,128)(2,1)S(1)}, u32[]{:S(2)}, u32[]{:S(2)}) collective-permute-start(bf16[4,512,128]{2,1,0:T(8,128)(2,1)S(1)} %get-tuple-element.233), channel_id=1, source_target_pairs={{0,6},{1,7},{2,4},{3,5},{4,2},{5,3},{6,0},{7,1},{8,14},{9,15},{10,... | collective-permute-start | bytes 1572872 | tf_op jit(solution)/shard_map/ppermute | solution.py:573
  41.3 23.7 %collective-permute-start.5 = (bf16[4,512,128]{2,1,0:T(8,128)(2,1)S(1)}, bf16[4,512,128]{2,1,0:T(8,128)(2,1)S(1)}, u32[]{:S(2)}, u32[]{:S(2)}) collective-permute-start(bf16[4,512,128]{2,1,0:T(8,128)(2,1)S(1)} %get-tuple-element.234), channel_id=1, source_target_pairs={{0,2},{1,3},{2,0},{3,1},{4,6},{5,7},{6,4},{7,5},{8,10},{9,11},{10,... | collective-permute-start | bytes 1572872 | tf_op jit(solution)/shard_map/ppermute | solution.py:573
  41.8 23.5 %collective-permute-start.6 = (bf16[4,512,128]{2,1,0:T(8,128)(2,1)S(1)}, bf16[4,512,128]{2,1,0:T(8,128)(2,1)S(1)}, u32[]{:S(2)}, u32[]{:S(2)}) collective-permute-start(bf16[4,512,128]{2,1,0:T(8,128)(2,1)S(1)} %get-tuple-element.235), channel_id=1, source_target_pairs={{0,4},{1,5},{2,6},{3,7},{4,0},{5,1},{6,2},{7,3},{8,12},{9,13},{10,... | collective-permute-start | bytes 1572872 | tf_op jit(solution)/shard_map/ppermute | solution.py:573
  65.3 5.2 %collective-permute-start.7 = (bf16[1040,512]{1,0:T(8,128)(2,1)S(1)}, bf16[1040,512]{1,0:T(8,128)(2,1)S(1)}, u32[]{:S(2)}, u32[]{:S(2)}) collective-permute-start(bf16[1040,512]{1,0:T(8,128)(2,1)S(1)} %get-tuple-element.246), channel_id=1, source_target_pairs={{0,1},{1,0},{2,3},{3,2},{4,5},{5,4},{6,7},{7,6},{8,9},{9,8},{10,11... | collective-permute-start | bytes 3194888 | tf_op jit(solution)/shard_map/ppermute | solution.py:573
  65.3 5.2 %collective-permute-start.8 = (bf16[528,512]{1,0:T(8,128)(2,1)S(1)}, bf16[528,512]{1,0:T(8,128)(2,1)S(1)}, u32[]{:S(2)}, u32[]{:S(2)}) collective-permute-start(bf16[528,512]{1,0:T(8,128)(2,1)S(1)} %get-tuple-element.247), channel_id=1, source_target_pairs={{0,1},{1,0},{2,3},{3,2},{4,5},{5,4},{6,7},{7,6},{8,9},{9,8},{10,11... | collective-permute-start | bytes 1622024 | tf_op jit(solution)/shard_map/ppermute | solution.py:573
  66.1 7.2 %collective-permute-start.9 = (bf16[512,128]{1,0:T(8,128)(2,1)S(1)}, bf16[512,128]{1,0:T(8,128)(2,1)S(1)}, u32[]{:S(2)}, u32[]{:S(2)}) collective-permute-start(bf16[512,128]{1,0:T(8,128)(2,1)S(1)} %get-tuple-element.253), channel_id=1, source_target_pairs={{0,8},{1,9},{2,10},{3,11},{4,12},{5,13},{6,14},{7,15},{8,0},{9,1},... | collective-permute-start | bytes 393224 | tf_op jit(solution)/shard_map/ppermute | solution.py:573
  67.7 12.9 %collective-permute-start.10 = (bf16[512,128]{1,0:T(8,128)(2,1)S(1)}, bf16[512,128]{1,0:T(8,128)(2,1)S(1)}, u32[]{:S(2)}, u32[]{:S(2)}) collective-permute-start(bf16[512,128]{1,0:T(8,128)(2,1)S(1)} %get-tuple-element.254), channel_id=1, source_target_pairs={{0,16},{1,17},{2,18},{3,19},{4,20},{5,21},{6,22},{7,23},{8,24},{9,... | collective-permute-start | bytes 393224 | tf_op jit(solution)/shard_map/ppermute | solution.py:573
  70.3 10.3 %collective-permute-start.11 = (bf16[512,128]{1,0:T(8,128)(2,1)S(1)}, bf16[512,128]{1,0:T(8,128)(2,1)S(1)}, u32[]{:S(2)}, u32[]{:S(2)}) collective-permute-start(bf16[512,128]{1,0:T(8,128)(2,1)S(1)} %get-tuple-element.255), channel_id=1, source_target_pairs={{0,24},{1,25},{2,26},{3,27},{4,28},{5,29},{6,30},{7,31},{8,16},{9,... | collective-permute-start | bytes 393224 | tf_op jit(solution)/shard_map/ppermute | solution.py:573
  71.0 13.4 %collective-permute-start.12 = (bf16[272,512]{1,0:T(8,128)(2,1)S(1)}, bf16[272,512]{1,0:T(8,128)(2,1)S(1)}, u32[]{:S(2)}, u32[]{:S(2)}) collective-permute-start(bf16[272,512]{1,0:T(8,128)(2,1)S(1)} %get-tuple-element.266), channel_id=1, source_target_pairs={{0,2},{1,3},{2,0},{3,1},{4,6},{5,7},{6,4},{7,5},{8,10},{9,11},{10,... | collective-permute-start | bytes 835592 | tf_op jit(solution)/shard_map/ppermute | solution.py:573
  72.5 12.7 %collective-permute-start.13 = (bf16[272,512]{1,0:T(8,128)(2,1)S(1)}, bf16[272,512]{1,0:T(8,128)(2,1)S(1)}, u32[]{:S(2)}, u32[]{:S(2)}) collective-permute-start(bf16[272,512]{1,0:T(8,128)(2,1)S(1)} %get-tuple-element.267), channel_id=1, source_target_pairs={{0,4},{1,5},{2,6},{3,7},{4,0},{5,1},{6,2},{7,3},{8,12},{9,13},{10,... | collective-permute-start | bytes 835592 | tf_op jit(solution)/shard_map/ppermute | solution.py:573
  73.3 13.3 %collective-permute-start.14 = (bf16[272,512]{1,0:T(8,128)(2,1)S(1)}, bf16[272,512]{1,0:T(8,128)(2,1)S(1)}, u32[]{:S(2)}, u32[]{:S(2)}) collective-permute-start(bf16[272,512]{1,0:T(8,128)(2,1)S(1)} %get-tuple-element.268), channel_id=1, source_target_pairs={{0,6},{1,7},{2,4},{3,5},{4,2},{5,3},{6,0},{7,1},{8,14},{9,15},{10,... | collective-permute-start | bytes 835592 | tf_op jit(solution)/shard_map/ppermute | solution.py:573
  80.7 14.8 %collective-permute-start.18 = (bf16[512,128]{1,0:T(8,128)(2,1)S(1)}, bf16[512,128]{1,0:T(8,128)(2,1)S(1)}, u32[]{:S(2)}, u32[]{:S(2)}) collective-permute-start(bf16[512,128]{1,0:T(8,128)(2,1)S(1)} %add_convert_fusion.2), channel_id=1, source_target_pairs={{0,24},{1,25},{2,26},{3,27},{4,28},{5,29},{6,30},{7,31},{8,16},{9,... | collective-permute-start | bytes 393224 | tf_op jit(solution)/shard_map/ppermute | solution.py:573
  83.2 12.4 %collective-permute-start.17 = (bf16[512,128]{1,0:T(8,128)(2,1)S(1)}, bf16[512,128]{1,0:T(8,128)(2,1)S(1)}, u32[]{:S(2)}, u32[]{:S(2)}) collective-permute-start(bf16[512,128]{1,0:T(8,128)(2,1)S(1)} %add_convert_fusion.2), channel_id=1, source_target_pairs={{0,16},{1,17},{2,18},{3,19},{4,20},{5,21},{6,22},{7,23},{8,24},{9,... | collective-permute-start | bytes 393224 | tf_op jit(solution)/shard_map/ppermute | solution.py:573
  84.4 11.2 %collective-permute-start.16 = (bf16[512,128]{1,0:T(8,128)(2,1)S(1)}, bf16[512,128]{1,0:T(8,128)(2,1)S(1)}, u32[]{:S(2)}, u32[]{:S(2)}) collective-permute-start(bf16[512,128]{1,0:T(8,128)(2,1)S(1)} %add_convert_fusion.2), channel_id=1, source_target_pairs={{0,8},{1,9},{2,10},{3,11},{4,12},{5,13},{6,14},{7,15},{8,0},{9,1},... | collective-permute-start | bytes 393224 | tf_op jit(solution)/shard_map/ppermute | solution.py:573
  85.2 10.4 %collective-permute-start.19 = (bf16[272,512]{1,0:T(8,128)(2,1)S(1)}, bf16[272,512]{1,0:T(8,128)(2,1)S(1)}, u32[]{:S(2)}, u32[]{:S(2)}) collective-permute-start(bf16[272,512]{1,0:T(8,128)(2,1)S(1)} %get-tuple-element.278), channel_id=1, source_target_pairs={{0,2},{1,3},{2,0},{3,1},{4,6},{5,7},{6,4},{7,5},{8,10},{9,11},{10,... | collective-permute-start | bytes 835592 | tf_op jit(solution)/shard_map/ppermute | solution.py:573
  86.9 8.5 %collective-permute-start.15 = (bf16[144,512]{1,0:T(8,128)(2,1)S(1)}, bf16[144,512]{1,0:T(8,128)(2,1)S(1)}, u32[]{:S(2)}, u32[]{:S(2)}) collective-permute-start(bf16[144,512]{1,0:T(8,128)(2,1)S(1)} %pad_maximum_fusion.12), channel_id=1, source_target_pairs={{0,8},{1,9},{2,10},{3,11},{4,12},{5,13},{6,14},{7,15},{8,0},{9,1},... | collective-permute-start | bytes 442376 | tf_op jit(solution)/shard_map/ppermute | solution.py:573
  95.7 11.1 %collective-permute-start.22 = (bf16[4,512,128]{2,1,0:T(8,128)(2,1)S(1)}, bf16[4,512,128]{2,1,0:T(8,128)(2,1)S(1)}, u32[]{:S(2)}, u32[]{:S(2)}) collective-permute-start(bf16[4,512,128]{2,1,0:T(8,128)(2,1)S(1)} %pad_maximum_fusion.2), channel_id=1, source_target_pairs={{0,4},{1,5},{2,6},{3,7},{4,0},{5,1},{6,2},{7,3},{8,12},{9,13},{10,... | collective-permute-start | bytes 1572872 | tf_op jit(solution)/shard_map/ppermute | solution.py:573
  97.3 10.8 %collective-permute-start.21 = (bf16[4,512,128]{2,1,0:T(8,128)(2,1)S(1)}, bf16[4,512,128]{2,1,0:T(8,128)(2,1)S(1)}, u32[]{:S(2)}, u32[]{:S(2)}) collective-permute-start(bf16[4,512,128]{2,1,0:T(8,128)(2,1)S(1)} %pad_maximum_fusion.2), channel_id=1, source_target_pairs={{0,2},{1,3},{2,0},{3,1},{4,6},{5,7},{6,4},{7,5},{8,10},{9,11},{10,... | collective-permute-start | bytes 1572872 | tf_op jit(solution)/shard_map/ppermute | solution.py:573
  98.0 7.5 %collective-permute-start.20 = (bf16[144,512]{1,0:T(8,128)(2,1)S(1)}, bf16[144,512]{1,0:T(8,128)(2,1)S(1)}, u32[]{:S(2)}, u32[]{:S(2)}) collective-permute-start(bf16[144,512]{1,0:T(8,128)(2,1)S(1)} %pad_maximum_fusion.13), channel_id=1, source_target_pairs={{0,16},{1,17},{2,18},{3,19},{4,20},{5,21},{6,22},{7,23},{8,24},{9,... | collective-permute-start | bytes 442376 | tf_op jit(solution)/shard_map/ppermute | solution.py:573
  108.3 9.2 %collective-permute-start.26 = (bf16[12,512,128]{2,1,0:T(8,128)(2,1)S(1)}, bf16[12,512,128]{2,1,0:T(8,128)(2,1)S(1)}, u32[]{:S(2)}, u32[]{:S(2)}) collective-permute-start(bf16[12,512,128]{2,1,0:T(8,128)(2,1)S(1)} %pad_maximum_fusion.refs_0_), channel_id=1, source_target_pairs={{0,1},{1,0},{2,3},{3,2},{4,5},{5,4},{6,7},{7,6},{8,9},{9,8},{10,11... | collective-permute-start | bytes 4718600 | tf_op jit(solution)/shard_map/ppermute | solution.py:573
  108.4 8.7 %collective-permute-start.24 = (bf16[2,512,128]{2,1,0:T(8,128)(2,1)S(1)}, bf16[2,512,128]{2,1,0:T(8,128)(2,1)S(1)}, u32[]{:S(2)}, u32[]{:S(2)}) collective-permute-start(bf16[2,512,128]{2,1,0:T(8,128)(2,1)S(1)} %slice.251), channel_id=1, source_target_pairs={{0,2},{1,3},{2,0},{3,1},{4,6},{5,7},{6,4},{7,5},{8,10},{9,11},{10,... | collective-permute-start | bytes 786440 | tf_op jit(solution)/shard_map/ppermute | solution.py:573
  109.2 8.4 %collective-permute-start.25 = (bf16[2,512,128]{2,1,0:T(8,128)(2,1)S(1)}, bf16[2,512,128]{2,1,0:T(8,128)(2,1)S(1)}, u32[]{:S(2)}, u32[]{:S(2)}) collective-permute-start(bf16[2,512,128]{2,1,0:T(8,128)(2,1)S(1)} %slice.252), channel_id=1, source_target_pairs={{0,4},{1,5},{2,6},{3,7},{4,0},{5,1},{6,2},{7,3},{8,12},{9,13},{10,... | collective-permute-start | bytes 786440 | tf_op jit(solution)/shard_map/ppermute | solution.py:573
  110.5 5.3 %collective-permute-start.23 = (bf16[128,512]{1,0:T(8,128)(2,1)S(1)}, bf16[128,512]{1,0:T(8,128)(2,1)S(1)}, u32[]{:S(2)}, u32[]{:S(2)}) collective-permute-start(bf16[128,512]{1,0:T(8,128)(2,1)S(1)} %add_convert_fusion), channel_id=1, source_target_pairs={{0,8},{1,9},{2,10},{3,11},{4,12},{5,13},{6,14},{7,15},{8,0},{9,1},... | collective-permute-start | bytes 393224 | tf_op jit(solution)/shard_map/ppermute | solution.py:573
  117.7 2.0 %collective-permute-start.27 = (bf16[4,512,128]{2,1,0:T(8,128)(2,1)S(1)}, bf16[4,512,128]{2,1,0:T(8,128)(2,1)S(1)}, u32[]{:S(2)}, u32[]{:S(2)}) collective-permute-start(bf16[4,512,128]{2,1,0:T(8,128)(2,1)S(1)} %pad_maximum_fusion.3.refs_0_), channel_id=1, source_target_pairs={{0,1},{1,0},{2,3},{3,2},{4,5},{5,4},{6,7},{7,6},{8,9},{9,8},{10,11... | collective-permute-start | bytes 1572872 | tf_op jit(solution)/shard_map/ppermute | solution.py:573
  117.7 8.7 %collective-permute-start.29 = (bf16[4,64,512]{2,1,0:T(8,128)(2,1)S(1)}, bf16[4,64,512]{2,1,0:T(8,128)(2,1)S(1)}, u32[]{:S(2)}, u32[]{:S(2)}) collective-permute-start(bf16[4,64,512]{2,1,0:T(8,128)(2,1)S(1)} %pad_maximum_fusion.10), channel_id=1, source_target_pairs={{0,4},{1,5},{2,6},{3,7},{4,0},{5,1},{6,2},{7,3},{8,12},{9,13},{10,... | collective-permute-start | bytes 786440 | tf_op jit(solution)/shard_map/ppermute | solution.py:573
  119.1 8.4 %collective-permute-start.28 = (bf16[4,64,512]{2,1,0:T(8,128)(2,1)S(1)}, bf16[4,64,512]{2,1,0:T(8,128)(2,1)S(1)}, u32[]{:S(2)}, u32[]{:S(2)}) collective-permute-start(bf16[4,64,512]{2,1,0:T(8,128)(2,1)S(1)} %pad_maximum_fusion.10), channel_id=1, source_target_pairs={{0,2},{1,3},{2,0},{3,1},{4,6},{5,7},{6,4},{7,5},{8,10},{9,11},{10,... | collective-permute-start | bytes 786440 | tf_op jit(solution)/shard_map/ppermute | solution.py:573
  127.6 2.4 %collective-permute-start.30 = (bf16[12,64,512]{2,1,0:T(8,128)(2,1)S(1)}, bf16[12,64,512]{2,1,0:T(8,128)(2,1)S(1)}, u32[]{:S(2)}, u32[]{:S(2)}) collective-permute-start(bf16[12,64,512]{2,1,0:T(8,128)(2,1)S(1)} %pad_maximum_fusion.1.refs_0_), channel_id=1, source_target_pairs={{0,1},{1,0},{2,3},{3,2},{4,5},{5,4},{6,7},{7,6},{8,9},{9,8},{10,11... | collective-permute-start | bytes 2359304 | tf_op jit(solution)/shard_map/ppermute | solution.py:573
  127.7 5.9 %collective-permute-start.31 = (bf16[2,64,512]{2,1,0:T(8,128)(2,1)S(1)}, bf16[2,64,512]{2,1,0:T(8,128)(2,1)S(1)}, u32[]{:S(2)}, u32[]{:S(2)}) collective-permute-start(bf16[2,64,512]{2,1,0:T(8,128)(2,1)S(1)} %slice.257), channel_id=1, source_target_pairs={{0,2},{1,3},{2,0},{3,1},{4,6},{5,7},{6,4},{7,5},{8,10},{9,11},{10,... | collective-permute-start | bytes 393224 | tf_op jit(solution)/shard_map/ppermute | solution.py:573
  128.3 5.6 %collective-permute-start.32 = (bf16[2,64,512]{2,1,0:T(8,128)(2,1)S(1)}, bf16[2,64,512]{2,1,0:T(8,128)(2,1)S(1)}, u32[]{:S(2)}, u32[]{:S(2)}) collective-permute-start(bf16[2,64,512]{2,1,0:T(8,128)(2,1)S(1)} %slice.258), channel_id=1, source_target_pairs={{0,4},{1,5},{2,6},{3,7},{4,0},{5,1},{6,2},{7,3},{8,12},{9,13},{10,... | collective-permute-start | bytes 393224 | tf_op jit(solution)/shard_map/ppermute | solution.py:573
  (16 other events, 117.7 us)
